TPU v7x, 32 devices: a whole 2x2x4 slice. The times are simulated.
32 devices in a mesh: dp: 16 (over z, x, core), tensor: 2 (over y).
Axes of the slice: x: 2, y: 2, z: 4, core: 2. Of those that a mesh axis runs over, the one named last changes fastest.
Arguments:
- patches: bfloat16 [16384, 768], P('dp'), may hold values from -6 to 6
- cotangent: bfloat16 [16384, 768], P('dp'), may hold values from -6 to 6
- image_size: int32 [16, 5], P('dp'), may hold values from 0 to 3, as said below
- block_slot: int32 [2, 504], P('tensor'), may hold values from 0 to 511, as said below
- pinv: bfloat16 [3, 3072, 768], replicated, may hold values from -0.109375 to 0.109375
- master_slots: float32 [2, 512, 128, 128], P('tensor', 'dp'), may hold values from -0.21875 to 0.21875
- left_basis: float32 [2, 512, 128, 128], P('tensor', 'dp'), may hold values from -0.5 to 0.5
- right_basis: float32 [2, 512, 128, 128], P('tensor', 'dp'), may hold values from -0.5 to 0.5
- mom_slots: float32 [2, 512, 128, 128], P('tensor', 'dp')
- var_slots: float32 [2, 512, 128, 128], P('tensor', 'dp'), as said below
- vec_master: float32 [2, 14336], P('tensor', 'dp')
- vec_mom: float32 [2, 14336], P('tensor', 'dp')
- vec_var: float32 [2, 14336], P('tensor', 'dp'), as said below
Outputs:
- output: float32 [16384, 768], P('dp')
- patch_grad: float32 [16384, 768], P('dp', 'tensor')
- grad_slots: float32 [2, 512, 128, 128], P('tensor', 'dp')
- new_master: float32 [2, 512, 128, 128], P('tensor', 'dp')
- new_mom: float32 [2, 512, 128, 128], P('tensor', 'dp')
- new_var: float32 [2, 512, 128, 128], P('tensor', 'dp')
- grad_vec: float32 [2, 14336], P('tensor', 'dp')
- new_vec: float32 [2, 14336], P('tensor', 'dp')
- new_vec_mom: float32 [2, 14336], P('tensor', 'dp')
- new_vec_var: float32 [2, 14336], P('tensor', 'dp')
Inputs may be any that keep to these rules, and one draw needn't show every extreme that they name: `image_size`: each row lists the size classes of one index of dp's images in order; class 3 (no image) stands only after the others. A row's images hold at most 997 tokens, and some row holds exactly that many in every draw. `block_slot`: each row names 504 different slots; slot s belongs to index s // 32 of dp, and the slots 0 and 511 are always named. `var_slots`: Positive. `vec_var`: Positive.
All inputs are finite; a program needn't handle non-finite values.
Results may differ from a plain program's by a relative error of at most 0.04.
Values may be sent and summed in bfloat16 or wider, within the bound.
No kernel may reach another device: no remote copies, remote signals or barrier semaphores. Data moves between devices by JAX's collectives and lax.ppermute only.
A program may use at most 256 MiB of HBM per device.

v0:
```python
import jax
import jax.numpy as jnp
from jax import lax
from jax.sharding import PartitionSpec as P

D = 768
HEAD_DIM = 64
FF = 3072
BASE_PIX = 3072
LAYERS = 2
LEN_A = 196
LEN_B = 225
LEN_C = 576
IMG_DEV = 5
BS = 128
QBLK = 512


precise = lax.Precision.HIGHEST
masked_score = -1e30
norm_eps = 1e-06
adam_eps = 1e-08
decay = 0.5
matrix_rate = 0.05
vector_rate = 0.3


def layer_norm(values, gain_vec, shift_vec):
    mean_val = jnp.mean(values, axis=-1, keepdims=True)
    centered = values - mean_val
    inv_std = lax.rsqrt(jnp.mean(centered * centered, axis=-1, keepdims=True) + norm_eps)
    return centered * inv_std * gain_vec + shift_vec


def gelu_exact(values):
    return jax.nn.gelu(values, approximate=False)


def left_product(left_rows, right_rows):
    return lax.dot_general(
        left_rows, right_rows, (((0,), (0,)), ((), ())), preferred_element_type=jnp.float32
    )


def right_product(left_rows, matrix):
    return lax.dot_general(
        left_rows, matrix, (((1,), (1,)), ((), ())), preferred_element_type=jnp.float32
    )


def matrix_shapes(part_d, part_ff):
    shapes = [(BASE_PIX, part_d)]
    for layer_idx in range(LAYERS):
        shapes += [(D, 3 * part_d), (part_d, D), (D, part_ff), (part_ff, D)]
    return shapes


def from_tiles(tile_rows, shapes):
    matrices = []
    offset = 0
    for rows_n, cols_n in shapes:
        tile_count = rows_n // BS * (cols_n // BS)
        tile_block = tile_rows[offset : offset + tile_count]
        matrices.append(
            tile_block.reshape(rows_n // BS, cols_n // BS, BS, BS)
            .transpose(0, 2, 1, 3)
            .reshape(rows_n, cols_n)
        )
        offset += tile_count
    return matrices


def to_tiles(matrix):
    rows_n, cols_n = matrix.shape
    return (
        matrix.reshape(rows_n // BS, BS, cols_n // BS, BS).transpose(0, 2, 1, 3).reshape(-1, BS, BS)
    )


def split_vector(vector, part_d, part_ff):
    lengths = [part_d]
    for layer_idx in range(LAYERS):
        lengths += [D, D, part_d, part_d, D, D, D, part_ff, D]
    pieces = []
    offset = 0
    for length in lengths:
        pieces.append(vector[offset : offset + length])
        offset += length
    return (
        pieces[0],
        [pieces[1 + 9 * layer_idx : 10 + 9 * layer_idx] for layer_idx in range(LAYERS)],
    )


def token_meta(size_row, tokens_n):
    lengths = jnp.where(
        size_row == 0, LEN_A, jnp.where(size_row == 1, LEN_B, jnp.where(size_row == 2, LEN_C, 0))
    )
    ends_at = jnp.cumsum(lengths)
    places = jnp.arange(tokens_n)
    segment = jnp.sum((places[:, None] >= ends_at[None, :]).astype(jnp.int32), axis=1)
    onehot = (segment[:, None] == jnp.arange(IMG_DEV)[None, :]).astype(jnp.int32)
    size_class = jnp.sum(onehot * size_row[None, :], axis=1) + 3 * (segment == IMG_DEV).astype(
        jnp.int32
    )
    valid_rows = (segment < IMG_DEV).astype(jnp.float32)
    return (segment, size_class, valid_rows)


def block_scores(query_blk, key_heads, seg_blk, segment):
    scores = jnp.einsum(
        "qhd,khd->hqk", query_blk, key_heads, preferred_element_type=jnp.float32
    ) * HEAD_DIM ** (-0.5)
    allowed = seg_blk[:, None] == segment[None, :]
    return jnp.where(allowed[None, :, :], scores, masked_score)


def attend(queries, key_rows, value_rows, segment):
    tokens_n = queries.shape[0]
    heads_here = queries.shape[1] // HEAD_DIM
    blocks_n = tokens_n // QBLK
    key_heads = key_rows.reshape(tokens_n, heads_here, HEAD_DIM)
    value_heads = value_rows.reshape(tokens_n, heads_here, HEAD_DIM)

    def one_block(carried, inputs):
        query_blk, seg_blk = inputs
        scores = block_scores(query_blk, key_heads, seg_blk, segment)
        row_max = jnp.max(scores, axis=-1, keepdims=True)
        exponent = jnp.exp(scores - row_max)
        summed = jnp.sum(exponent, axis=-1, keepdims=True)
        weights_p = (exponent / summed).astype(jnp.bfloat16)
        mixed_blk = jnp.einsum(
            "hqk,khd->qhd", weights_p, value_heads, preferred_element_type=jnp.float32
        )
        return (
            carried,
            (mixed_blk.reshape(QBLK, heads_here * HEAD_DIM), (row_max + jnp.log(summed))[..., 0]),
        )

    unused, (mixed, log_total) = lax.scan(
        one_block,
        0,
        (queries.reshape(blocks_n, QBLK, heads_here, HEAD_DIM), segment.reshape(blocks_n, QBLK)),
    )
    return (mixed.reshape(tokens_n, heads_here * HEAD_DIM), log_total)


def attend_back(queries, key_rows, value_rows, segment, log_total, grad_mixed):
    tokens_n = queries.shape[0]
    heads_here = queries.shape[1] // HEAD_DIM
    blocks_n = tokens_n // QBLK
    key_heads = key_rows.reshape(tokens_n, heads_here, HEAD_DIM)
    value_heads = value_rows.reshape(tokens_n, heads_here, HEAD_DIM)
    scale_low = jnp.asarray(HEAD_DIM ** (-0.5), jnp.bfloat16)

    def one_block(carried, inputs):
        grad_keys, grad_values = carried
        query_blk, seg_blk, total_blk, grad_blk = inputs
        scores = block_scores(query_blk, key_heads, seg_blk, segment)
        prob_full = jnp.exp(scores - total_blk[..., None])
        prob_low = prob_full.astype(jnp.bfloat16)
        grad_values = grad_values + jnp.einsum(
            "hqk,qhd->khd", prob_low, grad_blk, preferred_element_type=jnp.float32
        )
        grad_prob = jnp.einsum(
            "qhd,khd->hqk", grad_blk, value_heads, preferred_element_type=jnp.float32
        )
        row_inner = jnp.sum(prob_full * grad_prob, axis=-1, keepdims=True)
        grad_scores = (prob_full * (grad_prob - row_inner)).astype(jnp.bfloat16) * scale_low
        grad_query = jnp.einsum(
            "hqk,khd->qhd", grad_scores, key_heads, preferred_element_type=jnp.float32
        )
        grad_keys = grad_keys + jnp.einsum(
            "hqk,qhd->khd", grad_scores, query_blk, preferred_element_type=jnp.float32
        )
        return ((grad_keys, grad_values), grad_query.reshape(QBLK, heads_here * HEAD_DIM))

    zeroed = jnp.zeros((tokens_n, heads_here, HEAD_DIM), jnp.float32)
    inputs = (
        queries.reshape(blocks_n, QBLK, heads_here, HEAD_DIM),
        segment.reshape(blocks_n, QBLK),
        log_total,
        grad_mixed.reshape(blocks_n, QBLK, heads_here, HEAD_DIM),
    )
    (grad_keys, grad_values), grad_query = lax.scan(one_block, (zeroed, zeroed), inputs)
    width = heads_here * HEAD_DIM
    return (
        grad_query.reshape(tokens_n, width),
        grad_keys.reshape(tokens_n, width),
        grad_values.reshape(tokens_n, width),
    )


def rotate_step(master, grads, left, right, moment, variance):
    rotated = jnp.einsum("sji,sjk->sik", left, grads, precision=precise)
    rotated = jnp.einsum("sik,skl->sil", rotated, right, precision=precise)
    new_moment = decay * moment + (1.0 - decay) * rotated
    new_variance = decay * variance + (1.0 - decay) * rotated * rotated
    step_rot = new_moment / (jnp.sqrt(new_variance) + adam_eps)
    returned = jnp.einsum("sij,sjk->sik", left, step_rot, precision=precise)
    returned = jnp.einsum("sik,slk->sil", returned, right, precision=precise)
    return (master - matrix_rate * returned, new_moment, new_variance)


def shards(
    patches,
    cotangent,
    image_size,
    block_slot,
    pinv,
    master_slots,
    left_basis,
    right_basis,
    mom_slots,
    var_slots,
    vec_master,
    vec_mom,
    vec_var,
):
    tensor_count = lax.axis_size("tensor")
    tensor_pos = lax.axis_index("tensor")
    part_d = D // tensor_count
    part_ff = FF // tensor_count
    tokens_n = patches.shape[0]
    slot_tiles, vec_full = (
        lax.all_gather(master_slots[0].astype(jnp.bfloat16), "dp", axis=0, tiled=True).astype(
            jnp.float32
        ),
        lax.all_gather(vec_master[0].astype(jnp.bfloat16), "dp", axis=0, tiled=True).astype(
            jnp.float32
        ),
    )
    slot_list = block_slot[0]
    tile_rows = jnp.take(slot_tiles, slot_list, axis=0)
    low_mats = [
        matrix.astype(jnp.bfloat16)
        for matrix in from_tiles(tile_rows, matrix_shapes(part_d, part_ff))
    ]
    emb_bias, layer_vecs = split_vector(vec_full, part_d, part_ff)
    segment, size_class, valid_rows = token_meta(image_size[0], tokens_n)
    base = low_mats[0]
    resized_cat = jnp.concatenate(
        [
            lax.dot_general(
                pinv[size_idx], base, (((0,), (0,)), ((), ())), preferred_element_type=jnp.float32
            ).astype(jnp.bfloat16)
            for size_idx in range(3)
        ],
        axis=1,
    )
    select_f = (size_class[:, None] == jnp.arange(3)[None, :]).astype(jnp.float32)
    projected = jnp.dot(patches, resized_cat, preferred_element_type=jnp.float32).reshape(
        tokens_n, 3, part_d
    )
    embedded = jnp.sum(projected * select_f[:, :, None], axis=1) + emb_bias
    hidden = lax.all_gather(embedded.astype(jnp.bfloat16), "tensor", axis=1, tiled=True).astype(
        jnp.float32
    )
    caches = []
    for layer_idx in range(LAYERS):
        w_qkv, w_out, w_up, w_down = low_mats[1 + 4 * layer_idx : 5 + 4 * layer_idx]
        gain_one, shift_one, bias_q, bias_v, bias_out, gain_two, shift_two, bias_up, bias_down = (
            layer_vecs[layer_idx]
        )
        normed_low = layer_norm(hidden, gain_one, shift_one).astype(jnp.bfloat16)
        qkv_rows = jnp.dot(normed_low, w_qkv, preferred_element_type=jnp.float32)
        queries = (qkv_rows[:, :part_d] + bias_q).astype(jnp.bfloat16)
        key_rows = qkv_rows[:, part_d : 2 * part_d].astype(jnp.bfloat16)
        value_rows = (qkv_rows[:, 2 * part_d :] + bias_v).astype(jnp.bfloat16)
        mixed, log_total = attend(queries, key_rows, value_rows, segment)
        mixed_low = mixed.astype(jnp.bfloat16)
        partial_value = jnp.dot(mixed_low, w_out, preferred_element_type=jnp.float32) + bias_out
        attn_total = lax.psum(
            partial_value.astype(jnp.bfloat16).astype(jnp.float32).astype(jnp.bfloat16), "tensor"
        ).astype(jnp.float32)
        middle = hidden + attn_total
        normed2_low = layer_norm(middle, gain_two, shift_two).astype(jnp.bfloat16)
        up_proj = jnp.dot(normed2_low, w_up, preferred_element_type=jnp.float32) + bias_up
        activated = gelu_exact(up_proj).astype(jnp.bfloat16)
        partial2 = jnp.dot(activated, w_down, preferred_element_type=jnp.float32) + bias_down
        mlp_total = lax.psum(
            partial2.astype(jnp.bfloat16).astype(jnp.float32).astype(jnp.bfloat16), "tensor"
        ).astype(jnp.float32)
        kept_up = up_proj
        caches.append(
            (
                hidden,
                normed_low,
                queries,
                key_rows,
                value_rows,
                log_total,
                mixed_low,
                middle,
                normed2_low,
                kept_up,
                activated,
            )
        )
        hidden = middle + mlp_total
    output = hidden * valid_rows[:, None]
    grad_hidden = cotangent.astype(jnp.float32) * valid_rows[:, None]
    layer_mats = [None] * LAYERS
    layer_grads = [None] * LAYERS
    for layer_idx in reversed(range(LAYERS)):
        w_qkv, w_out, w_up, w_down = low_mats[1 + 4 * layer_idx : 5 + 4 * layer_idx]
        gain_one, shift_one, bias_q, bias_v, bias_out, gain_two, shift_two, bias_up, bias_down = (
            layer_vecs[layer_idx]
        )
        (
            hidden_in,
            normed_low,
            queries,
            key_rows,
            value_rows,
            log_total,
            mixed_low,
            middle,
            normed2_low,
            kept_up,
            activated,
        ) = caches[layer_idx]
        grad_m_low = grad_hidden.astype(jnp.bfloat16)
        grad_down = left_product(activated, grad_m_low)
        grad_bias_down = jnp.sum(grad_m_low.astype(jnp.float32), axis=0)
        grad_act = right_product(grad_m_low, w_down)
        up_proj = kept_up
        unused_out, gelu_back = jax.vjp(gelu_exact, up_proj)
        grad_up_low = gelu_back(grad_act)[0].astype(jnp.bfloat16)
        grad_up = left_product(normed2_low, grad_up_low)
        grad_bias_up = jnp.sum(grad_up_low.astype(jnp.float32), axis=0)
        grad_normed2 = right_product(grad_up_low, w_up)
        unused_ln, norm_back = jax.vjp(layer_norm, middle, gain_two, shift_two)
        part_middle, grad_gain_two, grad_shift_two = norm_back(grad_normed2)
        grad_middle = grad_hidden + lax.psum(part_middle.astype(jnp.bfloat16), "tensor").astype(
            jnp.float32
        )
        grad_a_low = grad_middle.astype(jnp.bfloat16)
        grad_out = left_product(mixed_low, grad_a_low)
        grad_bias_out = jnp.sum(grad_a_low.astype(jnp.float32), axis=0)
        grad_mixed = right_product(grad_a_low, w_out).astype(jnp.bfloat16)
        grad_query, grad_keys, grad_values = attend_back(
            queries, key_rows, value_rows, segment, log_total, grad_mixed
        )
        grad_q_low = grad_query.astype(jnp.bfloat16)
        grad_v_low = grad_values.astype(jnp.bfloat16)
        grad_qkv_low = jnp.concatenate(
            [grad_q_low, grad_keys.astype(jnp.bfloat16), grad_v_low], axis=1
        )
        grad_qkv = left_product(normed_low, grad_qkv_low)
        grad_bias_q = jnp.sum(grad_q_low.astype(jnp.float32), axis=0)
        grad_bias_v = jnp.sum(grad_v_low.astype(jnp.float32), axis=0)
        grad_normed = right_product(grad_qkv_low, w_qkv)
        unused_ln1, norm_back1 = jax.vjp(layer_norm, hidden_in, gain_one, shift_one)
        part_input, grad_gain_one, grad_shift_one = norm_back1(grad_normed)
        grad_hidden = grad_middle + lax.psum(part_input.astype(jnp.bfloat16), "tensor").astype(
            jnp.float32
        )
        layer_mats[layer_idx] = [grad_qkv, grad_out, grad_up, grad_down]
        layer_grads[layer_idx] = [
            grad_gain_one,
            grad_shift_one,
            grad_bias_q,
            grad_bias_v,
            grad_bias_out,
            grad_gain_two,
            grad_shift_two,
            grad_bias_up,
            grad_bias_down,
        ]
    grad_emb = lax.dynamic_slice_in_dim(grad_hidden, tensor_pos * part_d, part_d, 1)
    grad_emb_low = grad_emb.astype(jnp.bfloat16)
    grad_emb_bias = jnp.sum(grad_emb_low.astype(jnp.float32), axis=0)
    select_low = select_f.astype(jnp.bfloat16)
    spread = (grad_emb_low[:, None, :] * select_low[:, :, None]).reshape(tokens_n, 3 * part_d)
    grad_resized_low = left_product(patches, spread).astype(jnp.bfloat16)
    grad_base = jnp.zeros((BASE_PIX, part_d), jnp.float32)
    for size_idx in range(3):
        grad_base = grad_base + jnp.dot(
            pinv[size_idx],
            grad_resized_low[:, size_idx * part_d : (size_idx + 1) * part_d],
            preferred_element_type=jnp.float32,
        )
    grad_pixels = right_product(spread, resized_cat) * valid_rows[:, None]
    patch_grad = lax.psum_scatter(
        grad_pixels.astype(jnp.bfloat16), "tensor", scatter_dimension=1, tiled=True
    ).astype(jnp.float32)
    vector_grads = [grad_emb_bias]
    for layer_idx in range(LAYERS):
        vector_grads += layer_grads[layer_idx]
    vec_grad = jnp.concatenate(vector_grads)
    vec_grad = jnp.pad(vec_grad, (0, vec_full.shape[0] - vec_grad.shape[0]))
    matrix_grads = [grad_base]
    for layer_idx in range(LAYERS):
        matrix_grads += layer_mats[layer_idx]
    tiles_all = jnp.concatenate([to_tiles(matrix) for matrix in matrix_grads], axis=0)
    buffer = jnp.zeros(slot_tiles.shape, jnp.float32).at[slot_list].set(tiles_all)
    owned_grad, owned_vec_grad = (
        lax.psum_scatter(buffer, "dp", scatter_dimension=0, tiled=True),
        lax.psum_scatter(vec_grad, "dp", scatter_dimension=0, tiled=True),
    )
    new_master, new_mom, new_var = rotate_step(
        master_slots[0], owned_grad, left_basis[0], right_basis[0], mom_slots[0], var_slots[0]
    )
    new_vec_mom = decay * vec_mom[0] + (1.0 - decay) * owned_vec_grad
    new_vec_var = decay * vec_var[0] + (1.0 - decay) * owned_vec_grad * owned_vec_grad
    new_vec = vec_master[0] - vector_rate * new_vec_mom / (jnp.sqrt(new_vec_var) + adam_eps)
    return (
        output,
        patch_grad,
        owned_grad[None],
        new_master[None],
        new_mom[None],
        new_var[None],
        owned_vec_grad[None],
        new_vec[None],
        new_vec_mom[None],
        new_vec_var[None],
    )


def solution(mesh):
    in_specs = (
        P("dp", None),
        P("dp", None),
        P("dp", None),
        P("tensor", None),
        P(),
        P("tensor", "dp", None, None),
        P("tensor", "dp", None, None),
        P("tensor", "dp", None, None),
        P("tensor", "dp", None, None),
        P("tensor", "dp", None, None),
        P("tensor", "dp"),
        P("tensor", "dp"),
        P("tensor", "dp"),
    )
    out_specs = (
        P("dp", None),
        P("dp", "tensor"),
        P("tensor", "dp", None, None),
        P("tensor", "dp", None, None),
        P("tensor", "dp", None, None),
        P("tensor", "dp", None, None),
        P("tensor", "dp"),
        P("tensor", "dp"),
        P("tensor", "dp"),
        P("tensor", "dp"),
    )
    return jax.shard_map(shards, mesh=mesh, in_specs=in_specs, out_specs=out_specs, check_vma=False)
```

profile of v0, /device:TPU:0, one launch (start us, length us, event | category | flops | bytes accessed | tf_op | source)
XLA Modules:
  0.0 1725.3 jit_solution(16279752057979960152)
XLA Ops:
  10.3 23.7 %all-gather = bf16[16,1,896]{2,1,0:T(2,128)(2,1)S(1)} all-gather(bf16[1,1,896]{2,1,0:T(2,128)(2,1)S(1)} %reshape.672), channel_id=1, replica_groups=mesh['dp'=16,'tensor'=2] {'dp'}, dimensions={0}, use_global_device_ids=true | all-gather | bytes 30464 | tf_op jit(solution)/shard_map/all_gather | solution.py:229
  35.7 104.8 %all-gather.4.cloned.1.call-done = bf16[512,128,128]{2,1,0:T(8,128)(2,1)} async-done(((bf16[32,128,128]{2,1,0:T(8,128)(2,1)}), bf16[512,128,128]{2,1,0:T(8,128)(2,1)}) %all-gather.4.cloned.1.call-update) | async-done | bytes 16777232 | tf_op jit(solution)/shard_map/all_gather | solution.py:226
  140.4 19.6 %gather_fusion = bf16[504,128,128]{2,1,0:T(8,128)(2,1)} fusion(bf16[512,128,128]{2,1,0:T(8,128)(2,1)} %all-gather.4.cloned.1.call-done, s32[1024]{0:T(1024)S(1)} %pad_clamp_fusion), kind=kCustom, calls=%fused_computation | custom fusion | bytes 33032160 | tf_op jit(solution)/shard_map/jit(_take)/gather | solution.py:234
  160.1 9.7 broadcast_select_fusion
  220.3 12.4 all-gather.6.cloned.1.call-done
  254.1 39.5 %while.54 = (s32[]{:T(128)}, bf16[2,512,384]{2,1,0:T(8,128)(2,1)}, f32[2,6,512]{2,1,0:T(8,128)S(1)}, s32[2,512]{1,0:T(2,128)S(1)}, s32[1024]{0:T(1024)S(1)}, /*i...) while((s32[]{:T(128)}, bf16[2,512,384]{2,1,0:T(8,128)(2,1)}, ...), condition=%wide.region_9.10_spmd, body=%wide.region_6.9_spmd.sunk | while | flops 843576320 | bytes 47044752 | solution.py:140
  306.8 42.4 %all-reduce.11.cloned.1.call-done = bf16[1024,768]{1,0:T(8,128)(2,1)} async-done(((bf16[1024,768]{1,0:T(8,128)(2,1)}), bf16[1024,768]{1,0:T(8,128)(2,1)}) %all-reduce.11.cloned.1.call-update) | async-done | bytes 1572880 | tf_op jit(solution)/shard_map/psum | solution.py:273
  353.4 19.1 %multiply_convert_fusion.3 = (bf16[1024,1536]{1,0:T(8,128)(2,1)S(1)}, f32[1024,1536]{1,0:T(8,128)}, f32[1024,1536]{1,0:T(8,128)}) fusion(f32[1536]{0:T(1024)S(1)} %get-tuple-element.629, bf16[96,8,12,128]{3,2,1,0:T(8,128)(2,1)S(1)} %bitcast.512, bf16[1024,768]{1,0:T(8,128)(2,1)S(1)} %copy-done.20, bf16[1024,768]{1,0:T(8,128)(2,1)S(1)} %copy-done.6, ...), kind=kOutput, calls=%fused_computation.152 | convolution fusion | flops 2526019584 | bytes 21254144 | tf_op jit(solution)/shard_map/dot_general | solution.py:278
  383.7 45.7 %all-reduce.13.cloned.1.call-done = bf16[1024,768]{1,0:T(8,128)(2,1)} async-done(((bf16[1024,768]{1,0:T(8,128)(2,1)}), bf16[1024,768]{1,0:T(8,128)(2,1)}) %all-reduce.13.cloned.1.call-update) | async-done | bytes 1572880 | tf_op jit(solution)/shard_map/psum | solution.py:281
  451.1 28.8 %while.55 = (s32[]{:T(128)}, bf16[2,512,384]{2,1,0:T(8,128)(2,1)}, f32[2,6,512]{2,1,0:T(8,128)S(1)}, s32[2,512]{1,0:T(2,128)S(1)}, s32[1024]{0:T(1024)S(1)}, /*i...) while((s32[]{:T(128)}, bf16[2,512,384]{2,1,0:T(8,128)(2,1)}, ...), condition=%wide.region_19.20_spmd, body=%wide.region_16.19_spmd.sunk | while | flops 843576320 | bytes 47044752 | solution.py:140
  492.1 43.0 %all-reduce.15.cloned.1.call-done = bf16[1024,768]{1,0:T(8,128)(2,1)} async-done(((bf16[1024,768]{1,0:T(8,128)(2,1)}), bf16[1024,768]{1,0:T(8,128)(2,1)}) %all-reduce.15.cloned.1.call-update) | async-done | bytes 1572880 | tf_op jit(solution)/shard_map/psum | solution.py:273
  540.9 19.1 %multiply_convert_fusion.2 = (bf16[1024,1536]{1,0:T(8,128)(2,1)}, f32[1024,1536]{1,0:T(8,128)}, f32[1024,1536]{1,0:T(8,128)}) fusion(f32[1536]{0:T(1024)S(1)} %copy-done.115, bf16[96,8,12,128]{3,2,1,0:T(8,128)(2,1)S(1)} %bitcast.518, f32[1024,768]{1,0:T(8,128)S(1)} %get-tuple-element.603, f32[768]{0:T(1024)S(1)} %copy-done.123, f32[768]{0:T(1024)S(1)} %copy-done.93, ...), kind=kOutput, calls=%fused_computation.139 | convolution fusion | flops 2523660288 | bytes 21254144 | tf_op jit(solution)/shard_map/dot_general | solution.py:278
  560.0 8.5 convert_reduce_fusion
  575.2 51.6 %all-reduce.17.cloned.1.call-done = bf16[1024,768]{1,0:T(8,128)(2,1)} async-done(((bf16[1024,768]{1,0:T(8,128)(2,1)}), bf16[1024,768]{1,0:T(8,128)(2,1)}) %all-reduce.17.cloned.1.call-update) | async-done | bytes 1572880 | tf_op jit(solution)/shard_map/psum | solution.py:335
  641.8 145.6 %while.56 = (s32[]{:T(128)}, f32[1024,6,64]{0,2,1:T(8,128)}, f32[1024,6,64]{0,2,1:T(8,128)}, bf16[2,512,384]{2,1,0:T(8,128)(2,1)}, bf16[2,512,6,64]{1,3,2,0:T(8,...) while((s32[]{:T(128)}, f32[1024,6,64]{0,2,1:T(8,128)}, ...), condition=%wide.region_29.30_spmd.clone, body=%wide.region_27.29_spmd.clone.sunk | while | flops 2116034560 | bytes 184776944 | solution.py:185
  650.8 6.4 fusion.446
  657.2 26.6 %fusion.448 = bf16[6,512,64]{1,2,0:T(8,128)(2,1)} fusion(bf16[1024,6,64]{0,2,1:T(8,128)(2,1)S(1)} %get-tuple-element.988, f32[6,512,1024]{2,1,0:T(8,128)} %fusion.446, f32[6,512,1024]{2,1,0:T(8,128)} %copy-done.1, f32[6,512]{1,0:T(8,128)S(1)} %dynamic-slice_bitcast_fusion.4, pred[512,1024]{1,0:T(8,128)(4,1)S(1)} %broadcast_compare_fusion.10), kind=kOutput, calls=%fused_computation.46.clone.1 | convolution fusion | flops 446697472 | bytes 26882048 | tf_op jit(solution)/shard_map/while/body/eval_jaxpr/hqk,khd->qhd/dot_general | solution.py:170
  683.7 28.0 %bitcast_add_fusion.8 = f32[1024,6,64]{0,2,1:T(8,128)} fusion(f32[1024,6,64]{0,2,1:T(8,128)} %get-tuple-element.969, f32[6,512,1024]{2,1,0:T(8,128)} %fusion.446, f32[6,512,1024]{2,1,0:T(8,128)} %copy-done.1, f32[6,512]{1,0:T(8,128)S(1)} %dynamic-slice_bitcast_fusion.4, pred[512,1024]{1,0:T(8,128)(4,1)S(1)} %broadcast_compare_fusion.10, ...), kind=kOutput, calls=%fused_computation.53.clone.1 | convolution fusion | flops 447483904 | bytes 54951940 | tf_op jit(solution)/shard_map/while/body/eval_jaxpr/hqk,qhd->khd/dot_general | solution.py:173
  717.1 6.7 bitcast_add_fusion.9
  723.8 6.4 fusion.446
  730.2 26.6 %fusion.448 = bf16[6,512,64]{1,2,0:T(8,128)(2,1)} fusion(bf16[1024,6,64]{0,2,1:T(8,128)(2,1)S(1)} %get-tuple-element.988, f32[6,512,1024]{2,1,0:T(8,128)} %fusion.446, f32[6,512,1024]{2,1,0:T(8,128)} %copy-done.1, f32[6,512]{1,0:T(8,128)S(1)} %dynamic-slice_bitcast_fusion.4, pred[512,1024]{1,0:T(8,128)(4,1)S(1)} %broadcast_compare_fusion.10), kind=kOutput, calls=%fused_computation.46.clone.1 | convolution fusion | flops 446697472 | bytes 26882048 | tf_op jit(solution)/shard_map/while/body/eval_jaxpr/hqk,khd->qhd/dot_general | solution.py:170
  756.8 28.5 %bitcast_add_fusion.8 = f32[1024,6,64]{0,2,1:T(8,128)} fusion(f32[1024,6,64]{0,2,1:T(8,128)} %get-tuple-element.969, f32[6,512,1024]{2,1,0:T(8,128)} %fusion.446, f32[6,512,1024]{2,1,0:T(8,128)} %copy-done.1, f32[6,512]{1,0:T(8,128)S(1)} %dynamic-slice_bitcast_fusion.4, pred[512,1024]{1,0:T(8,128)(4,1)S(1)} %broadcast_compare_fusion.10, ...), kind=kOutput, calls=%fused_computation.53.clone.1 | convolution fusion | flops 447483904 | bytes 54951940 | tf_op jit(solution)/shard_map/while/body/eval_jaxpr/hqk,qhd->khd/dot_general | solution.py:173
  797.6 6.6 multiply_reduce_fusion.4
  810.7 48.0 %all-reduce.19.cloned.1.call-done = bf16[1024,768]{1,0:T(8,128)(2,1)} async-done(((bf16[1024,768]{1,0:T(8,128)(2,1)}), bf16[1024,768]{1,0:T(8,128)(2,1)}) %all-reduce.19.cloned.1.call-update) | async-done | bytes 1572880 | tf_op jit(solution)/shard_map/psum | solution.py:356
  862.7 8.8 convert_reduce_fusion.1
  879.1 8.0 fusion.327
  887.1 6.7 reshape.652
  893.8 6.7 copy.229
  905.1 6.6 reshape.654
  921.6 8.6 all-reduce.21.cloned.1.call-done
  946.9 145.6 %while.57 = (s32[]{:T(128)}, f32[1024,6,64]{0,2,1:T(8,128)}, f32[1024,6,64]{0,2,1:T(8,128)}, bf16[2,512,384]{2,1,0:T(8,128)(2,1)}, bf16[2,512,6,64]{1,3,2,0:T(8,...) while((s32[]{:T(128)}, f32[1024,6,64]{0,2,1:T(8,128)}, ...), condition=%wide.region_38.39_spmd.clone, body=%wide.region_36.38_spmd.clone.sunk | while | flops 2116034560 | bytes 184776944 | solution.py:185
  955.7 6.4 fusion.461
  962.1 26.6 %fusion.463 = bf16[6,512,64]{1,2,0:T(8,128)(2,1)} fusion(bf16[1024,6,64]{0,2,1:T(8,128)(2,1)S(1)} %get-tuple-element.1027, f32[6,512,1024]{2,1,0:T(8,128)} %fusion.461, f32[6,512,1024]{2,1,0:T(8,128)} %copy-done.2, f32[6,512]{1,0:T(8,128)S(1)} %dynamic-slice_bitcast_fusion.5, pred[512,1024]{1,0:T(8,128)(4,1)S(1)} %broadcast_compare_fusion.11), kind=kOutput, calls=%fused_computation.94.clone.1 | convolution fusion | flops 446697472 | bytes 26882048 | tf_op jit(solution)/shard_map/while/body/eval_jaxpr/hqk,khd->qhd/dot_general | solution.py:170
  988.6 28.0 %bitcast_add_fusion.10 = f32[1024,6,64]{0,2,1:T(8,128)} fusion(f32[1024,6,64]{0,2,1:T(8,128)} %get-tuple-element.1008, f32[6,512,1024]{2,1,0:T(8,128)} %fusion.461, f32[6,512,1024]{2,1,0:T(8,128)} %copy-done.2, f32[6,512]{1,0:T(8,128)S(1)} %dynamic-slice_bitcast_fusion.5, pred[512,1024]{1,0:T(8,128)(4,1)S(1)} %broadcast_compare_fusion.11, ...), kind=kOutput, calls=%fused_computation.101.clone.1 | convolution fusion | flops 447483904 | bytes 54951940 | tf_op jit(solution)/shard_map/while/body/eval_jaxpr/hqk,qhd->khd/dot_general | solution.py:173
  1022.0 6.7 bitcast_add_fusion.11
  1028.7 6.4 fusion.461
  1035.1 26.6 %fusion.463 = bf16[6,512,64]{1,2,0:T(8,128)(2,1)} fusion(bf16[1024,6,64]{0,2,1:T(8,128)(2,1)S(1)} %get-tuple-element.1027, f32[6,512,1024]{2,1,0:T(8,128)} %fusion.461, f32[6,512,1024]{2,1,0:T(8,128)} %copy-done.2, f32[6,512]{1,0:T(8,128)S(1)} %dynamic-slice_bitcast_fusion.5, pred[512,1024]{1,0:T(8,128)(4,1)S(1)} %broadcast_compare_fusion.11), kind=kOutput, calls=%fused_computation.94.clone.1 | convolution fusion | flops 446697472 | bytes 26882048 | tf_op jit(solution)/shard_map/while/body/eval_jaxpr/hqk,khd->qhd/dot_general | solution.py:170
  1061.7 28.5 %bitcast_add_fusion.10 = f32[1024,6,64]{0,2,1:T(8,128)} fusion(f32[1024,6,64]{0,2,1:T(8,128)} %get-tuple-element.1008, f32[6,512,1024]{2,1,0:T(8,128)} %fusion.461, f32[6,512,1024]{2,1,0:T(8,128)} %copy-done.2, f32[6,512]{1,0:T(8,128)S(1)} %dynamic-slice_bitcast_fusion.5, pred[512,1024]{1,0:T(8,128)(4,1)S(1)} %broadcast_compare_fusion.11, ...), kind=kOutput, calls=%fused_computation.101.clone.1 | convolution fusion | flops 447483904 | bytes 54951940 | tf_op jit(solution)/shard_map/while/body/eval_jaxpr/hqk,qhd->khd/dot_general | solution.py:173
  1110.5 6.8 fusion.289
  1134.0 7.1 fusion.328
  1141.1 6.7 reshape.645
  1147.8 6.6 copy.223
  1158.8 6.9 reshape.647
  1175.4 6.2 fusion.288
  1261.9 11.3 broadcast_in_dim.211
  1273.2 92.6 %scatter_fusion = f32[512,128,128]{2,1,0:T(8,128)} fusion(f32[512,128,128]{2,1,0:T(8,128)} %broadcast_in_dim.211, s32[504]{0:T(512)S(1)} %bitcast.551, f32[504,128,128]{2,1,0:T(8,128)} %constant_dynamic-update-slice_fusion.4), kind=kCustom, calls=%fused_computation.1 | custom fusion | bytes 99092448 | tf_op jit(solution)/shard_map/scatter | solution.py:397
  1369.8 61.6 %all-reduce.1 = f32[14336]{0:T(1024)S(1)} all-reduce(f32[14336]{0:T(1024)S(1)} %pad.4), channel_id=4, replica_groups=mesh['dp'=16,'tensor'=2] {'dp'}, use_global_device_ids=true, to_apply=%region_64.65.clone | all-reduce | flops 14336 | bytes 114688
  1441.0 257.9 %reduce-scatter.5.cloned.1.call-done = f32[32,128,128]{2,1,0:T(8,128)} async-done(((f32[512,128,128]{2,1,0:T(8,128)}), f32[32,128,128]{2,1,0:T(8,128)}) %reduce-scatter.5.cloned.1.call-update) | async-done | bytes 2097168 | tf_op jit(solution)/shard_map/reduce_scatter | solution.py:399
  (613 shorter events, 474.7 us)
Async XLA Ops:
  7.2 1691.7 %copy-start = (f32[1,32,128,128]{3,2,1,0:T(8,128)S(1)}, f32[1,32,128,128]{3,2,1,0:T(8,128)}, u32[]{:S(2)}) copy-start(f32[1,32,128,128]{3,2,1,0:T(8,128)} %param.27) | copy-start | bytes 6291460
  7.2 26.9 %copy-start.136 = (s32[1,5]{1,0:T(1,128)S(1)}, s32[1,5]{1,0:T(1,128)}, u32[]{:S(2)}) copy-start(s32[1,5]{1,0:T(1,128)} %param.23) | copy-start | bytes 64
  7.2 27.0 %copy-start.110 = (s32[1,504]{1,0:T(1,128)S(1)}, s32[1,504]{1,0:T(1,128)}, u32[]{:S(2)}) copy-start(s32[1,504]{1,0:T(1,128)} %param.24) | copy-start | bytes 6052
  7.2 133.2 %all-gather.4.cloned.1.call-start = ((), (), s32[]{:S(2)}) async-start(), calls=%async_computation.2 | async-start | bytes 17825792 | tf_op jit(solution)/shard_map/all_gather | solution.py:226
  10.2 222.5 %all-gather.6.cloned.1.call-start = ((), (), s32[]{:S(2)}) async-start(), calls=%async_computation.3 | async-start | bytes 2359296 | tf_op jit(solution)/shard_map/all_gather | solution.py:256
  10.2 149.8 %copy-start.78 = (f32[896]{0:T(1024)}, f32[896]{0:T(1024)S(1)}, u32[]{:S(2)}) copy-start(f32[896]{0:T(1024)S(1)} %reduce.4) | copy-start | bytes 10756
  34.3 125.8 %copy-start.81 = (s32[504,1]{0,1:T(1,128)}, s32[504,1]{0,1:T(1,128)S(1)}, u32[]{:S(2)}) copy-start(s32[504,1]{0,1:T(1,128)S(1)} %compare_select_fusion) | copy-start | bytes 6052
  169.8 9.2 copy-start.10
  188.6 9.1 copy-start.146
  207.1 142.0 %all-reduce.11.cloned.1.call-start = ((), (), s32[]{:S(2)}) async-start(), calls=%async_computation.4 | async-start | bytes 3145728 | tf_op jit(solution)/shard_map/psum | solution.py:273
  208.1 28.5 %copy-start.83 = (f32[768]{0:T(1024)}, f32[768]{0:T(1024)S(1)}, u32[]{:S(2)}) copy-start(f32[768]{0:T(1024)S(1)} %get-tuple-element.641) | copy-start | bytes 9220
  208.1 28.5 %copy-start.116 = (f32[768]{0:T(1024)}, f32[768]{0:T(1024)S(1)}, u32[]{:S(2)}) copy-start(f32[768]{0:T(1024)S(1)} %get-tuple-element.640) | copy-start | bytes 9220
  293.7 9.8 copy-start.3
  293.7 9.8 copy-start.56
  297.5 131.9 %all-reduce.13.cloned.1.call-start = ((), (), s32[]{:S(2)}) async-start(), calls=%async_computation.5 | async-start | bytes 3145728 | tf_op jit(solution)/shard_map/psum | solution.py:281
  298.2 55.2 %copy-start.113 = (f32[1536]{0:T(1024)}, f32[1536]{0:T(1024)S(1)}, u32[]{:S(2)}) copy-start(f32[1536]{0:T(1024)S(1)} %get-tuple-element.629) | copy-start | bytes 18436
  306.8 46.6 %copy-start.87 = (f32[768]{0:T(1024)S(1)}, f32[768]{0:T(1024)}, u32[]{:S(2)}) copy-start(f32[768]{0:T(1024)} %get-tuple-element.638) | copy-start | bytes 9220
  306.8 46.6 %copy-start.118 = (f32[768]{0:T(1024)S(1)}, f32[768]{0:T(1024)}, u32[]{:S(2)}) copy-start(f32[768]{0:T(1024)} %get-tuple-element.637) | copy-start | bytes 9220
  352.0 20.4 %copy-start.64 = (f32[1024]{0:T(1024)}, f32[1024]{0:T(1024)S(1)}, u32[]{:S(2)}) copy-start(f32[1024]{0:T(1024)S(1)} %broadcast_multiply_fusion.3) | copy-start | bytes 12292
  352.7 19.7 %copy-start.95 = (f32[1024]{0:T(1024)}, f32[1024]{0:T(1024)S(1)}, u32[]{:S(2)}) copy-start(f32[1024]{0:T(1024)S(1)} %fusion.308) | copy-start | bytes 12292
  353.3 20.7 %copy-start.40 = (bf16[12,6,128,128]{3,1,2,0:T(8,128)(2,1)S(1)}, bf16[12,6,128,128]{3,1,2,0:T(8,128)(2,1)}, u32[]{:S(2)}) copy-start(bf16[12,6,128,128]{3,1,2,0:T(8,128)(2,1)} %copy.195) | copy-start | bytes 7077892
  353.3 20.7 %copy-start.126 = (f32[768]{0:T(1024)S(1)}, f32[768]{0:T(1024)}, u32[]{:S(2)}) copy-start(f32[768]{0:T(1024)} %get-tuple-element.636) | copy-start | bytes 9220
  377.7 157.3 %all-reduce.15.cloned.1.call-start = ((), (), s32[]{:S(2)}) async-start(), calls=%async_computation.6 | async-start | bytes 3145728 | tf_op jit(solution)/shard_map/psum | solution.py:273
  451.1 28.8 %copy-start.125 = (f32[768]{0:T(1024)S(1)}, f32[768]{0:T(1024)}, u32[]{:S(2)}) copy-start(f32[768]{0:T(1024)} %get-tuple-element.633) | copy-start | bytes 9220
  483.4 143.4 %all-reduce.17.cloned.1.call-start = ((), (), s32[]{:S(2)}) async-start(), calls=%async_computation.7 | async-start | bytes 3145728 | tf_op jit(solution)/shard_map/psum | solution.py:335
  483.5 143.3 %copy-start.59 = (f32[1024]{0:T(1024)}, f32[1024]{0:T(1024)S(1)}, u32[]{:S(2)}) copy-start(f32[1024]{0:T(1024)S(1)} %compare_convert_fusion) | copy-start | bytes 12292
  537.8 34.4 %copy-start.11 = (f32[1024,768]{1,0:T(8,128)}, f32[1024,768]{1,0:T(8,128)S(1)}, u32[]{:S(2)}) copy-start(f32[1024,768]{1,0:T(8,128)S(1)} %get-tuple-element.603) | copy-start | bytes 9437188
  537.9 34.4 %copy-start.70 = (f32[1024]{0:T(1024)}, f32[1024]{0:T(1024)S(1)}, u32[]{:S(2)}) copy-start(f32[1024]{0:T(1024)S(1)} %broadcast_multiply_fusion.1) | copy-start | bytes 12292
  538.4 33.8 %copy-start.104 = (f32[1024]{0:T(1024)}, f32[1024]{0:T(1024)S(1)}, u32[]{:S(2)}) copy-start(f32[1024]{0:T(1024)S(1)} %fusion.310) | copy-start | bytes 12292
  540.9 19.1 %copy-start.25 = (bf16[1024,768]{1,0:T(8,128)(2,1)S(1)}, bf16[1024,768]{1,0:T(8,128)(2,1)}, u32[]{:S(2)}) copy-start(bf16[1024,768]{1,0:T(8,128)(2,1)} %param.22) | copy-start | bytes 4718596
  540.9 19.1 %copy-start.42 = (bf16[12,6,128,128]{3,1,2,0:T(8,128)(2,1)S(1)}, bf16[12,6,128,128]{3,1,2,0:T(8,128)(2,1)}, u32[]{:S(2)}) copy-start(bf16[12,6,128,128]{3,1,2,0:T(8,128)(2,1)} %copy.204) | copy-start | bytes 7077892
  575.2 283.6 %all-reduce.19.cloned.1.call-start = ((), (), s32[]{:S(2)}) async-start(), calls=%async_computation.8 | async-start | bytes 3145728 | tf_op jit(solution)/shard_map/psum | solution.py:356
  807.0 51.7 %copy-start.60 = (f32[1024]{0:T(1024)S(1)}, f32[1024]{0:T(1024)}, u32[]{:S(2)}) copy-start(f32[1024]{0:T(1024)} %copy-done.59) | copy-start | bytes 12292
  807.1 123.2 %all-reduce.21.cloned.1.call-start = ((), (), s32[]{:S(2)}) async-start(), calls=%async_computation.9 | async-start | bytes 3145728 | tf_op jit(solution)/shard_map/psum | solution.py:335
  810.7 52.0 %copy-start.114 = (f32[1536]{0:T(1024)S(1)}, f32[1536]{0:T(1024)}, u32[]{:S(2)}) copy-start(f32[1536]{0:T(1024)} %copy-done.113) | copy-start | bytes 18436
  862.6 8.9 copy-start.51
  862.7 8.9 copy-start.7
  862.7 8.9 copy-start.21
  862.7 8.9 copy-start.39
  862.7 8.9 copy-start.65
  862.7 8.9 copy-start.88
  862.7 8.9 copy-start.96
  878.6 317.9 %all-reduce.23.cloned.1.call-start = ((), (), s32[]{:S(2)}) async-start(), calls=%async_computation.12 | async-start | bytes 6291456 | tf_op jit(solution)/shard_map/psum | solution.py:281
  921.6 14.7 copy-start.45
  1110.4 327.8 %reduce-scatter.7.cloned.1.call-start = ((), (), s32[]{:S(2)}) async-start(), calls=%async_computation.11 | async-start | bytes 2359296
  1213.8 485.1 %reduce-scatter.5.cloned.1.call-start = ((), (), s32[]{:S(2)}) async-start(), calls=%async_computation.10 | async-start | bytes 35651584 | tf_op jit(solution)/shard_map/reduce_scatter | solution.py:399
  1261.9 11.3 copy-start.82
  1366.0 65.4 %copy-start.79 = (f32[896]{0:T(1024)S(1)}, f32[896]{0:T(1024)}, u32[]{:S(2)}) copy-start(f32[896]{0:T(1024)} %copy-done.78) | copy-start | bytes 10756
  (128 other events, 524.6 us)
Sparse Core Ops, SparseCore 0:
  10.8 129.6 all-gather.3
  207.2 25.3 all-gather.5
  297.6 51.4 all-reduce.10
  377.9 51.4 all-reduce.12
  483.6 51.4 all-reduce.14
  575.3 51.4 all-reduce.16
  807.2 51.4 all-reduce.18
  878.7 51.4 all-reduce.20
  1110.5 85.9 all-reduce.22
  1213.9 26.0 reduce-scatter.6
  1366.1 332.7 reduce-scatter.4
where the time goes:
time: 1740 us; the launch traced here: 1730 us
  waiting for transfers between devices  615 us (35%)
  matrix products  513 us (29%)
  local copies, waits for them, and re-layouts  381 us (22%)
  other arithmetic  100 us (6%)
  blocking collectives  85.3 us (5%)
    reduce_scatter x1, waiting for transfers between devices, shards(): lax.psum_scatter(buffer, 'dp', scatter_dimension=0, tiled=True)  258 us
    dot_general x4, matrix products, one_block(): jnp.einsum('hqk,qhd->khd', grad_scores, query_blk, preferred_element_type...  113 us
    dot_general x4, matrix products, one_block(): jnp.einsum('hqk,khd->qhd', grad_scores, key_heads, preferred_element_type...  106 us
    all_gather x1, waiting for transfers between devices, shards(): lax.all_gather(master_slots[0].astype(jnp.bfloat16), 'dp', axis=0, tiled=...  105 us
    scatter x1, local copies, waits for them, and re-layouts, shards(): jnp.zeros(slot_tiles.shape, jnp.float32).at[slot_list].set(tiles_all)  92.6 us
    psum x2, waiting for transfers between devices, shards(): lax.psum(partial_value.astype(jnp.bfloat16).astype(jnp.float32).astype(jn...  85.3 us
    unnamed x1, blocking collectives  61.6 us
    psum x2, waiting for transfers between devices, shards(): lax.psum(part_middle.astype(jnp.bfloat16), 'tensor').astype(jnp.float32)  60.2 us
  transfers between devices with their start and end apart: 11, of which 10 were waited for; matrix products, arithmetic and copies ran while one was open for 19% of the time, Pallas kernels for 0%

commit v1 on v0

v1 whole, which is shorter than its diff:
```python
import functools

import jax
import jax.numpy as jnp
import numpy as np
from jax import lax
from jax.experimental import pallas as pl
from jax.experimental.pallas import tpu as pltpu
from jax.sharding import PartitionSpec as P

D = 768
HEAD_DIM = 64
FF = 3072
BASE_PIX = 3072
LAYERS = 2
LEN_A = 196
LEN_B = 225
LEN_C = 576
IMG_DEV = 5
BS = 128
TENSOR = 2
HALF = D // TENSOR
HALF_FF = FF // TENSOR
HEADS = HALF // HEAD_DIM
ROWS = 256
VEC_ROWS = 16

AXES = ("dp", "tensor")
precise = lax.Precision.HIGHEST
masked_score = -1e30
norm_eps = 1e-06
adam_eps = 1e-08
decay = 0.5
matrix_rate = 0.05
vector_rate = 0.3
f32 = jnp.float32
bf16 = jnp.bfloat16
BIG_VMEM = 56 * 1024 * 1024

PANELS = {
    "up": (0, 6144),
    "down": (3072, 9216),
    "base": 12288,
    "out": (15360, 20736),
    "qkv": (16128, 18432),
}
PANEL_ROWS = 21504


def tile_targets():
    rows, cols = [], []

    def add(start, rows_n, cols_n):
        for i in range(rows_n // BS):
            for j in range(cols_n // BS):
                panel, inner = divmod(j * BS, HALF)
                rows.append(start + panel * rows_n + i * BS)
                cols.append(inner)

    add(PANELS["base"], BASE_PIX, HALF)
    for layer in range(LAYERS):
        add(PANELS["qkv"][layer], D, 3 * HALF)
        add(PANELS["out"][layer], HALF, D)
        add(PANELS["up"][layer], D, HALF_FF)
        add(PANELS["down"][layer], HALF_FF, D)
    return np.array(rows, np.int32), np.array(cols, np.int32)


TARGET_ROW, TARGET_COL = tile_targets()
LAYER_VECS = (D, D, HALF, HALF, D, D, D, HALF_FF, D)
VEC_NAMES = ("g1", "s1", "bq", "bv", "bo", "g2", "s2", "b1", "b2")


def vec_offsets():
    offset = HALF
    found = []
    for layer in range(LAYERS):
        here = {}
        for name, length in zip(VEC_NAMES, LAYER_VECS):
            here[name] = (offset, length)
            offset += length
        found.append(here)
    return found


VEC_AT = vec_offsets()


def params(limit=BIG_VMEM):
    return pltpu.CompilerParams(
        dimension_semantics=("arbitrary",), vmem_limit_bytes=limit
    )


def cost(flops, nbytes, trans=0):
    return pl.CostEstimate(flops=flops, bytes_accessed=nbytes, transcendentals=trans)


def rows_spec(width):
    return pl.BlockSpec((ROWS, width), lambda i, *_: (i, 0))


def fixed(shape, at=0):
    return pl.BlockSpec(shape, lambda i, *_: (at,) + (0,) * (len(shape) - 1))


def vec_piece(vec_ref, layer, name):
    start, length = VEC_AT[layer][name]
    return vec_ref[:, start : start + length]


def dot(left, right):
    return jnp.dot(left, right, preferred_element_type=f32)


def dot_nt(left, right, precision=None):
    return lax.dot_general(
        left, right, (((1,), (1,)), ((), ())), precision=precision, preferred_element_type=f32
    )


def dot_tn(left, right):
    return lax.dot_general(left, right, (((0,), (0,)), ((), ())), preferred_element_type=f32)


def norm_stats(values):
    mean_val = jnp.mean(values, axis=-1, keepdims=True)
    centered = values - mean_val
    inv_std = lax.rsqrt(jnp.mean(centered * centered, axis=-1, keepdims=True) + norm_eps)
    return centered * inv_std, inv_std


def norm_back(values, gain, grad):
    unit, inv_std = norm_stats(values)
    scaled = grad * gain
    mean_s = jnp.mean(scaled, axis=-1, keepdims=True)
    mean_u = jnp.mean(scaled * unit, axis=-1, keepdims=True)
    back = inv_std * (scaled - mean_s - unit * mean_u)
    return (
        back,
        jnp.sum(grad * unit, axis=0, keepdims=True),
        jnp.sum(grad, axis=0, keepdims=True),
    )


def accumulate(ref, value):
    first = pl.program_id(0) == 0

    @pl.when(first)
    def _():
        ref[...] = value

    @pl.when(jnp.logical_not(first))
    def _():
        ref[...] += value


def fence(*arrays):
    def nothing(*refs):
        pass

    anywhere = pl.BlockSpec(memory_space=pl.ANY)
    return pl.pallas_call(
        nothing,
        out_shape=[jax.ShapeDtypeStruct(a.shape, a.dtype) for a in arrays],
        in_specs=[anywhere] * len(arrays),
        out_specs=[anywhere] * len(arrays),
        input_output_aliases={i: i for i in range(len(arrays))},
    )(*arrays)


def gather_kernel(slots, count_a, count_b, owner, drow, dcol, flag, *refs):
    first = refs[:count_a]
    second = refs[count_a : count_a + count_b]
    panels, vectors, held, sem, vec_sem = refs[count_a + count_b :]

    def copy_all(sources):
        at = 0
        for src in sources:
            for n in range(src.shape[0]):
                who = owner[at]
                at += 1

                def body(i, carried, src=src, n=n, who=who):
                    slot = who * slots + i
                    row = drow[slot]

                    @pl.when(row >= 0)
                    def _():
                        start = pl.multiple_of(i * BS, BS)
                        pltpu.make_async_copy(
                            src.at[n, pl.ds(start, BS), :],
                            held.at[
                                pl.ds(pl.multiple_of(row, BS), BS),
                                pl.ds(pl.multiple_of(dcol[slot], BS), BS),
                            ],
                            sem,
                        ).start()

                    return carried

                lax.fori_loop(0, slots, body, 0)
                pltpu.make_async_copy(
                    src.at[n, pl.ds(slots * BS, VEC_ROWS), :], vectors.at[who], vec_sem
                ).start()

    if count_b:

        @pl.when(flag[0] == 1)
        def _():
            copy_all(first)

        @pl.when(flag[0] == 0)
        def _():
            copy_all(second)
    else:
        copy_all(first)
    pltpu.make_async_copy(held, held, sem).wait()
    out = pltpu.make_async_copy(held, panels, sem)
    out.start()
    pltpu.make_async_copy(vectors, vectors, vec_sem).wait()
    out.wait()


def gather_tiles(first, second, owner, drow, dcol, flag, slots, owners):
    anywhere = pl.BlockSpec(memory_space=pl.ANY)
    return pl.pallas_call(
        functools.partial(gather_kernel, slots, len(first), len(second)),
        out_shape=(
            jax.ShapeDtypeStruct((PANEL_ROWS, HALF), bf16),
            jax.ShapeDtypeStruct((owners, VEC_ROWS, BS), bf16),
        ),
        grid_spec=pltpu.PrefetchScalarGridSpec(
            num_scalar_prefetch=4,
            grid=(1,),
            in_specs=[anywhere] * (len(first) + len(second)),
            out_specs=(anywhere, fixed((owners, VEC_ROWS, BS))),
            scratch_shapes=[
                pltpu.VMEM((PANEL_ROWS, HALF), bf16),
                pltpu.SemaphoreType.DMA,
                pltpu.SemaphoreType.DMA,
            ],
        ),
        compiler_params=params(),
        cost_estimate=cost(0, 4 * PANEL_ROWS * HALF),
    )(owner, drow, dcol, flag, *first, *second)


def scatter_kernel(rows_n, cols_n, paired, parts, pos, part, own, *refs):
    if paired:
        recv, *refs = refs
        span = pl.num_programs(0) // parts
        here = jnp.logical_or(parts == 1, pl.program_id(0) // span == part[0])
    target, buf, sems = refs[-3:]
    step = pl.program_id(0)
    slot = lax.rem(step, 2)
    per = rows_n // BS * (cols_n // BS)

    def wait(at):
        pltpu.make_async_copy(buf.at[at], buf.at[at], sems.at[at]).wait()

    @pl.when(step >= 2)
    def _():
        wait(slot)

    for i in range(rows_n // BS):
        for j in range(cols_n // BS):
            area = (slice(i * BS, (i + 1) * BS), slice(j * BS, (j + 1) * BS))
            value = own[area]
            if paired:
                more = jnp.where(here, recv[area].astype(f32), 0.0)
                value = (value.astype(f32) + more).astype(bf16)
            buf[slot, i * (cols_n // BS) + j] = value
    for n in range(per):
        pltpu.make_async_copy(
            buf.at[slot, n],
            target.at[pl.ds(pl.multiple_of(pos[step * per + n], 16), BS), :],
            sems.at[slot],
        ).start()

    @pl.when(step == pl.num_programs(0) - 1)
    def _():
        wait(1 - slot)
        wait(slot)


def scatter_matrix(pos, own, recv, part, target, total_rows, rows_n):
    cols_n = own.shape[1]
    steps = own.shape[0] // rows_n
    anywhere = pl.BlockSpec(memory_space=pl.ANY)
    block = pl.BlockSpec((rows_n, cols_n), lambda i, *_: (i, 0))
    paired = recv is not None
    parts = own.shape[0] // recv.shape[0] if paired else 1
    span = steps // parts
    arrived = pl.BlockSpec(
        (rows_n, cols_n), lambda i, pos, part: (jnp.clip(i - part[0] * span, 0, span - 1), 0)
    )
    operands = [own] + ([recv] if paired else []) + ([] if target is None else [target])
    specs = [block] + ([block if parts == 1 else arrived] if paired else [])
    specs += [] if target is None else [anywhere]
    return pl.pallas_call(
        functools.partial(scatter_kernel, rows_n, cols_n, paired, parts),
        out_shape=jax.ShapeDtypeStruct((total_rows, BS), bf16),
        grid_spec=pltpu.PrefetchScalarGridSpec(
            num_scalar_prefetch=2,
            grid=(steps,),
            in_specs=specs,
            out_specs=anywhere,
            scratch_shapes=[
                pltpu.VMEM((2, rows_n // BS * (cols_n // BS), BS, BS), bf16),
                pltpu.SemaphoreType.DMA((2,)),
            ],
        ),
        input_output_aliases={} if target is None else {len(operands) + 1: 0},
        compiler_params=params(),
        cost_estimate=cost(own.size, own.size * 6),
    )(pos, part, *operands)


def scatter_vec_kernel(paired, pos, own, *refs):
    if paired:
        recv, *refs = refs
    target, buf, sem = refs[-3:]
    value = own[...]
    if paired:
        value = (value.astype(f32) + recv[...].astype(f32)).astype(bf16)
    buf[...] = value

    def body(n, carried):
        pltpu.make_async_copy(
            buf.at[n], target.at[pl.ds(pl.multiple_of(pos[n], 16), VEC_ROWS), :], sem
        ).start()
        return carried

    lax.fori_loop(0, own.shape[0], body, 0)
    pltpu.make_async_copy(buf, buf, sem).wait()


def scatter_vec(pos, own, recv, target):
    anywhere = pl.BlockSpec(memory_space=pl.ANY)
    block = fixed(own.shape)
    paired = recv is not None
    operands = [own] + ([recv] if paired else []) + [target]
    return pl.pallas_call(
        functools.partial(scatter_vec_kernel, paired),
        out_shape=jax.ShapeDtypeStruct(target.shape, bf16),
        grid_spec=pltpu.PrefetchScalarGridSpec(
            num_scalar_prefetch=1,
            grid=(1,),
            in_specs=[block] * (len(operands) - 1) + [anywhere],
            out_specs=anywhere,
            scratch_shapes=[pltpu.VMEM(own.shape, bf16), pltpu.SemaphoreType.DMA],
        ),
        input_output_aliases={len(operands): 0},
        compiler_params=params(),
    )(pos, *operands)


def qkv_kernel(layer, summed, *refs):
    if summed:
        base, own, recv, vec, weight, hid, normed, q_ref, k_ref, v_ref = refs
        values = base[...] + (own[...].astype(f32) + recv[...].astype(f32))
        hid[...] = values
    else:
        base, vec, weight, normed, q_ref, k_ref, v_ref = refs
        values = base[...]
    unit, unused = norm_stats(values)
    low = (unit * vec_piece(vec, layer, "g1") + vec_piece(vec, layer, "s1")).astype(bf16)
    normed[...] = low
    q_ref[...] = (dot(low, weight[0:D, :]) + vec_piece(vec, layer, "bq")).astype(bf16)
    k_ref[...] = dot(low, weight[D : 2 * D, :]).astype(bf16)
    v_ref[...] = (dot(low, weight[2 * D : 3 * D, :]) + vec_piece(vec, layer, "bv")).astype(bf16)


def qkv_call(layer, base, own, recv, vec, panels):
    tokens = base.shape[0]
    summed = own is not None
    shape = lambda width, kind: jax.ShapeDtypeStruct((tokens, width), kind)
    outs = ([shape(D, f32)] if summed else []) + [shape(D, bf16)] + [shape(HALF, bf16)] * 3
    operands = [base] + ([own, recv] if summed else []) + [vec, panels]
    return pl.pallas_call(
        functools.partial(qkv_kernel, layer, summed),
        out_shape=outs,
        grid=(tokens // ROWS,),
        in_specs=[rows_spec(D)] * (3 if summed else 1)
        + [fixed(vec.shape), fixed((3 * D, HALF), PANELS["qkv"][layer] // (3 * D))],
        out_specs=[rows_spec(o.shape[1]) for o in outs],
        compiler_params=params(),
        cost_estimate=cost(2 * tokens * D * 3 * HALF, tokens * D * 14),
    )(*operands)


def head_masks():
    lane = lax.broadcasted_iota(jnp.int32, (1, 2 * HEAD_DIM), 1)
    low = (lane < HEAD_DIM).astype(f32).astype(bf16)
    high = (lane >= HEAD_DIM).astype(f32).astype(bf16)
    return low, high


def attend_kernel(layer, q_ref, k_ref, v_ref, seg_q, seg_k, vec, w_out, o_ref, lse_ref, part):
    masks = head_masks()
    same = seg_q[...] == seg_k[...]
    lane = lax.broadcasted_iota(jnp.int32, (ROWS, BS), 1)
    totals = jnp.zeros((ROWS, BS), f32)
    scale = jnp.asarray(HEAD_DIM ** (-0.5), bf16)
    for pair in range(HEADS // 2):
        cols = slice(pair * BS, (pair + 1) * BS)
        q_two = q_ref[:, cols] * scale
        k_two = k_ref[:, cols]
        v_two = v_ref[:, cols]
        mixed = None
        for side in range(2):
            scores = dot_nt(q_two * masks[side], k_two)
            scores = jnp.where(same, scores, masked_score)
            top = jnp.max(scores, axis=1, keepdims=True)
            expo = jnp.exp(scores - top)
            total = jnp.sum(expo, axis=1, keepdims=True)
            weights = (expo * (1.0 / total)).astype(bf16)
            term = dot(weights, v_two * masks[side])
            mixed = term if mixed is None else mixed + term
            totals = jnp.where(lane == 2 * pair + side, top + jnp.log(total), totals)
        o_ref[:, cols] = mixed.astype(bf16)
    lse_ref[...] = totals.T[0:8, :]
    low = o_ref[...]
    bias = vec_piece(vec, layer, "bo")
    for panel in range(TENSOR):
        area = slice(panel * HALF, (panel + 1) * HALF)
        part[:, area] = (dot(low, w_out[area, :]) + bias[:, area]).astype(bf16)


def attend_call(layer, queries, keys, values, seg_col, seg_row, vec, panels):
    tokens = queries.shape[0]
    return pl.pallas_call(
        functools.partial(attend_kernel, layer),
        out_shape=[
            jax.ShapeDtypeStruct((tokens, HALF), bf16),
            jax.ShapeDtypeStruct((8, tokens), f32),
            jax.ShapeDtypeStruct((tokens, D), bf16),
        ],
        grid=(tokens // ROWS,),
        in_specs=[
            rows_spec(HALF),
            fixed(keys.shape),
            fixed(values.shape),
            rows_spec(1),
            fixed(seg_row.shape),
            fixed(vec.shape),
            fixed((D, HALF), PANELS["out"][layer] // D),
        ],
        out_specs=[
            rows_spec(HALF),
            pl.BlockSpec((8, ROWS), lambda i: (0, i)),
            rows_spec(D),
        ],
        compiler_params=params(),
        cost_estimate=cost(8 * HEADS * tokens * tokens * BS, tokens * D * 8, HEADS * tokens * tokens),
    )(queries, keys, values, seg_col, seg_row, vec, panels)


def gelu_parts(values):
    cdf = 0.5 * (1.0 + lax.erf(values * 0.7071067811865476))
    pdf = 0.3989422804014327 * jnp.exp(-0.5 * values * values)
    return values * cdf, cdf + values * pdf


def mlp_kernel(layer, base, own, recv, vec, w_up, w_down, hid, normed, act, slope, part):
    values = base[...] + (own[...].astype(f32) + recv[...].astype(f32))
    hid[...] = values
    unit, unused = norm_stats(values)
    low = (unit * vec_piece(vec, layer, "g2") + vec_piece(vec, layer, "s2")).astype(bf16)
    normed[...] = low
    bias_up = vec_piece(vec, layer, "b1")
    for panel in range(HALF_FF // HALF):
        area = slice(panel * HALF, (panel + 1) * HALF)
        up = dot(low, w_up[panel * D : (panel + 1) * D, :]) + bias_up[:, area]
        gelu, grad = gelu_parts(up)
        act[:, area] = gelu.astype(bf16)
        slope[:, area] = grad.astype(bf16)
    bias_down = vec_piece(vec, layer, "b2")
    hidden_units = act[...]
    for panel in range(TENSOR):
        area = slice(panel * HALF, (panel + 1) * HALF)
        down = dot(hidden_units, w_down[panel * HALF_FF : (panel + 1) * HALF_FF, :])
        part[:, area] = (down + bias_down[:, area]).astype(bf16)


def mlp_call(layer, base, own, recv, vec, panels):
    tokens = base.shape[0]
    shape = lambda width, kind: jax.ShapeDtypeStruct((tokens, width), kind)
    outs = [shape(D, f32), shape(D, bf16), shape(HALF_FF, bf16), shape(HALF_FF, bf16), shape(D, bf16)]
    return pl.pallas_call(
        functools.partial(mlp_kernel, layer),
        out_shape=outs,
        grid=(tokens // ROWS,),
        in_specs=[rows_spec(D)] * 3
        + [
            fixed(vec.shape),
            fixed((2 * HALF_FF, HALF), PANELS["up"][layer] // (2 * HALF_FF)),
            fixed((2 * HALF_FF, HALF), PANELS["down"][layer] // (2 * HALF_FF)),
        ],
        out_specs=[rows_spec(o.shape[1]) for o in outs],
        compiler_params=params(),
        cost_estimate=cost(4 * tokens * D * HALF_FF, tokens * D * 24, 2 * tokens * HALF_FF),
    )(base, own, recv, vec, panels, panels)


def mlp_back_kernel(layer, summed, *refs):
    if summed:
        base, own, recv, *refs = refs
        (hid, slope, vec, w_up, w_down, grad_full, grad_low, du_ref, back, dgain, dshift, db1, db2) = refs
        values = base[...].astype(f32) + (own[...].astype(f32) + recv[...].astype(f32))
        grad_full[...] = values
        low = values.astype(bf16)
    else:
        base, valid, *refs = refs
        (hid, slope, vec, w_up, w_down, grad_low, du_ref, back, dgain, dshift, db1, db2) = refs
        low = (base[...].astype(f32) * valid[...]).astype(bf16)
    grad_low[...] = low
    accumulate(db2, jnp.sum(low.astype(f32), axis=0, keepdims=True))
    for part in range(HALF_FF // HALF):
        area = slice(part * HALF, (part + 1) * HALF)
        grad_act = None
        for panel in range(TENSOR):
            start = panel * HALF_FF + part * HALF
            term = dot_nt(low[:, panel * HALF : (panel + 1) * HALF], w_down[start : start + HALF, :])
            grad_act = term if grad_act is None else grad_act + term
        du_ref[:, area] = (grad_act * slope[:, area].astype(f32)).astype(bf16)
    grad_normed = None
    for panel in range(HALF_FF // HALF):
        area = slice(panel * HALF, (panel + 1) * HALF)
        term = dot_nt(du_ref[:, area], w_up[panel * D : (panel + 1) * D, :])
        grad_normed = term if grad_normed is None else grad_normed + term
    accumulate(db1, jnp.sum(du_ref[...].astype(f32), axis=0, keepdims=True))
    part_back, gain_grad, shift_grad = norm_back(hid[...], vec_piece(vec, layer, "g2"), grad_normed)
    back[...] = part_back.astype(bf16)
    accumulate(dgain, gain_grad)
    accumulate(dshift, shift_grad)


def mlp_back_call(layer, base, own, recv, valid, hid, slope, vec, panels):
    tokens = base.shape[0]
    summed = own is not None
    shape = lambda width, kind: jax.ShapeDtypeStruct((tokens, width), kind)
    line = lambda width: jax.ShapeDtypeStruct((1, width), f32)
    outs = ([shape(D, f32)] if summed else []) + [shape(D, bf16), shape(HALF_FF, bf16), shape(D, bf16)]
    lines = [line(D), line(D), line(HALF_FF), line(D)]
    extra = [own, recv] if summed else [valid]
    return pl.pallas_call(
        functools.partial(mlp_back_kernel, layer, summed),
        out_shape=outs + lines,
        grid=(tokens // ROWS,),
        in_specs=[rows_spec(D)]
        + [rows_spec(e.shape[1]) for e in extra]
        + [
            rows_spec(D),
            rows_spec(HALF_FF),
            fixed(vec.shape),
            fixed((2 * HALF_FF, HALF), PANELS["up"][layer] // (2 * HALF_FF)),
            fixed((2 * HALF_FF, HALF), PANELS["down"][layer] // (2 * HALF_FF)),
        ],
        out_specs=[rows_spec(o.shape[1]) for o in outs] + [fixed(o.shape) for o in lines],
        compiler_params=params(),
        cost_estimate=cost(4 * tokens * D * HALF_FF, tokens * D * 24),
    )(base, *extra, hid, slope, vec, panels, panels)


def attend_back_kernel(
    low_ref, high_ref, base, own, recv, q_ref, k_ref, v_ref, o_ref, lse_ref, seg_k, seg_q, w_out,
    full_ref, grad_low, dq_ref, dk_ref, dv_ref, dbo, dk_acc, dv_acc, dq_acc, do_ref,
):
    step = pl.program_id(0)

    @pl.when(step == 0)
    def _():
        dk_acc[...] = jnp.zeros_like(dk_acc)
        dv_acc[...] = jnp.zeros_like(dv_acc)

    values = base[...].astype(f32) + (own[...].astype(f32) + recv[...].astype(f32))
    full_ref[...] = values
    low = values.astype(bf16)
    grad_low[...] = low
    accumulate(dbo, jnp.sum(low.astype(f32), axis=0, keepdims=True))
    grad_mixed = None
    for panel in range(TENSOR):
        area = slice(panel * HALF, (panel + 1) * HALF)
        term = dot_nt(low[:, area], w_out[area, :])
        grad_mixed = term if grad_mixed is None else grad_mixed + term
    do_ref[...] = grad_mixed.astype(bf16)
    product = do_ref[...].astype(f32) * o_ref[...].astype(f32)
    head = lax.broadcasted_iota(jnp.int32, (8, HALF), 0)
    lane = lax.broadcasted_iota(jnp.int32, (8, HALF), 1)
    pick = ((lane >= head * HEAD_DIM) & (lane < (head + 1) * HEAD_DIM)).astype(f32)
    inner = dot_nt(pick, product, precise)
    dq_acc[...] = jnp.zeros_like(dq_acc)
    masks = head_masks()
    scale = jnp.asarray(HEAD_DIM ** (-0.5), bf16)
    seg_row = seg_q[...]

    def one_block(block, carried):
        rows = pl.ds(pl.multiple_of(block * ROWS, ROWS), ROWS)
        same = seg_k[rows, :] == seg_row
        for pair in range(HEADS // 2):
            cols = slice(pair * BS, (pair + 1) * BS)
            q_two = q_ref[:, cols] * scale
            do_two = do_ref[:, cols]
            k_two = k_ref[rows, cols]
            v_two = v_ref[rows, cols]
            dv_two = dk_two = dq_two = None
            for side in range(2):
                at = 2 * pair + side
                q_one = q_two * masks[side]
                do_one = do_two * masks[side]
                scores = dot_nt(k_two, q_one)
                prob = jnp.where(same, jnp.exp(scores - lse_ref[at : at + 1, :]), 0.0)
                grad_prob = dot_nt(v_two, do_one)
                grad_scores = (prob * (grad_prob - inner[at : at + 1, :])).astype(bf16)
                dv_one = dot(prob.astype(bf16), do_one)
                dk_one = dot(grad_scores, q_one)
                dq_one = dot_tn(grad_scores, k_two * masks[side])
                dv_two = dv_one if dv_two is None else dv_two + dv_one
                dk_two = dk_one if dk_two is None else dk_two + dk_one
                dq_two = dq_one if dq_two is None else dq_two + dq_one
            dv_acc[rows, cols] += dv_two
            dk_acc[rows, cols] += dk_two
            dq_acc[:, cols] += dq_two
        return carried

    lax.fori_loop(low_ref[step], high_ref[step], one_block, 0)
    dq_ref[...] = (dq_acc[...] * HEAD_DIM ** (-0.5)).astype(bf16)

    @pl.when(step == pl.num_programs(0) - 1)
    def _():
        dk_ref[...] = dk_acc[...].astype(bf16)
        dv_ref[...] = dv_acc[...].astype(bf16)


def attend_back_call(
    layer, first, last, base, own, recv, queries, keys, values, mixed, lse, seg_col, seg_row, panels
):
    tokens = base.shape[0]
    shape = lambda width, kind: jax.ShapeDtypeStruct((tokens, width), kind)
    whole = (tokens, HALF)
    return pl.pallas_call(
        attend_back_kernel,
        out_shape=[
            shape(D, f32),
            shape(D, bf16),
            shape(HALF, bf16),
            shape(HALF, bf16),
            shape(HALF, bf16),
            jax.ShapeDtypeStruct((1, D), f32),
        ],
        grid_spec=pltpu.PrefetchScalarGridSpec(
            num_scalar_prefetch=2,
            grid=(tokens // ROWS,),
            in_specs=[
                rows_spec(D),
                rows_spec(D),
                rows_spec(D),
                rows_spec(HALF),
                fixed(whole),
                fixed(whole),
                rows_spec(HALF),
                pl.BlockSpec((8, ROWS), lambda i, *_: (0, i)),
                fixed(seg_col.shape),
                pl.BlockSpec((1, ROWS), lambda i, *_: (0, i)),
                fixed((D, HALF), PANELS["out"][layer] // D),
            ],
            out_specs=[
                rows_spec(D),
                rows_spec(D),
                rows_spec(HALF),
                fixed(whole),
                fixed(whole),
                fixed((1, D)),
            ],
            scratch_shapes=[
                pltpu.VMEM(whole, f32),
                pltpu.VMEM(whole, f32),
                pltpu.VMEM((ROWS, HALF), f32),
                pltpu.VMEM((ROWS, HALF), bf16),
            ],
        ),
        compiler_params=params(),
        cost_estimate=cost(14 * HEADS * tokens * tokens * BS, tokens * D * 20, HEADS * tokens * tokens),
    )(first, last, base, own, recv, queries, keys, values, mixed, lse, seg_col, seg_row, panels)


def qkv_back_kernel(layer, dq, dk, dv, hid, vec, weight, back, dgain, dshift, dbq, dbv):
    grad_normed = (
        dot_nt(dq[...], weight[0:D, :])
        + dot_nt(dk[...], weight[D : 2 * D, :])
        + dot_nt(dv[...], weight[2 * D : 3 * D, :])
    )
    part_back, gain_grad, shift_grad = norm_back(hid[...], vec_piece(vec, layer, "g1"), grad_normed)
    back[...] = part_back.astype(bf16)
    accumulate(dgain, gain_grad)
    accumulate(dshift, shift_grad)
    accumulate(dbq, jnp.sum(dq[...].astype(f32), axis=0, keepdims=True))
    accumulate(dbv, jnp.sum(dv[...].astype(f32), axis=0, keepdims=True))


def qkv_back_call(layer, dq, dk, dv, hid, vec, panels):
    tokens = dq.shape[0]
    line = lambda width: jax.ShapeDtypeStruct((1, width), f32)
    lines = [line(D), line(D), line(HALF), line(HALF)]
    return pl.pallas_call(
        functools.partial(qkv_back_kernel, layer),
        out_shape=[jax.ShapeDtypeStruct((tokens, D), bf16)] + lines,
        grid=(tokens // ROWS,),
        in_specs=[rows_spec(HALF)] * 3
        + [
            rows_spec(D),
            fixed(vec.shape),
            fixed((3 * D, HALF), PANELS["qkv"][layer] // (3 * D)),
        ],
        out_specs=[rows_spec(D)] + [fixed(o.shape) for o in lines],
        compiler_params=params(),
        cost_estimate=cost(2 * tokens * D * 3 * HALF, tokens * D * 10),
    )(dq, dk, dv, hid, vec, panels)


def rotate_step(master, grads, left, right, moment, variance):
    rotated = jnp.einsum("sji,sjk->sik", left, grads, precision=precise)
    rotated = jnp.einsum("sik,skl->sil", rotated, right, precision=precise)
    new_moment = decay * moment + (1.0 - decay) * rotated
    new_variance = decay * variance + (1.0 - decay) * rotated * rotated
    step_rot = new_moment / (jnp.sqrt(new_variance) + adam_eps)
    returned = jnp.einsum("sij,sjk->sik", left, step_rot, precision=precise)
    returned = jnp.einsum("sik,slk->sil", returned, right, precision=precise)
    return (master - matrix_rate * returned, new_moment, new_variance)


class Routes:
    def __init__(self, dp_n):
        pairs = [(d, t) for d in range(dp_n) for t in range(TENSOR)]
        at = lambda d, t: d * TENSOR + t
        home = [(d, t) for d, t in pairs if d % 2 == t]
        away = [(d, t) for d, t in pairs if d % 2 != t]
        self.core_all = [(at(d, t), at(d ^ 1, t)) for d, t in pairs]
        self.core_out = [(at(d, t), at(d ^ 1, t)) for d, t in home]
        self.core_in = [(at(d, t), at(d ^ 1, t)) for d, t in away]
        self.y_all = [(at(d, t), at(d, 1 - t)) for d, t in pairs]
        self.y_out = [(at(d, t), at(d, 1 - t)) for d, t in home]
        self.y_in = [(at(d, t), at(d, 1 - t)) for d, t in away]
        self.x_home = [(at(d, t), at(d ^ 2, t)) for d, t in home]
        self.x_away = [(at(d, t), at(d ^ 2, t)) for d, t in away]
        self.z_home = [(at(d, t), at((d + 4) % dp_n, t)) for d, t in home]


def send(value, route):
    return lax.ppermute(value, AXES, route)


def shards(
    patches,
    cotangent,
    image_size,
    block_slot,
    pinv,
    master_slots,
    left_basis,
    right_basis,
    mom_slots,
    var_slots,
    vec_master,
    vec_mom,
    vec_var,
):
    dp_n = lax.axis_size("dp")
    dp_pos = lax.axis_index("dp")
    y_pos = lax.axis_index("tensor")
    core = dp_pos % 2
    home = core == y_pos
    routes = Routes(dp_n)
    grid3 = dp_n == 16
    tokens_n = patches.shape[0]
    slots_per = master_slots.shape[1]
    vec_per = vec_master.shape[1]
    slots_n = slots_per * dp_n
    payload = slots_per * BS + VEC_ROWS

    patches = jnp.where(home, patches, send(patches, routes.core_out))
    cotangent = jnp.where(home, cotangent, send(cotangent, routes.core_out))
    size_row = jnp.where(home, image_size, send(image_size, routes.core_out))[0]
    own_slots = block_slot[0]
    slot_list = jnp.where(home, block_slot, send(block_slot, routes.y_all))[0]

    lengths = jnp.where(
        size_row == 0, LEN_A, jnp.where(size_row == 1, LEN_B, jnp.where(size_row == 2, LEN_C, 0))
    )
    order = jnp.arange(IMG_DEV)
    ends_at = jnp.sum(jnp.where(order[None, :] <= order[:, None], lengths[None, :], 0), axis=1)
    places = jnp.arange(tokens_n)
    segment = jnp.sum((places[:, None] >= ends_at[None, :]).astype(jnp.int32), axis=1)
    in_image = segment[:, None] == order[None, :]
    select = jnp.stack(
        [jnp.any(in_image & (size_row == s)[None, :], axis=1) for s in range(3)], axis=1
    )
    valid_col = (segment < IMG_DEV).astype(f32)[:, None]
    seg_col = segment[:, None]
    seg_row = segment[None, :]
    blocks_n = tokens_n // ROWS
    starts = jnp.arange(blocks_n) * ROWS
    begun = ends_at[None, :] <= starts[:, None]
    first_tok = jnp.max(jnp.where(begun, ends_at[None, :], 0), axis=1)
    after = ends_at[None, :] > (starts + ROWS - 1)[:, None]
    last_tok = jnp.min(jnp.where(after, ends_at[None, :], tokens_n), axis=1)
    first_blk = (first_tok // ROWS).astype(jnp.int32)
    last_blk = ((last_tok + ROWS - 1) // ROWS).astype(jnp.int32)

    select_low = select.astype(bf16)
    spread_in = patches[:, None, :] * select_low[:, :, None]
    base_pix = lax.dot_general(
        spread_in, pinv, (((1, 2), (0, 2)), ((), ())), preferred_element_type=f32
    ).astype(bf16)

    vec_low = jnp.pad(vec_master[0].astype(bf16), (0, VEC_ROWS * BS - vec_per))
    own_pack = jnp.concatenate(
        [
            master_slots[0].astype(bf16).reshape(slots_per * BS, BS),
            vec_low.reshape(VEC_ROWS, BS),
        ],
        axis=0,
    )
    named = slot_list[None, :] == jnp.arange(slots_n)[:, None]
    used = jnp.any(named, axis=1)
    drow = jnp.where(used, jnp.sum(jnp.where(named, TARGET_ROW[None, :], 0), axis=1), -1)
    dcol = jnp.sum(jnp.where(named, TARGET_COL[None, :], 0), axis=1)
    flag = home.astype(jnp.int32).reshape(1)
    if grid3:
        x_pos = (dp_pos // 2) % 2
        z_pos = dp_pos // 4
        pack = jnp.stack([own_pack, send(own_pack, routes.core_in)], axis=0)
        packs, acrosses, overs, corners = [pack], [], [], []
        for j in range(5):
            moved = []
            if j < 3:
                moved.append(send(packs[j], routes.z_home))
            if j < 4:
                moved += [send(packs[j], routes.x_home), send(packs[j], routes.y_out)]
            if j:
                moved += [
                    send(acrosses[j - 1][0:1], routes.y_out),
                    send(overs[j - 1][1:2], routes.x_away),
                ]
            if j < 4:
                moved = list(fence(*moved))
            if j < 3:
                packs.append(moved.pop(0))
            if j < 4:
                acrosses.append(moved.pop(0))
                overs.append(moved.pop(0))
            if j:
                corners.append(moved)
        first, second, owner = [], [], []
        for j in range(4):
            first += [packs[j], acrosses[j]]
            second += [overs[j]] + corners[j]
            for x_rel in range(2):
                for n in range(2):
                    owner.append(((z_pos - j) % 4) * 4 + (x_pos ^ x_rel) * 2 + (core ^ n))
        owner = jnp.stack(owner).astype(jnp.int32)
    else:
        everything = lax.all_gather(own_pack, AXES, axis=0)
        everything = everything.reshape(dp_n, TENSOR, payload, BS)
        first = [jnp.where(core == 0, everything[:, 0], everything[:, 1])]
        second = []
        owner = jnp.arange(dp_n, dtype=jnp.int32)
    panels, vec_rows = gather_tiles(first, second, owner, drow, dcol, flag, slots_per, dp_n)
    vec = vec_rows.reshape(dp_n, VEC_ROWS * BS)[:, :vec_per].astype(f32).reshape(1, dp_n * vec_per)

    base_w = panels[PANELS["base"] : PANELS["base"] + BASE_PIX]
    embedded = (dot(base_pix, base_w) + vec[:, :HALF]).astype(bf16)
    embedded_other = send(embedded, routes.core_all)
    hidden = jnp.concatenate(
        [
            jnp.where(core == 0, embedded, embedded_other),
            jnp.where(core == 0, embedded_other, embedded),
        ],
        axis=1,
    ).astype(f32)

    caches = []
    own = recv = None
    for layer in range(LAYERS):
        made = qkv_call(layer, hidden, own, recv, vec, panels)
        if own is not None:
            hidden, *made = made
        normed, queries, keys, values = made
        mixed, lse, part = attend_call(
            layer, queries, keys, values, seg_col, seg_row, vec, panels
        )
        other = send(part, routes.core_all)
        middle, normed2, act, slope, own = mlp_call(layer, hidden, part, other, vec, panels)
        recv = send(own, routes.core_all)
        caches.append((hidden, normed, queries, keys, values, mixed, lse, middle, normed2, act, slope))
        hidden = middle
    out_low = ((hidden + (own.astype(f32) + recv.astype(f32))) * valid_col).astype(bf16)
    output = jnp.where(home, out_low, send(out_low, routes.y_out)).astype(f32)

    owners = jnp.arange(dp_n)
    if grid3:
        place = (
            ((z_pos - 1 - owners // 4) % 4) * 4
            + (x_pos ^ ((owners // 2) % 2)) * 2
            + (core ^ (owners % 2))
        ).astype(jnp.int32)
        half_at = x_pos.astype(jnp.int32).reshape(1)
    else:
        place = owners.astype(jnp.int32)
        half_at = jnp.zeros((1,), jnp.int32)
    slot_owner = slot_list // slots_per
    owner_place = jnp.sum(
        jnp.where(slot_owner[:, None] == owners[None, :], place[None, :], 0), axis=1
    )
    tile_pos = (owner_place * payload + (slot_list % slots_per) * BS).astype(jnp.int32)
    vec_pos = (place * payload + slots_per * BS).astype(jnp.int32)
    total_rows = dp_n * payload
    offsets = {"base": 0}
    count = BASE_PIX // BS * (HALF // BS)
    for layer in range(LAYERS):
        for name, size in (("qkv", 3 * D * HALF), ("out", D * HALF), ("up", D * HALF_FF), ("down", D * HALF_FF)):
            offsets[name, layer] = count
            count += size // (BS * BS)

    def place_tiles(key, matrix, arrived, buffer):
        tiles = matrix.size // (BS * BS)
        pos = tile_pos[offsets[key] : offsets[key] + tiles]
        rows_n = BS if matrix.shape[0] < BASE_PIX else 4 * BS
        return scatter_matrix(pos, matrix, arrived, half_at, buffer, total_rows, rows_n)

    def over(matrix):
        return send(matrix, routes.y_in) if grid3 else None

    def halves_of(matrix):
        size = matrix.shape[0] // 2
        mine = lax.dynamic_slice_in_dim(matrix, x_pos * size, size, 0)
        theirs = lax.dynamic_slice_in_dim(matrix, (1 - x_pos) * size, size, 0)
        return mine, theirs

    def half_sum(matrix, arrived):
        mine, unused = halves_of(matrix)
        return (mine.astype(f32) + arrived.astype(f32)).astype(bf16)

    def beside(matrix):
        return send(halves_of(matrix)[1], routes.x_away) if grid3 else None

    def hold(*arrays):
        kept = [a for a in arrays if a is not None]
        done = iter(fence(*kept))
        return [None if a is None else next(done) for a in arrays]

    top, low = 1, 0
    vec_grads = [None] * LAYERS

    def mlp_step(layer, grad, own, recv):
        middle, normed2, act, slope = caches[layer][7:11]
        made = mlp_back_call(layer, grad, own, recv, valid_col, middle, slope, vec, panels)
        if own is not None:
            return made
        return [made[0]] + list(made)

    def attend_step(layer, grad, part, other):
        hid_in, normed, queries, keys, values, mixed, lse = caches[layer][:7]
        return attend_back_call(
            layer, first_blk, last_blk, grad, part, other, queries, keys, values, mixed, lse,
            seg_col, seg_row, panels,
        )

    grad, grad_low, du, part, dg2, ds2, db1, db2 = mlp_step(top, cotangent, None, None)
    other = send(part, routes.core_all)
    gd1 = dot_tn(caches[top][9], grad_low).astype(bf16)
    gu1 = dot_tn(caches[top][8], du).astype(bf16)
    part, other, gd1, gu1 = fence(part, other, gd1, gu1)
    ad1 = over(gd1)
    grad, grad_low, dq, dk, dv, dbo = attend_step(top, grad, part, other)
    dq, dk, dv, ad1 = hold(dq, dk, dv, ad1)
    au1 = over(gu1)
    own, dg1, ds1, dbq, dbv = qkv_back_call(top, dq, dk, dv, caches[top][0], vec, panels)
    recv = send(own, routes.core_all)
    go1 = dot_tn(caches[top][5], grad_low).astype(bf16)
    gq1 = dot_tn(caches[top][1], jnp.concatenate([dq, dk, dv], axis=1)).astype(bf16)
    vec_grads[top] = [dg1, ds1, dbq, dbv, dbo, dg2, ds2, db1, db2]
    grad, grad_low, du, part, dg2, ds2, db1, db2 = mlp_step(low, grad, own, recv)
    du, part, au1, go1, gq1 = hold(du, part, au1, go1, gq1)
    other = send(part, routes.core_all)
    xq1, ao1 = beside(gq1), over(go1)
    gd0 = dot_tn(caches[low][9], grad_low).astype(bf16)
    gu0 = dot_tn(caches[low][8], du).astype(bf16)
    part, other, gd0, gu0, xq1, ao1 = hold(part, other, gd0, gu0, xq1, ao1)
    aq1 = over(half_sum(gq1, xq1)) if grid3 else None
    xd0, xu0 = beside(gd0), beside(gu0)
    buffer = place_tiles(("down", top), gd1, ad1, None)
    buffer = place_tiles(("up", top), gu1, au1, buffer)
    grad, grad_low, dq, dk, dv, dbo = attend_step(low, grad, part, other)
    grad, grad_low, dq, dk, dv, aq1, xd0, xu0, buffer = hold(
        grad, grad_low, dq, dk, dv, aq1, xd0, xu0, buffer
    )
    ad0 = over(half_sum(gd0, xd0)) if grid3 else None
    au0 = over(half_sum(gu0, xu0)) if grid3 else None
    own, dg1, ds1, dbq, dbv = qkv_back_call(low, dq, dk, dv, caches[low][0], vec, panels)
    recv = send(own, routes.core_all)
    go0 = dot_tn(caches[low][5], grad_low).astype(bf16)
    gq0 = dot_tn(caches[low][1], jnp.concatenate([dq, dk, dv], axis=1)).astype(bf16)
    vec_grads[low] = [dg1, ds1, dbq, dbv, dbo, dg2, ds2, db1, db2]
    sides = [
        grad[:, s * HALF : (s + 1) * HALF]
        + (
            own[:, s * HALF : (s + 1) * HALF].astype(f32)
            + recv[:, s * HALF : (s + 1) * HALF].astype(f32)
        )
        for s in range(TENSOR)
    ]
    grad_emb = jnp.where(core == 0, sides[0], sides[1]).astype(bf16)
    grad_emb_bias = jnp.sum(grad_emb.astype(f32), axis=0, keepdims=True)
    gb = dot_tn(base_pix, grad_emb).astype(bf16)
    vec_grad = jnp.concatenate([grad_emb_bias] + vec_grads[0] + vec_grads[1], axis=1)[0]
    vec_grad = jnp.pad(vec_grad, (0, dp_n * vec_per - vec_grad.shape[0])).reshape(dp_n, vec_per)
    vec_grad = jnp.pad(vec_grad, ((0, 0), (0, VEC_ROWS * BS - vec_per)))
    vec_grad = vec_grad.astype(bf16).reshape(dp_n, VEC_ROWS, BS)
    ad0, au0, go0, gq0, gb, vec_grad, grad_emb = hold(ad0, au0, go0, gq0, gb, vec_grad, grad_emb)
    xq0 = beside(gq0)
    ab, ao0, av = over(gb), over(go0), over(vec_grad)
    buffer = place_tiles(("out", top), go1, ao1, buffer)
    buffer = place_tiles(("qkv", top), gq1, aq1, buffer)
    buffer = place_tiles(("down", low), gd0, ad0, buffer)
    buffer = place_tiles(("up", low), gu0, au0, buffer)
    resized = [dot_tn(pinv[s], base_w).astype(bf16) for s in range(3)]
    xq0, ab, ao0, av, buffer, *resized = hold(xq0, ab, ao0, av, buffer, *resized)
    aq0 = over(half_sum(gq0, xq0)) if grid3 else None
    buffer = place_tiles("base", gb, ab, buffer)
    buffer = place_tiles(("out", low), go0, ao0, buffer)
    buffer = scatter_vec(vec_pos, vec_grad, av, buffer)
    grad_pixels = sum(
        dot_nt(grad_emb * select_low[:, s : s + 1], resized[s]) for s in range(3)
    ).astype(bf16)
    aq0, buffer, grad_pixels = hold(aq0, buffer, grad_pixels)
    buffer = place_tiles(("qkv", low), gq0, aq0, buffer)

    if grid3:
        carried = None
        for j in range(4):
            block = buffer.reshape(4, 2, 2, payload, BS)
            arrived = send(block[j, 1], routes.x_home)
            if carried is not None:
                arrived, carried, buffer = fence(arrived, carried, buffer)
            else:
                arrived, buffer = fence(arrived, buffer)
            block = buffer.reshape(4, 2, 2, payload, BS)
            total = block[j, 0].astype(f32) + arrived.astype(f32)
            if carried is not None:
                total = total + carried.astype(f32)
            if j < 3:
                carried = send(total.astype(bf16), routes.z_home)
        rounded = total.astype(bf16)
        mine = jnp.where(home, rounded[0], send(rounded[1], routes.core_out)).astype(f32)
    else:
        held = buffer.reshape(dp_n, 1, payload, BS).astype(f32)
        nothing = jnp.zeros_like(held)
        both = jnp.concatenate(
            [jnp.where(core == 0, held, nothing), jnp.where(core == 0, nothing, held)], axis=1
        )
        used_rows = jnp.repeat(used, BS).reshape(dp_n, 1, slots_per * BS, 1)
        used_rows = jnp.concatenate(
            [used_rows, jnp.ones((dp_n, 1, VEC_ROWS, 1), bool)], axis=2
        )
        both = jnp.where(used_rows, both, 0.0).reshape(dp_n * TENSOR * payload, BS)
        mine = lax.psum_scatter(both, AXES, scatter_dimension=0, tiled=True)

    pixels_other = send(grad_pixels, routes.core_all)
    pixel_sides = [
        grad_pixels[:, s * HALF : (s + 1) * HALF].astype(f32)
        + pixels_other[:, s * HALF : (s + 1) * HALF].astype(f32)
        for s in range(TENSOR)
    ]
    near = jnp.where(core == 0, pixel_sides[0], pixel_sides[1])
    far = jnp.where(core == 0, pixel_sides[1], pixel_sides[0]).astype(bf16)
    patch_grad = jnp.where(home, near, send(far, routes.y_out).astype(f32))

    my_slots = dp_pos * slots_per + jnp.arange(slots_per)
    mine_used = jnp.any(own_slots[None, :] == my_slots[:, None], axis=1)
    owned_grad = mine[: slots_per * BS].reshape(slots_per, BS, BS)
    owned_grad = jnp.where(mine_used[:, None, None], owned_grad, 0.0)
    owned_vec_grad = mine[slots_per * BS :].reshape(VEC_ROWS * BS)[:vec_per]
    new_master, new_mom, new_var = rotate_step(
        master_slots[0], owned_grad, left_basis[0], right_basis[0], mom_slots[0], var_slots[0]
    )
    new_vec_mom = decay * vec_mom[0] + (1.0 - decay) * owned_vec_grad
    new_vec_var = decay * vec_var[0] + (1.0 - decay) * owned_vec_grad * owned_vec_grad
    new_vec = vec_master[0] - vector_rate * new_vec_mom / (jnp.sqrt(new_vec_var) + adam_eps)
    return (
        output,
        patch_grad,
        owned_grad[None],
        new_master[None],
        new_mom[None],
        new_var[None],
        owned_vec_grad[None],
        new_vec[None],
        new_vec_mom[None],
        new_vec_var[None],
    )


def solution(mesh):
    slots = P("tensor", "dp", None, None)
    vectors = P("tensor", "dp")
    tokens = P("dp", None)
    in_specs = (tokens, tokens, tokens, P("tensor", None), P()) + (slots,) * 5 + (vectors,) * 3
    out_specs = (tokens, P("dp", "tensor")) + (slots,) * 4 + (vectors,) * 4
    return jax.shard_map(shards, mesh=mesh, in_specs=in_specs, out_specs=out_specs, check_vma=False)
```

time: 1740 us -> 815 us (0.47)
  matrix products: 513 us -> 107 us
  waiting for transfers between devices: 615 us -> 218 us
  local copies, waits for them, and re-layouts: 381 us -> 48.6 us
  Pallas kernels: 0 us -> 260 us
  starting transfers between devices: 1.12 us -> 116 us
  blocking collectives: 85.3 us -> 0 us
  other arithmetic: 100 us -> 52.8 us
    dot_general x61 -> x17, matrix products: 496 us -> 90.6 us  [the longest x12 59.1 us: dot_tn(): lax.dot_general(left, right, (((0,), (0,)), ((), ())), preferred_element_...]
    pallas_call x0 -> x39, Pallas kernels: none -> 260 us  [the longest x2 59.7 us: attend_back_call(): pl.pallas_call(attend_back_kernel, out_shape=[shape(D, f32), shape(D, bf1...]
    reduce_scatter x1 -> x0, waiting for transfers between devices: 258 us -> none  [shards(): lax.psum_scatter(buffer, 'dp', scatter_dimension=0, tiled=True)]
    psum x7 -> x0, waiting for transfers between devices: 240 us -> none  [the longest x2 85.3 us: shards(): lax.psum(partial_value.astype(jnp.bfloat16).astype(jnp.float32).astype(jn...]
    ppermute x0 -> x58, waiting for transfers between devices: none -> 218 us  [send(): return lax.ppermute(value, AXES, route)]
    all_gather x2 -> x0, waiting for transfers between devices: 117 us -> none  [the longest x1 105 us: shards(): lax.all_gather(master_slots[0].astype(jnp.bfloat16), 'dp', axis=0, tiled=...]
    ppermute x0 -> x58, starting transfers between devices: none -> 116 us  [send(): return lax.ppermute(value, AXES, route)]
    scatter x1 -> x0, local copies, waits for them, and re-layouts: 92.6 us -> none  [shards(): jnp.zeros(slot_tiles.shape, jnp.float32).at[slot_list].set(tiles_all)]
  transfers between devices with their start and end apart: 11 -> 58, of which waited for: 10 -> 19; matrix products, arithmetic and copies ran while one was open for 19% -> 18% of each run, Pallas kernels for 0% -> 20%
where the time goes in v1:
time: 815 us; the launch traced here: 805 us
  Pallas kernels  260 us (32%)
  waiting for transfers between devices  218 us (27%)
  starting transfers between devices  116 us (14%)
  matrix products  107 us (13%)
  other arithmetic  52.8 us (6%)
  local copies, waits for them, and re-layouts  48.6 us (6%)
    ppermute x58, waiting for transfers between devices, send(): return lax.ppermute(value, AXES, route)  218 us
    ppermute x58, starting transfers between devices, send(): return lax.ppermute(value, AXES, route)  116 us
    pallas_call x2, Pallas kernels, attend_back_call(): pl.pallas_call(attend_back_kernel, out_shape=[shape(D, f32), shape(D, bf1...  59.7 us
    dot_general x12, matrix products, dot_tn(): lax.dot_general(left, right, (((0,), (0,)), ((), ())), preferred_element_...  59.1 us
    pallas_call x9, Pallas kernels, scatter_matrix(): pl.pallas_call(functools.partial(scatter_kernel, rows_n, cols_n, paired,...  53.5 us
    pallas_call x2, Pallas kernels, attend_call(): pl.pallas_call(functools.partial(attend_kernel, layer), out_shape=[jax.Sh...  39 us
    pallas_call x2, Pallas kernels, mlp_back_call(): pl.pallas_call(functools.partial(mlp_back_kernel, layer, summed), out_sha...  32.8 us
    pallas_call x2, Pallas kernels, mlp_call(): pl.pallas_call(functools.partial(mlp_kernel, layer), out_shape=outs, grid...  27 us
  transfers between devices with their start and end apart: 58, of which 19 were waited for; matrix products, arithmetic and copies ran while one was open for 18% of the time, Pallas kernels for 20%

profile of v1, /device:TPU:0, one launch (start us, length us, event | category | flops | bytes accessed | tf_op | source)
XLA Modules:
  0.0 805.2 jit_solution(2862131917351973840)
XLA Ops:
  8.2 4.9 collective-permute-start.4
  19.2 20.1 %collective-permute-done.4.refs_0_ = bf16[2,4112,128]{2,1,0:T(8,128)(2,1)S(1)} collective-permute-done((bf16[2,4112,128]{2,1,0:T(8,128)(2,1)S(1)}, bf16[2,4112,128]{2,1,0:T(8,128)(2,1)S(1)}, u32[]{:S(2)}, u32[]{:S(2)}) %collective-permute-start.4) | collective-permute-done | bytes 2105376 | tf_op jit(solution)/shard_map/ppermute | solution.py:752
  57.0 28.1 %collective-permute-done.10.refs_3_ = bf16[1,4112,128]{2,1,0:T(8,128)(2,1)S(1)} collective-permute-done((bf16[1,4112,128]{2,1,0:T(8,128)(2,1)S(1)}, bf16[1,4112,128]{2,1,0:T(8,128)(2,1)S(1)}, u32[]{:S(2)}, u32[]{:S(2)}) %collective-permute-start.10) | collective-permute-done | bytes 1052704 | tf_op jit(solution)/shard_map/ppermute | solution.py:752
  104.1 25.6 %collective-permute-done.15.refs_3_ = bf16[1,4112,128]{2,1,0:T(8,128)(2,1)S(1)} collective-permute-done((bf16[1,4112,128]{2,1,0:T(8,128)(2,1)}, bf16[1,4112,128]{2,1,0:T(8,128)(2,1)S(1)}, u32[]{:S(2)}, u32[]{:S(2)}) %collective-permute-start.15) | collective-permute-done | bytes 1052704 | tf_op jit(solution)/shard_map/ppermute | solution.py:752
  150.0 24.5 %collective-permute-done.19.refs_2_ = bf16[1,4112,128]{2,1,0:T(8,128)(2,1)S(1)} collective-permute-done((bf16[1,4112,128]{2,1,0:T(8,128)(2,1)S(1)}, bf16[1,4112,128]{2,1,0:T(8,128)(2,1)S(1)}, u32[]{:S(2)}, u32[]{:S(2)}) %collective-permute-start.19) | collective-permute-done | bytes 1052704 | tf_op jit(solution)/shard_map/ppermute | solution.py:752
  176.9 4.5 collective-permute-start.21
  183.4 19.1 %bitcast_convert_fusion = bf16[1024,3072]{1,0:T(8,128)(2,1)} fusion(bf16[3,3072,768]{2,1,0:T(8,128)(2,1)} %param.19, bf16[1024,3]{0,1:T(4,128)(2,1)S(1)} %add_convert_fusion.6, bf16[1024,768]{1,0:T(8,128)(2,1)S(1)} %copy-done.53), kind=kOutput, calls=%fused_computation | convolution fusion | flops 14501019648 | bytes 22026240 | tf_op jit(solution)/shard_map/dot_general | solution.py:814
  203.8 14.6 %shard_map.226 = (bf16[21504,384]{1,0:T(8,128)(2,1)}, bf16[16,16,128]{2,1,0:T(8,128)(2,1)}) custom-call(s32[16]{0:T(128)} %stack.92.owner, s32[512]{0:T(512)} %broadcast_select_fusion.6.drow, s32[512]{0:T(512)} %get-tuple-element.292.dcol, s32[1]{0:T(128)} %bitcast.22.flag, bf16[2,4112,128]{2,1,0:T(8,128)(2,1)} %copy-done.16, ...), custom_call_target="tpu_custom_call" | custom-call | bytes 33030144 | tf_op jit(solution)/shard_map/pallas_call | solution.py:227
  219.4 6.9 add_convert_fusion.5
  232.6 6.8 shard_map.227
  239.4 19.5 %shard_map.228 = (bf16[1024,384]{1,0:T(8,128)(2,1)}, f32[8,1024]{1,0:T(8,128)}, bf16[1024,768]{1,0:T(8,128)(2,1)}) custom-call(bf16[1024,384]{1,0:T(8,128)(2,1)} %get-tuple-element.167.q_ref, bf16[1024,384]{1,0:T(8,128)(2,1)} %get-tuple-element.168.k_ref, bf16[1024,384]{1,0:T(8,128)(2,1)} %get-tuple-element.169.v_ref, s32[1024,1]{1,0:T(8,128)} %copy.135.seg_q.seg_k, ...), custom_call_target="tpu_custom_call" | custom-call | flops 6442450944 | bytes 6291456 | tf_op jit(solution)/shard_map/pallas_call | solution.py:433
  263.7 13.5 %shard_map.229 = (f32[1024,768]{1,0:T(8,128)}, bf16[1024,768]{1,0:T(8,128)(2,1)}, bf16[1024,1536]{1,0:T(8,128)(2,1)}, bf16[1024,1536]{1,0:T(8,128)(2,1)}, bf16[1024,768]{1,0:T(8,128)(2,1)}) custom-call(f32[1024,768]{1,0:T(8,128)} %maximum_convert_fusion.refs_0_.base.hid, bf16[1024,768]{1,0:T(8,128)(2,1)} %get-tuple-element.170.own, ...), custom_call_target="tpu_custom_call" | custom-call | flops 4831838208 | bytes 18874368 | tf_op jit(solution)/shard_map/pallas_call | solution.py:491
  281.9 7.9 shard_map.230
  289.9 19.5 %shard_map.231 = (bf16[1024,384]{1,0:T(8,128)(2,1)}, f32[8,1024]{1,0:T(8,128)}, bf16[1024,768]{1,0:T(8,128)(2,1)}) custom-call(bf16[1024,384]{1,0:T(8,128)(2,1)} %get-tuple-element.174.q_ref, bf16[1024,384]{1,0:T(8,128)(2,1)} %get-tuple-element.175.k_ref, bf16[1024,384]{1,0:T(8,128)(2,1)} %get-tuple-element.176.v_ref, s32[1024,1]{1,0:T(8,128)} %copy.135.seg_q.seg_k, ...), custom_call_target="tpu_custom_call" | custom-call | flops 6442450944 | bytes 6291456 | tf_op jit(solution)/shard_map/pallas_call | solution.py:433
  314.2 13.5 %shard_map.232 = (f32[1024,768]{1,0:T(8,128)}, bf16[1024,768]{1,0:T(8,128)(2,1)}, bf16[1024,1536]{1,0:T(8,128)(2,1)}, bf16[1024,1536]{1,0:T(8,128)(2,1)}, bf16[1024,768]{1,0:T(8,128)(2,1)}) custom-call(f32[1024,768]{1,0:T(8,128)} %get-tuple-element.173.base.hid, bf16[1024,768]{1,0:T(8,128)(2,1)} %get-tuple-element.177.own, bf16[1024,768]{1,0:T(8,128)(2,1)} %copy-done.49, ...), custom_call_target="tpu_custom_call" | custom-call | flops 4831838208 | bytes 18874368 | tf_op jit(solution)/shard_map/pallas_call | solution.py:491
  327.7 16.0 %shard_map.233 = (bf16[1024,768]{1,0:T(8,128)(2,1)}, bf16[1024,1536]{1,0:T(8,128)(2,1)}, bf16[1024,768]{1,0:T(8,128)(2,1)}, f32[1,768]{1,0:T(1,128)}, f32[1,768]...) custom-call(bf16[1024,768]{1,0:T(8,128)(2,1)} %broadcast_select_fusion.refs_0_, ...), custom_call_target="tpu_custom_call" | custom-call | flops 4831838208 | bytes 18874368 | tf_op jit(solution)/shard_map/pallas_call | solution.py:548
  344.2 5.5 convolution_convert_fusion.4.refs_2_
  349.7 4.2 convolution_convert_fusion.3.refs_3_
  358.5 29.8 %shard_map.235 = (f32[1024,768]{1,0:T(8,128)}, bf16[1024,768]{1,0:T(8,128)(2,1)}, bf16[1024,384]{1,0:T(8,128)(2,1)}, bf16[1024,384]{1,0:T(8,128)(2,1)}, bf16[1024,384]{1,0:T(8,128)(2,1)}, /*index=5*/f32[1,768]{1,0:T(1,128)}) custom-call(s32[4]{0:T(128)} %get-tuple-element.324.low_ref, s32[4]{0:T(128)} %get-tuple-element.323.high_ref, ...), custom_call_target="tpu_custom_call" | custom-call | flops 11274289152 | bytes 15728640 | tf_op jit(solution)/shard_map/pallas_call | solution.py:643
  388.4 8.0 shard_map.237
  396.5 4.1 collective-permute-start.32
  407.7 16.7 %shard_map.238 = (f32[1024,768]{1,0:T(8,128)}, bf16[1024,768]{1,0:T(8,128)(2,1)}, bf16[1024,1536]{1,0:T(8,128)(2,1)}, bf16[1024,768]{1,0:T(8,128)(2,1)}, f32[1,7...) custom-call(f32[1024,768]{1,0:T(8,128)} %get-tuple-element.190.refs_0_, ...), custom_call_target="tpu_custom_call" | custom-call | flops 4831838208 | bytes 18874368 | tf_op jit(solution)/shard_map/pallas_call | solution.py:548
  425.2 9.0 %shard_map.242.refs_1_ = bf16[65792,128]{1,0:T(8,128)(2,1)} custom-call(s32[72]{0:T(128)} %get-tuple-element.317.pos, s32[1]{0:T(128)} %bitcast.29.part, bf16[1536,768]{1,0:T(8,128)(2,1)} %get-tuple-element.194.own, bf16[1536,768]{1,0:T(8,128)(2,1)} %get-tuple-element.226.refs_0_), custom_call_target="tpu_custom_call" | custom-call | flops 1179648 | bytes 7077888 | tf_op jit(solution)/shard_map/pallas_call | solution.py:301
  437.4 6.5 convolution_convert_fusion.2.refs_2_
  443.9 6.2 shard_map.243.refs_8_
  450.1 5.4 convolution_convert_fusion.1.refs_3_
  463.2 29.9 %shard_map.241 = (f32[1024,768]{1,0:T(8,128)}, bf16[1024,768]{1,0:T(8,128)(2,1)}, bf16[1024,384]{1,0:T(8,128)(2,1)}, bf16[1024,384]{1,0:T(8,128)(2,1)}, bf16[1024,384]{1,0:T(8,128)(2,1)}, /*index=5*/f32[1,768]{1,0:T(1,128)}) custom-call(s32[4]{0:T(128)} %get-tuple-element.324.low_ref, s32[4]{0:T(128)} %get-tuple-element.323.high_ref, ...), custom_call_target="tpu_custom_call" | custom-call | flops 11274289152 | bytes 15728640 | tf_op jit(solution)/shard_map/pallas_call | solution.py:643
  495.1 8.0 shard_map.245
  503.1 4.8 collective-permute-start.42
  522.6 7.7 convolution_convert_fusion.refs_4_
  530.3 10.1 %collective-permute-done.41.refs_1_ = bf16[384,1536]{1,0:T(8,128)(2,1)} collective-permute-done((bf16[384,1536]{1,0:T(8,128)(2,1)}, bf16[384,1536]{1,0:T(8,128)(2,1)}, u32[]{:S(2)}, u32[]{:S(2)}) %collective-permute-start.41) | collective-permute-done | bytes 1179680 | tf_op jit(solution)/shard_map/ppermute | solution.py:752
  542.3 6.6 fusion.77.refs_5_
  550.9 6.5 fusion.72.refs_6_
  560.0 6.5 fusion.67.refs_7_
  570.2 5.4 shard_map.248.refs_1_
  575.6 8.4 %shard_map.249.refs_1_ = bf16[65792,128]{1,0:T(8,128)(2,1)} custom-call(s32[72]{0:T(128)} %get-tuple-element.315.pos, s32[1]{0:T(128)} %bitcast.29.part, bf16[1536,768]{1,0:T(8,128)(2,1)} %get-tuple-element.212.own, bf16[768,768]{1,0:T(8,128)(2,1)} %get-tuple-element.259.refs_0_, bf16[65792,128]{1,0:T(8,128)(2,1)} %shard_map.248.refs_1_), custom_call_target="tpu_custom_call", output_to_operand_aliasing={{}: (4, {})} | custom-call | flops 1179648 | bytes 7077888 | tf_op jit(solution)/shard_map/pallas_call | solution.py:301
  584.0 5.8 shard_map.250.refs_4_
  595.7 5.9 shard_map.252.refs_1_
  613.0 5.4 shard_map.256.refs_1_
  623.1 25.1 %collective-permute-done.50.refs_0_ = bf16[2,4112,128]{2,1,0:T(8,128)(2,1)} collective-permute-done((bf16[2,4112,128]{2,1,0:T(8,128)(2,1)S(1)}, bf16[2,4112,128]{2,1,0:T(8,128)(2,1)}, u32[]{:S(2)}, u32[]{:S(2)}) %collective-permute-start.50) | collective-permute-done | bytes 2105376 | tf_op jit(solution)/shard_map/ppermute | solution.py:752
  658.8 19.3 %collective-permute-done.51.refs_0_ = bf16[2,4112,128]{2,1,0:T(8,128)(2,1)} collective-permute-done((bf16[2,4112,128]{2,1,0:T(8,128)(2,1)S(1)}, bf16[2,4112,128]{2,1,0:T(8,128)(2,1)}, u32[]{:S(2)}, u32[]{:S(2)}) %collective-permute-start.51) | collective-permute-done | bytes 2105376 | tf_op jit(solution)/shard_map/ppermute | solution.py:752
  678.1 7.5 collective-permute-done.52.refs_1_
  695.9 19.5 %collective-permute-done.53.refs_0_ = bf16[2,4112,128]{2,1,0:T(8,128)(2,1)} collective-permute-done((bf16[2,4112,128]{2,1,0:T(8,128)(2,1)S(1)}, bf16[2,4112,128]{2,1,0:T(8,128)(2,1)}, u32[]{:S(2)}, u32[]{:S(2)}) %collective-permute-start.53) | collective-permute-done | bytes 2105376 | tf_op jit(solution)/shard_map/ppermute | solution.py:752
  715.5 8.4 %collective-permute-done.54.refs_1_ = bf16[2,4112,128]{2,1,0:T(8,128)(2,1)} collective-permute-done((bf16[2,4112,128]{2,1,0:T(8,128)(2,1)S(1)}, bf16[2,4112,128]{2,1,0:T(8,128)(2,1)}, u32[]{:S(2)}, u32[]{:S(2)}) %collective-permute-start.54) | collective-permute-done | bytes 2105376 | tf_op jit(solution)/shard_map/ppermute | solution.py:752
  744.2 9.5 %collective-permute-done.55.refs_0_ = bf16[2,4112,128]{2,1,0:T(8,128)(2,1)} collective-permute-done((bf16[2,4112,128]{2,1,0:T(8,128)(2,1)S(1)}, bf16[2,4112,128]{2,1,0:T(8,128)(2,1)}, u32[]{:S(2)}, u32[]{:S(2)}) %collective-permute-start.55) | collective-permute-done | bytes 2105376 | tf_op jit(solution)/shard_map/ppermute | solution.py:752
  753.7 8.6 %collective-permute-done.56.refs_1_ = bf16[2,4112,128]{2,1,0:T(8,128)(2,1)} collective-permute-done((bf16[2,4112,128]{2,1,0:T(8,128)(2,1)S(1)}, bf16[2,4112,128]{2,1,0:T(8,128)(2,1)}, u32[]{:S(2)}, u32[]{:S(2)}) %collective-permute-start.56) | collective-permute-done | bytes 2105376 | tf_op jit(solution)/shard_map/ppermute | solution.py:752
  781.6 5.3 fusion.36
  798.3 5.8 fusion.38
  (432 shorter events, 241.5 us)
Async XLA Ops:
  8.2 31.1 %collective-permute-start.4 = (bf16[2,4112,128]{2,1,0:T(8,128)(2,1)S(1)}, bf16[2,4112,128]{2,1,0:T(8,128)(2,1)S(1)}, u32[]{:S(2)}, u32[]{:S(2)}) collective-permute-start(bf16[2,4112,128]{2,1,0:T(8,128)(2,1)S(1)} %pad_maximum_fusion.refs_0_), channel_id=1, source_target_pairs={{0,8},{3,11},{4,12},{7,15},{8,16},{11,19},{12,20},{15,23},{16,24},... | collective-permute-start | bytes 6316040 | tf_op jit(solution)/shard_map/ppermute | solution.py:752
  13.1 28.1 %collective-permute-start.5 = (bf16[2,4112,128]{2,1,0:T(8,128)(2,1)S(1)}, bf16[2,4112,128]{2,1,0:T(8,128)(2,1)}, u32[]{:S(2)}, u32[]{:S(2)}) collective-permute-start(bf16[2,4112,128]{2,1,0:T(8,128)(2,1)S(1)} %pad_maximum_fusion.refs_0_), channel_id=1, source_target_pairs={{0,4},{3,7},{4,0},{7,3},{8,12},{11,15},{12,8},{15,11},{16,20},{19,... | collective-permute-start | bytes 6316040 | tf_op jit(solution)/shard_map/ppermute | solution.py:752
  16.6 24.9 %collective-permute-start.6 = (bf16[2,4112,128]{2,1,0:T(8,128)(2,1)S(1)}, bf16[2,4112,128]{2,1,0:T(8,128)(2,1)}, u32[]{:S(2)}, u32[]{:S(2)}) collective-permute-start(bf16[2,4112,128]{2,1,0:T(8,128)(2,1)S(1)} %pad_maximum_fusion.refs_0_), channel_id=1, source_target_pairs={{0,1},{3,2},{4,5},{7,6},{8,9},{11,10},{12,13},{15,14},{16,17},{19,... | collective-permute-start | bytes 6316040 | tf_op jit(solution)/shard_map/ppermute | solution.py:752
  41.5 43.6 %collective-permute-start.7 = (bf16[2,4112,128]{2,1,0:T(8,128)(2,1)}, bf16[2,4112,128]{2,1,0:T(8,128)(2,1)}, u32[]{:S(2)}, u32[]{:S(2)}) collective-permute-start(bf16[2,4112,128]{2,1,0:T(8,128)(2,1)} %get-tuple-element.149.refs_2_), channel_id=1, source_target_pairs={{0,8},{3,11},{4,12},{7,15},{8,16},{11,19},{12,20},{15,23},{16,24},... | collective-permute-start | bytes 6316040 | tf_op jit(solution)/shard_map/ppermute | solution.py:752
  45.0 40.2 %collective-permute-start.8 = (bf16[2,4112,128]{2,1,0:T(8,128)(2,1)}, bf16[2,4112,128]{2,1,0:T(8,128)(2,1)}, u32[]{:S(2)}, u32[]{:S(2)}) collective-permute-start(bf16[2,4112,128]{2,1,0:T(8,128)(2,1)} %get-tuple-element.149.refs_2_), channel_id=1, source_target_pairs={{0,4},{3,7},{4,0},{7,3},{8,12},{11,15},{12,8},{15,11},{16,20},{19,... | collective-permute-start | bytes 6316040 | tf_op jit(solution)/shard_map/ppermute | solution.py:752
  48.2 37.0 %collective-permute-start.9 = (bf16[2,4112,128]{2,1,0:T(8,128)(2,1)}, bf16[2,4112,128]{2,1,0:T(8,128)(2,1)}, u32[]{:S(2)}, u32[]{:S(2)}) collective-permute-start(bf16[2,4112,128]{2,1,0:T(8,128)(2,1)} %get-tuple-element.149.refs_2_), channel_id=1, source_target_pairs={{0,1},{3,2},{4,5},{7,6},{8,9},{11,10},{12,13},{15,14},{16,17},{19,... | collective-permute-start | bytes 6316040 | tf_op jit(solution)/shard_map/ppermute | solution.py:752
  52.6 32.5 %collective-permute-start.10 = (bf16[1,4112,128]{2,1,0:T(8,128)(2,1)S(1)}, bf16[1,4112,128]{2,1,0:T(8,128)(2,1)S(1)}, u32[]{:S(2)}, u32[]{:S(2)}) collective-permute-start(bf16[1,4112,128]{2,1,0:T(8,128)(2,1)S(1)} %slice.147), channel_id=1, source_target_pairs={{0,1},{3,2},{4,5},{7,6},{8,9},{11,10},{12,13},{15,14},{16,17},{19,... | collective-permute-start | bytes 3158024 | tf_op jit(solution)/shard_map/ppermute | solution.py:752
  55.3 29.8 %collective-permute-start.11 = (bf16[1,4112,128]{2,1,0:T(8,128)(2,1)S(1)}, bf16[1,4112,128]{2,1,0:T(8,128)(2,1)}, u32[]{:S(2)}, u32[]{:S(2)}) collective-permute-start(bf16[1,4112,128]{2,1,0:T(8,128)(2,1)S(1)} %slice.148), channel_id=1, source_target_pairs={{1,5},{2,6},{5,1},{6,2},{9,13},{10,14},{13,9},{14,10},{17,21},{18,... | collective-permute-start | bytes 3158024 | tf_op jit(solution)/shard_map/ppermute | solution.py:752
  86.1 47.4 %collective-permute-start.12 = (bf16[2,4112,128]{2,1,0:T(8,128)(2,1)}, bf16[2,4112,128]{2,1,0:T(8,128)(2,1)}, u32[]{:S(2)}, u32[]{:S(2)}) collective-permute-start(bf16[2,4112,128]{2,1,0:T(8,128)(2,1)} %get-tuple-element.152.refs_4_), channel_id=1, source_target_pairs={{0,8},{3,11},{4,12},{7,15},{8,16},{11,19},{12,20},{15,23},{16,24},... | collective-permute-start | bytes 6316040 | tf_op jit(solution)/shard_map/ppermute | solution.py:752
  89.6 45.2 %collective-permute-start.13 = (bf16[2,4112,128]{2,1,0:T(8,128)(2,1)}, bf16[2,4112,128]{2,1,0:T(8,128)(2,1)}, u32[]{:S(2)}, u32[]{:S(2)}) collective-permute-start(bf16[2,4112,128]{2,1,0:T(8,128)(2,1)} %get-tuple-element.152.refs_4_), channel_id=1, source_target_pairs={{0,4},{3,7},{4,0},{7,3},{8,12},{11,15},{12,8},{15,11},{16,20},{19,... | collective-permute-start | bytes 6316040 | tf_op jit(solution)/shard_map/ppermute | solution.py:752
  92.0 42.7 %collective-permute-start.14 = (bf16[2,4112,128]{2,1,0:T(8,128)(2,1)}, bf16[2,4112,128]{2,1,0:T(8,128)(2,1)}, u32[]{:S(2)}, u32[]{:S(2)}) collective-permute-start(bf16[2,4112,128]{2,1,0:T(8,128)(2,1)} %get-tuple-element.152.refs_4_), channel_id=1, source_target_pairs={{0,1},{3,2},{4,5},{7,6},{8,9},{11,10},{12,13},{15,14},{16,17},{19,... | collective-permute-start | bytes 6316040 | tf_op jit(solution)/shard_map/ppermute | solution.py:752
  98.1 31.6 %collective-permute-start.15 = (bf16[1,4112,128]{2,1,0:T(8,128)(2,1)}, bf16[1,4112,128]{2,1,0:T(8,128)(2,1)S(1)}, u32[]{:S(2)}, u32[]{:S(2)}) collective-permute-start(bf16[1,4112,128]{2,1,0:T(8,128)(2,1)} %slice.149), channel_id=1, source_target_pairs={{0,1},{3,2},{4,5},{7,6},{8,9},{11,10},{12,13},{15,14},{16,17},{19,... | collective-permute-start | bytes 3158024 | tf_op jit(solution)/shard_map/ppermute | solution.py:752
  101.7 29.2 %collective-permute-start.16 = (bf16[1,4112,128]{2,1,0:T(8,128)(2,1)}, bf16[1,4112,128]{2,1,0:T(8,128)(2,1)}, u32[]{:S(2)}, u32[]{:S(2)}) collective-permute-start(bf16[1,4112,128]{2,1,0:T(8,128)(2,1)} %slice.150), channel_id=1, source_target_pairs={{1,5},{2,6},{5,1},{6,2},{9,13},{10,14},{13,9},{14,10},{17,21},{18,... | collective-permute-start | bytes 3158024 | tf_op jit(solution)/shard_map/ppermute | solution.py:752
  131.0 17.7 %collective-permute-start = (bf16[1024,768]{1,0:T(8,128)(2,1)}, bf16[1024,768]{1,0:T(8,128)(2,1)}, u32[]{:S(2)}, u32[]{:S(2)}) collective-permute-start(bf16[1024,768]{1,0:T(8,128)(2,1)} %param.15), channel_id=1, source_target_pairs={{0,2},{3,1},{4,6},{7,5},{8,10},{11,9},{12,14},{15,13},{16,18},{19,... | collective-permute-start | bytes 4718600 | tf_op jit(solution)/shard_map/ppermute | solution.py:752
  133.5 11.9 %collective-permute-start.2 = (s32[1,504]{1,0:T(1,128)S(1)}, s32[1,504]{1,0:T(1,128)S(1)}, u32[]{:S(2)}, u32[]{:S(2)}) collective-permute-start(s32[1,504]{1,0:T(1,128)S(1)} %copy-done.69), channel_id=1, source_target_pairs={{0,1},{1,0},{2,3},{3,2},{4,5},{5,4},{6,7},{7,6},{8,9},{9,8},{10,11... | collective-permute-start | bytes 6056 | tf_op jit(solution)/shard_map/ppermute | solution.py:752
  134.8 39.8 %collective-permute-start.17 = (bf16[2,4112,128]{2,1,0:T(8,128)(2,1)}, bf16[2,4112,128]{2,1,0:T(8,128)(2,1)}, u32[]{:S(2)}, u32[]{:S(2)}) collective-permute-start(bf16[2,4112,128]{2,1,0:T(8,128)(2,1)} %get-tuple-element.155.refs_6_), channel_id=1, source_target_pairs={{0,4},{3,7},{4,0},{7,3},{8,12},{11,15},{12,8},{15,11},{16,20},{19,... | collective-permute-start | bytes 6316040 | tf_op jit(solution)/shard_map/ppermute | solution.py:752
  137.2 37.3 %collective-permute-start.18 = (bf16[2,4112,128]{2,1,0:T(8,128)(2,1)}, bf16[2,4112,128]{2,1,0:T(8,128)(2,1)}, u32[]{:S(2)}, u32[]{:S(2)}) collective-permute-start(bf16[2,4112,128]{2,1,0:T(8,128)(2,1)} %get-tuple-element.155.refs_6_), channel_id=1, source_target_pairs={{0,1},{3,2},{4,5},{7,6},{8,9},{11,10},{12,13},{15,14},{16,17},{19,... | collective-permute-start | bytes 6316040 | tf_op jit(solution)/shard_map/ppermute | solution.py:752
  142.6 31.9 %collective-permute-start.19 = (bf16[1,4112,128]{2,1,0:T(8,128)(2,1)S(1)}, bf16[1,4112,128]{2,1,0:T(8,128)(2,1)S(1)}, u32[]{:S(2)}, u32[]{:S(2)}) collective-permute-start(bf16[1,4112,128]{2,1,0:T(8,128)(2,1)S(1)} %slice.151), channel_id=1, source_target_pairs={{0,1},{3,2},{4,5},{7,6},{8,9},{11,10},{12,13},{15,14},{16,17},{19,... | collective-permute-start | bytes 3158024 | tf_op jit(solution)/shard_map/ppermute | solution.py:752
  145.3 29.2 %collective-permute-start.20 = (bf16[1,4112,128]{2,1,0:T(8,128)(2,1)S(1)}, bf16[1,4112,128]{2,1,0:T(8,128)(2,1)}, u32[]{:S(2)}, u32[]{:S(2)}) collective-permute-start(bf16[1,4112,128]{2,1,0:T(8,128)(2,1)S(1)} %slice.152), channel_id=1, source_target_pairs={{1,5},{2,6},{5,1},{6,2},{9,13},{10,14},{13,9},{14,10},{17,21},{18,... | collective-permute-start | bytes 3158024 | tf_op jit(solution)/shard_map/ppermute | solution.py:752
  176.9 25.6 %collective-permute-start.21 = (bf16[1,4112,128]{2,1,0:T(8,128)(2,1)S(1)}, bf16[1,4112,128]{2,1,0:T(8,128)(2,1)S(1)}, u32[]{:S(2)}, u32[]{:S(2)}) collective-permute-start(bf16[1,4112,128]{2,1,0:T(8,128)(2,1)S(1)} %slice.153), channel_id=1, source_target_pairs={{0,1},{3,2},{4,5},{7,6},{8,9},{11,10},{12,13},{15,14},{16,17},{19,... | collective-permute-start | bytes 3158024 | tf_op jit(solution)/shard_map/ppermute | solution.py:752
  182.7 19.8 %collective-permute-start.22 = (bf16[1,4112,128]{2,1,0:T(8,128)(2,1)S(1)}, bf16[1,4112,128]{2,1,0:T(8,128)(2,1)S(1)}, u32[]{:S(2)}, u32[]{:S(2)}) collective-permute-start(bf16[1,4112,128]{2,1,0:T(8,128)(2,1)S(1)} %slice.154), channel_id=1, source_target_pairs={{1,5},{2,6},{5,1},{6,2},{9,13},{10,14},{13,9},{14,10},{17,21},{18,... | collective-permute-start | bytes 3158024 | tf_op jit(solution)/shard_map/ppermute | solution.py:752
  277.5 33.1 %collective-permute-start.29 = (bf16[1024,768]{1,0:T(8,128)(2,1)S(1)}, bf16[1024,768]{1,0:T(8,128)(2,1)S(1)}, u32[]{:S(2)}, u32[]{:S(2)}) collective-permute-start(bf16[1024,768]{1,0:T(8,128)(2,1)S(1)} %copy-done.52), channel_id=1, source_target_pairs={{0,2},{3,1},{4,6},{7,5},{8,10},{11,9},{12,14},{15,13},{16,18},{19,... | collective-permute-start | bytes 4718600 | tf_op jit(solution)/shard_map/ppermute | solution.py:752
  353.9 34.5 %collective-permute-start.31 = (bf16[1536,768]{1,0:T(8,128)(2,1)}, bf16[1536,768]{1,0:T(8,128)(2,1)}, u32[]{:S(2)}, u32[]{:S(2)}) collective-permute-start(bf16[1536,768]{1,0:T(8,128)(2,1)} %get-tuple-element.194.own), channel_id=1, source_target_pairs={{1,0},{2,3},{5,4},{6,7},{9,8},{10,11},{13,12},{14,15},{17,16},{18,... | collective-permute-start | bytes 7077896 | tf_op jit(solution)/shard_map/ppermute | solution.py:752
  357.3 67.2 %collective-permute-start.33 = (bf16[768,1536]{1,0:T(8,128)(2,1)}, bf16[768,1536]{1,0:T(8,128)(2,1)}, u32[]{:S(2)}, u32[]{:S(2)}) collective-permute-start(bf16[768,1536]{1,0:T(8,128)(2,1)} %get-tuple-element.202.own), channel_id=1, source_target_pairs={{1,0},{2,3},{5,4},{6,7},{9,8},{10,11},{13,12},{14,15},{17,16},{18,... | collective-permute-start | bytes 7077896 | tf_op jit(solution)/shard_map/ppermute | solution.py:752
  424.5 31.1 %collective-permute-start.34 = (bf16[1024,768]{1,0:T(8,128)(2,1)}, bf16[1024,768]{1,0:T(8,128)(2,1)}, u32[]{:S(2)}, u32[]{:S(2)}) collective-permute-start(bf16[1024,768]{1,0:T(8,128)(2,1)} %get-tuple-element.205.refs_0_), channel_id=1, source_target_pairs={{0,2},{1,3},{2,0},{3,1},{4,6},{5,7},{6,4},{7,5},{8,10},{9,11},{10,... | collective-permute-start | bytes 4718600 | tf_op jit(solution)/shard_map/ppermute | solution.py:752
  434.3 21.2 %collective-permute-start.35 = (bf16[384,1152]{1,0:T(8,128)(2,1)S(1)}, bf16[384,1152]{1,0:T(8,128)(2,1)}, u32[]{:S(2)}, u32[]{:S(2)}) collective-permute-start(bf16[384,1152]{1,0:T(8,128)(2,1)S(1)} %constant_dynamic-slice_fusion.2), channel_id=1, source_target_pairs={{1,5},{2,6},{5,1},{6,2},{9,13},{10,14},{13,9},{14,10},{17,21},{18,... | collective-permute-start | bytes 2654216 | tf_op jit(solution)/shard_map/ppermute | solution.py:752
  435.9 19.6 %collective-permute-start.36 = (bf16[384,768]{1,0:T(8,128)(2,1)S(1)}, bf16[384,768]{1,0:T(8,128)(2,1)S(1)}, u32[]{:S(2)}, u32[]{:S(2)}) collective-permute-start(bf16[384,768]{1,0:T(8,128)(2,1)S(1)} %copy-done.24), channel_id=1, source_target_pairs={{1,0},{2,3},{5,4},{6,7},{9,8},{10,11},{13,12},{14,15},{17,16},{18,... | collective-permute-start | bytes 1769480 | tf_op jit(solution)/shard_map/ppermute | solution.py:752
  457.8 35.3 %collective-permute-start.38 = (bf16[768,768]{1,0:T(8,128)(2,1)S(1)}, bf16[768,768]{1,0:T(8,128)(2,1)S(1)}, u32[]{:S(2)}, u32[]{:S(2)}) collective-permute-start(bf16[768,768]{1,0:T(8,128)(2,1)S(1)} %constant_dynamic-slice_fusion.1), channel_id=1, source_target_pairs={{1,5},{2,6},{5,1},{6,2},{9,13},{10,14},{13,9},{14,10},{17,21},{18,... | collective-permute-start | bytes 3538952 | tf_op jit(solution)/shard_map/ppermute | solution.py:752
  458.8 35.2 %collective-permute-start.39 = (bf16[384,1536]{1,0:T(8,128)(2,1)S(1)}, bf16[384,1536]{1,0:T(8,128)(2,1)}, u32[]{:S(2)}, u32[]{:S(2)}) collective-permute-start(bf16[384,1536]{1,0:T(8,128)(2,1)S(1)} %constant_dynamic-slice_fusion), channel_id=1, source_target_pairs={{1,5},{2,6},{5,1},{6,2},{9,13},{10,14},{13,9},{14,10},{17,21},{18,... | collective-permute-start | bytes 3538952 | tf_op jit(solution)/shard_map/ppermute | solution.py:752
  461.9 31.2 %collective-permute-start.37 = (bf16[384,1152]{1,0:T(8,128)(2,1)S(1)}, bf16[384,1152]{1,0:T(8,128)(2,1)S(1)}, u32[]{:S(2)}, u32[]{:S(2)}) collective-permute-start(bf16[384,1152]{1,0:T(8,128)(2,1)S(1)} %add_convert_fusion.4), channel_id=1, source_target_pairs={{1,0},{2,3},{5,4},{6,7},{9,8},{10,11},{13,12},{14,15},{17,16},{18,... | collective-permute-start | bytes 2654216 | tf_op jit(solution)/shard_map/ppermute | solution.py:752
  503.1 17.4 %collective-permute-start.42 = (bf16[1024,768]{1,0:T(8,128)(2,1)}, bf16[1024,768]{1,0:T(8,128)(2,1)S(1)}, u32[]{:S(2)}, u32[]{:S(2)}) collective-permute-start(bf16[1024,768]{1,0:T(8,128)(2,1)} %get-tuple-element.235), channel_id=1, source_target_pairs={{0,2},{1,3},{2,0},{3,1},{4,6},{5,7},{6,4},{7,5},{8,10},{9,11},{10,... | collective-permute-start | bytes 4718600 | tf_op jit(solution)/shard_map/ppermute | solution.py:752
  509.2 21.1 %collective-permute-start.40 = (bf16[768,768]{1,0:T(8,128)(2,1)}, bf16[768,768]{1,0:T(8,128)(2,1)}, u32[]{:S(2)}, u32[]{:S(2)}) collective-permute-start(bf16[768,768]{1,0:T(8,128)(2,1)} %add_convert_fusion.2), channel_id=1, source_target_pairs={{1,0},{2,3},{5,4},{6,7},{9,8},{10,11},{13,12},{14,15},{17,16},{18,... | collective-permute-start | bytes 3538952 | tf_op jit(solution)/shard_map/ppermute | solution.py:752
  513.4 27.0 %collective-permute-start.41 = (bf16[384,1536]{1,0:T(8,128)(2,1)}, bf16[384,1536]{1,0:T(8,128)(2,1)}, u32[]{:S(2)}, u32[]{:S(2)}) collective-permute-start(bf16[384,1536]{1,0:T(8,128)(2,1)} %add_convert_fusion.1), channel_id=1, source_target_pairs={{1,0},{2,3},{5,4},{6,7},{9,8},{10,11},{13,12},{14,15},{17,16},{18,... | collective-permute-start | bytes 3538952 | tf_op jit(solution)/shard_map/ppermute | solution.py:752
  540.4 49.5 %collective-permute-start.44 = (bf16[3072,384]{1,0:T(8,128)(2,1)}, bf16[3072,384]{1,0:T(8,128)(2,1)}, u32[]{:S(2)}, u32[]{:S(2)}) collective-permute-start(bf16[3072,384]{1,0:T(8,128)(2,1)} %get-tuple-element.255.own), channel_id=1, source_target_pairs={{1,0},{2,3},{5,4},{6,7},{9,8},{10,11},{13,12},{14,15},{17,16},{18,... | collective-permute-start | bytes 7077896 | tf_op jit(solution)/shard_map/ppermute | solution.py:752
  549.0 40.9 %collective-permute-start.43 = (bf16[384,1152]{1,0:T(8,128)(2,1)S(1)}, bf16[384,1152]{1,0:T(8,128)(2,1)}, u32[]{:S(2)}, u32[]{:S(2)}) collective-permute-start(bf16[384,1152]{1,0:T(8,128)(2,1)S(1)} %constant_dynamic-slice_fusion.3), channel_id=1, source_target_pairs={{1,5},{2,6},{5,1},{6,2},{9,13},{10,14},{13,9},{14,10},{17,21},{18,... | collective-permute-start | bytes 2654216 | tf_op jit(solution)/shard_map/ppermute | solution.py:752
  557.4 32.5 %collective-permute-start.45 = (bf16[384,768]{1,0:T(8,128)(2,1)S(1)}, bf16[384,768]{1,0:T(8,128)(2,1)S(1)}, u32[]{:S(2)}, u32[]{:S(2)}) collective-permute-start(bf16[384,768]{1,0:T(8,128)(2,1)S(1)} %copy-done.25), channel_id=1, source_target_pairs={{1,0},{2,3},{5,4},{6,7},{9,8},{10,11},{13,12},{14,15},{17,16},{18,... | collective-permute-start | bytes 1769480 | tf_op jit(solution)/shard_map/ppermute | solution.py:752
  558.7 31.2 %collective-permute-start.46 = (bf16[16,16,128]{2,1,0:T(8,128)(2,1)S(1)}, bf16[16,16,128]{2,1,0:T(8,128)(2,1)S(1)}, u32[]{:S(2)}, u32[]{:S(2)}) collective-permute-start(bf16[16,16,128]{2,1,0:T(8,128)(2,1)S(1)} %copy-done.61), channel_id=1, source_target_pairs={{1,0},{2,3},{5,4},{6,7},{9,8},{10,11},{13,12},{14,15},{17,16},{18,... | collective-permute-start | bytes 196616 | tf_op jit(solution)/shard_map/ppermute | solution.py:752
  593.4 18.7 %collective-permute-start.47 = (bf16[384,1152]{1,0:T(8,128)(2,1)}, bf16[384,1152]{1,0:T(8,128)(2,1)S(1)}, u32[]{:S(2)}, u32[]{:S(2)}) collective-permute-start(bf16[384,1152]{1,0:T(8,128)(2,1)} %add_convert_fusion.3), channel_id=1, source_target_pairs={{1,0},{2,3},{5,4},{6,7},{9,8},{10,11},{13,12},{14,15},{17,16},{18,... | collective-permute-start | bytes 2654216 | tf_op jit(solution)/shard_map/ppermute | solution.py:752
  620.1 28.1 %collective-permute-start.50 = (bf16[2,4112,128]{2,1,0:T(8,128)(2,1)S(1)}, bf16[2,4112,128]{2,1,0:T(8,128)(2,1)}, u32[]{:S(2)}, u32[]{:S(2)}) collective-permute-start(bf16[2,4112,128]{2,1,0:T(8,128)(2,1)S(1)} %slice_bitcast_fusion.7), channel_id=1, source_target_pairs={{0,4},{3,7},{4,0},{7,3},{8,12},{11,15},{12,8},{15,11},{16,20},{19,... | collective-permute-start | bytes 6316040 | tf_op jit(solution)/shard_map/ppermute | solution.py:752
  650.0 28.1 %collective-permute-start.51 = (bf16[2,4112,128]{2,1,0:T(8,128)(2,1)S(1)}, bf16[2,4112,128]{2,1,0:T(8,128)(2,1)}, u32[]{:S(2)}, u32[]{:S(2)}) collective-permute-start(bf16[2,4112,128]{2,1,0:T(8,128)(2,1)S(1)} %slice_bitcast_fusion.6), channel_id=1, source_target_pairs={{0,4},{3,7},{4,0},{7,3},{8,12},{11,15},{12,8},{15,11},{16,20},{19,... | collective-permute-start | bytes 6316040 | tf_op jit(solution)/shard_map/ppermute | solution.py:752
  655.7 29.9 %collective-permute-start.52 = (bf16[2,4112,128]{2,1,0:T(8,128)(2,1)S(1)}, bf16[2,4112,128]{2,1,0:T(8,128)(2,1)}, u32[]{:S(2)}, u32[]{:S(2)}) collective-permute-start(bf16[2,4112,128]{2,1,0:T(8,128)(2,1)S(1)} %fusion.16), channel_id=1, source_target_pairs={{0,8},{3,11},{4,12},{7,15},{8,16},{11,19},{12,20},{15,23},{16,24},... | collective-permute-start | bytes 6316040 | tf_op jit(solution)/shard_map/ppermute | solution.py:752
  687.4 28.1 %collective-permute-start.53 = (bf16[2,4112,128]{2,1,0:T(8,128)(2,1)S(1)}, bf16[2,4112,128]{2,1,0:T(8,128)(2,1)}, u32[]{:S(2)}, u32[]{:S(2)}) collective-permute-start(bf16[2,4112,128]{2,1,0:T(8,128)(2,1)S(1)} %slice_bitcast_fusion.4), channel_id=1, source_target_pairs={{0,4},{3,7},{4,0},{7,3},{8,12},{11,15},{12,8},{15,11},{16,20},{19,... | collective-permute-start | bytes 6316040 | tf_op jit(solution)/shard_map/ppermute | solution.py:752
  693.9 29.9 %collective-permute-start.54 = (bf16[2,4112,128]{2,1,0:T(8,128)(2,1)S(1)}, bf16[2,4112,128]{2,1,0:T(8,128)(2,1)}, u32[]{:S(2)}, u32[]{:S(2)}) collective-permute-start(bf16[2,4112,128]{2,1,0:T(8,128)(2,1)S(1)} %fusion.15), channel_id=1, source_target_pairs={{0,8},{3,11},{4,12},{7,15},{8,16},{11,19},{12,20},{15,23},{16,24},... | collective-permute-start | bytes 6316040 | tf_op jit(solution)/shard_map/ppermute | solution.py:752
  695.9 38.6 %collective-permute-start.27 = (bf16[1024,768]{1,0:T(8,128)(2,1)}, bf16[1024,768]{1,0:T(8,128)(2,1)}, u32[]{:S(2)}, u32[]{:S(2)}) collective-permute-start(bf16[1024,768]{1,0:T(8,128)(2,1)} %get-tuple-element.179), channel_id=1, source_target_pairs={{0,2},{1,3},{2,0},{3,1},{4,6},{5,7},{6,4},{7,5},{8,10},{9,11},{10,... | collective-permute-start | bytes 4718600 | tf_op jit(solution)/shard_map/ppermute | solution.py:752
  725.6 28.1 %collective-permute-start.55 = (bf16[2,4112,128]{2,1,0:T(8,128)(2,1)S(1)}, bf16[2,4112,128]{2,1,0:T(8,128)(2,1)}, u32[]{:S(2)}, u32[]{:S(2)}) collective-permute-start(bf16[2,4112,128]{2,1,0:T(8,128)(2,1)S(1)} %slice_bitcast_fusion.2), channel_id=1, source_target_pairs={{0,4},{3,7},{4,0},{7,3},{8,12},{11,15},{12,8},{15,11},{16,20},{19,... | collective-permute-start | bytes 6316040 | tf_op jit(solution)/shard_map/ppermute | solution.py:752
  732.4 29.9 %collective-permute-start.56 = (bf16[2,4112,128]{2,1,0:T(8,128)(2,1)S(1)}, bf16[2,4112,128]{2,1,0:T(8,128)(2,1)}, u32[]{:S(2)}, u32[]{:S(2)}) collective-permute-start(bf16[2,4112,128]{2,1,0:T(8,128)(2,1)S(1)} %fusion.13), channel_id=1, source_target_pairs={{0,8},{3,11},{4,12},{7,15},{8,16},{11,19},{12,20},{15,23},{16,24},... | collective-permute-start | bytes 6316040 | tf_op jit(solution)/shard_map/ppermute | solution.py:752
  738.1 31.8 %collective-permute-start.28 = (bf16[1024,768]{1,0:T(8,128)(2,1)}, bf16[1024,768]{1,0:T(8,128)(2,1)}, u32[]{:S(2)}, u32[]{:S(2)}) collective-permute-start(bf16[1024,768]{1,0:T(8,128)(2,1)} %multiply_convert_fusion), channel_id=1, source_target_pairs={{0,1},{3,2},{4,5},{7,6},{8,9},{11,10},{12,13},{15,14},{16,17},{19,... | collective-permute-start | bytes 4718600 | tf_op jit(solution)/shard_map/ppermute | solution.py:752
  742.0 31.5 %collective-permute-start.49 = (bf16[1024,384]{1,0:T(8,128)(2,1)}, bf16[1024,384]{1,0:T(8,128)(2,1)}, u32[]{:S(2)}, u32[]{:S(2)}) collective-permute-start(bf16[1024,384]{1,0:T(8,128)(2,1)} %select_convert_fusion), channel_id=1, source_target_pairs={{0,1},{3,2},{4,5},{7,6},{8,9},{11,10},{12,13},{15,14},{16,17},{19,... | collective-permute-start | bytes 2359304 | tf_op jit(solution)/shard_map/ppermute | solution.py:752
  (109 other events, 1431.8 us)

commit v2 on v1

--- a/solution.py
+++ b/solution.py
@@ -246,7 +246,7 @@
     )(owner, drow, dcol, flag, *first, *second)
 
 
-def scatter_kernel(rows_n, cols_n, paired, parts, pos, part, own, *refs):
+def scatter_kernel(rows_n, cols_n, steps, paired, parts, pos, part, own, *refs):
     if paired:
         recv, *refs = refs
         span = pl.num_programs(0) // parts
@@ -280,7 +280,8 @@
 
     @pl.when(step == pl.num_programs(0) - 1)
     def _():
-        wait(1 - slot)
+        if steps > 1:
+            wait(1 - slot)
         wait(slot)
 
 
@@ -299,7 +300,7 @@
     specs = [block] + ([block if parts == 1 else arrived] if paired else [])
     specs += [] if target is None else [anywhere]
     return pl.pallas_call(
-        functools.partial(scatter_kernel, rows_n, cols_n, paired, parts),
+        functools.partial(scatter_kernel, rows_n, cols_n, steps, paired, parts),
         out_shape=jax.ShapeDtypeStruct((total_rows, BS), bf16),
         grid_spec=pltpu.PrefetchScalarGridSpec(
             num_scalar_prefetch=2,
@@ -720,15 +721,61 @@
     )(dq, dk, dv, hid, vec, panels)
 
 
-def rotate_step(master, grads, left, right, moment, variance):
-    rotated = jnp.einsum("sji,sjk->sik", left, grads, precision=precise)
-    rotated = jnp.einsum("sik,skl->sil", rotated, right, precision=precise)
-    new_moment = decay * moment + (1.0 - decay) * rotated
-    new_variance = decay * variance + (1.0 - decay) * rotated * rotated
-    step_rot = new_moment / (jnp.sqrt(new_variance) + adam_eps)
-    returned = jnp.einsum("sij,sjk->sik", left, step_rot, precision=precise)
-    returned = jnp.einsum("sik,slk->sil", returned, right, precision=precise)
-    return (master - matrix_rate * returned, new_moment, new_variance)
+def split(values):
+    high = values.astype(bf16)
+    return high, (values - high.astype(f32)).astype(bf16)
+
+
+def product(left, right, left_dim, right_dim):
+    def one(a, b):
+        return lax.dot_general(
+            a, b, (((left_dim,), (right_dim,)), ((), ())), preferred_element_type=f32
+        )
+
+    return one(left[0], right[0]) + (one(left[0], right[1]) + one(left[1], right[0]))
+
+
+def owner_kernel(per, used, low, master, left, right, moment, variance, grad, out, out_mom, out_var):
+    here = range(per)
+    first = pl.program_id(0) * per
+    lefts = [split(left[i]) for i in here]
+    rights = [split(right[i]) for i in here]
+    rotated = []
+    for i in here:
+        tile = jnp.where(used[first + i] > 0, low[i * BS : (i + 1) * BS, :].astype(f32), 0.0)
+        grad[i] = tile
+        tile = tile.astype(bf16)
+        rotated.append(split(dot_tn(lefts[i][0], tile) + dot_tn(lefts[i][1], tile)))
+    rotated = [product(rotated[i], rights[i], 1, 0) for i in here]
+    steps = []
+    for i in here:
+        new_moment = decay * moment[i] + (1.0 - decay) * rotated[i]
+        new_variance = decay * variance[i] + (1.0 - decay) * rotated[i] * rotated[i]
+        out_mom[i] = new_moment
+        out_var[i] = new_variance
+        steps.append(split(new_moment / (jnp.sqrt(new_variance) + adam_eps)))
+    returned = [split(product(lefts[i], steps[i], 1, 0)) for i in here]
+    returned = [product(returned[i], rights[i], 1, 1) for i in here]
+    for i in here:
+        out[i] = master[i] - matrix_rate * returned[i]
+
+
+def owner_call(used, low, *arrays):
+    count = arrays[0].shape[0]
+    per = min(8, count)
+    block = pl.BlockSpec((per, BS, BS), lambda i, *_: (i, 0, 0))
+    return pl.pallas_call(
+        functools.partial(owner_kernel, per),
+        out_shape=[jax.ShapeDtypeStruct(arrays[0].shape, f32)] * 4,
+        grid_spec=pltpu.PrefetchScalarGridSpec(
+            num_scalar_prefetch=1,
+            grid=(count // per,),
+            in_specs=[pl.BlockSpec((per * BS, BS), lambda i, *_: (i, 0))] + [block] * 5,
+            out_specs=[block] * 4,
+        ),
+        compiler_params=params(),
+        cost_estimate=cost(count * 88 * BS**3, count * BS * BS * 38),
+    )(used, low, *arrays)
 
 
 class Routes:
@@ -844,7 +891,9 @@
                     send(acrosses[j - 1][0:1], routes.y_out),
                     send(overs[j - 1][1:2], routes.x_away),
                 ]
-            if j < 4:
+            if j == 1:
+                *moved, base_pix = fence(*moved, base_pix)
+            elif j < 4:
                 moved = list(fence(*moved))
             if j < 3:
                 packs.append(moved.pop(0))
@@ -897,7 +946,7 @@
         caches.append((hidden, normed, queries, keys, values, mixed, lse, middle, normed2, act, slope))
         hidden = middle
     out_low = ((hidden + (own.astype(f32) + recv.astype(f32))) * valid_col).astype(bf16)
-    output = jnp.where(home, out_low, send(out_low, routes.y_out)).astype(f32)
+    out_other = send(out_low, routes.y_out)
 
     owners = jnp.arange(dp_n)
     if grid3:
@@ -927,7 +976,7 @@
     def place_tiles(key, matrix, arrived, buffer):
         tiles = matrix.size // (BS * BS)
         pos = tile_pos[offsets[key] : offsets[key] + tiles]
-        rows_n = BS if matrix.shape[0] < BASE_PIX else 4 * BS
+        rows_n = matrix.shape[0] // 2 if matrix.shape[0] > HALF else HALF
         return scatter_matrix(pos, matrix, arrived, half_at, buffer, total_rows, rows_n)
 
     def over(matrix):
@@ -972,7 +1021,8 @@
     other = send(part, routes.core_all)
     gd1 = dot_tn(caches[top][9], grad_low).astype(bf16)
     gu1 = dot_tn(caches[top][8], du).astype(bf16)
-    part, other, gd1, gu1 = fence(part, other, gd1, gu1)
+    part, other, gd1, gu1, out_other = fence(part, other, gd1, gu1, out_other)
+    output = jnp.where(home, out_low, out_other).astype(f32)
     ad1 = over(gd1)
     grad, grad_low, dq, dk, dv, dbo = attend_step(top, grad, part, other)
     dq, dk, dv, ad1 = hold(dq, dk, dv, ad1)
@@ -997,12 +1047,15 @@
     grad, grad_low, dq, dk, dv, aq1, xd0, xu0, buffer = hold(
         grad, grad_low, dq, dk, dv, aq1, xd0, xu0, buffer
     )
-    ad0 = over(half_sum(gd0, xd0)) if grid3 else None
-    au0 = over(half_sum(gu0, xu0)) if grid3 else None
+    hd0 = half_sum(gd0, xd0) if grid3 else None
+    hu0 = half_sum(gu0, xu0) if grid3 else None
+    go0 = dot_tn(caches[low][5], grad_low).astype(bf16)
+    gq0 = dot_tn(caches[low][1], jnp.concatenate([dq, dk, dv], axis=1)).astype(bf16)
+    dq, dk, dv, hd0, hu0, go0, gq0 = hold(dq, dk, dv, hd0, hu0, go0, gq0)
+    ad0, au0 = over(hd0), over(hu0)
+    xq0 = beside(gq0)
     own, dg1, ds1, dbq, dbv = qkv_back_call(low, dq, dk, dv, caches[low][0], vec, panels)
     recv = send(own, routes.core_all)
-    go0 = dot_tn(caches[low][5], grad_low).astype(bf16)
-    gq0 = dot_tn(caches[low][1], jnp.concatenate([dq, dk, dv], axis=1)).astype(bf16)
     vec_grads[low] = [dg1, ds1, dbq, dbv, dbo, dg2, ds2, db1, db2]
     sides = [
         grad[:, s * HALF : (s + 1) * HALF]
@@ -1019,42 +1072,58 @@
     vec_grad = jnp.pad(vec_grad, (0, dp_n * vec_per - vec_grad.shape[0])).reshape(dp_n, vec_per)
     vec_grad = jnp.pad(vec_grad, ((0, 0), (0, VEC_ROWS * BS - vec_per)))
     vec_grad = vec_grad.astype(bf16).reshape(dp_n, VEC_ROWS, BS)
-    ad0, au0, go0, gq0, gb, vec_grad, grad_emb = hold(ad0, au0, go0, gq0, gb, vec_grad, grad_emb)
-    xq0 = beside(gq0)
-    ab, ao0, av = over(gb), over(go0), over(vec_grad)
+    gb, vec_grad, grad_emb, gq0, xq0 = hold(gb, vec_grad, grad_emb, gq0, xq0)
+    xb = beside(gb)
+    aq0 = over(half_sum(gq0, xq0)) if grid3 else None
+    ao0, av = over(go0), over(vec_grad)
     buffer = place_tiles(("out", top), go1, ao1, buffer)
     buffer = place_tiles(("qkv", top), gq1, aq1, buffer)
     buffer = place_tiles(("down", low), gd0, ad0, buffer)
     buffer = place_tiles(("up", low), gu0, au0, buffer)
-    resized = [dot_tn(pinv[s], base_w).astype(bf16) for s in range(3)]
-    xq0, ab, ao0, av, buffer, *resized = hold(xq0, ab, ao0, av, buffer, *resized)
-    aq0 = over(half_sum(gq0, xq0)) if grid3 else None
-    buffer = place_tiles("base", gb, ab, buffer)
+    xb, buffer = hold(xb, buffer)
+    ab = over(half_sum(gb, xb)) if grid3 else None
     buffer = place_tiles(("out", low), go0, ao0, buffer)
     buffer = scatter_vec(vec_pos, vec_grad, av, buffer)
-    grad_pixels = sum(
-        dot_nt(grad_emb * select_low[:, s : s + 1], resized[s]) for s in range(3)
-    ).astype(bf16)
-    aq0, buffer, grad_pixels = hold(aq0, buffer, grad_pixels)
     buffer = place_tiles(("qkv", low), gq0, aq0, buffer)
-
+    ab, buffer, panels, grad_emb = hold(ab, buffer, panels, grad_emb)
+    buffer = place_tiles("base", gb, ab, buffer)
+
+    def pixel_part(which):
+        base_here = panels[PANELS["base"] : PANELS["base"] + BASE_PIX]
+        return dot_tn(pinv[which], base_here).astype(bf16)
+
+    resized = []
+    grad_pixels = None
     if grid3:
-        carried = None
+        order = (1, 0)
+        block_of = lambda j, x_rel, n: buffer.reshape(4, 2, 2, payload, BS)[j, x_rel, n]
+        across = {n: send(block_of(0, 1, n), routes.x_home) for n in order}
+        carried = {n: None for n in order}
+        rounded = {}
         for j in range(4):
-            block = buffer.reshape(4, 2, 2, payload, BS)
-            arrived = send(block[j, 1], routes.x_home)
-            if carried is not None:
-                arrived, carried, buffer = fence(arrived, carried, buffer)
-            else:
-                arrived, buffer = fence(arrived, buffer)
-            block = buffer.reshape(4, 2, 2, payload, BS)
-            total = block[j, 0].astype(f32) + arrived.astype(f32)
-            if carried is not None:
-                total = total + carried.astype(f32)
-            if j < 3:
-                carried = send(total.astype(bf16), routes.z_home)
-        rounded = total.astype(bf16)
-        mine = jnp.where(home, rounded[0], send(rounded[1], routes.core_out)).astype(f32)
+            for n in order:
+                extra = []
+                if j == 0 or (j == 1 and n == order[0]):
+                    extra = [pixel_part(len(resized))]
+                elif j == 1:
+                    grad_pixels = sum(
+                        dot_nt(grad_emb * select_low[:, s : s + 1], resized[s]) for s in range(3)
+                    ).astype(bf16)
+                    extra = [grad_pixels]
+                across[n], buffer, carried[n], *extra = hold(across[n], buffer, carried[n], *extra)
+                if j == 0 or (j == 1 and n == order[0]):
+                    resized += extra
+                elif j == 1:
+                    [grad_pixels] = extra
+                total = block_of(j, 0, n).astype(f32) + across[n].astype(f32)
+                if carried[n] is not None:
+                    total = total + carried[n].astype(f32)
+                if j < 3:
+                    carried[n] = send(total.astype(bf16), routes.z_home)
+                    across[n] = send(block_of(j + 1, 1, n), routes.x_home)
+                else:
+                    rounded[n] = total.astype(bf16)
+        mine = jnp.where(home, rounded[0], send(rounded[1], routes.core_out))
     else:
         held = buffer.reshape(dp_n, 1, payload, BS).astype(f32)
         nothing = jnp.zeros_like(held)
@@ -1066,7 +1135,11 @@
             [used_rows, jnp.ones((dp_n, 1, VEC_ROWS, 1), bool)], axis=2
         )
         both = jnp.where(used_rows, both, 0.0).reshape(dp_n * TENSOR * payload, BS)
-        mine = lax.psum_scatter(both, AXES, scatter_dimension=0, tiled=True)
+        mine = lax.psum_scatter(both, AXES, scatter_dimension=0, tiled=True).astype(bf16)
+        resized = [pixel_part(s) for s in range(3)]
+        grad_pixels = sum(
+            dot_nt(grad_emb * select_low[:, s : s + 1], resized[s]) for s in range(3)
+        ).astype(bf16)
 
     pixels_other = send(grad_pixels, routes.core_all)
     pixel_sides = [
@@ -1079,13 +1152,11 @@
     patch_grad = jnp.where(home, near, send(far, routes.y_out).astype(f32))
 
     my_slots = dp_pos * slots_per + jnp.arange(slots_per)
-    mine_used = jnp.any(own_slots[None, :] == my_slots[:, None], axis=1)
-    owned_grad = mine[: slots_per * BS].reshape(slots_per, BS, BS)
-    owned_grad = jnp.where(mine_used[:, None, None], owned_grad, 0.0)
-    owned_vec_grad = mine[slots_per * BS :].reshape(VEC_ROWS * BS)[:vec_per]
-    new_master, new_mom, new_var = rotate_step(
-        master_slots[0], owned_grad, left_basis[0], right_basis[0], mom_slots[0], var_slots[0]
+    mine_used = jnp.any(own_slots[None, :] == my_slots[:, None], axis=1).astype(jnp.int32)
+    owned_grad, new_master, new_mom, new_var = owner_call(
+        mine_used, mine, master_slots[0], left_basis[0], right_basis[0], mom_slots[0], var_slots[0]
     )
+    owned_vec_grad = mine[slots_per * BS :].astype(f32).reshape(VEC_ROWS * BS)[:vec_per]
     new_vec_mom = decay * vec_mom[0] + (1.0 - decay) * owned_vec_grad
     new_vec_var = decay * vec_var[0] + (1.0 - decay) * owned_vec_grad * owned_vec_grad
     new_vec = vec_master[0] - vector_rate * new_vec_mom / (jnp.sqrt(new_vec_var) + adam_eps)

time: 815 us -> 771 us (0.946)
  waiting for transfers between devices: 218 us -> 165 us
  starting transfers between devices: 116 us -> 134 us
  Pallas kernels: 260 us -> 245 us
  matrix products: 107 us -> 95.3 us
  local copies, waits for them, and re-layouts: 48.6 us -> 60 us
    ppermute x58 -> x66, waiting for transfers between devices: 218 us -> 165 us  [send(): return lax.ppermute(value, AXES, route)]
    ppermute x58 -> x66, starting transfers between devices: 116 us -> 134 us  [send(): return lax.ppermute(value, AXES, route)]
    dot_general x4 -> x0, matrix products: 16.7 us -> none  [the longest x1 5.85 us: rotate_step(): returned = jnp.einsum('sik,slk->sil', returned, right, precision=precise)]
    unnamed x204 -> x225, local copies, waits for them, and re-layouts: 17.4 us -> 27.5 us
    pallas_call x9 -> x10, Pallas kernels: 53.5 us -> 45.1 us  [the longest x9 34.4 us: scatter_matrix(): pl.pallas_call(functools.partial(scatter_kernel, rows_n, cols_n, steps, p...]
    convert_element_type x6 -> x9, other arithmetic: 17.6 us -> 24 us  [the longest x6 18.2 us: shards(): carried[n] = send(total.astype(bf16), routes.z_home)]
  transfers between devices with their start and end apart: 58 -> 66, of which waited for: 19 -> 22; matrix products, arithmetic and copies ran while one was open for 18% -> 19% of each run, Pallas kernels for 20% -> 18%
where the time goes in v2:
time: 771 us; the launch traced here: 762 us
  Pallas kernels  245 us (32%)
  waiting for transfers between devices  165 us (21%)
  starting transfers between devices  134 us (17%)
  matrix products  95.3 us (12%)
  local copies, waits for them, and re-layouts  60 us (8%)
  other arithmetic  58.6 us (8%)
    ppermute x66, waiting for transfers between devices, send(): return lax.ppermute(value, AXES, route)  165 us
    ppermute x66, starting transfers between devices, send(): return lax.ppermute(value, AXES, route)  134 us
    dot_general x12, matrix products, dot_tn(): lax.dot_general(left, right, (((0,), (0,)), ((), ())), preferred_element_...  62.4 us
    pallas_call x2, Pallas kernels, attend_back_call(): pl.pallas_call(attend_back_kernel, out_shape=[shape(D, f32), shape(D, bf1...  53.2 us
    pallas_call x2, Pallas kernels, attend_call(): pl.pallas_call(functools.partial(attend_kernel, layer), out_shape=[jax.Sh...  39.4 us
    pallas_call x9, Pallas kernels, scatter_matrix(): pl.pallas_call(functools.partial(scatter_kernel, rows_n, cols_n, steps, p...  34.4 us
    pallas_call x2, Pallas kernels, mlp_back_call(): pl.pallas_call(functools.partial(mlp_back_kernel, layer, summed), out_sha...  32.8 us
    unnamed x225, local copies, waits for them, and re-layouts  27.5 us
  transfers between devices with their start and end apart: 66, of which 22 were waited for; matrix products, arithmetic and copies ran while one was open for 19% of the time, Pallas kernels for 18%

profile of v2, /device:TPU:0, one launch (start us, length us, event | category | flops | bytes accessed | tf_op | source)
XLA Modules:
  0.0 761.6 jit_solution(15028760737040617159)
XLA Ops:
  9.3 4.5 collective-permute-start.3
  28.4 9.2 %collective-permute-done.3.refs_2_ = bf16[2,4112,128]{2,1,0:T(8,128)(2,1)S(1)} collective-permute-done((bf16[2,4112,128]{2,1,0:T(8,128)(2,1)}, bf16[2,4112,128]{2,1,0:T(8,128)(2,1)S(1)}, u32[]{:S(2)}, u32[]{:S(2)}) %collective-permute-start.3) | collective-permute-done | bytes 2105376 | tf_op jit(solution)/shard_map/ppermute | solution.py:799
  37.6 4.5 collective-permute-done.2.refs_1_
  42.1 5.2 collective-permute-done.1.refs_0_
  56.9 19.1 %bitcast_convert_fusion.refs_5_ = bf16[1024,3072]{1,0:T(8,128)(2,1)} fusion(bf16[3,3072,768]{2,1,0:T(8,128)(2,1)} %param.19, bf16[1024,3]{0,1:T(4,128)(2,1)S(1)} %add_convert_fusion.7, bf16[1024,768]{1,0:T(8,128)(2,1)S(1)} %copy-done.61), kind=kOutput, calls=%fused_computation | convolution fusion | flops 14501019648 | bytes 22026240 | tf_op jit(solution)/shard_map/dot_general | solution.py:861
  76.0 7.9 %collective-permute-done.7.refs_3_ = bf16[1,4112,128]{2,1,0:T(8,128)(2,1)S(1)} collective-permute-done((bf16[1,4112,128]{2,1,0:T(8,128)(2,1)S(1)}, bf16[1,4112,128]{2,1,0:T(8,128)(2,1)S(1)}, u32[]{:S(2)}, u32[]{:S(2)}) %collective-permute-start.7) | collective-permute-done | bytes 1052704 | tf_op jit(solution)/shard_map/ppermute | solution.py:799
  86.2 5.8 collective-permute-start.14
  99.9 25.9 %collective-permute-done.15.refs_3_ = bf16[1,4112,128]{2,1,0:T(8,128)(2,1)S(1)} collective-permute-done((bf16[1,4112,128]{2,1,0:T(8,128)(2,1)S(1)}, bf16[1,4112,128]{2,1,0:T(8,128)(2,1)S(1)}, u32[]{:S(2)}, u32[]{:S(2)}) %collective-permute-start.15) | collective-permute-done | bytes 1052704 | tf_op jit(solution)/shard_map/ppermute | solution.py:799
  140.9 26.7 %collective-permute-done.19.refs_2_ = bf16[1,4112,128]{2,1,0:T(8,128)(2,1)S(1)} collective-permute-done((bf16[1,4112,128]{2,1,0:T(8,128)(2,1)S(1)}, bf16[1,4112,128]{2,1,0:T(8,128)(2,1)S(1)}, u32[]{:S(2)}, u32[]{:S(2)}) %collective-permute-start.19) | collective-permute-done | bytes 1052704 | tf_op jit(solution)/shard_map/ppermute | solution.py:799
  175.8 4.9 collective-permute-start.21
  181.3 10.8 %collective-permute-done.11 = s32[1,504]{1,0:T(1,128)S(1)} collective-permute-done((s32[1,504]{1,0:T(1,128)S(1)}, s32[1,504]{1,0:T(1,128)S(1)}, u32[]{:S(2)}, u32[]{:S(2)}) %collective-permute-start.11) | collective-permute-done | bytes 2048 | tf_op jit(solution)/shard_map/ppermute | solution.py:799
  193.8 14.9 %shard_map.226 = (bf16[21504,384]{1,0:T(8,128)(2,1)}, bf16[16,16,128]{2,1,0:T(8,128)(2,1)}) custom-call(s32[16]{0:T(128)} %stack.95.owner, s32[512]{0:T(512)} %broadcast_select_fusion.5.drow, s32[512]{0:T(512)} %get-tuple-element.334.dcol, s32[1]{0:T(128)} %bitcast.26.flag, bf16[2,4112,128]{2,1,0:T(8,128)(2,1)} %pad_maximum_fusion.refs_0_, ...), custom_call_target="tpu_custom_call" | custom-call | bytes 33030144 | tf_op jit(solution)/shard_map/pallas_call | solution.py:227
  209.7 5.1 add_convert_fusion.6
  219.2 6.8 shard_map.227
  226.0 19.5 %shard_map.228 = (bf16[1024,384]{1,0:T(8,128)(2,1)}, f32[8,1024]{1,0:T(8,128)}, bf16[1024,768]{1,0:T(8,128)(2,1)}) custom-call(bf16[1024,384]{1,0:T(8,128)(2,1)} %get-tuple-element.189.q_ref, bf16[1024,384]{1,0:T(8,128)(2,1)} %get-tuple-element.190.k_ref, bf16[1024,384]{1,0:T(8,128)(2,1)} %get-tuple-element.191.v_ref, s32[1024,1]{1,0:T(8,128)} %copy.148.seg_q.seg_k, ...), custom_call_target="tpu_custom_call" | custom-call | flops 6442450944 | bytes 6291456 | tf_op jit(solution)/shard_map/pallas_call | solution.py:434
  250.3 13.4 %shard_map.229 = (f32[1024,768]{1,0:T(8,128)}, bf16[1024,768]{1,0:T(8,128)(2,1)}, bf16[1024,1536]{1,0:T(8,128)(2,1)}, bf16[1024,1536]{1,0:T(8,128)(2,1)}, bf16[1024,768]{1,0:T(8,128)(2,1)}) custom-call(f32[1024,768]{1,0:T(8,128)} %maximum_convert_fusion.refs_0_.base.hid, bf16[1024,768]{1,0:T(8,128)(2,1)} %get-tuple-element.192.own, ...), custom_call_target="tpu_custom_call" | custom-call | flops 4831838208 | bytes 18874368 | tf_op jit(solution)/shard_map/pallas_call | solution.py:492
  268.5 7.9 %shard_map.230 = (f32[1024,768]{1,0:T(8,128)}, bf16[1024,768]{1,0:T(8,128)(2,1)}, bf16[1024,384]{1,0:T(8,128)(2,1)}, bf16[1024,384]{1,0:T(8,128)(2,1)}, bf16[1024,384]{1,0:T(8,128)(2,1)}) custom-call(f32[1024,768]{1,0:T(8,128)} %get-tuple-element.193.refs_0_.refs_3_, bf16[1024,768]{1,0:T(8,128)(2,1)} %get-tuple-element.194.refs_1_, ...), custom_call_target="tpu_custom_call" | custom-call | flops 1811939328 | bytes 11010048 | tf_op jit(solution)/shard_map/pallas_call | solution.py:382
  276.4 19.9 %shard_map.231 = (bf16[1024,384]{1,0:T(8,128)(2,1)}, f32[8,1024]{1,0:T(8,128)}, bf16[1024,768]{1,0:T(8,128)(2,1)}) custom-call(bf16[1024,384]{1,0:T(8,128)(2,1)} %get-tuple-element.196.q_ref, bf16[1024,384]{1,0:T(8,128)(2,1)} %get-tuple-element.197.k_ref, bf16[1024,384]{1,0:T(8,128)(2,1)} %get-tuple-element.198.v_ref, s32[1024,1]{1,0:T(8,128)} %copy.148.seg_q.seg_k, ...), custom_call_target="tpu_custom_call" | custom-call | flops 6442450944 | bytes 6291456 | tf_op jit(solution)/shard_map/pallas_call | solution.py:434
  301.1 13.6 %shard_map.232 = (f32[1024,768]{1,0:T(8,128)}, bf16[1024,768]{1,0:T(8,128)(2,1)}, bf16[1024,1536]{1,0:T(8,128)(2,1)}, bf16[1024,1536]{1,0:T(8,128)(2,1)}, bf16[1024,768]{1,0:T(8,128)(2,1)}) custom-call(f32[1024,768]{1,0:T(8,128)} %get-tuple-element.195.base.hid, bf16[1024,768]{1,0:T(8,128)(2,1)} %get-tuple-element.199.own, bf16[1024,768]{1,0:T(8,128)(2,1)} %copy-done.57, ...), custom_call_target="tpu_custom_call" | custom-call | flops 4831838208 | bytes 18874368 | tf_op jit(solution)/shard_map/pallas_call | solution.py:492
  317.0 16.1 %shard_map.233 = (bf16[1024,768]{1,0:T(8,128)(2,1)}, bf16[1024,1536]{1,0:T(8,128)(2,1)}, bf16[1024,768]{1,0:T(8,128)(2,1)}, f32[1,768]{1,0:T(1,128)}, f32[1,768]...) custom-call(bf16[1024,768]{1,0:T(8,128)(2,1)} %broadcast_select_fusion.refs_0_, ...), custom_call_target="tpu_custom_call" | custom-call | flops 4831838208 | bytes 18874368 | tf_op jit(solution)/shard_map/pallas_call | solution.py:549
  334.2 5.0 collective-permute-start.30
  339.2 4.2 convolution_convert_fusion.4.refs_2_
  343.4 4.1 convolution_convert_fusion.3.refs_3_
  347.4 9.5 %collective-permute-done.30.refs_4_ = bf16[1024,768]{1,0:T(8,128)(2,1)S(1)} collective-permute-done((bf16[1024,768]{1,0:T(8,128)(2,1)S(1)}, bf16[1024,768]{1,0:T(8,128)(2,1)S(1)}, u32[]{:S(2)}, u32[]{:S(2)}) %collective-permute-start.30) | collective-permute-done | bytes 1572896 | tf_op jit(solution)/shard_map/ppermute | solution.py:799
  361.5 26.6 %shard_map.235 = (f32[1024,768]{1,0:T(8,128)}, bf16[1024,768]{1,0:T(8,128)(2,1)}, bf16[1024,384]{1,0:T(8,128)(2,1)}, bf16[1024,384]{1,0:T(8,128)(2,1)}, bf16[1024,384]{1,0:T(8,128)(2,1)}, /*index=5*/f32[1,768]{1,0:T(1,128)}) custom-call(s32[4]{0:T(128)} %get-tuple-element.366.low_ref, s32[4]{0:T(128)} %get-tuple-element.365.high_ref, ...), custom_call_target="tpu_custom_call" | custom-call | flops 11274289152 | bytes 15728640 | tf_op jit(solution)/shard_map/pallas_call | solution.py:644
  389.2 7.9 %shard_map.237 = (bf16[1024,768]{1,0:T(8,128)(2,1)}, f32[1,768]{1,0:T(1,128)}, f32[1,768]{1,0:T(1,128)}, f32[1,384]{1,0:T(1,128)}, f32[1,384]{1,0:T(1,128)}) custom-call(bf16[1024,384]{1,0:T(8,128)(2,1)} %get-tuple-element.218.dq, bf16[1024,384]{1,0:T(8,128)(2,1)} %get-tuple-element.219.dk, bf16[1024,384]{1,0:T(8,128)(2,1)} %get-tuple-element.220.dv, ...), custom_call_target="tpu_custom_call" | custom-call | flops 1811939328 | bytes 7864320 | tf_op jit(solution)/shard_map/pallas_call | solution.py:708
  401.2 4.9 convolution_convert_fusion.6.refs_4_
  406.1 16.8 %shard_map.238 = (f32[1024,768]{1,0:T(8,128)}, bf16[1024,768]{1,0:T(8,128)(2,1)}, bf16[1024,1536]{1,0:T(8,128)(2,1)}, bf16[1024,768]{1,0:T(8,128)(2,1)}, f32[1,7...) custom-call(f32[1024,768]{1,0:T(8,128)} %get-tuple-element.213.refs_0_, ...), custom_call_target="tpu_custom_call" | custom-call | flops 4831838208 | bytes 18874368 | tf_op jit(solution)/shard_map/pallas_call | solution.py:549
  425.4 4.5 shard_map.242.refs_1_
  432.6 6.0 convolution_convert_fusion.2.refs_2_
  438.6 4.5 shard_map.243.refs_8_
  443.1 5.8 convolution_convert_fusion.1.refs_3_
  458.1 26.6 %shard_map.241 = (f32[1024,768]{1,0:T(8,128)}, bf16[1024,768]{1,0:T(8,128)(2,1)}, bf16[1024,384]{1,0:T(8,128)(2,1)}, bf16[1024,384]{1,0:T(8,128)(2,1)}, bf16[1024,384]{1,0:T(8,128)(2,1)}, /*index=5*/f32[1,768]{1,0:T(1,128)}) custom-call(s32[4]{0:T(128)} %get-tuple-element.366.low_ref, s32[4]{0:T(128)} %get-tuple-element.365.high_ref, ...), custom_call_target="tpu_custom_call" | custom-call | flops 11274289152 | bytes 15728640 | tf_op jit(solution)/shard_map/pallas_call | solution.py:644
  499.1 8.0 %shard_map.246 = (bf16[1024,768]{1,0:T(8,128)(2,1)}, f32[1,768]{1,0:T(1,128)}, f32[1,768]{1,0:T(1,128)}, f32[1,384]{1,0:T(1,128)}, f32[1,384]{1,0:T(1,128)}) custom-call(bf16[1024,384]{1,0:T(8,128)(2,1)} %get-tuple-element.258.dq, bf16[1024,384]{1,0:T(8,128)(2,1)} %get-tuple-element.259.dk, bf16[1024,384]{1,0:T(8,128)(2,1)} %get-tuple-element.260.dv, ...), custom_call_target="tpu_custom_call" | custom-call | flops 1811939328 | bytes 7864320 | tf_op jit(solution)/shard_map/pallas_call | solution.py:708
  507.0 12.2 %collective-permute-start.40 = (bf16[1024,768]{1,0:T(8,128)(2,1)}, bf16[1024,768]{1,0:T(8,128)(2,1)}, u32[]{:S(2)}, u32[]{:S(2)}) collective-permute-start(bf16[1024,768]{1,0:T(8,128)(2,1)} %get-tuple-element.261), channel_id=1, source_target_pairs={{0,2},{1,3},{2,0},{3,1},{4,6},{5,7},{6,4},{7,5},{8,10},{9,11},{10,... | collective-permute-start | bytes 4718600 | tf_op jit(solution)/shard_map/ppermute | solution.py:799
  528.2 7.7 %convolution_convert_fusion.refs_0_ = bf16[3072,384]{1,0:T(8,128)(2,1)} fusion(bf16[1024,3072]{1,0:T(8,128)(2,1)} %get-tuple-element.172, bf16[1024,384]{1,0:T(8,128)(2,1)S(1)} %get-tuple-element.345.refs_2_), kind=kOutput, calls=%fused_computation.11 | convolution fusion | flops 2417098752 | bytes 9437184 | tf_op jit(solution)/shard_map/dot_general | solution.py:123
  547.7 6.6 collective-permute-done.44.refs_0_
  554.2 4.1 shard_map.250.refs_1_
  558.4 4.1 shard_map.251.refs_1_
  572.0 28.3 %collective-permute-done.48.refs_0_ = bf16[384,768]{1,0:T(8,128)(2,1)S(1)} collective-permute-done((bf16[384,768]{1,0:T(8,128)(2,1)S(1)}, bf16[384,768]{1,0:T(8,128)(2,1)S(1)}, u32[]{:S(2)}, u32[]{:S(2)}) %collective-permute-start.48) | collective-permute-done | bytes 589856 | tf_op jit(solution)/shard_map/ppermute | solution.py:799
  612.6 6.6 fusion.63.refs_2_
  619.2 4.1 shard_map.257.refs_1_
  631.1 6.5 fusion.58.refs_3_
  637.6 6.5 fusion.68.refs_2_
  680.4 4.8 collective-permute-start.59
  711.7 4.8 collective-permute-done.60.refs_2_
  739.2 5.1 collective-permute-done.64.refs_2_
  750.4 10.7 %shard_map.266 = (f32[32,128,128]{2,1,0:T(8,128)}, f32[32,128,128]{2,1,0:T(8,128)}, f32[32,128,128]{2,1,0:T(8,128)}, f32[32,128,128]{2,1,0:T(8,128)}) custom-call(s32[32]{0:T(128)} %convert_element_type.376.used, bf16[4112,128]{1,0:T(8,128)(2,1)} %copy-done.66, f32[32,128,128]{2,1,0:T(8,128)} %bitcast.206, f32[32,128,128]{2,1,0:T(8,128)} %bitcast.221, ...), custom_call_target="tpu_custom_call" | custom-call | flops 5905580032 | bytes 19922944 | tf_op jit(solution)/shard_map/pallas_call | solution.py:767
  (477 shorter events, 270.4 us)
Async XLA Ops:
  9.3 28.3 %collective-permute-start.3 = (bf16[2,4112,128]{2,1,0:T(8,128)(2,1)}, bf16[2,4112,128]{2,1,0:T(8,128)(2,1)S(1)}, u32[]{:S(2)}, u32[]{:S(2)}) collective-permute-start(bf16[2,4112,128]{2,1,0:T(8,128)(2,1)} %pad_maximum_fusion.refs_0_), channel_id=1, source_target_pairs={{0,1},{3,2},{4,5},{7,6},{8,9},{11,10},{12,13},{15,14},{16,17},{19,... | collective-permute-start | bytes 6316040 | tf_op jit(solution)/shard_map/ppermute | solution.py:799
  13.8 28.3 %collective-permute-start.2 = (bf16[2,4112,128]{2,1,0:T(8,128)(2,1)}, bf16[2,4112,128]{2,1,0:T(8,128)(2,1)}, u32[]{:S(2)}, u32[]{:S(2)}) collective-permute-start(bf16[2,4112,128]{2,1,0:T(8,128)(2,1)} %pad_maximum_fusion.refs_0_), channel_id=1, source_target_pairs={{0,4},{3,7},{4,0},{7,3},{8,12},{11,15},{12,8},{15,11},{16,20},{19,... | collective-permute-start | bytes 6316040 | tf_op jit(solution)/shard_map/ppermute | solution.py:799
  17.2 30.1 %collective-permute-start.1 = (bf16[2,4112,128]{2,1,0:T(8,128)(2,1)}, bf16[2,4112,128]{2,1,0:T(8,128)(2,1)}, u32[]{:S(2)}, u32[]{:S(2)}) collective-permute-start(bf16[2,4112,128]{2,1,0:T(8,128)(2,1)} %pad_maximum_fusion.refs_0_), channel_id=1, source_target_pairs={{0,8},{3,11},{4,12},{7,15},{8,16},{11,19},{12,20},{15,23},{16,24},... | collective-permute-start | bytes 6316040 | tf_op jit(solution)/shard_map/ppermute | solution.py:799
  47.3 36.5 %collective-permute-start.6 = (bf16[2,4112,128]{2,1,0:T(8,128)(2,1)}, bf16[2,4112,128]{2,1,0:T(8,128)(2,1)S(1)}, u32[]{:S(2)}, u32[]{:S(2)}) collective-permute-start(bf16[2,4112,128]{2,1,0:T(8,128)(2,1)} %get-tuple-element.169.refs_2_), channel_id=1, source_target_pairs={{0,1},{3,2},{4,5},{7,6},{8,9},{11,10},{12,13},{15,14},{16,17},{19,... | collective-permute-start | bytes 6316040 | tf_op jit(solution)/shard_map/ppermute | solution.py:799
  48.9 36.0 %collective-permute-start.5 = (bf16[2,4112,128]{2,1,0:T(8,128)(2,1)}, bf16[2,4112,128]{2,1,0:T(8,128)(2,1)}, u32[]{:S(2)}, u32[]{:S(2)}) collective-permute-start(bf16[2,4112,128]{2,1,0:T(8,128)(2,1)} %get-tuple-element.169.refs_2_), channel_id=1, source_target_pairs={{0,4},{3,7},{4,0},{7,3},{8,12},{11,15},{12,8},{15,11},{16,20},{19,... | collective-permute-start | bytes 6316040 | tf_op jit(solution)/shard_map/ppermute | solution.py:799
  51.3 33.5 %collective-permute-start.4 = (bf16[2,4112,128]{2,1,0:T(8,128)(2,1)}, bf16[2,4112,128]{2,1,0:T(8,128)(2,1)}, u32[]{:S(2)}, u32[]{:S(2)}) collective-permute-start(bf16[2,4112,128]{2,1,0:T(8,128)(2,1)} %get-tuple-element.169.refs_2_), channel_id=1, source_target_pairs={{0,8},{3,11},{4,12},{7,15},{8,16},{11,19},{12,20},{15,23},{16,24},... | collective-permute-start | bytes 6316040 | tf_op jit(solution)/shard_map/ppermute | solution.py:799
  54.8 21.2 %collective-permute-start.8 = (bf16[1,4112,128]{2,1,0:T(8,128)(2,1)S(1)}, bf16[1,4112,128]{2,1,0:T(8,128)(2,1)S(1)}, u32[]{:S(2)}, u32[]{:S(2)}) collective-permute-start(bf16[1,4112,128]{2,1,0:T(8,128)(2,1)S(1)} %slice.169), channel_id=1, source_target_pairs={{1,5},{2,6},{5,1},{6,2},{9,13},{10,14},{13,9},{14,10},{17,21},{18,... | collective-permute-start | bytes 3158024 | tf_op jit(solution)/shard_map/ppermute | solution.py:799
  55.5 28.3 %collective-permute-start.7 = (bf16[1,4112,128]{2,1,0:T(8,128)(2,1)S(1)}, bf16[1,4112,128]{2,1,0:T(8,128)(2,1)S(1)}, u32[]{:S(2)}, u32[]{:S(2)}) collective-permute-start(bf16[1,4112,128]{2,1,0:T(8,128)(2,1)S(1)} %slice.168), channel_id=1, source_target_pairs={{0,1},{3,2},{4,5},{7,6},{8,9},{11,10},{12,13},{15,14},{16,17},{19,... | collective-permute-start | bytes 3158024 | tf_op jit(solution)/shard_map/ppermute | solution.py:799
  86.2 39.6 %collective-permute-start.14 = (bf16[2,4112,128]{2,1,0:T(8,128)(2,1)}, bf16[2,4112,128]{2,1,0:T(8,128)(2,1)}, u32[]{:S(2)}, u32[]{:S(2)}) collective-permute-start(bf16[2,4112,128]{2,1,0:T(8,128)(2,1)} %get-tuple-element.174.refs_4_), channel_id=1, source_target_pairs={{0,1},{3,2},{4,5},{7,6},{8,9},{11,10},{12,13},{15,14},{16,17},{19,... | collective-permute-start | bytes 6316040 | tf_op jit(solution)/shard_map/ppermute | solution.py:799
  92.0 37.7 %collective-permute-start.13 = (bf16[2,4112,128]{2,1,0:T(8,128)(2,1)}, bf16[2,4112,128]{2,1,0:T(8,128)(2,1)}, u32[]{:S(2)}, u32[]{:S(2)}) collective-permute-start(bf16[2,4112,128]{2,1,0:T(8,128)(2,1)} %get-tuple-element.174.refs_4_), channel_id=1, source_target_pairs={{0,4},{3,7},{4,0},{7,3},{8,12},{11,15},{12,8},{15,11},{16,20},{19,... | collective-permute-start | bytes 6316040 | tf_op jit(solution)/shard_map/ppermute | solution.py:799
  94.4 35.3 %collective-permute-start.12 = (bf16[2,4112,128]{2,1,0:T(8,128)(2,1)}, bf16[2,4112,128]{2,1,0:T(8,128)(2,1)S(1)}, u32[]{:S(2)}, u32[]{:S(2)}) collective-permute-start(bf16[2,4112,128]{2,1,0:T(8,128)(2,1)} %get-tuple-element.174.refs_4_), channel_id=1, source_target_pairs={{0,8},{3,11},{4,12},{7,15},{8,16},{11,19},{12,20},{15,23},{16,24},... | collective-permute-start | bytes 6316040 | tf_op jit(solution)/shard_map/ppermute | solution.py:799
  98.5 27.3 %collective-permute-start.15 = (bf16[1,4112,128]{2,1,0:T(8,128)(2,1)S(1)}, bf16[1,4112,128]{2,1,0:T(8,128)(2,1)S(1)}, u32[]{:S(2)}, u32[]{:S(2)}) collective-permute-start(bf16[1,4112,128]{2,1,0:T(8,128)(2,1)S(1)} %slice.170), channel_id=1, source_target_pairs={{0,1},{3,2},{4,5},{7,6},{8,9},{11,10},{12,13},{15,14},{16,17},{19,... | collective-permute-start | bytes 3158024 | tf_op jit(solution)/shard_map/ppermute | solution.py:799
  131.0 36.6 %collective-permute-start.18 = (bf16[2,4112,128]{2,1,0:T(8,128)(2,1)}, bf16[2,4112,128]{2,1,0:T(8,128)(2,1)S(1)}, u32[]{:S(2)}, u32[]{:S(2)}) collective-permute-start(bf16[2,4112,128]{2,1,0:T(8,128)(2,1)} %get-tuple-element.177.refs_6_), channel_id=1, source_target_pairs={{0,1},{3,2},{4,5},{7,6},{8,9},{11,10},{12,13},{15,14},{16,17},{19,... | collective-permute-start | bytes 6316040 | tf_op jit(solution)/shard_map/ppermute | solution.py:799
  132.6 38.6 %collective-permute-start.17 = (bf16[2,4112,128]{2,1,0:T(8,128)(2,1)}, bf16[2,4112,128]{2,1,0:T(8,128)(2,1)}, u32[]{:S(2)}, u32[]{:S(2)}) collective-permute-start(bf16[2,4112,128]{2,1,0:T(8,128)(2,1)} %get-tuple-element.177.refs_6_), channel_id=1, source_target_pairs={{0,4},{3,7},{4,0},{7,3},{8,12},{11,15},{12,8},{15,11},{16,20},{19,... | collective-permute-start | bytes 6316040 | tf_op jit(solution)/shard_map/ppermute | solution.py:799
  138.4 29.2 %collective-permute-start.19 = (bf16[1,4112,128]{2,1,0:T(8,128)(2,1)S(1)}, bf16[1,4112,128]{2,1,0:T(8,128)(2,1)S(1)}, u32[]{:S(2)}, u32[]{:S(2)}) collective-permute-start(bf16[1,4112,128]{2,1,0:T(8,128)(2,1)S(1)} %slice.172), channel_id=1, source_target_pairs={{0,1},{3,2},{4,5},{7,6},{8,9},{11,10},{12,13},{15,14},{16,17},{19,... | collective-permute-start | bytes 3158024 | tf_op jit(solution)/shard_map/ppermute | solution.py:799
  174.2 19.6 %collective-permute-start.22 = (bf16[1,4112,128]{2,1,0:T(8,128)(2,1)}, bf16[1,4112,128]{2,1,0:T(8,128)(2,1)}, u32[]{:S(2)}, u32[]{:S(2)}) collective-permute-start(bf16[1,4112,128]{2,1,0:T(8,128)(2,1)} %slice.175), channel_id=1, source_target_pairs={{1,5},{2,6},{5,1},{6,2},{9,13},{10,14},{13,9},{14,10},{17,21},{18,... | collective-permute-start | bytes 3158024 | tf_op jit(solution)/shard_map/ppermute | solution.py:799
  296.5 19.2 %collective-permute-start.28 = (bf16[1024,768]{1,0:T(8,128)(2,1)S(1)}, bf16[1024,768]{1,0:T(8,128)(2,1)S(1)}, u32[]{:S(2)}, u32[]{:S(2)}) collective-permute-start(bf16[1024,768]{1,0:T(8,128)(2,1)S(1)} %copy-done.59), channel_id=1, source_target_pairs={{0,2},{3,1},{4,6},{7,5},{8,10},{11,9},{12,14},{15,13},{16,18},{19,... | collective-permute-start | bytes 4718600 | tf_op jit(solution)/shard_map/ppermute | solution.py:799
  314.7 18.8 %collective-permute-start.27 = (bf16[1024,768]{1,0:T(8,128)(2,1)}, bf16[1024,768]{1,0:T(8,128)(2,1)S(1)}, u32[]{:S(2)}, u32[]{:S(2)}) collective-permute-start(bf16[1024,768]{1,0:T(8,128)(2,1)} %get-tuple-element.201), channel_id=1, source_target_pairs={{0,2},{1,3},{2,0},{3,1},{4,6},{5,7},{6,4},{7,5},{8,10},{9,11},{10,... | collective-permute-start | bytes 4718600 | tf_op jit(solution)/shard_map/ppermute | solution.py:799
  334.2 22.8 %collective-permute-start.30 = (bf16[1024,768]{1,0:T(8,128)(2,1)S(1)}, bf16[1024,768]{1,0:T(8,128)(2,1)S(1)}, u32[]{:S(2)}, u32[]{:S(2)}) collective-permute-start(bf16[1024,768]{1,0:T(8,128)(2,1)S(1)} %multiply_convert_fusion), channel_id=1, source_target_pairs={{0,1},{3,2},{4,5},{7,6},{8,9},{11,10},{12,13},{15,14},{16,17},{19,... | collective-permute-start | bytes 4718600 | tf_op jit(solution)/shard_map/ppermute | solution.py:799
  358.1 31.0 %collective-permute-start.31 = (bf16[1536,768]{1,0:T(8,128)(2,1)}, bf16[1536,768]{1,0:T(8,128)(2,1)}, u32[]{:S(2)}, u32[]{:S(2)}) collective-permute-start(bf16[1536,768]{1,0:T(8,128)(2,1)} %get-tuple-element.217.own), channel_id=1, source_target_pairs={{1,0},{2,3},{5,4},{6,7},{9,8},{10,11},{13,12},{14,15},{17,16},{18,... | collective-permute-start | bytes 7077896 | tf_op jit(solution)/shard_map/ppermute | solution.py:799
  360.2 62.6 %collective-permute-start.33 = (bf16[768,1536]{1,0:T(8,128)(2,1)}, bf16[768,1536]{1,0:T(8,128)(2,1)S(1)}, u32[]{:S(2)}, u32[]{:S(2)}) collective-permute-start(bf16[768,1536]{1,0:T(8,128)(2,1)} %get-tuple-element.226.own), channel_id=1, source_target_pairs={{1,0},{2,3},{5,4},{6,7},{9,8},{10,11},{13,12},{14,15},{17,16},{18,... | collective-permute-start | bytes 7077896 | tf_op jit(solution)/shard_map/ppermute | solution.py:799
  424.3 24.6 %collective-permute-start.34 = (bf16[1024,768]{1,0:T(8,128)(2,1)}, bf16[1024,768]{1,0:T(8,128)(2,1)S(1)}, u32[]{:S(2)}, u32[]{:S(2)}) collective-permute-start(bf16[1024,768]{1,0:T(8,128)(2,1)} %get-tuple-element.229.refs_0_), channel_id=1, source_target_pairs={{0,2},{1,3},{2,0},{3,1},{4,6},{5,7},{6,4},{7,5},{8,10},{9,11},{10,... | collective-permute-start | bytes 4718600 | tf_op jit(solution)/shard_map/ppermute | solution.py:799
  429.9 19.0 %collective-permute-start.36 = (bf16[384,768]{1,0:T(8,128)(2,1)S(1)}, bf16[384,768]{1,0:T(8,128)(2,1)S(1)}, u32[]{:S(2)}, u32[]{:S(2)}) collective-permute-start(bf16[384,768]{1,0:T(8,128)(2,1)S(1)} %copy-done.29), channel_id=1, source_target_pairs={{1,0},{2,3},{5,4},{6,7},{9,8},{10,11},{13,12},{14,15},{17,16},{18,... | collective-permute-start | bytes 1769480 | tf_op jit(solution)/shard_map/ppermute | solution.py:799
  452.7 32.1 %collective-permute-start.39 = (bf16[384,1536]{1,0:T(8,128)(2,1)S(1)}, bf16[384,1536]{1,0:T(8,128)(2,1)S(1)}, u32[]{:S(2)}, u32[]{:S(2)}) collective-permute-start(bf16[384,1536]{1,0:T(8,128)(2,1)S(1)} %constant_dynamic-slice_fusion.1), channel_id=1, source_target_pairs={{1,5},{2,6},{5,1},{6,2},{9,13},{10,14},{13,9},{14,10},{17,21},{18,... | collective-permute-start | bytes 3538952 | tf_op jit(solution)/shard_map/ppermute | solution.py:799
  453.7 32.0 %collective-permute-start.38 = (bf16[768,768]{1,0:T(8,128)(2,1)S(1)}, bf16[768,768]{1,0:T(8,128)(2,1)}, u32[]{:S(2)}, u32[]{:S(2)}) collective-permute-start(bf16[768,768]{1,0:T(8,128)(2,1)S(1)} %constant_dynamic-slice_fusion.2), channel_id=1, source_target_pairs={{1,5},{2,6},{5,1},{6,2},{9,13},{10,14},{13,9},{14,10},{17,21},{18,... | collective-permute-start | bytes 3538952 | tf_op jit(solution)/shard_map/ppermute | solution.py:799
  456.8 27.9 %collective-permute-start.37 = (bf16[384,1152]{1,0:T(8,128)(2,1)S(1)}, bf16[384,1152]{1,0:T(8,128)(2,1)S(1)}, u32[]{:S(2)}, u32[]{:S(2)}) collective-permute-start(bf16[384,1152]{1,0:T(8,128)(2,1)S(1)} %add_convert_fusion.5), channel_id=1, source_target_pairs={{1,0},{2,3},{5,4},{6,7},{9,8},{10,11},{13,12},{14,15},{17,16},{18,... | collective-permute-start | bytes 2654216 | tf_op jit(solution)/shard_map/ppermute | solution.py:799
  521.0 37.4 %collective-permute-start.43 = (bf16[384,1536]{1,0:T(8,128)(2,1)}, bf16[384,1536]{1,0:T(8,128)(2,1)}, u32[]{:S(2)}, u32[]{:S(2)}) collective-permute-start(bf16[384,1536]{1,0:T(8,128)(2,1)} %get-tuple-element.282), channel_id=1, source_target_pairs={{1,0},{2,3},{5,4},{6,7},{9,8},{10,11},{13,12},{14,15},{17,16},{18,... | collective-permute-start | bytes 3538952 | tf_op jit(solution)/shard_map/ppermute | solution.py:799
  522.3 32.0 %collective-permute-start.44 = (bf16[768,768]{1,0:T(8,128)(2,1)}, bf16[768,768]{1,0:T(8,128)(2,1)}, u32[]{:S(2)}, u32[]{:S(2)}) collective-permute-start(bf16[768,768]{1,0:T(8,128)(2,1)} %get-tuple-element.283), channel_id=1, source_target_pairs={{1,0},{2,3},{5,4},{6,7},{9,8},{10,11},{13,12},{14,15},{17,16},{18,... | collective-permute-start | bytes 3538952 | tf_op jit(solution)/shard_map/ppermute | solution.py:799
  539.2 23.3 %collective-permute-start.42 = (bf16[1536,384]{1,0:T(8,128)(2,1)}, bf16[1536,384]{1,0:T(8,128)(2,1)S(1)}, u32[]{:S(2)}, u32[]{:S(2)}) collective-permute-start(bf16[1536,384]{1,0:T(8,128)(2,1)} %constant_dynamic-slice_fusion.4), channel_id=1, source_target_pairs={{1,5},{2,6},{5,1},{6,2},{9,13},{10,14},{13,9},{14,10},{17,21},{18,... | collective-permute-start | bytes 3538952 | tf_op jit(solution)/shard_map/ppermute | solution.py:799
  566.3 45.2 %collective-permute-start.45 = (bf16[1536,384]{1,0:T(8,128)(2,1)S(1)}, bf16[1536,384]{1,0:T(8,128)(2,1)S(1)}, u32[]{:S(2)}, u32[]{:S(2)}) collective-permute-start(bf16[1536,384]{1,0:T(8,128)(2,1)S(1)} %add_convert_fusion.1), channel_id=1, source_target_pairs={{1,0},{2,3},{5,4},{6,7},{9,8},{10,11},{13,12},{14,15},{17,16},{18,... | collective-permute-start | bytes 3538952 | tf_op jit(solution)/shard_map/ppermute | solution.py:799
  568.1 38.9 %collective-permute-start.46 = (bf16[384,1152]{1,0:T(8,128)(2,1)S(1)}, bf16[384,1152]{1,0:T(8,128)(2,1)S(1)}, u32[]{:S(2)}, u32[]{:S(2)}) collective-permute-start(bf16[384,1152]{1,0:T(8,128)(2,1)S(1)} %add_convert_fusion.4), channel_id=1, source_target_pairs={{1,0},{2,3},{5,4},{6,7},{9,8},{10,11},{13,12},{14,15},{17,16},{18,... | collective-permute-start | bytes 2654216 | tf_op jit(solution)/shard_map/ppermute | solution.py:799
  569.4 31.0 %collective-permute-start.48 = (bf16[384,768]{1,0:T(8,128)(2,1)S(1)}, bf16[384,768]{1,0:T(8,128)(2,1)S(1)}, u32[]{:S(2)}, u32[]{:S(2)}) collective-permute-start(bf16[384,768]{1,0:T(8,128)(2,1)S(1)} %copy-done.30), channel_id=1, source_target_pairs={{1,0},{2,3},{5,4},{6,7},{9,8},{10,11},{13,12},{14,15},{17,16},{18,... | collective-permute-start | bytes 1769480 | tf_op jit(solution)/shard_map/ppermute | solution.py:799
  570.7 33.4 %collective-permute-start.47 = (bf16[16,16,128]{2,1,0:T(8,128)(2,1)S(1)}, bf16[16,16,128]{2,1,0:T(8,128)(2,1)S(1)}, u32[]{:S(2)}, u32[]{:S(2)}) collective-permute-start(bf16[16,16,128]{2,1,0:T(8,128)(2,1)S(1)} %copy-done.68), channel_id=1, source_target_pairs={{1,0},{2,3},{5,4},{6,7},{9,8},{10,11},{13,12},{14,15},{17,16},{18,... | collective-permute-start | bytes 196616 | tf_op jit(solution)/shard_map/ppermute | solution.py:799
  625.0 19.1 %collective-permute-start.50 = (bf16[4112,128]{1,0:T(8,128)(2,1)S(1)}, bf16[4112,128]{1,0:T(8,128)(2,1)S(1)}, u32[]{:S(2)}, u32[]{:S(2)}) collective-permute-start(bf16[4112,128]{1,0:T(8,128)(2,1)S(1)} %get-tuple-element.348), channel_id=1, source_target_pairs={{0,4},{3,7},{4,0},{7,3},{8,12},{11,15},{12,8},{15,11},{16,20},{19,... | collective-permute-start | bytes 3158024 | tf_op jit(solution)/shard_map/ppermute | solution.py:799
  627.8 26.8 %collective-permute-start.49 = (bf16[4112,128]{1,0:T(8,128)(2,1)S(1)}, bf16[4112,128]{1,0:T(8,128)(2,1)S(1)}, u32[]{:S(2)}, u32[]{:S(2)}) collective-permute-start(bf16[4112,128]{1,0:T(8,128)(2,1)S(1)} %get-tuple-element.349), channel_id=1, source_target_pairs={{0,4},{3,7},{4,0},{7,3},{8,12},{11,15},{12,8},{15,11},{16,20},{19,... | collective-permute-start | bytes 3158024 | tf_op jit(solution)/shard_map/ppermute | solution.py:799
  647.4 23.8 %collective-permute-start.52 = (bf16[4112,128]{1,0:T(8,128)(2,1)}, bf16[4112,128]{1,0:T(8,128)(2,1)}, u32[]{:S(2)}, u32[]{:S(2)}) collective-permute-start(bf16[4112,128]{1,0:T(8,128)(2,1)} %slice_bitcast_fusion.12), channel_id=1, source_target_pairs={{0,4},{3,7},{4,0},{7,3},{8,12},{11,15},{12,8},{15,11},{16,20},{19,... | collective-permute-start | bytes 3158024 | tf_op jit(solution)/shard_map/ppermute | solution.py:799
  652.8 18.8 %collective-permute-start.53 = (bf16[4112,128]{1,0:T(8,128)(2,1)}, bf16[4112,128]{1,0:T(8,128)(2,1)}, u32[]{:S(2)}, u32[]{:S(2)}) collective-permute-start(bf16[4112,128]{1,0:T(8,128)(2,1)} %fusion.37), channel_id=1, source_target_pairs={{0,8},{3,11},{4,12},{7,15},{8,16},{11,19},{12,20},{15,23},{16,24},... | collective-permute-start | bytes 3158024 | tf_op jit(solution)/shard_map/ppermute | solution.py:799
  660.8 27.7 %collective-permute-start.51 = (bf16[4112,128]{1,0:T(8,128)(2,1)}, bf16[4112,128]{1,0:T(8,128)(2,1)S(1)}, u32[]{:S(2)}, u32[]{:S(2)}) collective-permute-start(bf16[4112,128]{1,0:T(8,128)(2,1)} %slice_bitcast_fusion.13), channel_id=1, source_target_pairs={{0,4},{3,7},{4,0},{7,3},{8,12},{11,15},{12,8},{15,11},{16,20},{19,... | collective-permute-start | bytes 3158024 | tf_op jit(solution)/shard_map/ppermute | solution.py:799
  663.8 24.7 %collective-permute-start.54 = (bf16[4112,128]{1,0:T(8,128)(2,1)}, bf16[4112,128]{1,0:T(8,128)(2,1)}, u32[]{:S(2)}, u32[]{:S(2)}) collective-permute-start(bf16[4112,128]{1,0:T(8,128)(2,1)} %fusion.36), channel_id=1, source_target_pairs={{0,8},{3,11},{4,12},{7,15},{8,16},{11,19},{12,20},{15,23},{16,24},... | collective-permute-start | bytes 3158024 | tf_op jit(solution)/shard_map/ppermute | solution.py:799
  674.0 27.4 %collective-permute-start.58 = (bf16[4112,128]{1,0:T(8,128)(2,1)}, bf16[4112,128]{1,0:T(8,128)(2,1)}, u32[]{:S(2)}, u32[]{:S(2)}) collective-permute-start(bf16[4112,128]{1,0:T(8,128)(2,1)} %slice_bitcast_fusion.8), channel_id=1, source_target_pairs={{0,4},{3,7},{4,0},{7,3},{8,12},{11,15},{12,8},{15,11},{16,20},{19,... | collective-permute-start | bytes 3158024 | tf_op jit(solution)/shard_map/ppermute | solution.py:799
  680.4 21.0 %collective-permute-start.59 = (bf16[4112,128]{1,0:T(8,128)(2,1)}, bf16[4112,128]{1,0:T(8,128)(2,1)}, u32[]{:S(2)}, u32[]{:S(2)}) collective-permute-start(bf16[4112,128]{1,0:T(8,128)(2,1)} %fusion.35), channel_id=1, source_target_pairs={{0,8},{3,11},{4,12},{7,15},{8,16},{11,19},{12,20},{15,23},{16,24},... | collective-permute-start | bytes 3158024 | tf_op jit(solution)/shard_map/ppermute | solution.py:799
  691.9 19.9 %collective-permute-start.57 = (bf16[4112,128]{1,0:T(8,128)(2,1)}, bf16[4112,128]{1,0:T(8,128)(2,1)}, u32[]{:S(2)}, u32[]{:S(2)}) collective-permute-start(bf16[4112,128]{1,0:T(8,128)(2,1)} %slice_bitcast_fusion.9), channel_id=1, source_target_pairs={{0,4},{3,7},{4,0},{7,3},{8,12},{11,15},{12,8},{15,11},{16,20},{19,... | collective-permute-start | bytes 3158024 | tf_op jit(solution)/shard_map/ppermute | solution.py:799
  697.7 18.8 %collective-permute-start.60 = (bf16[4112,128]{1,0:T(8,128)(2,1)}, bf16[4112,128]{1,0:T(8,128)(2,1)}, u32[]{:S(2)}, u32[]{:S(2)}) collective-permute-start(bf16[4112,128]{1,0:T(8,128)(2,1)} %fusion.33), channel_id=1, source_target_pairs={{0,8},{3,11},{4,12},{7,15},{8,16},{11,19},{12,20},{15,23},{16,24},... | collective-permute-start | bytes 3158024 | tf_op jit(solution)/shard_map/ppermute | solution.py:799
  701.4 25.9 %collective-permute-start.55 = (bf16[1024,768]{1,0:T(8,128)(2,1)S(1)}, bf16[1024,768]{1,0:T(8,128)(2,1)S(1)}, u32[]{:S(2)}, u32[]{:S(2)}) collective-permute-start(bf16[1024,768]{1,0:T(8,128)(2,1)S(1)} %copy-done.4), channel_id=1, source_target_pairs={{0,2},{1,3},{2,0},{3,1},{4,6},{5,7},{6,4},{7,5},{8,10},{9,11},{10,... | collective-permute-start | bytes 4718600 | tf_op jit(solution)/shard_map/ppermute | solution.py:799
  703.8 27.1 %collective-permute-start.62 = (bf16[4112,128]{1,0:T(8,128)(2,1)}, bf16[4112,128]{1,0:T(8,128)(2,1)}, u32[]{:S(2)}, u32[]{:S(2)}) collective-permute-start(bf16[4112,128]{1,0:T(8,128)(2,1)} %slice_bitcast_fusion.4), channel_id=1, source_target_pairs={{0,4},{3,7},{4,0},{7,3},{8,12},{11,15},{12,8},{15,11},{16,20},{19,... | collective-permute-start | bytes 3158024 | tf_op jit(solution)/shard_map/ppermute | solution.py:799
  709.8 21.1 %collective-permute-start.63 = (bf16[4112,128]{1,0:T(8,128)(2,1)}, bf16[4112,128]{1,0:T(8,128)(2,1)}, u32[]{:S(2)}, u32[]{:S(2)}) collective-permute-start(bf16[4112,128]{1,0:T(8,128)(2,1)} %fusion.31), channel_id=1, source_target_pairs={{0,8},{3,11},{4,12},{7,15},{8,16},{11,19},{12,20},{15,23},{16,24},... | collective-permute-start | bytes 3158024 | tf_op jit(solution)/shard_map/ppermute | solution.py:799
  718.8 20.3 %collective-permute-start.61 = (bf16[4112,128]{1,0:T(8,128)(2,1)}, bf16[4112,128]{1,0:T(8,128)(2,1)}, u32[]{:S(2)}, u32[]{:S(2)}) collective-permute-start(bf16[4112,128]{1,0:T(8,128)(2,1)} %slice_bitcast_fusion.5), channel_id=1, source_target_pairs={{0,4},{3,7},{4,0},{7,3},{8,12},{11,15},{12,8},{15,11},{16,20},{19,... | collective-permute-start | bytes 3158024 | tf_op jit(solution)/shard_map/ppermute | solution.py:799
  725.4 18.8 %collective-permute-start.64 = (bf16[4112,128]{1,0:T(8,128)(2,1)}, bf16[4112,128]{1,0:T(8,128)(2,1)}, u32[]{:S(2)}, u32[]{:S(2)}) collective-permute-start(bf16[4112,128]{1,0:T(8,128)(2,1)} %fusion.29), channel_id=1, source_target_pairs={{0,8},{3,11},{4,12},{7,15},{8,16},{11,19},{12,20},{15,23},{16,24},... | collective-permute-start | bytes 3158024 | tf_op jit(solution)/shard_map/ppermute | solution.py:799
  (128 other events, 1018.1 us)

commit v3 on v2

--- a/solution.py
+++ b/solution.py
@@ -24,6 +24,7 @@
 HEADS = HALF // HEAD_DIM
 ROWS = 256
 VEC_ROWS = 16
+CHUNKS = 4
 
 AXES = ("dp", "tensor")
 precise = lax.Precision.HIGHEST
@@ -357,14 +358,41 @@
     )(pos, *operands)
 
 
-def qkv_kernel(layer, summed, *refs):
-    if summed:
+def embed_kernel(*refs):
+    *parts, vec, weight, out = refs
+    size = BASE_PIX // CHUNKS
+    total = vec[:, :HALF]
+    for c in range(CHUNKS):
+        total = total + dot(parts[c][...], weight[c * size : (c + 1) * size, :])
+    out[...] = total.astype(bf16)
+
+
+def embed_call(chunks, vec, panels):
+    tokens = chunks[0].shape[0]
+    return pl.pallas_call(
+        embed_kernel,
+        out_shape=jax.ShapeDtypeStruct((tokens, HALF), bf16),
+        grid=(tokens // ROWS,),
+        in_specs=[rows_spec(BASE_PIX // CHUNKS)] * CHUNKS
+        + [fixed(vec.shape), fixed((BASE_PIX, HALF), PANELS["base"] // BASE_PIX)],
+        out_specs=rows_spec(HALF),
+        compiler_params=params(),
+        cost_estimate=cost(2 * tokens * BASE_PIX * HALF, tokens * BASE_PIX * 3),
+    )(*chunks, vec, panels)
+
+
+def qkv_kernel(layer, first, core, *refs):
+    if first:
+        own, recv, vec, weight, hid, normed, q_ref, k_ref, v_ref = refs
+        mine, theirs = own[...].astype(f32), recv[...].astype(f32)
+        low = core[0] == 0
+        values = jnp.concatenate(
+            [jnp.where(low, mine, theirs), jnp.where(low, theirs, mine)], axis=1
+        )
+    else:
         base, own, recv, vec, weight, hid, normed, q_ref, k_ref, v_ref = refs
         values = base[...] + (own[...].astype(f32) + recv[...].astype(f32))
-        hid[...] = values
-    else:
-        base, vec, weight, normed, q_ref, k_ref, v_ref = refs
-        values = base[...]
+    hid[...] = values
     unit, unused = norm_stats(values)
     low = (unit * vec_piece(vec, layer, "g1") + vec_piece(vec, layer, "s1")).astype(bf16)
     normed[...] = low
@@ -373,22 +401,24 @@
     v_ref[...] = (dot(low, weight[2 * D : 3 * D, :]) + vec_piece(vec, layer, "bv")).astype(bf16)
 
 
-def qkv_call(layer, base, own, recv, vec, panels):
-    tokens = base.shape[0]
-    summed = own is not None
+def qkv_call(layer, base, own, recv, core, vec, panels):
+    tokens = own.shape[0]
     shape = lambda width, kind: jax.ShapeDtypeStruct((tokens, width), kind)
-    outs = ([shape(D, f32)] if summed else []) + [shape(D, bf16)] + [shape(HALF, bf16)] * 3
-    operands = [base] + ([own, recv] if summed else []) + [vec, panels]
+    outs = [shape(D, f32), shape(D, bf16)] + [shape(HALF, bf16)] * 3
+    operands = ([] if base is None else [base]) + [own, recv]
     return pl.pallas_call(
-        functools.partial(qkv_kernel, layer, summed),
+        functools.partial(qkv_kernel, layer, base is None),
         out_shape=outs,
-        grid=(tokens // ROWS,),
-        in_specs=[rows_spec(D)] * (3 if summed else 1)
-        + [fixed(vec.shape), fixed((3 * D, HALF), PANELS["qkv"][layer] // (3 * D))],
-        out_specs=[rows_spec(o.shape[1]) for o in outs],
+        grid_spec=pltpu.PrefetchScalarGridSpec(
+            num_scalar_prefetch=1,
+            grid=(tokens // ROWS,),
+            in_specs=[rows_spec(o.shape[1]) for o in operands]
+            + [fixed(vec.shape), fixed((3 * D, HALF), PANELS["qkv"][layer] // (3 * D))],
+            out_specs=[rows_spec(o.shape[1]) for o in outs],
+        ),
         compiler_params=params(),
         cost_estimate=cost(2 * tokens * D * 3 * HALF, tokens * D * 14),
-    )(*operands)
+    )(core, *operands, vec, panels)
 
 
 def head_masks():
@@ -735,14 +765,16 @@
     return one(left[0], right[0]) + (one(left[0], right[1]) + one(left[1], right[0]))
 
 
-def owner_kernel(per, used, low, master, left, right, moment, variance, grad, out, out_mom, out_var):
+def owner_kernel(per, used, home, near, far, master, left, right, moment, variance, grad, out, out_mom, out_var):
     here = range(per)
     first = pl.program_id(0) * per
     lefts = [split(left[i]) for i in here]
     rights = [split(right[i]) for i in here]
     rotated = []
     for i in here:
-        tile = jnp.where(used[first + i] > 0, low[i * BS : (i + 1) * BS, :].astype(f32), 0.0)
+        rows = slice(i * BS, (i + 1) * BS)
+        tile = jnp.where(home[0] > 0, near[rows, :].astype(f32), far[rows, :].astype(f32))
+        tile = jnp.where(used[first + i] > 0, tile, 0.0)
         grad[i] = tile
         tile = tile.astype(bf16)
         rotated.append(split(dot_tn(lefts[i][0], tile) + dot_tn(lefts[i][1], tile)))
@@ -760,7 +792,7 @@
         out[i] = master[i] - matrix_rate * returned[i]
 
 
-def owner_call(used, low, *arrays):
+def owner_call(used, home, near, far, *arrays):
     count = arrays[0].shape[0]
     per = min(8, count)
     block = pl.BlockSpec((per, BS, BS), lambda i, *_: (i, 0, 0))
@@ -768,14 +800,50 @@
         functools.partial(owner_kernel, per),
         out_shape=[jax.ShapeDtypeStruct(arrays[0].shape, f32)] * 4,
         grid_spec=pltpu.PrefetchScalarGridSpec(
-            num_scalar_prefetch=1,
+            num_scalar_prefetch=2,
             grid=(count // per,),
-            in_specs=[pl.BlockSpec((per * BS, BS), lambda i, *_: (i, 0))] + [block] * 5,
+            in_specs=[pl.BlockSpec((per * BS, BS), lambda i, *_: (i, 0))] * 2 + [block] * 5,
             out_specs=[block] * 4,
         ),
         compiler_params=params(),
         cost_estimate=cost(count * 88 * BS**3, count * BS * BS * 38),
-    )(used, low, *arrays)
+    )(used, home, near, far, *arrays)
+
+
+def reduce_kernel(carrying, last, *refs):
+    block, arrived, *refs = refs
+    total = block[...].astype(f32) + arrived[...].astype(f32)
+    if carrying:
+        carried, *refs = refs
+        total = total + carried[...].astype(f32)
+    if last:
+        [out] = refs
+    else:
+        following, out, later = refs
+        later[...] = following[...]
+    out[...] = total.astype(bf16)
+
+
+def reduce_call(j, n, buffer, arrived, carried, payload):
+    last = j == 3
+    at = lambda j, x_rel: pl.BlockSpec((payload, BS), lambda i: ((j * 2 + x_rel) * 2 + n, 0))
+    whole = fixed((payload, BS))
+    operands = [buffer, arrived] + ([] if carried is None else [carried])
+    specs = [at(j, 0)] + [whole] * (len(operands) - 1)
+    if not last:
+        operands.append(buffer)
+        specs.append(at(j + 1, 1))
+    outs = [jax.ShapeDtypeStruct((payload, BS), bf16)] * (1 if last else 2)
+    made = pl.pallas_call(
+        functools.partial(reduce_kernel, carried is not None, last),
+        out_shape=outs,
+        grid=(1,),
+        in_specs=specs,
+        out_specs=[whole] * len(outs),
+        compiler_params=params(),
+        cost_estimate=cost(payload * BS * 3, payload * BS * 12),
+    )(*operands)
+    return (made[0], None) if last else made
 
 
 class Routes:
@@ -831,7 +899,7 @@
     cotangent = jnp.where(home, cotangent, send(cotangent, routes.core_out))
     size_row = jnp.where(home, image_size, send(image_size, routes.core_out))[0]
     own_slots = block_slot[0]
-    slot_list = jnp.where(home, block_slot, send(block_slot, routes.y_all))[0]
+    slot_other = send(block_slot, routes.y_all)
 
     lengths = jnp.where(
         size_row == 0, LEN_A, jnp.where(size_row == 1, LEN_B, jnp.where(size_row == 2, LEN_C, 0))
@@ -858,9 +926,15 @@
 
     select_low = select.astype(bf16)
     spread_in = patches[:, None, :] * select_low[:, :, None]
-    base_pix = lax.dot_general(
-        spread_in, pinv, (((1, 2), (0, 2)), ((), ())), preferred_element_type=f32
-    ).astype(bf16)
+
+    def expand(which):
+        size = BASE_PIX // CHUNKS
+        return lax.dot_general(
+            spread_in,
+            pinv[:, which * size : (which + 1) * size],
+            (((1, 2), (0, 2)), ((), ())),
+            preferred_element_type=f32,
+        ).astype(bf16)
 
     vec_low = jnp.pad(vec_master[0].astype(bf16), (0, VEC_ROWS * BS - vec_per))
     own_pack = jnp.concatenate(
@@ -870,45 +944,51 @@
         ],
         axis=0,
     )
-    named = slot_list[None, :] == jnp.arange(slots_n)[:, None]
-    used = jnp.any(named, axis=1)
-    drow = jnp.where(used, jnp.sum(jnp.where(named, TARGET_ROW[None, :], 0), axis=1), -1)
-    dcol = jnp.sum(jnp.where(named, TARGET_COL[None, :], 0), axis=1)
     flag = home.astype(jnp.int32).reshape(1)
     if grid3:
         x_pos = (dp_pos // 2) % 2
         z_pos = dp_pos // 4
-        pack = jnp.stack([own_pack, send(own_pack, routes.core_in)], axis=0)
-        packs, acrosses, overs, corners = [pack], [], [], []
+        packs = [[own_pack], [send(own_pack, routes.core_in)]]
+        across, over_y, corner = [[], []], [[], []], [[], []]
+        token = jnp.zeros((8, BS), f32)
+        chunks = []
         for j in range(5):
-            moved = []
-            if j < 3:
-                moved.append(send(packs[j], routes.z_home))
-            if j < 4:
-                moved += [send(packs[j], routes.x_home), send(packs[j], routes.y_out)]
-            if j:
-                moved += [
-                    send(acrosses[j - 1][0:1], routes.y_out),
-                    send(overs[j - 1][1:2], routes.x_away),
-                ]
-            if j == 1:
-                *moved, base_pix = fence(*moved, base_pix)
-            elif j < 4:
-                moved = list(fence(*moved))
-            if j < 3:
-                packs.append(moved.pop(0))
-            if j < 4:
-                acrosses.append(moved.pop(0))
-                overs.append(moved.pop(0))
-            if j:
-                corners.append(moved)
+            for n in range(2):
+                moved = []
+                if j < 4:
+                    moved += [send(packs[n][j], routes.x_home), send(packs[n][j], routes.y_out)]
+                if j:
+                    source, route = (across, routes.y_out) if n == 0 else (over_y, routes.x_away)
+                    moved.append(send(source[n][j - 1], route))
+                if j < 3:
+                    moved.append(send(packs[n][j], routes.z_home))
+                work = []
+                if j + n == 0:
+                    work = [slot_other]
+                if 1 <= 2 * j + n <= CHUNKS:
+                    work = [expand(2 * j + n - 1)]
+                if j < 4:
+                    token, *moved = fence(token, *moved, *work)
+                    if j + n == 0:
+                        slot_other = moved.pop()
+                    elif work:
+                        chunks.append(moved.pop())
+                if j < 3:
+                    packs[n].append(moved.pop())
+                if j:
+                    corner[n].append(moved.pop())
+                if j < 4:
+                    across[n].append(moved[0])
+                    over_y[n].append(moved[1])
         first, second, owner = [], [], []
         for j in range(4):
-            first += [packs[j], acrosses[j]]
-            second += [overs[j]] + corners[j]
+            first += [packs[0][j], packs[1][j], across[0][j], across[1][j]]
+            second += [over_y[0][j], over_y[1][j], corner[0][j], corner[1][j]]
             for x_rel in range(2):
                 for n in range(2):
                     owner.append(((z_pos - j) % 4) * 4 + (x_pos ^ x_rel) * 2 + (core ^ n))
+        first = [v[None] for v in first]
+        second = [v[None] for v in second]
         owner = jnp.stack(owner).astype(jnp.int32)
     else:
         everything = lax.all_gather(own_pack, AXES, axis=0)
@@ -916,27 +996,25 @@
         first = [jnp.where(core == 0, everything[:, 0], everything[:, 1])]
         second = []
         owner = jnp.arange(dp_n, dtype=jnp.int32)
+        chunks = [expand(c) for c in range(CHUNKS)]
+    slot_list = jnp.where(home, block_slot, slot_other)[0]
+    named = slot_list[None, :] == jnp.arange(slots_n)[:, None]
+    used = jnp.any(named, axis=1)
+    drow = jnp.where(used, jnp.sum(jnp.where(named, TARGET_ROW[None, :], 0), axis=1), -1)
+    dcol = jnp.sum(jnp.where(named, TARGET_COL[None, :], 0), axis=1)
     panels, vec_rows = gather_tiles(first, second, owner, drow, dcol, flag, slots_per, dp_n)
     vec = vec_rows.reshape(dp_n, VEC_ROWS * BS)[:, :vec_per].astype(f32).reshape(1, dp_n * vec_per)
 
-    base_w = panels[PANELS["base"] : PANELS["base"] + BASE_PIX]
-    embedded = (dot(base_pix, base_w) + vec[:, :HALF]).astype(bf16)
+    embedded = embed_call(chunks, vec, panels)
     embedded_other = send(embedded, routes.core_all)
-    hidden = jnp.concatenate(
-        [
-            jnp.where(core == 0, embedded, embedded_other),
-            jnp.where(core == 0, embedded_other, embedded),
-        ],
-        axis=1,
-    ).astype(f32)
+    core_flag = core.astype(jnp.int32).reshape(1)
 
     caches = []
-    own = recv = None
+    hidden, own, recv = None, embedded, embedded_other
     for layer in range(LAYERS):
-        made = qkv_call(layer, hidden, own, recv, vec, panels)
-        if own is not None:
-            hidden, *made = made
-        normed, queries, keys, values = made
+        hidden, normed, queries, keys, values = qkv_call(
+            layer, hidden, own, recv, core_flag, vec, panels
+        )
         mixed, lse, part = attend_call(
             layer, queries, keys, values, seg_col, seg_row, vec, panels
         )
@@ -1067,63 +1145,54 @@
     ]
     grad_emb = jnp.where(core == 0, sides[0], sides[1]).astype(bf16)
     grad_emb_bias = jnp.sum(grad_emb.astype(f32), axis=0, keepdims=True)
-    gb = dot_tn(base_pix, grad_emb).astype(bf16)
+    gb = jnp.concatenate([dot_tn(c, grad_emb).astype(bf16) for c in chunks], axis=0)
     vec_grad = jnp.concatenate([grad_emb_bias] + vec_grads[0] + vec_grads[1], axis=1)[0]
     vec_grad = jnp.pad(vec_grad, (0, dp_n * vec_per - vec_grad.shape[0])).reshape(dp_n, vec_per)
     vec_grad = jnp.pad(vec_grad, ((0, 0), (0, VEC_ROWS * BS - vec_per)))
     vec_grad = vec_grad.astype(bf16).reshape(dp_n, VEC_ROWS, BS)
-    gb, vec_grad, grad_emb, gq0, xq0 = hold(gb, vec_grad, grad_emb, gq0, xq0)
+    hq0 = half_sum(gq0, xq0) if grid3 else None
+    gb, vec_grad, grad_emb, hq0 = hold(gb, vec_grad, grad_emb, hq0)
+    aq0, ao0, av = over(hq0), over(go0), over(vec_grad)
     xb = beside(gb)
-    aq0 = over(half_sum(gq0, xq0)) if grid3 else None
-    ao0, av = over(go0), over(vec_grad)
     buffer = place_tiles(("out", top), go1, ao1, buffer)
     buffer = place_tiles(("qkv", top), gq1, aq1, buffer)
     buffer = place_tiles(("down", low), gd0, ad0, buffer)
     buffer = place_tiles(("up", low), gu0, au0, buffer)
-    xb, buffer = hold(xb, buffer)
-    ab = over(half_sum(gb, xb)) if grid3 else None
+    hb = half_sum(gb, xb) if grid3 else None
+    hb, aq0, ao0, av, buffer, panels, grad_emb = hold(hb, aq0, ao0, av, buffer, panels, grad_emb)
+    ab = over(hb)
     buffer = place_tiles(("out", low), go0, ao0, buffer)
     buffer = scatter_vec(vec_pos, vec_grad, av, buffer)
     buffer = place_tiles(("qkv", low), gq0, aq0, buffer)
-    ab, buffer, panels, grad_emb = hold(ab, buffer, panels, grad_emb)
+    base_here = panels[PANELS["base"] : PANELS["base"] + BASE_PIX]
+    resized = [dot_tn(pinv[s], base_here).astype(bf16) for s in range(3)]
+    ab, buffer, *resized = hold(ab, buffer, *resized)
     buffer = place_tiles("base", gb, ab, buffer)
-
-    def pixel_part(which):
-        base_here = panels[PANELS["base"] : PANELS["base"] + BASE_PIX]
-        return dot_tn(pinv[which], base_here).astype(bf16)
-
-    resized = []
-    grad_pixels = None
+    grad_pixels = sum(
+        dot_nt(grad_emb * select_low[:, s : s + 1], resized[s]) for s in range(3)
+    ).astype(bf16)
+
     if grid3:
+        token = jnp.zeros((8, BS), f32)
         order = (1, 0)
-        block_of = lambda j, x_rel, n: buffer.reshape(4, 2, 2, payload, BS)[j, x_rel, n]
-        across = {n: send(block_of(0, 1, n), routes.x_home) for n in order}
         carried = {n: None for n in order}
+        across = {n: send(buffer.reshape(4, 2, 2, payload, BS)[0, 1, n], routes.x_home) for n in order}
         rounded = {}
         for j in range(4):
             for n in order:
-                extra = []
-                if j == 0 or (j == 1 and n == order[0]):
-                    extra = [pixel_part(len(resized))]
-                elif j == 1:
-                    grad_pixels = sum(
-                        dot_nt(grad_emb * select_low[:, s : s + 1], resized[s]) for s in range(3)
-                    ).astype(bf16)
-                    extra = [grad_pixels]
-                across[n], buffer, carried[n], *extra = hold(across[n], buffer, carried[n], *extra)
-                if j == 0 or (j == 1 and n == order[0]):
-                    resized += extra
-                elif j == 1:
-                    [grad_pixels] = extra
-                total = block_of(j, 0, n).astype(f32) + across[n].astype(f32)
-                if carried[n] is not None:
-                    total = total + carried[n].astype(f32)
+                extra = None
+                if j == 0 and n == order[1]:
+                    extra = grad_pixels
+                token, across[n], carried[n], extra = hold(token, across[n], carried[n], extra)
+                if extra is not None:
+                    grad_pixels = extra
+                total, later = reduce_call(j, n, buffer, across[n], carried[n], payload)
                 if j < 3:
-                    carried[n] = send(total.astype(bf16), routes.z_home)
-                    across[n] = send(block_of(j + 1, 1, n), routes.x_home)
+                    carried[n] = send(total, routes.z_home)
+                    across[n] = send(later, routes.x_home)
                 else:
-                    rounded[n] = total.astype(bf16)
-        mine = jnp.where(home, rounded[0], send(rounded[1], routes.core_out))
+                    rounded[n] = total
+        near_grad, far_grad = rounded[0], send(rounded[1], routes.core_out)
     else:
         held = buffer.reshape(dp_n, 1, payload, BS).astype(f32)
         nothing = jnp.zeros_like(held)
@@ -1135,11 +1204,8 @@
             [used_rows, jnp.ones((dp_n, 1, VEC_ROWS, 1), bool)], axis=2
         )
         both = jnp.where(used_rows, both, 0.0).reshape(dp_n * TENSOR * payload, BS)
-        mine = lax.psum_scatter(both, AXES, scatter_dimension=0, tiled=True).astype(bf16)
-        resized = [pixel_part(s) for s in range(3)]
-        grad_pixels = sum(
-            dot_nt(grad_emb * select_low[:, s : s + 1], resized[s]) for s in range(3)
-        ).astype(bf16)
+        near_grad = lax.psum_scatter(both, AXES, scatter_dimension=0, tiled=True).astype(bf16)
+        far_grad = near_grad
 
     pixels_other = send(grad_pixels, routes.core_all)
     pixel_sides = [
@@ -1154,9 +1220,10 @@
     my_slots = dp_pos * slots_per + jnp.arange(slots_per)
     mine_used = jnp.any(own_slots[None, :] == my_slots[:, None], axis=1).astype(jnp.int32)
     owned_grad, new_master, new_mom, new_var = owner_call(
-        mine_used, mine, master_slots[0], left_basis[0], right_basis[0], mom_slots[0], var_slots[0]
+        mine_used, flag, near_grad, far_grad, master_slots[0], left_basis[0], right_basis[0], mom_slots[0], var_slots[0]
     )
-    owned_vec_grad = mine[slots_per * BS :].astype(f32).reshape(VEC_ROWS * BS)[:vec_per]
+    vec_rows = jnp.where(home, near_grad[slots_per * BS :], far_grad[slots_per * BS :])
+    owned_vec_grad = vec_rows.astype(f32).reshape(VEC_ROWS * BS)[:vec_per]
     new_vec_mom = decay * vec_mom[0] + (1.0 - decay) * owned_vec_grad
     new_vec_var = decay * vec_var[0] + (1.0 - decay) * owned_vec_grad * owned_vec_grad
     new_vec = vec_master[0] - vector_rate * new_vec_mom / (jnp.sqrt(new_vec_var) + adam_eps)

time: 771 us -> 765 us (level)
  waiting for transfers between devices: 165 us -> 118 us
  starting transfers between devices: 134 us -> 175 us
  Pallas kernels: 245 us -> 281 us
  local copies, waits for them, and re-layouts: 60 us -> 39 us
  other arithmetic: 58.6 us -> 45.2 us
    ppermute x66 -> x77, waiting for transfers between devices: 165 us -> 118 us  [send(): return lax.ppermute(value, AXES, route)]
    ppermute x66 -> x77, starting transfers between devices: 134 us -> 175 us  [send(): return lax.ppermute(value, AXES, route)]
    pallas_call x2 -> x11, Pallas kernels: 14.7 us -> 50.2 us  [the longest x8 27.7 us: reduce_call(): pl.pallas_call(functools.partial(reduce_kernel, carried is not None, last...]
    convert_element_type x8 -> x0, other arithmetic: 23.5 us -> none  [the longest x6 18.2 us: shards(): carried[n] = send(total.astype(bf16), routes.z_home)]
    squeeze x7 -> x1, local copies, waits for them, and re-layouts: 15.7 us -> 2.65 us  [shards(): buffer.reshape(4, 2, 2, payload, BS)[0, 1, n]]
    unnamed x20 -> x19, other arithmetic: 0.2 us -> 9.86 us
    unnamed x225 -> x223, local copies, waits for them, and re-layouts: 27.5 us -> 22.3 us
    dot_general x2 -> x4, matrix products: 24.2 us -> 29.4 us  [expand(): lax.dot_general(spread_in, pinv[:, which * size:(which + 1) * size], (((1...]
  transfers between devices with their start and end apart: 66 -> 77, of which waited for: 22 -> 26; matrix products, arithmetic and copies ran while one was open for 19% -> 19% of each run, Pallas kernels for 18% -> 22%
where the time goes in v3:
time: 765 us; the launch traced here: 754 us
  Pallas kernels  281 us (37%)
  starting transfers between devices  175 us (23%)
  waiting for transfers between devices  118 us (15%)
  matrix products  92.9 us (12%)
  other arithmetic  45.2 us (6%)
  local copies, waits for them, and re-layouts  39 us (5%)
    ppermute x77, starting transfers between devices, send(): return lax.ppermute(value, AXES, route)  175 us
    ppermute x77, waiting for transfers between devices, send(): return lax.ppermute(value, AXES, route)  118 us
    dot_general x15, matrix products, dot_tn(): lax.dot_general(left, right, (((0,), (0,)), ((), ())), preferred_element_...  59.3 us
    pallas_call x2, Pallas kernels, attend_back_call(): pl.pallas_call(attend_back_kernel, out_shape=[shape(D, f32), shape(D, bf1...  53.3 us
    pallas_call x2, Pallas kernels, attend_call(): pl.pallas_call(functools.partial(attend_kernel, layer), out_shape=[jax.Sh...  39.2 us
    pallas_call x9, Pallas kernels, scatter_matrix(): pl.pallas_call(functools.partial(scatter_kernel, rows_n, cols_n, steps, p...  34.8 us
    pallas_call x2, Pallas kernels, mlp_back_call(): pl.pallas_call(functools.partial(mlp_back_kernel, layer, summed), out_sha...  32.8 us
    dot_general x4, matrix products, expand(): lax.dot_general(spread_in, pinv[:, which * size:(which + 1) * size], (((1...  29.4 us
  transfers between devices with their start and end apart: 77, of which 26 were waited for; matrix products, arithmetic and copies ran while one was open for 19% of the time, Pallas kernels for 22%

profile of v3, /device:TPU:0, one launch (start us, length us, event | category | flops | bytes accessed | tf_op | source)
XLA Modules:
  0.0 754.2 jit_solution(11279039827820284426)
XLA Ops:
  25.0 9.1 %collective-permute-done.2.refs_3_ = bf16[4112,128]{1,0:T(8,128)(2,1)} collective-permute-done((bf16[4112,128]{1,0:T(8,128)(2,1)S(1)}, bf16[4112,128]{1,0:T(8,128)(2,1)}, u32[]{:S(2)}, u32[]{:S(2)}) %collective-permute-start.2) | collective-permute-done | bytes 1052704 | tf_op jit(solution)/shard_map/ppermute | solution.py:867
  47.8 7.6 %bitcast_convert_fusion.3.refs_4_ = bf16[1024,768]{1,0:T(8,128)(2,1)} fusion(bf16[3,3072,768]{2,1,0:T(8,128)(2,1)} %param.19, bf16[1024,3]{0,1:T(4,128)(2,1)S(1)} %add_convert_fusion.6, bf16[1024,768]{1,0:T(8,128)(2,1)S(1)} %broadcast_select_fusion.1), kind=kOutput, calls=%fused_computation.30 | convolution fusion | flops 3627024384 | bytes 6690816 | tf_op jit(solution)/shard_map/dot_general | solution.py:932
  55.4 7.5 collective-permute-done.5.refs_1_
  64.9 4.0 collective-permute-start.12
  75.2 7.3 bitcast_convert_fusion.2.refs_5_
  88.0 6.1 collective-permute-done.14.refs_1_
  99.6 7.3 bitcast_convert_fusion.1.refs_5_
  120.9 7.3 bitcast_convert_fusion.refs_5_
  140.0 9.7 %collective-permute-start.30 = (bf16[4112,128]{1,0:T(8,128)(2,1)}, bf16[4112,128]{1,0:T(8,128)(2,1)}, u32[]{:S(2)}, u32[]{:S(2)}) collective-permute-start(bf16[4112,128]{1,0:T(8,128)(2,1)} %get-tuple-element.228), channel_id=1, source_target_pairs={{0,1},{3,2},{4,5},{7,6},{8,9},{11,10},{12,13},{15,14},{16,17},{19,... | collective-permute-start | bytes 3158024 | tf_op jit(solution)/shard_map/ppermute | solution.py:867
  151.4 7.1 collective-permute-done.28.refs_3_
  158.4 4.4 collective-permute-start.32
  162.9 6.1 collective-permute-done.29.refs_1_
  173.3 7.7 %collective-permute-done.32 = bf16[4112,128]{1,0:T(8,128)(2,1)S(1)} collective-permute-done((bf16[4112,128]{1,0:T(8,128)(2,1)}, bf16[4112,128]{1,0:T(8,128)(2,1)S(1)}, u32[]{:S(2)}, u32[]{:S(2)}) %collective-permute-start.32) | collective-permute-done | bytes 1052704 | tf_op jit(solution)/shard_map/ppermute | solution.py:867
  182.3 14.8 %shard_map.230 = (bf16[21504,384]{1,0:T(8,128)(2,1)}, bf16[16,16,128]{2,1,0:T(8,128)(2,1)}) custom-call(s32[16]{0:T(128)} %stack.83.owner, s32[512]{0:T(512)} %broadcast_select_fusion.3.drow, s32[512]{0:T(512)} %get-tuple-element.406.dcol, s32[1]{0:T(128)} %bitcast.28.flag.home, bf16[1,4112,128]{2,1,0:T(8,128)(2,1)} %get-tuple-element.422.refs_0_, ...), custom_call_target="tpu_custom_call" | custom-call | bytes 33030144 | tf_op jit(solution)/shard_map/pallas_call | solution.py:228
  198.7 7.5 shard_map.231.refs_0_
  211.5 7.1 shard_map.232
  218.6 19.5 %shard_map.233 = (bf16[1024,384]{1,0:T(8,128)(2,1)}, f32[8,1024]{1,0:T(8,128)}, bf16[1024,768]{1,0:T(8,128)(2,1)}) custom-call(bf16[1024,384]{1,0:T(8,128)(2,1)} %get-tuple-element.248.q_ref, bf16[1024,384]{1,0:T(8,128)(2,1)} %get-tuple-element.249.k_ref, bf16[1024,384]{1,0:T(8,128)(2,1)} %get-tuple-element.250.v_ref, s32[1024,1]{1,0:T(8,128)} %copy.169.seg_q.seg_k, ...), custom_call_target="tpu_custom_call" | custom-call | flops 6442450944 | bytes 6291456 | tf_op jit(solution)/shard_map/pallas_call | solution.py:464
  242.9 13.5 %shard_map.234 = (f32[1024,768]{1,0:T(8,128)}, bf16[1024,768]{1,0:T(8,128)(2,1)}, bf16[1024,1536]{1,0:T(8,128)(2,1)}, bf16[1024,1536]{1,0:T(8,128)(2,1)}, bf16[1024,768]{1,0:T(8,128)(2,1)}) custom-call(f32[1024,768]{1,0:T(8,128)} %get-tuple-element.247.base.hid, bf16[1024,768]{1,0:T(8,128)(2,1)} %get-tuple-element.251.own, bf16[1024,768]{1,0:T(8,128)(2,1)} %copy-done.57, ...), custom_call_target="tpu_custom_call" | custom-call | flops 4831838208 | bytes 18874368 | tf_op jit(solution)/shard_map/pallas_call | solution.py:522
  261.2 8.0 %shard_map.235 = (f32[1024,768]{1,0:T(8,128)}, bf16[1024,768]{1,0:T(8,128)(2,1)}, bf16[1024,384]{1,0:T(8,128)(2,1)}, bf16[1024,384]{1,0:T(8,128)(2,1)}, bf16[1024,384]{1,0:T(8,128)(2,1)}) custom-call(s32[1]{0:T(128)} %bitcast.core, f32[1024,768]{1,0:T(8,128)} %get-tuple-element.252.refs_0_.refs_3_, bf16[1024,768]{1,0:T(8,128)(2,1)} %get-tuple-element.253.refs_1_, ...), custom_call_target="tpu_custom_call" | custom-call | flops 1811939328 | bytes 11010048 | tf_op jit(solution)/shard_map/pallas_call | solution.py:409
  269.1 19.7 %shard_map.236 = (bf16[1024,384]{1,0:T(8,128)(2,1)}, f32[8,1024]{1,0:T(8,128)}, bf16[1024,768]{1,0:T(8,128)(2,1)}) custom-call(bf16[1024,384]{1,0:T(8,128)(2,1)} %get-tuple-element.255.q_ref, bf16[1024,384]{1,0:T(8,128)(2,1)} %get-tuple-element.256.k_ref, bf16[1024,384]{1,0:T(8,128)(2,1)} %get-tuple-element.257.v_ref, s32[1024,1]{1,0:T(8,128)} %copy.169.seg_q.seg_k, ...), custom_call_target="tpu_custom_call" | custom-call | flops 6442450944 | bytes 6291456 | tf_op jit(solution)/shard_map/pallas_call | solution.py:464
  293.7 13.6 %shard_map.237 = (f32[1024,768]{1,0:T(8,128)}, bf16[1024,768]{1,0:T(8,128)(2,1)}, bf16[1024,1536]{1,0:T(8,128)(2,1)}, bf16[1024,1536]{1,0:T(8,128)(2,1)}, bf16[1024,768]{1,0:T(8,128)(2,1)}) custom-call(f32[1024,768]{1,0:T(8,128)} %get-tuple-element.254.base.hid, bf16[1024,768]{1,0:T(8,128)(2,1)} %get-tuple-element.258.own, bf16[1024,768]{1,0:T(8,128)(2,1)} %copy-done.56, ...), custom_call_target="tpu_custom_call" | custom-call | flops 4831838208 | bytes 18874368 | tf_op jit(solution)/shard_map/pallas_call | solution.py:522
  309.8 16.0 %shard_map.238 = (bf16[1024,768]{1,0:T(8,128)(2,1)}, bf16[1024,1536]{1,0:T(8,128)(2,1)}, bf16[1024,768]{1,0:T(8,128)(2,1)}, f32[1,768]{1,0:T(1,128)}, f32[1,768]...) custom-call(bf16[1024,768]{1,0:T(8,128)(2,1)} %broadcast_select_fusion.refs_0_, ...), custom_call_target="tpu_custom_call" | custom-call | flops 4831838208 | bytes 18874368 | tf_op jit(solution)/shard_map/pallas_call | solution.py:579
  326.7 8.8 %collective-permute-start.41 = (bf16[1024,768]{1,0:T(8,128)(2,1)S(1)}, bf16[1024,768]{1,0:T(8,128)(2,1)S(1)}, u32[]{:S(2)}, u32[]{:S(2)}) collective-permute-start(bf16[1024,768]{1,0:T(8,128)(2,1)S(1)} %multiply_convert_fusion), channel_id=1, source_target_pairs={{0,1},{3,2},{4,5},{7,6},{8,9},{11,10},{12,13},{15,14},{16,17},{19,... | collective-permute-start | bytes 4718600 | tf_op jit(solution)/shard_map/ppermute | solution.py:867
  335.5 4.2 convolution_convert_fusion.2.refs_3_
  339.7 4.0 convolution_convert_fusion.3.refs_2_
  343.7 9.6 %collective-permute-done.41.refs_4_ = bf16[1024,768]{1,0:T(8,128)(2,1)S(1)} collective-permute-done((bf16[1024,768]{1,0:T(8,128)(2,1)S(1)}, bf16[1024,768]{1,0:T(8,128)(2,1)S(1)}, u32[]{:S(2)}, u32[]{:S(2)}) %collective-permute-start.41) | collective-permute-done | bytes 1572896 | tf_op jit(solution)/shard_map/ppermute | solution.py:867
  357.9 26.6 %shard_map.240 = (f32[1024,768]{1,0:T(8,128)}, bf16[1024,768]{1,0:T(8,128)(2,1)}, bf16[1024,384]{1,0:T(8,128)(2,1)}, bf16[1024,384]{1,0:T(8,128)(2,1)}, bf16[1024,384]{1,0:T(8,128)(2,1)}, /*index=5*/f32[1,768]{1,0:T(1,128)}) custom-call(s32[4]{0:T(128)} %get-tuple-element.436.low_ref, s32[4]{0:T(128)} %get-tuple-element.435.high_ref, ...), custom_call_target="tpu_custom_call" | custom-call | flops 11274289152 | bytes 15728640 | tf_op jit(solution)/shard_map/pallas_call | solution.py:674
  385.5 7.9 %shard_map.242 = (bf16[1024,768]{1,0:T(8,128)(2,1)}, f32[1,768]{1,0:T(1,128)}, f32[1,768]{1,0:T(1,128)}, f32[1,384]{1,0:T(1,128)}, f32[1,384]{1,0:T(1,128)}) custom-call(bf16[1024,384]{1,0:T(8,128)(2,1)} %get-tuple-element.277.dq, bf16[1024,384]{1,0:T(8,128)(2,1)} %get-tuple-element.278.dk, bf16[1024,384]{1,0:T(8,128)(2,1)} %get-tuple-element.279.dv, ...), custom_call_target="tpu_custom_call" | custom-call | flops 1811939328 | bytes 7864320 | tf_op jit(solution)/shard_map/pallas_call | solution.py:738
  397.5 4.9 convolution_convert_fusion.5.refs_4_
  402.4 16.8 %shard_map.243 = (f32[1024,768]{1,0:T(8,128)}, bf16[1024,768]{1,0:T(8,128)(2,1)}, bf16[1024,1536]{1,0:T(8,128)(2,1)}, bf16[1024,768]{1,0:T(8,128)(2,1)}, f32[1,7...) custom-call(f32[1024,768]{1,0:T(8,128)} %get-tuple-element.272.refs_0_, ...), custom_call_target="tpu_custom_call" | custom-call | flops 4831838208 | bytes 18874368 | tf_op jit(solution)/shard_map/pallas_call | solution.py:579
  421.8 4.5 shard_map.247.refs_1_
  429.1 6.4 convolution_convert_fusion.refs_3_
  435.6 4.5 shard_map.248.refs_8_
  440.1 6.0 convolution_convert_fusion.1.refs_2_
  455.3 26.7 %shard_map.246 = (f32[1024,768]{1,0:T(8,128)}, bf16[1024,768]{1,0:T(8,128)(2,1)}, bf16[1024,384]{1,0:T(8,128)(2,1)}, bf16[1024,384]{1,0:T(8,128)(2,1)}, bf16[1024,384]{1,0:T(8,128)(2,1)}, /*index=5*/f32[1,768]{1,0:T(1,128)}) custom-call(s32[4]{0:T(128)} %get-tuple-element.436.low_ref, s32[4]{0:T(128)} %get-tuple-element.435.high_ref, ...), custom_call_target="tpu_custom_call" | custom-call | flops 11274289152 | bytes 15728640 | tf_op jit(solution)/shard_map/pallas_call | solution.py:674
  495.7 8.0 %shard_map.251 = (bf16[1024,768]{1,0:T(8,128)(2,1)}, f32[1,768]{1,0:T(1,128)}, f32[1,768]{1,0:T(1,128)}, f32[1,384]{1,0:T(1,128)}, f32[1,384]{1,0:T(1,128)}) custom-call(bf16[1024,384]{1,0:T(8,128)(2,1)} %get-tuple-element.317.dq, bf16[1024,384]{1,0:T(8,128)(2,1)} %get-tuple-element.318.dk, bf16[1024,384]{1,0:T(8,128)(2,1)} %get-tuple-element.319.dv, ...), custom_call_target="tpu_custom_call" | custom-call | flops 1811939328 | bytes 7864320 | tf_op jit(solution)/shard_map/pallas_call | solution.py:738
  503.7 9.0 %collective-permute-start.51 = (bf16[1024,768]{1,0:T(8,128)(2,1)}, bf16[1024,768]{1,0:T(8,128)(2,1)}, u32[]{:S(2)}, u32[]{:S(2)}) collective-permute-start(bf16[1024,768]{1,0:T(8,128)(2,1)} %get-tuple-element.320), channel_id=1, source_target_pairs={{0,2},{1,3},{2,0},{3,1},{4,6},{5,7},{6,4},{7,5},{8,10},{9,11},{10,... | collective-permute-start | bytes 4718600 | tf_op jit(solution)/shard_map/ppermute | solution.py:867
  562.3 4.2 shard_map.255.refs_1_
  566.5 4.3 shard_map.256.refs_4_
  574.7 13.0 %collective-permute-done.55.refs_2_ = bf16[384,768]{1,0:T(8,128)(2,1)S(1)} collective-permute-done((bf16[384,768]{1,0:T(8,128)(2,1)S(1)}, bf16[384,768]{1,0:T(8,128)(2,1)S(1)}, u32[]{:S(2)}, u32[]{:S(2)}) %collective-permute-start.55) | collective-permute-done | bytes 589856 | tf_op jit(solution)/shard_map/ppermute | solution.py:867
  594.1 6.5 fusion.73.refs_4_
  609.5 6.5 fusion.78.refs_3_
  616.0 6.5 fusion.83.refs_2_
  623.5 4.2 shard_map.262.refs_0_.refs_2_.refs_3_
  636.3 10.8 %collective-permute-done.60.refs_1_ = bf16[4112,128]{1,0:T(8,128)(2,1)S(1)} collective-permute-done((bf16[4112,128]{1,0:T(8,128)(2,1)S(1)}, bf16[4112,128]{1,0:T(8,128)(2,1)S(1)}, u32[]{:S(2)}, u32[]{:S(2)}) %collective-permute-start.60) | collective-permute-done | bytes 1052704 | tf_op jit(solution)/shard_map/ppermute | solution.py:867
  682.7 4.0 collective-permute-done.67.refs_2_
  694.9 4.7 collective-permute-done.69.refs_2_
  742.7 11.0 %shard_map.279 = (f32[32,128,128]{2,1,0:T(8,128)}, f32[32,128,128]{2,1,0:T(8,128)}, f32[32,128,128]{2,1,0:T(8,128)}, f32[32,128,128]{2,1,0:T(8,128)}) custom-call(s32[32]{0:T(128)} %convert_element_type.270.used, s32[1]{0:T(128)} %bitcast.28.flag.home, bf16[4112,128]{1,0:T(8,128)(2,1)} %shard_map.277.near, bf16[4112,128]{1,0:T(8,128)(2,1)} %collective-permute-done.76.far, ...), custom_call_target="tpu_custom_call" | custom-call | flops 5905580032 | bytes 19922944 | tf_op jit(solution)/shard_map/pallas_call | solution.py:799
  (493 shorter events, 316.9 us)
Async XLA Ops:
  0.7 43.6 %collective-permute-start.8 = (bf16[1024,768]{1,0:T(8,128)(2,1)}, bf16[1024,768]{1,0:T(8,128)(2,1)}, u32[]{:S(2)}, u32[]{:S(2)}) collective-permute-start(bf16[1024,768]{1,0:T(8,128)(2,1)} %param.15), channel_id=1, source_target_pairs={{0,2},{3,1},{4,6},{7,5},{8,10},{11,9},{12,14},{15,13},{16,18},{19,... | collective-permute-start | bytes 4718600 | tf_op jit(solution)/shard_map/ppermute | solution.py:867
  19.2 20.5 %collective-permute-start.4 = (bf16[4112,128]{1,0:T(8,128)(2,1)S(1)}, bf16[4112,128]{1,0:T(8,128)(2,1)}, u32[]{:S(2)}, u32[]{:S(2)}) collective-permute-start(bf16[4112,128]{1,0:T(8,128)(2,1)S(1)} %get-tuple-element.423), channel_id=1, source_target_pairs={{1,3},{2,0},{5,7},{6,4},{9,11},{10,8},{13,15},{14,12},{17,19},{18,... | collective-permute-start | bytes 3158024 | tf_op jit(solution)/shard_map/ppermute | solution.py:867
  34.7 36.5 %collective-permute-start.10 = (bf16[4112,128]{1,0:T(8,128)(2,1)}, bf16[4112,128]{1,0:T(8,128)(2,1)S(1)}, u32[]{:S(2)}, u32[]{:S(2)}) collective-permute-start(bf16[4112,128]{1,0:T(8,128)(2,1)} %get-tuple-element.208), channel_id=1, source_target_pairs={{0,4},{3,7},{4,0},{7,3},{8,12},{11,15},{12,8},{15,11},{16,20},{19,... | collective-permute-start | bytes 3158024 | tf_op jit(solution)/shard_map/ppermute | solution.py:867
  38.3 35.2 %collective-permute-start.11 = (bf16[4112,128]{1,0:T(8,128)(2,1)}, bf16[4112,128]{1,0:T(8,128)(2,1)S(1)}, u32[]{:S(2)}, u32[]{:S(2)}) collective-permute-start(bf16[4112,128]{1,0:T(8,128)(2,1)} %get-tuple-element.208), channel_id=1, source_target_pairs={{0,1},{3,2},{4,5},{7,6},{8,9},{11,10},{12,13},{15,14},{16,17},{19,... | collective-permute-start | bytes 3158024 | tf_op jit(solution)/shard_map/ppermute | solution.py:867
  39.7 23.3 %collective-permute-start.5 = (bf16[4112,128]{1,0:T(8,128)(2,1)}, bf16[4112,128]{1,0:T(8,128)(2,1)S(1)}, u32[]{:S(2)}, u32[]{:S(2)}) collective-permute-start(bf16[4112,128]{1,0:T(8,128)(2,1)} %collective-permute-done.4), channel_id=1, source_target_pairs={{0,4},{3,7},{4,0},{7,3},{8,12},{11,15},{12,8},{15,11},{16,20},{19,... | collective-permute-start | bytes 3158024 | tf_op jit(solution)/shard_map/ppermute | solution.py:867
  42.0 22.9 %collective-permute-start.6 = (bf16[4112,128]{1,0:T(8,128)(2,1)}, bf16[4112,128]{1,0:T(8,128)(2,1)}, u32[]{:S(2)}, u32[]{:S(2)}) collective-permute-start(bf16[4112,128]{1,0:T(8,128)(2,1)} %collective-permute-done.4), channel_id=1, source_target_pairs={{0,1},{3,2},{4,5},{7,6},{8,9},{11,10},{12,13},{15,14},{16,17},{19,... | collective-permute-start | bytes 3158024 | tf_op jit(solution)/shard_map/ppermute | solution.py:867
  44.3 24.6 %collective-permute-start.7 = (bf16[4112,128]{1,0:T(8,128)(2,1)}, bf16[4112,128]{1,0:T(8,128)(2,1)}, u32[]{:S(2)}, u32[]{:S(2)}) collective-permute-start(bf16[4112,128]{1,0:T(8,128)(2,1)} %collective-permute-done.4), channel_id=1, source_target_pairs={{0,8},{3,11},{4,12},{7,15},{8,16},{11,19},{12,20},{15,23},{16,24},... | collective-permute-start | bytes 3158024 | tf_op jit(solution)/shard_map/ppermute | solution.py:867
  62.9 19.5 %collective-permute-start.13 = (bf16[4112,128]{1,0:T(8,128)(2,1)}, bf16[4112,128]{1,0:T(8,128)(2,1)}, u32[]{:S(2)}, u32[]{:S(2)}) collective-permute-start(bf16[4112,128]{1,0:T(8,128)(2,1)} %get-tuple-element.208), channel_id=1, source_target_pairs={{0,8},{3,11},{4,12},{7,15},{8,16},{11,19},{12,20},{15,23},{16,24},... | collective-permute-start | bytes 3158024 | tf_op jit(solution)/shard_map/ppermute | solution.py:867
  64.9 20.4 %collective-permute-start.12 = (bf16[4112,128]{1,0:T(8,128)(2,1)}, bf16[4112,128]{1,0:T(8,128)(2,1)}, u32[]{:S(2)}, u32[]{:S(2)}) collective-permute-start(bf16[4112,128]{1,0:T(8,128)(2,1)} %get-tuple-element.209), channel_id=1, source_target_pairs={{0,1},{3,2},{4,5},{7,6},{8,9},{11,10},{12,13},{15,14},{16,17},{19,... | collective-permute-start | bytes 3158024 | tf_op jit(solution)/shard_map/ppermute | solution.py:867
  68.9 25.1 %collective-permute-start.14 = (bf16[4112,128]{1,0:T(8,128)(2,1)}, bf16[4112,128]{1,0:T(8,128)(2,1)S(1)}, u32[]{:S(2)}, u32[]{:S(2)}) collective-permute-start(bf16[4112,128]{1,0:T(8,128)(2,1)} %get-tuple-element.212), channel_id=1, source_target_pairs={{0,4},{3,7},{4,0},{7,3},{8,12},{11,15},{12,8},{15,11},{16,20},{19,... | collective-permute-start | bytes 3158024 | tf_op jit(solution)/shard_map/ppermute | solution.py:867
  71.2 24.2 %collective-permute-start.15 = (bf16[4112,128]{1,0:T(8,128)(2,1)}, bf16[4112,128]{1,0:T(8,128)(2,1)}, u32[]{:S(2)}, u32[]{:S(2)}) collective-permute-start(bf16[4112,128]{1,0:T(8,128)(2,1)} %get-tuple-element.212), channel_id=1, source_target_pairs={{0,1},{3,2},{4,5},{7,6},{8,9},{11,10},{12,13},{15,14},{16,17},{19,... | collective-permute-start | bytes 3158024 | tf_op jit(solution)/shard_map/ppermute | solution.py:867
  73.5 24.1 %collective-permute-start.16 = (bf16[4112,128]{1,0:T(8,128)(2,1)}, bf16[4112,128]{1,0:T(8,128)(2,1)}, u32[]{:S(2)}, u32[]{:S(2)}) collective-permute-start(bf16[4112,128]{1,0:T(8,128)(2,1)} %get-tuple-element.213), channel_id=1, source_target_pairs={{1,5},{2,6},{5,1},{6,2},{9,13},{10,14},{13,9},{14,10},{17,21},{18,... | collective-permute-start | bytes 3158024 | tf_op jit(solution)/shard_map/ppermute | solution.py:867
  82.4 24.5 %collective-permute-start.17 = (bf16[4112,128]{1,0:T(8,128)(2,1)}, bf16[4112,128]{1,0:T(8,128)(2,1)}, u32[]{:S(2)}, u32[]{:S(2)}) collective-permute-start(bf16[4112,128]{1,0:T(8,128)(2,1)} %get-tuple-element.212), channel_id=1, source_target_pairs={{0,8},{3,11},{4,12},{7,15},{8,16},{11,19},{12,20},{15,23},{16,24},... | collective-permute-start | bytes 3158024 | tf_op jit(solution)/shard_map/ppermute | solution.py:867
  85.3 24.4 %collective-permute-start.18 = (bf16[4112,128]{1,0:T(8,128)(2,1)}, bf16[4112,128]{1,0:T(8,128)(2,1)S(1)}, u32[]{:S(2)}, u32[]{:S(2)}) collective-permute-start(bf16[4112,128]{1,0:T(8,128)(2,1)} %get-tuple-element.216), channel_id=1, source_target_pairs={{0,4},{3,7},{4,0},{7,3},{8,12},{11,15},{12,8},{15,11},{16,20},{19,... | collective-permute-start | bytes 3158024 | tf_op jit(solution)/shard_map/ppermute | solution.py:867
  95.4 23.9 %collective-permute-start.20 = (bf16[4112,128]{1,0:T(8,128)(2,1)}, bf16[4112,128]{1,0:T(8,128)(2,1)}, u32[]{:S(2)}, u32[]{:S(2)}) collective-permute-start(bf16[4112,128]{1,0:T(8,128)(2,1)} %get-tuple-element.217), channel_id=1, source_target_pairs={{0,1},{3,2},{4,5},{7,6},{8,9},{11,10},{12,13},{15,14},{16,17},{19,... | collective-permute-start | bytes 3158024 | tf_op jit(solution)/shard_map/ppermute | solution.py:867
  97.7 30.5 %collective-permute-start.21 = (bf16[4112,128]{1,0:T(8,128)(2,1)}, bf16[4112,128]{1,0:T(8,128)(2,1)}, u32[]{:S(2)}, u32[]{:S(2)}) collective-permute-start(bf16[4112,128]{1,0:T(8,128)(2,1)} %get-tuple-element.216), channel_id=1, source_target_pairs={{0,8},{3,11},{4,12},{7,15},{8,16},{11,19},{12,20},{15,23},{16,24},... | collective-permute-start | bytes 3158024 | tf_op jit(solution)/shard_map/ppermute | solution.py:867
  106.9 24.1 %collective-permute-start.22 = (bf16[4112,128]{1,0:T(8,128)(2,1)}, bf16[4112,128]{1,0:T(8,128)(2,1)S(1)}, u32[]{:S(2)}, u32[]{:S(2)}) collective-permute-start(bf16[4112,128]{1,0:T(8,128)(2,1)} %get-tuple-element.222), channel_id=1, source_target_pairs={{0,4},{3,7},{4,0},{7,3},{8,12},{11,15},{12,8},{15,11},{16,20},{19,... | collective-permute-start | bytes 3158024 | tf_op jit(solution)/shard_map/ppermute | solution.py:867
  109.7 24.9 %collective-permute-start.23 = (bf16[4112,128]{1,0:T(8,128)(2,1)}, bf16[4112,128]{1,0:T(8,128)(2,1)}, u32[]{:S(2)}, u32[]{:S(2)}) collective-permute-start(bf16[4112,128]{1,0:T(8,128)(2,1)} %get-tuple-element.222), channel_id=1, source_target_pairs={{0,1},{3,2},{4,5},{7,6},{8,9},{11,10},{12,13},{15,14},{16,17},{19,... | collective-permute-start | bytes 3158024 | tf_op jit(solution)/shard_map/ppermute | solution.py:867
  112.0 24.9 %collective-permute-start.25 = (bf16[4112,128]{1,0:T(8,128)(2,1)}, bf16[4112,128]{1,0:T(8,128)(2,1)}, u32[]{:S(2)}, u32[]{:S(2)}) collective-permute-start(bf16[4112,128]{1,0:T(8,128)(2,1)} %get-tuple-element.222), channel_id=1, source_target_pairs={{0,8},{3,11},{4,12},{7,15},{8,16},{11,19},{12,20},{15,23},{16,24},... | collective-permute-start | bytes 3158024 | tf_op jit(solution)/shard_map/ppermute | solution.py:867
  128.2 21.5 %collective-permute-start.26 = (bf16[4112,128]{1,0:T(8,128)(2,1)}, bf16[4112,128]{1,0:T(8,128)(2,1)S(1)}, u32[]{:S(2)}, u32[]{:S(2)}) collective-permute-start(bf16[4112,128]{1,0:T(8,128)(2,1)} %get-tuple-element.227), channel_id=1, source_target_pairs={{0,4},{3,7},{4,0},{7,3},{8,12},{11,15},{12,8},{15,11},{16,20},{19,... | collective-permute-start | bytes 3158024 | tf_op jit(solution)/shard_map/ppermute | solution.py:867
  131.0 20.4 %collective-permute-start.27 = (bf16[4112,128]{1,0:T(8,128)(2,1)}, bf16[4112,128]{1,0:T(8,128)(2,1)S(1)}, u32[]{:S(2)}, u32[]{:S(2)}) collective-permute-start(bf16[4112,128]{1,0:T(8,128)(2,1)} %get-tuple-element.227), channel_id=1, source_target_pairs={{0,1},{3,2},{4,5},{7,6},{8,9},{11,10},{12,13},{15,14},{16,17},{19,... | collective-permute-start | bytes 3158024 | tf_op jit(solution)/shard_map/ppermute | solution.py:867
  134.6 23.9 %collective-permute-start.28 = (bf16[4112,128]{1,0:T(8,128)(2,1)}, bf16[4112,128]{1,0:T(8,128)(2,1)}, u32[]{:S(2)}, u32[]{:S(2)}) collective-permute-start(bf16[4112,128]{1,0:T(8,128)(2,1)} %get-tuple-element.223), channel_id=1, source_target_pairs={{0,1},{3,2},{4,5},{7,6},{8,9},{11,10},{12,13},{15,14},{16,17},{19,... | collective-permute-start | bytes 3158024 | tf_op jit(solution)/shard_map/ppermute | solution.py:867
  136.9 32.1 %collective-permute-start.29 = (bf16[4112,128]{1,0:T(8,128)(2,1)}, bf16[4112,128]{1,0:T(8,128)(2,1)S(1)}, u32[]{:S(2)}, u32[]{:S(2)}) collective-permute-start(bf16[4112,128]{1,0:T(8,128)(2,1)} %get-tuple-element.228), channel_id=1, source_target_pairs={{0,4},{3,7},{4,0},{7,3},{8,12},{11,15},{12,8},{15,11},{16,20},{19,... | collective-permute-start | bytes 3158024 | tf_op jit(solution)/shard_map/ppermute | solution.py:867
  140.0 29.7 %collective-permute-start.30 = (bf16[4112,128]{1,0:T(8,128)(2,1)}, bf16[4112,128]{1,0:T(8,128)(2,1)}, u32[]{:S(2)}, u32[]{:S(2)}) collective-permute-start(bf16[4112,128]{1,0:T(8,128)(2,1)} %get-tuple-element.228), channel_id=1, source_target_pairs={{0,1},{3,2},{4,5},{7,6},{8,9},{11,10},{12,13},{15,14},{16,17},{19,... | collective-permute-start | bytes 3158024 | tf_op jit(solution)/shard_map/ppermute | solution.py:867
  149.7 20.0 %collective-permute-start.31 = (bf16[4112,128]{1,0:T(8,128)(2,1)}, bf16[4112,128]{1,0:T(8,128)(2,1)}, u32[]{:S(2)}, u32[]{:S(2)}) collective-permute-start(bf16[4112,128]{1,0:T(8,128)(2,1)} %get-tuple-element.232), channel_id=1, source_target_pairs={{1,5},{2,6},{5,1},{6,2},{9,13},{10,14},{13,9},{14,10},{17,21},{18,... | collective-permute-start | bytes 3158024 | tf_op jit(solution)/shard_map/ppermute | solution.py:867
  158.4 22.6 %collective-permute-start.32 = (bf16[4112,128]{1,0:T(8,128)(2,1)}, bf16[4112,128]{1,0:T(8,128)(2,1)S(1)}, u32[]{:S(2)}, u32[]{:S(2)}) collective-permute-start(bf16[4112,128]{1,0:T(8,128)(2,1)} %get-tuple-element.230), channel_id=1, source_target_pairs={{0,1},{3,2},{4,5},{7,6},{8,9},{11,10},{12,13},{15,14},{16,17},{19,... | collective-permute-start | bytes 3158024 | tf_op jit(solution)/shard_map/ppermute | solution.py:867
  289.2 19.3 %collective-permute-start.39 = (bf16[1024,768]{1,0:T(8,128)(2,1)S(1)}, bf16[1024,768]{1,0:T(8,128)(2,1)S(1)}, u32[]{:S(2)}, u32[]{:S(2)}) collective-permute-start(bf16[1024,768]{1,0:T(8,128)(2,1)S(1)} %copy-done.58), channel_id=1, source_target_pairs={{0,2},{3,1},{4,6},{7,5},{8,10},{11,9},{12,14},{15,13},{16,18},{19,... | collective-permute-start | bytes 4718600 | tf_op jit(solution)/shard_map/ppermute | solution.py:867
  326.7 26.6 %collective-permute-start.41 = (bf16[1024,768]{1,0:T(8,128)(2,1)S(1)}, bf16[1024,768]{1,0:T(8,128)(2,1)S(1)}, u32[]{:S(2)}, u32[]{:S(2)}) collective-permute-start(bf16[1024,768]{1,0:T(8,128)(2,1)S(1)} %multiply_convert_fusion), channel_id=1, source_target_pairs={{0,1},{3,2},{4,5},{7,6},{8,9},{11,10},{12,13},{15,14},{16,17},{19,... | collective-permute-start | bytes 4718600 | tf_op jit(solution)/shard_map/ppermute | solution.py:867
  354.4 31.0 %collective-permute-start.42 = (bf16[1536,768]{1,0:T(8,128)(2,1)}, bf16[1536,768]{1,0:T(8,128)(2,1)}, u32[]{:S(2)}, u32[]{:S(2)}) collective-permute-start(bf16[1536,768]{1,0:T(8,128)(2,1)} %get-tuple-element.276.own), channel_id=1, source_target_pairs={{1,0},{2,3},{5,4},{6,7},{9,8},{10,11},{13,12},{14,15},{17,16},{18,... | collective-permute-start | bytes 7077896 | tf_op jit(solution)/shard_map/ppermute | solution.py:867
  356.6 62.6 %collective-permute-start.44 = (bf16[768,1536]{1,0:T(8,128)(2,1)}, bf16[768,1536]{1,0:T(8,128)(2,1)S(1)}, u32[]{:S(2)}, u32[]{:S(2)}) collective-permute-start(bf16[768,1536]{1,0:T(8,128)(2,1)} %get-tuple-element.285.own), channel_id=1, source_target_pairs={{1,0},{2,3},{5,4},{6,7},{9,8},{10,11},{13,12},{14,15},{17,16},{18,... | collective-permute-start | bytes 7077896 | tf_op jit(solution)/shard_map/ppermute | solution.py:867
  420.7 25.4 %collective-permute-start.45 = (bf16[1024,768]{1,0:T(8,128)(2,1)}, bf16[1024,768]{1,0:T(8,128)(2,1)S(1)}, u32[]{:S(2)}, u32[]{:S(2)}) collective-permute-start(bf16[1024,768]{1,0:T(8,128)(2,1)} %get-tuple-element.288.refs_0_), channel_id=1, source_target_pairs={{0,2},{1,3},{2,0},{3,1},{4,6},{5,7},{6,4},{7,5},{8,10},{9,11},{10,... | collective-permute-start | bytes 4718600 | tf_op jit(solution)/shard_map/ppermute | solution.py:867
  426.5 19.6 %collective-permute-start.46 = (bf16[384,1152]{1,0:T(8,128)(2,1)S(1)}, bf16[384,1152]{1,0:T(8,128)(2,1)S(1)}, u32[]{:S(2)}, u32[]{:S(2)}) collective-permute-start(bf16[384,1152]{1,0:T(8,128)(2,1)S(1)} %constant_dynamic-slice_fusion.3), channel_id=1, source_target_pairs={{1,5},{2,6},{5,1},{6,2},{9,13},{10,14},{13,9},{14,10},{17,21},{18,... | collective-permute-start | bytes 2654216 | tf_op jit(solution)/shard_map/ppermute | solution.py:867
  449.8 32.3 %collective-permute-start.49 = (bf16[768,768]{1,0:T(8,128)(2,1)S(1)}, bf16[768,768]{1,0:T(8,128)(2,1)S(1)}, u32[]{:S(2)}, u32[]{:S(2)}) collective-permute-start(bf16[768,768]{1,0:T(8,128)(2,1)S(1)} %constant_dynamic-slice_fusion.2), channel_id=1, source_target_pairs={{1,5},{2,6},{5,1},{6,2},{9,13},{10,14},{13,9},{14,10},{17,21},{18,... | collective-permute-start | bytes 3538952 | tf_op jit(solution)/shard_map/ppermute | solution.py:867
  450.8 32.2 %collective-permute-start.50 = (bf16[384,1536]{1,0:T(8,128)(2,1)S(1)}, bf16[384,1536]{1,0:T(8,128)(2,1)}, u32[]{:S(2)}, u32[]{:S(2)}) collective-permute-start(bf16[384,1536]{1,0:T(8,128)(2,1)S(1)} %constant_dynamic-slice_fusion.1), channel_id=1, source_target_pairs={{1,5},{2,6},{5,1},{6,2},{9,13},{10,14},{13,9},{14,10},{17,21},{18,... | collective-permute-start | bytes 3538952 | tf_op jit(solution)/shard_map/ppermute | solution.py:867
  453.9 28.2 %collective-permute-start.48 = (bf16[384,1152]{1,0:T(8,128)(2,1)S(1)}, bf16[384,1152]{1,0:T(8,128)(2,1)S(1)}, u32[]{:S(2)}, u32[]{:S(2)}) collective-permute-start(bf16[384,1152]{1,0:T(8,128)(2,1)S(1)} %add_convert_fusion.5), channel_id=1, source_target_pairs={{1,0},{2,3},{5,4},{6,7},{9,8},{10,11},{13,12},{14,15},{17,16},{18,... | collective-permute-start | bytes 2654216 | tf_op jit(solution)/shard_map/ppermute | solution.py:867
  515.2 47.1 %collective-permute-start.58 = (bf16[768,768]{1,0:T(8,128)(2,1)}, bf16[768,768]{1,0:T(8,128)(2,1)}, u32[]{:S(2)}, u32[]{:S(2)}) collective-permute-start(bf16[768,768]{1,0:T(8,128)(2,1)} %get-tuple-element.345), channel_id=1, source_target_pairs={{1,0},{2,3},{5,4},{6,7},{9,8},{10,11},{13,12},{14,15},{17,16},{18,... | collective-permute-start | bytes 3538952 | tf_op jit(solution)/shard_map/ppermute | solution.py:867
  516.7 49.8 %collective-permute-start.57 = (bf16[384,1536]{1,0:T(8,128)(2,1)S(1)}, bf16[384,1536]{1,0:T(8,128)(2,1)}, u32[]{:S(2)}, u32[]{:S(2)}) collective-permute-start(bf16[384,1536]{1,0:T(8,128)(2,1)S(1)} %copy-done.28), channel_id=1, source_target_pairs={{1,0},{2,3},{5,4},{6,7},{9,8},{10,11},{13,12},{14,15},{17,16},{18,... | collective-permute-start | bytes 3538952 | tf_op jit(solution)/shard_map/ppermute | solution.py:867
  550.3 21.8 %collective-permute-start.53 = (bf16[1536,384]{1,0:T(8,128)(2,1)}, bf16[1536,384]{1,0:T(8,128)(2,1)}, u32[]{:S(2)}, u32[]{:S(2)}) collective-permute-start(bf16[1536,384]{1,0:T(8,128)(2,1)} %constant_dynamic-slice_fusion.4), channel_id=1, source_target_pairs={{1,5},{2,6},{5,1},{6,2},{9,13},{10,14},{13,9},{14,10},{17,21},{18,... | collective-permute-start | bytes 3538952 | tf_op jit(solution)/shard_map/ppermute | solution.py:867
  552.0 39.6 %collective-permute-start.54 = (bf16[384,1152]{1,0:T(8,128)(2,1)S(1)}, bf16[384,1152]{1,0:T(8,128)(2,1)S(1)}, u32[]{:S(2)}, u32[]{:S(2)}) collective-permute-start(bf16[384,1152]{1,0:T(8,128)(2,1)S(1)} %copy-done.44), channel_id=1, source_target_pairs={{1,0},{2,3},{5,4},{6,7},{9,8},{10,11},{13,12},{14,15},{17,16},{18,... | collective-permute-start | bytes 2654216 | tf_op jit(solution)/shard_map/ppermute | solution.py:867
  553.9 33.9 %collective-permute-start.55 = (bf16[384,768]{1,0:T(8,128)(2,1)S(1)}, bf16[384,768]{1,0:T(8,128)(2,1)S(1)}, u32[]{:S(2)}, u32[]{:S(2)}) collective-permute-start(bf16[384,768]{1,0:T(8,128)(2,1)S(1)} %copy-done.24), channel_id=1, source_target_pairs={{1,0},{2,3},{5,4},{6,7},{9,8},{10,11},{13,12},{14,15},{17,16},{18,... | collective-permute-start | bytes 1769480 | tf_op jit(solution)/shard_map/ppermute | solution.py:867
  570.8 20.8 %collective-permute-start.56 = (bf16[16,16,128]{2,1,0:T(8,128)(2,1)S(1)}, bf16[16,16,128]{2,1,0:T(8,128)(2,1)S(1)}, u32[]{:S(2)}, u32[]{:S(2)}) collective-permute-start(bf16[16,16,128]{2,1,0:T(8,128)(2,1)S(1)} %copy-done.68), channel_id=1, source_target_pairs={{1,0},{2,3},{5,4},{6,7},{9,8},{10,11},{13,12},{14,15},{17,16},{18,... | collective-permute-start | bytes 196616 | tf_op jit(solution)/shard_map/ppermute | solution.py:867
  592.5 30.0 %collective-permute-start.59 = (bf16[1536,384]{1,0:T(8,128)(2,1)}, bf16[1536,384]{1,0:T(8,128)(2,1)S(1)}, u32[]{:S(2)}, u32[]{:S(2)}) collective-permute-start(bf16[1536,384]{1,0:T(8,128)(2,1)} %get-tuple-element.350), channel_id=1, source_target_pairs={{1,0},{2,3},{5,4},{6,7},{9,8},{10,11},{13,12},{14,15},{17,16},{18,... | collective-permute-start | bytes 3538952 | tf_op jit(solution)/shard_map/ppermute | solution.py:867
  632.3 29.1 %collective-permute-start.61 = (bf16[4112,128]{1,0:T(8,128)(2,1)}, bf16[4112,128]{1,0:T(8,128)(2,1)}, u32[]{:S(2)}, u32[]{:S(2)}) collective-permute-start(bf16[4112,128]{1,0:T(8,128)(2,1)} %get-tuple-element.420), channel_id=1, source_target_pairs={{0,4},{3,7},{4,0},{7,3},{8,12},{11,15},{12,8},{15,11},{16,20},{19,... | collective-permute-start | bytes 3158024 | tf_op jit(solution)/shard_map/ppermute | solution.py:867
  667.8 18.9 %collective-permute-start.67 = (bf16[4112,128]{1,0:T(8,128)(2,1)}, bf16[4112,128]{1,0:T(8,128)(2,1)}, u32[]{:S(2)}, u32[]{:S(2)}) collective-permute-start(bf16[4112,128]{1,0:T(8,128)(2,1)} %get-tuple-element.371), channel_id=1, source_target_pairs={{0,8},{3,11},{4,12},{7,15},{8,16},{11,19},{12,20},{15,23},{16,24},... | collective-permute-start | bytes 3158024 | tf_op jit(solution)/shard_map/ppermute | solution.py:867
  682.6 24.4 %collective-permute-start.62 = (bf16[1024,768]{1,0:T(8,128)(2,1)S(1)}, bf16[1024,768]{1,0:T(8,128)(2,1)S(1)}, u32[]{:S(2)}, u32[]{:S(2)}) collective-permute-start(bf16[1024,768]{1,0:T(8,128)(2,1)S(1)} %copy-done.3), channel_id=1, source_target_pairs={{0,2},{1,3},{2,0},{3,1},{4,6},{5,7},{6,4},{7,5},{8,10},{9,11},{10,... | collective-permute-start | bytes 4718600 | tf_op jit(solution)/shard_map/ppermute | solution.py:867
  690.3 20.3 %collective-permute-start.70 = (bf16[4112,128]{1,0:T(8,128)(2,1)}, bf16[4112,128]{1,0:T(8,128)(2,1)}, u32[]{:S(2)}, u32[]{:S(2)}) collective-permute-start(bf16[4112,128]{1,0:T(8,128)(2,1)} %get-tuple-element.380), channel_id=1, source_target_pairs={{0,4},{3,7},{4,0},{7,3},{8,12},{11,15},{12,8},{15,11},{16,20},{19,... | collective-permute-start | bytes 3158024 | tf_op jit(solution)/shard_map/ppermute | solution.py:867
  708.4 23.7 %collective-permute-start.63 = (bf16[1024,384]{1,0:T(8,128)(2,1)}, bf16[1024,384]{1,0:T(8,128)(2,1)}, u32[]{:S(2)}, u32[]{:S(2)}) collective-permute-start(bf16[1024,384]{1,0:T(8,128)(2,1)} %select_convert_fusion), channel_id=1, source_target_pairs={{0,1},{3,2},{4,5},{7,6},{8,9},{11,10},{12,13},{15,14},{16,17},{19,... | collective-permute-start | bytes 2359304 | tf_op jit(solution)/shard_map/ppermute | solution.py:867
  715.4 19.6 %collective-permute-start.74 = (bf16[4112,128]{1,0:T(8,128)(2,1)}, bf16[4112,128]{1,0:T(8,128)(2,1)}, u32[]{:S(2)}, u32[]{:S(2)}) collective-permute-start(bf16[4112,128]{1,0:T(8,128)(2,1)} %get-tuple-element.390), channel_id=1, source_target_pairs={{0,4},{3,7},{4,0},{7,3},{8,12},{11,15},{12,8},{15,11},{16,20},{19,... | collective-permute-start | bytes 3158024 | tf_op jit(solution)/shard_map/ppermute | solution.py:867
  (138 other events, 1300.1 us)

commit v4 on v3

--- a/solution.py
+++ b/solution.py
@@ -356,6 +356,121 @@
         input_output_aliases={len(operands): 0},
         compiler_params=params(),
     )(pos, *operands)
+
+
+def expand_kernel(present, patch_ref, class_ref, pinv_ref, out, total):
+    for block in range(patch_ref.shape[0] // ROWS):
+        rows = slice(block * ROWS, (block + 1) * ROWS)
+        total[...] = jnp.zeros_like(total)
+        for which in range(3):
+
+            @pl.when(present[block, which] > 0)
+            def _(which=which, rows=rows):
+                chosen = jnp.where(class_ref[rows, :] == which, patch_ref[rows, :].astype(f32), 0.0)
+                total[...] += dot_nt(chosen.astype(bf16), pinv_ref[which])
+
+        out[rows, :] = total[...].astype(bf16)
+
+
+def expand_call(which, present, patches, class_col, pinv):
+    tokens = patches.shape[0]
+    size = BASE_PIX // CHUNKS
+    step = size // 3
+    return pl.pallas_call(
+        expand_kernel,
+        out_shape=jax.ShapeDtypeStruct((tokens, size), bf16),
+        grid_spec=pltpu.PrefetchScalarGridSpec(
+            num_scalar_prefetch=1,
+            grid=(3,),
+            in_specs=[
+                fixed(patches.shape),
+                fixed(class_col.shape),
+                pl.BlockSpec((3, step, pinv.shape[2]), lambda i, *_: (0, which * 3 + i, 0)),
+            ],
+            out_specs=pl.BlockSpec((tokens, step), lambda i, *_: (0, i)),
+            scratch_shapes=[pltpu.VMEM((ROWS, step), f32)],
+        ),
+        compiler_params=params(),
+        cost_estimate=cost(3 * tokens * size * D, tokens * size * 4 + size * D * 6),
+    )(present, patches, class_col, pinv)
+
+
+def resize_kernel(base, pinv_ref, out, turned):
+    @pl.when(pl.program_id(0) == 0)
+    def _():
+        turned[...] = base[...].T
+
+    out[0] = dot(turned[...], pinv_ref[0]).astype(bf16)
+
+
+def resize_call(panels, pinv):
+    return pl.pallas_call(
+        resize_kernel,
+        out_shape=jax.ShapeDtypeStruct((3, HALF, pinv.shape[2]), bf16),
+        grid=(3,),
+        in_specs=[
+            fixed((BASE_PIX, HALF), PANELS["base"] // BASE_PIX),
+            pl.BlockSpec((1, BASE_PIX, pinv.shape[2]), lambda i: (i, 0, 0)),
+        ],
+        out_specs=pl.BlockSpec((1, HALF, pinv.shape[2]), lambda i: (i, 0, 0)),
+        scratch_shapes=[pltpu.VMEM((HALF, BASE_PIX), bf16)],
+        compiler_params=params(),
+        cost_estimate=cost(6 * D * BASE_PIX * HALF, 6 * D * BASE_PIX),
+    )(panels, pinv)
+
+
+def embed_back_kernel(core, base, own, recv, out, bias):
+    low = (base[...] + (own[...].astype(f32) + recv[...].astype(f32))).astype(bf16)
+    out[...] = low
+    accumulate(bias, jnp.sum(low.astype(f32), axis=0, keepdims=True))
+
+
+def embed_back_call(core, base, own, recv):
+    tokens = base.shape[0]
+    half = pl.BlockSpec((ROWS, HALF), lambda i, core: (i, core[0]))
+    return pl.pallas_call(
+        embed_back_kernel,
+        out_shape=[
+            jax.ShapeDtypeStruct((tokens, HALF), bf16),
+            jax.ShapeDtypeStruct((1, HALF), f32),
+        ],
+        grid_spec=pltpu.PrefetchScalarGridSpec(
+            num_scalar_prefetch=1,
+            grid=(tokens // ROWS,),
+            in_specs=[half] * 3,
+            out_specs=[rows_spec(HALF), fixed((1, HALF))],
+        ),
+        compiler_params=params(),
+        cost_estimate=cost(tokens * D, tokens * D * 5),
+    )(core, base, own, recv)
+
+
+def pack_kernel(vec_per, *refs):
+    *pieces, out = refs
+    out[...] = jnp.zeros_like(out)
+    at = 0
+    for piece in pieces:
+        for k in range(piece.shape[1] // BS):
+            owner, row = divmod(at, vec_per // BS)
+            out[owner, row : row + 1, :] = piece[:, k * BS : (k + 1) * BS]
+            at += 1
+
+
+def pack_call(pieces, owners, vec_per):
+    if vec_per % BS:
+        joined = jnp.concatenate(pieces, axis=1)[0]
+        joined = jnp.pad(joined, (0, owners * vec_per - joined.shape[0])).reshape(owners, vec_per)
+        joined = jnp.pad(joined, ((0, 0), (0, VEC_ROWS * BS - vec_per)))
+        return joined.astype(bf16).reshape(owners, VEC_ROWS, BS)
+    return pl.pallas_call(
+        functools.partial(pack_kernel, vec_per),
+        out_shape=jax.ShapeDtypeStruct((owners, VEC_ROWS, BS), f32),
+        grid=(1,),
+        in_specs=[fixed(p.shape) for p in pieces],
+        out_specs=fixed((owners, VEC_ROWS, BS)),
+        compiler_params=params(),
+        cost_estimate=cost(0, owners * vec_per * 8),
+    )(*pieces).astype(bf16)
 
 
 def embed_kernel(*refs):
@@ -925,16 +1040,11 @@
     last_blk = ((last_tok + ROWS - 1) // ROWS).astype(jnp.int32)
 
     select_low = select.astype(bf16)
-    spread_in = patches[:, None, :] * select_low[:, :, None]
+    class_col = jnp.sum(jnp.where(select, jnp.arange(1, 4)[None, :], 0), axis=1, keepdims=True) - 1
+    present = jnp.any(select.reshape(blocks_n, ROWS, 3), axis=1).astype(jnp.int32)
 
     def expand(which):
-        size = BASE_PIX // CHUNKS
-        return lax.dot_general(
-            spread_in,
-            pinv[:, which * size : (which + 1) * size],
-            (((1, 2), (0, 2)), ((), ())),
-            preferred_element_type=f32,
-        ).astype(bf16)
+        return expand_call(which, present, patches, class_col, pinv)
 
     vec_low = jnp.pad(vec_master[0].astype(bf16), (0, VEC_ROWS * BS - vec_per))
     own_pack = jnp.concatenate(
@@ -1024,7 +1134,6 @@
         caches.append((hidden, normed, queries, keys, values, mixed, lse, middle, normed2, act, slope))
         hidden = middle
     out_low = ((hidden + (own.astype(f32) + recv.astype(f32))) * valid_col).astype(bf16)
-    out_other = send(out_low, routes.y_out)
 
     owners = jnp.arange(dp_n)
     if grid3:
@@ -1099,8 +1208,7 @@
     other = send(part, routes.core_all)
     gd1 = dot_tn(caches[top][9], grad_low).astype(bf16)
     gu1 = dot_tn(caches[top][8], du).astype(bf16)
-    part, other, gd1, gu1, out_other = fence(part, other, gd1, gu1, out_other)
-    output = jnp.where(home, out_low, out_other).astype(f32)
+    part, other, gd1, gu1 = fence(part, other, gd1, gu1)
     ad1 = over(gd1)
     grad, grad_low, dq, dk, dv, dbo = attend_step(top, grad, part, other)
     dq, dk, dv, ad1 = hold(dq, dk, dv, ad1)
@@ -1127,65 +1235,51 @@
     )
     hd0 = half_sum(gd0, xd0) if grid3 else None
     hu0 = half_sum(gu0, xu0) if grid3 else None
-    go0 = dot_tn(caches[low][5], grad_low).astype(bf16)
-    gq0 = dot_tn(caches[low][1], jnp.concatenate([dq, dk, dv], axis=1)).astype(bf16)
-    dq, dk, dv, hd0, hu0, go0, gq0 = hold(dq, dk, dv, hd0, hu0, go0, gq0)
+    dq, dk, dv, hd0, hu0 = hold(dq, dk, dv, hd0, hu0)
     ad0, au0 = over(hd0), over(hu0)
-    xq0 = beside(gq0)
     own, dg1, ds1, dbq, dbv = qkv_back_call(low, dq, dk, dv, caches[low][0], vec, panels)
     recv = send(own, routes.core_all)
+    gq0 = dot_tn(caches[low][1], jnp.concatenate([dq, dk, dv], axis=1)).astype(bf16)
     vec_grads[low] = [dg1, ds1, dbq, dbv, dbo, dg2, ds2, db1, db2]
-    sides = [
-        grad[:, s * HALF : (s + 1) * HALF]
-        + (
-            own[:, s * HALF : (s + 1) * HALF].astype(f32)
-            + recv[:, s * HALF : (s + 1) * HALF].astype(f32)
-        )
-        for s in range(TENSOR)
-    ]
-    grad_emb = jnp.where(core == 0, sides[0], sides[1]).astype(bf16)
-    grad_emb_bias = jnp.sum(grad_emb.astype(f32), axis=0, keepdims=True)
+    own, recv, gq0 = hold(own, recv, gq0)
+    xq0 = beside(gq0)
+    grad_emb, grad_emb_bias = embed_back_call(core_flag, grad, own, recv)
     gb = jnp.concatenate([dot_tn(c, grad_emb).astype(bf16) for c in chunks], axis=0)
-    vec_grad = jnp.concatenate([grad_emb_bias] + vec_grads[0] + vec_grads[1], axis=1)[0]
-    vec_grad = jnp.pad(vec_grad, (0, dp_n * vec_per - vec_grad.shape[0])).reshape(dp_n, vec_per)
-    vec_grad = jnp.pad(vec_grad, ((0, 0), (0, VEC_ROWS * BS - vec_per)))
-    vec_grad = vec_grad.astype(bf16).reshape(dp_n, VEC_ROWS, BS)
+    vec_grad = pack_call([grad_emb_bias] + vec_grads[0] + vec_grads[1], dp_n, vec_per)
+    go0 = dot_tn(caches[low][5], grad_low).astype(bf16)
+    gb, vec_grad, grad_emb, go0, gq0, xq0 = hold(gb, vec_grad, grad_emb, go0, gq0, xq0)
+    xb = beside(gb)
     hq0 = half_sum(gq0, xq0) if grid3 else None
-    gb, vec_grad, grad_emb, hq0 = hold(gb, vec_grad, grad_emb, hq0)
     aq0, ao0, av = over(hq0), over(go0), over(vec_grad)
-    xb = beside(gb)
     buffer = place_tiles(("out", top), go1, ao1, buffer)
     buffer = place_tiles(("qkv", top), gq1, aq1, buffer)
     buffer = place_tiles(("down", low), gd0, ad0, buffer)
     buffer = place_tiles(("up", low), gu0, au0, buffer)
+    gb, xb, aq0, ao0, av, buffer = hold(gb, xb, aq0, ao0, av, buffer)
     hb = half_sum(gb, xb) if grid3 else None
-    hb, aq0, ao0, av, buffer, panels, grad_emb = hold(hb, aq0, ao0, av, buffer, panels, grad_emb)
+    hb, gb, aq0, buffer = hold(hb, gb, aq0, buffer)
     ab = over(hb)
     buffer = place_tiles(("out", low), go0, ao0, buffer)
     buffer = scatter_vec(vec_pos, vec_grad, av, buffer)
     buffer = place_tiles(("qkv", low), gq0, aq0, buffer)
-    base_here = panels[PANELS["base"] : PANELS["base"] + BASE_PIX]
-    resized = [dot_tn(pinv[s], base_here).astype(bf16) for s in range(3)]
-    ab, buffer, *resized = hold(ab, buffer, *resized)
+    ab, buffer, panels, grad_emb, out_low = hold(ab, buffer, panels, grad_emb, out_low)
     buffer = place_tiles("base", gb, ab, buffer)
-    grad_pixels = sum(
-        dot_nt(grad_emb * select_low[:, s : s + 1], resized[s]) for s in range(3)
-    ).astype(bf16)
 
     if grid3:
         token = jnp.zeros((8, BS), f32)
         order = (1, 0)
+        resized = resize_call(panels, pinv)
         carried = {n: None for n in order}
         across = {n: send(buffer.reshape(4, 2, 2, payload, BS)[0, 1, n], routes.x_home) for n in order}
         rounded = {}
         for j in range(4):
             for n in order:
                 extra = None
-                if j == 0 and n == order[1]:
-                    extra = grad_pixels
+                if j == 0 and n == order[0]:
+                    extra = resized
                 token, across[n], carried[n], extra = hold(token, across[n], carried[n], extra)
                 if extra is not None:
-                    grad_pixels = extra
+                    resized = extra
                 total, later = reduce_call(j, n, buffer, across[n], carried[n], payload)
                 if j < 3:
                     carried[n] = send(total, routes.z_home)
@@ -1206,7 +1300,12 @@
         both = jnp.where(used_rows, both, 0.0).reshape(dp_n * TENSOR * payload, BS)
         near_grad = lax.psum_scatter(both, AXES, scatter_dimension=0, tiled=True).astype(bf16)
         far_grad = near_grad
-
+        resized = resize_call(panels, pinv)
+
+    output = jnp.where(home, out_low, send(out_low, routes.y_out)).astype(f32)
+    grad_pixels = sum(
+        dot(grad_emb * select_low[:, s : s + 1], resized[s]) for s in range(3)
+    ).astype(bf16)
     pixels_other = send(grad_pixels, routes.core_all)
     pixel_sides = [
         grad_pixels[:, s * HALF : (s + 1) * HALF].astype(f32)

time: 765 us -> 733 us (0.958)
  Pallas kernels: 281 us -> 338 us
  matrix products: 92.9 us -> 44.3 us
  waiting for transfers between devices: 118 us -> 69.6 us
  starting transfers between devices: 175 us -> 196 us
  local copies, waits for them, and re-layouts: 39 us -> 30.4 us
    pallas_call x0 -> x7, Pallas kernels: none -> 50.7 us  [the longest x4 34 us: expand_call(): pl.pallas_call(expand_kernel, out_shape=jax.ShapeDtypeStruct((tokens, siz...]
    ppermute x77, waiting for transfers between devices: 118 us -> 69.6 us  [send(): return lax.ppermute(value, AXES, route)]
    dot_general x7 -> x3, matrix products: 33.6 us -> 3.09 us  [dot(): return jnp.dot(left, right, preferred_element_type=f32)]
    ppermute x77, starting transfers between devices: 175 us -> 196 us  [send(): return lax.ppermute(value, AXES, route)]
    dot_general x15 -> x12, matrix products: 59.3 us -> 41.2 us  [dot_tn(): lax.dot_general(left, right, (((0,), (0,)), ((), ())), preferred_element_...]
    unnamed x19 -> x2, other arithmetic: 9.86 us -> 0.01 us
    unnamed x223 -> x152, local copies, waits for them, and re-layouts: 22.3 us -> 16.1 us
  transfers between devices with their start and end apart: 77 -> 77, of which waited for: 26 -> 23; matrix products, arithmetic and copies ran while one was open for 19% -> 12% of each run, Pallas kernels for 22% -> 31%
where the time goes in v4:
time: 733 us; the launch traced here: 722 us
  Pallas kernels  338 us (46%)
  starting transfers between devices  196 us (27%)
  waiting for transfers between devices  69.6 us (9%)
  matrix products  44.3 us (6%)
  other arithmetic  41.5 us (6%)
  local copies, waits for them, and re-layouts  30.4 us (4%)
    ppermute x77, starting transfers between devices, send(): return lax.ppermute(value, AXES, route)  196 us
    ppermute x77, waiting for transfers between devices, send(): return lax.ppermute(value, AXES, route)  69.6 us
    pallas_call x2, Pallas kernels, attend_back_call(): pl.pallas_call(attend_back_kernel, out_shape=[shape(D, f32), shape(D, bf1...  59.7 us
    dot_general x12, matrix products, dot_tn(): lax.dot_general(left, right, (((0,), (0,)), ((), ())), preferred_element_...  41.2 us
    pallas_call x2, Pallas kernels, attend_call(): pl.pallas_call(functools.partial(attend_kernel, layer), out_shape=[jax.Sh...  39.1 us
    pallas_call x9, Pallas kernels, scatter_matrix(): pl.pallas_call(functools.partial(scatter_kernel, rows_n, cols_n, steps, p...  34.9 us
    pallas_call x4, Pallas kernels, expand_call(): pl.pallas_call(expand_kernel, out_shape=jax.ShapeDtypeStruct((tokens, siz...  34 us
    pallas_call x2, Pallas kernels, mlp_back_call(): pl.pallas_call(functools.partial(mlp_back_kernel, layer, summed), out_sha...  32.7 us
  transfers between devices with their start and end apart: 77, of which 23 were waited for; matrix products, arithmetic and copies ran while one was open for 12% of the time, Pallas kernels for 31%

profile of v4, /device:TPU:0, one launch (start us, length us, event | category | flops | bytes accessed | tf_op | source)
XLA Modules:
  0.0 722.3 jit_solution(6532342933088801378)
XLA Ops:
  21.8 6.7 collective-permute-done.2.refs_3_
  28.5 5.0 collective-permute-done.refs_1_
  54.2 8.5 %shard_map.223.refs_4_ = bf16[1024,768]{1,0:T(8,128)(2,1)} custom-call(s32[4,3]{1,0:T(4,128)} %convert_element_type.165.present, bf16[1024,768]{1,0:T(8,128)(2,1)} %broadcast_select_fusion.1.patch_ref, s32[1024,1]{1,0:T(8,128)} %copy.185.class_ref, bf16[3,3072,768]{2,1,0:T(8,128)(2,1)} %pinv_ref.9), custom_call_target="tpu_custom_call" | custom-call | flops 1811939328 | bytes 6684672 | tf_op jit(solution)/shard_map/pallas_call | solution.py:379
  74.4 8.5 %shard_map.225.refs_5_ = bf16[1024,768]{1,0:T(8,128)(2,1)} custom-call(s32[4,3]{1,0:T(4,128)} %convert_element_type.165.present, bf16[1024,768]{1,0:T(8,128)(2,1)} %broadcast_select_fusion.1.patch_ref, s32[1024,1]{1,0:T(8,128)} %copy.185.class_ref, bf16[3,3072,768]{2,1,0:T(8,128)(2,1)} %pinv_ref.9), custom_call_target="tpu_custom_call" | custom-call | flops 1811939328 | bytes 6684672 | tf_op jit(solution)/shard_map/pallas_call | solution.py:379
  99.2 8.6 %shard_map.227.refs_5_ = bf16[1024,768]{1,0:T(8,128)(2,1)} custom-call(s32[4,3]{1,0:T(4,128)} %convert_element_type.165.present, bf16[1024,768]{1,0:T(8,128)(2,1)} %broadcast_select_fusion.1.patch_ref, s32[1024,1]{1,0:T(8,128)} %copy.185.class_ref, bf16[3,3072,768]{2,1,0:T(8,128)(2,1)} %pinv_ref.9), custom_call_target="tpu_custom_call" | custom-call | flops 1811939328 | bytes 6684672 | tf_op jit(solution)/shard_map/pallas_call | solution.py:379
  116.1 11.2 %collective-permute-start.25 = (bf16[4112,128]{1,0:T(8,128)(2,1)}, bf16[4112,128]{1,0:T(8,128)(2,1)}, u32[]{:S(2)}, u32[]{:S(2)}) collective-permute-start(bf16[4112,128]{1,0:T(8,128)(2,1)} %get-tuple-element.232), channel_id=1, source_target_pairs={{1,5},{2,6},{5,1},{6,2},{9,13},{10,14},{13,9},{14,10},{17,21},{18,... | collective-permute-start | bytes 3158024 | tf_op jit(solution)/shard_map/ppermute | solution.py:982
  127.3 8.5 %shard_map.229.refs_5_ = bf16[1024,768]{1,0:T(8,128)(2,1)} custom-call(s32[4,3]{1,0:T(4,128)} %convert_element_type.165.present, bf16[1024,768]{1,0:T(8,128)(2,1)} %broadcast_select_fusion.1.patch_ref, s32[1024,1]{1,0:T(8,128)} %copy.185.class_ref, bf16[3,3072,768]{2,1,0:T(8,128)(2,1)} %pinv_ref.9), custom_call_target="tpu_custom_call" | custom-call | flops 1811939328 | bytes 6684672 | tf_op jit(solution)/shard_map/pallas_call | solution.py:379
  135.8 4.2 collective-permute-start.29
  156.0 8.0 %collective-permute-done.28.refs_2_ = bf16[4112,128]{1,0:T(8,128)(2,1)S(1)} collective-permute-done((bf16[4112,128]{1,0:T(8,128)(2,1)}, bf16[4112,128]{1,0:T(8,128)(2,1)S(1)}, u32[]{:S(2)}, u32[]{:S(2)}) %collective-permute-start.28) | collective-permute-done | bytes 1052704 | tf_op jit(solution)/shard_map/ppermute | solution.py:982
  163.9 5.1 collective-permute-done.27.refs_1_
  170.4 4.8 collective-permute-done.31.refs_2_
  175.2 7.1 collective-permute-done.30.refs_1_
  187.9 14.8 %shard_map.234 = (bf16[21504,384]{1,0:T(8,128)(2,1)}, bf16[16,16,128]{2,1,0:T(8,128)(2,1)}) custom-call(s32[16]{0:T(128)} %stack.95.owner, s32[512]{0:T(512)} %broadcast_select_fusion.3.drow, s32[512]{0:T(512)} %get-tuple-element.420.dcol, s32[1]{0:T(128)} %bitcast.26.flag.home, bf16[1,4112,128]{2,1,0:T(8,128)(2,1)} %get-tuple-element.436.refs_0_, ...), custom_call_target="tpu_custom_call" | custom-call | bytes 33030144 | tf_op jit(solution)/shard_map/pallas_call | solution.py:228
  204.2 7.5 %shard_map.235.refs_0_ = bf16[1024,384]{1,0:T(8,128)(2,1)} custom-call(bf16[1024,768]{1,0:T(8,128)(2,1)} %get-tuple-element.213.refs_0_, bf16[1024,768]{1,0:T(8,128)(2,1)} %get-tuple-element.217.refs_1_, bf16[1024,768]{1,0:T(8,128)(2,1)} %get-tuple-element.221.refs_2_, bf16[1024,768]{1,0:T(8,128)(2,1)} %get-tuple-element.225.refs_3_, f32[1,14336]{1,0:T(1,128)} %bitcast.128, ...), custom_call_target="tpu_custom_call" | custom-call | flops 2415919104 | bytes 9437184 | tf_op jit(solution)/shard_map/pallas_call | solution.py:487
  211.7 5.8 collective-permute-start.35
  220.5 7.1 shard_map.236
  227.6 19.5 %shard_map.237 = (bf16[1024,384]{1,0:T(8,128)(2,1)}, f32[8,1024]{1,0:T(8,128)}, bf16[1024,768]{1,0:T(8,128)(2,1)}) custom-call(bf16[1024,384]{1,0:T(8,128)(2,1)} %get-tuple-element.255.q_ref, bf16[1024,384]{1,0:T(8,128)(2,1)} %get-tuple-element.256.k_ref, bf16[1024,384]{1,0:T(8,128)(2,1)} %get-tuple-element.257.v_ref, s32[1024,1]{1,0:T(8,128)} %copy.186.seg_q.seg_k, ...), custom_call_target="tpu_custom_call" | custom-call | flops 6442450944 | bytes 6291456 | tf_op jit(solution)/shard_map/pallas_call | solution.py:579
  251.9 13.6 %shard_map.238 = (f32[1024,768]{1,0:T(8,128)}, bf16[1024,768]{1,0:T(8,128)(2,1)}, bf16[1024,1536]{1,0:T(8,128)(2,1)}, bf16[1024,1536]{1,0:T(8,128)(2,1)}, bf16[1024,768]{1,0:T(8,128)(2,1)}) custom-call(f32[1024,768]{1,0:T(8,128)} %get-tuple-element.254.base.hid, bf16[1024,768]{1,0:T(8,128)(2,1)} %get-tuple-element.258.own, bf16[1024,768]{1,0:T(8,128)(2,1)} %copy-done.48, ...), custom_call_target="tpu_custom_call" | custom-call | flops 4831838208 | bytes 18874368 | tf_op jit(solution)/shard_map/pallas_call | solution.py:637
  270.3 7.9 %shard_map.239 = (f32[1024,768]{1,0:T(8,128)}, bf16[1024,768]{1,0:T(8,128)(2,1)}, bf16[1024,384]{1,0:T(8,128)(2,1)}, bf16[1024,384]{1,0:T(8,128)(2,1)}, bf16[1024,384]{1,0:T(8,128)(2,1)}) custom-call(s32[1]{0:T(128)} %bitcast.7.core, f32[1024,768]{1,0:T(8,128)} %get-tuple-element.259.refs_0_.refs_3_, bf16[1024,768]{1,0:T(8,128)(2,1)} %get-tuple-element.260.refs_1_, ...), custom_call_target="tpu_custom_call" | custom-call | flops 1811939328 | bytes 11010048 | tf_op jit(solution)/shard_map/pallas_call | solution.py:524
  278.2 19.5 %shard_map.240 = (bf16[1024,384]{1,0:T(8,128)(2,1)}, f32[8,1024]{1,0:T(8,128)}, bf16[1024,768]{1,0:T(8,128)(2,1)}) custom-call(bf16[1024,384]{1,0:T(8,128)(2,1)} %get-tuple-element.262.q_ref, bf16[1024,384]{1,0:T(8,128)(2,1)} %get-tuple-element.263.k_ref, bf16[1024,384]{1,0:T(8,128)(2,1)} %get-tuple-element.264.v_ref, s32[1024,1]{1,0:T(8,128)} %copy.186.seg_q.seg_k, ...), custom_call_target="tpu_custom_call" | custom-call | flops 6442450944 | bytes 6291456 | tf_op jit(solution)/shard_map/pallas_call | solution.py:579
  302.5 13.6 %shard_map.241 = (f32[1024,768]{1,0:T(8,128)}, bf16[1024,768]{1,0:T(8,128)(2,1)}, bf16[1024,1536]{1,0:T(8,128)(2,1)}, bf16[1024,1536]{1,0:T(8,128)(2,1)}, bf16[1024,768]{1,0:T(8,128)(2,1)}) custom-call(f32[1024,768]{1,0:T(8,128)} %get-tuple-element.261.base.hid, bf16[1024,768]{1,0:T(8,128)(2,1)} %get-tuple-element.265.own, bf16[1024,768]{1,0:T(8,128)(2,1)} %copy-done.47, ...), custom_call_target="tpu_custom_call" | custom-call | flops 4831838208 | bytes 18874368 | tf_op jit(solution)/shard_map/pallas_call | solution.py:637
  316.1 16.0 %shard_map.242 = (bf16[1024,768]{1,0:T(8,128)(2,1)}, bf16[1024,1536]{1,0:T(8,128)(2,1)}, bf16[1024,768]{1,0:T(8,128)(2,1)}, f32[1,768]{1,0:T(1,128)}, f32[1,768]...) custom-call(bf16[1024,768]{1,0:T(8,128)(2,1)} %broadcast_select_fusion.refs_0_, ...), custom_call_target="tpu_custom_call" | custom-call | flops 4831838208 | bytes 18874368 | tf_op jit(solution)/shard_map/pallas_call | solution.py:694
  332.5 5.5 convolution_convert_fusion.3.refs_2_
  338.0 4.1 convolution_convert_fusion.2.refs_3_
  346.7 29.9 %shard_map.244 = (f32[1024,768]{1,0:T(8,128)}, bf16[1024,768]{1,0:T(8,128)(2,1)}, bf16[1024,384]{1,0:T(8,128)(2,1)}, bf16[1024,384]{1,0:T(8,128)(2,1)}, bf16[1024,384]{1,0:T(8,128)(2,1)}, /*index=5*/f32[1,768]{1,0:T(1,128)}) custom-call(s32[4]{0:T(128)} %get-tuple-element.450.low_ref, s32[4]{0:T(128)} %get-tuple-element.449.high_ref, ...), custom_call_target="tpu_custom_call" | custom-call | flops 11274289152 | bytes 15728640 | tf_op jit(solution)/shard_map/pallas_call | solution.py:789
  376.6 7.9 %shard_map.246 = (bf16[1024,768]{1,0:T(8,128)(2,1)}, f32[1,768]{1,0:T(1,128)}, f32[1,768]{1,0:T(1,128)}, f32[1,384]{1,0:T(1,128)}, f32[1,384]{1,0:T(1,128)}) custom-call(bf16[1024,384]{1,0:T(8,128)(2,1)} %get-tuple-element.282.dq, bf16[1024,384]{1,0:T(8,128)(2,1)} %get-tuple-element.283.dk, bf16[1024,384]{1,0:T(8,128)(2,1)} %get-tuple-element.284.dv, ...), custom_call_target="tpu_custom_call" | custom-call | flops 1811939328 | bytes 7864320 | tf_op jit(solution)/shard_map/pallas_call | solution.py:853
  384.5 4.6 collective-permute-start.41
  393.0 4.9 convolution_convert_fusion.5.refs_4_
  397.9 16.7 %shard_map.247 = (f32[1024,768]{1,0:T(8,128)}, bf16[1024,768]{1,0:T(8,128)(2,1)}, bf16[1024,1536]{1,0:T(8,128)(2,1)}, bf16[1024,768]{1,0:T(8,128)(2,1)}, f32[1,7...) custom-call(f32[1024,768]{1,0:T(8,128)} %get-tuple-element.277.refs_0_, ...), custom_call_target="tpu_custom_call" | custom-call | flops 4831838208 | bytes 18874368 | tf_op jit(solution)/shard_map/pallas_call | solution.py:694
  416.8 4.5 shard_map.251.refs_1_
  423.8 6.0 convolution_convert_fusion.1.refs_2_
  429.8 4.9 shard_map.252.refs_8_
  434.7 4.0 convolution_convert_fusion.refs_3_
  446.7 29.9 %shard_map.250 = (f32[1024,768]{1,0:T(8,128)}, bf16[1024,768]{1,0:T(8,128)(2,1)}, bf16[1024,384]{1,0:T(8,128)(2,1)}, bf16[1024,384]{1,0:T(8,128)(2,1)}, bf16[1024,384]{1,0:T(8,128)(2,1)}, /*index=5*/f32[1,768]{1,0:T(1,128)}) custom-call(s32[4]{0:T(128)} %get-tuple-element.450.low_ref, s32[4]{0:T(128)} %get-tuple-element.449.high_ref, ...), custom_call_target="tpu_custom_call" | custom-call | flops 11274289152 | bytes 15728640 | tf_op jit(solution)/shard_map/pallas_call | solution.py:789
  484.0 8.0 %shard_map.255 = (bf16[1024,768]{1,0:T(8,128)(2,1)}, f32[1,768]{1,0:T(1,128)}, f32[1,768]{1,0:T(1,128)}, f32[1,384]{1,0:T(1,128)}, f32[1,384]{1,0:T(1,128)}) custom-call(bf16[1024,384]{1,0:T(8,128)(2,1)} %get-tuple-element.320.dq, bf16[1024,384]{1,0:T(8,128)(2,1)} %get-tuple-element.321.dk, bf16[1024,384]{1,0:T(8,128)(2,1)} %get-tuple-element.322.dv, ...), custom_call_target="tpu_custom_call" | custom-call | flops 1811939328 | bytes 7864320 | tf_op jit(solution)/shard_map/pallas_call | solution.py:853
  492.0 6.3 collective-permute-start.49
  504.6 4.9 convolution_convert_fusion.4.refs_2_
  509.5 4.0 shard_map.257
  534.8 15.5 %collective-permute-start.58 = (bf16[1024,768]{1,0:T(8,128)(2,1)}, bf16[1024,768]{1,0:T(8,128)(2,1)}, u32[]{:S(2)}, u32[]{:S(2)}) collective-permute-start(bf16[1024,768]{1,0:T(8,128)(2,1)} %get-tuple-element.369), channel_id=1, source_target_pairs={{0,2},{1,3},{2,0},{3,1},{4,6},{5,7},{6,4},{7,5},{8,10},{9,11},{10,... | collective-permute-start | bytes 4718600 | tf_op jit(solution)/shard_map/ppermute | solution.py:982
  559.3 4.1 shard_map.262.refs_1_
  563.5 4.1 shard_map.263.refs_5_
  582.6 3.7 shard_map.268.refs_1_
  586.2 4.3 collective-permute-done.57.refs_0_
  590.6 4.2 shard_map.270.refs_0_.refs_2_.refs_3_
  603.5 11.2 %shard_map.271.refs_2_ = bf16[3,384,768]{2,1,0:T(8,128)(2,1)} custom-call(bf16[21504,384]{1,0:T(8,128)(2,1)} %get-tuple-element.375.base, bf16[3,3072,768]{2,1,0:T(8,128)(2,1)} %pinv_ref.9), custom_call_target="tpu_custom_call" | custom-call | flops 5435817984 | bytes 14155776 | tf_op jit(solution)/shard_map/pallas_call | solution.py:407
  632.2 3.7 collective-permute-start.66
  641.2 3.7 shard_map.278
  711.1 11.0 %shard_map.288 = (f32[32,128,128]{2,1,0:T(8,128)}, f32[32,128,128]{2,1,0:T(8,128)}, f32[32,128,128]{2,1,0:T(8,128)}, f32[32,128,128]{2,1,0:T(8,128)}) custom-call(s32[32]{0:T(128)} %convert_element_type.208.used, s32[1]{0:T(128)} %bitcast.26.flag.home, bf16[4112,128]{1,0:T(8,128)(2,1)} %shard_map.286.near, bf16[4112,128]{1,0:T(8,128)(2,1)} %collective-permute-done.76.far, ...), custom_call_target="tpu_custom_call" | custom-call | flops 5905580032 | bytes 19922944 | tf_op jit(solution)/shard_map/pallas_call | solution.py:914
  (413 shorter events, 297.0 us)
Async XLA Ops:
  0.6 19.6 %collective-permute-start.3 = (s32[1,504]{1,0:T(1,128)}, s32[1,504]{1,0:T(1,128)S(1)}, u32[]{:S(2)}, u32[]{:S(2)}) collective-permute-start(s32[1,504]{1,0:T(1,128)} %param.18), channel_id=1, source_target_pairs={{0,1},{1,0},{2,3},{3,2},{4,5},{5,4},{6,7},{7,6},{8,9},{9,8},{10,11... | collective-permute-start | bytes 6056 | tf_op jit(solution)/shard_map/ppermute | solution.py:982
  3.7 41.6 %collective-permute-start.9 = (bf16[1024,768]{1,0:T(8,128)(2,1)}, bf16[1024,768]{1,0:T(8,128)(2,1)}, u32[]{:S(2)}, u32[]{:S(2)}) collective-permute-start(bf16[1024,768]{1,0:T(8,128)(2,1)} %param.15), channel_id=1, source_target_pairs={{0,2},{3,1},{4,6},{7,5},{8,10},{11,9},{12,14},{15,13},{16,18},{19,... | collective-permute-start | bytes 4718600 | tf_op jit(solution)/shard_map/ppermute | solution.py:982
  34.5 35.5 %collective-permute-start.13 = (bf16[4112,128]{1,0:T(8,128)(2,1)}, bf16[4112,128]{1,0:T(8,128)(2,1)S(1)}, u32[]{:S(2)}, u32[]{:S(2)}) collective-permute-start(bf16[4112,128]{1,0:T(8,128)(2,1)} %get-tuple-element.216), channel_id=1, source_target_pairs={{0,1},{3,2},{4,5},{7,6},{8,9},{11,10},{12,13},{15,14},{16,17},{19,... | collective-permute-start | bytes 3158024 | tf_op jit(solution)/shard_map/ppermute | solution.py:982
  35.9 26.7 %collective-permute-start.7 = (bf16[4112,128]{1,0:T(8,128)(2,1)}, bf16[4112,128]{1,0:T(8,128)(2,1)S(1)}, u32[]{:S(2)}, u32[]{:S(2)}) collective-permute-start(bf16[4112,128]{1,0:T(8,128)(2,1)} %collective-permute-done.4), channel_id=1, source_target_pairs={{0,8},{3,11},{4,12},{7,15},{8,16},{11,19},{12,20},{15,23},{16,24},... | collective-permute-start | bytes 3158024 | tf_op jit(solution)/shard_map/ppermute | solution.py:982
  39.4 25.5 %collective-permute-start.6 = (bf16[4112,128]{1,0:T(8,128)(2,1)}, bf16[4112,128]{1,0:T(8,128)(2,1)}, u32[]{:S(2)}, u32[]{:S(2)}) collective-permute-start(bf16[4112,128]{1,0:T(8,128)(2,1)} %collective-permute-done.4), channel_id=1, source_target_pairs={{0,1},{3,2},{4,5},{7,6},{8,9},{11,10},{12,13},{15,14},{16,17},{19,... | collective-permute-start | bytes 3158024 | tf_op jit(solution)/shard_map/ppermute | solution.py:982
  41.7 26.5 %collective-permute-start.5 = (bf16[4112,128]{1,0:T(8,128)(2,1)}, bf16[4112,128]{1,0:T(8,128)(2,1)}, u32[]{:S(2)}, u32[]{:S(2)}) collective-permute-start(bf16[4112,128]{1,0:T(8,128)(2,1)} %collective-permute-done.4), channel_id=1, source_target_pairs={{0,4},{3,7},{4,0},{7,3},{8,12},{11,15},{12,8},{15,11},{16,20},{19,... | collective-permute-start | bytes 3158024 | tf_op jit(solution)/shard_map/ppermute | solution.py:982
  45.3 26.8 %collective-permute-start.14 = (bf16[4112,128]{1,0:T(8,128)(2,1)}, bf16[4112,128]{1,0:T(8,128)(2,1)S(1)}, u32[]{:S(2)}, u32[]{:S(2)}) collective-permute-start(bf16[4112,128]{1,0:T(8,128)(2,1)} %get-tuple-element.215), channel_id=1, source_target_pairs={{0,8},{3,11},{4,12},{7,15},{8,16},{11,19},{12,20},{15,23},{16,24},... | collective-permute-start | bytes 3158024 | tf_op jit(solution)/shard_map/ppermute | solution.py:982
  62.6 20.3 %collective-permute-start.12 = (bf16[4112,128]{1,0:T(8,128)(2,1)}, bf16[4112,128]{1,0:T(8,128)(2,1)}, u32[]{:S(2)}, u32[]{:S(2)}) collective-permute-start(bf16[4112,128]{1,0:T(8,128)(2,1)} %get-tuple-element.215), channel_id=1, source_target_pairs={{0,1},{3,2},{4,5},{7,6},{8,9},{11,10},{12,13},{15,14},{16,17},{19,... | collective-permute-start | bytes 3158024 | tf_op jit(solution)/shard_map/ppermute | solution.py:982
  64.9 23.7 %collective-permute-start.11 = (bf16[4112,128]{1,0:T(8,128)(2,1)}, bf16[4112,128]{1,0:T(8,128)(2,1)}, u32[]{:S(2)}, u32[]{:S(2)}) collective-permute-start(bf16[4112,128]{1,0:T(8,128)(2,1)} %get-tuple-element.215), channel_id=1, source_target_pairs={{0,4},{3,7},{4,0},{7,3},{8,12},{11,15},{12,8},{15,11},{16,20},{19,... | collective-permute-start | bytes 3158024 | tf_op jit(solution)/shard_map/ppermute | solution.py:982
  68.3 21.6 %collective-permute-start.17 = (bf16[4112,128]{1,0:T(8,128)(2,1)}, bf16[4112,128]{1,0:T(8,128)(2,1)}, u32[]{:S(2)}, u32[]{:S(2)}) collective-permute-start(bf16[4112,128]{1,0:T(8,128)(2,1)} %get-tuple-element.220), channel_id=1, source_target_pairs={{1,5},{2,6},{5,1},{6,2},{9,13},{10,14},{13,9},{14,10},{17,21},{18,... | collective-permute-start | bytes 3158024 | tf_op jit(solution)/shard_map/ppermute | solution.py:982
  70.0 23.4 %collective-permute-start.18 = (bf16[4112,128]{1,0:T(8,128)(2,1)}, bf16[4112,128]{1,0:T(8,128)(2,1)}, u32[]{:S(2)}, u32[]{:S(2)}) collective-permute-start(bf16[4112,128]{1,0:T(8,128)(2,1)} %get-tuple-element.219), channel_id=1, source_target_pairs={{0,8},{3,11},{4,12},{7,15},{8,16},{11,19},{12,20},{15,23},{16,24},... | collective-permute-start | bytes 3158024 | tf_op jit(solution)/shard_map/ppermute | solution.py:982
  72.1 23.7 %collective-permute-start.16 = (bf16[4112,128]{1,0:T(8,128)(2,1)}, bf16[4112,128]{1,0:T(8,128)(2,1)}, u32[]{:S(2)}, u32[]{:S(2)}) collective-permute-start(bf16[4112,128]{1,0:T(8,128)(2,1)} %get-tuple-element.219), channel_id=1, source_target_pairs={{0,1},{3,2},{4,5},{7,6},{8,9},{11,10},{12,13},{15,14},{16,17},{19,... | collective-permute-start | bytes 3158024 | tf_op jit(solution)/shard_map/ppermute | solution.py:982
  82.9 24.9 %collective-permute-start.15 = (bf16[4112,128]{1,0:T(8,128)(2,1)S(1)}, bf16[4112,128]{1,0:T(8,128)(2,1)}, u32[]{:S(2)}, u32[]{:S(2)}) collective-permute-start(bf16[4112,128]{1,0:T(8,128)(2,1)S(1)} %copy-done.28), channel_id=1, source_target_pairs={{0,4},{3,7},{4,0},{7,3},{8,12},{11,15},{12,8},{15,11},{16,20},{19,... | collective-permute-start | bytes 3158024 | tf_op jit(solution)/shard_map/ppermute | solution.py:982
  88.6 22.8 %collective-permute-start.21 = (bf16[4112,128]{1,0:T(8,128)(2,1)}, bf16[4112,128]{1,0:T(8,128)(2,1)S(1)}, u32[]{:S(2)}, u32[]{:S(2)}) collective-permute-start(bf16[4112,128]{1,0:T(8,128)(2,1)} %get-tuple-element.224), channel_id=1, source_target_pairs={{0,1},{3,2},{4,5},{7,6},{8,9},{11,10},{12,13},{15,14},{16,17},{19,... | collective-permute-start | bytes 3158024 | tf_op jit(solution)/shard_map/ppermute | solution.py:982
  89.9 23.8 %collective-permute-start.22 = (bf16[4112,128]{1,0:T(8,128)(2,1)}, bf16[4112,128]{1,0:T(8,128)(2,1)S(1)}, u32[]{:S(2)}, u32[]{:S(2)}) collective-permute-start(bf16[4112,128]{1,0:T(8,128)(2,1)} %get-tuple-element.223), channel_id=1, source_target_pairs={{0,8},{3,11},{4,12},{7,15},{8,16},{11,19},{12,20},{15,23},{16,24},... | collective-permute-start | bytes 3158024 | tf_op jit(solution)/shard_map/ppermute | solution.py:982
  93.4 22.7 %collective-permute-start.20 = (bf16[4112,128]{1,0:T(8,128)(2,1)}, bf16[4112,128]{1,0:T(8,128)(2,1)}, u32[]{:S(2)}, u32[]{:S(2)}) collective-permute-start(bf16[4112,128]{1,0:T(8,128)(2,1)} %get-tuple-element.223), channel_id=1, source_target_pairs={{0,1},{3,2},{4,5},{7,6},{8,9},{11,10},{12,13},{15,14},{16,17},{19,... | collective-permute-start | bytes 3158024 | tf_op jit(solution)/shard_map/ppermute | solution.py:982
  95.8 40.0 %collective-permute-start.19 = (bf16[4112,128]{1,0:T(8,128)(2,1)}, bf16[4112,128]{1,0:T(8,128)(2,1)}, u32[]{:S(2)}, u32[]{:S(2)}) collective-permute-start(bf16[4112,128]{1,0:T(8,128)(2,1)} %get-tuple-element.223), channel_id=1, source_target_pairs={{0,4},{3,7},{4,0},{7,3},{8,12},{11,15},{12,8},{15,11},{16,20},{19,... | collective-permute-start | bytes 3158024 | tf_op jit(solution)/shard_map/ppermute | solution.py:982
  107.8 34.2 %collective-permute-start.26 = (bf16[4112,128]{1,0:T(8,128)(2,1)}, bf16[4112,128]{1,0:T(8,128)(2,1)S(1)}, u32[]{:S(2)}, u32[]{:S(2)}) collective-permute-start(bf16[4112,128]{1,0:T(8,128)(2,1)} %get-tuple-element.229), channel_id=1, source_target_pairs={{0,8},{3,11},{4,12},{7,15},{8,16},{11,19},{12,20},{15,23},{16,24},... | collective-permute-start | bytes 3158024 | tf_op jit(solution)/shard_map/ppermute | solution.py:982
  111.4 34.3 %collective-permute-start.24 = (bf16[4112,128]{1,0:T(8,128)(2,1)}, bf16[4112,128]{1,0:T(8,128)(2,1)}, u32[]{:S(2)}, u32[]{:S(2)}) collective-permute-start(bf16[4112,128]{1,0:T(8,128)(2,1)} %get-tuple-element.229), channel_id=1, source_target_pairs={{0,1},{3,2},{4,5},{7,6},{8,9},{11,10},{12,13},{15,14},{16,17},{19,... | collective-permute-start | bytes 3158024 | tf_op jit(solution)/shard_map/ppermute | solution.py:982
  113.7 32.0 %collective-permute-start.23 = (bf16[4112,128]{1,0:T(8,128)(2,1)}, bf16[4112,128]{1,0:T(8,128)(2,1)}, u32[]{:S(2)}, u32[]{:S(2)}) collective-permute-start(bf16[4112,128]{1,0:T(8,128)(2,1)} %get-tuple-element.229), channel_id=1, source_target_pairs={{0,4},{3,7},{4,0},{7,3},{8,12},{11,15},{12,8},{15,11},{16,20},{19,... | collective-permute-start | bytes 3158024 | tf_op jit(solution)/shard_map/ppermute | solution.py:982
  116.1 23.9 %collective-permute-start.25 = (bf16[4112,128]{1,0:T(8,128)(2,1)}, bf16[4112,128]{1,0:T(8,128)(2,1)}, u32[]{:S(2)}, u32[]{:S(2)}) collective-permute-start(bf16[4112,128]{1,0:T(8,128)(2,1)} %get-tuple-element.232), channel_id=1, source_target_pairs={{1,5},{2,6},{5,1},{6,2},{9,13},{10,14},{13,9},{14,10},{17,21},{18,... | collective-permute-start | bytes 3158024 | tf_op jit(solution)/shard_map/ppermute | solution.py:982
  140.1 23.9 %collective-permute-start.28 = (bf16[4112,128]{1,0:T(8,128)(2,1)}, bf16[4112,128]{1,0:T(8,128)(2,1)S(1)}, u32[]{:S(2)}, u32[]{:S(2)}) collective-permute-start(bf16[4112,128]{1,0:T(8,128)(2,1)} %get-tuple-element.234), channel_id=1, source_target_pairs={{0,1},{3,2},{4,5},{7,6},{8,9},{11,10},{12,13},{15,14},{16,17},{19,... | collective-permute-start | bytes 3158024 | tf_op jit(solution)/shard_map/ppermute | solution.py:982
  142.0 27.0 %collective-permute-start.27 = (bf16[4112,128]{1,0:T(8,128)(2,1)}, bf16[4112,128]{1,0:T(8,128)(2,1)}, u32[]{:S(2)}, u32[]{:S(2)}) collective-permute-start(bf16[4112,128]{1,0:T(8,128)(2,1)} %get-tuple-element.234), channel_id=1, source_target_pairs={{0,4},{3,7},{4,0},{7,3},{8,12},{11,15},{12,8},{15,11},{16,20},{19,... | collective-permute-start | bytes 3158024 | tf_op jit(solution)/shard_map/ppermute | solution.py:982
  145.7 24.7 %collective-permute-start.32 = (bf16[4112,128]{1,0:T(8,128)(2,1)}, bf16[4112,128]{1,0:T(8,128)(2,1)S(1)}, u32[]{:S(2)}, u32[]{:S(2)}) collective-permute-start(bf16[4112,128]{1,0:T(8,128)(2,1)} %get-tuple-element.239), channel_id=1, source_target_pairs={{1,5},{2,6},{5,1},{6,2},{9,13},{10,14},{13,9},{14,10},{17,21},{18,... | collective-permute-start | bytes 3158024 | tf_op jit(solution)/shard_map/ppermute | solution.py:982
  146.5 28.7 %collective-permute-start.31 = (bf16[4112,128]{1,0:T(8,128)(2,1)}, bf16[4112,128]{1,0:T(8,128)(2,1)}, u32[]{:S(2)}, u32[]{:S(2)}) collective-permute-start(bf16[4112,128]{1,0:T(8,128)(2,1)} %get-tuple-element.235), channel_id=1, source_target_pairs={{0,1},{3,2},{4,5},{7,6},{8,9},{11,10},{12,13},{15,14},{16,17},{19,... | collective-permute-start | bytes 3158024 | tf_op jit(solution)/shard_map/ppermute | solution.py:982
  152.7 29.7 %collective-permute-start.30 = (bf16[4112,128]{1,0:T(8,128)(2,1)}, bf16[4112,128]{1,0:T(8,128)(2,1)}, u32[]{:S(2)}, u32[]{:S(2)}) collective-permute-start(bf16[4112,128]{1,0:T(8,128)(2,1)} %get-tuple-element.235), channel_id=1, source_target_pairs={{0,4},{3,7},{4,0},{7,3},{8,12},{11,15},{12,8},{15,11},{16,20},{19,... | collective-permute-start | bytes 3158024 | tf_op jit(solution)/shard_map/ppermute | solution.py:982
  265.9 33.1 %collective-permute-start.10 = (bf16[1024,768]{1,0:T(8,128)(2,1)S(1)}, bf16[1024,768]{1,0:T(8,128)(2,1)S(1)}, u32[]{:S(2)}, u32[]{:S(2)}) collective-permute-start(bf16[1024,768]{1,0:T(8,128)(2,1)S(1)} %copy-done.49), channel_id=1, source_target_pairs={{0,2},{3,1},{4,6},{7,5},{8,10},{11,9},{12,14},{15,13},{16,18},{19,... | collective-permute-start | bytes 4718600 | tf_op jit(solution)/shard_map/ppermute | solution.py:982
  343.3 33.3 %collective-permute-start.40 = (bf16[1536,768]{1,0:T(8,128)(2,1)}, bf16[1536,768]{1,0:T(8,128)(2,1)}, u32[]{:S(2)}, u32[]{:S(2)}) collective-permute-start(bf16[1536,768]{1,0:T(8,128)(2,1)} %get-tuple-element.281.own), channel_id=1, source_target_pairs={{1,0},{2,3},{5,4},{6,7},{9,8},{10,11},{13,12},{14,15},{17,16},{18,... | collective-permute-start | bytes 7077896 | tf_op jit(solution)/shard_map/ppermute | solution.py:982
  345.4 69.2 %collective-permute-start.42 = (bf16[768,1536]{1,0:T(8,128)(2,1)}, bf16[768,1536]{1,0:T(8,128)(2,1)S(1)}, u32[]{:S(2)}, u32[]{:S(2)}) collective-permute-start(bf16[768,1536]{1,0:T(8,128)(2,1)} %get-tuple-element.290.own), channel_id=1, source_target_pairs={{1,0},{2,3},{5,4},{6,7},{9,8},{10,11},{13,12},{14,15},{17,16},{18,... | collective-permute-start | bytes 7077896 | tf_op jit(solution)/shard_map/ppermute | solution.py:982
  416.1 22.6 %collective-permute-start.43 = (bf16[1024,768]{1,0:T(8,128)(2,1)}, bf16[1024,768]{1,0:T(8,128)(2,1)}, u32[]{:S(2)}, u32[]{:S(2)}) collective-permute-start(bf16[1024,768]{1,0:T(8,128)(2,1)} %get-tuple-element.293.refs_0_), channel_id=1, source_target_pairs={{0,2},{1,3},{2,0},{3,1},{4,6},{5,7},{6,4},{7,5},{8,10},{9,11},{10,... | collective-permute-start | bytes 4718600 | tf_op jit(solution)/shard_map/ppermute | solution.py:982
  441.3 35.3 %collective-permute-start.48 = (bf16[384,1536]{1,0:T(8,128)(2,1)S(1)}, bf16[384,1536]{1,0:T(8,128)(2,1)S(1)}, u32[]{:S(2)}, u32[]{:S(2)}) collective-permute-start(bf16[384,1536]{1,0:T(8,128)(2,1)S(1)} %constant_dynamic-slice_fusion.2), channel_id=1, source_target_pairs={{1,5},{2,6},{5,1},{6,2},{9,13},{10,14},{13,9},{14,10},{17,21},{18,... | collective-permute-start | bytes 3538952 | tf_op jit(solution)/shard_map/ppermute | solution.py:982
  442.3 35.2 %collective-permute-start.47 = (bf16[768,768]{1,0:T(8,128)(2,1)S(1)}, bf16[768,768]{1,0:T(8,128)(2,1)}, u32[]{:S(2)}, u32[]{:S(2)}) collective-permute-start(bf16[768,768]{1,0:T(8,128)(2,1)S(1)} %constant_dynamic-slice_fusion.3), channel_id=1, source_target_pairs={{1,5},{2,6},{5,1},{6,2},{9,13},{10,14},{13,9},{14,10},{17,21},{18,... | collective-permute-start | bytes 3538952 | tf_op jit(solution)/shard_map/ppermute | solution.py:982
  445.4 31.2 %collective-permute-start.46 = (bf16[384,1152]{1,0:T(8,128)(2,1)S(1)}, bf16[384,1152]{1,0:T(8,128)(2,1)S(1)}, u32[]{:S(2)}, u32[]{:S(2)}) collective-permute-start(bf16[384,1152]{1,0:T(8,128)(2,1)S(1)} %add_convert_fusion.5), channel_id=1, source_target_pairs={{1,0},{2,3},{5,4},{6,7},{9,8},{10,11},{13,12},{14,15},{17,16},{18,... | collective-permute-start | bytes 2654216 | tf_op jit(solution)/shard_map/ppermute | solution.py:982
  498.3 36.5 %collective-permute-start.55 = (bf16[384,1536]{1,0:T(8,128)(2,1)S(1)}, bf16[384,1536]{1,0:T(8,128)(2,1)}, u32[]{:S(2)}, u32[]{:S(2)}) collective-permute-start(bf16[384,1536]{1,0:T(8,128)(2,1)S(1)} %copy-done.22), channel_id=1, source_target_pairs={{1,0},{2,3},{5,4},{6,7},{9,8},{10,11},{13,12},{14,15},{17,16},{18,... | collective-permute-start | bytes 3538952 | tf_op jit(solution)/shard_map/ppermute | solution.py:982
  499.6 51.3 %collective-permute-start.56 = (bf16[768,768]{1,0:T(8,128)(2,1)}, bf16[768,768]{1,0:T(8,128)(2,1)}, u32[]{:S(2)}, u32[]{:S(2)}) collective-permute-start(bf16[768,768]{1,0:T(8,128)(2,1)} %get-tuple-element.355), channel_id=1, source_target_pairs={{1,0},{2,3},{5,4},{6,7},{9,8},{10,11},{13,12},{14,15},{17,16},{18,... | collective-permute-start | bytes 3538952 | tf_op jit(solution)/shard_map/ppermute | solution.py:982
  528.0 39.8 %collective-permute-start.51 = (bf16[1536,384]{1,0:T(8,128)(2,1)}, bf16[1536,384]{1,0:T(8,128)(2,1)}, u32[]{:S(2)}, u32[]{:S(2)}) collective-permute-start(bf16[1536,384]{1,0:T(8,128)(2,1)} %constant_dynamic-slice_fusion), channel_id=1, source_target_pairs={{1,5},{2,6},{5,1},{6,2},{9,13},{10,14},{13,9},{14,10},{17,21},{18,... | collective-permute-start | bytes 3538952 | tf_op jit(solution)/shard_map/ppermute | solution.py:982
  532.2 35.6 %collective-permute-start.52 = (bf16[384,1152]{1,0:T(8,128)(2,1)}, bf16[384,1152]{1,0:T(8,128)(2,1)S(1)}, u32[]{:S(2)}, u32[]{:S(2)}) collective-permute-start(bf16[384,1152]{1,0:T(8,128)(2,1)} %add_convert_fusion.4), channel_id=1, source_target_pairs={{1,0},{2,3},{5,4},{6,7},{9,8},{10,11},{13,12},{14,15},{17,16},{18,... | collective-permute-start | bytes 2654216 | tf_op jit(solution)/shard_map/ppermute | solution.py:982
  533.5 34.3 %collective-permute-start.53 = (bf16[384,768]{1,0:T(8,128)(2,1)S(1)}, bf16[384,768]{1,0:T(8,128)(2,1)S(1)}, u32[]{:S(2)}, u32[]{:S(2)}) collective-permute-start(bf16[384,768]{1,0:T(8,128)(2,1)S(1)} %copy-done.19), channel_id=1, source_target_pairs={{1,0},{2,3},{5,4},{6,7},{9,8},{10,11},{13,12},{14,15},{17,16},{18,... | collective-permute-start | bytes 1769480 | tf_op jit(solution)/shard_map/ppermute | solution.py:982
  534.8 38.6 %collective-permute-start.58 = (bf16[1024,768]{1,0:T(8,128)(2,1)}, bf16[1024,768]{1,0:T(8,128)(2,1)}, u32[]{:S(2)}, u32[]{:S(2)}) collective-permute-start(bf16[1024,768]{1,0:T(8,128)(2,1)} %get-tuple-element.369), channel_id=1, source_target_pairs={{0,2},{1,3},{2,0},{3,1},{4,6},{5,7},{6,4},{7,5},{8,10},{9,11},{10,... | collective-permute-start | bytes 4718600 | tf_op jit(solution)/shard_map/ppermute | solution.py:982
  600.8 28.1 %collective-permute-start.63 = (bf16[4112,128]{1,0:T(8,128)(2,1)}, bf16[4112,128]{1,0:T(8,128)(2,1)}, u32[]{:S(2)}, u32[]{:S(2)}) collective-permute-start(bf16[4112,128]{1,0:T(8,128)(2,1)} %get-tuple-element.434), channel_id=1, source_target_pairs={{0,4},{3,7},{4,0},{7,3},{8,12},{11,15},{12,8},{15,11},{16,20},{19,... | collective-permute-start | bytes 3158024 | tf_op jit(solution)/shard_map/ppermute | solution.py:982
  628.8 44.4 %collective-permute-start.61 = (bf16[1024,768]{1,0:T(8,128)(2,1)S(1)}, bf16[1024,768]{1,0:T(8,128)(2,1)}, u32[]{:S(2)}, u32[]{:S(2)}) collective-permute-start(bf16[1024,768]{1,0:T(8,128)(2,1)S(1)} %add_convert_fusion), channel_id=1, source_target_pairs={{0,2},{1,3},{2,0},{3,1},{4,6},{5,7},{6,4},{7,5},{8,10},{9,11},{10,... | collective-permute-start | bytes 4718600 | tf_op jit(solution)/shard_map/ppermute | solution.py:982
  635.9 18.9 %collective-permute-start.67 = (bf16[4112,128]{1,0:T(8,128)(2,1)}, bf16[4112,128]{1,0:T(8,128)(2,1)}, u32[]{:S(2)}, u32[]{:S(2)}) collective-permute-start(bf16[4112,128]{1,0:T(8,128)(2,1)} %get-tuple-element.385), channel_id=1, source_target_pairs={{0,8},{3,11},{4,12},{7,15},{8,16},{11,19},{12,20},{15,23},{16,24},... | collective-permute-start | bytes 3158024 | tf_op jit(solution)/shard_map/ppermute | solution.py:982
  647.4 18.9 %collective-permute-start.69 = (bf16[4112,128]{1,0:T(8,128)(2,1)}, bf16[4112,128]{1,0:T(8,128)(2,1)}, u32[]{:S(2)}, u32[]{:S(2)}) collective-permute-start(bf16[4112,128]{1,0:T(8,128)(2,1)} %get-tuple-element.390), channel_id=1, source_target_pairs={{0,8},{3,11},{4,12},{7,15},{8,16},{11,19},{12,20},{15,23},{16,24},... | collective-permute-start | bytes 3158024 | tf_op jit(solution)/shard_map/ppermute | solution.py:982
  650.2 48.5 %collective-permute-start.59 = (bf16[1024,768]{1,0:T(8,128)(2,1)S(1)}, bf16[1024,768]{1,0:T(8,128)(2,1)}, u32[]{:S(2)}, u32[]{:S(2)}) collective-permute-start(bf16[1024,768]{1,0:T(8,128)(2,1)S(1)} %copy-done.8), channel_id=1, source_target_pairs={{0,1},{3,2},{4,5},{7,6},{8,9},{11,10},{12,13},{15,14},{16,17},{19,... | collective-permute-start | bytes 4718600 | tf_op jit(solution)/shard_map/ppermute | solution.py:982
  658.3 19.5 %collective-permute-start.70 = (bf16[4112,128]{1,0:T(8,128)(2,1)}, bf16[4112,128]{1,0:T(8,128)(2,1)}, u32[]{:S(2)}, u32[]{:S(2)}) collective-permute-start(bf16[4112,128]{1,0:T(8,128)(2,1)} %get-tuple-element.394), channel_id=1, source_target_pairs={{0,4},{3,7},{4,0},{7,3},{8,12},{11,15},{12,8},{15,11},{16,20},{19,... | collective-permute-start | bytes 3158024 | tf_op jit(solution)/shard_map/ppermute | solution.py:982
  673.2 18.9 %collective-permute-start.73 = (bf16[4112,128]{1,0:T(8,128)(2,1)}, bf16[4112,128]{1,0:T(8,128)(2,1)}, u32[]{:S(2)}, u32[]{:S(2)}) collective-permute-start(bf16[4112,128]{1,0:T(8,128)(2,1)} %get-tuple-element.400), channel_id=1, source_target_pairs={{0,8},{3,11},{4,12},{7,15},{8,16},{11,19},{12,20},{15,23},{16,24},... | collective-permute-start | bytes 3158024 | tf_op jit(solution)/shard_map/ppermute | solution.py:982
  677.8 22.7 %collective-permute-start.62 = (bf16[1024,384]{1,0:T(8,128)(2,1)}, bf16[1024,384]{1,0:T(8,128)(2,1)}, u32[]{:S(2)}, u32[]{:S(2)}) collective-permute-start(bf16[1024,384]{1,0:T(8,128)(2,1)} %select_convert_fusion), channel_id=1, source_target_pairs={{0,1},{3,2},{4,5},{7,6},{8,9},{11,10},{12,13},{15,14},{16,17},{19,... | collective-permute-start | bytes 2359304 | tf_op jit(solution)/shard_map/ppermute | solution.py:982
  684.4 19.4 %collective-permute-start.74 = (bf16[4112,128]{1,0:T(8,128)(2,1)}, bf16[4112,128]{1,0:T(8,128)(2,1)}, u32[]{:S(2)}, u32[]{:S(2)}) collective-permute-start(bf16[4112,128]{1,0:T(8,128)(2,1)} %get-tuple-element.404), channel_id=1, source_target_pairs={{0,4},{3,7},{4,0},{7,3},{8,12},{11,15},{12,8},{15,11},{16,20},{19,... | collective-permute-start | bytes 3158024 | tf_op jit(solution)/shard_map/ppermute | solution.py:982
  (104 other events, 1042.6 us)

commit v5 on v4

--- a/solution.py
+++ b/solution.py
@@ -23,6 +23,7 @@
 HALF_FF = FF // TENSOR
 HEADS = HALF // HEAD_DIM
 ROWS = 256
+KEYS = 512
 VEC_ROWS = 16
 CHUNKS = 4
 
@@ -36,7 +37,7 @@
 vector_rate = 0.3
 f32 = jnp.float32
 bf16 = jnp.bfloat16
-BIG_VMEM = 56 * 1024 * 1024
+MIB = 1024 * 1024
 
 PANELS = {
     "up": (0, 6144),
@@ -87,9 +88,9 @@
 VEC_AT = vec_offsets()
 
 
-def params(limit=BIG_VMEM):
+def params(limit=24):
     return pltpu.CompilerParams(
-        dimension_semantics=("arbitrary",), vmem_limit_bytes=limit
+        dimension_semantics=("arbitrary",), vmem_limit_bytes=limit * MIB
     )
 
 
@@ -122,6 +123,12 @@
 
 def dot_tn(left, right):
     return lax.dot_general(left, right, (((0,), (0,)), ((), ())), preferred_element_type=f32)
+
+
+def joined(ref, start, rows_n, panels):
+    return jnp.concatenate(
+        [ref[start + p * rows_n : start + (p + 1) * rows_n, :] for p in range(panels)], axis=1
+    )
 
 
 def norm_stats(values):
@@ -248,6 +255,12 @@
 
 
 def scatter_kernel(rows_n, cols_n, steps, paired, parts, pos, part, own, *refs):
+    @pl.when(part[1] > 0)
+    def _():
+        scatter_body(rows_n, cols_n, steps, paired, parts, pos, part, own, *refs)
+
+
+def scatter_body(rows_n, cols_n, steps, paired, parts, pos, part, own, *refs):
     if paired:
         recv, *refs = refs
         span = pl.num_programs(0) // parts
@@ -319,6 +332,46 @@
     )(pos, part, *operands)
 
 
+def half_sum_kernel(part, own, arrived, out):
+    out[...] = (own[...].astype(f32) + arrived[...].astype(f32)).astype(bf16)
+
+
+def half_sum(part, own, arrived):
+    block = arrived.shape
+    return pl.pallas_call(
+        half_sum_kernel,
+        out_shape=jax.ShapeDtypeStruct(block, bf16),
+        grid_spec=pltpu.PrefetchScalarGridSpec(
+            num_scalar_prefetch=1,
+            grid=(1,),
+            in_specs=[pl.BlockSpec(block, lambda i, part: (part[0], 0)), fixed(block)],
+            out_specs=fixed(block),
+        ),
+        compiler_params=params(),
+        cost_estimate=cost(arrived.size, arrived.size * 6),
+    )(part, own, arrived)
+
+
+def half_copy_kernel(part, own, out):
+    out[...] = own[...]
+
+
+def other_half(part, own):
+    block = (own.shape[0] // 2, own.shape[1])
+    return pl.pallas_call(
+        half_copy_kernel,
+        out_shape=jax.ShapeDtypeStruct(block, bf16),
+        grid_spec=pltpu.PrefetchScalarGridSpec(
+            num_scalar_prefetch=1,
+            grid=(1,),
+            in_specs=[pl.BlockSpec(block, lambda i, part: (1 - part[0], 0))],
+            out_specs=fixed(block),
+        ),
+        compiler_params=params(),
+        cost_estimate=cost(0, own.size * 2),
+    )(part, own)
+
+
 def scatter_vec_kernel(paired, pos, own, *refs):
     if paired:
         recv, *refs = refs
@@ -358,7 +411,7 @@
     )(pos, *operands)
 
 
-def expand_kernel(present, patch_ref, class_ref, pinv_ref, out, total):
+def expand_kernel(present, half, patch_ref, class_ref, pinv_ref, out, total):
     for block in range(patch_ref.shape[0] // ROWS):
         rows = slice(block * ROWS, (block + 1) * ROWS)
         total[...] = jnp.zeros_like(total)
@@ -372,27 +425,30 @@
         out[rows, :] = total[...].astype(bf16)
 
 
-def expand_call(which, present, patches, class_col, pinv):
+def expand_call(which, present, half, patches, class_col, pinv):
     tokens = patches.shape[0]
     size = BASE_PIX // CHUNKS
-    step = size // 3
+    step = size
     return pl.pallas_call(
         expand_kernel,
         out_shape=jax.ShapeDtypeStruct((tokens, size), bf16),
         grid_spec=pltpu.PrefetchScalarGridSpec(
-            num_scalar_prefetch=1,
-            grid=(3,),
+            num_scalar_prefetch=2,
+            grid=(1,),
             in_specs=[
                 fixed(patches.shape),
                 fixed(class_col.shape),
-                pl.BlockSpec((3, step, pinv.shape[2]), lambda i, *_: (0, which * 3 + i, 0)),
+                pl.BlockSpec(
+                    (3, step, pinv.shape[2]),
+                    lambda i, present, half: (0, (which + half[0] * (CHUNKS // 2)) % CHUNKS, 0),
+                ),
             ],
             out_specs=pl.BlockSpec((tokens, step), lambda i, *_: (0, i)),
             scratch_shapes=[pltpu.VMEM((ROWS, step), f32)],
         ),
         compiler_params=params(),
         cost_estimate=cost(3 * tokens * size * D, tokens * size * 4 + size * D * 6),
-    )(present, patches, class_col, pinv)
+    )(present, half, patches, class_col, pinv)
 
 
 def resize_kernel(base, pinv_ref, out, turned):
@@ -473,27 +529,32 @@
     )(*pieces).astype(bf16)
 
 
-def embed_kernel(*refs):
+def embed_kernel(half, *refs):
     *parts, vec, weight, out = refs
     size = BASE_PIX // CHUNKS
     total = vec[:, :HALF]
     for c in range(CHUNKS):
-        total = total + dot(parts[c][...], weight[c * size : (c + 1) * size, :])
+        at = lax.rem(c + half[0] * (CHUNKS // 2), CHUNKS)
+        rows = pl.ds(pl.multiple_of(at * size, size), size)
+        total = total + dot(parts[c][...], weight[rows, :])
     out[...] = total.astype(bf16)
 
 
-def embed_call(chunks, vec, panels):
+def embed_call(half, chunks, vec, panels):
     tokens = chunks[0].shape[0]
     return pl.pallas_call(
         embed_kernel,
         out_shape=jax.ShapeDtypeStruct((tokens, HALF), bf16),
-        grid=(tokens // ROWS,),
-        in_specs=[rows_spec(BASE_PIX // CHUNKS)] * CHUNKS
-        + [fixed(vec.shape), fixed((BASE_PIX, HALF), PANELS["base"] // BASE_PIX)],
-        out_specs=rows_spec(HALF),
+        grid_spec=pltpu.PrefetchScalarGridSpec(
+            num_scalar_prefetch=1,
+            grid=(tokens // ROWS,),
+            in_specs=[rows_spec(BASE_PIX // CHUNKS)] * CHUNKS
+            + [fixed(vec.shape), fixed((BASE_PIX, HALF), PANELS["base"] // BASE_PIX)],
+            out_specs=rows_spec(HALF),
+        ),
         compiler_params=params(),
         cost_estimate=cost(2 * tokens * BASE_PIX * HALF, tokens * BASE_PIX * 3),
-    )(*chunks, vec, panels)
+    )(half, *chunks, vec, panels)
 
 
 def qkv_kernel(layer, first, core, *refs):
@@ -511,9 +572,10 @@
     unit, unused = norm_stats(values)
     low = (unit * vec_piece(vec, layer, "g1") + vec_piece(vec, layer, "s1")).astype(bf16)
     normed[...] = low
-    q_ref[...] = (dot(low, weight[0:D, :]) + vec_piece(vec, layer, "bq")).astype(bf16)
-    k_ref[...] = dot(low, weight[D : 2 * D, :]).astype(bf16)
-    v_ref[...] = (dot(low, weight[2 * D : 3 * D, :]) + vec_piece(vec, layer, "bv")).astype(bf16)
+    made = dot(low, joined(weight, 0, D, 3))
+    q_ref[...] = (made[:, :HALF] + vec_piece(vec, layer, "bq")).astype(bf16)
+    k_ref[...] = made[:, HALF : 2 * HALF].astype(bf16)
+    v_ref[...] = (made[:, 2 * HALF :] + vec_piece(vec, layer, "bv")).astype(bf16)
 
 
 def qkv_call(layer, base, own, recv, core, vec, panels):
@@ -543,38 +605,69 @@
     return low, high
 
 
-def attend_kernel(layer, q_ref, k_ref, v_ref, seg_q, seg_k, vec, w_out, o_ref, lse_ref, part):
+def attend_kernel(
+    layer, low_ref, high_ref, q_ref, k_ref, v_ref, seg_q, seg_k, vec, w_out, o_ref, lse_ref, part,
+    scores_ref, top_ref, acc_ref,
+):
+    step = pl.program_id(0)
+    first, last = low_ref[step], high_ref[step]
     masks = head_masks()
-    same = seg_q[...] == seg_k[...]
-    lane = lax.broadcasted_iota(jnp.int32, (ROWS, BS), 1)
+    scale = jnp.asarray(HEAD_DIM ** (-0.5), bf16)
+    lane = lax.broadcasted_iota(jnp.int32, (1, BS), 1)
+    sums = [(lane == HEAD_DIM).astype(f32).astype(bf16), (lane == 0).astype(f32).astype(bf16)]
+    top_ref[...] = jnp.full(top_ref.shape, masked_score, f32)
+    acc_ref[...] = jnp.zeros_like(acc_ref)
+    seg_col = seg_q[...]
+
+    def score_block(block, carried):
+        rows = pl.ds(pl.multiple_of(block * ROWS, ROWS), ROWS)
+        same = seg_col == seg_k[:, rows]
+        for pair in range(HEADS // 2):
+            cols = slice(pair * BS, (pair + 1) * BS)
+            q_two = q_ref[:, cols] * scale
+            k_two = k_ref[rows, cols]
+            for side in range(2):
+                head = 2 * pair + side
+                scores = jnp.where(same, dot_nt(q_two * masks[side], k_two), masked_score)
+                scores_ref[head, block] = scores
+                top = top_ref[head]
+                for piece in range(ROWS // BS):
+                    top = jnp.maximum(top, scores[:, piece * BS : (piece + 1) * BS])
+                top_ref[head] = top
+        return carried
+
+    lax.fori_loop(first, last, score_block, 0)
+    tops = [jnp.max(top_ref[head], axis=1, keepdims=True) for head in range(HEADS)]
+
+    def mix_block(block, carried):
+        rows = pl.ds(pl.multiple_of(block * ROWS, ROWS), ROWS)
+        for pair in range(HEADS // 2):
+            v_two = v_ref[rows, pair * BS : (pair + 1) * BS]
+            for side in range(2):
+                head = 2 * pair + side
+                expo = jnp.exp(scores_ref[head, block] - tops[head]).astype(bf16)
+                acc_ref[head] += dot(expo, v_two * masks[side] + sums[side])
+        return carried
+
+    lax.fori_loop(first, last, mix_block, 0)
     totals = jnp.zeros((ROWS, BS), f32)
-    scale = jnp.asarray(HEAD_DIM ** (-0.5), bf16)
     for pair in range(HEADS // 2):
-        cols = slice(pair * BS, (pair + 1) * BS)
-        q_two = q_ref[:, cols] * scale
-        k_two = k_ref[:, cols]
-        v_two = v_ref[:, cols]
-        mixed = None
+        sides = []
         for side in range(2):
-            scores = dot_nt(q_two * masks[side], k_two)
-            scores = jnp.where(same, scores, masked_score)
-            top = jnp.max(scores, axis=1, keepdims=True)
-            expo = jnp.exp(scores - top)
-            total = jnp.sum(expo, axis=1, keepdims=True)
-            weights = (expo * (1.0 / total)).astype(bf16)
-            term = dot(weights, v_two * masks[side])
-            mixed = term if mixed is None else mixed + term
-            totals = jnp.where(lane == 2 * pair + side, top + jnp.log(total), totals)
-        o_ref[:, cols] = mixed.astype(bf16)
+            head = 2 * pair + side
+            mixed = acc_ref[head]
+            at = HEAD_DIM * (1 - side)
+            total = mixed[:, at : at + 1]
+            totals = jnp.where(lane == head, tops[head] + jnp.log(total), totals)
+            sides.append(mixed * (1.0 / total))
+        o_ref[:, pair * BS : (pair + 1) * BS] = jnp.where(lane < HEAD_DIM, *sides).astype(bf16)
     lse_ref[...] = totals.T[0:8, :]
     low = o_ref[...]
     bias = vec_piece(vec, layer, "bo")
-    for panel in range(TENSOR):
-        area = slice(panel * HALF, (panel + 1) * HALF)
-        part[:, area] = (dot(low, w_out[area, :]) + bias[:, area]).astype(bf16)
-
-
-def attend_call(layer, queries, keys, values, seg_col, seg_row, vec, panels):
+    part[...] = (dot(low, joined(w_out, 0, HALF, TENSOR)) + bias).astype(bf16)
+
+
+def attend_call(layer, first, last, queries, keys, values, seg_col, seg_row, vec, panels):
     tokens = queries.shape[0]
     return pl.pallas_call(
         functools.partial(attend_kernel, layer),
@@ -583,24 +676,32 @@
             jax.ShapeDtypeStruct((8, tokens), f32),
             jax.ShapeDtypeStruct((tokens, D), bf16),
         ],
-        grid=(tokens // ROWS,),
-        in_specs=[
-            rows_spec(HALF),
-            fixed(keys.shape),
-            fixed(values.shape),
-            rows_spec(1),
-            fixed(seg_row.shape),
-            fixed(vec.shape),
-            fixed((D, HALF), PANELS["out"][layer] // D),
-        ],
-        out_specs=[
-            rows_spec(HALF),
-            pl.BlockSpec((8, ROWS), lambda i: (0, i)),
-            rows_spec(D),
-        ],
+        grid_spec=pltpu.PrefetchScalarGridSpec(
+            num_scalar_prefetch=2,
+            grid=(tokens // ROWS,),
+            in_specs=[
+                rows_spec(HALF),
+                fixed(keys.shape),
+                fixed(values.shape),
+                rows_spec(1),
+                fixed(seg_row.shape),
+                fixed(vec.shape),
+                fixed((D, HALF), PANELS["out"][layer] // D),
+            ],
+            out_specs=[
+                rows_spec(HALF),
+                pl.BlockSpec((8, ROWS), lambda i, *_: (0, i)),
+                rows_spec(D),
+            ],
+            scratch_shapes=[
+                pltpu.VMEM((HEADS, tokens // ROWS, ROWS, ROWS), f32),
+                pltpu.VMEM((HEADS, ROWS, BS), f32),
+                pltpu.VMEM((HEADS, ROWS, BS), f32),
+            ],
+        ),
         compiler_params=params(),
         cost_estimate=cost(8 * HEADS * tokens * tokens * BS, tokens * D * 8, HEADS * tokens * tokens),
-    )(queries, keys, values, seg_col, seg_row, vec, panels)
+    )(first, last, queries, keys, values, seg_col, seg_row, vec, panels)
 
 
 def gelu_parts(values):
@@ -616,18 +717,14 @@
     low = (unit * vec_piece(vec, layer, "g2") + vec_piece(vec, layer, "s2")).astype(bf16)
     normed[...] = low
     bias_up = vec_piece(vec, layer, "b1")
-    for panel in range(HALF_FF // HALF):
-        area = slice(panel * HALF, (panel + 1) * HALF)
-        up = dot(low, w_up[panel * D : (panel + 1) * D, :]) + bias_up[:, area]
+    for pair in range(HALF_FF // D):
+        area = slice(pair * D, (pair + 1) * D)
+        up = dot(low, joined(w_up, pair * 2 * D, D, 2)) + bias_up[:, area]
         gelu, grad = gelu_parts(up)
         act[:, area] = gelu.astype(bf16)
         slope[:, area] = grad.astype(bf16)
     bias_down = vec_piece(vec, layer, "b2")
-    hidden_units = act[...]
-    for panel in range(TENSOR):
-        area = slice(panel * HALF, (panel + 1) * HALF)
-        down = dot(hidden_units, w_down[panel * HALF_FF : (panel + 1) * HALF_FF, :])
-        part[:, area] = (down + bias_down[:, area]).astype(bf16)
+    part[...] = (dot(act[...], joined(w_down, 0, HALF_FF, TENSOR)) + bias_down).astype(bf16)
 
 
 def mlp_call(layer, base, own, recv, vec, panels):
@@ -663,19 +760,14 @@
         low = (base[...].astype(f32) * valid[...]).astype(bf16)
     grad_low[...] = low
     accumulate(db2, jnp.sum(low.astype(f32), axis=0, keepdims=True))
-    for part in range(HALF_FF // HALF):
-        area = slice(part * HALF, (part + 1) * HALF)
-        grad_act = None
-        for panel in range(TENSOR):
-            start = panel * HALF_FF + part * HALF
-            term = dot_nt(low[:, panel * HALF : (panel + 1) * HALF], w_down[start : start + HALF, :])
-            grad_act = term if grad_act is None else grad_act + term
-        du_ref[:, area] = (grad_act * slope[:, area].astype(f32)).astype(bf16)
-    grad_normed = None
-    for panel in range(HALF_FF // HALF):
-        area = slice(panel * HALF, (panel + 1) * HALF)
-        term = dot_nt(du_ref[:, area], w_up[panel * D : (panel + 1) * D, :])
-        grad_normed = term if grad_normed is None else grad_normed + term
+    for part in range(HALF_FF // D):
+        area = slice(part * D, (part + 1) * D)
+        rows = jnp.concatenate(
+            [w_down[p * HALF_FF + part * D : p * HALF_FF + (part + 1) * D, :] for p in range(TENSOR)],
+            axis=1,
+        )
+        du_ref[:, area] = (dot_nt(low, rows) * slope[:, area].astype(f32)).astype(bf16)
+    grad_normed = dot_nt(du_ref[...], joined(w_up, 0, D, HALF_FF // HALF))
     accumulate(db1, jnp.sum(du_ref[...].astype(f32), axis=0, keepdims=True))
     part_back, gain_grad, shift_grad = norm_back(hid[...], vec_piece(vec, layer, "g2"), grad_normed)
     back[...] = part_back.astype(bf16)
@@ -726,24 +818,21 @@
     low = values.astype(bf16)
     grad_low[...] = low
     accumulate(dbo, jnp.sum(low.astype(f32), axis=0, keepdims=True))
-    grad_mixed = None
-    for panel in range(TENSOR):
-        area = slice(panel * HALF, (panel + 1) * HALF)
-        term = dot_nt(low[:, area], w_out[area, :])
-        grad_mixed = term if grad_mixed is None else grad_mixed + term
-    do_ref[...] = grad_mixed.astype(bf16)
+    do_ref[...] = dot_nt(low, joined(w_out, 0, HALF, TENSOR)).astype(bf16)
     product = do_ref[...].astype(f32) * o_ref[...].astype(f32)
     head = lax.broadcasted_iota(jnp.int32, (8, HALF), 0)
     lane = lax.broadcasted_iota(jnp.int32, (8, HALF), 1)
     pick = ((lane >= head * HEAD_DIM) & (lane < (head + 1) * HEAD_DIM)).astype(f32)
-    inner = dot_nt(pick, product, precise)
+    high, rest = split(product)
+    pick = pick.astype(bf16)
+    inner = dot_nt(pick, high) + dot_nt(pick, rest)
     dq_acc[...] = jnp.zeros_like(dq_acc)
     masks = head_masks()
     scale = jnp.asarray(HEAD_DIM ** (-0.5), bf16)
     seg_row = seg_q[...]
 
     def one_block(block, carried):
-        rows = pl.ds(pl.multiple_of(block * ROWS, ROWS), ROWS)
+        rows = pl.ds(pl.multiple_of(block * KEYS, KEYS), KEYS)
         same = seg_k[rows, :] == seg_row
         for pair in range(HEADS // 2):
             cols = slice(pair * BS, (pair + 1) * BS)
@@ -763,9 +852,9 @@
                 dv_one = dot(prob.astype(bf16), do_one)
                 dk_one = dot(grad_scores, q_one)
                 dq_one = dot_tn(grad_scores, k_two * masks[side])
+                dq_two = dq_one if dq_two is None else dq_two + dq_one
                 dv_two = dv_one if dv_two is None else dv_two + dv_one
                 dk_two = dk_one if dk_two is None else dk_two + dk_one
-                dq_two = dq_one if dq_two is None else dq_two + dq_one
             dv_acc[rows, cols] += dv_two
             dk_acc[rows, cols] += dk_two
             dq_acc[:, cols] += dq_two
@@ -833,11 +922,8 @@
 
 
 def qkv_back_kernel(layer, dq, dk, dv, hid, vec, weight, back, dgain, dshift, dbq, dbv):
-    grad_normed = (
-        dot_nt(dq[...], weight[0:D, :])
-        + dot_nt(dk[...], weight[D : 2 * D, :])
-        + dot_nt(dv[...], weight[2 * D : 3 * D, :])
-    )
+    grad_three = jnp.concatenate([dq[...], dk[...], dv[...]], axis=1)
+    grad_normed = dot_nt(grad_three, joined(weight, 0, D, 3))
     part_back, gain_grad, shift_grad = norm_back(hid[...], vec_piece(vec, layer, "g1"), grad_normed)
     back[...] = part_back.astype(bf16)
     accumulate(dgain, gain_grad)
@@ -1004,6 +1090,8 @@
     home = core == y_pos
     routes = Routes(dp_n)
     grid3 = dp_n == 16
+    x_pos = (dp_pos // 2) % 2
+    half_at = (x_pos if grid3 else x_pos * 0).astype(jnp.int32).reshape(1)
     tokens_n = patches.shape[0]
     slots_per = master_slots.shape[1]
     vec_per = vec_master.shape[1]
@@ -1038,13 +1126,15 @@
     last_tok = jnp.min(jnp.where(after, ends_at[None, :], tokens_n), axis=1)
     first_blk = (first_tok // ROWS).astype(jnp.int32)
     last_blk = ((last_tok + ROWS - 1) // ROWS).astype(jnp.int32)
+    first_key = (first_tok // KEYS).astype(jnp.int32)
+    last_key = ((last_tok + KEYS - 1) // KEYS).astype(jnp.int32)
 
     select_low = select.astype(bf16)
     class_col = jnp.sum(jnp.where(select, jnp.arange(1, 4)[None, :], 0), axis=1, keepdims=True) - 1
     present = jnp.any(select.reshape(blocks_n, ROWS, 3), axis=1).astype(jnp.int32)
 
     def expand(which):
-        return expand_call(which, present, patches, class_col, pinv)
+        return expand_call(which, present, half_at, patches, class_col, pinv)
 
     vec_low = jnp.pad(vec_master[0].astype(bf16), (0, VEC_ROWS * BS - vec_per))
     own_pack = jnp.concatenate(
@@ -1056,7 +1146,6 @@
     )
     flag = home.astype(jnp.int32).reshape(1)
     if grid3:
-        x_pos = (dp_pos // 2) % 2
         z_pos = dp_pos // 4
         packs = [[own_pack], [send(own_pack, routes.core_in)]]
         across, over_y, corner = [[], []], [[], []], [[], []]
@@ -1115,7 +1204,7 @@
     panels, vec_rows = gather_tiles(first, second, owner, drow, dcol, flag, slots_per, dp_n)
     vec = vec_rows.reshape(dp_n, VEC_ROWS * BS)[:, :vec_per].astype(f32).reshape(1, dp_n * vec_per)
 
-    embedded = embed_call(chunks, vec, panels)
+    embedded = embed_call(half_at, chunks, vec, panels)
     embedded_other = send(embedded, routes.core_all)
     core_flag = core.astype(jnp.int32).reshape(1)
 
@@ -1126,7 +1215,7 @@
             layer, hidden, own, recv, core_flag, vec, panels
         )
         mixed, lse, part = attend_call(
-            layer, queries, keys, values, seg_col, seg_row, vec, panels
+            layer, first_blk, last_blk, queries, keys, values, seg_col, seg_row, vec, panels
         )
         other = send(part, routes.core_all)
         middle, normed2, act, slope, own = mlp_call(layer, hidden, part, other, vec, panels)
@@ -1142,10 +1231,8 @@
             + (x_pos ^ ((owners // 2) % 2)) * 2
             + (core ^ (owners % 2))
         ).astype(jnp.int32)
-        half_at = x_pos.astype(jnp.int32).reshape(1)
     else:
         place = owners.astype(jnp.int32)
-        half_at = jnp.zeros((1,), jnp.int32)
     slot_owner = slot_list // slots_per
     owner_place = jnp.sum(
         jnp.where(slot_owner[:, None] == owners[None, :], place[None, :], 0), axis=1
@@ -1153,6 +1240,7 @@
     tile_pos = (owner_place * payload + (slot_list % slots_per) * BS).astype(jnp.int32)
     vec_pos = (place * payload + slots_per * BS).astype(jnp.int32)
     total_rows = dp_n * payload
+    where_to = jnp.concatenate([half_at, flag if grid3 else flag * 0 + 1])
     offsets = {"base": 0}
     count = BASE_PIX // BS * (HALF // BS)
     for layer in range(LAYERS):
@@ -1164,23 +1252,22 @@
         tiles = matrix.size // (BS * BS)
         pos = tile_pos[offsets[key] : offsets[key] + tiles]
         rows_n = matrix.shape[0] // 2 if matrix.shape[0] > HALF else HALF
-        return scatter_matrix(pos, matrix, arrived, half_at, buffer, total_rows, rows_n)
+        return scatter_matrix(pos, matrix, arrived, where_to, buffer, total_rows, rows_n)
+
+    def place_base(rel, matrix, arrived, buffer):
+        size = BASE_PIX * HALF // (BS * BS) // 2
+        low_pos, high_pos = tile_pos[:size], tile_pos[size : 2 * size]
+        pos = jnp.where(half_at[0] == rel, low_pos, high_pos)
+        return scatter_matrix(pos, matrix, arrived, where_to, buffer, total_rows, D)
 
     def over(matrix):
         return send(matrix, routes.y_in) if grid3 else None
 
-    def halves_of(matrix):
-        size = matrix.shape[0] // 2
-        mine = lax.dynamic_slice_in_dim(matrix, x_pos * size, size, 0)
-        theirs = lax.dynamic_slice_in_dim(matrix, (1 - x_pos) * size, size, 0)
-        return mine, theirs
-
-    def half_sum(matrix, arrived):
-        mine, unused = halves_of(matrix)
-        return (mine.astype(f32) + arrived.astype(f32)).astype(bf16)
-
     def beside(matrix):
-        return send(halves_of(matrix)[1], routes.x_away) if grid3 else None
+        return send(other_half(half_at, matrix), routes.x_away) if grid3 else None
+
+    def summed(matrix, arrived):
+        return half_sum(half_at, matrix, arrived) if grid3 else None
 
     def hold(*arrays):
         kept = [a for a in arrays if a is not None]
@@ -1200,7 +1287,7 @@
     def attend_step(layer, grad, part, other):
         hid_in, normed, queries, keys, values, mixed, lse = caches[layer][:7]
         return attend_back_call(
-            layer, first_blk, last_blk, grad, part, other, queries, keys, values, mixed, lse,
+            layer, first_key, last_key, grad, part, other, queries, keys, values, mixed, lse,
             seg_col, seg_row, panels,
         )
 
@@ -1208,7 +1295,7 @@
     other = send(part, routes.core_all)
     gd1 = dot_tn(caches[top][9], grad_low).astype(bf16)
     gu1 = dot_tn(caches[top][8], du).astype(bf16)
-    part, other, gd1, gu1 = fence(part, other, gd1, gu1)
+    part, other, gd1, gu1, out_low = fence(part, other, gd1, gu1, out_low)
     ad1 = over(gd1)
     grad, grad_low, dq, dk, dv, dbo = attend_step(top, grad, part, other)
     dq, dk, dv, ad1 = hold(dq, dk, dv, ad1)
@@ -1225,7 +1312,7 @@
     gd0 = dot_tn(caches[low][9], grad_low).astype(bf16)
     gu0 = dot_tn(caches[low][8], du).astype(bf16)
     part, other, gd0, gu0, xq1, ao1 = hold(part, other, gd0, gu0, xq1, ao1)
-    aq1 = over(half_sum(gq1, xq1)) if grid3 else None
+    aq1 = over(summed(gq1, xq1)) if grid3 else None
     xd0, xu0 = beside(gd0), beside(gu0)
     buffer = place_tiles(("down", top), gd1, ad1, None)
     buffer = place_tiles(("up", top), gu1, au1, buffer)
@@ -1233,8 +1320,7 @@
     grad, grad_low, dq, dk, dv, aq1, xd0, xu0, buffer = hold(
         grad, grad_low, dq, dk, dv, aq1, xd0, xu0, buffer
     )
-    hd0 = half_sum(gd0, xd0) if grid3 else None
-    hu0 = half_sum(gu0, xu0) if grid3 else None
+    hd0, hu0 = summed(gd0, xd0), summed(gu0, xu0)
     dq, dk, dv, hd0, hu0 = hold(dq, dk, dv, hd0, hu0)
     ad0, au0 = over(hd0), over(hu0)
     own, dg1, ds1, dbq, dbv = qkv_back_call(low, dq, dk, dv, caches[low][0], vec, panels)
@@ -1244,26 +1330,34 @@
     own, recv, gq0 = hold(own, recv, gq0)
     xq0 = beside(gq0)
     grad_emb, grad_emb_bias = embed_back_call(core_flag, grad, own, recv)
-    gb = jnp.concatenate([dot_tn(c, grad_emb).astype(bf16) for c in chunks], axis=0)
+    middle = CHUNKS // 2
+
+    def base_grad(parts):
+        return jnp.concatenate([dot_tn(c, grad_emb).astype(bf16) for c in parts], axis=0)
+
+    gbt = base_grad(chunks[middle:])
+    gbt, grad_emb, gq0 = hold(gbt, grad_emb, gq0)
+    xb = send(gbt, routes.x_away) if grid3 else None
+    gbm = base_grad(chunks[:middle])
     vec_grad = pack_call([grad_emb_bias] + vec_grads[0] + vec_grads[1], dp_n, vec_per)
     go0 = dot_tn(caches[low][5], grad_low).astype(bf16)
-    gb, vec_grad, grad_emb, go0, gq0, xq0 = hold(gb, vec_grad, grad_emb, go0, gq0, xq0)
-    xb = beside(gb)
-    hq0 = half_sum(gq0, xq0) if grid3 else None
+    hq0 = summed(gq0, xq0)
+    gbm, vec_grad, go0, hq0 = hold(gbm, vec_grad, go0, hq0)
     aq0, ao0, av = over(hq0), over(go0), over(vec_grad)
+    gbm, xb = hold(gbm, xb)
+    hb = (gbm.astype(f32) + xb.astype(f32)).astype(bf16) if grid3 else None
+    hb, gbm, gbt, buffer = hold(hb, gbm, gbt, buffer)
+    ab = over(hb)
     buffer = place_tiles(("out", top), go1, ao1, buffer)
     buffer = place_tiles(("qkv", top), gq1, aq1, buffer)
     buffer = place_tiles(("down", low), gd0, ad0, buffer)
     buffer = place_tiles(("up", low), gu0, au0, buffer)
-    gb, xb, aq0, ao0, av, buffer = hold(gb, xb, aq0, ao0, av, buffer)
-    hb = half_sum(gb, xb) if grid3 else None
-    hb, gb, aq0, buffer = hold(hb, gb, aq0, buffer)
-    ab = over(hb)
+    buffer = place_base(1, gbt, None, buffer)
     buffer = place_tiles(("out", low), go0, ao0, buffer)
     buffer = scatter_vec(vec_pos, vec_grad, av, buffer)
     buffer = place_tiles(("qkv", low), gq0, aq0, buffer)
     ab, buffer, panels, grad_emb, out_low = hold(ab, buffer, panels, grad_emb, out_low)
-    buffer = place_tiles("base", gb, ab, buffer)
+    buffer = place_base(0, gbm, ab, buffer)
 
     if grid3:
         token = jnp.zeros((8, BS), f32)

time: 733 us -> 849 us (1.16)
  local copies, waits for them, and re-layouts: 30.4 us -> 290 us
  Pallas kernels: 338 us -> 242 us
  starting transfers between devices: 196 us -> 178 us
  other arithmetic: 41.5 us -> 26.6 us
  waiting for transfers between devices: 69.6 us -> 58.8 us
    unnamed x152 -> x416, local copies, waits for them, and re-layouts: 16.1 us -> 286 us
    pallas_call x2, Pallas kernels: 59.7 us -> 40.2 us  [attend_back_call(): pl.pallas_call(attend_back_kernel, out_shape=[shape(D, f32), shape(D, bf1...]
    pallas_call x4, Pallas kernels: 34 us -> 15.6 us  [expand_call(): pl.pallas_call(expand_kernel, out_shape=jax.ShapeDtypeStruct((tokens, siz...]
    ppermute x77, starting transfers between devices: 196 us -> 178 us  [send(): return lax.ppermute(value, AXES, route)]
    pallas_call x2, Pallas kernels: 39.1 us -> 26.3 us  [attend_call(): pl.pallas_call(functools.partial(attend_kernel, layer), out_shape=[jax.Sh...]
    pallas_call x8, Pallas kernels: 27.6 us -> 15.6 us  [reduce_call(): pl.pallas_call(functools.partial(reduce_kernel, carried is not None, last...]
    pallas_call x2, Pallas kernels: 32.7 us -> 21.8 us  [mlp_back_call(): pl.pallas_call(functools.partial(mlp_back_kernel, layer, summed), out_sha...]
    ppermute x77, waiting for transfers between devices: 69.6 us -> 58.8 us  [send(): return lax.ppermute(value, AXES, route)]
  transfers between devices with their start and end apart: 77 -> 77, of which waited for: 23 -> 16; matrix products, arithmetic and copies ran while one was open for 12% -> 7% of each run, Pallas kernels for 31% -> 19%
where the time goes in v5:
time: 849 us; the launch traced here: 835 us
  local copies, waits for them, and re-layouts  290 us (34%)
  Pallas kernels  242 us (29%)
  starting transfers between devices  178 us (21%)
  waiting for transfers between devices  58.8 us (7%)
  matrix products  36.9 us (4%)
  other arithmetic  26.6 us (3%)
    unnamed x416, local copies, waits for them, and re-layouts  286 us
    ppermute x77, starting transfers between devices, send(): return lax.ppermute(value, AXES, route)  178 us
    ppermute x77, waiting for transfers between devices, send(): return lax.ppermute(value, AXES, route)  58.8 us
    pallas_call x10, Pallas kernels, scatter_matrix(): pl.pallas_call(functools.partial(scatter_kernel, rows_n, cols_n, steps, p...  41.6 us
    pallas_call x2, Pallas kernels, attend_back_call(): pl.pallas_call(attend_back_kernel, out_shape=[shape(D, f32), shape(D, bf1...  40.2 us
    dot_general x12, matrix products, dot_tn(): lax.dot_general(left, right, (((0,), (0,)), ((), ())), preferred_element_...  32.6 us
    pallas_call x2, Pallas kernels, attend_call(): pl.pallas_call(functools.partial(attend_kernel, layer), out_shape=[jax.Sh...  26.3 us
    pallas_call x2, Pallas kernels, mlp_back_call(): pl.pallas_call(functools.partial(mlp_back_kernel, layer, summed), out_sha...  21.8 us
  transfers between devices with their start and end apart: 77, of which 16 were waited for; matrix products, arithmetic and copies ran while one was open for 7% of the time, Pallas kernels for 19%

profile of v5, /device:TPU:0, one launch (start us, length us, event | category | flops | bytes accessed | tf_op | source)
XLA Modules:
  0.0 835.2 jit_solution(11312795192700567171)
XLA Ops:
  25.6 8.4 %collective-permute-done.2.refs_3_ = bf16[4112,128]{1,0:T(8,128)(2,1)} collective-permute-done((bf16[4112,128]{1,0:T(8,128)(2,1)}, bf16[4112,128]{1,0:T(8,128)(2,1)}, u32[]{:S(2)}, u32[]{:S(2)}) %collective-permute-start.2) | collective-permute-done | bytes 1052704 | tf_op jit(solution)/shard_map/ppermute | solution.py:1068
  144.1 6.5 collective-permute-done.27.refs_1_
  152.2 7.8 collective-permute-done.29.refs_3_
  173.8 8.8 %collective-permute-done.33 = bf16[4112,128]{1,0:T(8,128)(2,1)} collective-permute-done((bf16[4112,128]{1,0:T(8,128)(2,1)}, bf16[4112,128]{1,0:T(8,128)(2,1)}, u32[]{:S(2)}, u32[]{:S(2)}) %collective-permute-start.33) | collective-permute-done | bytes 1052704 | tf_op jit(solution)/shard_map/ppermute | solution.py:1068
  187.5 15.3 %shard_map.234 = (bf16[21504,384]{1,0:T(8,128)(2,1)}, bf16[16,16,128]{2,1,0:T(8,128)(2,1)S(1)}) custom-call(s32[16]{0:T(128)S(1)} %stack.95.owner, s32[512]{0:T(512)S(1)} %broadcast_select_fusion.3.drow, s32[512]{0:T(512)S(1)} %get-tuple-element.416.dcol, s32[1]{0:T(128)} %bitcast.27.flag.home, bf16[1,4112,128]{2,1,0:T(8,128)(2,1)S(1)} %copy-done.112, ...), custom_call_target="tpu_custom_call" | custom-call | bytes 33030144 | tf_op jit(solution)/shard_map/pallas_call | solution.py:235
  218.1 5.7 copy-done.24
  228.6 13.1 %shard_map.237 = (bf16[1024,384]{1,0:T(8,128)(2,1)S(1)}, f32[8,1024]{1,0:T(8,128)S(1)}, bf16[1024,768]{1,0:T(8,128)(2,1)S(1)}) custom-call(s32[4]{0:T(128)S(1)} %get-tuple-element.451.low_ref, s32[4]{0:T(128)S(1)} %get-tuple-element.444.high_ref, bf16[1024,384]{1,0:T(8,128)(2,1)S(1)} %get-tuple-element.253.q_ref, ...), custom_call_target="tpu_custom_call" | custom-call | flops 6442450944 | bytes 6291456 | tf_op jit(solution)/shard_map/pallas_call | solution.py:672
  246.1 10.8 %shard_map.238 = (f32[1024,768]{1,0:T(8,128)S(1)}, bf16[1024,768]{1,0:T(8,128)(2,1)S(1)}, bf16[1024,1536]{1,0:T(8,128)(2,1)S(1)}, bf16[1024,1536]{1,0:T(8,128)(2,1)S(1)}, bf16[1024,768]{1,0:T(8,128)(2,1)S(1)}) custom-call(f32[1024,768]{1,0:T(8,128)S(1)} %get-tuple-element.252.base.hid, bf16[1024,768]{1,0:T(8,128)(2,1)S(1)} %get-tuple-element.256.own, ...), custom_call_target="tpu_custom_call" | custom-call | flops 4831838208 | bytes 18874368 | tf_op jit(solution)/shard_map/pallas_call | solution.py:734
  274.4 13.2 %shard_map.240 = (bf16[1024,384]{1,0:T(8,128)(2,1)S(1)}, f32[8,1024]{1,0:T(8,128)S(1)}, bf16[1024,768]{1,0:T(8,128)(2,1)S(1)}) custom-call(s32[4]{0:T(128)S(1)} %get-tuple-element.451.low_ref, s32[4]{0:T(128)S(1)} %get-tuple-element.444.high_ref, bf16[1024,384]{1,0:T(8,128)(2,1)S(1)} %get-tuple-element.260.q_ref, ...), custom_call_target="tpu_custom_call" | custom-call | flops 6442450944 | bytes 6291456 | tf_op jit(solution)/shard_map/pallas_call | solution.py:672
  291.1 10.9 %shard_map.241 = (f32[1024,768]{1,0:T(8,128)S(1)}, bf16[1024,768]{1,0:T(8,128)(2,1)S(1)}, bf16[1024,1536]{1,0:T(8,128)(2,1)S(1)}, bf16[1024,1536]{1,0:T(8,128)(2,1)S(1)}, bf16[1024,768]{1,0:T(8,128)(2,1)S(1)}) custom-call(f32[1024,768]{1,0:T(8,128)S(1)} %get-tuple-element.259.base.hid, bf16[1024,768]{1,0:T(8,128)(2,1)S(1)} %get-tuple-element.263.own, ...), custom_call_target="tpu_custom_call" | custom-call | flops 4831838208 | bytes 18874368 | tf_op jit(solution)/shard_map/pallas_call | solution.py:734
  305.2 5.7 copy-done.26
  310.9 9.7 %shard_map.242 = (bf16[1024,768]{1,0:T(8,128)(2,1)S(1)}, bf16[1024,1536]{1,0:T(8,128)(2,1)S(1)}, bf16[1024,768]{1,0:T(8,128)(2,1)S(1)}, f32[1,768]{1,0:T(1,128)S...) custom-call(bf16[1024,768]{1,0:T(8,128)(2,1)S(1)} %broadcast_select_fusion.refs_0_, ...), custom_call_target="tpu_custom_call" | custom-call | flops 4831838208 | bytes 18874368 | tf_op jit(solution)/shard_map/pallas_call | solution.py:786
  342.0 20.0 %shard_map.244 = (f32[1024,768]{1,0:T(8,128)S(1)}, bf16[1024,768]{1,0:T(8,128)(2,1)S(1)}, bf16[1024,384]{1,0:T(8,128)(2,1)S(1)}, bf16[1024,384]{1,0:T(8,128)(2,1...) custom-call(s32[4]{0:T(128)S(1)} %get-tuple-element.450.low_ref, s32[4]{0:T(128)S(1)} %get-tuple-element.445.high_ref, ...), custom_call_target="tpu_custom_call" | custom-call | flops 11274289152 | bytes 15728640 | tf_op jit(solution)/shard_map/pallas_call | solution.py:878
  367.6 5.7 copy-done.27
  382.8 8.7 %collective-permute-start.42 = (bf16[1024,768]{1,0:T(8,128)(2,1)S(1)}, bf16[1024,768]{1,0:T(8,128)(2,1)S(1)}, u32[]{:S(2)}, u32[]{:S(2)}) collective-permute-start(bf16[1024,768]{1,0:T(8,128)(2,1)S(1)} %get-tuple-element.284.refs_1_), channel_id=1, source_target_pairs={{0,2},{1,3},{2,0},{3,1},{4,6},{5,7},{6,4},{7,5},{8,10},{9,11},{10,... | collective-permute-start | bytes 4718600 | tf_op jit(solution)/shard_map/ppermute | solution.py:1068
  396.7 12.1 %shard_map.247 = (f32[1024,768]{1,0:T(8,128)S(1)}, bf16[1024,768]{1,0:T(8,128)(2,1)S(1)}, bf16[1024,1536]{1,0:T(8,128)(2,1)S(1)}, bf16[1024,768]{1,0:T(8,128)(2,...) custom-call(f32[1024,768]{1,0:T(8,128)S(1)} %copy-done.135, ...), custom_call_target="tpu_custom_call" | custom-call | flops 4831838208 | bytes 18874368 | tf_op jit(solution)/shard_map/pallas_call | solution.py:786
  418.4 6.5 convolution_convert_fusion.refs_3_
  437.3 5.9 shard_map.255.refs_1_
  443.3 6.1 shard_map.256.refs_8_
  449.4 5.8 copy-done
  457.1 20.2 %shard_map.251 = (f32[1024,768]{1,0:T(8,128)S(1)}, bf16[1024,768]{1,0:T(8,128)(2,1)S(1)}, bf16[1024,384]{1,0:T(8,128)(2,1)S(1)}, bf16[1024,384]{1,0:T(8,128)(2,1...) custom-call(s32[4]{0:T(128)S(1)} %get-tuple-element.450.low_ref, s32[4]{0:T(128)S(1)} %get-tuple-element.445.high_ref, ...), custom_call_target="tpu_custom_call" | custom-call | flops 11274289152 | bytes 15728640 | tf_op jit(solution)/shard_map/pallas_call | solution.py:878
  549.1 5.8 copy-done.1
  556.4 5.8 copy-done.2
  562.2 5.8 copy-done.3
  571.7 5.8 copy-done.4
  577.5 5.8 copy-done.5
  583.3 6.1 shard_map.273.refs_1_
  589.4 5.9 shard_map.274.refs_0_
  595.4 5.8 copy-done.6
  601.2 5.8 copy-done.7
  611.0 5.8 copy-done.8
  616.9 5.8 copy-done.9
  623.5 5.8 copy-done.10
  629.3 5.8 copy-done.11
  639.9 5.7 copy-done.12
  646.9 5.8 copy-done.13
  657.4 5.7 copy-done.14
  674.1 8.3 shard_map.281.refs_2_
  684.6 5.8 copy-done.15
  697.1 7.8 collective-permute-start.65
  710.2 5.8 copy-done.16
  724.0 5.8 copy-done.17
  743.5 5.8 copy-done.18
  759.1 5.8 copy-done.19
  781.7 5.8 copy-done.20
  795.2 5.8 copy-done.21
  814.7 5.8 copy-done.22
  827.1 7.7 shard_map.298
  (681 shorter events, 461.5 us)
Async XLA Ops:
  0.7 44.1 %collective-permute-start.9 = (bf16[1024,768]{1,0:T(8,128)(2,1)}, bf16[1024,768]{1,0:T(8,128)(2,1)S(1)}, u32[]{:S(2)}, u32[]{:S(2)}) collective-permute-start(bf16[1024,768]{1,0:T(8,128)(2,1)} %param.15), channel_id=1, source_target_pairs={{0,2},{3,1},{4,6},{7,5},{8,10},{11,9},{12,14},{15,13},{16,18},{19,... | collective-permute-start | bytes 4718600 | tf_op jit(solution)/shard_map/ppermute | solution.py:1068
  34.6 35.9 %collective-permute-start.10 = (bf16[4112,128]{1,0:T(8,128)(2,1)}, bf16[4112,128]{1,0:T(8,128)(2,1)S(1)}, u32[]{:S(2)}, u32[]{:S(2)}) collective-permute-start(bf16[4112,128]{1,0:T(8,128)(2,1)} %get-tuple-element.213), channel_id=1, source_target_pairs={{0,4},{3,7},{4,0},{7,3},{8,12},{11,15},{12,8},{15,11},{16,20},{19,... | collective-permute-start | bytes 3158024 | tf_op jit(solution)/shard_map/ppermute | solution.py:1068
  37.9 25.0 %collective-permute-start.5 = (bf16[4112,128]{1,0:T(8,128)(2,1)}, bf16[4112,128]{1,0:T(8,128)(2,1)}, u32[]{:S(2)}, u32[]{:S(2)}) collective-permute-start(bf16[4112,128]{1,0:T(8,128)(2,1)} %collective-permute-done.4), channel_id=1, source_target_pairs={{0,4},{3,7},{4,0},{7,3},{8,12},{11,15},{12,8},{15,11},{16,20},{19,... | collective-permute-start | bytes 3158024 | tf_op jit(solution)/shard_map/ppermute | solution.py:1068
  40.4 24.4 %collective-permute-start.6 = (bf16[4112,128]{1,0:T(8,128)(2,1)}, bf16[4112,128]{1,0:T(8,128)(2,1)}, u32[]{:S(2)}, u32[]{:S(2)}) collective-permute-start(bf16[4112,128]{1,0:T(8,128)(2,1)} %collective-permute-done.4), channel_id=1, source_target_pairs={{0,1},{3,2},{4,5},{7,6},{8,9},{11,10},{12,13},{15,14},{16,17},{19,... | collective-permute-start | bytes 3158024 | tf_op jit(solution)/shard_map/ppermute | solution.py:1068
  42.7 24.4 %collective-permute-start.7 = (bf16[4112,128]{1,0:T(8,128)(2,1)}, bf16[4112,128]{1,0:T(8,128)(2,1)}, u32[]{:S(2)}, u32[]{:S(2)}) collective-permute-start(bf16[4112,128]{1,0:T(8,128)(2,1)} %collective-permute-done.4), channel_id=1, source_target_pairs={{0,8},{3,11},{4,12},{7,15},{8,16},{11,19},{12,20},{15,23},{16,24},... | collective-permute-start | bytes 3158024 | tf_op jit(solution)/shard_map/ppermute | solution.py:1068
  44.8 27.9 %collective-permute-start.11 = (bf16[4112,128]{1,0:T(8,128)(2,1)}, bf16[4112,128]{1,0:T(8,128)(2,1)}, u32[]{:S(2)}, u32[]{:S(2)}) collective-permute-start(bf16[4112,128]{1,0:T(8,128)(2,1)} %get-tuple-element.213), channel_id=1, source_target_pairs={{0,1},{3,2},{4,5},{7,6},{8,9},{11,10},{12,13},{15,14},{16,17},{19,... | collective-permute-start | bytes 3158024 | tf_op jit(solution)/shard_map/ppermute | solution.py:1068
  62.9 21.7 %collective-permute-start.13 = (bf16[4112,128]{1,0:T(8,128)(2,1)}, bf16[4112,128]{1,0:T(8,128)(2,1)}, u32[]{:S(2)}, u32[]{:S(2)}) collective-permute-start(bf16[4112,128]{1,0:T(8,128)(2,1)} %get-tuple-element.213), channel_id=1, source_target_pairs={{0,8},{3,11},{4,12},{7,15},{8,16},{11,19},{12,20},{15,23},{16,24},... | collective-permute-start | bytes 3158024 | tf_op jit(solution)/shard_map/ppermute | solution.py:1068
  64.8 22.5 %collective-permute-start.12 = (bf16[4112,128]{1,0:T(8,128)(2,1)}, bf16[4112,128]{1,0:T(8,128)(2,1)}, u32[]{:S(2)}, u32[]{:S(2)}) collective-permute-start(bf16[4112,128]{1,0:T(8,128)(2,1)} %get-tuple-element.214), channel_id=1, source_target_pairs={{0,1},{3,2},{4,5},{7,6},{8,9},{11,10},{12,13},{15,14},{16,17},{19,... | collective-permute-start | bytes 3158024 | tf_op jit(solution)/shard_map/ppermute | solution.py:1068
  67.1 25.4 %collective-permute-start.14 = (bf16[4112,128]{1,0:T(8,128)(2,1)}, bf16[4112,128]{1,0:T(8,128)(2,1)}, u32[]{:S(2)}, u32[]{:S(2)}) collective-permute-start(bf16[4112,128]{1,0:T(8,128)(2,1)} %get-tuple-element.216), channel_id=1, source_target_pairs={{0,4},{3,7},{4,0},{7,3},{8,12},{11,15},{12,8},{15,11},{16,20},{19,... | collective-permute-start | bytes 3158024 | tf_op jit(solution)/shard_map/ppermute | solution.py:1068
  70.5 24.4 %collective-permute-start.15 = (bf16[4112,128]{1,0:T(8,128)(2,1)}, bf16[4112,128]{1,0:T(8,128)(2,1)}, u32[]{:S(2)}, u32[]{:S(2)}) collective-permute-start(bf16[4112,128]{1,0:T(8,128)(2,1)} %get-tuple-element.216), channel_id=1, source_target_pairs={{0,1},{3,2},{4,5},{7,6},{8,9},{11,10},{12,13},{15,14},{16,17},{19,... | collective-permute-start | bytes 3158024 | tf_op jit(solution)/shard_map/ppermute | solution.py:1068
  72.7 24.4 %collective-permute-start.16 = (bf16[4112,128]{1,0:T(8,128)(2,1)}, bf16[4112,128]{1,0:T(8,128)(2,1)}, u32[]{:S(2)}, u32[]{:S(2)}) collective-permute-start(bf16[4112,128]{1,0:T(8,128)(2,1)} %get-tuple-element.217), channel_id=1, source_target_pairs={{1,5},{2,6},{5,1},{6,2},{9,13},{10,14},{13,9},{14,10},{17,21},{18,... | collective-permute-start | bytes 3158024 | tf_op jit(solution)/shard_map/ppermute | solution.py:1068
  84.6 24.4 %collective-permute-start.17 = (bf16[4112,128]{1,0:T(8,128)(2,1)}, bf16[4112,128]{1,0:T(8,128)(2,1)}, u32[]{:S(2)}, u32[]{:S(2)}) collective-permute-start(bf16[4112,128]{1,0:T(8,128)(2,1)} %get-tuple-element.216), channel_id=1, source_target_pairs={{0,8},{3,11},{4,12},{7,15},{8,16},{11,19},{12,20},{15,23},{16,24},... | collective-permute-start | bytes 3158024 | tf_op jit(solution)/shard_map/ppermute | solution.py:1068
  87.3 25.0 %collective-permute-start.19 = (bf16[4112,128]{1,0:T(8,128)(2,1)}, bf16[4112,128]{1,0:T(8,128)(2,1)S(1)}, u32[]{:S(2)}, u32[]{:S(2)}) collective-permute-start(bf16[4112,128]{1,0:T(8,128)(2,1)} %get-tuple-element.221), channel_id=1, source_target_pairs={{0,4},{3,7},{4,0},{7,3},{8,12},{11,15},{12,8},{15,11},{16,20},{19,... | collective-permute-start | bytes 3158024 | tf_op jit(solution)/shard_map/ppermute | solution.py:1068
  92.5 22.1 %collective-permute-start.20 = (bf16[4112,128]{1,0:T(8,128)(2,1)}, bf16[4112,128]{1,0:T(8,128)(2,1)}, u32[]{:S(2)}, u32[]{:S(2)}) collective-permute-start(bf16[4112,128]{1,0:T(8,128)(2,1)} %get-tuple-element.221), channel_id=1, source_target_pairs={{0,1},{3,2},{4,5},{7,6},{8,9},{11,10},{12,13},{15,14},{16,17},{19,... | collective-permute-start | bytes 3158024 | tf_op jit(solution)/shard_map/ppermute | solution.py:1068
  94.8 23.6 %collective-permute-start.21 = (bf16[4112,128]{1,0:T(8,128)(2,1)}, bf16[4112,128]{1,0:T(8,128)(2,1)}, u32[]{:S(2)}, u32[]{:S(2)}) collective-permute-start(bf16[4112,128]{1,0:T(8,128)(2,1)} %get-tuple-element.222), channel_id=1, source_target_pairs={{0,1},{3,2},{4,5},{7,6},{8,9},{11,10},{12,13},{15,14},{16,17},{19,... | collective-permute-start | bytes 3158024 | tf_op jit(solution)/shard_map/ppermute | solution.py:1068
  97.1 33.4 %collective-permute-start.22 = (bf16[4112,128]{1,0:T(8,128)(2,1)}, bf16[4112,128]{1,0:T(8,128)(2,1)}, u32[]{:S(2)}, u32[]{:S(2)}) collective-permute-start(bf16[4112,128]{1,0:T(8,128)(2,1)} %get-tuple-element.221), channel_id=1, source_target_pairs={{0,8},{3,11},{4,12},{7,15},{8,16},{11,19},{12,20},{15,23},{16,24},... | collective-permute-start | bytes 3158024 | tf_op jit(solution)/shard_map/ppermute | solution.py:1068
  108.9 24.2 %collective-permute-start.23 = (bf16[4112,128]{1,0:T(8,128)(2,1)}, bf16[4112,128]{1,0:T(8,128)(2,1)}, u32[]{:S(2)}, u32[]{:S(2)}) collective-permute-start(bf16[4112,128]{1,0:T(8,128)(2,1)} %get-tuple-element.227), channel_id=1, source_target_pairs={{0,4},{3,7},{4,0},{7,3},{8,12},{11,15},{12,8},{15,11},{16,20},{19,... | collective-permute-start | bytes 3158024 | tf_op jit(solution)/shard_map/ppermute | solution.py:1068
  112.4 23.8 %collective-permute-start.24 = (bf16[4112,128]{1,0:T(8,128)(2,1)}, bf16[4112,128]{1,0:T(8,128)(2,1)}, u32[]{:S(2)}, u32[]{:S(2)}) collective-permute-start(bf16[4112,128]{1,0:T(8,128)(2,1)} %get-tuple-element.227), channel_id=1, source_target_pairs={{0,1},{3,2},{4,5},{7,6},{8,9},{11,10},{12,13},{15,14},{16,17},{19,... | collective-permute-start | bytes 3158024 | tf_op jit(solution)/shard_map/ppermute | solution.py:1068
  114.6 22.9 %collective-permute-start.26 = (bf16[4112,128]{1,0:T(8,128)(2,1)}, bf16[4112,128]{1,0:T(8,128)(2,1)}, u32[]{:S(2)}, u32[]{:S(2)}) collective-permute-start(bf16[4112,128]{1,0:T(8,128)(2,1)} %get-tuple-element.227), channel_id=1, source_target_pairs={{0,8},{3,11},{4,12},{7,15},{8,16},{11,19},{12,20},{15,23},{16,24},... | collective-permute-start | bytes 3158024 | tf_op jit(solution)/shard_map/ppermute | solution.py:1068
  136.2 23.9 %collective-permute-start.29 = (bf16[4112,128]{1,0:T(8,128)(2,1)}, bf16[4112,128]{1,0:T(8,128)(2,1)S(1)}, u32[]{:S(2)}, u32[]{:S(2)}) collective-permute-start(bf16[4112,128]{1,0:T(8,128)(2,1)} %get-tuple-element.228), channel_id=1, source_target_pairs={{0,1},{3,2},{4,5},{7,6},{8,9},{11,10},{12,13},{15,14},{16,17},{19,... | collective-permute-start | bytes 3158024 | tf_op jit(solution)/shard_map/ppermute | solution.py:1068
  137.6 33.5 %collective-permute-start.30 = (bf16[4112,128]{1,0:T(8,128)(2,1)}, bf16[4112,128]{1,0:T(8,128)(2,1)}, u32[]{:S(2)}, u32[]{:S(2)}) collective-permute-start(bf16[4112,128]{1,0:T(8,128)(2,1)} %get-tuple-element.233), channel_id=1, source_target_pairs={{0,4},{3,7},{4,0},{7,3},{8,12},{11,15},{12,8},{15,11},{16,20},{19,... | collective-permute-start | bytes 3158024 | tf_op jit(solution)/shard_map/ppermute | solution.py:1068
  140.5 30.8 %collective-permute-start.31 = (bf16[4112,128]{1,0:T(8,128)(2,1)}, bf16[4112,128]{1,0:T(8,128)(2,1)}, u32[]{:S(2)}, u32[]{:S(2)}) collective-permute-start(bf16[4112,128]{1,0:T(8,128)(2,1)} %get-tuple-element.233), channel_id=1, source_target_pairs={{0,1},{3,2},{4,5},{7,6},{8,9},{11,10},{12,13},{15,14},{16,17},{19,... | collective-permute-start | bytes 3158024 | tf_op jit(solution)/shard_map/ppermute | solution.py:1068
  260.7 27.4 %collective-permute-start.18 = (bf16[1024,768]{1,0:T(8,128)(2,1)S(1)}, bf16[1024,768]{1,0:T(8,128)(2,1)S(1)}, u32[]{:S(2)}, u32[]{:S(2)}) collective-permute-start(bf16[1024,768]{1,0:T(8,128)(2,1)S(1)} %copy-done.191), channel_id=1, source_target_pairs={{0,2},{3,1},{4,6},{7,5},{8,10},{11,9},{12,14},{15,13},{16,18},{19,... | collective-permute-start | bytes 4718600 | tf_op jit(solution)/shard_map/ppermute | solution.py:1068
  304.8 24.1 %collective-permute-start.40 = (bf16[1024,768]{1,0:T(8,128)(2,1)S(1)}, bf16[1024,768]{1,0:T(8,128)(2,1)S(1)}, u32[]{:S(2)}, u32[]{:S(2)}) collective-permute-start(bf16[1024,768]{1,0:T(8,128)(2,1)S(1)} %get-tuple-element.271), channel_id=1, source_target_pairs={{0,2},{1,3},{2,0},{3,1},{4,6},{5,7},{6,4},{7,5},{8,10},{9,11},{10,... | collective-permute-start | bytes 4718600 | tf_op jit(solution)/shard_map/ppermute | solution.py:1068
  330.6 36.9 %collective-permute-start.41 = (bf16[1536,768]{1,0:T(8,128)(2,1)}, bf16[1536,768]{1,0:T(8,128)(2,1)}, u32[]{:S(2)}, u32[]{:S(2)}) collective-permute-start(bf16[1536,768]{1,0:T(8,128)(2,1)} %get-tuple-element.280.own), channel_id=1, source_target_pairs={{1,0},{2,3},{5,4},{6,7},{9,8},{10,11},{13,12},{14,15},{17,16},{18,... | collective-permute-start | bytes 7077896 | tf_op jit(solution)/shard_map/ppermute | solution.py:1068
  331.9 82.5 %collective-permute-start.43 = (bf16[768,1536]{1,0:T(8,128)(2,1)}, bf16[768,1536]{1,0:T(8,128)(2,1)}, u32[]{:S(2)}, u32[]{:S(2)}) collective-permute-start(bf16[768,1536]{1,0:T(8,128)(2,1)} %get-tuple-element.289.own), channel_id=1, source_target_pairs={{1,0},{2,3},{5,4},{6,7},{9,8},{10,11},{13,12},{14,15},{17,16},{18,... | collective-permute-start | bytes 7077896 | tf_op jit(solution)/shard_map/ppermute | solution.py:1068
  432.9 49.8 %collective-permute-start.48 = (bf16[768,768]{1,0:T(8,128)(2,1)S(1)}, bf16[768,768]{1,0:T(8,128)(2,1)}, u32[]{:S(2)}, u32[]{:S(2)}) collective-permute-start(bf16[768,768]{1,0:T(8,128)(2,1)S(1)} %shard_map.253), channel_id=1, source_target_pairs={{1,5},{2,6},{5,1},{6,2},{9,13},{10,14},{13,9},{14,10},{17,21},{18,... | collective-permute-start | bytes 3538952 | tf_op jit(solution)/shard_map/ppermute | solution.py:1068
  434.9 47.9 %collective-permute-start.49 = (bf16[384,1536]{1,0:T(8,128)(2,1)S(1)}, bf16[384,1536]{1,0:T(8,128)(2,1)}, u32[]{:S(2)}, u32[]{:S(2)}) collective-permute-start(bf16[384,1536]{1,0:T(8,128)(2,1)S(1)} %shard_map.254), channel_id=1, source_target_pairs={{1,5},{2,6},{5,1},{6,2},{9,13},{10,14},{13,9},{14,10},{17,21},{18,... | collective-permute-start | bytes 3538952 | tf_op jit(solution)/shard_map/ppermute | solution.py:1068
  455.4 27.3 %collective-permute-start.47 = (bf16[384,1152]{1,0:T(8,128)(2,1)S(1)}, bf16[384,1152]{1,0:T(8,128)(2,1)S(1)}, u32[]{:S(2)}, u32[]{:S(2)}) collective-permute-start(bf16[384,1152]{1,0:T(8,128)(2,1)S(1)} %shard_map.252), channel_id=1, source_target_pairs={{1,0},{2,3},{5,4},{6,7},{9,8},{10,11},{13,12},{14,15},{17,16},{18,... | collective-permute-start | bytes 2654216 | tf_op jit(solution)/shard_map/ppermute | solution.py:1068
  528.5 60.9 %collective-permute-start.57 = (bf16[384,1536]{1,0:T(8,128)(2,1)}, bf16[384,1536]{1,0:T(8,128)(2,1)}, u32[]{:S(2)}, u32[]{:S(2)}) collective-permute-start(bf16[384,1536]{1,0:T(8,128)(2,1)} %get-tuple-element.360), channel_id=1, source_target_pairs={{1,0},{2,3},{5,4},{6,7},{9,8},{10,11},{13,12},{14,15},{17,16},{18,... | collective-permute-start | bytes 3538952 | tf_op jit(solution)/shard_map/ppermute | solution.py:1068
  539.1 106.5 %collective-permute-start.53 = (bf16[1536,384]{1,0:T(8,128)(2,1)}, bf16[1536,384]{1,0:T(8,128)(2,1)}, u32[]{:S(2)}, u32[]{:S(2)}) collective-permute-start(bf16[1536,384]{1,0:T(8,128)(2,1)} %get-tuple-element.355), channel_id=1, source_target_pairs={{1,0},{2,3},{5,4},{6,7},{9,8},{10,11},{13,12},{14,15},{17,16},{18,... | collective-permute-start | bytes 3538952 | tf_op jit(solution)/shard_map/ppermute | solution.py:1068
  540.6 88.7 %collective-permute-start.54 = (bf16[384,1152]{1,0:T(8,128)(2,1)}, bf16[384,1152]{1,0:T(8,128)(2,1)}, u32[]{:S(2)}, u32[]{:S(2)}) collective-permute-start(bf16[384,1152]{1,0:T(8,128)(2,1)} %get-tuple-element.356), channel_id=1, source_target_pairs={{1,0},{2,3},{5,4},{6,7},{9,8},{10,11},{13,12},{14,15},{17,16},{18,... | collective-permute-start | bytes 2654216 | tf_op jit(solution)/shard_map/ppermute | solution.py:1068
  541.9 67.6 %collective-permute-start.56 = (bf16[384,768]{1,0:T(8,128)(2,1)S(1)}, bf16[384,768]{1,0:T(8,128)(2,1)S(1)}, u32[]{:S(2)}, u32[]{:S(2)}) collective-permute-start(bf16[384,768]{1,0:T(8,128)(2,1)S(1)} %copy-done.87), channel_id=1, source_target_pairs={{1,0},{2,3},{5,4},{6,7},{9,8},{10,11},{13,12},{14,15},{17,16},{18,... | collective-permute-start | bytes 1769480 | tf_op jit(solution)/shard_map/ppermute | solution.py:1068
  546.9 69.9 %collective-permute-start.55 = (bf16[16,16,128]{2,1,0:T(8,128)(2,1)}, bf16[16,16,128]{2,1,0:T(8,128)(2,1)S(1)}, u32[]{:S(2)}, u32[]{:S(2)}) collective-permute-start(bf16[16,16,128]{2,1,0:T(8,128)(2,1)} %get-tuple-element.357.own), channel_id=1, source_target_pairs={{1,0},{2,3},{5,4},{6,7},{9,8},{10,11},{13,12},{14,15},{17,16},{18,... | collective-permute-start | bytes 196616 | tf_op jit(solution)/shard_map/ppermute | solution.py:1068
  667.1 42.1 %collective-permute-start.63 = (bf16[4112,128]{1,0:T(8,128)(2,1)}, bf16[4112,128]{1,0:T(8,128)(2,1)S(1)}, u32[]{:S(2)}, u32[]{:S(2)}) collective-permute-start(bf16[4112,128]{1,0:T(8,128)(2,1)} %get-tuple-element.430), channel_id=1, source_target_pairs={{0,4},{3,7},{4,0},{7,3},{8,12},{11,15},{12,8},{15,11},{16,20},{19,... | collective-permute-start | bytes 3158024 | tf_op jit(solution)/shard_map/ppermute | solution.py:1068
  693.1 29.6 %collective-permute-start.64 = (bf16[4112,128]{1,0:T(8,128)(2,1)}, bf16[4112,128]{1,0:T(8,128)(2,1)S(1)}, u32[]{:S(2)}, u32[]{:S(2)}) collective-permute-start(bf16[4112,128]{1,0:T(8,128)(2,1)} %get-tuple-element.376), channel_id=1, source_target_pairs={{0,4},{3,7},{4,0},{7,3},{8,12},{11,15},{12,8},{15,11},{16,20},{19,... | collective-permute-start | bytes 3158024 | tf_op jit(solution)/shard_map/ppermute | solution.py:1068
  697.1 25.5 %collective-permute-start.65 = (bf16[4112,128]{1,0:T(8,128)(2,1)}, bf16[4112,128]{1,0:T(8,128)(2,1)S(1)}, u32[]{:S(2)}, u32[]{:S(2)}) collective-permute-start(bf16[4112,128]{1,0:T(8,128)(2,1)} %get-tuple-element.377), channel_id=1, source_target_pairs={{0,8},{3,11},{4,12},{7,15},{8,16},{11,19},{12,20},{15,23},{16,24},... | collective-permute-start | bytes 3158024 | tf_op jit(solution)/shard_map/ppermute | solution.py:1068
  709.2 61.4 %collective-permute-start.61 = (bf16[1024,768]{1,0:T(8,128)(2,1)}, bf16[1024,768]{1,0:T(8,128)(2,1)}, u32[]{:S(2)}, u32[]{:S(2)}) collective-permute-start(bf16[1024,768]{1,0:T(8,128)(2,1)} %add_convert_fusion), channel_id=1, source_target_pairs={{0,2},{1,3},{2,0},{3,1},{4,6},{5,7},{6,4},{7,5},{8,10},{9,11},{10,... | collective-permute-start | bytes 4718600 | tf_op jit(solution)/shard_map/ppermute | solution.py:1068
  718.8 22.2 %collective-permute-start.66 = (bf16[4112,128]{1,0:T(8,128)(2,1)}, bf16[4112,128]{1,0:T(8,128)(2,1)S(1)}, u32[]{:S(2)}, u32[]{:S(2)}) collective-permute-start(bf16[4112,128]{1,0:T(8,128)(2,1)} %get-tuple-element.380), channel_id=1, source_target_pairs={{0,4},{3,7},{4,0},{7,3},{8,12},{11,15},{12,8},{15,11},{16,20},{19,... | collective-permute-start | bytes 3158024 | tf_op jit(solution)/shard_map/ppermute | solution.py:1068
  720.7 22.8 %collective-permute-start.67 = (bf16[4112,128]{1,0:T(8,128)(2,1)}, bf16[4112,128]{1,0:T(8,128)(2,1)}, u32[]{:S(2)}, u32[]{:S(2)}) collective-permute-start(bf16[4112,128]{1,0:T(8,128)(2,1)} %get-tuple-element.381), channel_id=1, source_target_pairs={{0,8},{3,11},{4,12},{7,15},{8,16},{11,19},{12,20},{15,23},{16,24},... | collective-permute-start | bytes 3158024 | tf_op jit(solution)/shard_map/ppermute | solution.py:1068
  733.9 23.2 %collective-permute-start.68 = (bf16[4112,128]{1,0:T(8,128)(2,1)}, bf16[4112,128]{1,0:T(8,128)(2,1)S(1)}, u32[]{:S(2)}, u32[]{:S(2)}) collective-permute-start(bf16[4112,128]{1,0:T(8,128)(2,1)} %get-tuple-element.385), channel_id=1, source_target_pairs={{0,4},{3,7},{4,0},{7,3},{8,12},{11,15},{12,8},{15,11},{16,20},{19,... | collective-permute-start | bytes 3158024 | tf_op jit(solution)/shard_map/ppermute | solution.py:1068
  741.0 65.4 %collective-permute-start.59 = (bf16[1024,768]{1,0:T(8,128)(2,1)}, bf16[1024,768]{1,0:T(8,128)(2,1)}, u32[]{:S(2)}, u32[]{:S(2)}) collective-permute-start(bf16[1024,768]{1,0:T(8,128)(2,1)} %get-tuple-element.366), channel_id=1, source_target_pairs={{0,1},{3,2},{4,5},{7,6},{8,9},{11,10},{12,13},{15,14},{16,17},{19,... | collective-permute-start | bytes 4718600 | tf_op jit(solution)/shard_map/ppermute | solution.py:1068
  753.1 26.2 %collective-permute-start.70 = (bf16[4112,128]{1,0:T(8,128)(2,1)}, bf16[4112,128]{1,0:T(8,128)(2,1)S(1)}, u32[]{:S(2)}, u32[]{:S(2)}) collective-permute-start(bf16[4112,128]{1,0:T(8,128)(2,1)} %get-tuple-element.390), channel_id=1, source_target_pairs={{0,4},{3,7},{4,0},{7,3},{8,12},{11,15},{12,8},{15,11},{16,20},{19,... | collective-permute-start | bytes 3158024 | tf_op jit(solution)/shard_map/ppermute | solution.py:1068
  757.1 24.6 %collective-permute-start.71 = (bf16[4112,128]{1,0:T(8,128)(2,1)}, bf16[4112,128]{1,0:T(8,128)(2,1)}, u32[]{:S(2)}, u32[]{:S(2)}) collective-permute-start(bf16[4112,128]{1,0:T(8,128)(2,1)} %get-tuple-element.391), channel_id=1, source_target_pairs={{0,8},{3,11},{4,12},{7,15},{8,16},{11,19},{12,20},{15,23},{16,24},... | collective-permute-start | bytes 3158024 | tf_op jit(solution)/shard_map/ppermute | solution.py:1068
  768.7 24.6 %collective-permute-start.72 = (bf16[4112,128]{1,0:T(8,128)(2,1)S(1)}, bf16[4112,128]{1,0:T(8,128)(2,1)S(1)}, u32[]{:S(2)}, u32[]{:S(2)}) collective-permute-start(bf16[4112,128]{1,0:T(8,128)(2,1)S(1)} %get-tuple-element.395), channel_id=1, source_target_pairs={{0,4},{3,7},{4,0},{7,3},{8,12},{11,15},{12,8},{15,11},{16,20},{19,... | collective-permute-start | bytes 3158024 | tf_op jit(solution)/shard_map/ppermute | solution.py:1068
  770.6 24.6 %collective-permute-start.73 = (bf16[4112,128]{1,0:T(8,128)(2,1)}, bf16[4112,128]{1,0:T(8,128)(2,1)}, u32[]{:S(2)}, u32[]{:S(2)}) collective-permute-start(bf16[4112,128]{1,0:T(8,128)(2,1)} %get-tuple-element.396), channel_id=1, source_target_pairs={{0,8},{3,11},{4,12},{7,15},{8,16},{11,19},{12,20},{15,23},{16,24},... | collective-permute-start | bytes 3158024 | tf_op jit(solution)/shard_map/ppermute | solution.py:1068
  779.4 30.3 %collective-permute-start.62 = (bf16[1024,384]{1,0:T(8,128)(2,1)}, bf16[1024,384]{1,0:T(8,128)(2,1)}, u32[]{:S(2)}, u32[]{:S(2)}) collective-permute-start(bf16[1024,384]{1,0:T(8,128)(2,1)} %select_convert_fusion), channel_id=1, source_target_pairs={{0,1},{3,2},{4,5},{7,6},{8,9},{11,10},{12,13},{15,14},{16,17},{19,... | collective-permute-start | bytes 2359304 | tf_op jit(solution)/shard_map/ppermute | solution.py:1068
  791.3 22.1 %collective-permute-start.74 = (bf16[4112,128]{1,0:T(8,128)(2,1)}, bf16[4112,128]{1,0:T(8,128)(2,1)S(1)}, u32[]{:S(2)}, u32[]{:S(2)}) collective-permute-start(bf16[4112,128]{1,0:T(8,128)(2,1)} %get-tuple-element.400), channel_id=1, source_target_pairs={{0,4},{3,7},{4,0},{7,3},{8,12},{11,15},{12,8},{15,11},{16,20},{19,... | collective-permute-start | bytes 3158024 | tf_op jit(solution)/shard_map/ppermute | solution.py:1068
  (236 other events, 1447.4 us)

commit v6 on v5

--- a/solution.py
+++ b/solution.py
@@ -163,6 +163,10 @@
         ref[...] += value
 
 
+def stay(value):
+    return pltpu.with_memory_space_constraint(value, pltpu.HBM)
+
+
 def fence(*arrays):
     def nothing(*refs):
         pass
@@ -174,7 +178,7 @@
         in_specs=[anywhere] * len(arrays),
         out_specs=[anywhere] * len(arrays),
         input_output_aliases={i: i for i in range(len(arrays))},
-    )(*arrays)
+    )(*[stay(a) if a.size > 4 * MIB else a for a in arrays])
 
 
 def gather_kernel(slots, count_a, count_b, owner, drow, dcol, flag, *refs):
@@ -235,7 +239,7 @@
     return pl.pallas_call(
         functools.partial(gather_kernel, slots, len(first), len(second)),
         out_shape=(
-            jax.ShapeDtypeStruct((PANEL_ROWS, HALF), bf16),
+            pltpu.HBM((PANEL_ROWS, HALF), bf16),
             jax.ShapeDtypeStruct((owners, VEC_ROWS, BS), bf16),
         ),
         grid_spec=pltpu.PrefetchScalarGridSpec(
@@ -310,12 +314,12 @@
     arrived = pl.BlockSpec(
         (rows_n, cols_n), lambda i, pos, part: (jnp.clip(i - part[0] * span, 0, span - 1), 0)
     )
-    operands = [own] + ([recv] if paired else []) + ([] if target is None else [target])
+    operands = [own] + ([recv] if paired else []) + ([] if target is None else [stay(target)])
     specs = [block] + ([block if parts == 1 else arrived] if paired else [])
     specs += [] if target is None else [anywhere]
     return pl.pallas_call(
         functools.partial(scatter_kernel, rows_n, cols_n, steps, paired, parts),
-        out_shape=jax.ShapeDtypeStruct((total_rows, BS), bf16),
+        out_shape=pltpu.HBM((total_rows, BS), bf16),
         grid_spec=pltpu.PrefetchScalarGridSpec(
             num_scalar_prefetch=2,
             grid=(steps,),
@@ -395,10 +399,10 @@
     anywhere = pl.BlockSpec(memory_space=pl.ANY)
     block = fixed(own.shape)
     paired = recv is not None
-    operands = [own] + ([recv] if paired else []) + [target]
+    operands = [own] + ([recv] if paired else []) + [stay(target)]
     return pl.pallas_call(
         functools.partial(scatter_vec_kernel, paired),
-        out_shape=jax.ShapeDtypeStruct(target.shape, bf16),
+        out_shape=pltpu.HBM(target.shape, bf16),
         grid_spec=pltpu.PrefetchScalarGridSpec(
             num_scalar_prefetch=1,
             grid=(1,),
@@ -448,7 +452,7 @@
         ),
         compiler_params=params(),
         cost_estimate=cost(3 * tokens * size * D, tokens * size * 4 + size * D * 6),
-    )(present, half, patches, class_col, pinv)
+    )(present, half, patches, class_col, stay(pinv))
 
 
 def resize_kernel(base, pinv_ref, out, turned):
@@ -472,7 +476,7 @@
         scratch_shapes=[pltpu.VMEM((HALF, BASE_PIX), bf16)],
         compiler_params=params(),
         cost_estimate=cost(6 * D * BASE_PIX * HALF, 6 * D * BASE_PIX),
-    )(panels, pinv)
+    )(stay(panels), stay(pinv))
 
 
 def embed_back_kernel(core, base, own, recv, out, bias):
@@ -554,7 +558,7 @@
         ),
         compiler_params=params(),
         cost_estimate=cost(2 * tokens * BASE_PIX * HALF, tokens * BASE_PIX * 3),
-    )(half, *chunks, vec, panels)
+    )(half, *chunks, vec, stay(panels))
 
 
 def qkv_kernel(layer, first, core, *refs):
@@ -581,7 +585,7 @@
 def qkv_call(layer, base, own, recv, core, vec, panels):
     tokens = own.shape[0]
     shape = lambda width, kind: jax.ShapeDtypeStruct((tokens, width), kind)
-    outs = [shape(D, f32), shape(D, bf16)] + [shape(HALF, bf16)] * 3
+    outs = [shape(D, f32), pltpu.HBM((tokens, D), bf16)] + [shape(HALF, bf16)] * 3
     operands = ([] if base is None else [base]) + [own, recv]
     return pl.pallas_call(
         functools.partial(qkv_kernel, layer, base is None),
@@ -595,7 +599,7 @@
         ),
         compiler_params=params(),
         cost_estimate=cost(2 * tokens * D * 3 * HALF, tokens * D * 14),
-    )(core, *operands, vec, panels)
+    )(core, *operands, vec, stay(panels))
 
 
 def head_masks():
@@ -701,7 +705,7 @@
         ),
         compiler_params=params(),
         cost_estimate=cost(8 * HEADS * tokens * tokens * BS, tokens * D * 8, HEADS * tokens * tokens),
-    )(first, last, queries, keys, values, seg_col, seg_row, vec, panels)
+    )(first, last, queries, keys, values, seg_col, seg_row, vec, stay(panels))
 
 
 def gelu_parts(values):
@@ -730,7 +734,8 @@
 def mlp_call(layer, base, own, recv, vec, panels):
     tokens = base.shape[0]
     shape = lambda width, kind: jax.ShapeDtypeStruct((tokens, width), kind)
-    outs = [shape(D, f32), shape(D, bf16), shape(HALF_FF, bf16), shape(HALF_FF, bf16), shape(D, bf16)]
+    kept = lambda width: pltpu.HBM((tokens, width), bf16)
+    outs = [shape(D, f32), kept(D), kept(HALF_FF), kept(HALF_FF), shape(D, bf16)]
     return pl.pallas_call(
         functools.partial(mlp_kernel, layer),
         out_shape=outs,
@@ -744,7 +749,7 @@
         out_specs=[rows_spec(o.shape[1]) for o in outs],
         compiler_params=params(),
         cost_estimate=cost(4 * tokens * D * HALF_FF, tokens * D * 24, 2 * tokens * HALF_FF),
-    )(base, own, recv, vec, panels, panels)
+    )(base, own, recv, vec, stay(panels), stay(panels))
 
 
 def mlp_back_kernel(layer, summed, *refs):
@@ -799,7 +804,7 @@
         out_specs=[rows_spec(o.shape[1]) for o in outs] + [fixed(o.shape) for o in lines],
         compiler_params=params(),
         cost_estimate=cost(4 * tokens * D * HALF_FF, tokens * D * 24),
-    )(base, *extra, hid, slope, vec, panels, panels)
+    )(base, *extra, stay(hid), stay(slope), vec, stay(panels), stay(panels))
 
 
 def attend_back_kernel(
@@ -918,7 +923,10 @@
         ),
         compiler_params=params(),
         cost_estimate=cost(14 * HEADS * tokens * tokens * BS, tokens * D * 20, HEADS * tokens * tokens),
-    )(first, last, base, own, recv, queries, keys, values, mixed, lse, seg_col, seg_row, panels)
+    )(
+        first, last, base, own, recv, stay(queries), stay(keys), stay(values), stay(mixed), stay(lse),
+        seg_col, seg_row, stay(panels),
+    )
 
 
 def qkv_back_kernel(layer, dq, dk, dv, hid, vec, weight, back, dgain, dshift, dbq, dbv):
@@ -949,7 +957,7 @@
         out_specs=[rows_spec(D)] + [fixed(o.shape) for o in lines],
         compiler_params=params(),
         cost_estimate=cost(2 * tokens * D * 3 * HALF, tokens * D * 10),
-    )(dq, dk, dv, hid, vec, panels)
+    )(dq, dk, dv, stay(hid), vec, stay(panels))
 
 
 def split(values):
@@ -1008,7 +1016,7 @@
         ),
         compiler_params=params(),
         cost_estimate=cost(count * 88 * BS**3, count * BS * BS * 38),
-    )(used, home, near, far, *arrays)
+    )(used, home, near, far, *[stay(a) for a in arrays])
 
 
 def reduce_kernel(carrying, last, *refs):
@@ -1029,10 +1037,10 @@
     last = j == 3
     at = lambda j, x_rel: pl.BlockSpec((payload, BS), lambda i: ((j * 2 + x_rel) * 2 + n, 0))
     whole = fixed((payload, BS))
-    operands = [buffer, arrived] + ([] if carried is None else [carried])
+    operands = [stay(buffer), arrived] + ([] if carried is None else [carried])
     specs = [at(j, 0)] + [whole] * (len(operands) - 1)
     if not last:
-        operands.append(buffer)
+        operands.append(stay(buffer))
         specs.append(at(j + 1, 1))
     outs = [jax.ShapeDtypeStruct((payload, BS), bf16)] * (1 if last else 2)
     made = pl.pallas_call(

time: 849 us -> 703 us (0.83)
  local copies, waits for them, and re-layouts: 290 us -> 80.1 us
  waiting for transfers between devices: 58.8 us -> 96.1 us
  Pallas kernels: 242 us -> 274 us
    unnamed x416 -> x314, local copies, waits for them, and re-layouts: 286 us -> 74.8 us
    ppermute x77, waiting for transfers between devices: 58.8 us -> 96.1 us  [send(): return lax.ppermute(value, AXES, route)]
    pallas_call x10, Pallas kernels: 41.6 us -> 26.7 us  [scatter_matrix(): pl.pallas_call(functools.partial(scatter_kernel, rows_n, cols_n, steps, p...]
  transfers between devices with their start and end apart: 77 -> 77, of which waited for: 16 -> 26; matrix products, arithmetic and copies ran while one was open for 7% -> 9% of each run, Pallas kernels for 19% -> 26%
where the time goes in v6:
time: 703 us; the launch traced here: 692 us
  Pallas kernels  274 us (39%)
  starting transfers between devices  176 us (25%)
  waiting for transfers between devices  96.1 us (14%)
  local copies, waits for them, and re-layouts  80.1 us (11%)
  matrix products  36.4 us (5%)
  other arithmetic  26.5 us (4%)
    ppermute x77, starting transfers between devices, send(): return lax.ppermute(value, AXES, route)  176 us
    ppermute x77, waiting for transfers between devices, send(): return lax.ppermute(value, AXES, route)  96.1 us
    unnamed x314, local copies, waits for them, and re-layouts  74.8 us
    pallas_call x2, Pallas kernels, attend_back_call(): pl.pallas_call(attend_back_kernel, out_shape=[shape(D, f32), shape(D, bf1...  46.1 us
    pallas_call x2, Pallas kernels, attend_call(): pl.pallas_call(functools.partial(attend_kernel, layer), out_shape=[jax.Sh...  32.4 us
    dot_general x12, matrix products, dot_tn(): lax.dot_general(left, right, (((0,), (0,)), ((), ())), preferred_element_...  32.2 us
    pallas_call x10, Pallas kernels, scatter_matrix(): pl.pallas_call(functools.partial(scatter_kernel, rows_n, cols_n, steps, p...  26.7 us
    pallas_call x2, Pallas kernels, mlp_back_call(): pl.pallas_call(functools.partial(mlp_back_kernel, layer, summed), out_sha...  25.3 us
  transfers between devices with their start and end apart: 77, of which 26 were waited for; matrix products, arithmetic and copies ran while one was open for 9% of the time, Pallas kernels for 26%

profile of v6, /device:TPU:0, one launch (start us, length us, event | category | flops | bytes accessed | tf_op | source)
XLA Modules:
  0.0 691.8 jit_solution(1699755024581672330)
XLA Ops:
  20.2 5.1 collective-permute-done.refs_1_
  25.6 8.4 %collective-permute-done.2.refs_3_ = bf16[4112,128]{1,0:T(8,128)(2,1)} collective-permute-done((bf16[4112,128]{1,0:T(8,128)(2,1)}, bf16[4112,128]{1,0:T(8,128)(2,1)}, u32[]{:S(2)}, u32[]{:S(2)}) %collective-permute-start.2) | collective-permute-done | bytes 1052704 | tf_op jit(solution)/shard_map/ppermute | solution.py:1076
  49.9 5.5 shard_map.223.refs_4_
  56.6 6.3 collective-permute-done.5.refs_1_
  74.4 6.0 shard_map.225.refs_5_
  87.4 5.1 collective-permute-done.14.refs_1_
  99.0 5.5 shard_map.227.refs_5_
  119.4 5.7 shard_map.229.refs_5_
  129.7 4.0 collective-permute-start.28
  137.0 11.7 %collective-permute-start.31 = (bf16[4112,128]{1,0:T(8,128)(2,1)}, bf16[4112,128]{1,0:T(8,128)(2,1)}, u32[]{:S(2)}, u32[]{:S(2)}) collective-permute-start(bf16[4112,128]{1,0:T(8,128)(2,1)} %get-tuple-element.233), channel_id=1, source_target_pairs={{0,1},{3,2},{4,5},{7,6},{8,9},{11,10},{12,13},{15,14},{16,17},{19,... | collective-permute-start | bytes 3158024 | tf_op jit(solution)/shard_map/ppermute | solution.py:1076
  150.4 7.1 %collective-permute-done.29.refs_3_ = bf16[4112,128]{1,0:T(8,128)(2,1)S(1)} collective-permute-done((bf16[4112,128]{1,0:T(8,128)(2,1)}, bf16[4112,128]{1,0:T(8,128)(2,1)S(1)}, u32[]{:S(2)}, u32[]{:S(2)}) %collective-permute-start.29) | collective-permute-done | bytes 1052704 | tf_op jit(solution)/shard_map/ppermute | solution.py:1076
  158.6 5.3 collective-permute-start.33
  163.8 4.0 collective-permute-done.30.refs_1_
  171.3 8.7 %collective-permute-done.33 = bf16[4112,128]{1,0:T(8,128)(2,1)} collective-permute-done((bf16[4112,128]{1,0:T(8,128)(2,1)}, bf16[4112,128]{1,0:T(8,128)(2,1)}, u32[]{:S(2)}, u32[]{:S(2)}) %collective-permute-start.33) | collective-permute-done | bytes 1052704 | tf_op jit(solution)/shard_map/ppermute | solution.py:1076
  185.0 15.3 %shard_map.234 = (bf16[21504,384]{1,0:T(8,128)(2,1)}, bf16[16,16,128]{2,1,0:T(8,128)(2,1)S(1)}) custom-call(s32[16]{0:T(128)S(1)} %stack.95.owner, s32[512]{0:T(512)S(1)} %broadcast_select_fusion.3.drow, s32[512]{0:T(512)S(1)} %get-tuple-element.416.dcol, s32[1]{0:T(128)} %bitcast.27.flag.home, bf16[1,4112,128]{2,1,0:T(8,128)(2,1)S(1)} %copy-done.81, ...), custom_call_target="tpu_custom_call" | custom-call | bytes 33030144 | tf_op jit(solution)/shard_map/pallas_call | solution.py:239
  200.5 5.7 shard_map.235.refs_0_
  210.6 5.6 shard_map.236
  216.3 16.2 %shard_map.237 = (bf16[1024,384]{1,0:T(8,128)(2,1)S(1)}, f32[8,1024]{1,0:T(8,128)S(1)}, bf16[1024,768]{1,0:T(8,128)(2,1)S(1)}) custom-call(s32[4]{0:T(128)S(1)} %get-tuple-element.451.low_ref, s32[4]{0:T(128)S(1)} %get-tuple-element.444.high_ref, bf16[1024,384]{1,0:T(8,128)(2,1)S(1)} %get-tuple-element.253.q_ref, ...), custom_call_target="tpu_custom_call" | custom-call | flops 6442450944 | bytes 6291456 | tf_op jit(solution)/shard_map/pallas_call | solution.py:676
  236.0 11.8 %shard_map.238 = (f32[1024,768]{1,0:T(8,128)S(1)}, bf16[1024,768]{1,0:T(8,128)(2,1)}, bf16[1024,1536]{1,0:T(8,128)(2,1)}, bf16[1024,1536]{1,0:T(8,128)(2,1)}, bf16[1024,768]{1,0:T(8,128)(2,1)S(1)}) custom-call(f32[1024,768]{1,0:T(8,128)S(1)} %get-tuple-element.252.base.hid, bf16[1024,768]{1,0:T(8,128)(2,1)S(1)} %get-tuple-element.256.own, ...), custom_call_target="tpu_custom_call" | custom-call | flops 4831838208 | bytes 18874368 | tf_op jit(solution)/shard_map/pallas_call | solution.py:739
  251.3 5.8 shard_map.239
  257.1 16.2 %shard_map.240 = (bf16[1024,384]{1,0:T(8,128)(2,1)S(1)}, f32[8,1024]{1,0:T(8,128)S(1)}, bf16[1024,768]{1,0:T(8,128)(2,1)S(1)}) custom-call(s32[4]{0:T(128)S(1)} %get-tuple-element.451.low_ref, s32[4]{0:T(128)S(1)} %get-tuple-element.444.high_ref, bf16[1024,384]{1,0:T(8,128)(2,1)S(1)} %get-tuple-element.260.q_ref, ...), custom_call_target="tpu_custom_call" | custom-call | flops 6442450944 | bytes 6291456 | tf_op jit(solution)/shard_map/pallas_call | solution.py:676
  276.9 11.8 %shard_map.241 = (f32[1024,768]{1,0:T(8,128)S(1)}, bf16[1024,768]{1,0:T(8,128)(2,1)}, bf16[1024,1536]{1,0:T(8,128)(2,1)}, bf16[1024,1536]{1,0:T(8,128)(2,1)}, bf16[1024,768]{1,0:T(8,128)(2,1)S(1)}) custom-call(f32[1024,768]{1,0:T(8,128)S(1)} %get-tuple-element.259.base.hid, bf16[1024,768]{1,0:T(8,128)(2,1)S(1)} %get-tuple-element.263.own, ...), custom_call_target="tpu_custom_call" | custom-call | flops 4831838208 | bytes 18874368 | tf_op jit(solution)/shard_map/pallas_call | solution.py:739
  290.6 12.7 %shard_map.242 = (bf16[1024,768]{1,0:T(8,128)(2,1)S(1)}, bf16[1024,1536]{1,0:T(8,128)(2,1)S(1)}, bf16[1024,768]{1,0:T(8,128)(2,1)S(1)}, f32[1,768]{1,0:T(1,128)S...) custom-call(bf16[1024,768]{1,0:T(8,128)(2,1)S(1)} %broadcast_select_fusion.refs_0_, ...), custom_call_target="tpu_custom_call" | custom-call | flops 4831838208 | bytes 18874368 | tf_op jit(solution)/shard_map/pallas_call | solution.py:791
  303.6 4.0 convolution_convert_fusion.2.refs_3_
  307.6 4.0 convolution_convert_fusion.3.refs_2_
  319.2 23.2 %shard_map.244 = (f32[1024,768]{1,0:T(8,128)S(1)}, bf16[1024,768]{1,0:T(8,128)(2,1)S(1)}, bf16[1024,384]{1,0:T(8,128)(2,1)S(1)}, bf16[1024,384]{1,0:T(8,128)(2,1...) custom-call(s32[4]{0:T(128)S(1)} %get-tuple-element.450.low_ref, s32[4]{0:T(128)S(1)} %get-tuple-element.445.high_ref, ...), custom_call_target="tpu_custom_call" | custom-call | flops 11274289152 | bytes 15728640 | tf_op jit(solution)/shard_map/pallas_call | solution.py:883
  351.5 6.3 shard_map.246
  357.8 8.2 %collective-permute-start.42 = (bf16[1024,768]{1,0:T(8,128)(2,1)S(1)}, bf16[1024,768]{1,0:T(8,128)(2,1)S(1)}, u32[]{:S(2)}, u32[]{:S(2)}) collective-permute-start(bf16[1024,768]{1,0:T(8,128)(2,1)S(1)} %get-tuple-element.284.refs_1_), channel_id=1, source_target_pairs={{0,2},{1,3},{2,0},{3,1},{4,6},{5,7},{6,4},{7,5},{8,10},{9,11},{10,... | collective-permute-start | bytes 4718600 | tf_op jit(solution)/shard_map/ppermute | solution.py:1076
  367.8 3.5 convolution_convert_fusion.5.refs_4_
  371.2 12.7 %shard_map.247 = (f32[1024,768]{1,0:T(8,128)S(1)}, bf16[1024,768]{1,0:T(8,128)(2,1)S(1)}, bf16[1024,1536]{1,0:T(8,128)(2,1)S(1)}, bf16[1024,768]{1,0:T(8,128)(2,...) custom-call(f32[1024,768]{1,0:T(8,128)S(1)} %copy-done.102, ...), custom_call_target="tpu_custom_call" | custom-call | flops 4831838208 | bytes 18874368 | tf_op jit(solution)/shard_map/pallas_call | solution.py:791
  395.0 6.0 convolution_convert_fusion.refs_3_
  401.0 3.9 convolution_convert_fusion.1.refs_2_
  413.8 3.8 shard_map.255.refs_1_
  422.3 23.0 %shard_map.251 = (f32[1024,768]{1,0:T(8,128)S(1)}, bf16[1024,768]{1,0:T(8,128)(2,1)S(1)}, bf16[1024,384]{1,0:T(8,128)(2,1)S(1)}, bf16[1024,384]{1,0:T(8,128)(2,1...) custom-call(s32[4]{0:T(128)S(1)} %get-tuple-element.450.low_ref, s32[4]{0:T(128)S(1)} %get-tuple-element.445.high_ref, ...), custom_call_target="tpu_custom_call" | custom-call | flops 11274289152 | bytes 15728640 | tf_op jit(solution)/shard_map/pallas_call | solution.py:883
  460.5 6.2 shard_map.261
  468.6 3.5 convolution_convert_fusion.4.refs_2_
  503.8 4.4 collective-permute-done.58.refs_0_
  514.4 3.8 shard_map.273.refs_1_
  520.8 3.7 shard_map.274.refs_0_
  526.3 22.9 %collective-permute-done.56.refs_0_ = bf16[384,768]{1,0:T(8,128)(2,1)S(1)} collective-permute-done((bf16[384,768]{1,0:T(8,128)(2,1)S(1)}, bf16[384,768]{1,0:T(8,128)(2,1)S(1)}, u32[]{:S(2)}, u32[]{:S(2)}) %collective-permute-start.56) | collective-permute-done | bytes 589856 | tf_op jit(solution)/shard_map/ppermute | solution.py:1076
  564.1 3.9 collective-permute-start.63
  568.0 10.2 %shard_map.281.refs_2_ = bf16[3,384,768]{2,1,0:T(8,128)(2,1)S(1)} custom-call(bf16[21504,384]{1,0:T(8,128)(2,1)} %get-tuple-element.371.base, bf16[3,3072,768]{2,1,0:T(8,128)(2,1)} %pinv_ref.9), custom_call_target="tpu_custom_call" | custom-call | flops 5435817984 | bytes 14155776 | tf_op jit(solution)/shard_map/pallas_call | solution.py:467
  598.0 3.8 collective-permute-start.66
  611.8 3.8 collective-permute-start.68
  628.7 3.6 collective-permute-start.71
  652.8 3.9 collective-permute-start.74
  668.8 3.7 convert_select_fusion
  681.2 10.2 %shard_map.298 = (f32[32,128,128]{2,1,0:T(8,128)}, f32[32,128,128]{2,1,0:T(8,128)}, f32[32,128,128]{2,1,0:T(8,128)}, f32[32,128,128]{2,1,0:T(8,128)}) custom-call(s32[32]{0:T(128)S(1)} %convert_element_type.160.used, s32[1]{0:T(128)} %bitcast.27.flag.home, bf16[4112,128]{1,0:T(8,128)(2,1)S(1)} %shard_map.296.near, ...), custom_call_target="tpu_custom_call" | custom-call | flops 5905580032 | bytes 19922944 | tf_op jit(solution)/shard_map/pallas_call | solution.py:1008
  (579 shorter events, 313.0 us)
Async XLA Ops:
  0.7 44.1 %collective-permute-start.9 = (bf16[1024,768]{1,0:T(8,128)(2,1)}, bf16[1024,768]{1,0:T(8,128)(2,1)S(1)}, u32[]{:S(2)}, u32[]{:S(2)}) collective-permute-start(bf16[1024,768]{1,0:T(8,128)(2,1)} %param.15), channel_id=1, source_target_pairs={{0,2},{3,1},{4,6},{7,5},{8,10},{11,9},{12,14},{15,13},{16,18},{19,... | collective-permute-start | bytes 4718600 | tf_op jit(solution)/shard_map/ppermute | solution.py:1076
  18.6 19.2 %collective-permute-start.4 = (bf16[4112,128]{1,0:T(8,128)(2,1)}, bf16[4112,128]{1,0:T(8,128)(2,1)}, u32[]{:S(2)}, u32[]{:S(2)}) collective-permute-start(bf16[4112,128]{1,0:T(8,128)(2,1)} %get-tuple-element.433), channel_id=1, source_target_pairs={{1,3},{2,0},{5,7},{6,4},{9,11},{10,8},{13,15},{14,12},{17,19},{18,... | collective-permute-start | bytes 3158024 | tf_op jit(solution)/shard_map/ppermute | solution.py:1076
  34.6 35.8 %collective-permute-start.10 = (bf16[4112,128]{1,0:T(8,128)(2,1)}, bf16[4112,128]{1,0:T(8,128)(2,1)S(1)}, u32[]{:S(2)}, u32[]{:S(2)}) collective-permute-start(bf16[4112,128]{1,0:T(8,128)(2,1)} %get-tuple-element.213), channel_id=1, source_target_pairs={{0,4},{3,7},{4,0},{7,3},{8,12},{11,15},{12,8},{15,11},{16,20},{19,... | collective-permute-start | bytes 3158024 | tf_op jit(solution)/shard_map/ppermute | solution.py:1076
  37.9 25.0 %collective-permute-start.5 = (bf16[4112,128]{1,0:T(8,128)(2,1)}, bf16[4112,128]{1,0:T(8,128)(2,1)}, u32[]{:S(2)}, u32[]{:S(2)}) collective-permute-start(bf16[4112,128]{1,0:T(8,128)(2,1)} %collective-permute-done.4), channel_id=1, source_target_pairs={{0,4},{3,7},{4,0},{7,3},{8,12},{11,15},{12,8},{15,11},{16,20},{19,... | collective-permute-start | bytes 3158024 | tf_op jit(solution)/shard_map/ppermute | solution.py:1076
  40.4 24.4 %collective-permute-start.6 = (bf16[4112,128]{1,0:T(8,128)(2,1)}, bf16[4112,128]{1,0:T(8,128)(2,1)}, u32[]{:S(2)}, u32[]{:S(2)}) collective-permute-start(bf16[4112,128]{1,0:T(8,128)(2,1)} %collective-permute-done.4), channel_id=1, source_target_pairs={{0,1},{3,2},{4,5},{7,6},{8,9},{11,10},{12,13},{15,14},{16,17},{19,... | collective-permute-start | bytes 3158024 | tf_op jit(solution)/shard_map/ppermute | solution.py:1076
  42.7 24.4 %collective-permute-start.7 = (bf16[4112,128]{1,0:T(8,128)(2,1)}, bf16[4112,128]{1,0:T(8,128)(2,1)}, u32[]{:S(2)}, u32[]{:S(2)}) collective-permute-start(bf16[4112,128]{1,0:T(8,128)(2,1)} %collective-permute-done.4), channel_id=1, source_target_pairs={{0,8},{3,11},{4,12},{7,15},{8,16},{11,19},{12,20},{15,23},{16,24},... | collective-permute-start | bytes 3158024 | tf_op jit(solution)/shard_map/ppermute | solution.py:1076
  44.8 27.9 %collective-permute-start.11 = (bf16[4112,128]{1,0:T(8,128)(2,1)}, bf16[4112,128]{1,0:T(8,128)(2,1)}, u32[]{:S(2)}, u32[]{:S(2)}) collective-permute-start(bf16[4112,128]{1,0:T(8,128)(2,1)} %get-tuple-element.213), channel_id=1, source_target_pairs={{0,1},{3,2},{4,5},{7,6},{8,9},{11,10},{12,13},{15,14},{16,17},{19,... | collective-permute-start | bytes 3158024 | tf_op jit(solution)/shard_map/ppermute | solution.py:1076
  64.8 19.5 %collective-permute-start.12 = (bf16[4112,128]{1,0:T(8,128)(2,1)}, bf16[4112,128]{1,0:T(8,128)(2,1)}, u32[]{:S(2)}, u32[]{:S(2)}) collective-permute-start(bf16[4112,128]{1,0:T(8,128)(2,1)} %get-tuple-element.214), channel_id=1, source_target_pairs={{0,1},{3,2},{4,5},{7,6},{8,9},{11,10},{12,13},{15,14},{16,17},{19,... | collective-permute-start | bytes 3158024 | tf_op jit(solution)/shard_map/ppermute | solution.py:1076
  67.1 25.4 %collective-permute-start.14 = (bf16[4112,128]{1,0:T(8,128)(2,1)}, bf16[4112,128]{1,0:T(8,128)(2,1)}, u32[]{:S(2)}, u32[]{:S(2)}) collective-permute-start(bf16[4112,128]{1,0:T(8,128)(2,1)} %get-tuple-element.216), channel_id=1, source_target_pairs={{0,4},{3,7},{4,0},{7,3},{8,12},{11,15},{12,8},{15,11},{16,20},{19,... | collective-permute-start | bytes 3158024 | tf_op jit(solution)/shard_map/ppermute | solution.py:1076
  70.4 24.3 %collective-permute-start.15 = (bf16[4112,128]{1,0:T(8,128)(2,1)}, bf16[4112,128]{1,0:T(8,128)(2,1)}, u32[]{:S(2)}, u32[]{:S(2)}) collective-permute-start(bf16[4112,128]{1,0:T(8,128)(2,1)} %get-tuple-element.216), channel_id=1, source_target_pairs={{0,1},{3,2},{4,5},{7,6},{8,9},{11,10},{12,13},{15,14},{16,17},{19,... | collective-permute-start | bytes 3158024 | tf_op jit(solution)/shard_map/ppermute | solution.py:1076
  72.7 24.4 %collective-permute-start.16 = (bf16[4112,128]{1,0:T(8,128)(2,1)}, bf16[4112,128]{1,0:T(8,128)(2,1)}, u32[]{:S(2)}, u32[]{:S(2)}) collective-permute-start(bf16[4112,128]{1,0:T(8,128)(2,1)} %get-tuple-element.217), channel_id=1, source_target_pairs={{1,5},{2,6},{5,1},{6,2},{9,13},{10,14},{13,9},{14,10},{17,21},{18,... | collective-permute-start | bytes 3158024 | tf_op jit(solution)/shard_map/ppermute | solution.py:1076
  81.7 24.0 %collective-permute-start.17 = (bf16[4112,128]{1,0:T(8,128)(2,1)}, bf16[4112,128]{1,0:T(8,128)(2,1)}, u32[]{:S(2)}, u32[]{:S(2)}) collective-permute-start(bf16[4112,128]{1,0:T(8,128)(2,1)} %get-tuple-element.216), channel_id=1, source_target_pairs={{0,8},{3,11},{4,12},{7,15},{8,16},{11,19},{12,20},{15,23},{16,24},... | collective-permute-start | bytes 3158024 | tf_op jit(solution)/shard_map/ppermute | solution.py:1076
  84.3 24.8 %collective-permute-start.19 = (bf16[4112,128]{1,0:T(8,128)(2,1)}, bf16[4112,128]{1,0:T(8,128)(2,1)S(1)}, u32[]{:S(2)}, u32[]{:S(2)}) collective-permute-start(bf16[4112,128]{1,0:T(8,128)(2,1)} %get-tuple-element.221), channel_id=1, source_target_pairs={{0,4},{3,7},{4,0},{7,3},{8,12},{11,15},{12,8},{15,11},{16,20},{19,... | collective-permute-start | bytes 3158024 | tf_op jit(solution)/shard_map/ppermute | solution.py:1076
  94.8 23.0 %collective-permute-start.21 = (bf16[4112,128]{1,0:T(8,128)(2,1)}, bf16[4112,128]{1,0:T(8,128)(2,1)}, u32[]{:S(2)}, u32[]{:S(2)}) collective-permute-start(bf16[4112,128]{1,0:T(8,128)(2,1)} %get-tuple-element.222), channel_id=1, source_target_pairs={{0,1},{3,2},{4,5},{7,6},{8,9},{11,10},{12,13},{15,14},{16,17},{19,... | collective-permute-start | bytes 3158024 | tf_op jit(solution)/shard_map/ppermute | solution.py:1076
  97.1 29.2 %collective-permute-start.22 = (bf16[4112,128]{1,0:T(8,128)(2,1)}, bf16[4112,128]{1,0:T(8,128)(2,1)}, u32[]{:S(2)}, u32[]{:S(2)}) collective-permute-start(bf16[4112,128]{1,0:T(8,128)(2,1)} %get-tuple-element.221), channel_id=1, source_target_pairs={{0,8},{3,11},{4,12},{7,15},{8,16},{11,19},{12,20},{15,23},{16,24},... | collective-permute-start | bytes 3158024 | tf_op jit(solution)/shard_map/ppermute | solution.py:1076
  105.7 23.9 %collective-permute-start.23 = (bf16[4112,128]{1,0:T(8,128)(2,1)}, bf16[4112,128]{1,0:T(8,128)(2,1)}, u32[]{:S(2)}, u32[]{:S(2)}) collective-permute-start(bf16[4112,128]{1,0:T(8,128)(2,1)} %get-tuple-element.227), channel_id=1, source_target_pairs={{0,4},{3,7},{4,0},{7,3},{8,12},{11,15},{12,8},{15,11},{16,20},{19,... | collective-permute-start | bytes 3158024 | tf_op jit(solution)/shard_map/ppermute | solution.py:1076
  109.1 24.6 %collective-permute-start.24 = (bf16[4112,128]{1,0:T(8,128)(2,1)}, bf16[4112,128]{1,0:T(8,128)(2,1)}, u32[]{:S(2)}, u32[]{:S(2)}) collective-permute-start(bf16[4112,128]{1,0:T(8,128)(2,1)} %get-tuple-element.227), channel_id=1, source_target_pairs={{0,1},{3,2},{4,5},{7,6},{8,9},{11,10},{12,13},{15,14},{16,17},{19,... | collective-permute-start | bytes 3158024 | tf_op jit(solution)/shard_map/ppermute | solution.py:1076
  111.4 23.7 %collective-permute-start.26 = (bf16[4112,128]{1,0:T(8,128)(2,1)}, bf16[4112,128]{1,0:T(8,128)(2,1)}, u32[]{:S(2)}, u32[]{:S(2)}) collective-permute-start(bf16[4112,128]{1,0:T(8,128)(2,1)} %get-tuple-element.227), channel_id=1, source_target_pairs={{0,8},{3,11},{4,12},{7,15},{8,16},{11,19},{12,20},{15,23},{16,24},... | collective-permute-start | bytes 3158024 | tf_op jit(solution)/shard_map/ppermute | solution.py:1076
  126.3 22.4 %collective-permute-start.27 = (bf16[4112,128]{1,0:T(8,128)(2,1)}, bf16[4112,128]{1,0:T(8,128)(2,1)S(1)}, u32[]{:S(2)}, u32[]{:S(2)}) collective-permute-start(bf16[4112,128]{1,0:T(8,128)(2,1)} %get-tuple-element.232), channel_id=1, source_target_pairs={{0,4},{3,7},{4,0},{7,3},{8,12},{11,15},{12,8},{15,11},{16,20},{19,... | collective-permute-start | bytes 3158024 | tf_op jit(solution)/shard_map/ppermute | solution.py:1076
  129.7 20.7 %collective-permute-start.28 = (bf16[4112,128]{1,0:T(8,128)(2,1)}, bf16[4112,128]{1,0:T(8,128)(2,1)S(1)}, u32[]{:S(2)}, u32[]{:S(2)}) collective-permute-start(bf16[4112,128]{1,0:T(8,128)(2,1)} %get-tuple-element.232), channel_id=1, source_target_pairs={{0,1},{3,2},{4,5},{7,6},{8,9},{11,10},{12,13},{15,14},{16,17},{19,... | collective-permute-start | bytes 3158024 | tf_op jit(solution)/shard_map/ppermute | solution.py:1076
  133.7 23.9 %collective-permute-start.29 = (bf16[4112,128]{1,0:T(8,128)(2,1)}, bf16[4112,128]{1,0:T(8,128)(2,1)S(1)}, u32[]{:S(2)}, u32[]{:S(2)}) collective-permute-start(bf16[4112,128]{1,0:T(8,128)(2,1)} %get-tuple-element.228), channel_id=1, source_target_pairs={{0,1},{3,2},{4,5},{7,6},{8,9},{11,10},{12,13},{15,14},{16,17},{19,... | collective-permute-start | bytes 3158024 | tf_op jit(solution)/shard_map/ppermute | solution.py:1076
  135.1 32.8 %collective-permute-start.30 = (bf16[4112,128]{1,0:T(8,128)(2,1)}, bf16[4112,128]{1,0:T(8,128)(2,1)}, u32[]{:S(2)}, u32[]{:S(2)}) collective-permute-start(bf16[4112,128]{1,0:T(8,128)(2,1)} %get-tuple-element.233), channel_id=1, source_target_pairs={{0,4},{3,7},{4,0},{7,3},{8,12},{11,15},{12,8},{15,11},{16,20},{19,... | collective-permute-start | bytes 3158024 | tf_op jit(solution)/shard_map/ppermute | solution.py:1076
  137.0 31.8 %collective-permute-start.31 = (bf16[4112,128]{1,0:T(8,128)(2,1)}, bf16[4112,128]{1,0:T(8,128)(2,1)}, u32[]{:S(2)}, u32[]{:S(2)}) collective-permute-start(bf16[4112,128]{1,0:T(8,128)(2,1)} %get-tuple-element.233), channel_id=1, source_target_pairs={{0,1},{3,2},{4,5},{7,6},{8,9},{11,10},{12,13},{15,14},{16,17},{19,... | collective-permute-start | bytes 3158024 | tf_op jit(solution)/shard_map/ppermute | solution.py:1076
  148.7 20.1 %collective-permute-start.32 = (bf16[4112,128]{1,0:T(8,128)(2,1)}, bf16[4112,128]{1,0:T(8,128)(2,1)}, u32[]{:S(2)}, u32[]{:S(2)}) collective-permute-start(bf16[4112,128]{1,0:T(8,128)(2,1)} %get-tuple-element.237), channel_id=1, source_target_pairs={{1,5},{2,6},{5,1},{6,2},{9,13},{10,14},{13,9},{14,10},{17,21},{18,... | collective-permute-start | bytes 3158024 | tf_op jit(solution)/shard_map/ppermute | solution.py:1076
  158.6 21.5 %collective-permute-start.33 = (bf16[4112,128]{1,0:T(8,128)(2,1)}, bf16[4112,128]{1,0:T(8,128)(2,1)}, u32[]{:S(2)}, u32[]{:S(2)}) collective-permute-start(bf16[4112,128]{1,0:T(8,128)(2,1)} %get-tuple-element.235), channel_id=1, source_target_pairs={{0,1},{3,2},{4,5},{7,6},{8,9},{11,10},{12,13},{15,14},{16,17},{19,... | collective-permute-start | bytes 3158024 | tf_op jit(solution)/shard_map/ppermute | solution.py:1076
  248.3 25.6 %collective-permute-start.18 = (bf16[1024,768]{1,0:T(8,128)(2,1)S(1)}, bf16[1024,768]{1,0:T(8,128)(2,1)S(1)}, u32[]{:S(2)}, u32[]{:S(2)}) collective-permute-start(bf16[1024,768]{1,0:T(8,128)(2,1)S(1)} %copy-done.134), channel_id=1, source_target_pairs={{0,2},{3,1},{4,6},{7,5},{8,10},{11,9},{12,14},{15,13},{16,18},{19,... | collective-permute-start | bytes 4718600 | tf_op jit(solution)/shard_map/ppermute | solution.py:1076
  290.3 21.4 %collective-permute-start.40 = (bf16[1024,768]{1,0:T(8,128)(2,1)S(1)}, bf16[1024,768]{1,0:T(8,128)(2,1)S(1)}, u32[]{:S(2)}, u32[]{:S(2)}) collective-permute-start(bf16[1024,768]{1,0:T(8,128)(2,1)S(1)} %get-tuple-element.271), channel_id=1, source_target_pairs={{0,2},{1,3},{2,0},{3,1},{4,6},{5,7},{6,4},{7,5},{8,10},{9,11},{10,... | collective-permute-start | bytes 4718600 | tf_op jit(solution)/shard_map/ppermute | solution.py:1076
  313.4 34.7 %collective-permute-start.41 = (bf16[1536,768]{1,0:T(8,128)(2,1)}, bf16[1536,768]{1,0:T(8,128)(2,1)}, u32[]{:S(2)}, u32[]{:S(2)}) collective-permute-start(bf16[1536,768]{1,0:T(8,128)(2,1)} %get-tuple-element.280.own), channel_id=1, source_target_pairs={{1,0},{2,3},{5,4},{6,7},{9,8},{10,11},{13,12},{14,15},{17,16},{18,... | collective-permute-start | bytes 7077896 | tf_op jit(solution)/shard_map/ppermute | solution.py:1076
  314.7 74.9 %collective-permute-start.43 = (bf16[768,1536]{1,0:T(8,128)(2,1)}, bf16[768,1536]{1,0:T(8,128)(2,1)S(1)}, u32[]{:S(2)}, u32[]{:S(2)}) collective-permute-start(bf16[768,1536]{1,0:T(8,128)(2,1)} %get-tuple-element.289.own), channel_id=1, source_target_pairs={{1,0},{2,3},{5,4},{6,7},{9,8},{10,11},{13,12},{14,15},{17,16},{18,... | collective-permute-start | bytes 7077896 | tf_op jit(solution)/shard_map/ppermute | solution.py:1076
  409.5 41.3 %collective-permute-start.48 = (bf16[768,768]{1,0:T(8,128)(2,1)S(1)}, bf16[768,768]{1,0:T(8,128)(2,1)}, u32[]{:S(2)}, u32[]{:S(2)}) collective-permute-start(bf16[768,768]{1,0:T(8,128)(2,1)S(1)} %shard_map.253), channel_id=1, source_target_pairs={{1,5},{2,6},{5,1},{6,2},{9,13},{10,14},{13,9},{14,10},{17,21},{18,... | collective-permute-start | bytes 3538952 | tf_op jit(solution)/shard_map/ppermute | solution.py:1076
  411.4 39.4 %collective-permute-start.49 = (bf16[384,1536]{1,0:T(8,128)(2,1)S(1)}, bf16[384,1536]{1,0:T(8,128)(2,1)}, u32[]{:S(2)}, u32[]{:S(2)}) collective-permute-start(bf16[384,1536]{1,0:T(8,128)(2,1)S(1)} %shard_map.254), channel_id=1, source_target_pairs={{1,5},{2,6},{5,1},{6,2},{9,13},{10,14},{13,9},{14,10},{17,21},{18,... | collective-permute-start | bytes 3538952 | tf_op jit(solution)/shard_map/ppermute | solution.py:1076
  420.3 30.5 %collective-permute-start.47 = (bf16[384,1152]{1,0:T(8,128)(2,1)S(1)}, bf16[384,1152]{1,0:T(8,128)(2,1)S(1)}, u32[]{:S(2)}, u32[]{:S(2)}) collective-permute-start(bf16[384,1152]{1,0:T(8,128)(2,1)S(1)} %shard_map.252), channel_id=1, source_target_pairs={{1,0},{2,3},{5,4},{6,7},{9,8},{10,11},{13,12},{14,15},{17,16},{18,... | collective-permute-start | bytes 2654216 | tf_op jit(solution)/shard_map/ppermute | solution.py:1076
  487.7 20.5 %collective-permute-start.58 = (bf16[768,768]{1,0:T(8,128)(2,1)}, bf16[768,768]{1,0:T(8,128)(2,1)}, u32[]{:S(2)}, u32[]{:S(2)}) collective-permute-start(bf16[768,768]{1,0:T(8,128)(2,1)} %get-tuple-element.361), channel_id=1, source_target_pairs={{1,0},{2,3},{5,4},{6,7},{9,8},{10,11},{13,12},{14,15},{17,16},{18,... | collective-permute-start | bytes 3538952 | tf_op jit(solution)/shard_map/ppermute | solution.py:1076
  489.0 31.8 %collective-permute-start.57 = (bf16[384,1536]{1,0:T(8,128)(2,1)}, bf16[384,1536]{1,0:T(8,128)(2,1)}, u32[]{:S(2)}, u32[]{:S(2)}) collective-permute-start(bf16[384,1536]{1,0:T(8,128)(2,1)} %get-tuple-element.360), channel_id=1, source_target_pairs={{1,0},{2,3},{5,4},{6,7},{9,8},{10,11},{13,12},{14,15},{17,16},{18,... | collective-permute-start | bytes 3538952 | tf_op jit(solution)/shard_map/ppermute | solution.py:1076
  499.6 55.7 %collective-permute-start.53 = (bf16[1536,384]{1,0:T(8,128)(2,1)}, bf16[1536,384]{1,0:T(8,128)(2,1)}, u32[]{:S(2)}, u32[]{:S(2)}) collective-permute-start(bf16[1536,384]{1,0:T(8,128)(2,1)} %get-tuple-element.355), channel_id=1, source_target_pairs={{1,0},{2,3},{5,4},{6,7},{9,8},{10,11},{13,12},{14,15},{17,16},{18,... | collective-permute-start | bytes 3538952 | tf_op jit(solution)/shard_map/ppermute | solution.py:1076
  501.0 51.0 %collective-permute-start.54 = (bf16[384,1152]{1,0:T(8,128)(2,1)}, bf16[384,1152]{1,0:T(8,128)(2,1)}, u32[]{:S(2)}, u32[]{:S(2)}) collective-permute-start(bf16[384,1152]{1,0:T(8,128)(2,1)} %get-tuple-element.356), channel_id=1, source_target_pairs={{1,0},{2,3},{5,4},{6,7},{9,8},{10,11},{13,12},{14,15},{17,16},{18,... | collective-permute-start | bytes 2654216 | tf_op jit(solution)/shard_map/ppermute | solution.py:1076
  502.3 46.8 %collective-permute-start.56 = (bf16[384,768]{1,0:T(8,128)(2,1)S(1)}, bf16[384,768]{1,0:T(8,128)(2,1)S(1)}, u32[]{:S(2)}, u32[]{:S(2)}) collective-permute-start(bf16[384,768]{1,0:T(8,128)(2,1)S(1)} %copy-done.56), channel_id=1, source_target_pairs={{1,0},{2,3},{5,4},{6,7},{9,8},{10,11},{13,12},{14,15},{17,16},{18,... | collective-permute-start | bytes 1769480 | tf_op jit(solution)/shard_map/ppermute | solution.py:1076
  508.2 42.5 %collective-permute-start.55 = (bf16[16,16,128]{2,1,0:T(8,128)(2,1)}, bf16[16,16,128]{2,1,0:T(8,128)(2,1)S(1)}, u32[]{:S(2)}, u32[]{:S(2)}) collective-permute-start(bf16[16,16,128]{2,1,0:T(8,128)(2,1)} %get-tuple-element.357.own), channel_id=1, source_target_pairs={{1,0},{2,3},{5,4},{6,7},{9,8},{10,11},{13,12},{14,15},{17,16},{18,... | collective-permute-start | bytes 196616 | tf_op jit(solution)/shard_map/ppermute | solution.py:1076
  564.1 28.7 %collective-permute-start.63 = (bf16[4112,128]{1,0:T(8,128)(2,1)}, bf16[4112,128]{1,0:T(8,128)(2,1)S(1)}, u32[]{:S(2)}, u32[]{:S(2)}) collective-permute-start(bf16[4112,128]{1,0:T(8,128)(2,1)} %get-tuple-element.430), channel_id=1, source_target_pairs={{0,4},{3,7},{4,0},{7,3},{8,12},{11,15},{12,8},{15,11},{16,20},{19,... | collective-permute-start | bytes 3158024 | tf_op jit(solution)/shard_map/ppermute | solution.py:1076
  584.6 20.4 %collective-permute-start.64 = (bf16[4112,128]{1,0:T(8,128)(2,1)}, bf16[4112,128]{1,0:T(8,128)(2,1)S(1)}, u32[]{:S(2)}, u32[]{:S(2)}) collective-permute-start(bf16[4112,128]{1,0:T(8,128)(2,1)} %get-tuple-element.376), channel_id=1, source_target_pairs={{0,4},{3,7},{4,0},{7,3},{8,12},{11,15},{12,8},{15,11},{16,20},{19,... | collective-permute-start | bytes 3158024 | tf_op jit(solution)/shard_map/ppermute | solution.py:1076
  592.8 48.1 %collective-permute-start.61 = (bf16[1024,768]{1,0:T(8,128)(2,1)}, bf16[1024,768]{1,0:T(8,128)(2,1)}, u32[]{:S(2)}, u32[]{:S(2)}) collective-permute-start(bf16[1024,768]{1,0:T(8,128)(2,1)} %add_convert_fusion), channel_id=1, source_target_pairs={{0,2},{1,3},{2,0},{3,1},{4,6},{5,7},{6,4},{7,5},{8,10},{9,11},{10,... | collective-permute-start | bytes 4718600 | tf_op jit(solution)/shard_map/ppermute | solution.py:1076
  598.0 20.7 %collective-permute-start.66 = (bf16[4112,128]{1,0:T(8,128)(2,1)}, bf16[4112,128]{1,0:T(8,128)(2,1)S(1)}, u32[]{:S(2)}, u32[]{:S(2)}) collective-permute-start(bf16[4112,128]{1,0:T(8,128)(2,1)} %get-tuple-element.380), channel_id=1, source_target_pairs={{0,4},{3,7},{4,0},{7,3},{8,12},{11,15},{12,8},{15,11},{16,20},{19,... | collective-permute-start | bytes 3158024 | tf_op jit(solution)/shard_map/ppermute | solution.py:1076
  601.8 19.3 %collective-permute-start.67 = (bf16[4112,128]{1,0:T(8,128)(2,1)}, bf16[4112,128]{1,0:T(8,128)(2,1)}, u32[]{:S(2)}, u32[]{:S(2)}) collective-permute-start(bf16[4112,128]{1,0:T(8,128)(2,1)} %get-tuple-element.381), channel_id=1, source_target_pairs={{0,8},{3,11},{4,12},{7,15},{8,16},{11,19},{12,20},{15,23},{16,24},... | collective-permute-start | bytes 3158024 | tf_op jit(solution)/shard_map/ppermute | solution.py:1076
  618.7 46.8 %collective-permute-start.59 = (bf16[1024,768]{1,0:T(8,128)(2,1)}, bf16[1024,768]{1,0:T(8,128)(2,1)}, u32[]{:S(2)}, u32[]{:S(2)}) collective-permute-start(bf16[1024,768]{1,0:T(8,128)(2,1)} %get-tuple-element.366), channel_id=1, source_target_pairs={{0,1},{3,2},{4,5},{7,6},{8,9},{11,10},{12,13},{15,14},{16,17},{19,... | collective-permute-start | bytes 4718600 | tf_op jit(solution)/shard_map/ppermute | solution.py:1076
  625.7 20.4 %collective-permute-start.70 = (bf16[4112,128]{1,0:T(8,128)(2,1)}, bf16[4112,128]{1,0:T(8,128)(2,1)S(1)}, u32[]{:S(2)}, u32[]{:S(2)}) collective-permute-start(bf16[4112,128]{1,0:T(8,128)(2,1)} %get-tuple-element.390), channel_id=1, source_target_pairs={{0,4},{3,7},{4,0},{7,3},{8,12},{11,15},{12,8},{15,11},{16,20},{19,... | collective-permute-start | bytes 3158024 | tf_op jit(solution)/shard_map/ppermute | solution.py:1076
  628.7 19.5 %collective-permute-start.71 = (bf16[4112,128]{1,0:T(8,128)(2,1)}, bf16[4112,128]{1,0:T(8,128)(2,1)}, u32[]{:S(2)}, u32[]{:S(2)}) collective-permute-start(bf16[4112,128]{1,0:T(8,128)(2,1)} %get-tuple-element.391), channel_id=1, source_target_pairs={{0,8},{3,11},{4,12},{7,15},{8,16},{11,19},{12,20},{15,23},{16,24},... | collective-permute-start | bytes 3158024 | tf_op jit(solution)/shard_map/ppermute | solution.py:1076
  646.1 22.7 %collective-permute-start.62 = (bf16[1024,384]{1,0:T(8,128)(2,1)}, bf16[1024,384]{1,0:T(8,128)(2,1)}, u32[]{:S(2)}, u32[]{:S(2)}) collective-permute-start(bf16[1024,384]{1,0:T(8,128)(2,1)} %select_convert_fusion), channel_id=1, source_target_pairs={{0,1},{3,2},{4,5},{7,6},{8,9},{11,10},{12,13},{15,14},{16,17},{19,... | collective-permute-start | bytes 2359304 | tf_op jit(solution)/shard_map/ppermute | solution.py:1076
  652.8 19.7 %collective-permute-start.74 = (bf16[4112,128]{1,0:T(8,128)(2,1)}, bf16[4112,128]{1,0:T(8,128)(2,1)S(1)}, u32[]{:S(2)}, u32[]{:S(2)}) collective-permute-start(bf16[4112,128]{1,0:T(8,128)(2,1)} %get-tuple-element.400), channel_id=1, source_target_pairs={{0,4},{3,7},{4,0},{7,3},{8,12},{11,15},{12,8},{15,11},{16,20},{19,... | collective-permute-start | bytes 3158024 | tf_op jit(solution)/shard_map/ppermute | solution.py:1076
  (185 other events, 1213.8 us)

commit v7 on v6

--- a/solution.py
+++ b/solution.py
@@ -39,14 +39,14 @@
 bf16 = jnp.bfloat16
 MIB = 1024 * 1024
 
-PANELS = {
-    "up": (0, 6144),
-    "down": (3072, 9216),
-    "base": 12288,
-    "out": (15360, 20736),
-    "qkv": (16128, 18432),
-}
-PANEL_ROWS = 21504
+WEIGHTS = [("base", 0, BASE_PIX)]
+for layer in range(LAYERS):
+    WEIGHTS += [("qkv", layer, 3 * D), ("out", layer, D), ("up", layer, FF), ("down", layer, FF)]
+STARTS = {}
+PANEL_ROWS = 0
+for name, layer, size in WEIGHTS:
+    STARTS[name, layer] = PANEL_ROWS
+    PANEL_ROWS += size
 
 
 def tile_targets():
@@ -59,12 +59,12 @@
                 rows.append(start + panel * rows_n + i * BS)
                 cols.append(inner)
 
-    add(PANELS["base"], BASE_PIX, HALF)
+    add(STARTS["base", 0], BASE_PIX, HALF)
     for layer in range(LAYERS):
-        add(PANELS["qkv"][layer], D, 3 * HALF)
-        add(PANELS["out"][layer], HALF, D)
-        add(PANELS["up"][layer], D, HALF_FF)
-        add(PANELS["down"][layer], HALF_FF, D)
+        add(STARTS["qkv", layer], D, 3 * HALF)
+        add(STARTS["out", layer], HALF, D)
+        add(STARTS["up", layer], D, HALF_FF)
+        add(STARTS["down", layer], HALF_FF, D)
     return np.array(rows, np.int32), np.array(cols, np.int32)
 
 
@@ -178,13 +178,13 @@
         in_specs=[anywhere] * len(arrays),
         out_specs=[anywhere] * len(arrays),
         input_output_aliases={i: i for i in range(len(arrays))},
-    )(*[stay(a) if a.size > 4 * MIB else a for a in arrays])
+    )(*[stay(a) if a.size > 32 * 1024 else a for a in arrays])
 
 
 def gather_kernel(slots, count_a, count_b, owner, drow, dcol, flag, *refs):
     first = refs[:count_a]
     second = refs[count_a : count_a + count_b]
-    panels, vectors, held, sem, vec_sem = refs[count_a + count_b :]
+    *panels, vectors, held, sem, vec_sem = refs[count_a + count_b :]
 
     def copy_all(sources):
         at = 0
@@ -228,25 +228,26 @@
     else:
         copy_all(first)
     pltpu.make_async_copy(held, held, sem).wait()
-    out = pltpu.make_async_copy(held, panels, sem)
-    out.start()
+    at = 0
+    for panel in panels:
+        size = panel.shape[0]
+        pltpu.make_async_copy(held.at[pl.ds(at, size), :], panel, sem).start()
+        at += size
     pltpu.make_async_copy(vectors, vectors, vec_sem).wait()
-    out.wait()
+    pltpu.make_async_copy(held, held, sem).wait()
 
 
 def gather_tiles(first, second, owner, drow, dcol, flag, slots, owners):
     anywhere = pl.BlockSpec(memory_space=pl.ANY)
-    return pl.pallas_call(
+    *panels, vectors = pl.pallas_call(
         functools.partial(gather_kernel, slots, len(first), len(second)),
-        out_shape=(
-            pltpu.HBM((PANEL_ROWS, HALF), bf16),
-            jax.ShapeDtypeStruct((owners, VEC_ROWS, BS), bf16),
-        ),
+        out_shape=[pltpu.HBM((size, HALF), bf16) for unused, unused2, size in WEIGHTS]
+        + [jax.ShapeDtypeStruct((owners, VEC_ROWS, BS), bf16)],
         grid_spec=pltpu.PrefetchScalarGridSpec(
             num_scalar_prefetch=4,
             grid=(1,),
             in_specs=[anywhere] * (len(first) + len(second)),
-            out_specs=(anywhere, fixed((owners, VEC_ROWS, BS))),
+            out_specs=[anywhere] * len(WEIGHTS) + [fixed((owners, VEC_ROWS, BS))],
             scratch_shapes=[
                 pltpu.VMEM((PANEL_ROWS, HALF), bf16),
                 pltpu.SemaphoreType.DMA,
@@ -255,7 +256,8 @@
         ),
         compiler_params=params(),
         cost_estimate=cost(0, 4 * PANEL_ROWS * HALF),
-    )(owner, drow, dcol, flag, *first, *second)
+    )(owner, drow, dcol, flag, *[stay(v) for v in first], *[stay(v) for v in second])
+    return {(name, layer): p for (name, layer, unused), p in zip(WEIGHTS, panels)}, vectors
 
 
 def scatter_kernel(rows_n, cols_n, steps, paired, parts, pos, part, own, *refs):
@@ -314,7 +316,7 @@
     arrived = pl.BlockSpec(
         (rows_n, cols_n), lambda i, pos, part: (jnp.clip(i - part[0] * span, 0, span - 1), 0)
     )
-    operands = [own] + ([recv] if paired else []) + ([] if target is None else [stay(target)])
+    operands = [stay(own)] + ([stay(recv)] if paired else []) + ([] if target is None else [stay(target)])
     specs = [block] + ([block if parts == 1 else arrived] if paired else [])
     specs += [] if target is None else [anywhere]
     return pl.pallas_call(
@@ -344,7 +346,7 @@
     block = arrived.shape
     return pl.pallas_call(
         half_sum_kernel,
-        out_shape=jax.ShapeDtypeStruct(block, bf16),
+        out_shape=pltpu.HBM(block, bf16),
         grid_spec=pltpu.PrefetchScalarGridSpec(
             num_scalar_prefetch=1,
             grid=(1,),
@@ -353,7 +355,7 @@
         ),
         compiler_params=params(),
         cost_estimate=cost(arrived.size, arrived.size * 6),
-    )(part, own, arrived)
+    )(part, stay(own), stay(arrived))
 
 
 def half_copy_kernel(part, own, out):
@@ -364,7 +366,7 @@
     block = (own.shape[0] // 2, own.shape[1])
     return pl.pallas_call(
         half_copy_kernel,
-        out_shape=jax.ShapeDtypeStruct(block, bf16),
+        out_shape=pltpu.HBM(block, bf16),
         grid_spec=pltpu.PrefetchScalarGridSpec(
             num_scalar_prefetch=1,
             grid=(1,),
@@ -373,7 +375,7 @@
         ),
         compiler_params=params(),
         cost_estimate=cost(0, own.size * 2),
-    )(part, own)
+    )(part, stay(own))
 
 
 def scatter_vec_kernel(paired, pos, own, *refs):
@@ -463,20 +465,20 @@
     out[0] = dot(turned[...], pinv_ref[0]).astype(bf16)
 
 
-def resize_call(panels, pinv):
+def resize_call(weights, pinv):
     return pl.pallas_call(
         resize_kernel,
         out_shape=jax.ShapeDtypeStruct((3, HALF, pinv.shape[2]), bf16),
         grid=(3,),
         in_specs=[
-            fixed((BASE_PIX, HALF), PANELS["base"] // BASE_PIX),
+            fixed((BASE_PIX, HALF)),
             pl.BlockSpec((1, BASE_PIX, pinv.shape[2]), lambda i: (i, 0, 0)),
         ],
         out_specs=pl.BlockSpec((1, HALF, pinv.shape[2]), lambda i: (i, 0, 0)),
         scratch_shapes=[pltpu.VMEM((HALF, BASE_PIX), bf16)],
         compiler_params=params(),
         cost_estimate=cost(6 * D * BASE_PIX * HALF, 6 * D * BASE_PIX),
-    )(stay(panels), stay(pinv))
+    )(stay(weights["base", 0]), stay(pinv))
 
 
 def embed_back_kernel(core, base, own, recv, out, bias):
@@ -544,7 +546,7 @@
     out[...] = total.astype(bf16)
 
 
-def embed_call(half, chunks, vec, panels):
+def embed_call(half, chunks, vec, weights):
     tokens = chunks[0].shape[0]
     return pl.pallas_call(
         embed_kernel,
@@ -553,12 +555,12 @@
             num_scalar_prefetch=1,
             grid=(tokens // ROWS,),
             in_specs=[rows_spec(BASE_PIX // CHUNKS)] * CHUNKS
-            + [fixed(vec.shape), fixed((BASE_PIX, HALF), PANELS["base"] // BASE_PIX)],
+            + [fixed(vec.shape), fixed((BASE_PIX, HALF))],
             out_specs=rows_spec(HALF),
         ),
         compiler_params=params(),
         cost_estimate=cost(2 * tokens * BASE_PIX * HALF, tokens * BASE_PIX * 3),
-    )(half, *chunks, vec, stay(panels))
+    )(half, *[stay(c) for c in chunks], vec, stay(weights["base", 0]))
 
 
 def qkv_kernel(layer, first, core, *refs):
@@ -582,7 +584,7 @@
     v_ref[...] = (made[:, 2 * HALF :] + vec_piece(vec, layer, "bv")).astype(bf16)
 
 
-def qkv_call(layer, base, own, recv, core, vec, panels):
+def qkv_call(layer, base, own, recv, core, vec, weights):
     tokens = own.shape[0]
     shape = lambda width, kind: jax.ShapeDtypeStruct((tokens, width), kind)
     outs = [shape(D, f32), pltpu.HBM((tokens, D), bf16)] + [shape(HALF, bf16)] * 3
@@ -594,12 +596,12 @@
             num_scalar_prefetch=1,
             grid=(tokens // ROWS,),
             in_specs=[rows_spec(o.shape[1]) for o in operands]
-            + [fixed(vec.shape), fixed((3 * D, HALF), PANELS["qkv"][layer] // (3 * D))],
+            + [fixed(vec.shape), fixed((3 * D, HALF))],
             out_specs=[rows_spec(o.shape[1]) for o in outs],
         ),
         compiler_params=params(),
         cost_estimate=cost(2 * tokens * D * 3 * HALF, tokens * D * 14),
-    )(core, *operands, vec, stay(panels))
+    )(core, *operands, vec, weights["qkv", layer])
 
 
 def head_masks():
@@ -671,7 +673,7 @@
     part[...] = (dot(low, joined(w_out, 0, HALF, TENSOR)) + bias).astype(bf16)
 
 
-def attend_call(layer, first, last, queries, keys, values, seg_col, seg_row, vec, panels):
+def attend_call(layer, first, last, queries, keys, values, seg_col, seg_row, vec, weights):
     tokens = queries.shape[0]
     return pl.pallas_call(
         functools.partial(attend_kernel, layer),
@@ -690,7 +692,7 @@
                 rows_spec(1),
                 fixed(seg_row.shape),
                 fixed(vec.shape),
-                fixed((D, HALF), PANELS["out"][layer] // D),
+                fixed((D, HALF)),
             ],
             out_specs=[
                 rows_spec(HALF),
@@ -705,7 +707,7 @@
         ),
         compiler_params=params(),
         cost_estimate=cost(8 * HEADS * tokens * tokens * BS, tokens * D * 8, HEADS * tokens * tokens),
-    )(first, last, queries, keys, values, seg_col, seg_row, vec, stay(panels))
+    )(first, last, queries, keys, values, seg_col, seg_row, vec, weights["out", layer])
 
 
 def gelu_parts(values):
@@ -731,7 +733,7 @@
     part[...] = (dot(act[...], joined(w_down, 0, HALF_FF, TENSOR)) + bias_down).astype(bf16)
 
 
-def mlp_call(layer, base, own, recv, vec, panels):
+def mlp_call(layer, base, own, recv, vec, weights):
     tokens = base.shape[0]
     shape = lambda width, kind: jax.ShapeDtypeStruct((tokens, width), kind)
     kept = lambda width: pltpu.HBM((tokens, width), bf16)
@@ -743,13 +745,13 @@
         in_specs=[rows_spec(D)] * 3
         + [
             fixed(vec.shape),
-            fixed((2 * HALF_FF, HALF), PANELS["up"][layer] // (2 * HALF_FF)),
-            fixed((2 * HALF_FF, HALF), PANELS["down"][layer] // (2 * HALF_FF)),
+            fixed((2 * HALF_FF, HALF)),
+            fixed((2 * HALF_FF, HALF)),
         ],
         out_specs=[rows_spec(o.shape[1]) for o in outs],
         compiler_params=params(),
         cost_estimate=cost(4 * tokens * D * HALF_FF, tokens * D * 24, 2 * tokens * HALF_FF),
-    )(base, own, recv, vec, stay(panels), stay(panels))
+    )(base, own, recv, vec, weights["up", layer], weights["down", layer])
 
 
 def mlp_back_kernel(layer, summed, *refs):
@@ -780,7 +782,7 @@
     accumulate(dshift, shift_grad)
 
 
-def mlp_back_call(layer, base, own, recv, valid, hid, slope, vec, panels):
+def mlp_back_call(layer, base, own, recv, valid, hid, slope, vec, weights):
     tokens = base.shape[0]
     summed = own is not None
     shape = lambda width, kind: jax.ShapeDtypeStruct((tokens, width), kind)
@@ -798,13 +800,13 @@
             rows_spec(D),
             rows_spec(HALF_FF),
             fixed(vec.shape),
-            fixed((2 * HALF_FF, HALF), PANELS["up"][layer] // (2 * HALF_FF)),
-            fixed((2 * HALF_FF, HALF), PANELS["down"][layer] // (2 * HALF_FF)),
+            fixed((2 * HALF_FF, HALF)),
+            fixed((2 * HALF_FF, HALF)),
         ],
         out_specs=[rows_spec(o.shape[1]) for o in outs] + [fixed(o.shape) for o in lines],
         compiler_params=params(),
         cost_estimate=cost(4 * tokens * D * HALF_FF, tokens * D * 24),
-    )(base, *extra, stay(hid), stay(slope), vec, stay(panels), stay(panels))
+    )(base, *extra, stay(hid), stay(slope), vec, weights["up", layer], weights["down", layer])
 
 
 def attend_back_kernel(
@@ -875,7 +877,7 @@
 
 
 def attend_back_call(
-    layer, first, last, base, own, recv, queries, keys, values, mixed, lse, seg_col, seg_row, panels
+    layer, first, last, base, own, recv, queries, keys, values, mixed, lse, seg_col, seg_row, weights
 ):
     tokens = base.shape[0]
     shape = lambda width, kind: jax.ShapeDtypeStruct((tokens, width), kind)
@@ -904,7 +906,7 @@
                 pl.BlockSpec((8, ROWS), lambda i, *_: (0, i)),
                 fixed(seg_col.shape),
                 pl.BlockSpec((1, ROWS), lambda i, *_: (0, i)),
-                fixed((D, HALF), PANELS["out"][layer] // D),
+                fixed((D, HALF)),
             ],
             out_specs=[
                 rows_spec(D),
@@ -924,8 +926,8 @@
         compiler_params=params(),
         cost_estimate=cost(14 * HEADS * tokens * tokens * BS, tokens * D * 20, HEADS * tokens * tokens),
     )(
-        first, last, base, own, recv, stay(queries), stay(keys), stay(values), stay(mixed), stay(lse),
-        seg_col, seg_row, stay(panels),
+        first, last, base, own, recv, stay(queries), stay(keys), stay(values), stay(mixed), lse,
+        seg_col, seg_row, weights["out", layer],
     )
 
 
@@ -940,7 +942,7 @@
     accumulate(dbv, jnp.sum(dv[...].astype(f32), axis=0, keepdims=True))
 
 
-def qkv_back_call(layer, dq, dk, dv, hid, vec, panels):
+def qkv_back_call(layer, dq, dk, dv, hid, vec, weights):
     tokens = dq.shape[0]
     line = lambda width: jax.ShapeDtypeStruct((1, width), f32)
     lines = [line(D), line(D), line(HALF), line(HALF)]
@@ -952,12 +954,12 @@
         + [
             rows_spec(D),
             fixed(vec.shape),
-            fixed((3 * D, HALF), PANELS["qkv"][layer] // (3 * D)),
+            fixed((3 * D, HALF)),
         ],
         out_specs=[rows_spec(D)] + [fixed(o.shape) for o in lines],
         compiler_params=params(),
         cost_estimate=cost(2 * tokens * D * 3 * HALF, tokens * D * 10),
-    )(dq, dk, dv, stay(hid), vec, stay(panels))
+    )(dq, dk, dv, stay(hid), vec, weights["qkv", layer])
 
 
 def split(values):
@@ -1016,7 +1018,7 @@
         ),
         compiler_params=params(),
         cost_estimate=cost(count * 88 * BS**3, count * BS * BS * 38),
-    )(used, home, near, far, *[stay(a) for a in arrays])
+    )(used, home, stay(near), stay(far), *[stay(a) for a in arrays])
 
 
 def reduce_kernel(carrying, last, *refs):
@@ -1037,12 +1039,12 @@
     last = j == 3
     at = lambda j, x_rel: pl.BlockSpec((payload, BS), lambda i: ((j * 2 + x_rel) * 2 + n, 0))
     whole = fixed((payload, BS))
-    operands = [stay(buffer), arrived] + ([] if carried is None else [carried])
+    operands = [stay(buffer), stay(arrived)] + ([] if carried is None else [stay(carried)])
     specs = [at(j, 0)] + [whole] * (len(operands) - 1)
     if not last:
         operands.append(stay(buffer))
         specs.append(at(j + 1, 1))
-    outs = [jax.ShapeDtypeStruct((payload, BS), bf16)] * (1 if last else 2)
+    outs = [pltpu.HBM((payload, BS), bf16)] * (1 if last else 2)
     made = pl.pallas_call(
         functools.partial(reduce_kernel, carried is not None, last),
         out_shape=outs,
@@ -1069,6 +1071,7 @@
         self.y_in = [(at(d, t), at(d, 1 - t)) for d, t in away]
         self.x_home = [(at(d, t), at(d ^ 2, t)) for d, t in home]
         self.x_away = [(at(d, t), at(d ^ 2, t)) for d, t in away]
+        self.z_all = [(at(d, t), at((d + 4) % dp_n, t)) for d, t in pairs]
         self.z_home = [(at(d, t), at((d + 4) % dp_n, t)) for d, t in home]
 
 
@@ -1161,32 +1164,37 @@
         chunks = []
         for j in range(5):
             for n in range(2):
-                moved = []
-                if j < 4:
-                    moved += [send(packs[n][j], routes.x_home), send(packs[n][j], routes.y_out)]
+                moved = {}
+                if j < 3:
+                    moved["x"] = send(packs[n][j], routes.x_home)
+                    moved["y"] = send(packs[n][j], routes.y_out)
                 if j:
                     source, route = (across, routes.y_out) if n == 0 else (over_y, routes.x_away)
-                    moved.append(send(source[n][j - 1], route))
+                    moved["corner"] = send(source[n][j - 1], route)
                 if j < 3:
-                    moved.append(send(packs[n][j], routes.z_home))
+                    moved["z"] = send(packs[n][j], routes.z_home)
+                if j == 3:
+                    ring = jnp.where(home, across[n][2], over_y[n][2])
+                    moved["x"] = moved["y"] = send(ring, routes.z_all)
                 work = []
                 if j + n == 0:
                     work = [slot_other]
                 if 1 <= 2 * j + n <= CHUNKS:
                     work = [expand(2 * j + n - 1)]
                 if j < 4:
-                    token, *moved = fence(token, *moved, *work)
+                    keys_here = [k for k in moved if k != "y" or j < 3]
+                    token, *made = fence(token, *[moved[k] for k in keys_here], *work)
                     if j + n == 0:
-                        slot_other = moved.pop()
+                        slot_other = made.pop()
                     elif work:
-                        chunks.append(moved.pop())
+                        chunks.append(made.pop())
+                    moved = dict(zip(keys_here, made))
+                    across[n].append(moved["x"])
+                    over_y[n].append(moved["y"] if j < 3 else moved["x"])
                 if j < 3:
-                    packs[n].append(moved.pop())
+                    packs[n].append(moved["z"])
                 if j:
-                    corner[n].append(moved.pop())
-                if j < 4:
-                    across[n].append(moved[0])
-                    over_y[n].append(moved[1])
+                    corner[n].append(moved["corner"])
         first, second, owner = [], [], []
         for j in range(4):
             first += [packs[0][j], packs[1][j], across[0][j], across[1][j]]
@@ -1209,10 +1217,10 @@
     used = jnp.any(named, axis=1)
     drow = jnp.where(used, jnp.sum(jnp.where(named, TARGET_ROW[None, :], 0), axis=1), -1)
     dcol = jnp.sum(jnp.where(named, TARGET_COL[None, :], 0), axis=1)
-    panels, vec_rows = gather_tiles(first, second, owner, drow, dcol, flag, slots_per, dp_n)
+    weights, vec_rows = gather_tiles(first, second, owner, drow, dcol, flag, slots_per, dp_n)
     vec = vec_rows.reshape(dp_n, VEC_ROWS * BS)[:, :vec_per].astype(f32).reshape(1, dp_n * vec_per)
 
-    embedded = embed_call(half_at, chunks, vec, panels)
+    embedded = embed_call(half_at, chunks, vec, weights)
     embedded_other = send(embedded, routes.core_all)
     core_flag = core.astype(jnp.int32).reshape(1)
 
@@ -1220,13 +1228,13 @@
     hidden, own, recv = None, embedded, embedded_other
     for layer in range(LAYERS):
         hidden, normed, queries, keys, values = qkv_call(
-            layer, hidden, own, recv, core_flag, vec, panels
+            layer, hidden, own, recv, core_flag, vec, weights
         )
         mixed, lse, part = attend_call(
-            layer, first_blk, last_blk, queries, keys, values, seg_col, seg_row, vec, panels
+            layer, first_blk, last_blk, queries, keys, values, seg_col, seg_row, vec, weights
         )
         other = send(part, routes.core_all)
-        middle, normed2, act, slope, own = mlp_call(layer, hidden, part, other, vec, panels)
+        middle, normed2, act, slope, own = mlp_call(layer, hidden, part, other, vec, weights)
         recv = send(own, routes.core_all)
         caches.append((hidden, normed, queries, keys, values, mixed, lse, middle, normed2, act, slope))
         hidden = middle
@@ -1287,55 +1295,51 @@
 
     def mlp_step(layer, grad, own, recv):
         middle, normed2, act, slope = caches[layer][7:11]
-        made = mlp_back_call(layer, grad, own, recv, valid_col, middle, slope, vec, panels)
+        made = mlp_back_call(layer, grad, own, recv, valid_col, middle, slope, vec, weights)
         if own is not None:
             return made
         return [made[0]] + list(made)
 
-    def attend_step(layer, grad, part, other):
-        hid_in, normed, queries, keys, values, mixed, lse = caches[layer][:7]
+    def attend_step(layer, grad, part, other, lse):
+        hid_in, normed, queries, keys, values, mixed = caches[layer][:6]
         return attend_back_call(
             layer, first_key, last_key, grad, part, other, queries, keys, values, mixed, lse,
-            seg_col, seg_row, panels,
+            seg_col, seg_row, weights,
         )
 
     grad, grad_low, du, part, dg2, ds2, db1, db2 = mlp_step(top, cotangent, None, None)
     other = send(part, routes.core_all)
     gd1 = dot_tn(caches[top][9], grad_low).astype(bf16)
     gu1 = dot_tn(caches[top][8], du).astype(bf16)
-    part, other, gd1, gu1, out_low = fence(part, other, gd1, gu1, out_low)
+    lse, gd1, gu1, out_low = fence(caches[top][6], gd1, gu1, out_low)
     ad1 = over(gd1)
-    grad, grad_low, dq, dk, dv, dbo = attend_step(top, grad, part, other)
-    dq, dk, dv, ad1 = hold(dq, dk, dv, ad1)
+    grad, grad_low, dq, dk, dv, dbo = attend_step(top, grad, part, other, lse)
+    vec, dbo, ad1, gu1 = hold(vec, dbo, ad1, gu1)
     au1 = over(gu1)
-    own, dg1, ds1, dbq, dbv = qkv_back_call(top, dq, dk, dv, caches[top][0], vec, panels)
+    own, dg1, ds1, dbq, dbv = qkv_back_call(top, dq, dk, dv, caches[top][0], vec, weights)
     recv = send(own, routes.core_all)
     go1 = dot_tn(caches[top][5], grad_low).astype(bf16)
     gq1 = dot_tn(caches[top][1], jnp.concatenate([dq, dk, dv], axis=1)).astype(bf16)
     vec_grads[top] = [dg1, ds1, dbq, dbv, dbo, dg2, ds2, db1, db2]
     grad, grad_low, du, part, dg2, ds2, db1, db2 = mlp_step(low, grad, own, recv)
-    du, part, au1, go1, gq1 = hold(du, part, au1, go1, gq1)
     other = send(part, routes.core_all)
+    db2, au1, go1, gq1 = hold(db2, au1, go1, gq1)
     xq1, ao1 = beside(gq1), over(go1)
     gd0 = dot_tn(caches[low][9], grad_low).astype(bf16)
     gu0 = dot_tn(caches[low][8], du).astype(bf16)
-    part, other, gd0, gu0, xq1, ao1 = hold(part, other, gd0, gu0, xq1, ao1)
-    aq1 = over(summed(gq1, xq1)) if grid3 else None
-    xd0, xu0 = beside(gd0), beside(gu0)
+    lse, gd0, gu0, xq1, ao1 = hold(caches[low][6], gd0, gu0, xq1, ao1)
+    aq1 = over(summed(gq1, xq1))
+    ad0 = over(gd0)
+    xu0 = beside(gu0)
     buffer = place_tiles(("down", top), gd1, ad1, None)
     buffer = place_tiles(("up", top), gu1, au1, buffer)
-    grad, grad_low, dq, dk, dv, dbo = attend_step(low, grad, part, other)
-    grad, grad_low, dq, dk, dv, aq1, xd0, xu0, buffer = hold(
-        grad, grad_low, dq, dk, dv, aq1, xd0, xu0, buffer
-    )
-    hd0, hu0 = summed(gd0, xd0), summed(gu0, xu0)
-    dq, dk, dv, hd0, hu0 = hold(dq, dk, dv, hd0, hu0)
-    ad0, au0 = over(hd0), over(hu0)
-    own, dg1, ds1, dbq, dbv = qkv_back_call(low, dq, dk, dv, caches[low][0], vec, panels)
+    grad, grad_low, dq, dk, dv, dbo = attend_step(low, grad, part, other, lse)
+    vec, dbo, aq1, xu0, buffer = hold(vec, dbo, aq1, xu0, buffer)
+    au0 = over(summed(gu0, xu0))
+    own, dg1, ds1, dbq, dbv = qkv_back_call(low, dq, dk, dv, caches[low][0], vec, weights)
     recv = send(own, routes.core_all)
     gq0 = dot_tn(caches[low][1], jnp.concatenate([dq, dk, dv], axis=1)).astype(bf16)
     vec_grads[low] = [dg1, ds1, dbq, dbv, dbo, dg2, ds2, db1, db2]
-    own, recv, gq0 = hold(own, recv, gq0)
     xq0 = beside(gq0)
     grad_emb, grad_emb_bias = embed_back_call(core_flag, grad, own, recv)
     middle = CHUNKS // 2
@@ -1344,18 +1348,15 @@
         return jnp.concatenate([dot_tn(c, grad_emb).astype(bf16) for c in parts], axis=0)
 
     gbt = base_grad(chunks[middle:])
-    gbt, grad_emb, gq0 = hold(gbt, grad_emb, gq0)
+    gbt, ad0, au0, xq0 = hold(gbt, ad0, au0, xq0)
     xb = send(gbt, routes.x_away) if grid3 else None
+    aq0 = over(summed(gq0, xq0))
     gbm = base_grad(chunks[:middle])
     vec_grad = pack_call([grad_emb_bias] + vec_grads[0] + vec_grads[1], dp_n, vec_per)
     go0 = dot_tn(caches[low][5], grad_low).astype(bf16)
-    hq0 = summed(gq0, xq0)
-    gbm, vec_grad, go0, hq0 = hold(gbm, vec_grad, go0, hq0)
-    aq0, ao0, av = over(hq0), over(go0), over(vec_grad)
-    gbm, xb = hold(gbm, xb)
-    hb = (gbm.astype(f32) + xb.astype(f32)).astype(bf16) if grid3 else None
-    hb, gbm, gbt, buffer = hold(hb, gbm, gbt, buffer)
-    ab = over(hb)
+    ao0, av = over(go0), over(vec_grad)
+    gbm, xb, aq0, ao0, av, buffer = hold(gbm, xb, aq0, ao0, av, buffer)
+    ab = over(half_sum(half_at * 0, gbm, xb)) if grid3 else None
     buffer = place_tiles(("out", top), go1, ao1, buffer)
     buffer = place_tiles(("qkv", top), gq1, aq1, buffer)
     buffer = place_tiles(("down", low), gd0, ad0, buffer)
@@ -1364,13 +1365,15 @@
     buffer = place_tiles(("out", low), go0, ao0, buffer)
     buffer = scatter_vec(vec_pos, vec_grad, av, buffer)
     buffer = place_tiles(("qkv", low), gq0, aq0, buffer)
-    ab, buffer, panels, grad_emb, out_low = hold(ab, buffer, panels, grad_emb, out_low)
+    base_weight = weights["base", 0]
+    ab, buffer, base_weight, out_low = hold(ab, buffer, base_weight, out_low)
+    weights["base", 0] = base_weight
     buffer = place_base(0, gbm, ab, buffer)
 
     if grid3:
         token = jnp.zeros((8, BS), f32)
         order = (1, 0)
-        resized = resize_call(panels, pinv)
+        resized = resize_call(weights, pinv)
         carried = {n: None for n in order}
         across = {n: send(buffer.reshape(4, 2, 2, payload, BS)[0, 1, n], routes.x_home) for n in order}
         rounded = {}
@@ -1402,7 +1405,7 @@
         both = jnp.where(used_rows, both, 0.0).reshape(dp_n * TENSOR * payload, BS)
         near_grad = lax.psum_scatter(both, AXES, scatter_dimension=0, tiled=True).astype(bf16)
         far_grad = near_grad
-        resized = resize_call(panels, pinv)
+        resized = resize_call(weights, pinv)
 
     output = jnp.where(home, out_low, send(out_low, routes.y_out)).astype(f32)
     grad_pixels = sum(

time: 703 us -> 709 us (level)
  waiting for transfers between devices: 96.1 us -> 146 us
  starting transfers between devices: 176 us -> 148 us
  local copies, waits for them, and re-layouts: 80.1 us -> 53.5 us
  Pallas kernels: 274 us -> 290 us
    ppermute x77 -> x74, waiting for transfers between devices: 96.1 us -> 146 us  [send(): return lax.ppermute(value, AXES, route)]
    ppermute x77 -> x74, starting transfers between devices: 176 us -> 148 us  [send(): return lax.ppermute(value, AXES, route)]
    unnamed x314 -> x248, local copies, waits for them, and re-layouts: 74.8 us -> 47.3 us
    pallas_call x8 -> x7, Pallas kernels: 5.97 us -> 18.1 us  [the longest x4 11.4 us: half_sum(): pl.pallas_call(half_sum_kernel, out_shape=pltpu.HBM(block, bf16), grid_sp...]
    pallas_call x10, Pallas kernels: 26.7 us -> 35.7 us  [scatter_matrix(): pl.pallas_call(functools.partial(scatter_kernel, rows_n, cols_n, steps, p...]
  transfers between devices with their start and end apart: 77 -> 74, of which waited for: 26 -> 29; matrix products, arithmetic and copies ran while one was open for 9% -> 9% of each run, Pallas kernels for 26% -> 30%
where the time goes in v7:
time: 709 us; the launch traced here: 700 us
  Pallas kernels  290 us (41%)
  starting transfers between devices  148 us (21%)
  waiting for transfers between devices  146 us (21%)
  local copies, waits for them, and re-layouts  53.5 us (8%)
  matrix products  34.7 us (5%)
  other arithmetic  25.3 us (4%)
    ppermute x74, starting transfers between devices, send(): return lax.ppermute(value, AXES, route)  148 us
    ppermute x74, waiting for transfers between devices, send(): return lax.ppermute(value, AXES, route)  146 us
    pallas_call x2, Pallas kernels, attend_back_call(): pl.pallas_call(attend_back_kernel, out_shape=[shape(D, f32), shape(D, bf1...  47.3 us
    unnamed x248, local copies, waits for them, and re-layouts  47.3 us
    pallas_call x10, Pallas kernels, scatter_matrix(): pl.pallas_call(functools.partial(scatter_kernel, rows_n, cols_n, steps, p...  35.7 us
    dot_general x12, matrix products, dot_tn(): lax.dot_general(left, right, (((0,), (0,)), ((), ())), preferred_element_...  31.6 us
    pallas_call x2, Pallas kernels, attend_call(): pl.pallas_call(functools.partial(attend_kernel, layer), out_shape=[jax.Sh...  30.5 us
    pallas_call x8, Pallas kernels, reduce_call(): pl.pallas_call(functools.partial(reduce_kernel, carried is not None, last...  27.6 us
  transfers between devices with their start and end apart: 74, of which 29 were waited for; matrix products, arithmetic and copies ran while one was open for 9% of the time, Pallas kernels for 30%

profile of v7, /device:TPU:0, one launch (start us, length us, event | category | flops | bytes accessed | tf_op | source)
XLA Modules:
  0.0 699.7 jit_solution(9354942785253472102)
XLA Ops:
  22.2 5.1 collective-permute-done.refs_1_
  27.6 8.4 %collective-permute-done.2.refs_3_ = bf16[4112,128]{1,0:T(8,128)(2,1)} collective-permute-done((bf16[4112,128]{1,0:T(8,128)(2,1)}, bf16[4112,128]{1,0:T(8,128)(2,1)}, u32[]{:S(2)}, u32[]{:S(2)}) %collective-permute-start.2) | collective-permute-done | bytes 1052704 | tf_op jit(solution)/shard_map/ppermute | solution.py:1079
  51.8 5.6 shard_map.223.refs_4_
  58.6 6.3 collective-permute-done.5.refs_1_
  75.5 5.7 shard_map.225.refs_5_
  89.1 6.8 collective-permute-done.15.refs_1_
  102.4 5.6 shard_map.227.refs_5_
  109.2 5.6 shard_map.229.refs_5_
  120.5 4.2 collective-permute-start.26
  131.3 12.8 %collective-permute-done.23.refs_1_ = bf16[4112,128]{1,0:T(8,128)(2,1)S(1)} collective-permute-done((bf16[4112,128]{1,0:T(8,128)(2,1)}, bf16[4112,128]{1,0:T(8,128)(2,1)S(1)}, u32[]{:S(2)}, u32[]{:S(2)}) %collective-permute-start.23) | collective-permute-done | bytes 1052704 | tf_op jit(solution)/shard_map/ppermute | solution.py:1079
  144.9 5.4 collective-permute-done.26.refs_4_
  154.3 15.7 %collective-permute-done.28.refs_2_ = bf16[4112,128]{1,0:T(8,128)(2,1)S(1)} collective-permute-done((bf16[4112,128]{1,0:T(8,128)(2,1)}, bf16[4112,128]{1,0:T(8,128)(2,1)S(1)}, u32[]{:S(2)}, u32[]{:S(2)}) %collective-permute-start.28) | collective-permute-done | bytes 1052704 | tf_op jit(solution)/shard_map/ppermute | solution.py:1079
  172.5 11.9 %collective-permute-done.30.refs_2_ = bf16[4112,128]{1,0:T(8,128)(2,1)S(1)} collective-permute-done((bf16[4112,128]{1,0:T(8,128)(2,1)}, bf16[4112,128]{1,0:T(8,128)(2,1)S(1)}, u32[]{:S(2)}, u32[]{:S(2)}) %collective-permute-start.30) | collective-permute-done | bytes 1052704 | tf_op jit(solution)/shard_map/ppermute | solution.py:1079
  188.2 14.2 %shard_map.234 = (bf16[3072,384]{1,0:T(8,128)(2,1)}, bf16[2304,384]{1,0:T(8,128)(2,1)}, bf16[768,384]{1,0:T(8,128)(2,1)}, bf16[3072,384]{1,0:T(8,128)(2,1)}, bf1...) custom-call(s32[16]{0:T(128)S(1)} %stack.95.owner, ...), custom_call_target="tpu_custom_call" | custom-call | bytes 33030144 | tf_op jit(solution)/shard_map/pallas_call | solution.py:242
  202.5 6.9 shard_map.235.refs_0_
  209.5 6.0 collective-permute-start.33
  217.5 4.8 shard_map.236
  222.4 15.3 %shard_map.237 = (bf16[1024,384]{1,0:T(8,128)(2,1)S(1)}, f32[8,1024]{1,0:T(8,128)S(1)}, bf16[1024,768]{1,0:T(8,128)(2,1)S(1)}) custom-call(s32[4]{0:T(128)S(1)} %get-tuple-element.425.low_ref, s32[4]{0:T(128)S(1)} %get-tuple-element.418.high_ref, bf16[1024,384]{1,0:T(8,128)(2,1)S(1)} %get-tuple-element.239.q_ref, ...), custom_call_target="tpu_custom_call" | custom-call | flops 6442450944 | bytes 6291456 | tf_op jit(solution)/shard_map/pallas_call | solution.py:678
  242.6 9.5 %shard_map.238 = (f32[1024,768]{1,0:T(8,128)S(1)}, bf16[1024,768]{1,0:T(8,128)(2,1)}, bf16[1024,1536]{1,0:T(8,128)(2,1)}, bf16[1024,1536]{1,0:T(8,128)(2,1)}, bf16[1024,768]{1,0:T(8,128)(2,1)S(1)}) custom-call(f32[1024,768]{1,0:T(8,128)S(1)} %get-tuple-element.238.base.hid, bf16[1024,768]{1,0:T(8,128)(2,1)S(1)} %get-tuple-element.243.own, ...), custom_call_target="tpu_custom_call" | custom-call | flops 4831838208 | bytes 18874368 | tf_op jit(solution)/shard_map/pallas_call | solution.py:741
  255.6 4.4 shard_map.239
  260.0 15.3 %shard_map.240 = (bf16[1024,384]{1,0:T(8,128)(2,1)S(1)}, f32[8,1024]{1,0:T(8,128)S(1)}, bf16[1024,768]{1,0:T(8,128)(2,1)S(1)}) custom-call(s32[4]{0:T(128)S(1)} %get-tuple-element.425.low_ref, s32[4]{0:T(128)S(1)} %get-tuple-element.418.high_ref, bf16[1024,384]{1,0:T(8,128)(2,1)S(1)} %get-tuple-element.250.q_ref, ...), custom_call_target="tpu_custom_call" | custom-call | flops 6442450944 | bytes 6291456 | tf_op jit(solution)/shard_map/pallas_call | solution.py:678
  278.8 9.4 %shard_map.241 = (f32[1024,768]{1,0:T(8,128)S(1)}, bf16[1024,768]{1,0:T(8,128)(2,1)}, bf16[1024,1536]{1,0:T(8,128)(2,1)}, bf16[1024,1536]{1,0:T(8,128)(2,1)}, bf16[1024,768]{1,0:T(8,128)(2,1)S(1)}) custom-call(f32[1024,768]{1,0:T(8,128)S(1)} %get-tuple-element.249.base.hid, bf16[1024,768]{1,0:T(8,128)(2,1)S(1)} %get-tuple-element.254.own, ...), custom_call_target="tpu_custom_call" | custom-call | flops 4831838208 | bytes 18874368 | tf_op jit(solution)/shard_map/pallas_call | solution.py:741
  290.1 12.0 %shard_map.242 = (bf16[1024,768]{1,0:T(8,128)(2,1)S(1)}, bf16[1024,1536]{1,0:T(8,128)(2,1)S(1)}, bf16[1024,768]{1,0:T(8,128)(2,1)}, f32[1,768]{1,0:T(1,128)S(1)}...) custom-call(bf16[1024,768]{1,0:T(8,128)(2,1)S(1)} %broadcast_select_fusion.refs_0_, ...), custom_call_target="tpu_custom_call" | custom-call | flops 4831838208 | bytes 18874368 | tf_op jit(solution)/shard_map/pallas_call | solution.py:793
  302.3 3.9 convolution_convert_fusion.3.refs_1_
  306.3 4.0 convolution_convert_fusion.2.refs_2_
  316.8 23.7 %shard_map.244 = (f32[1024,768]{1,0:T(8,128)S(1)}, bf16[1024,768]{1,0:T(8,128)(2,1)S(1)}, bf16[1024,384]{1,0:T(8,128)(2,1)S(1)}, bf16[1024,384]{1,0:T(8,128)(2,1...) custom-call(s32[4]{0:T(128)S(1)} %get-tuple-element.424.low_ref, s32[4]{0:T(128)S(1)} %get-tuple-element.419.high_ref, ...), custom_call_target="tpu_custom_call" | custom-call | flops 11274289152 | bytes 15728640 | tf_op jit(solution)/shard_map/pallas_call | solution.py:885
  351.4 5.7 shard_map.246
  357.1 7.4 %collective-permute-start.40 = (bf16[1024,768]{1,0:T(8,128)(2,1)S(1)}, bf16[1024,768]{1,0:T(8,128)(2,1)S(1)}, u32[]{:S(2)}, u32[]{:S(2)}) collective-permute-start(bf16[1024,768]{1,0:T(8,128)(2,1)S(1)} %get-tuple-element.276.refs_1_), channel_id=1, source_target_pairs={{0,2},{1,3},{2,0},{3,1},{4,6},{5,7},{6,4},{7,5},{8,10},{9,11},{10,... | collective-permute-start | bytes 4718600 | tf_op jit(solution)/shard_map/ppermute | solution.py:1079
  368.3 12.1 %shard_map.247 = (f32[1024,768]{1,0:T(8,128)S(1)}, bf16[1024,768]{1,0:T(8,128)(2,1)S(1)}, bf16[1024,1536]{1,0:T(8,128)(2,1)S(1)}, bf16[1024,768]{1,0:T(8,128)(2,...) custom-call(f32[1024,768]{1,0:T(8,128)S(1)} %copy-done.70, ...), custom_call_target="tpu_custom_call" | custom-call | flops 4831838208 | bytes 18874368 | tf_op jit(solution)/shard_map/pallas_call | solution.py:793
  390.0 6.2 convolution_convert_fusion.1.refs_1_
  397.5 4.0 convolution_convert_fusion.refs_2_
  401.5 6.4 collective-permute-done.44.refs_4_
  412.3 4.2 shard_map.254.refs_1_
  416.5 4.5 shard_map.255.refs_4_
  425.1 23.6 %shard_map.251 = (f32[1024,768]{1,0:T(8,128)S(1)}, bf16[1024,768]{1,0:T(8,128)(2,1)S(1)}, bf16[1024,384]{1,0:T(8,128)(2,1)S(1)}, bf16[1024,384]{1,0:T(8,128)(2,1...) custom-call(s32[4]{0:T(128)S(1)} %get-tuple-element.424.low_ref, s32[4]{0:T(128)S(1)} %get-tuple-element.419.high_ref, ...), custom_call_target="tpu_custom_call" | custom-call | flops 11274289152 | bytes 15728640 | tf_op jit(solution)/shard_map/pallas_call | solution.py:885
  460.5 5.7 shard_map.257
  484.3 13.2 %collective-permute-done.48.refs_1_ = bf16[1536,768]{1,0:T(8,128)(2,1)S(1)} collective-permute-done((bf16[1536,768]{1,0:T(8,128)(2,1)S(1)}, bf16[1536,768]{1,0:T(8,128)(2,1)S(1)}, u32[]{:S(2)}, u32[]{:S(2)}) %collective-permute-start.48) | collective-permute-done | bytes 2359328 | tf_op jit(solution)/shard_map/ppermute | solution.py:1079
  499.0 11.2 %collective-permute-done.49.refs_2_ = bf16[384,1536]{1,0:T(8,128)(2,1)S(1)} collective-permute-done((bf16[384,1536]{1,0:T(8,128)(2,1)}, bf16[384,1536]{1,0:T(8,128)(2,1)S(1)}, u32[]{:S(2)}, u32[]{:S(2)}) %collective-permute-start.49) | collective-permute-done | bytes 1179680 | tf_op jit(solution)/shard_map/ppermute | solution.py:1079
  523.0 13.2 %collective-permute-done.53.refs_3_ = bf16[384,768]{1,0:T(8,128)(2,1)S(1)} collective-permute-done((bf16[384,768]{1,0:T(8,128)(2,1)S(1)}, bf16[384,768]{1,0:T(8,128)(2,1)S(1)}, u32[]{:S(2)}, u32[]{:S(2)}) %collective-permute-start.53) | collective-permute-done | bytes 589856 | tf_op jit(solution)/shard_map/ppermute | solution.py:1079
  549.1 4.3 shard_map.268.refs_1_
  553.4 4.0 shard_map.269.refs_0_
  576.9 3.8 collective-permute-start.60
  580.8 10.2 %shard_map.276.refs_2_ = bf16[3,384,768]{2,1,0:T(8,128)(2,1)S(1)} custom-call(bf16[3072,384]{1,0:T(8,128)(2,1)} %get-tuple-element.345.base, bf16[3,3072,768]{2,1,0:T(8,128)(2,1)} %pinv_ref.9), custom_call_target="tpu_custom_call" | custom-call | flops 5435817984 | bytes 14155776 | tf_op jit(solution)/shard_map/pallas_call | solution.py:469
  607.1 3.7 collective-permute-start.63
  617.5 3.7 shard_map.283
  621.3 3.7 collective-permute-start.65
  679.5 3.8 collective-permute-done.72.refs_2_
  688.6 10.9 %shard_map.293 = (f32[32,128,128]{2,1,0:T(8,128)}, f32[32,128,128]{2,1,0:T(8,128)}, f32[32,128,128]{2,1,0:T(8,128)}, f32[32,128,128]{2,1,0:T(8,128)}) custom-call(s32[32]{0:T(128)S(1)} %convert_element_type.148.used, s32[1]{0:T(128)} %bitcast.27.flag.home, bf16[4112,128]{1,0:T(8,128)(2,1)} %shard_map.291.near, ...), custom_call_target="tpu_custom_call" | custom-call | flops 5905580032 | bytes 19922944 | tf_op jit(solution)/shard_map/pallas_call | solution.py:1010
  (503 shorter events, 302.8 us)
Async XLA Ops:
  0.6 19.9 %collective-permute-start.3 = (s32[1,504]{1,0:T(1,128)}, s32[1,504]{1,0:T(1,128)S(1)}, u32[]{:S(2)}, u32[]{:S(2)}) collective-permute-start(s32[1,504]{1,0:T(1,128)} %param.18), channel_id=1, source_target_pairs={{0,1},{1,0},{2,3},{3,2},{4,5},{5,4},{6,7},{7,6},{8,9},{9,8},{10,11... | collective-permute-start | bytes 6056 | tf_op jit(solution)/shard_map/ppermute | solution.py:1079
  3.7 43.3 %collective-permute-start.9 = (bf16[1024,768]{1,0:T(8,128)(2,1)}, bf16[1024,768]{1,0:T(8,128)(2,1)}, u32[]{:S(2)}, u32[]{:S(2)}) collective-permute-start(bf16[1024,768]{1,0:T(8,128)(2,1)} %param.15), channel_id=1, source_target_pairs={{0,2},{3,1},{4,6},{7,5},{8,10},{11,9},{12,14},{15,13},{16,18},{19,... | collective-permute-start | bytes 4718600 | tf_op jit(solution)/shard_map/ppermute | solution.py:1079
  20.6 20.6 %collective-permute-start.4 = (bf16[4112,128]{1,0:T(8,128)(2,1)}, bf16[4112,128]{1,0:T(8,128)(2,1)}, u32[]{:S(2)}, u32[]{:S(2)}) collective-permute-start(bf16[4112,128]{1,0:T(8,128)(2,1)} %get-tuple-element.407), channel_id=1, source_target_pairs={{1,3},{2,0},{5,7},{6,4},{9,11},{10,8},{13,15},{14,12},{17,19},{18,... | collective-permute-start | bytes 3158024 | tf_op jit(solution)/shard_map/ppermute | solution.py:1079
  36.5 35.0 %collective-permute-start.11 = (bf16[4112,128]{1,0:T(8,128)(2,1)}, bf16[4112,128]{1,0:T(8,128)(2,1)S(1)}, u32[]{:S(2)}, u32[]{:S(2)}) collective-permute-start(bf16[4112,128]{1,0:T(8,128)(2,1)} %get-tuple-element.200), channel_id=1, source_target_pairs={{0,4},{3,7},{4,0},{7,3},{8,12},{11,15},{12,8},{15,11},{16,20},{19,... | collective-permute-start | bytes 3158024 | tf_op jit(solution)/shard_map/ppermute | solution.py:1079
  39.0 34.9 %collective-permute-start.12 = (bf16[4112,128]{1,0:T(8,128)(2,1)}, bf16[4112,128]{1,0:T(8,128)(2,1)}, u32[]{:S(2)}, u32[]{:S(2)}) collective-permute-start(bf16[4112,128]{1,0:T(8,128)(2,1)} %get-tuple-element.200), channel_id=1, source_target_pairs={{0,1},{3,2},{4,5},{7,6},{8,9},{11,10},{12,13},{15,14},{16,17},{19,... | collective-permute-start | bytes 3158024 | tf_op jit(solution)/shard_map/ppermute | solution.py:1079
  41.2 23.6 %collective-permute-start.5 = (bf16[4112,128]{1,0:T(8,128)(2,1)}, bf16[4112,128]{1,0:T(8,128)(2,1)}, u32[]{:S(2)}, u32[]{:S(2)}) collective-permute-start(bf16[4112,128]{1,0:T(8,128)(2,1)} %collective-permute-done.4), channel_id=1, source_target_pairs={{0,4},{3,7},{4,0},{7,3},{8,12},{11,15},{12,8},{15,11},{16,20},{19,... | collective-permute-start | bytes 3158024 | tf_op jit(solution)/shard_map/ppermute | solution.py:1079
  44.6 22.5 %collective-permute-start.6 = (bf16[4112,128]{1,0:T(8,128)(2,1)}, bf16[4112,128]{1,0:T(8,128)(2,1)}, u32[]{:S(2)}, u32[]{:S(2)}) collective-permute-start(bf16[4112,128]{1,0:T(8,128)(2,1)} %collective-permute-done.4), channel_id=1, source_target_pairs={{0,1},{3,2},{4,5},{7,6},{8,9},{11,10},{12,13},{15,14},{16,17},{19,... | collective-permute-start | bytes 3158024 | tf_op jit(solution)/shard_map/ppermute | solution.py:1079
  46.9 22.1 %collective-permute-start.7 = (bf16[4112,128]{1,0:T(8,128)(2,1)}, bf16[4112,128]{1,0:T(8,128)(2,1)}, u32[]{:S(2)}, u32[]{:S(2)}) collective-permute-start(bf16[4112,128]{1,0:T(8,128)(2,1)} %collective-permute-done.4), channel_id=1, source_target_pairs={{0,8},{3,11},{4,12},{7,15},{8,16},{11,19},{12,20},{15,23},{16,24},... | collective-permute-start | bytes 3158024 | tf_op jit(solution)/shard_map/ppermute | solution.py:1079
  69.0 26.8 %collective-permute-start.15 = (bf16[4112,128]{1,0:T(8,128)(2,1)}, bf16[4112,128]{1,0:T(8,128)(2,1)}, u32[]{:S(2)}, u32[]{:S(2)}) collective-permute-start(bf16[4112,128]{1,0:T(8,128)(2,1)} %get-tuple-element.204), channel_id=1, source_target_pairs={{0,4},{3,7},{4,0},{7,3},{8,12},{11,15},{12,8},{15,11},{16,20},{19,... | collective-permute-start | bytes 3158024 | tf_op jit(solution)/shard_map/ppermute | solution.py:1079
  71.5 26.7 %collective-permute-start.16 = (bf16[4112,128]{1,0:T(8,128)(2,1)}, bf16[4112,128]{1,0:T(8,128)(2,1)}, u32[]{:S(2)}, u32[]{:S(2)}) collective-permute-start(bf16[4112,128]{1,0:T(8,128)(2,1)} %get-tuple-element.204), channel_id=1, source_target_pairs={{0,1},{3,2},{4,5},{7,6},{8,9},{11,10},{12,13},{15,14},{16,17},{19,... | collective-permute-start | bytes 3158024 | tf_op jit(solution)/shard_map/ppermute | solution.py:1079
  73.8 26.7 %collective-permute-start.17 = (bf16[4112,128]{1,0:T(8,128)(2,1)}, bf16[4112,128]{1,0:T(8,128)(2,1)}, u32[]{:S(2)}, u32[]{:S(2)}) collective-permute-start(bf16[4112,128]{1,0:T(8,128)(2,1)} %get-tuple-element.205), channel_id=1, source_target_pairs={{1,5},{2,6},{5,1},{6,2},{9,13},{10,14},{13,9},{14,10},{17,21},{18,... | collective-permute-start | bytes 3158024 | tf_op jit(solution)/shard_map/ppermute | solution.py:1079
  82.4 33.5 %collective-permute-start.18 = (bf16[4112,128]{1,0:T(8,128)(2,1)}, bf16[4112,128]{1,0:T(8,128)(2,1)}, u32[]{:S(2)}, u32[]{:S(2)}) collective-permute-start(bf16[4112,128]{1,0:T(8,128)(2,1)} %get-tuple-element.204), channel_id=1, source_target_pairs={{0,8},{3,11},{4,12},{7,15},{8,16},{11,19},{12,20},{15,23},{16,24},... | collective-permute-start | bytes 3158024 | tf_op jit(solution)/shard_map/ppermute | solution.py:1079
  85.9 32.3 %collective-permute-start.19 = (bf16[4112,128]{1,0:T(8,128)(2,1)}, bf16[4112,128]{1,0:T(8,128)(2,1)S(1)}, u32[]{:S(2)}, u32[]{:S(2)}) collective-permute-start(bf16[4112,128]{1,0:T(8,128)(2,1)} %get-tuple-element.208), channel_id=1, source_target_pairs={{0,4},{3,7},{4,0},{7,3},{8,12},{11,15},{12,8},{15,11},{16,20},{19,... | collective-permute-start | bytes 3158024 | tf_op jit(solution)/shard_map/ppermute | solution.py:1079
  95.9 24.7 %collective-permute-start.20 = (bf16[4112,128]{1,0:T(8,128)(2,1)}, bf16[4112,128]{1,0:T(8,128)(2,1)}, u32[]{:S(2)}, u32[]{:S(2)}) collective-permute-start(bf16[4112,128]{1,0:T(8,128)(2,1)} %get-tuple-element.208), channel_id=1, source_target_pairs={{0,1},{3,2},{4,5},{7,6},{8,9},{11,10},{12,13},{15,14},{16,17},{19,... | collective-permute-start | bytes 3158024 | tf_op jit(solution)/shard_map/ppermute | solution.py:1079
  98.2 26.6 %collective-permute-start.21 = (bf16[4112,128]{1,0:T(8,128)(2,1)}, bf16[4112,128]{1,0:T(8,128)(2,1)}, u32[]{:S(2)}, u32[]{:S(2)}) collective-permute-start(bf16[4112,128]{1,0:T(8,128)(2,1)} %get-tuple-element.209), channel_id=1, source_target_pairs={{0,1},{3,2},{4,5},{7,6},{8,9},{11,10},{12,13},{15,14},{16,17},{19,... | collective-permute-start | bytes 3158024 | tf_op jit(solution)/shard_map/ppermute | solution.py:1079
  100.5 26.0 %collective-permute-start.22 = (bf16[4112,128]{1,0:T(8,128)(2,1)}, bf16[4112,128]{1,0:T(8,128)(2,1)}, u32[]{:S(2)}, u32[]{:S(2)}) collective-permute-start(bf16[4112,128]{1,0:T(8,128)(2,1)} %get-tuple-element.208), channel_id=1, source_target_pairs={{0,8},{3,11},{4,12},{7,15},{8,16},{11,19},{12,20},{15,23},{16,24},... | collective-permute-start | bytes 3158024 | tf_op jit(solution)/shard_map/ppermute | solution.py:1079
  115.9 28.2 %collective-permute-start.23 = (bf16[4112,128]{1,0:T(8,128)(2,1)}, bf16[4112,128]{1,0:T(8,128)(2,1)S(1)}, u32[]{:S(2)}, u32[]{:S(2)}) collective-permute-start(bf16[4112,128]{1,0:T(8,128)(2,1)} %get-tuple-element.214), channel_id=1, source_target_pairs={{0,4},{3,7},{4,0},{7,3},{8,12},{11,15},{12,8},{15,11},{16,20},{19,... | collective-permute-start | bytes 3158024 | tf_op jit(solution)/shard_map/ppermute | solution.py:1079
  118.3 26.6 %collective-permute-start.24 = (bf16[4112,128]{1,0:T(8,128)(2,1)}, bf16[4112,128]{1,0:T(8,128)(2,1)}, u32[]{:S(2)}, u32[]{:S(2)}) collective-permute-start(bf16[4112,128]{1,0:T(8,128)(2,1)} %get-tuple-element.214), channel_id=1, source_target_pairs={{0,1},{3,2},{4,5},{7,6},{8,9},{11,10},{12,13},{15,14},{16,17},{19,... | collective-permute-start | bytes 3158024 | tf_op jit(solution)/shard_map/ppermute | solution.py:1079
  120.5 29.8 %collective-permute-start.26 = (bf16[4112,128]{1,0:T(8,128)(2,1)}, bf16[4112,128]{1,0:T(8,128)(2,1)}, u32[]{:S(2)}, u32[]{:S(2)}) collective-permute-start(bf16[4112,128]{1,0:T(8,128)(2,1)} %get-tuple-element.214), channel_id=1, source_target_pairs={{0,8},{3,11},{4,12},{7,15},{8,16},{11,19},{12,20},{15,23},{16,24},... | collective-permute-start | bytes 3158024 | tf_op jit(solution)/shard_map/ppermute | solution.py:1079
  124.8 20.1 %collective-permute-start.25 = (bf16[4112,128]{1,0:T(8,128)(2,1)}, bf16[4112,128]{1,0:T(8,128)(2,1)}, u32[]{:S(2)}, u32[]{:S(2)}) collective-permute-start(bf16[4112,128]{1,0:T(8,128)(2,1)} %get-tuple-element.217), channel_id=1, source_target_pairs={{1,5},{2,6},{5,1},{6,2},{9,13},{10,14},{13,9},{14,10},{17,21},{18,... | collective-permute-start | bytes 3158024 | tf_op jit(solution)/shard_map/ppermute | solution.py:1079
  126.5 27.8 %collective-permute-start.27 = (bf16[4112,128]{1,0:T(8,128)(2,1)}, bf16[4112,128]{1,0:T(8,128)(2,1)S(1)}, u32[]{:S(2)}, u32[]{:S(2)}) collective-permute-start(bf16[4112,128]{1,0:T(8,128)(2,1)} %get-tuple-element.215), channel_id=1, source_target_pairs={{0,1},{3,2},{4,5},{7,6},{8,9},{11,10},{12,13},{15,14},{16,17},{19,... | collective-permute-start | bytes 3158024 | tf_op jit(solution)/shard_map/ppermute | solution.py:1079
  144.1 25.9 %collective-permute-start.28 = (bf16[4112,128]{1,0:T(8,128)(2,1)}, bf16[4112,128]{1,0:T(8,128)(2,1)S(1)}, u32[]{:S(2)}, u32[]{:S(2)}) collective-permute-start(bf16[4112,128]{1,0:T(8,128)(2,1)} %broadcast_select_fusion.3), channel_id=1, source_target_pairs={{0,8},{1,9},{2,10},{3,11},{4,12},{5,13},{6,14},{7,15},{8,16},{9,17... | collective-permute-start | bytes 3158024 | tf_op jit(solution)/shard_map/ppermute | solution.py:1079
  150.3 22.1 %collective-permute-start.29 = (bf16[4112,128]{1,0:T(8,128)(2,1)}, bf16[4112,128]{1,0:T(8,128)(2,1)}, u32[]{:S(2)}, u32[]{:S(2)}) collective-permute-start(bf16[4112,128]{1,0:T(8,128)(2,1)} %get-tuple-element.225), channel_id=1, source_target_pairs={{1,5},{2,6},{5,1},{6,2},{9,13},{10,14},{13,9},{14,10},{17,21},{18,... | collective-permute-start | bytes 3158024 | tf_op jit(solution)/shard_map/ppermute | solution.py:1079
  154.3 30.1 %collective-permute-start.30 = (bf16[4112,128]{1,0:T(8,128)(2,1)}, bf16[4112,128]{1,0:T(8,128)(2,1)S(1)}, u32[]{:S(2)}, u32[]{:S(2)}) collective-permute-start(bf16[4112,128]{1,0:T(8,128)(2,1)} %broadcast_select_fusion.2), channel_id=1, source_target_pairs={{0,8},{1,9},{2,10},{3,11},{4,12},{5,13},{6,14},{7,15},{8,16},{9,17... | collective-permute-start | bytes 3158024 | tf_op jit(solution)/shard_map/ppermute | solution.py:1079
  252.5 23.3 %collective-permute-start.10 = (bf16[1024,768]{1,0:T(8,128)(2,1)S(1)}, bf16[1024,768]{1,0:T(8,128)(2,1)S(1)}, u32[]{:S(2)}, u32[]{:S(2)}) collective-permute-start(bf16[1024,768]{1,0:T(8,128)(2,1)S(1)} %copy-done.104), channel_id=1, source_target_pairs={{0,2},{3,1},{4,6},{7,5},{8,10},{11,9},{12,14},{15,13},{16,18},{19,... | collective-permute-start | bytes 4718600 | tf_op jit(solution)/shard_map/ppermute | solution.py:1079
  289.8 20.5 %collective-permute-start.38 = (bf16[1024,768]{1,0:T(8,128)(2,1)S(1)}, bf16[1024,768]{1,0:T(8,128)(2,1)S(1)}, u32[]{:S(2)}, u32[]{:S(2)}) collective-permute-start(bf16[1024,768]{1,0:T(8,128)(2,1)S(1)} %get-tuple-element.266), channel_id=1, source_target_pairs={{0,2},{1,3},{2,0},{3,1},{4,6},{5,7},{6,4},{7,5},{8,10},{9,11},{10,... | collective-permute-start | bytes 4718600 | tf_op jit(solution)/shard_map/ppermute | solution.py:1079
  312.1 34.9 %collective-permute-start.39 = (bf16[1536,768]{1,0:T(8,128)(2,1)}, bf16[1536,768]{1,0:T(8,128)(2,1)}, u32[]{:S(2)}, u32[]{:S(2)}) collective-permute-start(bf16[1536,768]{1,0:T(8,128)(2,1)} %get-tuple-element.273.own), channel_id=1, source_target_pairs={{1,0},{2,3},{5,4},{6,7},{9,8},{10,11},{13,12},{14,15},{17,16},{18,... | collective-permute-start | bytes 7077896 | tf_op jit(solution)/shard_map/ppermute | solution.py:1079
  347.0 38.3 %collective-permute-start.42 = (bf16[768,1536]{1,0:T(8,128)(2,1)}, bf16[768,1536]{1,0:T(8,128)(2,1)S(1)}, u32[]{:S(2)}, u32[]{:S(2)}) collective-permute-start(bf16[768,1536]{1,0:T(8,128)(2,1)} %get-tuple-element.287.own), channel_id=1, source_target_pairs={{1,0},{2,3},{5,4},{6,7},{9,8},{10,11},{13,12},{14,15},{17,16},{18,... | collective-permute-start | bytes 7077896 | tf_op jit(solution)/shard_map/ppermute | solution.py:1079
  383.7 41.3 %collective-permute-start.41 = (bf16[1024,768]{1,0:T(8,128)(2,1)}, bf16[1024,768]{1,0:T(8,128)(2,1)}, u32[]{:S(2)}, u32[]{:S(2)}) collective-permute-start(bf16[1024,768]{1,0:T(8,128)(2,1)} %get-tuple-element.279.own), channel_id=1, source_target_pairs={{0,2},{1,3},{2,0},{3,1},{4,6},{5,7},{6,4},{7,5},{8,10},{9,11},{10,... | collective-permute-start | bytes 4718600 | tf_op jit(solution)/shard_map/ppermute | solution.py:1079
  389.1 18.9 %collective-permute-start.43 = (bf16[384,1152]{1,0:T(8,128)(2,1)}, bf16[384,1152]{1,0:T(8,128)(2,1)S(1)}, u32[]{:S(2)}, u32[]{:S(2)}) collective-permute-start(bf16[384,1152]{1,0:T(8,128)(2,1)} %shard_map.249), channel_id=1, source_target_pairs={{1,5},{2,6},{5,1},{6,2},{9,13},{10,14},{13,9},{14,10},{17,21},{18,... | collective-permute-start | bytes 2654216 | tf_op jit(solution)/shard_map/ppermute | solution.py:1079
  411.4 42.5 %collective-permute-start.46 = (bf16[384,1536]{1,0:T(8,128)(2,1)}, bf16[384,1536]{1,0:T(8,128)(2,1)S(1)}, u32[]{:S(2)}, u32[]{:S(2)}) collective-permute-start(bf16[384,1536]{1,0:T(8,128)(2,1)} %shard_map.253), channel_id=1, source_target_pairs={{1,5},{2,6},{5,1},{6,2},{9,13},{10,14},{13,9},{14,10},{17,21},{18,... | collective-permute-start | bytes 3538952 | tf_op jit(solution)/shard_map/ppermute | solution.py:1079
  423.8 30.2 %collective-permute-start.45 = (bf16[384,1152]{1,0:T(8,128)(2,1)}, bf16[384,1152]{1,0:T(8,128)(2,1)S(1)}, u32[]{:S(2)}, u32[]{:S(2)}) collective-permute-start(bf16[384,1152]{1,0:T(8,128)(2,1)} %shard_map.252), channel_id=1, source_target_pairs={{1,0},{2,3},{5,4},{6,7},{9,8},{10,11},{13,12},{14,15},{17,16},{18,... | collective-permute-start | bytes 2654216 | tf_op jit(solution)/shard_map/ppermute | solution.py:1079
  466.8 30.7 %collective-permute-start.48 = (bf16[1536,768]{1,0:T(8,128)(2,1)S(1)}, bf16[1536,768]{1,0:T(8,128)(2,1)S(1)}, u32[]{:S(2)}, u32[]{:S(2)}) collective-permute-start(bf16[1536,768]{1,0:T(8,128)(2,1)S(1)} %copy-done.85), channel_id=1, source_target_pairs={{1,0},{2,3},{5,4},{6,7},{9,8},{10,11},{13,12},{14,15},{17,16},{18,... | collective-permute-start | bytes 7077896 | tf_op jit(solution)/shard_map/ppermute | solution.py:1079
  471.2 39.0 %collective-permute-start.49 = (bf16[384,1536]{1,0:T(8,128)(2,1)}, bf16[384,1536]{1,0:T(8,128)(2,1)S(1)}, u32[]{:S(2)}, u32[]{:S(2)}) collective-permute-start(bf16[384,1536]{1,0:T(8,128)(2,1)} %shard_map.259), channel_id=1, source_target_pairs={{1,0},{2,3},{5,4},{6,7},{9,8},{10,11},{13,12},{14,15},{17,16},{18,... | collective-permute-start | bytes 3538952 | tf_op jit(solution)/shard_map/ppermute | solution.py:1079
  511.2 25.8 %collective-permute-start.51 = (bf16[1536,384]{1,0:T(8,128)(2,1)}, bf16[1536,384]{1,0:T(8,128)(2,1)S(1)}, u32[]{:S(2)}, u32[]{:S(2)}) collective-permute-start(bf16[1536,384]{1,0:T(8,128)(2,1)} %get-tuple-element.308.own), channel_id=1, source_target_pairs={{1,5},{2,6},{5,1},{6,2},{9,13},{10,14},{13,9},{14,10},{17,21},{18,... | collective-permute-start | bytes 3538952 | tf_op jit(solution)/shard_map/ppermute | solution.py:1079
  514.7 22.3 %collective-permute-start.52 = (bf16[384,1152]{1,0:T(8,128)(2,1)}, bf16[384,1152]{1,0:T(8,128)(2,1)S(1)}, u32[]{:S(2)}, u32[]{:S(2)}) collective-permute-start(bf16[384,1152]{1,0:T(8,128)(2,1)} %shard_map.262), channel_id=1, source_target_pairs={{1,0},{2,3},{5,4},{6,7},{9,8},{10,11},{13,12},{14,15},{17,16},{18,... | collective-permute-start | bytes 2654216 | tf_op jit(solution)/shard_map/ppermute | solution.py:1079
  517.0 19.3 %collective-permute-start.53 = (bf16[384,768]{1,0:T(8,128)(2,1)S(1)}, bf16[384,768]{1,0:T(8,128)(2,1)S(1)}, u32[]{:S(2)}, u32[]{:S(2)}) collective-permute-start(bf16[384,768]{1,0:T(8,128)(2,1)S(1)} %convolution_convert_fusion.6.own), channel_id=1, source_target_pairs={{1,0},{2,3},{5,4},{6,7},{9,8},{10,11},{13,12},{14,15},{17,16},{18,... | collective-permute-start | bytes 1769480 | tf_op jit(solution)/shard_map/ppermute | solution.py:1079
  541.2 26.6 %collective-permute-start.55 = (bf16[1536,384]{1,0:T(8,128)(2,1)}, bf16[1536,384]{1,0:T(8,128)(2,1)S(1)}, u32[]{:S(2)}, u32[]{:S(2)}) collective-permute-start(bf16[1536,384]{1,0:T(8,128)(2,1)} %shard_map.265), channel_id=1, source_target_pairs={{1,0},{2,3},{5,4},{6,7},{9,8},{10,11},{13,12},{14,15},{17,16},{18,... | collective-permute-start | bytes 3538952 | tf_op jit(solution)/shard_map/ppermute | solution.py:1079
  576.9 26.9 %collective-permute-start.60 = (bf16[4112,128]{1,0:T(8,128)(2,1)}, bf16[4112,128]{1,0:T(8,128)(2,1)}, u32[]{:S(2)}, u32[]{:S(2)}) collective-permute-start(bf16[4112,128]{1,0:T(8,128)(2,1)} %get-tuple-element.404), channel_id=1, source_target_pairs={{0,4},{3,7},{4,0},{7,3},{8,12},{11,15},{12,8},{15,11},{16,20},{19,... | collective-permute-start | bytes 3158024 | tf_op jit(solution)/shard_map/ppermute | solution.py:1079
  598.7 18.9 %collective-permute-start.62 = (bf16[4112,128]{1,0:T(8,128)(2,1)}, bf16[4112,128]{1,0:T(8,128)(2,1)}, u32[]{:S(2)}, u32[]{:S(2)}) collective-permute-start(bf16[4112,128]{1,0:T(8,128)(2,1)} %get-tuple-element.351), channel_id=1, source_target_pairs={{0,8},{3,11},{4,12},{7,15},{8,16},{11,19},{12,20},{15,23},{16,24},... | collective-permute-start | bytes 3158024 | tf_op jit(solution)/shard_map/ppermute | solution.py:1079
  603.7 45.8 %collective-permute-start.58 = (bf16[1024,768]{1,0:T(8,128)(2,1)S(1)}, bf16[1024,768]{1,0:T(8,128)(2,1)}, u32[]{:S(2)}, u32[]{:S(2)}) collective-permute-start(bf16[1024,768]{1,0:T(8,128)(2,1)S(1)} %add_convert_fusion), channel_id=1, source_target_pairs={{0,2},{1,3},{2,0},{3,1},{4,6},{5,7},{6,4},{7,5},{8,10},{9,11},{10,... | collective-permute-start | bytes 4718600 | tf_op jit(solution)/shard_map/ppermute | solution.py:1079
  607.1 19.8 %collective-permute-start.63 = (bf16[4112,128]{1,0:T(8,128)(2,1)}, bf16[4112,128]{1,0:T(8,128)(2,1)}, u32[]{:S(2)}, u32[]{:S(2)}) collective-permute-start(bf16[4112,128]{1,0:T(8,128)(2,1)} %get-tuple-element.354), channel_id=1, source_target_pairs={{0,4},{3,7},{4,0},{7,3},{8,12},{11,15},{12,8},{15,11},{16,20},{19,... | collective-permute-start | bytes 3158024 | tf_op jit(solution)/shard_map/ppermute | solution.py:1079
  610.8 18.9 %collective-permute-start.64 = (bf16[4112,128]{1,0:T(8,128)(2,1)}, bf16[4112,128]{1,0:T(8,128)(2,1)}, u32[]{:S(2)}, u32[]{:S(2)}) collective-permute-start(bf16[4112,128]{1,0:T(8,128)(2,1)} %get-tuple-element.355), channel_id=1, source_target_pairs={{0,8},{3,11},{4,12},{7,15},{8,16},{11,19},{12,20},{15,23},{16,24},... | collective-permute-start | bytes 3158024 | tf_op jit(solution)/shard_map/ppermute | solution.py:1079
  624.9 18.9 %collective-permute-start.66 = (bf16[4112,128]{1,0:T(8,128)(2,1)}, bf16[4112,128]{1,0:T(8,128)(2,1)}, u32[]{:S(2)}, u32[]{:S(2)}) collective-permute-start(bf16[4112,128]{1,0:T(8,128)(2,1)} %get-tuple-element.360), channel_id=1, source_target_pairs={{0,8},{3,11},{4,12},{7,15},{8,16},{11,19},{12,20},{15,23},{16,24},... | collective-permute-start | bytes 3158024 | tf_op jit(solution)/shard_map/ppermute | solution.py:1079
  626.9 47.5 %collective-permute-start.56 = (bf16[1024,768]{1,0:T(8,128)(2,1)S(1)}, bf16[1024,768]{1,0:T(8,128)(2,1)}, u32[]{:S(2)}, u32[]{:S(2)}) collective-permute-start(bf16[1024,768]{1,0:T(8,128)(2,1)S(1)} %copy-done.80), channel_id=1, source_target_pairs={{0,1},{3,2},{4,5},{7,6},{8,9},{11,10},{12,13},{15,14},{16,17},{19,... | collective-permute-start | bytes 4718600 | tf_op jit(solution)/shard_map/ppermute | solution.py:1079
  633.2 20.9 %collective-permute-start.67 = (bf16[4112,128]{1,0:T(8,128)(2,1)}, bf16[4112,128]{1,0:T(8,128)(2,1)}, u32[]{:S(2)}, u32[]{:S(2)}) collective-permute-start(bf16[4112,128]{1,0:T(8,128)(2,1)} %get-tuple-element.364), channel_id=1, source_target_pairs={{0,4},{3,7},{4,0},{7,3},{8,12},{11,15},{12,8},{15,11},{16,20},{19,... | collective-permute-start | bytes 3158024 | tf_op jit(solution)/shard_map/ppermute | solution.py:1079
  649.5 18.9 %collective-permute-start.70 = (bf16[4112,128]{1,0:T(8,128)(2,1)}, bf16[4112,128]{1,0:T(8,128)(2,1)}, u32[]{:S(2)}, u32[]{:S(2)}) collective-permute-start(bf16[4112,128]{1,0:T(8,128)(2,1)} %get-tuple-element.370), channel_id=1, source_target_pairs={{0,8},{3,11},{4,12},{7,15},{8,16},{11,19},{12,20},{15,23},{16,24},... | collective-permute-start | bytes 3158024 | tf_op jit(solution)/shard_map/ppermute | solution.py:1079
  654.2 22.1 %collective-permute-start.59 = (bf16[1024,384]{1,0:T(8,128)(2,1)}, bf16[1024,384]{1,0:T(8,128)(2,1)}, u32[]{:S(2)}, u32[]{:S(2)}) collective-permute-start(bf16[1024,384]{1,0:T(8,128)(2,1)} %select_convert_fusion), channel_id=1, source_target_pairs={{0,1},{3,2},{4,5},{7,6},{8,9},{11,10},{12,13},{15,14},{16,17},{19,... | collective-permute-start | bytes 2359304 | tf_op jit(solution)/shard_map/ppermute | solution.py:1079
  (149 other events, 1104.5 us)

commit v8 on v7

--- a/solution.py
+++ b/solution.py
@@ -178,6 +178,7 @@
         in_specs=[anywhere] * len(arrays),
         out_specs=[anywhere] * len(arrays),
         input_output_aliases={i: i for i in range(len(arrays))},
+        compiler_params=pltpu.CompilerParams(vmem_limit_bytes=MIB),
     )(*[stay(a) if a.size > 32 * 1024 else a for a in arrays])
 
 
@@ -333,7 +334,7 @@
             ],
         ),
         input_output_aliases={} if target is None else {len(operands) + 1: 0},
-        compiler_params=params(),
+        compiler_params=params(12),
         cost_estimate=cost(own.size, own.size * 6),
     )(pos, part, *operands)
 
@@ -353,7 +354,7 @@
             in_specs=[pl.BlockSpec(block, lambda i, part: (part[0], 0)), fixed(block)],
             out_specs=fixed(block),
         ),
-        compiler_params=params(),
+        compiler_params=params(8),
         cost_estimate=cost(arrived.size, arrived.size * 6),
     )(part, stay(own), stay(arrived))
 
@@ -373,7 +374,7 @@
             in_specs=[pl.BlockSpec(block, lambda i, part: (1 - part[0], 0))],
             out_specs=fixed(block),
         ),
-        compiler_params=params(),
+        compiler_params=params(8),
         cost_estimate=cost(0, own.size * 2),
     )(part, stay(own))
 
@@ -413,7 +414,7 @@
             scratch_shapes=[pltpu.VMEM(own.shape, bf16), pltpu.SemaphoreType.DMA],
         ),
         input_output_aliases={len(operands): 0},
-        compiler_params=params(),
+        compiler_params=params(4),
     )(pos, *operands)
 
 
@@ -502,7 +503,7 @@
             in_specs=[half] * 3,
             out_specs=[rows_spec(HALF), fixed((1, HALF))],
         ),
-        compiler_params=params(),
+        compiler_params=params(8),
         cost_estimate=cost(tokens * D, tokens * D * 5),
     )(core, base, own, recv)
 
@@ -530,7 +531,7 @@
         grid=(1,),
         in_specs=[fixed(p.shape) for p in pieces],
         out_specs=fixed((owners, VEC_ROWS, BS)),
-        compiler_params=params(),
+        compiler_params=params(4),
         cost_estimate=cost(0, owners * vec_per * 8),
     )(*pieces).astype(bf16)
 
@@ -1018,7 +1019,7 @@
         ),
         compiler_params=params(),
         cost_estimate=cost(count * 88 * BS**3, count * BS * BS * 38),
-    )(used, home, stay(near), stay(far), *[stay(a) for a in arrays])
+    )(used, home, stay(near), stay(far), *arrays)
 
 
 def reduce_kernel(carrying, last, *refs):
@@ -1051,7 +1052,7 @@
         grid=(1,),
         in_specs=specs,
         out_specs=[whole] * len(outs),
-        compiler_params=params(),
+        compiler_params=params(8),
         cost_estimate=cost(payload * BS * 3, payload * BS * 12),
     )(*operands)
     return (made[0], None) if last else made
@@ -1071,7 +1072,6 @@
         self.y_in = [(at(d, t), at(d, 1 - t)) for d, t in away]
         self.x_home = [(at(d, t), at(d ^ 2, t)) for d, t in home]
         self.x_away = [(at(d, t), at(d ^ 2, t)) for d, t in away]
-        self.z_all = [(at(d, t), at((d + 4) % dp_n, t)) for d, t in pairs]
         self.z_home = [(at(d, t), at((d + 4) % dp_n, t)) for d, t in home]
 
 
@@ -1165,7 +1165,7 @@
         for j in range(5):
             for n in range(2):
                 moved = {}
-                if j < 3:
+                if j < 4:
                     moved["x"] = send(packs[n][j], routes.x_home)
                     moved["y"] = send(packs[n][j], routes.y_out)
                 if j:
@@ -1173,24 +1173,20 @@
                     moved["corner"] = send(source[n][j - 1], route)
                 if j < 3:
                     moved["z"] = send(packs[n][j], routes.z_home)
-                if j == 3:
-                    ring = jnp.where(home, across[n][2], over_y[n][2])
-                    moved["x"] = moved["y"] = send(ring, routes.z_all)
                 work = []
                 if j + n == 0:
                     work = [slot_other]
                 if 1 <= 2 * j + n <= CHUNKS:
                     work = [expand(2 * j + n - 1)]
                 if j < 4:
-                    keys_here = [k for k in moved if k != "y" or j < 3]
-                    token, *made = fence(token, *[moved[k] for k in keys_here], *work)
+                    token, *made = fence(token, *moved.values(), *work)
                     if j + n == 0:
                         slot_other = made.pop()
                     elif work:
                         chunks.append(made.pop())
-                    moved = dict(zip(keys_here, made))
+                    moved = dict(zip(moved, made))
                     across[n].append(moved["x"])
-                    over_y[n].append(moved["y"] if j < 3 else moved["x"])
+                    over_y[n].append(moved["y"])
                 if j < 3:
                     packs[n].append(moved["z"])
                 if j:
@@ -1328,14 +1324,15 @@
     gd0 = dot_tn(caches[low][9], grad_low).astype(bf16)
     gu0 = dot_tn(caches[low][8], du).astype(bf16)
     lse, gd0, gu0, xq1, ao1 = hold(caches[low][6], gd0, gu0, xq1, ao1)
-    aq1 = over(summed(gq1, xq1))
+    hq1 = summed(gq1, xq1)
     ad0 = over(gd0)
     xu0 = beside(gu0)
     buffer = place_tiles(("down", top), gd1, ad1, None)
     buffer = place_tiles(("up", top), gu1, au1, buffer)
     grad, grad_low, dq, dk, dv, dbo = attend_step(low, grad, part, other, lse)
-    vec, dbo, aq1, xu0, buffer = hold(vec, dbo, aq1, xu0, buffer)
+    vec, dbo, ad0, xu0, hq1, buffer = hold(vec, dbo, ad0, xu0, hq1, buffer)
     au0 = over(summed(gu0, xu0))
+    aq1 = over(hq1)
     own, dg1, ds1, dbq, dbv = qkv_back_call(low, dq, dk, dv, caches[low][0], vec, weights)
     recv = send(own, routes.core_all)
     gq0 = dot_tn(caches[low][1], jnp.concatenate([dq, dk, dv], axis=1)).astype(bf16)
@@ -1348,14 +1345,14 @@
         return jnp.concatenate([dot_tn(c, grad_emb).astype(bf16) for c in parts], axis=0)
 
     gbt = base_grad(chunks[middle:])
-    gbt, ad0, au0, xq0 = hold(gbt, ad0, au0, xq0)
+    gbt, au0, xq0 = hold(gbt, au0, xq0)
     xb = send(gbt, routes.x_away) if grid3 else None
     aq0 = over(summed(gq0, xq0))
     gbm = base_grad(chunks[:middle])
     vec_grad = pack_call([grad_emb_bias] + vec_grads[0] + vec_grads[1], dp_n, vec_per)
     go0 = dot_tn(caches[low][5], grad_low).astype(bf16)
     ao0, av = over(go0), over(vec_grad)
-    gbm, xb, aq0, ao0, av, buffer = hold(gbm, xb, aq0, ao0, av, buffer)
+    gbm, xb, aq0, ao0, av, aq1, buffer = hold(gbm, xb, aq0, ao0, av, aq1, buffer)
     ab = over(half_sum(half_at * 0, gbm, xb)) if grid3 else None
     buffer = place_tiles(("out", top), go1, ao1, buffer)
     buffer = place_tiles(("qkv", top), gq1, aq1, buffer)

time: 709 us -> 668 us (0.942)
  waiting for transfers between devices: 146 us -> 122 us
  local copies, waits for them, and re-layouts: 53.5 us -> 39.8 us
  starting transfers between devices: 148 us -> 156 us
    ppermute x74 -> x76, waiting for transfers between devices: 146 us -> 122 us  [send(): return lax.ppermute(value, AXES, route)]
    unnamed x248 -> x228, local copies, waits for them, and re-layouts: 47.3 us -> 35 us
    ppermute x74 -> x76, starting transfers between devices: 148 us -> 156 us  [send(): return lax.ppermute(value, AXES, route)]
  transfers between devices with their start and end apart: 74 -> 76, of which waited for: 29 -> 25; matrix products, arithmetic and copies ran while one was open for 9% -> 8% of each run, Pallas kernels for 30% -> 31%
where the time goes in v8:
time: 668 us; the launch traced here: 657 us
  Pallas kernels  283 us (42%)
  starting transfers between devices  156 us (23%)
  waiting for transfers between devices  122 us (18%)
  local copies, waits for them, and re-layouts  39.8 us (6%)
  matrix products  32.5 us (5%)
  other arithmetic  19.8 us (3%)
    ppermute x76, starting transfers between devices, send(): return lax.ppermute(value, AXES, route)  156 us
    ppermute x76, waiting for transfers between devices, send(): return lax.ppermute(value, AXES, route)  122 us
    pallas_call x2, Pallas kernels, attend_back_call(): pl.pallas_call(attend_back_kernel, out_shape=[shape(D, f32), shape(D, bf1...  45.6 us
    pallas_call x10, Pallas kernels, scatter_matrix(): pl.pallas_call(functools.partial(scatter_kernel, rows_n, cols_n, steps, p...  35.4 us
    unnamed x228, local copies, waits for them, and re-layouts  35 us
    pallas_call x2, Pallas kernels, attend_call(): pl.pallas_call(functools.partial(attend_kernel, layer), out_shape=[jax.Sh...  29.7 us
    dot_general x12, matrix products, dot_tn(): lax.dot_general(left, right, (((0,), (0,)), ((), ())), preferred_element_...  29.4 us
    pallas_call x8, Pallas kernels, reduce_call(): pl.pallas_call(functools.partial(reduce_kernel, carried is not None, last...  27.7 us
  transfers between devices with their start and end apart: 76, of which 25 were waited for; matrix products, arithmetic and copies ran while one was open for 8% of the time, Pallas kernels for 31%

profile of v8, /device:TPU:0, one launch (start us, length us, event | category | flops | bytes accessed | tf_op | source)
XLA Modules:
  0.0 657.2 jit_solution(16943690184536004127)
XLA Ops:
  22.3 6.8 %collective-permute-done.2.refs_3_ = bf16[4112,128]{1,0:T(8,128)(2,1)S(1)} collective-permute-done((bf16[4112,128]{1,0:T(8,128)(2,1)}, bf16[4112,128]{1,0:T(8,128)(2,1)S(1)}, u32[]{:S(2)}, u32[]{:S(2)}) %collective-permute-start.2) | collective-permute-done | bytes 1052704 | tf_op jit(solution)/shard_map/ppermute | solution.py:1079
  29.0 5.1 collective-permute-done.refs_1_
  52.2 5.5 shard_map.223.refs_4_
  69.8 6.0 shard_map.225.refs_5_
  79.9 8.3 %collective-permute-done.11.refs_1_ = bf16[4112,128]{1,0:T(8,128)(2,1)S(1)} collective-permute-done((bf16[4112,128]{1,0:T(8,128)(2,1)S(1)}, bf16[4112,128]{1,0:T(8,128)(2,1)S(1)}, u32[]{:S(2)}, u32[]{:S(2)}) %collective-permute-start.11) | collective-permute-done | bytes 1052704 | tf_op jit(solution)/shard_map/ppermute | solution.py:1079
  98.9 5.5 shard_map.227.refs_5_
  115.1 5.7 shard_map.229.refs_5_
  123.0 7.0 %collective-permute-start.29 = (bf16[4112,128]{1,0:T(8,128)(2,1)}, bf16[4112,128]{1,0:T(8,128)(2,1)S(1)}, u32[]{:S(2)}, u32[]{:S(2)}) collective-permute-start(bf16[4112,128]{1,0:T(8,128)(2,1)} %get-tuple-element.218), channel_id=1, source_target_pairs={{0,1},{3,2},{4,5},{7,6},{8,9},{11,10},{12,13},{15,14},{16,17},{19,... | collective-permute-start | bytes 3158024 | tf_op jit(solution)/shard_map/ppermute | solution.py:1079
  130.1 7.2 %collective-permute-start.28 = (bf16[4112,128]{1,0:T(8,128)(2,1)}, bf16[4112,128]{1,0:T(8,128)(2,1)S(1)}, u32[]{:S(2)}, u32[]{:S(2)}) collective-permute-start(bf16[4112,128]{1,0:T(8,128)(2,1)} %get-tuple-element.222), channel_id=1, source_target_pairs={{0,1},{3,2},{4,5},{7,6},{8,9},{11,10},{12,13},{15,14},{16,17},{19,... | collective-permute-start | bytes 3158024 | tf_op jit(solution)/shard_map/ppermute | solution.py:1079
  146.6 7.3 %collective-permute-done.28.refs_2_ = bf16[4112,128]{1,0:T(8,128)(2,1)S(1)} collective-permute-done((bf16[4112,128]{1,0:T(8,128)(2,1)}, bf16[4112,128]{1,0:T(8,128)(2,1)S(1)}, u32[]{:S(2)}, u32[]{:S(2)}) %collective-permute-start.28) | collective-permute-done | bytes 1052704 | tf_op jit(solution)/shard_map/ppermute | solution.py:1079
  153.9 8.6 %collective-permute-done.27.refs_1_ = bf16[4112,128]{1,0:T(8,128)(2,1)S(1)} collective-permute-done((bf16[4112,128]{1,0:T(8,128)(2,1)}, bf16[4112,128]{1,0:T(8,128)(2,1)S(1)}, u32[]{:S(2)}, u32[]{:S(2)}) %collective-permute-start.27) | collective-permute-done | bytes 1052704 | tf_op jit(solution)/shard_map/ppermute | solution.py:1079
  165.2 15.1 %collective-permute-done.30.refs_1_ = bf16[4112,128]{1,0:T(8,128)(2,1)S(1)} collective-permute-done((bf16[4112,128]{1,0:T(8,128)(2,1)}, bf16[4112,128]{1,0:T(8,128)(2,1)S(1)}, u32[]{:S(2)}, u32[]{:S(2)}) %collective-permute-start.30) | collective-permute-done | bytes 1052704 | tf_op jit(solution)/shard_map/ppermute | solution.py:1079
  184.2 14.2 %shard_map.234 = (bf16[3072,384]{1,0:T(8,128)(2,1)}, bf16[2304,384]{1,0:T(8,128)(2,1)}, bf16[768,384]{1,0:T(8,128)(2,1)}, bf16[3072,384]{1,0:T(8,128)(2,1)}, bf1...) custom-call(s32[16]{0:T(128)S(1)} %stack.95.owner, ...), custom_call_target="tpu_custom_call" | custom-call | bytes 33030144 | tf_op jit(solution)/shard_map/pallas_call | solution.py:243
  198.5 6.8 %shard_map.235.refs_0_ = bf16[1024,384]{1,0:T(8,128)(2,1)S(1)} custom-call(s32[1]{0:T(128)} %bitcast.6.half.part, bf16[1024,768]{1,0:T(8,128)(2,1)} %get-tuple-element.201.refs_0_, bf16[1024,768]{1,0:T(8,128)(2,1)} %get-tuple-element.205.refs_1_, bf16[1024,768]{1,0:T(8,128)(2,1)} %get-tuple-element.209.refs_2_, ...), custom_call_target="tpu_custom_call" | custom-call | flops 2415919104 | bytes 9437184 | tf_op jit(solution)/shard_map/pallas_call | solution.py:552
  209.2 4.8 shard_map.236
  214.1 14.9 %shard_map.237 = (bf16[1024,384]{1,0:T(8,128)(2,1)S(1)}, f32[8,1024]{1,0:T(8,128)S(1)}, bf16[1024,768]{1,0:T(8,128)(2,1)S(1)}) custom-call(s32[4]{0:T(128)S(1)} %get-tuple-element.431.low_ref, s32[4]{0:T(128)S(1)} %get-tuple-element.424.high_ref, bf16[1024,384]{1,0:T(8,128)(2,1)S(1)} %get-tuple-element.244.q_ref, ...), custom_call_target="tpu_custom_call" | custom-call | flops 6442450944 | bytes 6291456 | tf_op jit(solution)/shard_map/pallas_call | solution.py:679
  233.4 9.4 %shard_map.238 = (f32[1024,768]{1,0:T(8,128)S(1)}, bf16[1024,768]{1,0:T(8,128)(2,1)}, bf16[1024,1536]{1,0:T(8,128)(2,1)}, bf16[1024,1536]{1,0:T(8,128)(2,1)}, bf16[1024,768]{1,0:T(8,128)(2,1)S(1)}) custom-call(f32[1024,768]{1,0:T(8,128)S(1)} %get-tuple-element.243.base.hid, bf16[1024,768]{1,0:T(8,128)(2,1)S(1)} %get-tuple-element.248.own, ...), custom_call_target="tpu_custom_call" | custom-call | flops 4831838208 | bytes 18874368 | tf_op jit(solution)/shard_map/pallas_call | solution.py:742
  246.2 4.4 shard_map.239
  250.6 14.8 %shard_map.240 = (bf16[1024,384]{1,0:T(8,128)(2,1)S(1)}, f32[8,1024]{1,0:T(8,128)S(1)}, bf16[1024,768]{1,0:T(8,128)(2,1)S(1)}) custom-call(s32[4]{0:T(128)S(1)} %get-tuple-element.431.low_ref, s32[4]{0:T(128)S(1)} %get-tuple-element.424.high_ref, bf16[1024,384]{1,0:T(8,128)(2,1)S(1)} %get-tuple-element.255.q_ref, ...), custom_call_target="tpu_custom_call" | custom-call | flops 6442450944 | bytes 6291456 | tf_op jit(solution)/shard_map/pallas_call | solution.py:679
  269.0 9.4 %shard_map.241 = (f32[1024,768]{1,0:T(8,128)S(1)}, bf16[1024,768]{1,0:T(8,128)(2,1)}, bf16[1024,1536]{1,0:T(8,128)(2,1)}, bf16[1024,1536]{1,0:T(8,128)(2,1)}, bf16[1024,768]{1,0:T(8,128)(2,1)S(1)}) custom-call(f32[1024,768]{1,0:T(8,128)S(1)} %get-tuple-element.254.base.hid, bf16[1024,768]{1,0:T(8,128)(2,1)S(1)} %get-tuple-element.259.own, ...), custom_call_target="tpu_custom_call" | custom-call | flops 4831838208 | bytes 18874368 | tf_op jit(solution)/shard_map/pallas_call | solution.py:742
  280.5 11.3 %shard_map.242 = (bf16[1024,768]{1,0:T(8,128)(2,1)S(1)}, bf16[1024,1536]{1,0:T(8,128)(2,1)S(1)}, bf16[1024,768]{1,0:T(8,128)(2,1)S(1)}, f32[1,768]{1,0:T(1,128)S...) custom-call(bf16[1024,768]{1,0:T(8,128)(2,1)S(1)} %broadcast_select_fusion.refs_0_, ...), custom_call_target="tpu_custom_call" | custom-call | flops 4831838208 | bytes 18874368 | tf_op jit(solution)/shard_map/pallas_call | solution.py:794
  292.0 4.0 convolution_convert_fusion.3.refs_1_
  296.0 4.0 convolution_convert_fusion.2.refs_2_
  303.4 22.8 %shard_map.244 = (f32[1024,768]{1,0:T(8,128)S(1)}, bf16[1024,768]{1,0:T(8,128)(2,1)S(1)}, bf16[1024,384]{1,0:T(8,128)(2,1)S(1)}, bf16[1024,384]{1,0:T(8,128)(2,1...) custom-call(s32[4]{0:T(128)S(1)} %get-tuple-element.430.low_ref, s32[4]{0:T(128)S(1)} %get-tuple-element.425.high_ref, ...), custom_call_target="tpu_custom_call" | custom-call | flops 11274289152 | bytes 15728640 | tf_op jit(solution)/shard_map/pallas_call | solution.py:886
  326.3 6.4 collective-permute-done.41.refs_2_
  335.4 5.6 shard_map.246
  346.3 11.2 %shard_map.247 = (f32[1024,768]{1,0:T(8,128)S(1)}, bf16[1024,768]{1,0:T(8,128)(2,1)S(1)}, bf16[1024,1536]{1,0:T(8,128)(2,1)S(1)}, bf16[1024,768]{1,0:T(8,128)(2,...) custom-call(f32[1024,768]{1,0:T(8,128)S(1)} %get-tuple-element.273.refs_0_, ...), custom_call_target="tpu_custom_call" | custom-call | flops 4831838208 | bytes 18874368 | tf_op jit(solution)/shard_map/pallas_call | solution.py:794
  358.0 7.0 %collective-permute-done.44.refs_1_ = bf16[768,1536]{1,0:T(8,128)(2,1)S(1)} collective-permute-done((bf16[768,1536]{1,0:T(8,128)(2,1)}, bf16[768,1536]{1,0:T(8,128)(2,1)S(1)}, u32[]{:S(2)}, u32[]{:S(2)}) %collective-permute-start.44) | collective-permute-done | bytes 2359328 | tf_op jit(solution)/shard_map/ppermute | solution.py:1079
  369.5 4.0 convolution_convert_fusion.1.refs_1_
  374.9 4.0 convolution_convert_fusion.refs_2_
  378.9 6.3 collective-permute-done.46.refs_4_
  391.0 4.2 shard_map.254.refs_1_
  395.2 4.2 shard_map.255.refs_5_
  402.1 22.8 %shard_map.251 = (f32[1024,768]{1,0:T(8,128)S(1)}, bf16[1024,768]{1,0:T(8,128)(2,1)S(1)}, bf16[1024,384]{1,0:T(8,128)(2,1)S(1)}, bf16[1024,384]{1,0:T(8,128)(2,1...) custom-call(s32[4]{0:T(128)S(1)} %get-tuple-element.430.low_ref, s32[4]{0:T(128)S(1)} %get-tuple-element.425.high_ref, ...), custom_call_target="tpu_custom_call" | custom-call | flops 11274289152 | bytes 15728640 | tf_op jit(solution)/shard_map/pallas_call | solution.py:886
  426.7 5.6 shard_map.257
  448.1 5.7 collective-permute-done.50.refs_1_
  468.0 26.2 %collective-permute-done.54.refs_3_ = bf16[384,768]{1,0:T(8,128)(2,1)S(1)} collective-permute-done((bf16[384,768]{1,0:T(8,128)(2,1)S(1)}, bf16[384,768]{1,0:T(8,128)(2,1)S(1)}, u32[]{:S(2)}, u32[]{:S(2)}) %collective-permute-start.54) | collective-permute-done | bytes 589856 | tf_op jit(solution)/shard_map/ppermute | solution.py:1079
  507.0 4.2 shard_map.268.refs_1_
  511.2 4.1 shard_map.269.refs_0_
  522.1 3.6 shard_map.273.refs_1_
  533.7 3.9 collective-permute-start.62
  537.6 10.2 %shard_map.276.refs_2_ = bf16[3,384,768]{2,1,0:T(8,128)(2,1)S(1)} custom-call(bf16[3072,384]{1,0:T(8,128)(2,1)} %get-tuple-element.351.base, bf16[3,3072,768]{2,1,0:T(8,128)(2,1)} %pinv_ref.9), custom_call_target="tpu_custom_call" | custom-call | flops 5435817984 | bytes 14155776 | tf_op jit(solution)/shard_map/pallas_call | solution.py:470
  555.3 4.2 collective-permute-start.64
  569.7 5.2 collective-permute-start.66
  576.2 3.7 shard_map.283
  616.7 3.6 shard_map.289
  625.3 3.8 collective-permute-done.72.refs_2_
  648.1 8.7 %shard_map.293 = (f32[32,128,128]{2,1,0:T(8,128)}, f32[32,128,128]{2,1,0:T(8,128)}, f32[32,128,128]{2,1,0:T(8,128)}, f32[32,128,128]{2,1,0:T(8,128)}) custom-call(s32[32]{0:T(128)S(1)} %convert_element_type.148.used, s32[1]{0:T(128)} %bitcast.27.flag.home, bf16[4112,128]{1,0:T(8,128)(2,1)} %shard_map.291.near, ...), custom_call_target="tpu_custom_call" | custom-call | flops 5905580032 | bytes 19922944 | tf_op jit(solution)/shard_map/pallas_call | solution.py:1011
  (485 shorter events, 276.3 us)
Async XLA Ops:
  0.6 20.0 %collective-permute-start.3 = (s32[1,504]{1,0:T(1,128)}, s32[1,504]{1,0:T(1,128)S(1)}, u32[]{:S(2)}, u32[]{:S(2)}) collective-permute-start(s32[1,504]{1,0:T(1,128)} %param.18), channel_id=1, source_target_pairs={{0,1},{1,0},{2,3},{3,2},{4,5},{5,4},{6,7},{7,6},{8,9},{9,8},{10,11... | collective-permute-start | bytes 6056 | tf_op jit(solution)/shard_map/ppermute | solution.py:1079
  3.7 42.2 %collective-permute-start.9 = (bf16[1024,768]{1,0:T(8,128)(2,1)}, bf16[1024,768]{1,0:T(8,128)(2,1)}, u32[]{:S(2)}, u32[]{:S(2)}) collective-permute-start(bf16[1024,768]{1,0:T(8,128)(2,1)} %param.15), channel_id=1, source_target_pairs={{0,2},{3,1},{4,6},{7,5},{8,10},{11,9},{12,14},{15,13},{16,18},{19,... | collective-permute-start | bytes 4718600 | tf_op jit(solution)/shard_map/ppermute | solution.py:1079
  35.2 29.4 %collective-permute-start.13 = (bf16[4112,128]{1,0:T(8,128)(2,1)}, bf16[4112,128]{1,0:T(8,128)(2,1)S(1)}, u32[]{:S(2)}, u32[]{:S(2)}) collective-permute-start(bf16[4112,128]{1,0:T(8,128)(2,1)} %get-tuple-element.204), channel_id=1, source_target_pairs={{0,1},{3,2},{4,5},{7,6},{8,9},{11,10},{12,13},{15,14},{16,17},{19,... | collective-permute-start | bytes 3158024 | tf_op jit(solution)/shard_map/ppermute | solution.py:1079
  36.5 22.4 %collective-permute-start.7 = (bf16[4112,128]{1,0:T(8,128)(2,1)}, bf16[4112,128]{1,0:T(8,128)(2,1)}, u32[]{:S(2)}, u32[]{:S(2)}) collective-permute-start(bf16[4112,128]{1,0:T(8,128)(2,1)} %collective-permute-done.4), channel_id=1, source_target_pairs={{0,8},{3,11},{4,12},{7,15},{8,16},{11,19},{12,20},{15,23},{16,24},... | collective-permute-start | bytes 3158024 | tf_op jit(solution)/shard_map/ppermute | solution.py:1079
  40.0 20.4 %collective-permute-start.6 = (bf16[4112,128]{1,0:T(8,128)(2,1)}, bf16[4112,128]{1,0:T(8,128)(2,1)}, u32[]{:S(2)}, u32[]{:S(2)}) collective-permute-start(bf16[4112,128]{1,0:T(8,128)(2,1)} %collective-permute-done.4), channel_id=1, source_target_pairs={{0,1},{3,2},{4,5},{7,6},{8,9},{11,10},{12,13},{15,14},{16,17},{19,... | collective-permute-start | bytes 3158024 | tf_op jit(solution)/shard_map/ppermute | solution.py:1079
  42.3 21.5 %collective-permute-start.5 = (bf16[4112,128]{1,0:T(8,128)(2,1)}, bf16[4112,128]{1,0:T(8,128)(2,1)}, u32[]{:S(2)}, u32[]{:S(2)}) collective-permute-start(bf16[4112,128]{1,0:T(8,128)(2,1)} %collective-permute-done.4), channel_id=1, source_target_pairs={{0,4},{3,7},{4,0},{7,3},{8,12},{11,15},{12,8},{15,11},{16,20},{19,... | collective-permute-start | bytes 3158024 | tf_op jit(solution)/shard_map/ppermute | solution.py:1079
  45.9 22.2 %collective-permute-start.14 = (bf16[4112,128]{1,0:T(8,128)(2,1)}, bf16[4112,128]{1,0:T(8,128)(2,1)S(1)}, u32[]{:S(2)}, u32[]{:S(2)}) collective-permute-start(bf16[4112,128]{1,0:T(8,128)(2,1)} %get-tuple-element.203), channel_id=1, source_target_pairs={{0,8},{3,11},{4,12},{7,15},{8,16},{11,19},{12,20},{15,23},{16,24},... | collective-permute-start | bytes 3158024 | tf_op jit(solution)/shard_map/ppermute | solution.py:1079
  60.4 27.8 %collective-permute-start.11 = (bf16[4112,128]{1,0:T(8,128)(2,1)S(1)}, bf16[4112,128]{1,0:T(8,128)(2,1)S(1)}, u32[]{:S(2)}, u32[]{:S(2)}) collective-permute-start(bf16[4112,128]{1,0:T(8,128)(2,1)S(1)} %copy-done.84), channel_id=1, source_target_pairs={{0,4},{3,7},{4,0},{7,3},{8,12},{11,15},{12,8},{15,11},{16,20},{19,... | collective-permute-start | bytes 3158024 | tf_op jit(solution)/shard_map/ppermute | solution.py:1079
  63.8 26.7 %collective-permute-start.17 = (bf16[4112,128]{1,0:T(8,128)(2,1)}, bf16[4112,128]{1,0:T(8,128)(2,1)S(1)}, u32[]{:S(2)}, u32[]{:S(2)}) collective-permute-start(bf16[4112,128]{1,0:T(8,128)(2,1)} %get-tuple-element.208), channel_id=1, source_target_pairs={{1,5},{2,6},{5,1},{6,2},{9,13},{10,14},{13,9},{14,10},{17,21},{18,... | collective-permute-start | bytes 3158024 | tf_op jit(solution)/shard_map/ppermute | solution.py:1079
  64.6 29.5 %collective-permute-start.18 = (bf16[4112,128]{1,0:T(8,128)(2,1)}, bf16[4112,128]{1,0:T(8,128)(2,1)S(1)}, u32[]{:S(2)}, u32[]{:S(2)}) collective-permute-start(bf16[4112,128]{1,0:T(8,128)(2,1)} %get-tuple-element.207), channel_id=1, source_target_pairs={{0,8},{3,11},{4,12},{7,15},{8,16},{11,19},{12,20},{15,23},{16,24},... | collective-permute-start | bytes 3158024 | tf_op jit(solution)/shard_map/ppermute | solution.py:1079
  68.1 27.4 %collective-permute-start.16 = (bf16[4112,128]{1,0:T(8,128)(2,1)}, bf16[4112,128]{1,0:T(8,128)(2,1)S(1)}, u32[]{:S(2)}, u32[]{:S(2)}) collective-permute-start(bf16[4112,128]{1,0:T(8,128)(2,1)} %get-tuple-element.207), channel_id=1, source_target_pairs={{0,1},{3,2},{4,5},{7,6},{8,9},{11,10},{12,13},{15,14},{16,17},{19,... | collective-permute-start | bytes 3158024 | tf_op jit(solution)/shard_map/ppermute | solution.py:1079
  77.0 28.6 %collective-permute-start.15 = (bf16[4112,128]{1,0:T(8,128)(2,1)}, bf16[4112,128]{1,0:T(8,128)(2,1)S(1)}, u32[]{:S(2)}, u32[]{:S(2)}) collective-permute-start(bf16[4112,128]{1,0:T(8,128)(2,1)} %get-tuple-element.207), channel_id=1, source_target_pairs={{0,4},{3,7},{4,0},{7,3},{8,12},{11,15},{12,8},{15,11},{16,20},{19,... | collective-permute-start | bytes 3158024 | tf_op jit(solution)/shard_map/ppermute | solution.py:1079
  89.2 20.9 %collective-permute-start.21 = (bf16[4112,128]{1,0:T(8,128)(2,1)}, bf16[4112,128]{1,0:T(8,128)(2,1)S(1)}, u32[]{:S(2)}, u32[]{:S(2)}) collective-permute-start(bf16[4112,128]{1,0:T(8,128)(2,1)} %get-tuple-element.212), channel_id=1, source_target_pairs={{0,1},{3,2},{4,5},{7,6},{8,9},{11,10},{12,13},{15,14},{16,17},{19,... | collective-permute-start | bytes 3158024 | tf_op jit(solution)/shard_map/ppermute | solution.py:1079
  90.6 20.9 %collective-permute-start.22 = (bf16[4112,128]{1,0:T(8,128)(2,1)}, bf16[4112,128]{1,0:T(8,128)(2,1)S(1)}, u32[]{:S(2)}, u32[]{:S(2)}) collective-permute-start(bf16[4112,128]{1,0:T(8,128)(2,1)} %get-tuple-element.211), channel_id=1, source_target_pairs={{0,8},{3,11},{4,12},{7,15},{8,16},{11,19},{12,20},{15,23},{16,24},... | collective-permute-start | bytes 3158024 | tf_op jit(solution)/shard_map/ppermute | solution.py:1079
  94.1 20.3 %collective-permute-start.20 = (bf16[4112,128]{1,0:T(8,128)(2,1)}, bf16[4112,128]{1,0:T(8,128)(2,1)S(1)}, u32[]{:S(2)}, u32[]{:S(2)}) collective-permute-start(bf16[4112,128]{1,0:T(8,128)(2,1)} %get-tuple-element.211), channel_id=1, source_target_pairs={{0,1},{3,2},{4,5},{7,6},{8,9},{11,10},{12,13},{15,14},{16,17},{19,... | collective-permute-start | bytes 3158024 | tf_op jit(solution)/shard_map/ppermute | solution.py:1079
  95.5 26.6 %collective-permute-start.19 = (bf16[4112,128]{1,0:T(8,128)(2,1)}, bf16[4112,128]{1,0:T(8,128)(2,1)S(1)}, u32[]{:S(2)}, u32[]{:S(2)}) collective-permute-start(bf16[4112,128]{1,0:T(8,128)(2,1)} %get-tuple-element.211), channel_id=1, source_target_pairs={{0,4},{3,7},{4,0},{7,3},{8,12},{11,15},{12,8},{15,11},{16,20},{19,... | collective-permute-start | bytes 3158024 | tf_op jit(solution)/shard_map/ppermute | solution.py:1079
  106.6 30.7 %collective-permute-start.26 = (bf16[4112,128]{1,0:T(8,128)(2,1)}, bf16[4112,128]{1,0:T(8,128)(2,1)S(1)}, u32[]{:S(2)}, u32[]{:S(2)}) collective-permute-start(bf16[4112,128]{1,0:T(8,128)(2,1)} %get-tuple-element.217), channel_id=1, source_target_pairs={{0,8},{3,11},{4,12},{7,15},{8,16},{11,19},{12,20},{15,23},{16,24},... | collective-permute-start | bytes 3158024 | tf_op jit(solution)/shard_map/ppermute | solution.py:1079
  110.1 29.6 %collective-permute-start.24 = (bf16[4112,128]{1,0:T(8,128)(2,1)}, bf16[4112,128]{1,0:T(8,128)(2,1)S(1)}, u32[]{:S(2)}, u32[]{:S(2)}) collective-permute-start(bf16[4112,128]{1,0:T(8,128)(2,1)} %get-tuple-element.217), channel_id=1, source_target_pairs={{0,1},{3,2},{4,5},{7,6},{8,9},{11,10},{12,13},{15,14},{16,17},{19,... | collective-permute-start | bytes 3158024 | tf_op jit(solution)/shard_map/ppermute | solution.py:1079
  111.5 28.3 %collective-permute-start.23 = (bf16[4112,128]{1,0:T(8,128)(2,1)}, bf16[4112,128]{1,0:T(8,128)(2,1)S(1)}, u32[]{:S(2)}, u32[]{:S(2)}) collective-permute-start(bf16[4112,128]{1,0:T(8,128)(2,1)} %get-tuple-element.217), channel_id=1, source_target_pairs={{0,4},{3,7},{4,0},{7,3},{8,12},{11,15},{12,8},{15,11},{16,20},{19,... | collective-permute-start | bytes 3158024 | tf_op jit(solution)/shard_map/ppermute | solution.py:1079
  123.0 20.2 %collective-permute-start.29 = (bf16[4112,128]{1,0:T(8,128)(2,1)}, bf16[4112,128]{1,0:T(8,128)(2,1)S(1)}, u32[]{:S(2)}, u32[]{:S(2)}) collective-permute-start(bf16[4112,128]{1,0:T(8,128)(2,1)} %get-tuple-element.218), channel_id=1, source_target_pairs={{0,1},{3,2},{4,5},{7,6},{8,9},{11,10},{12,13},{15,14},{16,17},{19,... | collective-permute-start | bytes 3158024 | tf_op jit(solution)/shard_map/ppermute | solution.py:1079
  130.1 23.9 %collective-permute-start.28 = (bf16[4112,128]{1,0:T(8,128)(2,1)}, bf16[4112,128]{1,0:T(8,128)(2,1)S(1)}, u32[]{:S(2)}, u32[]{:S(2)}) collective-permute-start(bf16[4112,128]{1,0:T(8,128)(2,1)} %get-tuple-element.222), channel_id=1, source_target_pairs={{0,1},{3,2},{4,5},{7,6},{8,9},{11,10},{12,13},{15,14},{16,17},{19,... | collective-permute-start | bytes 3158024 | tf_op jit(solution)/shard_map/ppermute | solution.py:1079
  137.3 25.2 %collective-permute-start.27 = (bf16[4112,128]{1,0:T(8,128)(2,1)}, bf16[4112,128]{1,0:T(8,128)(2,1)S(1)}, u32[]{:S(2)}, u32[]{:S(2)}) collective-permute-start(bf16[4112,128]{1,0:T(8,128)(2,1)} %get-tuple-element.222), channel_id=1, source_target_pairs={{0,4},{3,7},{4,0},{7,3},{8,12},{11,15},{12,8},{15,11},{16,20},{19,... | collective-permute-start | bytes 3158024 | tf_op jit(solution)/shard_map/ppermute | solution.py:1079
  141.1 23.8 %collective-permute-start.32 = (bf16[4112,128]{1,0:T(8,128)(2,1)}, bf16[4112,128]{1,0:T(8,128)(2,1)S(1)}, u32[]{:S(2)}, u32[]{:S(2)}) collective-permute-start(bf16[4112,128]{1,0:T(8,128)(2,1)} %get-tuple-element.227), channel_id=1, source_target_pairs={{1,5},{2,6},{5,1},{6,2},{9,13},{10,14},{13,9},{14,10},{17,21},{18,... | collective-permute-start | bytes 3158024 | tf_op jit(solution)/shard_map/ppermute | solution.py:1079
  141.8 23.4 %collective-permute-start.31 = (bf16[4112,128]{1,0:T(8,128)(2,1)}, bf16[4112,128]{1,0:T(8,128)(2,1)S(1)}, u32[]{:S(2)}, u32[]{:S(2)}) collective-permute-start(bf16[4112,128]{1,0:T(8,128)(2,1)} %get-tuple-element.223), channel_id=1, source_target_pairs={{0,1},{3,2},{4,5},{7,6},{8,9},{11,10},{12,13},{15,14},{16,17},{19,... | collective-permute-start | bytes 3158024 | tf_op jit(solution)/shard_map/ppermute | solution.py:1079
  143.2 37.1 %collective-permute-start.30 = (bf16[4112,128]{1,0:T(8,128)(2,1)}, bf16[4112,128]{1,0:T(8,128)(2,1)S(1)}, u32[]{:S(2)}, u32[]{:S(2)}) collective-permute-start(bf16[4112,128]{1,0:T(8,128)(2,1)} %get-tuple-element.223), channel_id=1, source_target_pairs={{0,4},{3,7},{4,0},{7,3},{8,12},{11,15},{12,8},{15,11},{16,20},{19,... | collective-permute-start | bytes 3158024 | tf_op jit(solution)/shard_map/ppermute | solution.py:1079
  163.5 19.4 %collective-permute-start.33 = (bf16[4112,128]{1,0:T(8,128)(2,1)}, bf16[4112,128]{1,0:T(8,128)(2,1)S(1)}, u32[]{:S(2)}, u32[]{:S(2)}) collective-permute-start(bf16[4112,128]{1,0:T(8,128)(2,1)} %get-tuple-element.225), channel_id=1, source_target_pairs={{0,1},{3,2},{4,5},{7,6},{8,9},{11,10},{12,13},{15,14},{16,17},{19,... | collective-permute-start | bytes 3158024 | tf_op jit(solution)/shard_map/ppermute | solution.py:1079
  243.2 22.9 %collective-permute-start.10 = (bf16[1024,768]{1,0:T(8,128)(2,1)S(1)}, bf16[1024,768]{1,0:T(8,128)(2,1)S(1)}, u32[]{:S(2)}, u32[]{:S(2)}) collective-permute-start(bf16[1024,768]{1,0:T(8,128)(2,1)S(1)} %copy-done.95), channel_id=1, source_target_pairs={{0,2},{3,1},{4,6},{7,5},{8,10},{11,9},{12,14},{15,13},{16,18},{19,... | collective-permute-start | bytes 4718600 | tf_op jit(solution)/shard_map/ppermute | solution.py:1079
  280.1 19.8 %collective-permute-start.40 = (bf16[1024,768]{1,0:T(8,128)(2,1)S(1)}, bf16[1024,768]{1,0:T(8,128)(2,1)S(1)}, u32[]{:S(2)}, u32[]{:S(2)}) collective-permute-start(bf16[1024,768]{1,0:T(8,128)(2,1)S(1)} %get-tuple-element.271), channel_id=1, source_target_pairs={{0,2},{1,3},{2,0},{3,1},{4,6},{5,7},{6,4},{7,5},{8,10},{9,11},{10,... | collective-permute-start | bytes 4718600 | tf_op jit(solution)/shard_map/ppermute | solution.py:1079
  301.7 30.9 %collective-permute-start.41 = (bf16[1536,768]{1,0:T(8,128)(2,1)}, bf16[1536,768]{1,0:T(8,128)(2,1)S(1)}, u32[]{:S(2)}, u32[]{:S(2)}) collective-permute-start(bf16[1536,768]{1,0:T(8,128)(2,1)} %get-tuple-element.278.own), channel_id=1, source_target_pairs={{1,0},{2,3},{5,4},{6,7},{9,8},{10,11},{13,12},{14,15},{17,16},{18,... | collective-permute-start | bytes 7077896 | tf_op jit(solution)/shard_map/ppermute | solution.py:1079
  334.1 30.9 %collective-permute-start.44 = (bf16[768,1536]{1,0:T(8,128)(2,1)}, bf16[768,1536]{1,0:T(8,128)(2,1)S(1)}, u32[]{:S(2)}, u32[]{:S(2)}) collective-permute-start(bf16[768,1536]{1,0:T(8,128)(2,1)} %get-tuple-element.292.own), channel_id=1, source_target_pairs={{1,0},{2,3},{5,4},{6,7},{9,8},{10,11},{13,12},{14,15},{17,16},{18,... | collective-permute-start | bytes 7077896 | tf_op jit(solution)/shard_map/ppermute | solution.py:1079
  357.5 44.6 %collective-permute-start.43 = (bf16[1024,768]{1,0:T(8,128)(2,1)S(1)}, bf16[1024,768]{1,0:T(8,128)(2,1)S(1)}, u32[]{:S(2)}, u32[]{:S(2)}) collective-permute-start(bf16[1024,768]{1,0:T(8,128)(2,1)S(1)} %get-tuple-element.284.own), channel_id=1, source_target_pairs={{0,2},{1,3},{2,0},{3,1},{4,6},{5,7},{6,4},{7,5},{8,10},{9,11},{10,... | collective-permute-start | bytes 4718600 | tf_op jit(solution)/shard_map/ppermute | solution.py:1079
  386.3 38.6 %collective-permute-start.47 = (bf16[1536,768]{1,0:T(8,128)(2,1)}, bf16[1536,768]{1,0:T(8,128)(2,1)S(1)}, u32[]{:S(2)}, u32[]{:S(2)}) collective-permute-start(bf16[1536,768]{1,0:T(8,128)(2,1)} %get-tuple-element.303.own), channel_id=1, source_target_pairs={{1,0},{2,3},{5,4},{6,7},{9,8},{10,11},{13,12},{14,15},{17,16},{18,... | collective-permute-start | bytes 7077896 | tf_op jit(solution)/shard_map/ppermute | solution.py:1079
  390.2 34.7 %collective-permute-start.48 = (bf16[384,1536]{1,0:T(8,128)(2,1)}, bf16[384,1536]{1,0:T(8,128)(2,1)S(1)}, u32[]{:S(2)}, u32[]{:S(2)}) collective-permute-start(bf16[384,1536]{1,0:T(8,128)(2,1)} %shard_map.252), channel_id=1, source_target_pairs={{1,5},{2,6},{5,1},{6,2},{9,13},{10,14},{13,9},{14,10},{17,21},{18,... | collective-permute-start | bytes 3538952 | tf_op jit(solution)/shard_map/ppermute | solution.py:1079
  454.8 40.1 %collective-permute-start.52 = (bf16[1536,384]{1,0:T(8,128)(2,1)}, bf16[1536,384]{1,0:T(8,128)(2,1)S(1)}, u32[]{:S(2)}, u32[]{:S(2)}) collective-permute-start(bf16[1536,384]{1,0:T(8,128)(2,1)} %get-tuple-element.313.own), channel_id=1, source_target_pairs={{1,5},{2,6},{5,1},{6,2},{9,13},{10,14},{13,9},{14,10},{17,21},{18,... | collective-permute-start | bytes 3538952 | tf_op jit(solution)/shard_map/ppermute | solution.py:1079
  455.7 38.5 %collective-permute-start.56 = (bf16[384,1152]{1,0:T(8,128)(2,1)S(1)}, bf16[384,1152]{1,0:T(8,128)(2,1)S(1)}, u32[]{:S(2)}, u32[]{:S(2)}) collective-permute-start(bf16[384,1152]{1,0:T(8,128)(2,1)S(1)} %copy-done.89), channel_id=1, source_target_pairs={{1,0},{2,3},{5,4},{6,7},{9,8},{10,11},{13,12},{14,15},{17,16},{18,... | collective-permute-start | bytes 2654216 | tf_op jit(solution)/shard_map/ppermute | solution.py:1079
  459.7 35.2 %collective-permute-start.53 = (bf16[384,1152]{1,0:T(8,128)(2,1)}, bf16[384,1152]{1,0:T(8,128)(2,1)S(1)}, u32[]{:S(2)}, u32[]{:S(2)}) collective-permute-start(bf16[384,1152]{1,0:T(8,128)(2,1)} %shard_map.262), channel_id=1, source_target_pairs={{1,0},{2,3},{5,4},{6,7},{9,8},{10,11},{13,12},{14,15},{17,16},{18,... | collective-permute-start | bytes 2654216 | tf_op jit(solution)/shard_map/ppermute | solution.py:1079
  462.0 32.2 %collective-permute-start.54 = (bf16[384,768]{1,0:T(8,128)(2,1)S(1)}, bf16[384,768]{1,0:T(8,128)(2,1)S(1)}, u32[]{:S(2)}, u32[]{:S(2)}) collective-permute-start(bf16[384,768]{1,0:T(8,128)(2,1)S(1)} %convolution_convert_fusion.6.own), channel_id=1, source_target_pairs={{1,0},{2,3},{5,4},{6,7},{9,8},{10,11},{13,12},{14,15},{17,16},{18,... | collective-permute-start | bytes 1769480 | tf_op jit(solution)/shard_map/ppermute | solution.py:1079
  464.5 30.4 %collective-permute-start.55 = (bf16[16,16,128]{2,1,0:T(8,128)(2,1)S(1)}, bf16[16,16,128]{2,1,0:T(8,128)(2,1)S(1)}, u32[]{:S(2)}, u32[]{:S(2)}) collective-permute-start(bf16[16,16,128]{2,1,0:T(8,128)(2,1)S(1)} %convert_element_type.138.own), channel_id=1, source_target_pairs={{1,0},{2,3},{5,4},{6,7},{9,8},{10,11},{13,12},{14,15},{17,16},{18,... | collective-permute-start | bytes 196616 | tf_op jit(solution)/shard_map/ppermute | solution.py:1079
  499.1 26.6 %collective-permute-start.57 = (bf16[1536,384]{1,0:T(8,128)(2,1)}, bf16[1536,384]{1,0:T(8,128)(2,1)S(1)}, u32[]{:S(2)}, u32[]{:S(2)}) collective-permute-start(bf16[1536,384]{1,0:T(8,128)(2,1)} %shard_map.265), channel_id=1, source_target_pairs={{1,0},{2,3},{5,4},{6,7},{9,8},{10,11},{13,12},{14,15},{17,16},{18,... | collective-permute-start | bytes 3538952 | tf_op jit(solution)/shard_map/ppermute | solution.py:1079
  533.7 29.0 %collective-permute-start.62 = (bf16[4112,128]{1,0:T(8,128)(2,1)S(1)}, bf16[4112,128]{1,0:T(8,128)(2,1)S(1)}, u32[]{:S(2)}, u32[]{:S(2)}) collective-permute-start(bf16[4112,128]{1,0:T(8,128)(2,1)S(1)} %get-tuple-element.410), channel_id=1, source_target_pairs={{0,4},{3,7},{4,0},{7,3},{8,12},{11,15},{12,8},{15,11},{16,20},{19,... | collective-permute-start | bytes 3158024 | tf_op jit(solution)/shard_map/ppermute | solution.py:1079
  553.3 21.6 %collective-permute-start.63 = (bf16[4112,128]{1,0:T(8,128)(2,1)}, bf16[4112,128]{1,0:T(8,128)(2,1)S(1)}, u32[]{:S(2)}, u32[]{:S(2)}) collective-permute-start(bf16[4112,128]{1,0:T(8,128)(2,1)} %get-tuple-element.356), channel_id=1, source_target_pairs={{0,4},{3,7},{4,0},{7,3},{8,12},{11,15},{12,8},{15,11},{16,20},{19,... | collective-permute-start | bytes 3158024 | tf_op jit(solution)/shard_map/ppermute | solution.py:1079
  555.3 19.7 %collective-permute-start.64 = (bf16[4112,128]{1,0:T(8,128)(2,1)}, bf16[4112,128]{1,0:T(8,128)(2,1)S(1)}, u32[]{:S(2)}, u32[]{:S(2)}) collective-permute-start(bf16[4112,128]{1,0:T(8,128)(2,1)} %get-tuple-element.357), channel_id=1, source_target_pairs={{0,8},{3,11},{4,12},{7,15},{8,16},{11,19},{12,20},{15,23},{16,24},... | collective-permute-start | bytes 3158024 | tf_op jit(solution)/shard_map/ppermute | solution.py:1079
  562.6 46.5 %collective-permute-start.60 = (bf16[1024,768]{1,0:T(8,128)(2,1)S(1)}, bf16[1024,768]{1,0:T(8,128)(2,1)S(1)}, u32[]{:S(2)}, u32[]{:S(2)}) collective-permute-start(bf16[1024,768]{1,0:T(8,128)(2,1)S(1)} %add_convert_fusion), channel_id=1, source_target_pairs={{0,2},{1,3},{2,0},{3,1},{4,6},{5,7},{6,4},{7,5},{8,10},{9,11},{10,... | collective-permute-start | bytes 4718600 | tf_op jit(solution)/shard_map/ppermute | solution.py:1079
  584.5 50.4 %collective-permute-start.58 = (bf16[1024,768]{1,0:T(8,128)(2,1)S(1)}, bf16[1024,768]{1,0:T(8,128)(2,1)}, u32[]{:S(2)}, u32[]{:S(2)}) collective-permute-start(bf16[1024,768]{1,0:T(8,128)(2,1)S(1)} %copy-done.38), channel_id=1, source_target_pairs={{0,1},{3,2},{4,5},{7,6},{8,9},{11,10},{12,13},{15,14},{16,17},{19,... | collective-permute-start | bytes 4718600 | tf_op jit(solution)/shard_map/ppermute | solution.py:1079
  593.0 21.4 %collective-permute-start.69 = (bf16[4112,128]{1,0:T(8,128)(2,1)}, bf16[4112,128]{1,0:T(8,128)(2,1)S(1)}, u32[]{:S(2)}, u32[]{:S(2)}) collective-permute-start(bf16[4112,128]{1,0:T(8,128)(2,1)} %get-tuple-element.370), channel_id=1, source_target_pairs={{0,4},{3,7},{4,0},{7,3},{8,12},{11,15},{12,8},{15,11},{16,20},{19,... | collective-permute-start | bytes 3158024 | tf_op jit(solution)/shard_map/ppermute | solution.py:1079
  596.9 19.8 %collective-permute-start.70 = (bf16[4112,128]{1,0:T(8,128)(2,1)}, bf16[4112,128]{1,0:T(8,128)(2,1)}, u32[]{:S(2)}, u32[]{:S(2)}) collective-permute-start(bf16[4112,128]{1,0:T(8,128)(2,1)} %get-tuple-element.371), channel_id=1, source_target_pairs={{0,8},{3,11},{4,12},{7,15},{8,16},{11,19},{12,20},{15,23},{16,24},... | collective-permute-start | bytes 3158024 | tf_op jit(solution)/shard_map/ppermute | solution.py:1079
  614.5 22.3 %collective-permute-start.61 = (bf16[1024,384]{1,0:T(8,128)(2,1)S(1)}, bf16[1024,384]{1,0:T(8,128)(2,1)}, u32[]{:S(2)}, u32[]{:S(2)}) collective-permute-start(bf16[1024,384]{1,0:T(8,128)(2,1)S(1)} %select_convert_fusion), channel_id=1, source_target_pairs={{0,1},{3,2},{4,5},{7,6},{8,9},{11,10},{12,13},{15,14},{16,17},{19,... | collective-permute-start | bytes 2359304 | tf_op jit(solution)/shard_map/ppermute | solution.py:1079
  620.3 20.4 %collective-permute-start.73 = (bf16[4112,128]{1,0:T(8,128)(2,1)}, bf16[4112,128]{1,0:T(8,128)(2,1)S(1)}, u32[]{:S(2)}, u32[]{:S(2)}) collective-permute-start(bf16[4112,128]{1,0:T(8,128)(2,1)} %get-tuple-element.380), channel_id=1, source_target_pairs={{0,4},{3,7},{4,0},{7,3},{8,12},{11,15},{12,8},{15,11},{16,20},{19,... | collective-permute-start | bytes 3158024 | tf_op jit(solution)/shard_map/ppermute | solution.py:1079
  (141 other events, 978.0 us)

commit v9 on v8

--- a/solution.py
+++ b/solution.py
@@ -125,10 +125,22 @@
     return lax.dot_general(left, right, (((0,), (0,)), ((), ())), preferred_element_type=f32)
 
 
-def joined(ref, start, rows_n, panels):
+def joined(ref, start, rows_n, panels, stride=None):
+    stride = rows_n if stride is None else stride
     return jnp.concatenate(
-        [ref[start + p * rows_n : start + (p + 1) * rows_n, :] for p in range(panels)], axis=1
+        [ref[pl.ds(start + p * stride, rows_n), :] for p in range(panels)], axis=1
     )
+
+
+def part_at(half, part):
+    return lax.rem(part + half[0], 2)
+
+
+def swapped(half, values):
+    size = values.shape[1] // 2
+    left, right = values[:, :size], values[:, size:]
+    first = half[0] == 0
+    return jnp.where(first, left, right), jnp.where(first, right, left)
 
 
 def norm_stats(values):
@@ -339,46 +351,6 @@
     )(pos, part, *operands)
 
 
-def half_sum_kernel(part, own, arrived, out):
-    out[...] = (own[...].astype(f32) + arrived[...].astype(f32)).astype(bf16)
-
-
-def half_sum(part, own, arrived):
-    block = arrived.shape
-    return pl.pallas_call(
-        half_sum_kernel,
-        out_shape=pltpu.HBM(block, bf16),
-        grid_spec=pltpu.PrefetchScalarGridSpec(
-            num_scalar_prefetch=1,
-            grid=(1,),
-            in_specs=[pl.BlockSpec(block, lambda i, part: (part[0], 0)), fixed(block)],
-            out_specs=fixed(block),
-        ),
-        compiler_params=params(8),
-        cost_estimate=cost(arrived.size, arrived.size * 6),
-    )(part, stay(own), stay(arrived))
-
-
-def half_copy_kernel(part, own, out):
-    out[...] = own[...]
-
-
-def other_half(part, own):
-    block = (own.shape[0] // 2, own.shape[1])
-    return pl.pallas_call(
-        half_copy_kernel,
-        out_shape=pltpu.HBM(block, bf16),
-        grid_spec=pltpu.PrefetchScalarGridSpec(
-            num_scalar_prefetch=1,
-            grid=(1,),
-            in_specs=[pl.BlockSpec(block, lambda i, part: (1 - part[0], 0))],
-            out_specs=fixed(block),
-        ),
-        compiler_params=params(8),
-        cost_estimate=cost(0, own.size * 2),
-    )(part, stay(own))
-
-
 def scatter_vec_kernel(paired, pos, own, *refs):
     if paired:
         recv, *refs = refs
@@ -564,37 +536,40 @@
     )(half, *[stay(c) for c in chunks], vec, stay(weights["base", 0]))
 
 
-def qkv_kernel(layer, first, core, *refs):
+def qkv_kernel(layer, first, core, half, *refs):
     if first:
-        own, recv, vec, weight, hid, normed, q_ref, k_ref, v_ref = refs
+        own, recv, vec, weight, hid, normed_m, normed_t, q_ref, k_ref, v_ref = refs
         mine, theirs = own[...].astype(f32), recv[...].astype(f32)
         low = core[0] == 0
         values = jnp.concatenate(
             [jnp.where(low, mine, theirs), jnp.where(low, theirs, mine)], axis=1
         )
     else:
-        base, own, recv, vec, weight, hid, normed, q_ref, k_ref, v_ref = refs
+        base, own, recv, vec, weight, hid, normed_m, normed_t, q_ref, k_ref, v_ref = refs
         values = base[...] + (own[...].astype(f32) + recv[...].astype(f32))
     hid[...] = values
     unit, unused = norm_stats(values)
-    low = (unit * vec_piece(vec, layer, "g1") + vec_piece(vec, layer, "s1")).astype(bf16)
-    normed[...] = low
+    low = unit * vec_piece(vec, layer, "g1") + vec_piece(vec, layer, "s1")
+    halves = swapped(half, low)
+    normed_m[...] = halves[0].astype(bf16)
+    normed_t[...] = halves[1].astype(bf16)
+    low = low.astype(bf16)
     made = dot(low, joined(weight, 0, D, 3))
     q_ref[...] = (made[:, :HALF] + vec_piece(vec, layer, "bq")).astype(bf16)
     k_ref[...] = made[:, HALF : 2 * HALF].astype(bf16)
     v_ref[...] = (made[:, 2 * HALF :] + vec_piece(vec, layer, "bv")).astype(bf16)
 
 
-def qkv_call(layer, base, own, recv, core, vec, weights):
+def qkv_call(layer, base, own, recv, core, half, vec, weights):
     tokens = own.shape[0]
     shape = lambda width, kind: jax.ShapeDtypeStruct((tokens, width), kind)
-    outs = [shape(D, f32), pltpu.HBM((tokens, D), bf16)] + [shape(HALF, bf16)] * 3
+    outs = [shape(D, f32)] + [pltpu.HBM((tokens, HALF), bf16)] * 2 + [shape(HALF, bf16)] * 3
     operands = ([] if base is None else [base]) + [own, recv]
     return pl.pallas_call(
         functools.partial(qkv_kernel, layer, base is None),
         out_shape=outs,
         grid_spec=pltpu.PrefetchScalarGridSpec(
-            num_scalar_prefetch=1,
+            num_scalar_prefetch=2,
             grid=(tokens // ROWS,),
             in_specs=[rows_spec(o.shape[1]) for o in operands]
             + [fixed(vec.shape), fixed((3 * D, HALF))],
@@ -602,7 +577,7 @@
         ),
         compiler_params=params(),
         cost_estimate=cost(2 * tokens * D * 3 * HALF, tokens * D * 14),
-    )(core, *operands, vec, weights["qkv", layer])
+    )(core, half, *operands, vec, weights["qkv", layer])
 
 
 def head_masks():
@@ -717,102 +692,106 @@
     return values * cdf, cdf + values * pdf
 
 
-def mlp_kernel(layer, base, own, recv, vec, w_up, w_down, hid, normed, act, slope, part):
+def mlp_kernel(
+    layer, half, base, own, recv, vec, w_up, w_down, hid, normed, act_m, act_t, slope, part
+):
     values = base[...] + (own[...].astype(f32) + recv[...].astype(f32))
     hid[...] = values
     unit, unused = norm_stats(values)
     low = (unit * vec_piece(vec, layer, "g2") + vec_piece(vec, layer, "s2")).astype(bf16)
     normed[...] = low
-    bias_up = vec_piece(vec, layer, "b1")
-    for pair in range(HALF_FF // D):
-        area = slice(pair * D, (pair + 1) * D)
-        up = dot(low, joined(w_up, pair * 2 * D, D, 2)) + bias_up[:, area]
+    biases = swapped(half, vec_piece(vec, layer, "b1"))
+    down = vec_piece(vec, layer, "b2")
+    for which, act in enumerate((act_m, act_t)):
+        at = part_at(half, which)
+        up = dot(low, joined(w_up, pl.multiple_of(at * 2 * D, D), D, 2)) + biases[which]
         gelu, grad = gelu_parts(up)
-        act[:, area] = gelu.astype(bf16)
-        slope[:, area] = grad.astype(bf16)
-    bias_down = vec_piece(vec, layer, "b2")
-    part[...] = (dot(act[...], joined(w_down, 0, HALF_FF, TENSOR)) + bias_down).astype(bf16)
-
-
-def mlp_call(layer, base, own, recv, vec, weights):
+        units = gelu.astype(bf16)
+        act[...] = units
+        slope[:, which * D : (which + 1) * D] = grad.astype(bf16)
+        down = down + dot(units, joined(w_down, pl.multiple_of(at * D, D), D, TENSOR, HALF_FF))
+    part[...] = down.astype(bf16)
+
+
+def mlp_call(layer, half, base, own, recv, vec, weights):
     tokens = base.shape[0]
     shape = lambda width, kind: jax.ShapeDtypeStruct((tokens, width), kind)
     kept = lambda width: pltpu.HBM((tokens, width), bf16)
-    outs = [shape(D, f32), kept(D), kept(HALF_FF), kept(HALF_FF), shape(D, bf16)]
+    outs = [shape(D, f32), kept(D), kept(D), kept(D), kept(HALF_FF), shape(D, bf16)]
     return pl.pallas_call(
         functools.partial(mlp_kernel, layer),
         out_shape=outs,
-        grid=(tokens // ROWS,),
-        in_specs=[rows_spec(D)] * 3
-        + [
-            fixed(vec.shape),
-            fixed((2 * HALF_FF, HALF)),
-            fixed((2 * HALF_FF, HALF)),
-        ],
-        out_specs=[rows_spec(o.shape[1]) for o in outs],
+        grid_spec=pltpu.PrefetchScalarGridSpec(
+            num_scalar_prefetch=1,
+            grid=(tokens // ROWS,),
+            in_specs=[rows_spec(D)] * 3
+            + [fixed(vec.shape), fixed((2 * HALF_FF, HALF)), fixed((2 * HALF_FF, HALF))],
+            out_specs=[rows_spec(o.shape[1]) for o in outs],
+        ),
         compiler_params=params(),
         cost_estimate=cost(4 * tokens * D * HALF_FF, tokens * D * 24, 2 * tokens * HALF_FF),
-    )(base, own, recv, vec, weights["up", layer], weights["down", layer])
-
-
-def mlp_back_kernel(layer, summed, *refs):
+    )(half, base, own, recv, vec, weights["up", layer], weights["down", layer])
+
+
+def mlp_back_kernel(layer, summed, half, *refs):
     if summed:
         base, own, recv, *refs = refs
-        (hid, slope, vec, w_up, w_down, grad_full, grad_low, du_ref, back, dgain, dshift, db1, db2) = refs
+        (hid, slope, vec, w_up, w_down, grad_full, grad_low, du_m, du_t, back, dgain, dshift, db1, db2) = refs
         values = base[...].astype(f32) + (own[...].astype(f32) + recv[...].astype(f32))
         grad_full[...] = values
         low = values.astype(bf16)
     else:
         base, valid, *refs = refs
-        (hid, slope, vec, w_up, w_down, grad_low, du_ref, back, dgain, dshift, db1, db2) = refs
+        (hid, slope, vec, w_up, w_down, grad_low, du_m, du_t, back, dgain, dshift, db1, db2) = refs
         low = (base[...].astype(f32) * valid[...]).astype(bf16)
     grad_low[...] = low
     accumulate(db2, jnp.sum(low.astype(f32), axis=0, keepdims=True))
-    for part in range(HALF_FF // D):
-        area = slice(part * D, (part + 1) * D)
-        rows = jnp.concatenate(
-            [w_down[p * HALF_FF + part * D : p * HALF_FF + (part + 1) * D, :] for p in range(TENSOR)],
-            axis=1,
-        )
-        du_ref[:, area] = (dot_nt(low, rows) * slope[:, area].astype(f32)).astype(bf16)
-    grad_normed = dot_nt(du_ref[...], joined(w_up, 0, D, HALF_FF // HALF))
-    accumulate(db1, jnp.sum(du_ref[...].astype(f32), axis=0, keepdims=True))
+    grad_normed = None
+    sums = []
+    for which, out in enumerate((du_m, du_t)):
+        at = part_at(half, which)
+        rows = joined(w_down, pl.multiple_of(at * D, D), D, TENSOR, HALF_FF)
+        grads = dot_nt(low, rows) * slope[:, which * D : (which + 1) * D].astype(f32)
+        grads = grads.astype(bf16)
+        out[...] = grads
+        sums.append(jnp.sum(grads.astype(f32), axis=0, keepdims=True))
+        term = dot_nt(grads, joined(w_up, pl.multiple_of(at * 2 * D, D), D, 2))
+        grad_normed = term if grad_normed is None else grad_normed + term
+    accumulate(db1, jnp.concatenate(swapped(half, jnp.concatenate(sums, axis=1)), axis=1))
     part_back, gain_grad, shift_grad = norm_back(hid[...], vec_piece(vec, layer, "g2"), grad_normed)
     back[...] = part_back.astype(bf16)
     accumulate(dgain, gain_grad)
     accumulate(dshift, shift_grad)
 
 
-def mlp_back_call(layer, base, own, recv, valid, hid, slope, vec, weights):
+def mlp_back_call(layer, half, base, own, recv, valid, hid, slope, vec, weights):
     tokens = base.shape[0]
     summed = own is not None
     shape = lambda width, kind: jax.ShapeDtypeStruct((tokens, width), kind)
     line = lambda width: jax.ShapeDtypeStruct((1, width), f32)
-    outs = ([shape(D, f32)] if summed else []) + [shape(D, bf16), shape(HALF_FF, bf16), shape(D, bf16)]
+    outs = ([shape(D, f32)] if summed else []) + [shape(D, bf16)] * 4
     lines = [line(D), line(D), line(HALF_FF), line(D)]
     extra = [own, recv] if summed else [valid]
     return pl.pallas_call(
         functools.partial(mlp_back_kernel, layer, summed),
         out_shape=outs + lines,
-        grid=(tokens // ROWS,),
-        in_specs=[rows_spec(D)]
-        + [rows_spec(e.shape[1]) for e in extra]
-        + [
-            rows_spec(D),
-            rows_spec(HALF_FF),
-            fixed(vec.shape),
-            fixed((2 * HALF_FF, HALF)),
-            fixed((2 * HALF_FF, HALF)),
-        ],
-        out_specs=[rows_spec(o.shape[1]) for o in outs] + [fixed(o.shape) for o in lines],
+        grid_spec=pltpu.PrefetchScalarGridSpec(
+            num_scalar_prefetch=1,
+            grid=(tokens // ROWS,),
+            in_specs=[rows_spec(D)]
+            + [rows_spec(e.shape[1]) for e in extra]
+            + [rows_spec(D), rows_spec(HALF_FF), fixed(vec.shape)]
+            + [fixed((2 * HALF_FF, HALF))] * 2,
+            out_specs=[rows_spec(o.shape[1]) for o in outs] + [fixed(o.shape) for o in lines],
+        ),
         compiler_params=params(),
         cost_estimate=cost(4 * tokens * D * HALF_FF, tokens * D * 24),
-    )(base, *extra, stay(hid), stay(slope), vec, weights["up", layer], weights["down", layer])
+    )(half, base, *extra, stay(hid), stay(slope), vec, weights["up", layer], weights["down", layer])
 
 
 def attend_back_kernel(
-    low_ref, high_ref, base, own, recv, q_ref, k_ref, v_ref, o_ref, lse_ref, seg_k, seg_q, w_out,
-    full_ref, grad_low, dq_ref, dk_ref, dv_ref, dbo, dk_acc, dv_acc, dq_acc, do_ref,
+    low_ref, high_ref, half, base, own, recv, q_ref, k_ref, v_ref, o_ref, lse_ref, seg_k, seg_q, w_out,
+    full_ref, low_m, low_t, dq_ref, dk_ref, dv_ref, dbo, dk_acc, dv_acc, dq_acc, do_ref,
 ):
     step = pl.program_id(0)
 
@@ -824,7 +803,9 @@
     values = base[...].astype(f32) + (own[...].astype(f32) + recv[...].astype(f32))
     full_ref[...] = values
     low = values.astype(bf16)
-    grad_low[...] = low
+    halves = swapped(half, values)
+    low_m[...] = halves[0].astype(bf16)
+    low_t[...] = halves[1].astype(bf16)
     accumulate(dbo, jnp.sum(low.astype(f32), axis=0, keepdims=True))
     do_ref[...] = dot_nt(low, joined(w_out, 0, HALF, TENSOR)).astype(bf16)
     product = do_ref[...].astype(f32) * o_ref[...].astype(f32)
@@ -878,7 +859,7 @@
 
 
 def attend_back_call(
-    layer, first, last, base, own, recv, queries, keys, values, mixed, lse, seg_col, seg_row, weights
+    layer, first, last, half, base, own, recv, queries, keys, values, mixed, lse, seg_col, seg_row, weights
 ):
     tokens = base.shape[0]
     shape = lambda width, kind: jax.ShapeDtypeStruct((tokens, width), kind)
@@ -887,14 +868,15 @@
         attend_back_kernel,
         out_shape=[
             shape(D, f32),
-            shape(D, bf16),
+            shape(HALF, bf16),
+            shape(HALF, bf16),
             shape(HALF, bf16),
             shape(HALF, bf16),
             shape(HALF, bf16),
             jax.ShapeDtypeStruct((1, D), f32),
         ],
         grid_spec=pltpu.PrefetchScalarGridSpec(
-            num_scalar_prefetch=2,
+            num_scalar_prefetch=3,
             grid=(tokens // ROWS,),
             in_specs=[
                 rows_spec(D),
@@ -911,7 +893,8 @@
             ],
             out_specs=[
                 rows_spec(D),
-                rows_spec(D),
+                rows_spec(HALF),
+                rows_spec(HALF),
                 rows_spec(HALF),
                 fixed(whole),
                 fixed(whole),
@@ -927,7 +910,7 @@
         compiler_params=params(),
         cost_estimate=cost(14 * HEADS * tokens * tokens * BS, tokens * D * 20, HEADS * tokens * tokens),
     )(
-        first, last, base, own, recv, stay(queries), stay(keys), stay(values), stay(mixed), lse,
+        first, last, half, base, own, recv, stay(queries), stay(keys), stay(values), stay(mixed), lse,
         seg_col, seg_row, weights["out", layer],
     )
 
@@ -1223,16 +1206,23 @@
     caches = []
     hidden, own, recv = None, embedded, embedded_other
     for layer in range(LAYERS):
-        hidden, normed, queries, keys, values = qkv_call(
-            layer, hidden, own, recv, core_flag, vec, weights
+        hidden, normed_m, normed_t, queries, keys, values = qkv_call(
+            layer, hidden, own, recv, core_flag, half_at, vec, weights
         )
         mixed, lse, part = attend_call(
             layer, first_blk, last_blk, queries, keys, values, seg_col, seg_row, vec, weights
         )
         other = send(part, routes.core_all)
-        middle, normed2, act, slope, own = mlp_call(layer, hidden, part, other, vec, weights)
+        middle, normed2, act_m, act_t, slope, own = mlp_call(
+            layer, half_at, hidden, part, other, vec, weights
+        )
         recv = send(own, routes.core_all)
-        caches.append((hidden, normed, queries, keys, values, mixed, lse, middle, normed2, act, slope))
+        caches.append(
+            dict(
+                hidden=hidden, normed=(normed_m, normed_t), qkv=(queries, keys, values), mixed=mixed,
+                lse=lse, middle=middle, normed2=normed2, act=(act_m, act_t), slope=slope,
+            )
+        )
         hidden = middle
     out_low = ((hidden + (own.astype(f32) + recv.astype(f32))) * valid_col).astype(bf16)
 
@@ -1260,26 +1250,36 @@
             offsets[name, layer] = count
             count += size // (BS * BS)
 
-    def place_tiles(key, matrix, arrived, buffer):
-        tiles = matrix.size // (BS * BS)
-        pos = tile_pos[offsets[key] : offsets[key] + tiles]
-        rows_n = matrix.shape[0] // 2 if matrix.shape[0] > HALF else HALF
-        return scatter_matrix(pos, matrix, arrived, where_to, buffer, total_rows, rows_n)
-
-    def place_base(rel, matrix, arrived, buffer):
-        size = BASE_PIX * HALF // (BS * BS) // 2
-        low_pos, high_pos = tile_pos[:size], tile_pos[size : 2 * size]
-        pos = jnp.where(half_at[0] == rel, low_pos, high_pos)
-        return scatter_matrix(pos, matrix, arrived, where_to, buffer, total_rows, D)
+    tile_grid = {
+        "base": (BASE_PIX // BS, HALF // BS),
+        "qkv": (D // BS, 3 * HALF // BS),
+        "out": (HALF // BS, D // BS),
+        "up": (D // BS, HALF_FF // BS),
+        "down": (HALF_FF // BS, D // BS),
+    }
+
+    def place_tiles(name, layer, rel, matrix, arrived, buffer):
+        key = "base" if name == "base" else (name, layer)
+        rows_n, cols_n = tile_grid[name]
+        pos = tile_pos[offsets[key] : offsets[key] + rows_n * cols_n].reshape(rows_n, cols_n)
+        axis = 1 if name in ("up", "out") else 0
+        low_pos, high_pos = jnp.split(pos, 2, axis=axis)
+        pos = jnp.where(half_at[0] == rel, low_pos, high_pos).reshape(-1)
+        steps = 1 if name in ("qkv", "out") else 2
+        return scatter_matrix(
+            pos, matrix, arrived, where_to, buffer, total_rows, matrix.shape[0] // steps
+        )
 
     def over(matrix):
         return send(matrix, routes.y_in) if grid3 else None
 
     def beside(matrix):
-        return send(other_half(half_at, matrix), routes.x_away) if grid3 else None
-
-    def summed(matrix, arrived):
-        return half_sum(half_at, matrix, arrived) if grid3 else None
+        return send(matrix, routes.x_away) if grid3 else None
+
+    def with_arrived(product, arrived):
+        if arrived is not None:
+            product = product + arrived.astype(f32)
+        return product.astype(bf16)
 
     def hold(*arrays):
         kept = [a for a in arrays if a is not None]
@@ -1290,82 +1290,128 @@
     vec_grads = [None] * LAYERS
 
     def mlp_step(layer, grad, own, recv):
-        middle, normed2, act, slope = caches[layer][7:11]
-        made = mlp_back_call(layer, grad, own, recv, valid_col, middle, slope, vec, weights)
+        kept = caches[layer]
+        made = mlp_back_call(
+            layer, half_at, grad, own, recv, valid_col, kept["middle"], kept["slope"], vec, weights
+        )
         if own is not None:
             return made
         return [made[0]] + list(made)
 
     def attend_step(layer, grad, part, other, lse):
-        hid_in, normed, queries, keys, values, mixed = caches[layer][:6]
+        kept = caches[layer]
         return attend_back_call(
-            layer, first_key, last_key, grad, part, other, queries, keys, values, mixed, lse,
+            layer, first_key, last_key, half_at, grad, part, other, *kept["qkv"], kept["mixed"], lse,
             seg_col, seg_row, weights,
         )
 
-    grad, grad_low, du, part, dg2, ds2, db1, db2 = mlp_step(top, cotangent, None, None)
+    def down_grad(layer, which, grad_low):
+        return dot_tn(caches[layer]["act"][which], grad_low)
+
+    def up_grad(layer, du_part):
+        return dot_tn(caches[layer]["normed2"], du_part)
+
+    def qkv_grad(layer, which, three):
+        return dot_tn(caches[layer]["normed"][which], three)
+
+    def out_grad(layer, low_part):
+        return dot_tn(caches[layer]["mixed"], low_part)
+
+    grad, grad_low, du_m, du_t, part, dg2, ds2, db1, db2 = mlp_step(top, cotangent, None, None)
     other = send(part, routes.core_all)
-    gd1 = dot_tn(caches[top][9], grad_low).astype(bf16)
-    gu1 = dot_tn(caches[top][8], du).astype(bf16)
-    lse, gd1, gu1, out_low = fence(caches[top][6], gd1, gu1, out_low)
-    ad1 = over(gd1)
-    grad, grad_low, dq, dk, dv, dbo = attend_step(top, grad, part, other, lse)
-    vec, dbo, ad1, gu1 = hold(vec, dbo, ad1, gu1)
-    au1 = over(gu1)
-    own, dg1, ds1, dbq, dbv = qkv_back_call(top, dq, dk, dv, caches[top][0], vec, weights)
+    gd1t = down_grad(top, 1, grad_low).astype(bf16)
+    gu1t = up_grad(top, du_t).astype(bf16)
+    lse, gd1t, gu1t, out_low = fence(caches[top]["lse"], gd1t, gu1t, out_low)
+    xd1 = beside(gd1t)
+    xu1 = beside(gu1t)
+    mlp_low1 = grad_low
+    grad, low_m, low_t, dq, dk, dv, dbo = attend_step(top, grad, part, other, lse)
+    vec, dbo, xd1 = hold(vec, dbo, xd1)
+    gd1 = with_arrived(down_grad(top, 0, mlp_low1), xd1)
+    yd1 = over(gd1)
+    own, dg1, ds1, dbq, dbv = qkv_back_call(
+        top, dq, dk, dv, caches[top]["hidden"], vec, weights
+    )
     recv = send(own, routes.core_all)
-    go1 = dot_tn(caches[top][5], grad_low).astype(bf16)
-    gq1 = dot_tn(caches[top][1], jnp.concatenate([dq, dk, dv], axis=1)).astype(bf16)
+    three = jnp.concatenate([dq, dk, dv], axis=1)
+    go1t = out_grad(top, low_t).astype(bf16)
+    gq1t = qkv_grad(top, 1, three).astype(bf16)
     vec_grads[top] = [dg1, ds1, dbq, dbv, dbo, dg2, ds2, db1, db2]
-    grad, grad_low, du, part, dg2, ds2, db1, db2 = mlp_step(low, grad, own, recv)
+    upper = (du_m, low_m, three)
+    grad, grad_low, du_m, du_t, part, dg2, ds2, db1, db2 = mlp_step(low, grad, own, recv)
     other = send(part, routes.core_all)
-    db2, au1, go1, gq1 = hold(db2, au1, go1, gq1)
-    xq1, ao1 = beside(gq1), over(go1)
-    gd0 = dot_tn(caches[low][9], grad_low).astype(bf16)
-    gu0 = dot_tn(caches[low][8], du).astype(bf16)
-    lse, gd0, gu0, xq1, ao1 = hold(caches[low][6], gd0, gu0, xq1, ao1)
-    hq1 = summed(gq1, xq1)
-    ad0 = over(gd0)
-    xu0 = beside(gu0)
-    buffer = place_tiles(("down", top), gd1, ad1, None)
-    buffer = place_tiles(("up", top), gu1, au1, buffer)
-    grad, grad_low, dq, dk, dv, dbo = attend_step(low, grad, part, other, lse)
-    vec, dbo, ad0, xu0, hq1, buffer = hold(vec, dbo, ad0, xu0, hq1, buffer)
-    au0 = over(summed(gu0, xu0))
-    aq1 = over(hq1)
-    own, dg1, ds1, dbq, dbv = qkv_back_call(low, dq, dk, dv, caches[low][0], vec, weights)
+    db2, xu1, yd1, go1t, gq1t = hold(db2, xu1, yd1, go1t, gq1t)
+    gu1 = with_arrived(up_grad(top, upper[0]), xu1)
+    yu1 = over(gu1)
+    xq1, xo1 = beside(gq1t), beside(go1t)
+    gd0t = down_grad(low, 1, grad_low).astype(bf16)
+    gu0t = up_grad(low, du_t).astype(bf16)
+    lse, gd0t, gu0t, gu1 = hold(caches[low]["lse"], gd0t, gu0t, gu1)
+    xd0 = beside(gd0t)
+    buffer = place_tiles("down", top, 1, gd1t, None, None)
+    buffer = place_tiles("up", top, 1, gu1t, None, buffer)
+    mlp_low0 = grad_low
+    grad, low_m, low_t, dq, dk, dv, dbo = attend_step(low, grad, part, other, lse)
+    vec, dbo, yu1, xq1, xo1, xd0, buffer = hold(vec, dbo, yu1, xq1, xo1, xd0, buffer)
+    gq1 = with_arrived(qkv_grad(top, 0, upper[2]), xq1)
+    go1 = with_arrived(out_grad(top, upper[1]), xo1)
+    gd0 = with_arrived(down_grad(low, 0, mlp_low0), xd0)
+    yq1, yo1, yd0 = over(gq1), over(go1), over(gd0)
+    xu0 = beside(gu0t)
+    own, dg1, ds1, dbq, dbv = qkv_back_call(
+        low, dq, dk, dv, caches[low]["hidden"], vec, weights
+    )
     recv = send(own, routes.core_all)
-    gq0 = dot_tn(caches[low][1], jnp.concatenate([dq, dk, dv], axis=1)).astype(bf16)
+    three = jnp.concatenate([dq, dk, dv], axis=1)
+    gq0t = qkv_grad(low, 1, three).astype(bf16)
+    go0t = out_grad(low, low_t).astype(bf16)
     vec_grads[low] = [dg1, ds1, dbq, dbv, dbo, dg2, ds2, db1, db2]
-    xq0 = beside(gq0)
     grad_emb, grad_emb_bias = embed_back_call(core_flag, grad, own, recv)
     middle = CHUNKS // 2
-
-    def base_grad(parts):
-        return jnp.concatenate([dot_tn(c, grad_emb).astype(bf16) for c in parts], axis=0)
-
-    gbt = base_grad(chunks[middle:])
-    gbt, au0, xq0 = hold(gbt, au0, xq0)
-    xb = send(gbt, routes.x_away) if grid3 else None
-    aq0 = over(summed(gq0, xq0))
-    gbm = base_grad(chunks[:middle])
+    gbt = jnp.concatenate([dot_tn(c, grad_emb).astype(bf16) for c in chunks[middle:]], axis=0)
+    gbt, xu0, gq0t, go0t, yq1 = hold(gbt, xu0, gq0t, go0t, yq1)
+    xb = beside(gbt)
+    xq0, xo0 = beside(gq0t), beside(go0t)
+    gu0 = with_arrived(up_grad(low, du_m), xu0)
+    yu0 = over(gu0)
     vec_grad = pack_call([grad_emb_bias] + vec_grads[0] + vec_grads[1], dp_n, vec_per)
-    go0 = dot_tn(caches[low][5], grad_low).astype(bf16)
-    ao0, av = over(go0), over(vec_grad)
-    gbm, xb, aq0, ao0, av, aq1, buffer = hold(gbm, xb, aq0, ao0, av, aq1, buffer)
-    ab = over(half_sum(half_at * 0, gbm, xb)) if grid3 else None
-    buffer = place_tiles(("out", top), go1, ao1, buffer)
-    buffer = place_tiles(("qkv", top), gq1, aq1, buffer)
-    buffer = place_tiles(("down", low), gd0, ad0, buffer)
-    buffer = place_tiles(("up", low), gu0, au0, buffer)
-    buffer = place_base(1, gbt, None, buffer)
-    buffer = place_tiles(("out", low), go0, ao0, buffer)
+    av = over(vec_grad)
+    buffer = place_tiles("down", top, 0, gd1, yd1, buffer)
+    buffer = place_tiles("up", top, 0, gu1, yu1, buffer)
+    buffer = place_tiles("qkv", top, 1, gq1t, None, buffer)
+    buffer = place_tiles("out", top, 1, go1t, None, buffer)
+    buffer = place_tiles("down", low, 1, gd0t, None, buffer)
+    buffer = place_tiles("up", low, 1, gu0t, None, buffer)
+    xb, xq0, xo0, yd0, buffer = hold(xb, xq0, xo0, yd0, buffer)
+    gbm = jnp.concatenate(
+        [
+            with_arrived(
+                dot_tn(c, grad_emb),
+                None if xb is None else xb[k * D : (k + 1) * D],
+            )
+            for k, c in enumerate(chunks[:middle])
+        ],
+        axis=0,
+    )
+    yb = over(gbm)
+    gq0 = with_arrived(qkv_grad(low, 0, three), xq0)
+    go0 = with_arrived(out_grad(low, low_m), xo0)
+    yq0, yo0 = over(gq0), over(go0)
+    buffer = place_tiles("qkv", top, 0, gq1, yq1, buffer)
+    buffer = place_tiles("out", top, 0, go1, yo1, buffer)
+    buffer = place_tiles("down", low, 0, gd0, yd0, buffer)
+    buffer = place_tiles("base", 0, 1, gbt, None, buffer)
+    buffer = place_tiles("qkv", low, 1, gq0t, None, buffer)
+    buffer = place_tiles("out", low, 1, go0t, None, buffer)
+    yu0, av, buffer = hold(yu0, av, buffer)
+    buffer = place_tiles("up", low, 0, gu0, yu0, buffer)
     buffer = scatter_vec(vec_pos, vec_grad, av, buffer)
-    buffer = place_tiles(("qkv", low), gq0, aq0, buffer)
     base_weight = weights["base", 0]
-    ab, buffer, base_weight, out_low = hold(ab, buffer, base_weight, out_low)
+    yb, yq0, yo0, buffer, base_weight, out_low = hold(yb, yq0, yo0, buffer, base_weight, out_low)
     weights["base", 0] = base_weight
-    buffer = place_base(0, gbm, ab, buffer)
+    buffer = place_tiles("out", low, 0, go0, yo0, buffer)
+    buffer = place_tiles("qkv", low, 0, gq0, yq0, buffer)
+    buffer = place_tiles("base", 0, 0, gbm, yb, buffer)
 
     if grid3:
         token = jnp.zeros((8, BS), f32)

time: 668 us -> 714 us (1.069)
  local copies, waits for them, and re-layouts: 39.8 us -> 55.7 us
  matrix products: 32.5 us -> 45.8 us
  starting transfers between devices: 156 us -> 168 us
  waiting for transfers between devices: 122 us -> 114 us
    pallas_call x10 -> x18, Pallas kernels: 35.4 us -> 51.9 us  [scatter_matrix(): pl.pallas_call(functools.partial(scatter_kernel, rows_n, cols_n, steps, p...]
    pallas_call x9 -> x2, Pallas kernels: 63.7 us -> 47.7 us  [attend_back_call(): pl.pallas_call(attend_back_kernel, out_shape=[shape(D, f32), shape(HALF,...]
    dot_general x12 -> x20, matrix products: 29.4 us -> 42.7 us  [dot_tn(): lax.dot_general(left, right, (((0,), (0,)), ((), ())), preferred_element_...]
    unnamed x228 -> x302, local copies, waits for them, and re-layouts: 35 us -> 47.7 us
    ppermute x76 -> x81, starting transfers between devices: 156 us -> 168 us  [send(): return lax.ppermute(value, AXES, route)]
    ppermute x76 -> x81, waiting for transfers between devices: 122 us -> 114 us  [send(): return lax.ppermute(value, AXES, route)]
  transfers between devices with their start and end apart: 76 -> 81, of which waited for: 25 -> 25; matrix products, arithmetic and copies ran while one was open for 8% -> 11% of each run, Pallas kernels for 31% -> 28%
where the time goes in v9:
time: 714 us; the launch traced here: 701 us
  Pallas kernels  289 us (40%)
  starting transfers between devices  168 us (24%)
  waiting for transfers between devices  114 us (16%)
  local copies, waits for them, and re-layouts  55.7 us (8%)
  matrix products  45.8 us (6%)
  other arithmetic  25.8 us (4%)
    ppermute x81, starting transfers between devices, send(): return lax.ppermute(value, AXES, route)  168 us
    ppermute x81, waiting for transfers between devices, send(): return lax.ppermute(value, AXES, route)  114 us
    pallas_call x18, Pallas kernels, scatter_matrix(): pl.pallas_call(functools.partial(scatter_kernel, rows_n, cols_n, steps, p...  51.9 us
    unnamed x302, local copies, waits for them, and re-layouts  47.7 us
    pallas_call x2, Pallas kernels, attend_back_call(): pl.pallas_call(attend_back_kernel, out_shape=[shape(D, f32), shape(HALF,...  47.7 us
    dot_general x20, matrix products, dot_tn(): lax.dot_general(left, right, (((0,), (0,)), ((), ())), preferred_element_...  42.7 us
    pallas_call x2, Pallas kernels, attend_call(): pl.pallas_call(functools.partial(attend_kernel, layer), out_shape=[jax.Sh...  31.3 us
    pallas_call x8, Pallas kernels, reduce_call(): pl.pallas_call(functools.partial(reduce_kernel, carried is not None, last...  27.7 us
  transfers between devices with their start and end apart: 81, of which 25 were waited for; matrix products, arithmetic and copies ran while one was open for 11% of the time, Pallas kernels for 28%

profile of v9, /device:TPU:0, one launch (start us, length us, event | category | flops | bytes accessed | tf_op | source)
XLA Modules:
  0.0 701.4 jit_solution(2087489580810525624)
XLA Ops:
  17.1 3.5 collective-permute-start.2
  22.2 5.0 collective-permute-done.refs_1_
  27.6 8.2 %collective-permute-done.2.refs_3_ = bf16[4112,128]{1,0:T(8,128)(2,1)S(1)} collective-permute-done((bf16[4112,128]{1,0:T(8,128)(2,1)}, bf16[4112,128]{1,0:T(8,128)(2,1)S(1)}, u32[]{:S(2)}, u32[]{:S(2)}) %collective-permute-start.2) | collective-permute-done | bytes 1052704 | tf_op jit(solution)/shard_map/ppermute | solution.py:1062
  39.3 3.4 collective-permute-start.5
  51.2 5.6 shard_map.223.refs_4_
  58.0 7.2 %collective-permute-done.5.refs_1_ = bf16[4112,128]{1,0:T(8,128)(2,1)} collective-permute-done((bf16[4112,128]{1,0:T(8,128)(2,1)}, bf16[4112,128]{1,0:T(8,128)(2,1)}, u32[]{:S(2)}, u32[]{:S(2)}) %collective-permute-start.5) | collective-permute-done | bytes 1052704 | tf_op jit(solution)/shard_map/ppermute | solution.py:1062
  73.0 5.7 shard_map.225.refs_5_
  88.5 5.7 collective-permute-done.15.refs_1_
  98.9 5.5 shard_map.227.refs_5_
  113.1 6.3 collective-permute-done.21.refs_3_
  120.1 5.8 shard_map.229.refs_5_
  130.5 4.4 collective-permute-start.28
  141.0 11.1 %collective-permute-start.31 = (bf16[4112,128]{1,0:T(8,128)(2,1)}, bf16[4112,128]{1,0:T(8,128)(2,1)S(1)}, u32[]{:S(2)}, u32[]{:S(2)}) collective-permute-start(bf16[4112,128]{1,0:T(8,128)(2,1)} %get-tuple-element.236), channel_id=1, source_target_pairs={{0,1},{3,2},{4,5},{7,6},{8,9},{11,10},{12,13},{15,14},{16,17},{19,... | collective-permute-start | bytes 3158024 | tf_op jit(solution)/shard_map/ppermute | solution.py:1062
  152.8 5.9 collective-permute-done.29.refs_3_
  159.7 4.3 collective-permute-start.33
  164.1 4.5 collective-permute-done.30.refs_1_
  174.2 7.2 %collective-permute-done.33 = bf16[4112,128]{1,0:T(8,128)(2,1)S(1)} collective-permute-done((bf16[4112,128]{1,0:T(8,128)(2,1)}, bf16[4112,128]{1,0:T(8,128)(2,1)S(1)}, u32[]{:S(2)}, u32[]{:S(2)}) %collective-permute-start.33) | collective-permute-done | bytes 1052704 | tf_op jit(solution)/shard_map/ppermute | solution.py:1062
  182.6 14.2 %shard_map.234 = (bf16[3072,384]{1,0:T(8,128)(2,1)}, bf16[2304,384]{1,0:T(8,128)(2,1)}, bf16[768,384]{1,0:T(8,128)(2,1)}, bf16[3072,384]{1,0:T(8,128)(2,1)}, bf1...) custom-call(s32[16]{0:T(128)S(1)} %stack.95.owner, ...), custom_call_target="tpu_custom_call" | custom-call | bytes 33030144 | tf_op jit(solution)/shard_map/pallas_call | solution.py:255
  196.9 6.9 shard_map.235.refs_0_
  207.8 5.3 shard_map.236
  213.2 15.3 %shard_map.237 = (bf16[1024,384]{1,0:T(8,128)(2,1)S(1)}, f32[8,1024]{1,0:T(8,128)S(1)}, bf16[1024,768]{1,0:T(8,128)(2,1)S(1)}) custom-call(s32[4]{0:T(128)S(1)} %get-tuple-element.467.low_ref, s32[4]{0:T(128)S(1)} %get-tuple-element.460.high_ref, bf16[1024,384]{1,0:T(8,128)(2,1)S(1)} %get-tuple-element.257.q_ref, ...), custom_call_target="tpu_custom_call" | custom-call | flops 6442450944 | bytes 6291456 | tf_op jit(solution)/shard_map/pallas_call | solution.py:654
  232.0 9.3 %shard_map.238 = (f32[1024,768]{1,0:T(8,128)S(1)}, bf16[1024,768]{1,0:T(8,128)(2,1)}, bf16[1024,768]{1,0:T(8,128)(2,1)}, bf16[1024,768]{1,0:T(8,128)(2,1)}, bf16...) custom-call(s32[1]{0:T(128)} %bitcast.6.half, f32[1024,768]{1,0:T(8,128)S(1)} %get-tuple-element.256.base.hid, ...), custom_call_target="tpu_custom_call" | custom-call | flops 4831838208 | bytes 18874368 | tf_op jit(solution)/shard_map/pallas_call | solution.py:721
  244.7 4.5 shard_map.239
  250.9 16.0 %shard_map.240 = (bf16[1024,384]{1,0:T(8,128)(2,1)S(1)}, f32[8,1024]{1,0:T(8,128)S(1)}, bf16[1024,768]{1,0:T(8,128)(2,1)}) custom-call(s32[4]{0:T(128)S(1)} %get-tuple-element.467.low_ref, s32[4]{0:T(128)S(1)} %get-tuple-element.460.high_ref, bf16[1024,384]{1,0:T(8,128)(2,1)S(1)} %get-tuple-element.268.q_ref, ...), custom_call_target="tpu_custom_call" | custom-call | flops 6442450944 | bytes 6291456 | tf_op jit(solution)/shard_map/pallas_call | solution.py:654
  268.2 3.6 collective-permute-start.10
  277.1 10.6 %shard_map.241 = (f32[1024,768]{1,0:T(8,128)S(1)}, bf16[1024,768]{1,0:T(8,128)(2,1)}, bf16[1024,768]{1,0:T(8,128)(2,1)}, bf16[1024,768]{1,0:T(8,128)(2,1)}, bf16...) custom-call(s32[1]{0:T(128)} %bitcast.6.half, f32[1024,768]{1,0:T(8,128)S(1)} %copy-done.16, ...), custom_call_target="tpu_custom_call" | custom-call | flops 4831838208 | bytes 18874368 | tf_op jit(solution)/shard_map/pallas_call | solution.py:721
  290.4 12.5 %shard_map.242 = (bf16[1024,768]{1,0:T(8,128)(2,1)S(1)}, bf16[1024,768]{1,0:T(8,128)(2,1)S(1)}, bf16[1024,768]{1,0:T(8,128)(2,1)S(1)}, bf16[1024,768]{1,0:T(8,12...) custom-call(s32[1]{0:T(128)} %bitcast.6.half, ...), custom_call_target="tpu_custom_call" | custom-call | flops 4831838208 | bytes 18874368 | tf_op jit(solution)/shard_map/pallas_call | solution.py:775
  306.7 4.5 convolution_convert_fusion.5.refs_1_
  313.7 3.6 multiply_convert_fusion.refs_3_
  320.9 24.0 %shard_map.244 = (f32[1024,768]{1,0:T(8,128)S(1)}, bf16[1024,384]{1,0:T(8,128)(2,1)S(1)}, bf16[1024,384]{1,0:T(8,128)(2,1)S(1)}, bf16[1024,384]{1,0:T(8,128)(2,1...) custom-call(s32[4]{0:T(128)S(1)} %get-tuple-element.466.low_ref, ...), custom_call_target="tpu_custom_call" | custom-call | flops 11274289152 | bytes 15728640 | tf_op jit(solution)/shard_map/pallas_call | solution.py:867
  345.0 5.9 shard_map.246
  362.0 11.8 %shard_map.247 = (f32[1024,768]{1,0:T(8,128)S(1)}, bf16[1024,768]{1,0:T(8,128)(2,1)S(1)}, bf16[1024,768]{1,0:T(8,128)(2,1)S(1)}, bf16[1024,768]{1,0:T(8,128)(2,1...) custom-call(s32[1]{0:T(128)} %bitcast.6.half, ...), custom_call_target="tpu_custom_call" | custom-call | flops 4831838208 | bytes 18874368 | tf_op jit(solution)/shard_map/pallas_call | solution.py:775
  377.3 6.5 collective-permute-start.43
  387.1 3.7 add_convert_fusion.3.refs_3_
  404.8 4.8 collective-permute-done.46.refs_2_
  411.6 23.7 %shard_map.250 = (f32[1024,768]{1,0:T(8,128)S(1)}, bf16[1024,384]{1,0:T(8,128)(2,1)S(1)}, bf16[1024,384]{1,0:T(8,128)(2,1)S(1)}, bf16[1024,384]{1,0:T(8,128)(2,1...) custom-call(s32[4]{0:T(128)S(1)} %get-tuple-element.466.low_ref, ...), custom_call_target="tpu_custom_call" | custom-call | flops 11274289152 | bytes 15728640 | tf_op jit(solution)/shard_map/pallas_call | solution.py:867
  439.2 5.6 shard_map.254
  444.7 5.4 collective-permute-start.50
  465.4 4.8 collective-permute-done.52.refs_4_
  505.6 3.4 fusion.1.own
  514.4 25.8 %collective-permute-done.62.refs_0_ = bf16[384,384]{1,0:T(8,128)(2,1)S(1)} collective-permute-done((bf16[384,384]{1,0:T(8,128)(2,1)S(1)}, bf16[384,384]{1,0:T(8,128)(2,1)S(1)}, u32[]{:S(2)}, u32[]{:S(2)}) %collective-permute-start.62) | collective-permute-done | bytes 294944 | tf_op jit(solution)/shard_map/ppermute | solution.py:1062
  581.8 10.2 %shard_map.278.refs_2_ = bf16[3,384,768]{2,1,0:T(8,128)(2,1)S(1)} custom-call(bf16[3072,384]{1,0:T(8,128)(2,1)} %get-tuple-element.377.base, bf16[3,3072,768]{2,1,0:T(8,128)(2,1)} %pinv_ref.9), custom_call_target="tpu_custom_call" | custom-call | flops 5435817984 | bytes 14155776 | tf_op jit(solution)/shard_map/pallas_call | solution.py:442
  615.4 3.7 collective-permute-done.69.refs_2_
  620.0 3.7 shard_map.285
  633.1 3.6 shard_map.287
  646.6 3.6 shard_map.289
  659.7 3.6 shard_map.291
  692.3 8.8 %shard_map.295 = (f32[32,128,128]{2,1,0:T(8,128)}, f32[32,128,128]{2,1,0:T(8,128)}, f32[32,128,128]{2,1,0:T(8,128)}, f32[32,128,128]{2,1,0:T(8,128)}) custom-call(s32[32]{0:T(128)S(1)} %convert_element_type.220.used, s32[1]{0:T(128)} %bitcast.27.flag.home, bf16[4112,128]{1,0:T(8,128)(2,1)} %shard_map.293.near, ...), custom_call_target="tpu_custom_call" | custom-call | flops 5905580032 | bytes 19922944 | tf_op jit(solution)/shard_map/pallas_call | solution.py:994
  (612 shorter events, 329.5 us)
Async XLA Ops:
  0.6 19.9 %collective-permute-start.3 = (s32[1,504]{1,0:T(1,128)}, s32[1,504]{1,0:T(1,128)S(1)}, u32[]{:S(2)}, u32[]{:S(2)}) collective-permute-start(s32[1,504]{1,0:T(1,128)} %param.18), channel_id=1, source_target_pairs={{0,1},{1,0},{2,3},{3,2},{4,5},{5,4},{6,7},{7,6},{8,9},{9,8},{10,11... | collective-permute-start | bytes 6056 | tf_op jit(solution)/shard_map/ppermute | solution.py:1062
  3.7 43.3 %collective-permute-start.9 = (bf16[1024,768]{1,0:T(8,128)(2,1)}, bf16[1024,768]{1,0:T(8,128)(2,1)}, u32[]{:S(2)}, u32[]{:S(2)}) collective-permute-start(bf16[1024,768]{1,0:T(8,128)(2,1)} %param.15), channel_id=1, source_target_pairs={{0,2},{3,1},{4,6},{7,5},{8,10},{11,9},{12,14},{15,13},{16,18},{19,... | collective-permute-start | bytes 4718600 | tf_op jit(solution)/shard_map/ppermute | solution.py:1062
  36.8 34.1 %collective-permute-start.11 = (bf16[4112,128]{1,0:T(8,128)(2,1)}, bf16[4112,128]{1,0:T(8,128)(2,1)S(1)}, u32[]{:S(2)}, u32[]{:S(2)}) collective-permute-start(bf16[4112,128]{1,0:T(8,128)(2,1)} %get-tuple-element.216), channel_id=1, source_target_pairs={{0,4},{3,7},{4,0},{7,3},{8,12},{11,15},{12,8},{15,11},{16,20},{19,... | collective-permute-start | bytes 3158024 | tf_op jit(solution)/shard_map/ppermute | solution.py:1062
  39.3 25.9 %collective-permute-start.5 = (bf16[4112,128]{1,0:T(8,128)(2,1)}, bf16[4112,128]{1,0:T(8,128)(2,1)}, u32[]{:S(2)}, u32[]{:S(2)}) collective-permute-start(bf16[4112,128]{1,0:T(8,128)(2,1)} %collective-permute-done.4), channel_id=1, source_target_pairs={{0,4},{3,7},{4,0},{7,3},{8,12},{11,15},{12,8},{15,11},{16,20},{19,... | collective-permute-start | bytes 3158024 | tf_op jit(solution)/shard_map/ppermute | solution.py:1062
  42.7 23.8 %collective-permute-start.6 = (bf16[4112,128]{1,0:T(8,128)(2,1)}, bf16[4112,128]{1,0:T(8,128)(2,1)}, u32[]{:S(2)}, u32[]{:S(2)}) collective-permute-start(bf16[4112,128]{1,0:T(8,128)(2,1)} %collective-permute-done.4), channel_id=1, source_target_pairs={{0,1},{3,2},{4,5},{7,6},{8,9},{11,10},{12,13},{15,14},{16,17},{19,... | collective-permute-start | bytes 3158024 | tf_op jit(solution)/shard_map/ppermute | solution.py:1062
  44.9 23.5 %collective-permute-start.7 = (bf16[4112,128]{1,0:T(8,128)(2,1)}, bf16[4112,128]{1,0:T(8,128)(2,1)}, u32[]{:S(2)}, u32[]{:S(2)}) collective-permute-start(bf16[4112,128]{1,0:T(8,128)(2,1)} %collective-permute-done.4), channel_id=1, source_target_pairs={{0,8},{3,11},{4,12},{7,15},{8,16},{11,19},{12,20},{15,23},{16,24},... | collective-permute-start | bytes 3158024 | tf_op jit(solution)/shard_map/ppermute | solution.py:1062
  47.0 25.3 %collective-permute-start.12 = (bf16[4112,128]{1,0:T(8,128)(2,1)}, bf16[4112,128]{1,0:T(8,128)(2,1)S(1)}, u32[]{:S(2)}, u32[]{:S(2)}) collective-permute-start(bf16[4112,128]{1,0:T(8,128)(2,1)} %get-tuple-element.216), channel_id=1, source_target_pairs={{0,1},{3,2},{4,5},{7,6},{8,9},{11,10},{12,13},{15,14},{16,17},{19,... | collective-permute-start | bytes 3158024 | tf_op jit(solution)/shard_map/ppermute | solution.py:1062
  68.5 25.7 %collective-permute-start.15 = (bf16[4112,128]{1,0:T(8,128)(2,1)}, bf16[4112,128]{1,0:T(8,128)(2,1)S(1)}, u32[]{:S(2)}, u32[]{:S(2)}) collective-permute-start(bf16[4112,128]{1,0:T(8,128)(2,1)} %get-tuple-element.220), channel_id=1, source_target_pairs={{0,4},{3,7},{4,0},{7,3},{8,12},{11,15},{12,8},{15,11},{16,20},{19,... | collective-permute-start | bytes 3158024 | tf_op jit(solution)/shard_map/ppermute | solution.py:1062
  70.9 24.6 %collective-permute-start.16 = (bf16[4112,128]{1,0:T(8,128)(2,1)}, bf16[4112,128]{1,0:T(8,128)(2,1)S(1)}, u32[]{:S(2)}, u32[]{:S(2)}) collective-permute-start(bf16[4112,128]{1,0:T(8,128)(2,1)} %get-tuple-element.220), channel_id=1, source_target_pairs={{0,1},{3,2},{4,5},{7,6},{8,9},{11,10},{12,13},{15,14},{16,17},{19,... | collective-permute-start | bytes 3158024 | tf_op jit(solution)/shard_map/ppermute | solution.py:1062
  72.3 24.6 %collective-permute-start.17 = (bf16[4112,128]{1,0:T(8,128)(2,1)}, bf16[4112,128]{1,0:T(8,128)(2,1)S(1)}, u32[]{:S(2)}, u32[]{:S(2)}) collective-permute-start(bf16[4112,128]{1,0:T(8,128)(2,1)} %get-tuple-element.221), channel_id=1, source_target_pairs={{1,5},{2,6},{5,1},{6,2},{9,13},{10,14},{13,9},{14,10},{17,21},{18,... | collective-permute-start | bytes 3158024 | tf_op jit(solution)/shard_map/ppermute | solution.py:1062
  79.9 25.6 %collective-permute-start.18 = (bf16[4112,128]{1,0:T(8,128)(2,1)}, bf16[4112,128]{1,0:T(8,128)(2,1)S(1)}, u32[]{:S(2)}, u32[]{:S(2)}) collective-permute-start(bf16[4112,128]{1,0:T(8,128)(2,1)} %get-tuple-element.220), channel_id=1, source_target_pairs={{0,8},{3,11},{4,12},{7,15},{8,16},{11,19},{12,20},{15,23},{16,24},... | collective-permute-start | bytes 3158024 | tf_op jit(solution)/shard_map/ppermute | solution.py:1062
  86.0 23.0 %collective-permute-start.19 = (bf16[4112,128]{1,0:T(8,128)(2,1)}, bf16[4112,128]{1,0:T(8,128)(2,1)S(1)}, u32[]{:S(2)}, u32[]{:S(2)}) collective-permute-start(bf16[4112,128]{1,0:T(8,128)(2,1)} %get-tuple-element.224), channel_id=1, source_target_pairs={{0,4},{3,7},{4,0},{7,3},{8,12},{11,15},{12,8},{15,11},{16,20},{19,... | collective-permute-start | bytes 3158024 | tf_op jit(solution)/shard_map/ppermute | solution.py:1062
  95.5 23.9 %collective-permute-start.21 = (bf16[4112,128]{1,0:T(8,128)(2,1)}, bf16[4112,128]{1,0:T(8,128)(2,1)S(1)}, u32[]{:S(2)}, u32[]{:S(2)}) collective-permute-start(bf16[4112,128]{1,0:T(8,128)(2,1)} %get-tuple-element.225), channel_id=1, source_target_pairs={{0,1},{3,2},{4,5},{7,6},{8,9},{11,10},{12,13},{15,14},{16,17},{19,... | collective-permute-start | bytes 3158024 | tf_op jit(solution)/shard_map/ppermute | solution.py:1062
  96.9 30.1 %collective-permute-start.22 = (bf16[4112,128]{1,0:T(8,128)(2,1)}, bf16[4112,128]{1,0:T(8,128)(2,1)S(1)}, u32[]{:S(2)}, u32[]{:S(2)}) collective-permute-start(bf16[4112,128]{1,0:T(8,128)(2,1)} %get-tuple-element.224), channel_id=1, source_target_pairs={{0,8},{3,11},{4,12},{7,15},{8,16},{11,19},{12,20},{15,23},{16,24},... | collective-permute-start | bytes 3158024 | tf_op jit(solution)/shard_map/ppermute | solution.py:1062
  106.6 23.9 %collective-permute-start.23 = (bf16[4112,128]{1,0:T(8,128)(2,1)}, bf16[4112,128]{1,0:T(8,128)(2,1)S(1)}, u32[]{:S(2)}, u32[]{:S(2)}) collective-permute-start(bf16[4112,128]{1,0:T(8,128)(2,1)} %get-tuple-element.230), channel_id=1, source_target_pairs={{0,4},{3,7},{4,0},{7,3},{8,12},{11,15},{12,8},{15,11},{16,20},{19,... | collective-permute-start | bytes 3158024 | tf_op jit(solution)/shard_map/ppermute | solution.py:1062
  109.0 25.9 %collective-permute-start.24 = (bf16[4112,128]{1,0:T(8,128)(2,1)}, bf16[4112,128]{1,0:T(8,128)(2,1)S(1)}, u32[]{:S(2)}, u32[]{:S(2)}) collective-permute-start(bf16[4112,128]{1,0:T(8,128)(2,1)} %get-tuple-element.230), channel_id=1, source_target_pairs={{0,1},{3,2},{4,5},{7,6},{8,9},{11,10},{12,13},{15,14},{16,17},{19,... | collective-permute-start | bytes 3158024 | tf_op jit(solution)/shard_map/ppermute | solution.py:1062
  110.4 25.9 %collective-permute-start.26 = (bf16[4112,128]{1,0:T(8,128)(2,1)}, bf16[4112,128]{1,0:T(8,128)(2,1)S(1)}, u32[]{:S(2)}, u32[]{:S(2)}) collective-permute-start(bf16[4112,128]{1,0:T(8,128)(2,1)} %get-tuple-element.230), channel_id=1, source_target_pairs={{0,8},{3,11},{4,12},{7,15},{8,16},{11,19},{12,20},{15,23},{16,24},... | collective-permute-start | bytes 3158024 | tf_op jit(solution)/shard_map/ppermute | solution.py:1062
  128.1 24.0 %collective-permute-start.27 = (bf16[4112,128]{1,0:T(8,128)(2,1)}, bf16[4112,128]{1,0:T(8,128)(2,1)S(1)}, u32[]{:S(2)}, u32[]{:S(2)}) collective-permute-start(bf16[4112,128]{1,0:T(8,128)(2,1)} %get-tuple-element.235), channel_id=1, source_target_pairs={{0,4},{3,7},{4,0},{7,3},{8,12},{11,15},{12,8},{15,11},{16,20},{19,... | collective-permute-start | bytes 3158024 | tf_op jit(solution)/shard_map/ppermute | solution.py:1062
  130.5 22.3 %collective-permute-start.28 = (bf16[4112,128]{1,0:T(8,128)(2,1)}, bf16[4112,128]{1,0:T(8,128)(2,1)S(1)}, u32[]{:S(2)}, u32[]{:S(2)}) collective-permute-start(bf16[4112,128]{1,0:T(8,128)(2,1)} %get-tuple-element.235), channel_id=1, source_target_pairs={{0,1},{3,2},{4,5},{7,6},{8,9},{11,10},{12,13},{15,14},{16,17},{19,... | collective-permute-start | bytes 3158024 | tf_op jit(solution)/shard_map/ppermute | solution.py:1062
  134.9 23.9 %collective-permute-start.29 = (bf16[4112,128]{1,0:T(8,128)(2,1)}, bf16[4112,128]{1,0:T(8,128)(2,1)S(1)}, u32[]{:S(2)}, u32[]{:S(2)}) collective-permute-start(bf16[4112,128]{1,0:T(8,128)(2,1)} %get-tuple-element.231), channel_id=1, source_target_pairs={{0,1},{3,2},{4,5},{7,6},{8,9},{11,10},{12,13},{15,14},{16,17},{19,... | collective-permute-start | bytes 3158024 | tf_op jit(solution)/shard_map/ppermute | solution.py:1062
  137.6 31.0 %collective-permute-start.30 = (bf16[4112,128]{1,0:T(8,128)(2,1)}, bf16[4112,128]{1,0:T(8,128)(2,1)S(1)}, u32[]{:S(2)}, u32[]{:S(2)}) collective-permute-start(bf16[4112,128]{1,0:T(8,128)(2,1)} %get-tuple-element.236), channel_id=1, source_target_pairs={{0,4},{3,7},{4,0},{7,3},{8,12},{11,15},{12,8},{15,11},{16,20},{19,... | collective-permute-start | bytes 3158024 | tf_op jit(solution)/shard_map/ppermute | solution.py:1062
  141.0 29.1 %collective-permute-start.31 = (bf16[4112,128]{1,0:T(8,128)(2,1)}, bf16[4112,128]{1,0:T(8,128)(2,1)S(1)}, u32[]{:S(2)}, u32[]{:S(2)}) collective-permute-start(bf16[4112,128]{1,0:T(8,128)(2,1)} %get-tuple-element.236), channel_id=1, source_target_pairs={{0,1},{3,2},{4,5},{7,6},{8,9},{11,10},{12,13},{15,14},{16,17},{19,... | collective-permute-start | bytes 3158024 | tf_op jit(solution)/shard_map/ppermute | solution.py:1062
  159.7 21.6 %collective-permute-start.33 = (bf16[4112,128]{1,0:T(8,128)(2,1)}, bf16[4112,128]{1,0:T(8,128)(2,1)S(1)}, u32[]{:S(2)}, u32[]{:S(2)}) collective-permute-start(bf16[4112,128]{1,0:T(8,128)(2,1)} %get-tuple-element.238), channel_id=1, source_target_pairs={{0,1},{3,2},{4,5},{7,6},{8,9},{11,10},{12,13},{15,14},{16,17},{19,... | collective-permute-start | bytes 3158024 | tf_op jit(solution)/shard_map/ppermute | solution.py:1062
  268.2 19.6 %collective-permute-start.10 = (bf16[1024,768]{1,0:T(8,128)(2,1)}, bf16[1024,768]{1,0:T(8,128)(2,1)}, u32[]{:S(2)}, u32[]{:S(2)}) collective-permute-start(bf16[1024,768]{1,0:T(8,128)(2,1)} %param.16), channel_id=1, source_target_pairs={{0,2},{3,1},{4,6},{7,5},{8,10},{11,9},{12,14},{15,13},{16,18},{19,... | collective-permute-start | bytes 4718600 | tf_op jit(solution)/shard_map/ppermute | solution.py:1062
  287.7 26.0 %collective-permute-start.40 = (bf16[1024,768]{1,0:T(8,128)(2,1)}, bf16[1024,768]{1,0:T(8,128)(2,1)}, u32[]{:S(2)}, u32[]{:S(2)}) collective-permute-start(bf16[1024,768]{1,0:T(8,128)(2,1)} %get-tuple-element.284), channel_id=1, source_target_pairs={{0,2},{1,3},{2,0},{3,1},{4,6},{5,7},{6,4},{7,5},{8,10},{9,11},{10,... | collective-permute-start | bytes 4718600 | tf_op jit(solution)/shard_map/ppermute | solution.py:1062
  317.3 27.6 %collective-permute-start.41 = (bf16[768,768]{1,0:T(8,128)(2,1)}, bf16[768,768]{1,0:T(8,128)(2,1)}, u32[]{:S(2)}, u32[]{:S(2)}) collective-permute-start(bf16[768,768]{1,0:T(8,128)(2,1)} %get-tuple-element.291.own), channel_id=1, source_target_pairs={{1,5},{2,6},{5,1},{6,2},{9,13},{10,14},{13,9},{14,10},{17,21},{18,... | collective-permute-start | bytes 3538952 | tf_op jit(solution)/shard_map/ppermute | solution.py:1062
  352.4 31.4 %collective-permute-start.44 = (bf16[768,768]{1,0:T(8,128)(2,1)S(1)}, bf16[768,768]{1,0:T(8,128)(2,1)S(1)}, u32[]{:S(2)}, u32[]{:S(2)}) collective-permute-start(bf16[768,768]{1,0:T(8,128)(2,1)S(1)} %copy-done.68), channel_id=1, source_target_pairs={{1,5},{2,6},{5,1},{6,2},{9,13},{10,14},{13,9},{14,10},{17,21},{18,... | collective-permute-start | bytes 3538952 | tf_op jit(solution)/shard_map/ppermute | solution.py:1062
  356.6 27.3 %collective-permute-start.45 = (bf16[768,768]{1,0:T(8,128)(2,1)S(1)}, bf16[768,768]{1,0:T(8,128)(2,1)S(1)}, u32[]{:S(2)}, u32[]{:S(2)}) collective-permute-start(bf16[768,768]{1,0:T(8,128)(2,1)S(1)} %add_convert_fusion.4.own), channel_id=1, source_target_pairs={{1,0},{2,3},{5,4},{6,7},{9,8},{10,11},{13,12},{14,15},{17,16},{18,... | collective-permute-start | bytes 3538952 | tf_op jit(solution)/shard_map/ppermute | solution.py:1062
  377.3 34.3 %collective-permute-start.43 = (bf16[1024,768]{1,0:T(8,128)(2,1)S(1)}, bf16[1024,768]{1,0:T(8,128)(2,1)}, u32[]{:S(2)}, u32[]{:S(2)}) collective-permute-start(bf16[1024,768]{1,0:T(8,128)(2,1)S(1)} %get-tuple-element.296.own), channel_id=1, source_target_pairs={{0,2},{1,3},{2,0},{3,1},{4,6},{5,7},{6,4},{7,5},{8,10},{9,11},{10,... | collective-permute-start | bytes 4718600 | tf_op jit(solution)/shard_map/ppermute | solution.py:1062
  398.3 37.9 %collective-permute-start.47 = (bf16[384,1152]{1,0:T(8,128)(2,1)S(1)}, bf16[384,1152]{1,0:T(8,128)(2,1)S(1)}, u32[]{:S(2)}, u32[]{:S(2)}) collective-permute-start(bf16[384,1152]{1,0:T(8,128)(2,1)S(1)} %copy-done.67), channel_id=1, source_target_pairs={{1,5},{2,6},{5,1},{6,2},{9,13},{10,14},{13,9},{14,10},{17,21},{18,... | collective-permute-start | bytes 2654216 | tf_op jit(solution)/shard_map/ppermute | solution.py:1062
  399.1 37.2 %collective-permute-start.48 = (bf16[384,384]{1,0:T(8,128)(2,1)S(1)}, bf16[384,384]{1,0:T(8,128)(2,1)S(1)}, u32[]{:S(2)}, u32[]{:S(2)}) collective-permute-start(bf16[384,384]{1,0:T(8,128)(2,1)S(1)} %copy-done.117), channel_id=1, source_target_pairs={{1,5},{2,6},{5,1},{6,2},{9,13},{10,14},{13,9},{14,10},{17,21},{18,... | collective-permute-start | bytes 884744 | tf_op jit(solution)/shard_map/ppermute | solution.py:1062
  409.6 26.7 %collective-permute-start.49 = (bf16[768,768]{1,0:T(8,128)(2,1)}, bf16[768,768]{1,0:T(8,128)(2,1)S(1)}, u32[]{:S(2)}, u32[]{:S(2)}) collective-permute-start(bf16[768,768]{1,0:T(8,128)(2,1)} %get-tuple-element.319.own), channel_id=1, source_target_pairs={{1,5},{2,6},{5,1},{6,2},{9,13},{10,14},{13,9},{14,10},{17,21},{18,... | collective-permute-start | bytes 3538952 | tf_op jit(solution)/shard_map/ppermute | solution.py:1062
  410.5 54.9 %collective-permute-start.51 = (bf16[768,768]{1,0:T(8,128)(2,1)}, bf16[768,768]{1,0:T(8,128)(2,1)S(1)}, u32[]{:S(2)}, u32[]{:S(2)}) collective-permute-start(bf16[768,768]{1,0:T(8,128)(2,1)} %get-tuple-element.323.own), channel_id=1, source_target_pairs={{1,5},{2,6},{5,1},{6,2},{9,13},{10,14},{13,9},{14,10},{17,21},{18,... | collective-permute-start | bytes 3538952 | tf_op jit(solution)/shard_map/ppermute | solution.py:1062
  459.1 38.9 %collective-permute-start.56 = (bf16[768,768]{1,0:T(8,128)(2,1)}, bf16[768,768]{1,0:T(8,128)(2,1)}, u32[]{:S(2)}, u32[]{:S(2)}) collective-permute-start(bf16[768,768]{1,0:T(8,128)(2,1)} %add_convert_fusion.2.own), channel_id=1, source_target_pairs={{1,0},{2,3},{5,4},{6,7},{9,8},{10,11},{13,12},{14,15},{17,16},{18,... | collective-permute-start | bytes 3538952 | tf_op jit(solution)/shard_map/ppermute | solution.py:1062
  471.1 26.9 %collective-permute-start.53 = (bf16[1536,384]{1,0:T(8,128)(2,1)}, bf16[1536,384]{1,0:T(8,128)(2,1)}, u32[]{:S(2)}, u32[]{:S(2)}) collective-permute-start(bf16[1536,384]{1,0:T(8,128)(2,1)} %get-tuple-element.328.own), channel_id=1, source_target_pairs={{1,5},{2,6},{5,1},{6,2},{9,13},{10,14},{13,9},{14,10},{17,21},{18,... | collective-permute-start | bytes 3538952 | tf_op jit(solution)/shard_map/ppermute | solution.py:1062
  473.6 24.4 %collective-permute-start.54 = (bf16[384,1152]{1,0:T(8,128)(2,1)}, bf16[384,1152]{1,0:T(8,128)(2,1)}, u32[]{:S(2)}, u32[]{:S(2)}) collective-permute-start(bf16[384,1152]{1,0:T(8,128)(2,1)} %get-tuple-element.329.own), channel_id=1, source_target_pairs={{1,5},{2,6},{5,1},{6,2},{9,13},{10,14},{13,9},{14,10},{17,21},{18,... | collective-permute-start | bytes 2654216 | tf_op jit(solution)/shard_map/ppermute | solution.py:1062
  496.6 62.5 %collective-permute-start.60 = (bf16[768,768]{1,0:T(8,128)(2,1)}, bf16[768,768]{1,0:T(8,128)(2,1)S(1)}, u32[]{:S(2)}, u32[]{:S(2)}) collective-permute-start(bf16[768,768]{1,0:T(8,128)(2,1)} %add_convert_fusion.1.own), channel_id=1, source_target_pairs={{1,0},{2,3},{5,4},{6,7},{9,8},{10,11},{13,12},{14,15},{17,16},{18,... | collective-permute-start | bytes 3538952 | tf_op jit(solution)/shard_map/ppermute | solution.py:1062
  504.2 60.3 %collective-permute-start.57 = (bf16[1536,384]{1,0:T(8,128)(2,1)}, bf16[1536,384]{1,0:T(8,128)(2,1)}, u32[]{:S(2)}, u32[]{:S(2)}) collective-permute-start(bf16[1536,384]{1,0:T(8,128)(2,1)} %pad_maximum_fusion.1.own), channel_id=1, source_target_pairs={{1,0},{2,3},{5,4},{6,7},{9,8},{10,11},{13,12},{14,15},{17,16},{18,... | collective-permute-start | bytes 3538952 | tf_op jit(solution)/shard_map/ppermute | solution.py:1062
  509.0 55.5 %collective-permute-start.58 = (bf16[384,1152]{1,0:T(8,128)(2,1)}, bf16[384,1152]{1,0:T(8,128)(2,1)}, u32[]{:S(2)}, u32[]{:S(2)}) collective-permute-start(bf16[384,1152]{1,0:T(8,128)(2,1)} %fusion.1.own), channel_id=1, source_target_pairs={{1,0},{2,3},{5,4},{6,7},{9,8},{10,11},{13,12},{14,15},{17,16},{18,... | collective-permute-start | bytes 2654216 | tf_op jit(solution)/shard_map/ppermute | solution.py:1062
  511.1 29.2 %collective-permute-start.62 = (bf16[384,384]{1,0:T(8,128)(2,1)S(1)}, bf16[384,384]{1,0:T(8,128)(2,1)S(1)}, u32[]{:S(2)}, u32[]{:S(2)}) collective-permute-start(bf16[384,384]{1,0:T(8,128)(2,1)S(1)} %fusion.5.own), channel_id=1, source_target_pairs={{1,0},{2,3},{5,4},{6,7},{9,8},{10,11},{13,12},{14,15},{17,16},{18,... | collective-permute-start | bytes 884744 | tf_op jit(solution)/shard_map/ppermute | solution.py:1062
  513.0 51.5 %collective-permute-start.59 = (bf16[384,384]{1,0:T(8,128)(2,1)S(1)}, bf16[384,384]{1,0:T(8,128)(2,1)S(1)}, u32[]{:S(2)}, u32[]{:S(2)}) collective-permute-start(bf16[384,384]{1,0:T(8,128)(2,1)S(1)} %fusion.4.own), channel_id=1, source_target_pairs={{1,0},{2,3},{5,4},{6,7},{9,8},{10,11},{13,12},{14,15},{17,16},{18,... | collective-permute-start | bytes 884744 | tf_op jit(solution)/shard_map/ppermute | solution.py:1062
  578.5 27.3 %collective-permute-start.67 = (bf16[4112,128]{1,0:T(8,128)(2,1)S(1)}, bf16[4112,128]{1,0:T(8,128)(2,1)S(1)}, u32[]{:S(2)}, u32[]{:S(2)}) collective-permute-start(bf16[4112,128]{1,0:T(8,128)(2,1)S(1)} %get-tuple-element.438), channel_id=1, source_target_pairs={{0,4},{3,7},{4,0},{7,3},{8,12},{11,15},{12,8},{15,11},{16,20},{19,... | collective-permute-start | bytes 3158024 | tf_op jit(solution)/shard_map/ppermute | solution.py:1062
  605.7 47.2 %collective-permute-start.65 = (bf16[1024,768]{1,0:T(8,128)(2,1)S(1)}, bf16[1024,768]{1,0:T(8,128)(2,1)}, u32[]{:S(2)}, u32[]{:S(2)}) collective-permute-start(bf16[1024,768]{1,0:T(8,128)(2,1)S(1)} %add_convert_fusion), channel_id=1, source_target_pairs={{0,2},{1,3},{2,0},{3,1},{4,6},{5,7},{6,4},{7,5},{8,10},{9,11},{10,... | collective-permute-start | bytes 4718600 | tf_op jit(solution)/shard_map/ppermute | solution.py:1062
  628.8 48.9 %collective-permute-start.63 = (bf16[1024,768]{1,0:T(8,128)(2,1)S(1)}, bf16[1024,768]{1,0:T(8,128)(2,1)}, u32[]{:S(2)}, u32[]{:S(2)}) collective-permute-start(bf16[1024,768]{1,0:T(8,128)(2,1)S(1)} %copy-done.62), channel_id=1, source_target_pairs={{0,1},{3,2},{4,5},{7,6},{8,9},{11,10},{12,13},{15,14},{16,17},{19,... | collective-permute-start | bytes 4718600 | tf_op jit(solution)/shard_map/ppermute | solution.py:1062
  636.7 20.8 %collective-permute-start.74 = (bf16[4112,128]{1,0:T(8,128)(2,1)}, bf16[4112,128]{1,0:T(8,128)(2,1)}, u32[]{:S(2)}, u32[]{:S(2)}) collective-permute-start(bf16[4112,128]{1,0:T(8,128)(2,1)} %get-tuple-element.396), channel_id=1, source_target_pairs={{0,4},{3,7},{4,0},{7,3},{8,12},{11,15},{12,8},{15,11},{16,20},{19,... | collective-permute-start | bytes 3158024 | tf_op jit(solution)/shard_map/ppermute | solution.py:1062
  640.7 19.0 %collective-permute-start.75 = (bf16[4112,128]{1,0:T(8,128)(2,1)}, bf16[4112,128]{1,0:T(8,128)(2,1)}, u32[]{:S(2)}, u32[]{:S(2)}) collective-permute-start(bf16[4112,128]{1,0:T(8,128)(2,1)} %get-tuple-element.397), channel_id=1, source_target_pairs={{0,8},{3,11},{4,12},{7,15},{8,16},{11,19},{12,20},{15,23},{16,24},... | collective-permute-start | bytes 3158024 | tf_op jit(solution)/shard_map/ppermute | solution.py:1062
  657.5 22.1 %collective-permute-start.66 = (bf16[1024,384]{1,0:T(8,128)(2,1)}, bf16[1024,384]{1,0:T(8,128)(2,1)}, u32[]{:S(2)}, u32[]{:S(2)}) collective-permute-start(bf16[1024,384]{1,0:T(8,128)(2,1)} %select_convert_fusion), channel_id=1, source_target_pairs={{0,1},{3,2},{4,5},{7,6},{8,9},{11,10},{12,13},{15,14},{16,17},{19,... | collective-permute-start | bytes 2359304 | tf_op jit(solution)/shard_map/ppermute | solution.py:1062
  663.3 19.6 %collective-permute-start.78 = (bf16[4112,128]{1,0:T(8,128)(2,1)}, bf16[4112,128]{1,0:T(8,128)(2,1)}, u32[]{:S(2)}, u32[]{:S(2)}) collective-permute-start(bf16[4112,128]{1,0:T(8,128)(2,1)} %get-tuple-element.406), channel_id=1, source_target_pairs={{0,4},{3,7},{4,0},{7,3},{8,12},{11,15},{12,8},{15,11},{16,20},{19,... | collective-permute-start | bytes 3158024 | tf_op jit(solution)/shard_map/ppermute | solution.py:1062
  (181 other events, 1197.7 us)

commit v10 on v8

--- a/solution.py
+++ b/solution.py
@@ -1037,14 +1037,14 @@
 
 
 def reduce_call(j, n, buffer, arrived, carried, payload):
-    last = j == 3
+    last = j >= 2
     at = lambda j, x_rel: pl.BlockSpec((payload, BS), lambda i: ((j * 2 + x_rel) * 2 + n, 0))
     whole = fixed((payload, BS))
     operands = [stay(buffer), stay(arrived)] + ([] if carried is None else [stay(carried)])
     specs = [at(j, 0)] + [whole] * (len(operands) - 1)
     if not last:
         operands.append(stay(buffer))
-        specs.append(at(j + 1, 1))
+        specs.append(at(j + 2, 1))
     outs = [pltpu.HBM((payload, BS), bf16)] * (1 if last else 2)
     made = pl.pallas_call(
         functools.partial(reduce_kernel, carried is not None, last),
@@ -1072,6 +1072,8 @@
         self.y_in = [(at(d, t), at(d, 1 - t)) for d, t in away]
         self.x_home = [(at(d, t), at(d ^ 2, t)) for d, t in home]
         self.x_away = [(at(d, t), at(d ^ 2, t)) for d, t in away]
+        self.x_all = [(at(d, t), at(d ^ 2, t)) for d, t in pairs]
+        self.z_all = [(at(d, t), at((d + 4) % dp_n, t)) for d, t in pairs]
         self.z_home = [(at(d, t), at((d + 4) % dp_n, t)) for d, t in home]
 
 
@@ -1158,46 +1160,34 @@
     flag = home.astype(jnp.int32).reshape(1)
     if grid3:
         z_pos = dp_pos // 4
-        packs = [[own_pack], [send(own_pack, routes.core_in)]]
-        across, over_y, corner = [[], []], [[], []], [[], []]
-        token = jnp.zeros((8, BS), f32)
-        chunks = []
-        for j in range(5):
-            for n in range(2):
-                moved = {}
-                if j < 4:
-                    moved["x"] = send(packs[n][j], routes.x_home)
-                    moved["y"] = send(packs[n][j], routes.y_out)
-                if j:
-                    source, route = (across, routes.y_out) if n == 0 else (over_y, routes.x_away)
-                    moved["corner"] = send(source[n][j - 1], route)
-                if j < 3:
-                    moved["z"] = send(packs[n][j], routes.z_home)
-                work = []
-                if j + n == 0:
-                    work = [slot_other]
-                if 1 <= 2 * j + n <= CHUNKS:
-                    work = [expand(2 * j + n - 1)]
-                if j < 4:
-                    token, *made = fence(token, *moved.values(), *work)
-                    if j + n == 0:
-                        slot_other = made.pop()
-                    elif work:
-                        chunks.append(made.pop())
-                    moved = dict(zip(moved, made))
-                    across[n].append(moved["x"])
-                    over_y[n].append(moved["y"])
-                if j < 3:
-                    packs[n].append(moved["z"])
-                if j:
-                    corner[n].append(moved["corner"])
-        first, second, owner = [], [], []
+        pack = own_pack
+        chunks, first, second, owner = [], [], [], []
+        middle_row = slots_per * BS // 2
         for j in range(4):
-            first += [packs[0][j], packs[1][j], across[0][j], across[1][j]]
-            second += [over_y[0][j], over_y[1][j], corner[0][j], corner[1][j]]
+            beside_x, beside_y = send(pack, routes.x_all), send(pack, routes.y_all)
+            if j < 3:
+                further = send(pack, routes.z_all)
+                work = [expand(j)] + ([slot_other] if j == 0 else [])
+                further, chunk, *work = fence(further, *work)
+                chunks.append(chunk)
+                if j == 0:
+                    [slot_other] = work
+            else:
+                beside_x, chunk = fence(beside_x, expand(j))
+                chunks.append(chunk)
+            corner = jnp.concatenate(
+                [send(beside_x[:middle_row], routes.y_all), send(beside_y[middle_row:], routes.x_all)],
+                axis=0,
+            )
+            near_two = send(jnp.where(home, beside_y, pack), routes.core_all)
+            far_two = send(jnp.where(home, corner, beside_x), routes.core_all)
+            first += [pack, near_two, beside_x, far_two]
+            second += [beside_y, near_two, corner, far_two]
             for x_rel in range(2):
                 for n in range(2):
                     owner.append(((z_pos - j) % 4) * 4 + (x_pos ^ x_rel) * 2 + (core ^ n))
+            if j < 3:
+                pack = further
         first = [v[None] for v in first]
         second = [v[None] for v in second]
         owner = jnp.stack(owner).astype(jnp.int32)
@@ -1352,13 +1342,13 @@
     vec_grad = pack_call([grad_emb_bias] + vec_grads[0] + vec_grads[1], dp_n, vec_per)
     go0 = dot_tn(caches[low][5], grad_low).astype(bf16)
     ao0, av = over(go0), over(vec_grad)
-    gbm, xb, aq0, ao0, av, aq1, buffer = hold(gbm, xb, aq0, ao0, av, aq1, buffer)
-    ab = over(half_sum(half_at * 0, gbm, xb)) if grid3 else None
     buffer = place_tiles(("out", top), go1, ao1, buffer)
-    buffer = place_tiles(("qkv", top), gq1, aq1, buffer)
     buffer = place_tiles(("down", low), gd0, ad0, buffer)
     buffer = place_tiles(("up", low), gu0, au0, buffer)
     buffer = place_base(1, gbt, None, buffer)
+    gbm, xb, aq0, ao0, av, aq1, buffer = hold(gbm, xb, aq0, ao0, av, aq1, buffer)
+    ab = over(half_sum(half_at * 0, gbm, xb)) if grid3 else None
+    buffer = place_tiles(("qkv", top), gq1, aq1, buffer)
     buffer = place_tiles(("out", low), go0, ao0, buffer)
     buffer = scatter_vec(vec_pos, vec_grad, av, buffer)
     buffer = place_tiles(("qkv", low), gq0, aq0, buffer)
@@ -1372,7 +1362,9 @@
         order = (1, 0)
         resized = resize_call(weights, pinv)
         carried = {n: None for n in order}
-        across = {n: send(buffer.reshape(4, 2, 2, payload, BS)[0, 1, n], routes.x_home) for n in order}
+        blocks = buffer.reshape(4, 2, 2, payload, BS)
+        across = {n: send(blocks[0, 1, n], routes.x_home) for n in order}
+        following = {n: blocks[1, 1, n] for n in order}
         rounded = {}
         for j in range(4):
             for n in order:
@@ -1382,10 +1374,12 @@
                 token, across[n], carried[n], extra = hold(token, across[n], carried[n], extra)
                 if extra is not None:
                     resized = extra
-                total, later = reduce_call(j, n, buffer, across[n], carried[n], payload)
+                arrived = across[n]
+                if j < 3:
+                    across[n] = send(following[n], routes.x_home)
+                total, following[n] = reduce_call(j, n, buffer, arrived, carried[n], payload)
                 if j < 3:
                     carried[n] = send(total, routes.z_home)
-                    across[n] = send(later, routes.x_home)
                 else:
                     rounded[n] = total
         near_grad, far_grad = rounded[0], send(rounded[1], routes.core_out)

time: 668 us -> 659 us (0.987)
  starting transfers between devices: 156 us -> 101 us
  waiting for transfers between devices: 122 us -> 168 us
    ppermute x76 -> x72, starting transfers between devices: 156 us -> 101 us  [send(): return lax.ppermute(value, AXES, route)]
    ppermute x76 -> x72, waiting for transfers between devices: 122 us -> 168 us  [send(): return lax.ppermute(value, AXES, route)]
    select_n x0 -> x8, other arithmetic: none -> 7.76 us  [the longest x4 4.98 us: shards(): near_two = send(jnp.where(home, beside_y, pack), routes.core_all)]
    unnamed x228 -> x234, local copies, waits for them, and re-layouts: 35 us -> 30.1 us
  transfers between devices with their start and end apart: 76 -> 72, of which waited for: 25 -> 31; matrix products, arithmetic and copies ran while one was open for 8% -> 9% of each run, Pallas kernels for 31% -> 31%
where the time goes in v10:
time: 659 us; the launch traced here: 648 us
  Pallas kernels  278 us (42%)
  waiting for transfers between devices  168 us (25%)
  starting transfers between devices  101 us (15%)
  local copies, waits for them, and re-layouts  39.3 us (6%)
  matrix products  32.7 us (5%)
  other arithmetic  26.2 us (4%)
    ppermute x72, waiting for transfers between devices, send(): return lax.ppermute(value, AXES, route)  168 us
    ppermute x72, starting transfers between devices, send(): return lax.ppermute(value, AXES, route)  101 us
    pallas_call x2, Pallas kernels, attend_back_call(): pl.pallas_call(attend_back_kernel, out_shape=[shape(D, f32), shape(D, bf1...  40.8 us
    pallas_call x10, Pallas kernels, scatter_matrix(): pl.pallas_call(functools.partial(scatter_kernel, rows_n, cols_n, steps, p...  35.4 us
    unnamed x234, local copies, waits for them, and re-layouts  30.1 us
    dot_general x12, matrix products, dot_tn(): lax.dot_general(left, right, (((0,), (0,)), ((), ())), preferred_element_...  29.6 us
    pallas_call x8, Pallas kernels, reduce_call(): pl.pallas_call(functools.partial(reduce_kernel, carried is not None, last...  27.1 us
    pallas_call x2, Pallas kernels, attend_call(): pl.pallas_call(functools.partial(attend_kernel, layer), out_shape=[jax.Sh...  26.5 us
  transfers between devices with their start and end apart: 72, of which 31 were waited for; matrix products, arithmetic and copies ran while one was open for 9% of the time, Pallas kernels for 31%

profile of v10, /device:TPU:0, one launch (start us, length us, event | category | flops | bytes accessed | tf_op | source)
XLA Modules:
  0.0 647.6 jit_solution(10788196173117095817)
XLA Ops:
  17.6 13.1 %collective-permute-done.8 = bf16[4112,128]{1,0:T(8,128)(2,1)} collective-permute-done((bf16[4112,128]{1,0:T(8,128)(2,1)}, bf16[4112,128]{1,0:T(8,128)(2,1)}, u32[]{:S(2)}, u32[]{:S(2)}) %collective-permute-start.8) | collective-permute-done | bytes 1052704 | tf_op jit(solution)/shard_map/ppermute | solution.py:1081
  37.8 5.5 shard_map.222.refs_1_
  49.0 6.0 shard_map.228.refs_1_
  55.0 5.5 shard_map.226.refs_1_
  61.7 5.5 shard_map.224.refs_1_
  75.0 17.7 %collective-permute-done.5.refs_0_ = bf16[4112,128]{1,0:T(8,128)(2,1)S(1)} collective-permute-done((bf16[4112,128]{1,0:T(8,128)(2,1)S(1)}, bf16[4112,128]{1,0:T(8,128)(2,1)S(1)}, u32[]{:S(2)}, u32[]{:S(2)}) %collective-permute-start.5) | collective-permute-done | bytes 1052704 | tf_op jit(solution)/shard_map/ppermute | solution.py:1081
  99.8 17.0 %collective-permute-done.22 = bf16[4112,128]{1,0:T(8,128)(2,1)S(1)} collective-permute-done((bf16[4112,128]{1,0:T(8,128)(2,1)}, bf16[4112,128]{1,0:T(8,128)(2,1)S(1)}, u32[]{:S(2)}, u32[]{:S(2)}) %collective-permute-start.22) | collective-permute-done | bytes 1052704 | tf_op jit(solution)/shard_map/ppermute | solution.py:1081
  116.8 4.2 collective-permute-start.23
  124.5 6.9 %collective-permute-done.23 = bf16[2048,128]{1,0:T(8,128)(2,1)S(1)} collective-permute-done((bf16[2048,128]{1,0:T(8,128)(2,1)S(1)}, bf16[2048,128]{1,0:T(8,128)(2,1)S(1)}, u32[]{:S(2)}, u32[]{:S(2)}) %collective-permute-start.23) | collective-permute-done | bytes 524320 | tf_op jit(solution)/shard_map/ppermute | solution.py:1081
  135.4 19.0 %collective-permute-done.26 = bf16[4112,128]{1,0:T(8,128)(2,1)S(1)} collective-permute-done((bf16[4112,128]{1,0:T(8,128)(2,1)}, bf16[4112,128]{1,0:T(8,128)(2,1)S(1)}, u32[]{:S(2)}, u32[]{:S(2)}) %collective-permute-start.26) | collective-permute-done | bytes 1052704 | tf_op jit(solution)/shard_map/ppermute | solution.py:1081
  161.0 7.8 %collective-permute-done.28 = bf16[2048,128]{1,0:T(8,128)(2,1)S(1)} collective-permute-done((bf16[2048,128]{1,0:T(8,128)(2,1)S(1)}, bf16[2048,128]{1,0:T(8,128)(2,1)S(1)}, u32[]{:S(2)}, u32[]{:S(2)}) %collective-permute-start.28) | collective-permute-done | bytes 524320 | tf_op jit(solution)/shard_map/ppermute | solution.py:1081
  178.0 14.2 %shard_map.230 = (bf16[3072,384]{1,0:T(8,128)(2,1)}, bf16[2304,384]{1,0:T(8,128)(2,1)}, bf16[768,384]{1,0:T(8,128)(2,1)}, bf16[3072,384]{1,0:T(8,128)(2,1)}, bf1...) custom-call(s32[16]{0:T(128)S(1)} %stack.95.owner, ...), custom_call_target="tpu_custom_call" | custom-call | bytes 33030144 | tf_op jit(solution)/shard_map/pallas_call | solution.py:243
  192.3 6.8 %shard_map.231.refs_0_ = bf16[1024,384]{1,0:T(8,128)(2,1)S(1)} custom-call(s32[1]{0:T(128)} %bitcast.6.half.part, bf16[1024,768]{1,0:T(8,128)(2,1)} %get-tuple-element.165.refs_0_, bf16[1024,768]{1,0:T(8,128)(2,1)} %get-tuple-element.167.refs_1_, bf16[1024,768]{1,0:T(8,128)(2,1)} %get-tuple-element.169.refs_2_, ...), custom_call_target="tpu_custom_call" | custom-call | flops 2415919104 | bytes 9437184 | tf_op jit(solution)/shard_map/pallas_call | solution.py:552
  201.6 4.9 shard_map.232
  206.6 13.2 %shard_map.233 = (bf16[1024,384]{1,0:T(8,128)(2,1)S(1)}, f32[8,1024]{1,0:T(8,128)S(1)}, bf16[1024,768]{1,0:T(8,128)(2,1)S(1)}) custom-call(s32[4]{0:T(128)S(1)} %get-tuple-element.363.low_ref, s32[4]{0:T(128)S(1)} %get-tuple-element.356.high_ref, bf16[1024,384]{1,0:T(8,128)(2,1)S(1)} %get-tuple-element.178.q_ref, ...), custom_call_target="tpu_custom_call" | custom-call | flops 6442450944 | bytes 6291456 | tf_op jit(solution)/shard_map/pallas_call | solution.py:679
  224.2 9.6 %shard_map.234 = (f32[1024,768]{1,0:T(8,128)S(1)}, bf16[1024,768]{1,0:T(8,128)(2,1)}, bf16[1024,1536]{1,0:T(8,128)(2,1)}, bf16[1024,1536]{1,0:T(8,128)(2,1)}, bf16[1024,768]{1,0:T(8,128)(2,1)S(1)}) custom-call(f32[1024,768]{1,0:T(8,128)S(1)} %get-tuple-element.177.base.hid, bf16[1024,768]{1,0:T(8,128)(2,1)S(1)} %get-tuple-element.182.own, ...), custom_call_target="tpu_custom_call" | custom-call | flops 4831838208 | bytes 18874368 | tf_op jit(solution)/shard_map/pallas_call | solution.py:742
  237.2 4.4 shard_map.235
  241.7 13.3 %shard_map.236 = (bf16[1024,384]{1,0:T(8,128)(2,1)S(1)}, f32[8,1024]{1,0:T(8,128)S(1)}, bf16[1024,768]{1,0:T(8,128)(2,1)S(1)}) custom-call(s32[4]{0:T(128)S(1)} %get-tuple-element.363.low_ref, s32[4]{0:T(128)S(1)} %get-tuple-element.356.high_ref, bf16[1024,384]{1,0:T(8,128)(2,1)S(1)} %get-tuple-element.189.q_ref, ...), custom_call_target="tpu_custom_call" | custom-call | flops 6442450944 | bytes 6291456 | tf_op jit(solution)/shard_map/pallas_call | solution.py:679
  258.5 9.6 %shard_map.237 = (f32[1024,768]{1,0:T(8,128)S(1)}, bf16[1024,768]{1,0:T(8,128)(2,1)}, bf16[1024,1536]{1,0:T(8,128)(2,1)}, bf16[1024,1536]{1,0:T(8,128)(2,1)}, bf16[1024,768]{1,0:T(8,128)(2,1)S(1)}) custom-call(f32[1024,768]{1,0:T(8,128)S(1)} %get-tuple-element.188.base.hid, bf16[1024,768]{1,0:T(8,128)(2,1)S(1)} %get-tuple-element.193.own, ...), custom_call_target="tpu_custom_call" | custom-call | flops 4831838208 | bytes 18874368 | tf_op jit(solution)/shard_map/pallas_call | solution.py:742
  269.9 11.3 %shard_map.238 = (bf16[1024,768]{1,0:T(8,128)(2,1)S(1)}, bf16[1024,1536]{1,0:T(8,128)(2,1)S(1)}, bf16[1024,768]{1,0:T(8,128)(2,1)S(1)}, f32[1,768]{1,0:T(1,128)S...) custom-call(bf16[1024,768]{1,0:T(8,128)(2,1)S(1)} %broadcast_select_fusion.refs_0_, ...), custom_call_target="tpu_custom_call" | custom-call | flops 4831838208 | bytes 18874368 | tf_op jit(solution)/shard_map/pallas_call | solution.py:794
  281.7 4.0 convolution_convert_fusion.3.refs_1_
  285.6 4.0 convolution_convert_fusion.2.refs_2_
  293.1 20.5 %shard_map.240 = (f32[1024,768]{1,0:T(8,128)S(1)}, bf16[1024,768]{1,0:T(8,128)(2,1)S(1)}, bf16[1024,384]{1,0:T(8,128)(2,1)S(1)}, bf16[1024,384]{1,0:T(8,128)(2,1...) custom-call(s32[4]{0:T(128)S(1)} %get-tuple-element.362.low_ref, s32[4]{0:T(128)S(1)} %get-tuple-element.357.high_ref, ...), custom_call_target="tpu_custom_call" | custom-call | flops 11274289152 | bytes 15728640 | tf_op jit(solution)/shard_map/pallas_call | solution.py:886
  313.6 8.8 %collective-permute-done.37.refs_2_ = bf16[1536,768]{1,0:T(8,128)(2,1)S(1)} collective-permute-done((bf16[1536,768]{1,0:T(8,128)(2,1)}, bf16[1536,768]{1,0:T(8,128)(2,1)S(1)}, u32[]{:S(2)}, u32[]{:S(2)}) %collective-permute-start.37) | collective-permute-done | bytes 2359328 | tf_op jit(solution)/shard_map/ppermute | solution.py:1081
  325.1 5.7 shard_map.242
  336.4 11.2 %shard_map.243 = (f32[1024,768]{1,0:T(8,128)S(1)}, bf16[1024,768]{1,0:T(8,128)(2,1)S(1)}, bf16[1024,1536]{1,0:T(8,128)(2,1)S(1)}, bf16[1024,768]{1,0:T(8,128)(2,...) custom-call(f32[1024,768]{1,0:T(8,128)S(1)} %get-tuple-element.207.refs_0_, ...), custom_call_target="tpu_custom_call" | custom-call | flops 4831838208 | bytes 18874368 | tf_op jit(solution)/shard_map/pallas_call | solution.py:794
  347.7 7.0 %collective-permute-done.40.refs_1_ = bf16[768,1536]{1,0:T(8,128)(2,1)S(1)} collective-permute-done((bf16[768,1536]{1,0:T(8,128)(2,1)}, bf16[768,1536]{1,0:T(8,128)(2,1)S(1)}, u32[]{:S(2)}, u32[]{:S(2)}) %collective-permute-start.40) | collective-permute-done | bytes 2359328 | tf_op jit(solution)/shard_map/ppermute | solution.py:1081
  359.2 4.0 convolution_convert_fusion.1.refs_1_
  364.7 4.2 convolution_convert_fusion.refs_2_
  368.8 8.3 %collective-permute-done.42.refs_4_ = bf16[384,768]{1,0:T(8,128)(2,1)S(1)} collective-permute-done((bf16[384,768]{1,0:T(8,128)(2,1)S(1)}, bf16[384,768]{1,0:T(8,128)(2,1)S(1)}, u32[]{:S(2)}, u32[]{:S(2)}) %collective-permute-start.42) | collective-permute-done | bytes 589856 | tf_op jit(solution)/shard_map/ppermute | solution.py:1081
  382.9 4.2 shard_map.250.refs_1_
  387.1 4.2 shard_map.251.refs_5_
  394.0 20.4 %shard_map.247 = (f32[1024,768]{1,0:T(8,128)S(1)}, bf16[1024,768]{1,0:T(8,128)(2,1)S(1)}, bf16[1024,384]{1,0:T(8,128)(2,1)S(1)}, bf16[1024,384]{1,0:T(8,128)(2,1...) custom-call(s32[4]{0:T(128)S(1)} %get-tuple-element.362.low_ref, s32[4]{0:T(128)S(1)} %get-tuple-element.357.high_ref, ...), custom_call_target="tpu_custom_call" | custom-call | flops 11274289152 | bytes 15728640 | tf_op jit(solution)/shard_map/pallas_call | solution.py:886
  418.3 6.5 shard_map.253
  442.2 4.5 collective-permute-done.46.refs_1_
  458.8 4.2 shard_map.261.refs_1_
  467.6 4.1 shard_map.262.refs_0_
  474.5 14.3 %collective-permute-done.50.refs_3_ = bf16[384,768]{1,0:T(8,128)(2,1)S(1)} collective-permute-done((bf16[384,768]{1,0:T(8,128)(2,1)S(1)}, bf16[384,768]{1,0:T(8,128)(2,1)S(1)}, u32[]{:S(2)}, u32[]{:S(2)}) %collective-permute-start.50) | collective-permute-done | bytes 589856 | tf_op jit(solution)/shard_map/ppermute | solution.py:1081
  506.9 5.7 collective-permute-done.53.refs_0_
  521.3 3.9 collective-permute-start.59
  527.2 10.2 %shard_map.272.refs_2_ = bf16[3,384,768]{2,1,0:T(8,128)(2,1)S(1)} custom-call(bf16[3072,384]{1,0:T(8,128)(2,1)} %get-tuple-element.285.base, bf16[3,3072,768]{2,1,0:T(8,128)(2,1)} %pinv_ref.9), custom_call_target="tpu_custom_call" | custom-call | flops 5435817984 | bytes 14155776 | tf_op jit(solution)/shard_map/pallas_call | solution.py:470
  548.3 3.9 collective-permute-start.61
  552.2 6.4 collective-permute-done.58.refs_1_
  567.8 3.7 shard_map.279
  571.5 3.9 collective-permute-start.64
  589.2 3.8 collective-permute-done.64.refs_2_
  606.1 3.9 collective-permute-start.69
  638.4 8.7 %shard_map.289 = (f32[32,128,128]{2,1,0:T(8,128)}, f32[32,128,128]{2,1,0:T(8,128)}, f32[32,128,128]{2,1,0:T(8,128)}, f32[32,128,128]{2,1,0:T(8,128)}) custom-call(s32[32]{0:T(128)S(1)} %convert_element_type.148.used, s32[1]{0:T(128)} %bitcast.27.flag.home, bf16[4112,128]{1,0:T(8,128)(2,1)} %shard_map.287.near, ...), custom_call_target="tpu_custom_call" | custom-call | flops 5905580032 | bytes 19922944 | tf_op jit(solution)/shard_map/pallas_call | solution.py:1011
  (498 shorter events, 255.1 us)
Async XLA Ops:
  4.2 26.5 %collective-permute-start.8 = (bf16[4112,128]{1,0:T(8,128)(2,1)}, bf16[4112,128]{1,0:T(8,128)(2,1)}, u32[]{:S(2)}, u32[]{:S(2)}) collective-permute-start(bf16[4112,128]{1,0:T(8,128)(2,1)} %pad_maximum_fusion.2), channel_id=1, source_target_pairs={{0,1},{1,0},{2,3},{3,2},{4,5},{5,4},{6,7},{7,6},{8,9},{9,8},{10,11... | collective-permute-start | bytes 3158024 | tf_op jit(solution)/shard_map/ppermute | solution.py:1081
  7.1 29.1 %collective-permute-start.10 = (bf16[4112,128]{1,0:T(8,128)(2,1)}, bf16[4112,128]{1,0:T(8,128)(2,1)}, u32[]{:S(2)}, u32[]{:S(2)}) collective-permute-start(bf16[4112,128]{1,0:T(8,128)(2,1)} %pad_maximum_fusion.2), channel_id=1, source_target_pairs={{0,4},{1,5},{2,6},{3,7},{4,0},{5,1},{6,2},{7,3},{8,12},{9,13},{10,... | collective-permute-start | bytes 3158024 | tf_op jit(solution)/shard_map/ppermute | solution.py:1081
  8.6 35.8 %collective-permute-start = (bf16[4112,128]{1,0:T(8,128)(2,1)}, bf16[4112,128]{1,0:T(8,128)(2,1)S(1)}, u32[]{:S(2)}, u32[]{:S(2)}) collective-permute-start(bf16[4112,128]{1,0:T(8,128)(2,1)} %pad_maximum_fusion.2), channel_id=1, source_target_pairs={{0,8},{1,9},{2,10},{3,11},{4,12},{5,13},{6,14},{7,15},{8,16},{9,17... | collective-permute-start | bytes 3158024 | tf_op jit(solution)/shard_map/ppermute | solution.py:1081
  11.5 33.0 %collective-permute-start.3 = (s32[1,504]{1,0:T(1,128)S(1)}, s32[1,504]{1,0:T(1,128)S(1)}, u32[]{:S(2)}, u32[]{:S(2)}) collective-permute-start(s32[1,504]{1,0:T(1,128)S(1)} %copy-done.100), channel_id=1, source_target_pairs={{0,1},{1,0},{2,3},{3,2},{4,5},{5,4},{6,7},{7,6},{8,9},{9,8},{10,11... | collective-permute-start | bytes 6056 | tf_op jit(solution)/shard_map/ppermute | solution.py:1081
  12.3 25.1 %collective-permute-start.2 = (bf16[1024,768]{1,0:T(8,128)(2,1)}, bf16[1024,768]{1,0:T(8,128)(2,1)}, u32[]{:S(2)}, u32[]{:S(2)}) collective-permute-start(bf16[1024,768]{1,0:T(8,128)(2,1)} %param.15), channel_id=1, source_target_pairs={{0,2},{3,1},{4,6},{7,5},{8,10},{11,9},{12,14},{15,13},{16,18},{19,... | collective-permute-start | bytes 4718600 | tf_op jit(solution)/shard_map/ppermute | solution.py:1081
  31.8 38.0 %collective-permute-start.12 = (bf16[2064,128]{1,0:T(8,128)(2,1)S(1)}, bf16[2064,128]{1,0:T(8,128)(2,1)S(1)}, u32[]{:S(2)}, u32[]{:S(2)}) collective-permute-start(bf16[2064,128]{1,0:T(8,128)(2,1)S(1)} %slice.149), channel_id=1, source_target_pairs={{0,4},{1,5},{2,6},{3,7},{4,0},{5,1},{6,2},{7,3},{8,12},{9,13},{10,... | collective-permute-start | bytes 1585160 | tf_op jit(solution)/shard_map/ppermute | solution.py:1081
  36.3 134.7 %collective-permute-start.9 = (bf16[4112,128]{1,0:T(8,128)(2,1)S(1)}, bf16[4112,128]{1,0:T(8,128)(2,1)S(1)}, u32[]{:S(2)}, u32[]{:S(2)}) collective-permute-start(bf16[4112,128]{1,0:T(8,128)(2,1)S(1)} %get-tuple-element.344), channel_id=1, source_target_pairs={{0,2},{1,3},{2,0},{3,1},{4,6},{5,7},{6,4},{7,5},{8,10},{9,11},{10,... | collective-permute-start | bytes 3158024 | tf_op jit(solution)/shard_map/ppermute | solution.py:1081
  37.4 29.8 %collective-permute-start.11 = (bf16[2048,128]{1,0:T(8,128)(2,1)S(1)}, bf16[2048,128]{1,0:T(8,128)(2,1)S(1)}, u32[]{:S(2)}, u32[]{:S(2)}) collective-permute-start(bf16[2048,128]{1,0:T(8,128)(2,1)S(1)} %slice.148), channel_id=1, source_target_pairs={{0,1},{1,0},{2,3},{3,2},{4,5},{5,4},{6,7},{7,6},{8,9},{9,8},{10,11... | collective-permute-start | bytes 1572872 | tf_op jit(solution)/shard_map/ppermute | solution.py:1081
  45.5 25.6 %collective-permute-start.16 = (bf16[4112,128]{1,0:T(8,128)(2,1)}, bf16[4112,128]{1,0:T(8,128)(2,1)S(1)}, u32[]{:S(2)}, u32[]{:S(2)}) collective-permute-start(bf16[4112,128]{1,0:T(8,128)(2,1)} %get-tuple-element.166), channel_id=1, source_target_pairs={{0,4},{1,5},{2,6},{3,7},{4,0},{5,1},{6,2},{7,3},{8,12},{9,13},{10,... | collective-permute-start | bytes 3158024 | tf_op jit(solution)/shard_map/ppermute | solution.py:1081
  46.0 28.3 %collective-permute-start.14 = (bf16[4112,128]{1,0:T(8,128)(2,1)}, bf16[4112,128]{1,0:T(8,128)(2,1)S(1)}, u32[]{:S(2)}, u32[]{:S(2)}) collective-permute-start(bf16[4112,128]{1,0:T(8,128)(2,1)} %get-tuple-element.166), channel_id=1, source_target_pairs={{0,1},{1,0},{2,3},{3,2},{4,5},{5,4},{6,7},{7,6},{8,9},{9,8},{10,11... | collective-permute-start | bytes 3158024 | tf_op jit(solution)/shard_map/ppermute | solution.py:1081
  67.2 25.5 %collective-permute-start.5 = (bf16[4112,128]{1,0:T(8,128)(2,1)S(1)}, bf16[4112,128]{1,0:T(8,128)(2,1)S(1)}, u32[]{:S(2)}, u32[]{:S(2)}) collective-permute-start(bf16[4112,128]{1,0:T(8,128)(2,1)S(1)} %copy-done.53), channel_id=1, source_target_pairs={{0,8},{1,9},{2,10},{3,11},{4,12},{5,13},{6,14},{7,15},{8,16},{9,17... | collective-permute-start | bytes 3158024 | tf_op jit(solution)/shard_map/ppermute | solution.py:1081
  70.9 101.1 %collective-permute-start.13 = (bf16[4112,128]{1,0:T(8,128)(2,1)S(1)}, bf16[4112,128]{1,0:T(8,128)(2,1)S(1)}, u32[]{:S(2)}, u32[]{:S(2)}) collective-permute-start(bf16[4112,128]{1,0:T(8,128)(2,1)S(1)} %broadcast_select_fusion.8), channel_id=1, source_target_pairs={{0,2},{1,3},{2,0},{3,1},{4,6},{5,7},{6,4},{7,5},{8,10},{9,11},{10,... | collective-permute-start | bytes 3158024 | tf_op jit(solution)/shard_map/ppermute | solution.py:1081
  71.1 24.4 %collective-permute-start.17 = (bf16[2048,128]{1,0:T(8,128)(2,1)S(1)}, bf16[2048,128]{1,0:T(8,128)(2,1)S(1)}, u32[]{:S(2)}, u32[]{:S(2)}) collective-permute-start(bf16[2048,128]{1,0:T(8,128)(2,1)S(1)} %slice.150), channel_id=1, source_target_pairs={{0,1},{1,0},{2,3},{3,2},{4,5},{5,4},{6,7},{7,6},{8,9},{9,8},{10,11... | collective-permute-start | bytes 1572872 | tf_op jit(solution)/shard_map/ppermute | solution.py:1081
  74.4 23.6 %collective-permute-start.18 = (bf16[2064,128]{1,0:T(8,128)(2,1)S(1)}, bf16[2064,128]{1,0:T(8,128)(2,1)S(1)}, u32[]{:S(2)}, u32[]{:S(2)}) collective-permute-start(bf16[2064,128]{1,0:T(8,128)(2,1)S(1)} %slice.151), channel_id=1, source_target_pairs={{0,4},{1,5},{2,6},{3,7},{4,0},{5,1},{6,2},{7,3},{8,12},{9,13},{10,... | collective-permute-start | bytes 1585160 | tf_op jit(solution)/shard_map/ppermute | solution.py:1081
  93.7 23.1 %collective-permute-start.22 = (bf16[4112,128]{1,0:T(8,128)(2,1)}, bf16[4112,128]{1,0:T(8,128)(2,1)S(1)}, u32[]{:S(2)}, u32[]{:S(2)}) collective-permute-start(bf16[4112,128]{1,0:T(8,128)(2,1)} %get-tuple-element.168), channel_id=1, source_target_pairs={{0,4},{1,5},{2,6},{3,7},{4,0},{5,1},{6,2},{7,3},{8,12},{9,13},{10,... | collective-permute-start | bytes 3158024 | tf_op jit(solution)/shard_map/ppermute | solution.py:1081
  95.5 25.6 %collective-permute-start.20 = (bf16[4112,128]{1,0:T(8,128)(2,1)S(1)}, bf16[4112,128]{1,0:T(8,128)(2,1)S(1)}, u32[]{:S(2)}, u32[]{:S(2)}) collective-permute-start(bf16[4112,128]{1,0:T(8,128)(2,1)S(1)} %copy-done.55), channel_id=1, source_target_pairs={{0,1},{1,0},{2,3},{3,2},{4,5},{5,4},{6,7},{7,6},{8,9},{9,8},{10,11... | collective-permute-start | bytes 3158024 | tf_op jit(solution)/shard_map/ppermute | solution.py:1081
  97.9 25.6 %collective-permute-start.6 = (bf16[4112,128]{1,0:T(8,128)(2,1)S(1)}, bf16[4112,128]{1,0:T(8,128)(2,1)S(1)}, u32[]{:S(2)}, u32[]{:S(2)}) collective-permute-start(bf16[4112,128]{1,0:T(8,128)(2,1)S(1)} %copy-done.55), channel_id=1, source_target_pairs={{0,8},{1,9},{2,10},{3,11},{4,12},{5,13},{6,14},{7,15},{8,16},{9,17... | collective-permute-start | bytes 3158024 | tf_op jit(solution)/shard_map/ppermute | solution.py:1081
  123.5 49.0 %collective-permute-start.15 = (bf16[4112,128]{1,0:T(8,128)(2,1)S(1)}, bf16[4112,128]{1,0:T(8,128)(2,1)S(1)}, u32[]{:S(2)}, u32[]{:S(2)}) collective-permute-start(bf16[4112,128]{1,0:T(8,128)(2,1)S(1)} %broadcast_select_fusion.7), channel_id=1, source_target_pairs={{0,2},{1,3},{2,0},{3,1},{4,6},{5,7},{6,4},{7,5},{8,10},{9,11},{10,... | collective-permute-start | bytes 3158024 | tf_op jit(solution)/shard_map/ppermute | solution.py:1081
  131.4 23.0 %collective-permute-start.26 = (bf16[4112,128]{1,0:T(8,128)(2,1)}, bf16[4112,128]{1,0:T(8,128)(2,1)S(1)}, u32[]{:S(2)}, u32[]{:S(2)}) collective-permute-start(bf16[4112,128]{1,0:T(8,128)(2,1)} %get-tuple-element.170), channel_id=1, source_target_pairs={{0,1},{1,0},{2,3},{3,2},{4,5},{5,4},{6,7},{7,6},{8,9},{9,8},{10,11... | collective-permute-start | bytes 3158024 | tf_op jit(solution)/shard_map/ppermute | solution.py:1081
  133.2 24.3 %collective-permute-start.7 = (bf16[4112,128]{1,0:T(8,128)(2,1)}, bf16[4112,128]{1,0:T(8,128)(2,1)S(1)}, u32[]{:S(2)}, u32[]{:S(2)}) collective-permute-start(bf16[4112,128]{1,0:T(8,128)(2,1)} %get-tuple-element.170), channel_id=1, source_target_pairs={{0,4},{1,5},{2,6},{3,7},{4,0},{5,1},{6,2},{7,3},{8,12},{9,13},{10,... | collective-permute-start | bytes 3158024 | tf_op jit(solution)/shard_map/ppermute | solution.py:1081
  234.0 21.3 %collective-permute-start.4 = (bf16[1024,768]{1,0:T(8,128)(2,1)S(1)}, bf16[1024,768]{1,0:T(8,128)(2,1)S(1)}, u32[]{:S(2)}, u32[]{:S(2)}) collective-permute-start(bf16[1024,768]{1,0:T(8,128)(2,1)S(1)} %copy-done.97), channel_id=1, source_target_pairs={{0,2},{3,1},{4,6},{7,5},{8,10},{11,9},{12,14},{15,13},{16,18},{19,... | collective-permute-start | bytes 4718600 | tf_op jit(solution)/shard_map/ppermute | solution.py:1081
  269.7 19.9 %collective-permute-start.36 = (bf16[1024,768]{1,0:T(8,128)(2,1)S(1)}, bf16[1024,768]{1,0:T(8,128)(2,1)S(1)}, u32[]{:S(2)}, u32[]{:S(2)}) collective-permute-start(bf16[1024,768]{1,0:T(8,128)(2,1)S(1)} %get-tuple-element.205), channel_id=1, source_target_pairs={{0,2},{1,3},{2,0},{3,1},{4,6},{5,7},{6,4},{7,5},{8,10},{9,11},{10,... | collective-permute-start | bytes 4718600 | tf_op jit(solution)/shard_map/ppermute | solution.py:1081
  291.4 30.9 %collective-permute-start.37 = (bf16[1536,768]{1,0:T(8,128)(2,1)}, bf16[1536,768]{1,0:T(8,128)(2,1)S(1)}, u32[]{:S(2)}, u32[]{:S(2)}) collective-permute-start(bf16[1536,768]{1,0:T(8,128)(2,1)} %get-tuple-element.212.own), channel_id=1, source_target_pairs={{1,0},{2,3},{5,4},{6,7},{9,8},{10,11},{13,12},{14,15},{17,16},{18,... | collective-permute-start | bytes 7077896 | tf_op jit(solution)/shard_map/ppermute | solution.py:1081
  323.8 30.9 %collective-permute-start.40 = (bf16[768,1536]{1,0:T(8,128)(2,1)}, bf16[768,1536]{1,0:T(8,128)(2,1)S(1)}, u32[]{:S(2)}, u32[]{:S(2)}) collective-permute-start(bf16[768,1536]{1,0:T(8,128)(2,1)} %get-tuple-element.226.own), channel_id=1, source_target_pairs={{1,0},{2,3},{5,4},{6,7},{9,8},{10,11},{13,12},{14,15},{17,16},{18,... | collective-permute-start | bytes 7077896 | tf_op jit(solution)/shard_map/ppermute | solution.py:1081
  347.5 46.5 %collective-permute-start.39 = (bf16[1024,768]{1,0:T(8,128)(2,1)S(1)}, bf16[1024,768]{1,0:T(8,128)(2,1)S(1)}, u32[]{:S(2)}, u32[]{:S(2)}) collective-permute-start(bf16[1024,768]{1,0:T(8,128)(2,1)S(1)} %get-tuple-element.218.own), channel_id=1, source_target_pairs={{0,2},{1,3},{2,0},{3,1},{4,6},{5,7},{6,4},{7,5},{8,10},{9,11},{10,... | collective-permute-start | bytes 4718600 | tf_op jit(solution)/shard_map/ppermute | solution.py:1081
  378.2 36.3 %collective-permute-start.43 = (bf16[1536,768]{1,0:T(8,128)(2,1)}, bf16[1536,768]{1,0:T(8,128)(2,1)S(1)}, u32[]{:S(2)}, u32[]{:S(2)}) collective-permute-start(bf16[1536,768]{1,0:T(8,128)(2,1)} %get-tuple-element.237.own), channel_id=1, source_target_pairs={{1,0},{2,3},{5,4},{6,7},{9,8},{10,11},{13,12},{14,15},{17,16},{18,... | collective-permute-start | bytes 7077896 | tf_op jit(solution)/shard_map/ppermute | solution.py:1081
  382.1 32.3 %collective-permute-start.44 = (bf16[384,1536]{1,0:T(8,128)(2,1)}, bf16[384,1536]{1,0:T(8,128)(2,1)S(1)}, u32[]{:S(2)}, u32[]{:S(2)}) collective-permute-start(bf16[384,1536]{1,0:T(8,128)(2,1)} %shard_map.248), channel_id=1, source_target_pairs={{1,5},{2,6},{5,1},{6,2},{9,13},{10,14},{13,9},{14,10},{17,21},{18,... | collective-permute-start | bytes 3538952 | tf_op jit(solution)/shard_map/ppermute | solution.py:1081
  447.7 41.8 %collective-permute-start.48 = (bf16[1536,384]{1,0:T(8,128)(2,1)}, bf16[1536,384]{1,0:T(8,128)(2,1)S(1)}, u32[]{:S(2)}, u32[]{:S(2)}) collective-permute-start(bf16[1536,384]{1,0:T(8,128)(2,1)} %get-tuple-element.247.own), channel_id=1, source_target_pairs={{1,5},{2,6},{5,1},{6,2},{9,13},{10,14},{13,9},{14,10},{17,21},{18,... | collective-permute-start | bytes 3538952 | tf_op jit(solution)/shard_map/ppermute | solution.py:1081
  448.5 40.3 %collective-permute-start.52 = (bf16[384,1152]{1,0:T(8,128)(2,1)S(1)}, bf16[384,1152]{1,0:T(8,128)(2,1)S(1)}, u32[]{:S(2)}, u32[]{:S(2)}) collective-permute-start(bf16[384,1152]{1,0:T(8,128)(2,1)S(1)} %copy-done.90), channel_id=1, source_target_pairs={{1,0},{2,3},{5,4},{6,7},{9,8},{10,11},{13,12},{14,15},{17,16},{18,... | collective-permute-start | bytes 2654216 | tf_op jit(solution)/shard_map/ppermute | solution.py:1081
  452.5 37.0 %collective-permute-start.49 = (bf16[384,1152]{1,0:T(8,128)(2,1)}, bf16[384,1152]{1,0:T(8,128)(2,1)S(1)}, u32[]{:S(2)}, u32[]{:S(2)}) collective-permute-start(bf16[384,1152]{1,0:T(8,128)(2,1)} %shard_map.258), channel_id=1, source_target_pairs={{1,0},{2,3},{5,4},{6,7},{9,8},{10,11},{13,12},{14,15},{17,16},{18,... | collective-permute-start | bytes 2654216 | tf_op jit(solution)/shard_map/ppermute | solution.py:1081
  454.7 34.2 %collective-permute-start.50 = (bf16[384,768]{1,0:T(8,128)(2,1)S(1)}, bf16[384,768]{1,0:T(8,128)(2,1)S(1)}, u32[]{:S(2)}, u32[]{:S(2)}) collective-permute-start(bf16[384,768]{1,0:T(8,128)(2,1)S(1)} %convolution_convert_fusion.6.own), channel_id=1, source_target_pairs={{1,0},{2,3},{5,4},{6,7},{9,8},{10,11},{13,12},{14,15},{17,16},{18,... | collective-permute-start | bytes 1769480 | tf_op jit(solution)/shard_map/ppermute | solution.py:1081
  464.2 25.4 %collective-permute-start.51 = (bf16[16,16,128]{2,1,0:T(8,128)(2,1)S(1)}, bf16[16,16,128]{2,1,0:T(8,128)(2,1)S(1)}, u32[]{:S(2)}, u32[]{:S(2)}) collective-permute-start(bf16[16,16,128]{2,1,0:T(8,128)(2,1)S(1)} %convert_element_type.138.own), channel_id=1, source_target_pairs={{1,0},{2,3},{5,4},{6,7},{9,8},{10,11},{13,12},{14,15},{17,16},{18,... | collective-permute-start | bytes 196616 | tf_op jit(solution)/shard_map/ppermute | solution.py:1081
  519.3 19.2 %collective-permute-start.55 = (bf16[4112,128]{1,0:T(8,128)(2,1)S(1)}, bf16[4112,128]{1,0:T(8,128)(2,1)S(1)}, u32[]{:S(2)}, u32[]{:S(2)}) collective-permute-start(bf16[4112,128]{1,0:T(8,128)(2,1)S(1)} %get-tuple-element.343), channel_id=1, source_target_pairs={{0,4},{3,7},{4,0},{7,3},{8,12},{11,15},{12,8},{15,11},{16,20},{19,... | collective-permute-start | bytes 3158024 | tf_op jit(solution)/shard_map/ppermute | solution.py:1081
  521.3 43.5 %collective-permute-start.59 = (bf16[4112,128]{1,0:T(8,128)(2,1)S(1)}, bf16[4112,128]{1,0:T(8,128)(2,1)S(1)}, u32[]{:S(2)}, u32[]{:S(2)}) collective-permute-start(bf16[4112,128]{1,0:T(8,128)(2,1)S(1)} %get-tuple-element.341), channel_id=1, source_target_pairs={{0,4},{3,7},{4,0},{7,3},{8,12},{11,15},{12,8},{15,11},{16,20},{19,... | collective-permute-start | bytes 3158024 | tf_op jit(solution)/shard_map/ppermute | solution.py:1081
  525.2 33.4 %collective-permute-start.58 = (bf16[4112,128]{1,0:T(8,128)(2,1)S(1)}, bf16[4112,128]{1,0:T(8,128)(2,1)S(1)}, u32[]{:S(2)}, u32[]{:S(2)}) collective-permute-start(bf16[4112,128]{1,0:T(8,128)(2,1)S(1)} %get-tuple-element.342), channel_id=1, source_target_pairs={{0,4},{3,7},{4,0},{7,3},{8,12},{11,15},{12,8},{15,11},{16,20},{19,... | collective-permute-start | bytes 3158024 | tf_op jit(solution)/shard_map/ppermute | solution.py:1081
  542.9 23.9 %collective-permute-start.60 = (bf16[4112,128]{1,0:T(8,128)(2,1)}, bf16[4112,128]{1,0:T(8,128)(2,1)S(1)}, u32[]{:S(2)}, u32[]{:S(2)}) collective-permute-start(bf16[4112,128]{1,0:T(8,128)(2,1)} %get-tuple-element.290), channel_id=1, source_target_pairs={{0,8},{3,11},{4,12},{7,15},{8,16},{11,19},{12,20},{15,23},{16,24},... | collective-permute-start | bytes 3158024 | tf_op jit(solution)/shard_map/ppermute | solution.py:1081
  548.2 49.9 %collective-permute-start.56 = (bf16[1024,768]{1,0:T(8,128)(2,1)S(1)}, bf16[1024,768]{1,0:T(8,128)(2,1)S(1)}, u32[]{:S(2)}, u32[]{:S(2)}) collective-permute-start(bf16[1024,768]{1,0:T(8,128)(2,1)S(1)} %add_convert_fusion), channel_id=1, source_target_pairs={{0,2},{1,3},{2,0},{3,1},{4,6},{5,7},{6,4},{7,5},{8,10},{9,11},{10,... | collective-permute-start | bytes 4718600 | tf_op jit(solution)/shard_map/ppermute | solution.py:1081
  548.3 27.2 %collective-permute-start.61 = (bf16[4112,128]{1,0:T(8,128)(2,1)S(1)}, bf16[4112,128]{1,0:T(8,128)(2,1)S(1)}, u32[]{:S(2)}, u32[]{:S(2)}) collective-permute-start(bf16[4112,128]{1,0:T(8,128)(2,1)S(1)} %get-tuple-element.340), channel_id=1, source_target_pairs={{0,4},{3,7},{4,0},{7,3},{8,12},{11,15},{12,8},{15,11},{16,20},{19,... | collective-permute-start | bytes 3158024 | tf_op jit(solution)/shard_map/ppermute | solution.py:1081
  564.9 22.4 %collective-permute-start.63 = (bf16[4112,128]{1,0:T(8,128)(2,1)S(1)}, bf16[4112,128]{1,0:T(8,128)(2,1)S(1)}, u32[]{:S(2)}, u32[]{:S(2)}) collective-permute-start(bf16[4112,128]{1,0:T(8,128)(2,1)S(1)} %copy-done.108), channel_id=1, source_target_pairs={{0,4},{3,7},{4,0},{7,3},{8,12},{11,15},{12,8},{15,11},{16,20},{19,... | collective-permute-start | bytes 3158024 | tf_op jit(solution)/shard_map/ppermute | solution.py:1081
  571.5 21.4 %collective-permute-start.64 = (bf16[4112,128]{1,0:T(8,128)(2,1)}, bf16[4112,128]{1,0:T(8,128)(2,1)S(1)}, u32[]{:S(2)}, u32[]{:S(2)}) collective-permute-start(bf16[4112,128]{1,0:T(8,128)(2,1)} %get-tuple-element.298), channel_id=1, source_target_pairs={{0,8},{3,11},{4,12},{7,15},{8,16},{11,19},{12,20},{15,23},{16,24},... | collective-permute-start | bytes 3158024 | tf_op jit(solution)/shard_map/ppermute | solution.py:1081
  575.5 48.3 %collective-permute-start.54 = (bf16[1024,768]{1,0:T(8,128)(2,1)S(1)}, bf16[1024,768]{1,0:T(8,128)(2,1)}, u32[]{:S(2)}, u32[]{:S(2)}) collective-permute-start(bf16[1024,768]{1,0:T(8,128)(2,1)S(1)} %copy-done.49), channel_id=1, source_target_pairs={{0,1},{3,2},{4,5},{7,6},{8,9},{11,10},{12,13},{15,14},{16,17},{19,... | collective-permute-start | bytes 4718600 | tf_op jit(solution)/shard_map/ppermute | solution.py:1081
  581.7 22.3 %collective-permute-start.65 = (bf16[4112,128]{1,0:T(8,128)(2,1)}, bf16[4112,128]{1,0:T(8,128)(2,1)}, u32[]{:S(2)}, u32[]{:S(2)}) collective-permute-start(bf16[4112,128]{1,0:T(8,128)(2,1)} %get-tuple-element.300), channel_id=1, source_target_pairs={{0,4},{3,7},{4,0},{7,3},{8,12},{11,15},{12,8},{15,11},{16,20},{19,... | collective-permute-start | bytes 3158024 | tf_op jit(solution)/shard_map/ppermute | solution.py:1081
  587.2 18.9 %collective-permute-start.66 = (bf16[4112,128]{1,0:T(8,128)(2,1)}, bf16[4112,128]{1,0:T(8,128)(2,1)}, u32[]{:S(2)}, u32[]{:S(2)}) collective-permute-start(bf16[4112,128]{1,0:T(8,128)(2,1)} %get-tuple-element.303), channel_id=1, source_target_pairs={{0,8},{3,11},{4,12},{7,15},{8,16},{11,19},{12,20},{15,23},{16,24},... | collective-permute-start | bytes 3158024 | tf_op jit(solution)/shard_map/ppermute | solution.py:1081
  592.9 20.3 %collective-permute-start.67 = (bf16[4112,128]{1,0:T(8,128)(2,1)}, bf16[4112,128]{1,0:T(8,128)(2,1)}, u32[]{:S(2)}, u32[]{:S(2)}) collective-permute-start(bf16[4112,128]{1,0:T(8,128)(2,1)} %get-tuple-element.305), channel_id=1, source_target_pairs={{0,4},{3,7},{4,0},{7,3},{8,12},{11,15},{12,8},{15,11},{16,20},{19,... | collective-permute-start | bytes 3158024 | tf_op jit(solution)/shard_map/ppermute | solution.py:1081
  599.3 18.8 %collective-permute-start.68 = (bf16[4112,128]{1,0:T(8,128)(2,1)}, bf16[4112,128]{1,0:T(8,128)(2,1)}, u32[]{:S(2)}, u32[]{:S(2)}) collective-permute-start(bf16[4112,128]{1,0:T(8,128)(2,1)} %shard_map.283), channel_id=1, source_target_pairs={{0,8},{3,11},{4,12},{7,15},{8,16},{11,19},{12,20},{15,23},{16,24},... | collective-permute-start | bytes 3158024 | tf_op jit(solution)/shard_map/ppermute | solution.py:1081
  604.0 21.7 %collective-permute-start.57 = (bf16[1024,384]{1,0:T(8,128)(2,1)}, bf16[1024,384]{1,0:T(8,128)(2,1)}, u32[]{:S(2)}, u32[]{:S(2)}) collective-permute-start(bf16[1024,384]{1,0:T(8,128)(2,1)} %select_convert_fusion), channel_id=1, source_target_pairs={{0,1},{3,2},{4,5},{7,6},{8,9},{11,10},{12,13},{15,14},{16,17},{19,... | collective-permute-start | bytes 2359304 | tf_op jit(solution)/shard_map/ppermute | solution.py:1081
  606.1 22.3 %collective-permute-start.69 = (bf16[4112,128]{1,0:T(8,128)(2,1)}, bf16[4112,128]{1,0:T(8,128)(2,1)}, u32[]{:S(2)}, u32[]{:S(2)}) collective-permute-start(bf16[4112,128]{1,0:T(8,128)(2,1)} %get-tuple-element.309), channel_id=1, source_target_pairs={{0,4},{3,7},{4,0},{7,3},{8,12},{11,15},{12,8},{15,11},{16,20},{19,... | collective-permute-start | bytes 3158024 | tf_op jit(solution)/shard_map/ppermute | solution.py:1081
  613.3 18.8 %collective-permute-start.70 = (bf16[4112,128]{1,0:T(8,128)(2,1)}, bf16[4112,128]{1,0:T(8,128)(2,1)}, u32[]{:S(2)}, u32[]{:S(2)}) collective-permute-start(bf16[4112,128]{1,0:T(8,128)(2,1)} %shard_map.285), channel_id=1, source_target_pairs={{0,8},{3,11},{4,12},{7,15},{8,16},{11,19},{12,20},{15,23},{16,24},... | collective-permute-start | bytes 3158024 | tf_op jit(solution)/shard_map/ppermute | solution.py:1081
  (138 other events, 908.3 us)

commit v11 on v10

--- a/solution.py
+++ b/solution.py
@@ -455,7 +455,7 @@
         ),
         compiler_params=params(),
         cost_estimate=cost(3 * tokens * size * D, tokens * size * 4 + size * D * 6),
-    )(present, half, patches, class_col, stay(pinv))
+    )(present, half, stay(patches), class_col, stay(pinv))
 
 
 def resize_kernel(base, pinv_ref, out, turned):
@@ -1146,8 +1146,8 @@
     class_col = jnp.sum(jnp.where(select, jnp.arange(1, 4)[None, :], 0), axis=1, keepdims=True) - 1
     present = jnp.any(select.reshape(blocks_n, ROWS, 3), axis=1).astype(jnp.int32)
 
-    def expand(which):
-        return expand_call(which, present, half_at, patches, class_col, pinv)
+    def expand(which, rows):
+        return expand_call(which, present, half_at, rows, class_col, pinv)
 
     vec_low = jnp.pad(vec_master[0].astype(bf16), (0, VEC_ROWS * BS - vec_per))
     own_pack = jnp.concatenate(
@@ -1167,14 +1167,11 @@
             beside_x, beside_y = send(pack, routes.x_all), send(pack, routes.y_all)
             if j < 3:
                 further = send(pack, routes.z_all)
-                work = [expand(j)] + ([slot_other] if j == 0 else [])
-                further, chunk, *work = fence(further, *work)
-                chunks.append(chunk)
-                if j == 0:
-                    [slot_other] = work
-            else:
-                beside_x, chunk = fence(beside_x, expand(j))
-                chunks.append(chunk)
+            work = [expand(j, patches)] + ([slot_other] if j == 0 else [])
+            beside_x, patches, chunk, *work = fence(beside_x, patches, *work)
+            chunks.append(chunk)
+            if j == 0:
+                [slot_other] = work
             corner = jnp.concatenate(
                 [send(beside_x[:middle_row], routes.y_all), send(beside_y[middle_row:], routes.x_all)],
                 axis=0,
@@ -1197,7 +1194,7 @@
         first = [jnp.where(core == 0, everything[:, 0], everything[:, 1])]
         second = []
         owner = jnp.arange(dp_n, dtype=jnp.int32)
-        chunks = [expand(c) for c in range(CHUNKS)]
+        chunks = [expand(c, patches) for c in range(CHUNKS)]
     slot_list = jnp.where(home, block_slot, slot_other)[0]
     named = slot_list[None, :] == jnp.arange(slots_n)[:, None]
     used = jnp.any(named, axis=1)
@@ -1335,7 +1332,7 @@
         return jnp.concatenate([dot_tn(c, grad_emb).astype(bf16) for c in parts], axis=0)
 
     gbt = base_grad(chunks[middle:])
-    gbt, au0, xq0 = hold(gbt, au0, xq0)
+    gbt, au0, xq0, aq1 = hold(gbt, au0, xq0, aq1)
     xb = send(gbt, routes.x_away) if grid3 else None
     aq0 = over(summed(gq0, xq0))
     gbm = base_grad(chunks[:middle])
@@ -1343,12 +1340,12 @@
     go0 = dot_tn(caches[low][5], grad_low).astype(bf16)
     ao0, av = over(go0), over(vec_grad)
     buffer = place_tiles(("out", top), go1, ao1, buffer)
+    buffer = place_tiles(("qkv", top), gq1, aq1, buffer)
     buffer = place_tiles(("down", low), gd0, ad0, buffer)
     buffer = place_tiles(("up", low), gu0, au0, buffer)
     buffer = place_base(1, gbt, None, buffer)
-    gbm, xb, aq0, ao0, av, aq1, buffer = hold(gbm, xb, aq0, ao0, av, aq1, buffer)
+    gbm, xb, aq0, ao0, av, buffer = hold(gbm, xb, aq0, ao0, av, buffer)
     ab = over(half_sum(half_at * 0, gbm, xb)) if grid3 else None
-    buffer = place_tiles(("qkv", top), gq1, aq1, buffer)
     buffer = place_tiles(("out", low), go0, ao0, buffer)
     buffer = scatter_vec(vec_pos, vec_grad, av, buffer)
     buffer = place_tiles(("qkv", low), gq0, aq0, buffer)

time: 659 us -> 667 us (1.012)
  Pallas kernels: 278 us -> 288 us
    unnamed x234 -> x232, local copies, waits for them, and re-layouts: 30.1 us -> 30.1 us
  transfers between devices with their start and end apart: 72 -> 72, of which waited for: 31 -> 27; matrix products, arithmetic and copies ran while one was open for 9% -> 10% of each run, Pallas kernels for 31% -> 31%
where the time goes in v11:
time: 667 us; the launch traced here: 656 us
  Pallas kernels  288 us (43%)
  waiting for transfers between devices  166 us (25%)
  starting transfers between devices  97.6 us (15%)
  local copies, waits for them, and re-layouts  41.4 us (6%)
  matrix products  32.5 us (5%)
  other arithmetic  28.6 us (4%)
    ppermute x72, waiting for transfers between devices, send(): return lax.ppermute(value, AXES, route)  166 us
    ppermute x72, starting transfers between devices, send(): return lax.ppermute(value, AXES, route)  97.6 us
    pallas_call x2, Pallas kernels, attend_back_call(): pl.pallas_call(attend_back_kernel, out_shape=[shape(D, f32), shape(D, bf1...  45.6 us
    pallas_call x10, Pallas kernels, scatter_matrix(): pl.pallas_call(functools.partial(scatter_kernel, rows_n, cols_n, steps, p...  35.3 us
    unnamed x232, local copies, waits for them, and re-layouts  30.1 us
    pallas_call x2, Pallas kernels, attend_call(): pl.pallas_call(functools.partial(attend_kernel, layer), out_shape=[jax.Sh...  29.7 us
    dot_general x12, matrix products, dot_tn(): lax.dot_general(left, right, (((0,), (0,)), ((), ())), preferred_element_...  29.4 us
    pallas_call x8, Pallas kernels, reduce_call(): pl.pallas_call(functools.partial(reduce_kernel, carried is not None, last...  27.1 us
  transfers between devices with their start and end apart: 72, of which 27 were waited for; matrix products, arithmetic and copies ran while one was open for 10% of the time, Pallas kernels for 31%

profile of v11, /device:TPU:0, one launch (start us, length us, event | category | flops | bytes accessed | tf_op | source)
XLA Modules:
  0.0 656.5 jit_solution(5749094924232944785)
XLA Ops:
  15.7 15.0 %collective-permute-done.11 = bf16[4112,128]{1,0:T(8,128)(2,1)} collective-permute-done((bf16[4112,128]{1,0:T(8,128)(2,1)}, bf16[4112,128]{1,0:T(8,128)(2,1)}, u32[]{:S(2)}, u32[]{:S(2)}) %collective-permute-start.11) | collective-permute-done | bytes 1052704 | tf_op jit(solution)/shard_map/ppermute | solution.py:1081
  36.3 6.0 shard_map.222.refs_2_
  51.4 6.4 shard_map.224.refs_2_
  61.6 19.0 %collective-permute-done.16 = bf16[4112,128]{1,0:T(8,128)(2,1)S(1)} collective-permute-done((bf16[4112,128]{1,0:T(8,128)(2,1)}, bf16[4112,128]{1,0:T(8,128)(2,1)S(1)}, u32[]{:S(2)}, u32[]{:S(2)}) %collective-permute-start.16) | collective-permute-done | bytes 1052704 | tf_op jit(solution)/shard_map/ppermute | solution.py:1081
  81.0 4.7 collective-permute-done.6.refs_0_
  91.3 6.0 shard_map.226.refs_2_
  97.3 5.4 collective-permute-done.18
  107.6 11.3 %collective-permute-done.21 = bf16[4112,128]{1,0:T(8,128)(2,1)S(1)} collective-permute-done((bf16[4112,128]{1,0:T(8,128)(2,1)S(1)}, bf16[4112,128]{1,0:T(8,128)(2,1)S(1)}, u32[]{:S(2)}, u32[]{:S(2)}) %collective-permute-start.21) | collective-permute-done | bytes 1052704 | tf_op jit(solution)/shard_map/ppermute | solution.py:1081
  128.6 6.1 shard_map.228.refs_2_
  139.6 20.9 %collective-permute-done.26 = bf16[4112,128]{1,0:T(8,128)(2,1)S(1)} collective-permute-done((bf16[4112,128]{1,0:T(8,128)(2,1)S(1)}, bf16[4112,128]{1,0:T(8,128)(2,1)S(1)}, u32[]{:S(2)}, u32[]{:S(2)}) %collective-permute-start.26) | collective-permute-done | bytes 1052704 | tf_op jit(solution)/shard_map/ppermute | solution.py:1081
  165.7 11.3 %collective-permute-done.28 = bf16[2048,128]{1,0:T(8,128)(2,1)S(1)} collective-permute-done((bf16[2048,128]{1,0:T(8,128)(2,1)S(1)}, bf16[2048,128]{1,0:T(8,128)(2,1)S(1)}, u32[]{:S(2)}, u32[]{:S(2)}) %collective-permute-start.28) | collective-permute-done | bytes 524320 | tf_op jit(solution)/shard_map/ppermute | solution.py:1081
  186.0 14.1 %shard_map.230 = (bf16[3072,384]{1,0:T(8,128)(2,1)}, bf16[2304,384]{1,0:T(8,128)(2,1)}, bf16[768,384]{1,0:T(8,128)(2,1)}, bf16[3072,384]{1,0:T(8,128)(2,1)}, bf1...) custom-call(s32[16]{0:T(128)S(1)} %stack.95.owner, ...), custom_call_target="tpu_custom_call" | custom-call | bytes 33030144 | tf_op jit(solution)/shard_map/pallas_call | solution.py:243
  200.2 6.8 %shard_map.231.refs_0_ = bf16[1024,384]{1,0:T(8,128)(2,1)S(1)} custom-call(s32[1]{0:T(128)} %bitcast.6.half.part, bf16[1024,768]{1,0:T(8,128)(2,1)} %get-tuple-element.168.refs_0_, bf16[1024,768]{1,0:T(8,128)(2,1)} %get-tuple-element.170.refs_1_, bf16[1024,768]{1,0:T(8,128)(2,1)} %get-tuple-element.172.refs_2_, ...), custom_call_target="tpu_custom_call" | custom-call | flops 2415919104 | bytes 9437184 | tf_op jit(solution)/shard_map/pallas_call | solution.py:552
  209.6 4.8 shard_map.232
  214.5 14.8 %shard_map.233 = (bf16[1024,384]{1,0:T(8,128)(2,1)S(1)}, f32[8,1024]{1,0:T(8,128)S(1)}, bf16[1024,768]{1,0:T(8,128)(2,1)S(1)}) custom-call(s32[4]{0:T(128)S(1)} %get-tuple-element.369.low_ref, s32[4]{0:T(128)S(1)} %get-tuple-element.362.high_ref, bf16[1024,384]{1,0:T(8,128)(2,1)S(1)} %get-tuple-element.184.q_ref, ...), custom_call_target="tpu_custom_call" | custom-call | flops 6442450944 | bytes 6291456 | tf_op jit(solution)/shard_map/pallas_call | solution.py:679
  233.7 9.6 %shard_map.234 = (f32[1024,768]{1,0:T(8,128)S(1)}, bf16[1024,768]{1,0:T(8,128)(2,1)}, bf16[1024,1536]{1,0:T(8,128)(2,1)}, bf16[1024,1536]{1,0:T(8,128)(2,1)}, bf16[1024,768]{1,0:T(8,128)(2,1)S(1)}) custom-call(f32[1024,768]{1,0:T(8,128)S(1)} %get-tuple-element.183.base.hid, bf16[1024,768]{1,0:T(8,128)(2,1)S(1)} %get-tuple-element.188.own, ...), custom_call_target="tpu_custom_call" | custom-call | flops 4831838208 | bytes 18874368 | tf_op jit(solution)/shard_map/pallas_call | solution.py:742
  246.7 4.4 shard_map.235
  251.1 14.9 %shard_map.236 = (bf16[1024,384]{1,0:T(8,128)(2,1)S(1)}, f32[8,1024]{1,0:T(8,128)S(1)}, bf16[1024,768]{1,0:T(8,128)(2,1)S(1)}) custom-call(s32[4]{0:T(128)S(1)} %get-tuple-element.369.low_ref, s32[4]{0:T(128)S(1)} %get-tuple-element.362.high_ref, bf16[1024,384]{1,0:T(8,128)(2,1)S(1)} %get-tuple-element.195.q_ref, ...), custom_call_target="tpu_custom_call" | custom-call | flops 6442450944 | bytes 6291456 | tf_op jit(solution)/shard_map/pallas_call | solution.py:679
  269.5 9.6 %shard_map.237 = (f32[1024,768]{1,0:T(8,128)S(1)}, bf16[1024,768]{1,0:T(8,128)(2,1)}, bf16[1024,1536]{1,0:T(8,128)(2,1)}, bf16[1024,1536]{1,0:T(8,128)(2,1)}, bf16[1024,768]{1,0:T(8,128)(2,1)S(1)}) custom-call(f32[1024,768]{1,0:T(8,128)S(1)} %get-tuple-element.194.base.hid, bf16[1024,768]{1,0:T(8,128)(2,1)S(1)} %get-tuple-element.199.own, ...), custom_call_target="tpu_custom_call" | custom-call | flops 4831838208 | bytes 18874368 | tf_op jit(solution)/shard_map/pallas_call | solution.py:742
  280.9 11.3 %shard_map.238 = (bf16[1024,768]{1,0:T(8,128)(2,1)S(1)}, bf16[1024,1536]{1,0:T(8,128)(2,1)S(1)}, bf16[1024,768]{1,0:T(8,128)(2,1)S(1)}, f32[1,768]{1,0:T(1,128)S...) custom-call(bf16[1024,768]{1,0:T(8,128)(2,1)S(1)} %broadcast_select_fusion.refs_0_, ...), custom_call_target="tpu_custom_call" | custom-call | flops 4831838208 | bytes 18874368 | tf_op jit(solution)/shard_map/pallas_call | solution.py:794
  292.7 4.0 convolution_convert_fusion.3.refs_1_
  296.7 4.0 convolution_convert_fusion.2.refs_2_
  304.2 22.8 %shard_map.240 = (f32[1024,768]{1,0:T(8,128)S(1)}, bf16[1024,768]{1,0:T(8,128)(2,1)S(1)}, bf16[1024,384]{1,0:T(8,128)(2,1)S(1)}, bf16[1024,384]{1,0:T(8,128)(2,1...) custom-call(s32[4]{0:T(128)S(1)} %get-tuple-element.368.low_ref, s32[4]{0:T(128)S(1)} %get-tuple-element.363.high_ref, ...), custom_call_target="tpu_custom_call" | custom-call | flops 11274289152 | bytes 15728640 | tf_op jit(solution)/shard_map/pallas_call | solution.py:886
  327.0 6.4 collective-permute-done.37.refs_2_
  336.1 5.7 shard_map.242
  343.8 3.5 convolution_convert_fusion.5.refs_3_
  347.3 11.2 %shard_map.243 = (f32[1024,768]{1,0:T(8,128)S(1)}, bf16[1024,768]{1,0:T(8,128)(2,1)S(1)}, bf16[1024,1536]{1,0:T(8,128)(2,1)S(1)}, bf16[1024,768]{1,0:T(8,128)(2,...) custom-call(f32[1024,768]{1,0:T(8,128)S(1)} %get-tuple-element.213.refs_0_, ...), custom_call_target="tpu_custom_call" | custom-call | flops 4831838208 | bytes 18874368 | tf_op jit(solution)/shard_map/pallas_call | solution.py:794
  358.8 7.0 %collective-permute-done.40.refs_1_ = bf16[768,1536]{1,0:T(8,128)(2,1)S(1)} collective-permute-done((bf16[768,1536]{1,0:T(8,128)(2,1)}, bf16[768,1536]{1,0:T(8,128)(2,1)S(1)}, u32[]{:S(2)}, u32[]{:S(2)}) %collective-permute-start.40) | collective-permute-done | bytes 2359328 | tf_op jit(solution)/shard_map/ppermute | solution.py:1081
  370.3 4.0 convolution_convert_fusion.1.refs_1_
  375.7 4.0 convolution_convert_fusion.refs_2_
  379.8 6.3 collective-permute-done.42.refs_4_
  391.8 4.2 shard_map.250.refs_1_
  396.1 4.3 shard_map.251.refs_5_
  403.0 22.8 %shard_map.247 = (f32[1024,768]{1,0:T(8,128)S(1)}, bf16[1024,768]{1,0:T(8,128)(2,1)S(1)}, bf16[1024,384]{1,0:T(8,128)(2,1)S(1)}, bf16[1024,384]{1,0:T(8,128)(2,1...) custom-call(s32[4]{0:T(128)S(1)} %get-tuple-element.368.low_ref, s32[4]{0:T(128)S(1)} %get-tuple-element.363.high_ref, ...), custom_call_target="tpu_custom_call" | custom-call | flops 11274289152 | bytes 15728640 | tf_op jit(solution)/shard_map/pallas_call | solution.py:886
  429.7 6.5 shard_map.253
  455.0 12.1 %collective-permute-done.48.refs_3_ = bf16[384,1152]{1,0:T(8,128)(2,1)S(1)} collective-permute-done((bf16[384,1152]{1,0:T(8,128)(2,1)S(1)}, bf16[384,1152]{1,0:T(8,128)(2,1)S(1)}, u32[]{:S(2)}, u32[]{:S(2)}) %collective-permute-start.48) | collective-permute-done | bytes 884768 | tf_op jit(solution)/shard_map/ppermute | solution.py:1081
  483.4 3.6 shard_map.261.refs_1_
  487.0 4.2 shard_map.262.refs_1_
  491.2 4.0 shard_map.263.refs_0_
  508.5 3.5 shard_map.269.refs_1_
  512.0 9.4 %collective-permute-done.53.refs_0_ = bf16[1536,384]{1,0:T(8,128)(2,1)S(1)} collective-permute-done((bf16[1536,384]{1,0:T(8,128)(2,1)}, bf16[1536,384]{1,0:T(8,128)(2,1)S(1)}, u32[]{:S(2)}, u32[]{:S(2)}) %collective-permute-start.53) | collective-permute-done | bytes 1179680 | tf_op jit(solution)/shard_map/ppermute | solution.py:1081
  536.6 10.2 %shard_map.272.refs_2_ = bf16[3,384,768]{2,1,0:T(8,128)(2,1)S(1)} custom-call(bf16[3072,384]{1,0:T(8,128)(2,1)} %get-tuple-element.291.base, bf16[3,3072,768]{2,1,0:T(8,128)(2,1)} %pinv_ref.9), custom_call_target="tpu_custom_call" | custom-call | flops 5435817984 | bytes 14155776 | tf_op jit(solution)/shard_map/pallas_call | solution.py:470
  561.7 5.7 collective-permute-done.58.refs_1_
  577.8 3.7 shard_map.279
  586.1 4.3 collective-permute-done.62.refs_2_
  593.0 3.6 shard_map.281
  624.0 3.5 collective-permute-done.68.refs_2_
  647.3 8.7 %shard_map.289 = (f32[32,128,128]{2,1,0:T(8,128)}, f32[32,128,128]{2,1,0:T(8,128)}, f32[32,128,128]{2,1,0:T(8,128)}, f32[32,128,128]{2,1,0:T(8,128)}) custom-call(s32[32]{0:T(128)S(1)} %convert_element_type.148.used, s32[1]{0:T(128)} %bitcast.27.flag.home, bf16[4112,128]{1,0:T(8,128)(2,1)} %shard_map.287.near, ...), custom_call_target="tpu_custom_call" | custom-call | flops 5905580032 | bytes 19922944 | tf_op jit(solution)/shard_map/pallas_call | solution.py:1011
  (496 shorter events, 257.9 us)
Async XLA Ops:
  4.2 26.5 %collective-permute-start.11 = (bf16[4112,128]{1,0:T(8,128)(2,1)}, bf16[4112,128]{1,0:T(8,128)(2,1)}, u32[]{:S(2)}, u32[]{:S(2)}) collective-permute-start(bf16[4112,128]{1,0:T(8,128)(2,1)} %pad_maximum_fusion.2), channel_id=1, source_target_pairs={{0,1},{1,0},{2,3},{3,2},{4,5},{5,4},{6,7},{7,6},{8,9},{9,8},{10,11... | collective-permute-start | bytes 3158024 | tf_op jit(solution)/shard_map/ppermute | solution.py:1081
  7.2 42.6 %collective-permute-start.5 = (bf16[4112,128]{1,0:T(8,128)(2,1)}, bf16[4112,128]{1,0:T(8,128)(2,1)}, u32[]{:S(2)}, u32[]{:S(2)}) collective-permute-start(bf16[4112,128]{1,0:T(8,128)(2,1)} %pad_maximum_fusion.2), channel_id=1, source_target_pairs={{0,8},{1,9},{2,10},{3,11},{4,12},{5,13},{6,14},{7,15},{8,16},{9,17... | collective-permute-start | bytes 3158024 | tf_op jit(solution)/shard_map/ppermute | solution.py:1081
  8.7 34.7 %collective-permute-start = (bf16[4112,128]{1,0:T(8,128)(2,1)}, bf16[4112,128]{1,0:T(8,128)(2,1)S(1)}, u32[]{:S(2)}, u32[]{:S(2)}) collective-permute-start(bf16[4112,128]{1,0:T(8,128)(2,1)} %pad_maximum_fusion.2), channel_id=1, source_target_pairs={{0,4},{1,5},{2,6},{3,7},{4,0},{5,1},{6,2},{7,3},{8,12},{9,13},{10,... | collective-permute-start | bytes 3158024 | tf_op jit(solution)/shard_map/ppermute | solution.py:1081
  11.5 22.1 %collective-permute-start.1 = (bf16[1024,768]{1,0:T(8,128)(2,1)}, bf16[1024,768]{1,0:T(8,128)(2,1)}, u32[]{:S(2)}, u32[]{:S(2)}) collective-permute-start(bf16[1024,768]{1,0:T(8,128)(2,1)} %param.15), channel_id=1, source_target_pairs={{0,2},{3,1},{4,6},{7,5},{8,10},{11,9},{12,14},{15,13},{16,18},{19,... | collective-permute-start | bytes 4718600 | tf_op jit(solution)/shard_map/ppermute | solution.py:1081
  14.0 29.5 %collective-permute-start.3 = (s32[1,504]{1,0:T(1,128)S(1)}, s32[1,504]{1,0:T(1,128)S(1)}, u32[]{:S(2)}, u32[]{:S(2)}) collective-permute-start(s32[1,504]{1,0:T(1,128)S(1)} %copy-done.99), channel_id=1, source_target_pairs={{0,1},{1,0},{2,3},{3,2},{4,5},{5,4},{6,7},{7,6},{8,9},{9,8},{10,11... | collective-permute-start | bytes 6056 | tf_op jit(solution)/shard_map/ppermute | solution.py:1081
  31.8 28.7 %collective-permute-start.14 = (bf16[2064,128]{1,0:T(8,128)(2,1)S(1)}, bf16[2064,128]{1,0:T(8,128)(2,1)S(1)}, u32[]{:S(2)}, u32[]{:S(2)}) collective-permute-start(bf16[2064,128]{1,0:T(8,128)(2,1)S(1)} %slice.148), channel_id=1, source_target_pairs={{0,4},{1,5},{2,6},{3,7},{4,0},{5,1},{6,2},{7,3},{8,12},{9,13},{10,... | collective-permute-start | bytes 1585160 | tf_op jit(solution)/shard_map/ppermute | solution.py:1081
  49.7 129.3 %collective-permute-start.12 = (bf16[4112,128]{1,0:T(8,128)(2,1)S(1)}, bf16[4112,128]{1,0:T(8,128)(2,1)S(1)}, u32[]{:S(2)}, u32[]{:S(2)}) collective-permute-start(bf16[4112,128]{1,0:T(8,128)(2,1)S(1)} %get-tuple-element.350), channel_id=1, source_target_pairs={{0,2},{1,3},{2,0},{3,1},{4,6},{5,7},{6,4},{7,5},{8,10},{9,11},{10,... | collective-permute-start | bytes 3158024 | tf_op jit(solution)/shard_map/ppermute | solution.py:1081
  49.7 30.9 %collective-permute-start.16 = (bf16[4112,128]{1,0:T(8,128)(2,1)}, bf16[4112,128]{1,0:T(8,128)(2,1)S(1)}, u32[]{:S(2)}, u32[]{:S(2)}) collective-permute-start(bf16[4112,128]{1,0:T(8,128)(2,1)} %collective-permute-done.5), channel_id=1, source_target_pairs={{0,1},{1,0},{2,3},{3,2},{4,5},{5,4},{6,7},{7,6},{8,9},{9,8},{10,11... | collective-permute-start | bytes 3158024 | tf_op jit(solution)/shard_map/ppermute | solution.py:1081
  49.7 40.2 %collective-permute-start.7 = (bf16[4112,128]{1,0:T(8,128)(2,1)}, bf16[4112,128]{1,0:T(8,128)(2,1)S(1)}, u32[]{:S(2)}, u32[]{:S(2)}) collective-permute-start(bf16[4112,128]{1,0:T(8,128)(2,1)} %collective-permute-done.5), channel_id=1, source_target_pairs={{0,8},{1,9},{2,10},{3,11},{4,12},{5,13},{6,14},{7,15},{8,16},{9,17... | collective-permute-start | bytes 3158024 | tf_op jit(solution)/shard_map/ppermute | solution.py:1081
  60.4 25.3 %collective-permute-start.6 = (bf16[4112,128]{1,0:T(8,128)(2,1)}, bf16[4112,128]{1,0:T(8,128)(2,1)S(1)}, u32[]{:S(2)}, u32[]{:S(2)}) collective-permute-start(bf16[4112,128]{1,0:T(8,128)(2,1)} %collective-permute-done.5), channel_id=1, source_target_pairs={{0,4},{1,5},{2,6},{3,7},{4,0},{5,1},{6,2},{7,3},{8,12},{9,13},{10,... | collective-permute-start | bytes 3158024 | tf_op jit(solution)/shard_map/ppermute | solution.py:1081
  61.6 118.4 %collective-permute-start.15 = (bf16[4112,128]{1,0:T(8,128)(2,1)S(1)}, bf16[4112,128]{1,0:T(8,128)(2,1)}, u32[]{:S(2)}, u32[]{:S(2)}) collective-permute-start(bf16[4112,128]{1,0:T(8,128)(2,1)S(1)} %broadcast_select_fusion.8), channel_id=1, source_target_pairs={{0,2},{1,3},{2,0},{3,1},{4,6},{5,7},{6,4},{7,5},{8,10},{9,11},{10,... | collective-permute-start | bytes 3158024 | tf_op jit(solution)/shard_map/ppermute | solution.py:1081
  80.7 23.6 %collective-permute-start.19 = (bf16[2064,128]{1,0:T(8,128)(2,1)S(1)}, bf16[2064,128]{1,0:T(8,128)(2,1)S(1)}, u32[]{:S(2)}, u32[]{:S(2)}) collective-permute-start(bf16[2064,128]{1,0:T(8,128)(2,1)S(1)} %slice.149), channel_id=1, source_target_pairs={{0,4},{1,5},{2,6},{3,7},{4,0},{5,1},{6,2},{7,3},{8,12},{9,13},{10,... | collective-permute-start | bytes 1585160 | tf_op jit(solution)/shard_map/ppermute | solution.py:1081
  89.9 28.9 %collective-permute-start.21 = (bf16[4112,128]{1,0:T(8,128)(2,1)S(1)}, bf16[4112,128]{1,0:T(8,128)(2,1)S(1)}, u32[]{:S(2)}, u32[]{:S(2)}) collective-permute-start(bf16[4112,128]{1,0:T(8,128)(2,1)S(1)} %collective-permute-done.7), channel_id=1, source_target_pairs={{0,1},{1,0},{2,3},{3,2},{4,5},{5,4},{6,7},{7,6},{8,9},{9,8},{10,11... | collective-permute-start | bytes 3158024 | tf_op jit(solution)/shard_map/ppermute | solution.py:1081
  102.7 32.1 %collective-permute-start.9 = (bf16[4112,128]{1,0:T(8,128)(2,1)S(1)}, bf16[4112,128]{1,0:T(8,128)(2,1)S(1)}, u32[]{:S(2)}, u32[]{:S(2)}) collective-permute-start(bf16[4112,128]{1,0:T(8,128)(2,1)S(1)} %collective-permute-done.7), channel_id=1, source_target_pairs={{0,8},{1,9},{2,10},{3,11},{4,12},{5,13},{6,14},{7,15},{8,16},{9,17... | collective-permute-start | bytes 3158024 | tf_op jit(solution)/shard_map/ppermute | solution.py:1081
  104.3 18.6 %collective-permute-start.8 = (bf16[4112,128]{1,0:T(8,128)(2,1)S(1)}, bf16[4112,128]{1,0:T(8,128)(2,1)S(1)}, u32[]{:S(2)}, u32[]{:S(2)}) collective-permute-start(bf16[4112,128]{1,0:T(8,128)(2,1)S(1)} %collective-permute-done.7), channel_id=1, source_target_pairs={{0,4},{1,5},{2,6},{3,7},{4,0},{5,1},{6,2},{7,3},{8,12},{9,13},{10,... | collective-permute-start | bytes 3158024 | tf_op jit(solution)/shard_map/ppermute | solution.py:1081
  134.8 45.7 %collective-permute-start.17 = (bf16[4112,128]{1,0:T(8,128)(2,1)S(1)}, bf16[4112,128]{1,0:T(8,128)(2,1)S(1)}, u32[]{:S(2)}, u32[]{:S(2)}) collective-permute-start(bf16[4112,128]{1,0:T(8,128)(2,1)S(1)} %broadcast_select_fusion.7), channel_id=1, source_target_pairs={{0,2},{1,3},{2,0},{3,1},{4,6},{5,7},{6,4},{7,5},{8,10},{9,11},{10,... | collective-permute-start | bytes 3158024 | tf_op jit(solution)/shard_map/ppermute | solution.py:1081
  134.9 25.7 %collective-permute-start.26 = (bf16[4112,128]{1,0:T(8,128)(2,1)S(1)}, bf16[4112,128]{1,0:T(8,128)(2,1)S(1)}, u32[]{:S(2)}, u32[]{:S(2)}) collective-permute-start(bf16[4112,128]{1,0:T(8,128)(2,1)S(1)} %collective-permute-done.9), channel_id=1, source_target_pairs={{0,1},{1,0},{2,3},{3,2},{4,5},{5,4},{6,7},{7,6},{8,9},{9,8},{10,11... | collective-permute-start | bytes 3158024 | tf_op jit(solution)/shard_map/ppermute | solution.py:1081
  136.7 25.1 %collective-permute-start.10 = (bf16[4112,128]{1,0:T(8,128)(2,1)S(1)}, bf16[4112,128]{1,0:T(8,128)(2,1)S(1)}, u32[]{:S(2)}, u32[]{:S(2)}) collective-permute-start(bf16[4112,128]{1,0:T(8,128)(2,1)S(1)} %collective-permute-done.9), channel_id=1, source_target_pairs={{0,4},{1,5},{2,6},{3,7},{4,0},{5,1},{6,2},{7,3},{8,12},{9,13},{10,... | collective-permute-start | bytes 3158024 | tf_op jit(solution)/shard_map/ppermute | solution.py:1081
  243.4 22.9 %collective-permute-start.4 = (bf16[1024,768]{1,0:T(8,128)(2,1)S(1)}, bf16[1024,768]{1,0:T(8,128)(2,1)S(1)}, u32[]{:S(2)}, u32[]{:S(2)}) collective-permute-start(bf16[1024,768]{1,0:T(8,128)(2,1)S(1)} %copy-done.96), channel_id=1, source_target_pairs={{0,2},{3,1},{4,6},{7,5},{8,10},{11,9},{12,14},{15,13},{16,18},{19,... | collective-permute-start | bytes 4718600 | tf_op jit(solution)/shard_map/ppermute | solution.py:1081
  280.8 19.9 %collective-permute-start.36 = (bf16[1024,768]{1,0:T(8,128)(2,1)S(1)}, bf16[1024,768]{1,0:T(8,128)(2,1)S(1)}, u32[]{:S(2)}, u32[]{:S(2)}) collective-permute-start(bf16[1024,768]{1,0:T(8,128)(2,1)S(1)} %get-tuple-element.211), channel_id=1, source_target_pairs={{0,2},{1,3},{2,0},{3,1},{4,6},{5,7},{6,4},{7,5},{8,10},{9,11},{10,... | collective-permute-start | bytes 4718600 | tf_op jit(solution)/shard_map/ppermute | solution.py:1081
  302.5 30.9 %collective-permute-start.37 = (bf16[1536,768]{1,0:T(8,128)(2,1)}, bf16[1536,768]{1,0:T(8,128)(2,1)S(1)}, u32[]{:S(2)}, u32[]{:S(2)}) collective-permute-start(bf16[1536,768]{1,0:T(8,128)(2,1)} %get-tuple-element.218.own), channel_id=1, source_target_pairs={{1,0},{2,3},{5,4},{6,7},{9,8},{10,11},{13,12},{14,15},{17,16},{18,... | collective-permute-start | bytes 7077896 | tf_op jit(solution)/shard_map/ppermute | solution.py:1081
  334.8 30.9 %collective-permute-start.40 = (bf16[768,1536]{1,0:T(8,128)(2,1)}, bf16[768,1536]{1,0:T(8,128)(2,1)S(1)}, u32[]{:S(2)}, u32[]{:S(2)}) collective-permute-start(bf16[768,1536]{1,0:T(8,128)(2,1)} %get-tuple-element.232.own), channel_id=1, source_target_pairs={{1,0},{2,3},{5,4},{6,7},{9,8},{10,11},{13,12},{14,15},{17,16},{18,... | collective-permute-start | bytes 7077896 | tf_op jit(solution)/shard_map/ppermute | solution.py:1081
  358.4 44.5 %collective-permute-start.39 = (bf16[1024,768]{1,0:T(8,128)(2,1)S(1)}, bf16[1024,768]{1,0:T(8,128)(2,1)S(1)}, u32[]{:S(2)}, u32[]{:S(2)}) collective-permute-start(bf16[1024,768]{1,0:T(8,128)(2,1)S(1)} %get-tuple-element.224.own), channel_id=1, source_target_pairs={{0,2},{1,3},{2,0},{3,1},{4,6},{5,7},{6,4},{7,5},{8,10},{9,11},{10,... | collective-permute-start | bytes 4718600 | tf_op jit(solution)/shard_map/ppermute | solution.py:1081
  387.1 38.7 %collective-permute-start.43 = (bf16[1536,768]{1,0:T(8,128)(2,1)}, bf16[1536,768]{1,0:T(8,128)(2,1)S(1)}, u32[]{:S(2)}, u32[]{:S(2)}) collective-permute-start(bf16[1536,768]{1,0:T(8,128)(2,1)} %get-tuple-element.243.own), channel_id=1, source_target_pairs={{1,0},{2,3},{5,4},{6,7},{9,8},{10,11},{13,12},{14,15},{17,16},{18,... | collective-permute-start | bytes 7077896 | tf_op jit(solution)/shard_map/ppermute | solution.py:1081
  391.0 34.8 %collective-permute-start.44 = (bf16[384,1536]{1,0:T(8,128)(2,1)}, bf16[384,1536]{1,0:T(8,128)(2,1)S(1)}, u32[]{:S(2)}, u32[]{:S(2)}) collective-permute-start(bf16[384,1536]{1,0:T(8,128)(2,1)} %shard_map.248), channel_id=1, source_target_pairs={{1,5},{2,6},{5,1},{6,2},{9,13},{10,14},{13,9},{14,10},{17,21},{18,... | collective-permute-start | bytes 3538952 | tf_op jit(solution)/shard_map/ppermute | solution.py:1081
  439.4 27.8 %collective-permute-start.46 = (bf16[384,1536]{1,0:T(8,128)(2,1)}, bf16[384,1536]{1,0:T(8,128)(2,1)S(1)}, u32[]{:S(2)}, u32[]{:S(2)}) collective-permute-start(bf16[384,1536]{1,0:T(8,128)(2,1)} %shard_map.255), channel_id=1, source_target_pairs={{1,0},{2,3},{5,4},{6,7},{9,8},{10,11},{13,12},{14,15},{17,16},{18,... | collective-permute-start | bytes 3538952 | tf_op jit(solution)/shard_map/ppermute | solution.py:1081
  447.1 20.0 %collective-permute-start.48 = (bf16[384,1152]{1,0:T(8,128)(2,1)S(1)}, bf16[384,1152]{1,0:T(8,128)(2,1)S(1)}, u32[]{:S(2)}, u32[]{:S(2)}) collective-permute-start(bf16[384,1152]{1,0:T(8,128)(2,1)S(1)} %copy-done.89), channel_id=1, source_target_pairs={{1,0},{2,3},{5,4},{6,7},{9,8},{10,11},{13,12},{14,15},{17,16},{18,... | collective-permute-start | bytes 2654216 | tf_op jit(solution)/shard_map/ppermute | solution.py:1081
  469.1 29.1 %collective-permute-start.49 = (bf16[1536,384]{1,0:T(8,128)(2,1)}, bf16[1536,384]{1,0:T(8,128)(2,1)S(1)}, u32[]{:S(2)}, u32[]{:S(2)}) collective-permute-start(bf16[1536,384]{1,0:T(8,128)(2,1)} %get-tuple-element.254.own), channel_id=1, source_target_pairs={{1,5},{2,6},{5,1},{6,2},{9,13},{10,14},{13,9},{14,10},{17,21},{18,... | collective-permute-start | bytes 3538952 | tf_op jit(solution)/shard_map/ppermute | solution.py:1081
  472.6 25.5 %collective-permute-start.50 = (bf16[384,1152]{1,0:T(8,128)(2,1)}, bf16[384,1152]{1,0:T(8,128)(2,1)S(1)}, u32[]{:S(2)}, u32[]{:S(2)}) collective-permute-start(bf16[384,1152]{1,0:T(8,128)(2,1)} %shard_map.258), channel_id=1, source_target_pairs={{1,0},{2,3},{5,4},{6,7},{9,8},{10,11},{13,12},{14,15},{17,16},{18,... | collective-permute-start | bytes 2654216 | tf_op jit(solution)/shard_map/ppermute | solution.py:1081
  474.8 23.3 %collective-permute-start.51 = (bf16[384,768]{1,0:T(8,128)(2,1)S(1)}, bf16[384,768]{1,0:T(8,128)(2,1)S(1)}, u32[]{:S(2)}, u32[]{:S(2)}) collective-permute-start(bf16[384,768]{1,0:T(8,128)(2,1)S(1)} %convolution_convert_fusion.6.own), channel_id=1, source_target_pairs={{1,0},{2,3},{5,4},{6,7},{9,8},{10,11},{13,12},{14,15},{17,16},{18,... | collective-permute-start | bytes 1769480 | tf_op jit(solution)/shard_map/ppermute | solution.py:1081
  503.1 18.3 %collective-permute-start.53 = (bf16[1536,384]{1,0:T(8,128)(2,1)}, bf16[1536,384]{1,0:T(8,128)(2,1)S(1)}, u32[]{:S(2)}, u32[]{:S(2)}) collective-permute-start(bf16[1536,384]{1,0:T(8,128)(2,1)} %shard_map.266), channel_id=1, source_target_pairs={{1,0},{2,3},{5,4},{6,7},{9,8},{10,11},{13,12},{14,15},{17,16},{18,... | collective-permute-start | bytes 3538952 | tf_op jit(solution)/shard_map/ppermute | solution.py:1081
  528.1 19.9 %collective-permute-start.55 = (bf16[4112,128]{1,0:T(8,128)(2,1)S(1)}, bf16[4112,128]{1,0:T(8,128)(2,1)S(1)}, u32[]{:S(2)}, u32[]{:S(2)}) collective-permute-start(bf16[4112,128]{1,0:T(8,128)(2,1)S(1)} %get-tuple-element.349), channel_id=1, source_target_pairs={{0,4},{3,7},{4,0},{7,3},{8,12},{11,15},{12,8},{15,11},{16,20},{19,... | collective-permute-start | bytes 3158024 | tf_op jit(solution)/shard_map/ppermute | solution.py:1081
  530.7 43.6 %collective-permute-start.59 = (bf16[4112,128]{1,0:T(8,128)(2,1)S(1)}, bf16[4112,128]{1,0:T(8,128)(2,1)S(1)}, u32[]{:S(2)}, u32[]{:S(2)}) collective-permute-start(bf16[4112,128]{1,0:T(8,128)(2,1)S(1)} %get-tuple-element.347), channel_id=1, source_target_pairs={{0,4},{3,7},{4,0},{7,3},{8,12},{11,15},{12,8},{15,11},{16,20},{19,... | collective-permute-start | bytes 3158024 | tf_op jit(solution)/shard_map/ppermute | solution.py:1081
  534.0 33.4 %collective-permute-start.58 = (bf16[4112,128]{1,0:T(8,128)(2,1)S(1)}, bf16[4112,128]{1,0:T(8,128)(2,1)S(1)}, u32[]{:S(2)}, u32[]{:S(2)}) collective-permute-start(bf16[4112,128]{1,0:T(8,128)(2,1)S(1)} %get-tuple-element.348), channel_id=1, source_target_pairs={{0,4},{3,7},{4,0},{7,3},{8,12},{11,15},{12,8},{15,11},{16,20},{19,... | collective-permute-start | bytes 3158024 | tf_op jit(solution)/shard_map/ppermute | solution.py:1081
  552.3 24.5 %collective-permute-start.60 = (bf16[4112,128]{1,0:T(8,128)(2,1)}, bf16[4112,128]{1,0:T(8,128)(2,1)S(1)}, u32[]{:S(2)}, u32[]{:S(2)}) collective-permute-start(bf16[4112,128]{1,0:T(8,128)(2,1)} %get-tuple-element.296), channel_id=1, source_target_pairs={{0,8},{3,11},{4,12},{7,15},{8,16},{11,19},{12,20},{15,23},{16,24},... | collective-permute-start | bytes 3158024 | tf_op jit(solution)/shard_map/ppermute | solution.py:1081
  558.2 49.3 %collective-permute-start.56 = (bf16[1024,768]{1,0:T(8,128)(2,1)S(1)}, bf16[1024,768]{1,0:T(8,128)(2,1)S(1)}, u32[]{:S(2)}, u32[]{:S(2)}) collective-permute-start(bf16[1024,768]{1,0:T(8,128)(2,1)S(1)} %add_convert_fusion), channel_id=1, source_target_pairs={{0,2},{1,3},{2,0},{3,1},{4,6},{5,7},{6,4},{7,5},{8,10},{9,11},{10,... | collective-permute-start | bytes 4718600 | tf_op jit(solution)/shard_map/ppermute | solution.py:1081
  558.3 25.3 %collective-permute-start.61 = (bf16[4112,128]{1,0:T(8,128)(2,1)S(1)}, bf16[4112,128]{1,0:T(8,128)(2,1)S(1)}, u32[]{:S(2)}, u32[]{:S(2)}) collective-permute-start(bf16[4112,128]{1,0:T(8,128)(2,1)S(1)} %get-tuple-element.346), channel_id=1, source_target_pairs={{0,4},{3,7},{4,0},{7,3},{8,12},{11,15},{12,8},{15,11},{16,20},{19,... | collective-permute-start | bytes 3158024 | tf_op jit(solution)/shard_map/ppermute | solution.py:1081
  571.7 18.7 %collective-permute-start.62 = (bf16[4112,128]{1,0:T(8,128)(2,1)}, bf16[4112,128]{1,0:T(8,128)(2,1)S(1)}, u32[]{:S(2)}, u32[]{:S(2)}) collective-permute-start(bf16[4112,128]{1,0:T(8,128)(2,1)} %get-tuple-element.299), channel_id=1, source_target_pairs={{0,8},{3,11},{4,12},{7,15},{8,16},{11,19},{12,20},{15,23},{16,24},... | collective-permute-start | bytes 3158024 | tf_op jit(solution)/shard_map/ppermute | solution.py:1081
  574.4 22.2 %collective-permute-start.63 = (bf16[4112,128]{1,0:T(8,128)(2,1)S(1)}, bf16[4112,128]{1,0:T(8,128)(2,1)S(1)}, u32[]{:S(2)}, u32[]{:S(2)}) collective-permute-start(bf16[4112,128]{1,0:T(8,128)(2,1)S(1)} %copy-done.107), channel_id=1, source_target_pairs={{0,4},{3,7},{4,0},{7,3},{8,12},{11,15},{12,8},{15,11},{16,20},{19,... | collective-permute-start | bytes 3158024 | tf_op jit(solution)/shard_map/ppermute | solution.py:1081
  581.5 20.2 %collective-permute-start.64 = (bf16[4112,128]{1,0:T(8,128)(2,1)}, bf16[4112,128]{1,0:T(8,128)(2,1)S(1)}, u32[]{:S(2)}, u32[]{:S(2)}) collective-permute-start(bf16[4112,128]{1,0:T(8,128)(2,1)} %get-tuple-element.304), channel_id=1, source_target_pairs={{0,8},{3,11},{4,12},{7,15},{8,16},{11,19},{12,20},{15,23},{16,24},... | collective-permute-start | bytes 3158024 | tf_op jit(solution)/shard_map/ppermute | solution.py:1081
  583.6 49.6 %collective-permute-start.54 = (bf16[1024,768]{1,0:T(8,128)(2,1)S(1)}, bf16[1024,768]{1,0:T(8,128)(2,1)}, u32[]{:S(2)}, u32[]{:S(2)}) collective-permute-start(bf16[1024,768]{1,0:T(8,128)(2,1)S(1)} %copy-done.49), channel_id=1, source_target_pairs={{0,1},{3,2},{4,5},{7,6},{8,9},{11,10},{12,13},{15,14},{16,17},{19,... | collective-permute-start | bytes 4718600 | tf_op jit(solution)/shard_map/ppermute | solution.py:1081
  590.4 22.9 %collective-permute-start.65 = (bf16[4112,128]{1,0:T(8,128)(2,1)}, bf16[4112,128]{1,0:T(8,128)(2,1)}, u32[]{:S(2)}, u32[]{:S(2)}) collective-permute-start(bf16[4112,128]{1,0:T(8,128)(2,1)} %get-tuple-element.306), channel_id=1, source_target_pairs={{0,4},{3,7},{4,0},{7,3},{8,12},{11,15},{12,8},{15,11},{16,20},{19,... | collective-permute-start | bytes 3158024 | tf_op jit(solution)/shard_map/ppermute | solution.py:1081
  596.6 19.0 %collective-permute-start.66 = (bf16[4112,128]{1,0:T(8,128)(2,1)}, bf16[4112,128]{1,0:T(8,128)(2,1)}, u32[]{:S(2)}, u32[]{:S(2)}) collective-permute-start(bf16[4112,128]{1,0:T(8,128)(2,1)} %get-tuple-element.309), channel_id=1, source_target_pairs={{0,8},{3,11},{4,12},{7,15},{8,16},{11,19},{12,20},{15,23},{16,24},... | collective-permute-start | bytes 3158024 | tf_op jit(solution)/shard_map/ppermute | solution.py:1081
  601.7 20.4 %collective-permute-start.67 = (bf16[4112,128]{1,0:T(8,128)(2,1)}, bf16[4112,128]{1,0:T(8,128)(2,1)}, u32[]{:S(2)}, u32[]{:S(2)}) collective-permute-start(bf16[4112,128]{1,0:T(8,128)(2,1)} %get-tuple-element.311), channel_id=1, source_target_pairs={{0,4},{3,7},{4,0},{7,3},{8,12},{11,15},{12,8},{15,11},{16,20},{19,... | collective-permute-start | bytes 3158024 | tf_op jit(solution)/shard_map/ppermute | solution.py:1081
  608.7 18.8 %collective-permute-start.68 = (bf16[4112,128]{1,0:T(8,128)(2,1)}, bf16[4112,128]{1,0:T(8,128)(2,1)}, u32[]{:S(2)}, u32[]{:S(2)}) collective-permute-start(bf16[4112,128]{1,0:T(8,128)(2,1)} %shard_map.283), channel_id=1, source_target_pairs={{0,8},{3,11},{4,12},{7,15},{8,16},{11,19},{12,20},{15,23},{16,24},... | collective-permute-start | bytes 3158024 | tf_op jit(solution)/shard_map/ppermute | solution.py:1081
  613.4 21.7 %collective-permute-start.57 = (bf16[1024,384]{1,0:T(8,128)(2,1)}, bf16[1024,384]{1,0:T(8,128)(2,1)}, u32[]{:S(2)}, u32[]{:S(2)}) collective-permute-start(bf16[1024,384]{1,0:T(8,128)(2,1)} %select_convert_fusion), channel_id=1, source_target_pairs={{0,1},{3,2},{4,5},{7,6},{8,9},{11,10},{12,13},{15,14},{16,17},{19,... | collective-permute-start | bytes 2359304 | tf_op jit(solution)/shard_map/ppermute | solution.py:1081
  615.6 22.3 %collective-permute-start.69 = (bf16[4112,128]{1,0:T(8,128)(2,1)}, bf16[4112,128]{1,0:T(8,128)(2,1)}, u32[]{:S(2)}, u32[]{:S(2)}) collective-permute-start(bf16[4112,128]{1,0:T(8,128)(2,1)} %get-tuple-element.315), channel_id=1, source_target_pairs={{0,4},{3,7},{4,0},{7,3},{8,12},{11,15},{12,8},{15,11},{16,20},{19,... | collective-permute-start | bytes 3158024 | tf_op jit(solution)/shard_map/ppermute | solution.py:1081
  622.1 18.8 %collective-permute-start.70 = (bf16[4112,128]{1,0:T(8,128)(2,1)}, bf16[4112,128]{1,0:T(8,128)(2,1)}, u32[]{:S(2)}, u32[]{:S(2)}) collective-permute-start(bf16[4112,128]{1,0:T(8,128)(2,1)} %shard_map.285), channel_id=1, source_target_pairs={{0,8},{3,11},{4,12},{7,15},{8,16},{11,19},{12,20},{15,23},{16,24},... | collective-permute-start | bytes 3158024 | tf_op jit(solution)/shard_map/ppermute | solution.py:1081
  (137 other events, 958.9 us)

commit v12 on v10

--- a/solution.py
+++ b/solution.py
@@ -1297,10 +1297,10 @@
     other = send(part, routes.core_all)
     gd1 = dot_tn(caches[top][9], grad_low).astype(bf16)
     gu1 = dot_tn(caches[top][8], du).astype(bf16)
-    lse, gd1, gu1, out_low = fence(caches[top][6], gd1, gu1, out_low)
     ad1 = over(gd1)
+    lse, gu1 = fence(caches[top][6], gu1)
     grad, grad_low, dq, dk, dv, dbo = attend_step(top, grad, part, other, lse)
-    vec, dbo, ad1, gu1 = hold(vec, dbo, ad1, gu1)
+    vec, dbo, ad1, gu1, out_low = hold(vec, dbo, ad1, gu1, out_low)
     au1 = over(gu1)
     own, dg1, ds1, dbq, dbv = qkv_back_call(top, dq, dk, dv, caches[top][0], vec, weights)
     recv = send(own, routes.core_all)
@@ -1309,18 +1309,18 @@
     vec_grads[top] = [dg1, ds1, dbq, dbv, dbo, dg2, ds2, db1, db2]
     grad, grad_low, du, part, dg2, ds2, db1, db2 = mlp_step(low, grad, own, recv)
     other = send(part, routes.core_all)
-    db2, au1, go1, gq1 = hold(db2, au1, go1, gq1)
+    db2, go1, gq1 = hold(db2, go1, gq1)
     xq1, ao1 = beside(gq1), over(go1)
     gd0 = dot_tn(caches[low][9], grad_low).astype(bf16)
     gu0 = dot_tn(caches[low][8], du).astype(bf16)
-    lse, gd0, gu0, xq1, ao1 = hold(caches[low][6], gd0, gu0, xq1, ao1)
+    lse, gd0, gu0, xq1, au1 = hold(caches[low][6], gd0, gu0, xq1, au1)
     hq1 = summed(gq1, xq1)
     ad0 = over(gd0)
     xu0 = beside(gu0)
     buffer = place_tiles(("down", top), gd1, ad1, None)
     buffer = place_tiles(("up", top), gu1, au1, buffer)
     grad, grad_low, dq, dk, dv, dbo = attend_step(low, grad, part, other, lse)
-    vec, dbo, ad0, xu0, hq1, buffer = hold(vec, dbo, ad0, xu0, hq1, buffer)
+    vec, dbo, ad0, ao1, xu0, hq1, buffer = hold(vec, dbo, ad0, ao1, xu0, hq1, buffer)
     au0 = over(summed(gu0, xu0))
     aq1 = over(hq1)
     own, dg1, ds1, dbq, dbv = qkv_back_call(low, dq, dk, dv, caches[low][0], vec, weights)

time: 659 us -> 645 us (0.979)
  waiting for transfers between devices: 168 us -> 154 us
    ppermute x72, waiting for transfers between devices: 168 us -> 154 us  [send(): return lax.ppermute(value, AXES, route)]
    unnamed x234 -> x238, local copies, waits for them, and re-layouts: 30.1 us -> 29.2 us
  transfers between devices with their start and end apart: 72 -> 72, of which waited for: 31 -> 29; matrix products, arithmetic and copies ran while one was open for 9% -> 9% of each run, Pallas kernels for 31% -> 30%
where the time goes in v12:
time: 645 us; the launch traced here: 635 us
  Pallas kernels  277 us (43%)
  waiting for transfers between devices  154 us (24%)
  starting transfers between devices  105 us (16%)
  local copies, waits for them, and re-layouts  38.4 us (6%)
  matrix products  31.5 us (5%)
  other arithmetic  26.2 us (4%)
    ppermute x72, waiting for transfers between devices, send(): return lax.ppermute(value, AXES, route)  154 us
    ppermute x72, starting transfers between devices, send(): return lax.ppermute(value, AXES, route)  105 us
    pallas_call x2, Pallas kernels, attend_back_call(): pl.pallas_call(attend_back_kernel, out_shape=[shape(D, f32), shape(D, bf1...  40.8 us
    pallas_call x10, Pallas kernels, scatter_matrix(): pl.pallas_call(functools.partial(scatter_kernel, rows_n, cols_n, steps, p...  35.3 us
    unnamed x238, local copies, waits for them, and re-layouts  29.2 us
    dot_general x12, matrix products, dot_tn(): lax.dot_general(left, right, (((0,), (0,)), ((), ())), preferred_element_...  28.4 us
    pallas_call x8, Pallas kernels, reduce_call(): pl.pallas_call(functools.partial(reduce_kernel, carried is not None, last...  27.1 us
    pallas_call x2, Pallas kernels, attend_call(): pl.pallas_call(functools.partial(attend_kernel, layer), out_shape=[jax.Sh...  26.4 us
  transfers between devices with their start and end apart: 72, of which 29 were waited for; matrix products, arithmetic and copies ran while one was open for 9% of the time, Pallas kernels for 30%

profile of v12, /device:TPU:0, one launch (start us, length us, event | category | flops | bytes accessed | tf_op | source)
XLA Modules:
  0.0 635.2 jit_solution(11431724254014452975)
XLA Ops:
  12.3 3.7 collective-permute-start.2
  17.6 13.1 %collective-permute-done.8 = bf16[4112,128]{1,0:T(8,128)(2,1)} collective-permute-done((bf16[4112,128]{1,0:T(8,128)(2,1)}, bf16[4112,128]{1,0:T(8,128)(2,1)}, u32[]{:S(2)}, u32[]{:S(2)}) %collective-permute-start.8) | collective-permute-done | bytes 1052704 | tf_op jit(solution)/shard_map/ppermute | solution.py:1081
  37.8 5.5 shard_map.222.refs_1_
  49.0 6.0 shard_map.228.refs_1_
  55.0 5.5 shard_map.226.refs_1_
  61.7 5.5 shard_map.224.refs_1_
  67.2 3.6 collective-permute-start.5
  74.7 18.7 %collective-permute-done.5.refs_0_ = bf16[4112,128]{1,0:T(8,128)(2,1)S(1)} collective-permute-done((bf16[4112,128]{1,0:T(8,128)(2,1)S(1)}, bf16[4112,128]{1,0:T(8,128)(2,1)S(1)}, u32[]{:S(2)}, u32[]{:S(2)}) %collective-permute-start.5) | collective-permute-done | bytes 1052704 | tf_op jit(solution)/shard_map/ppermute | solution.py:1081
  98.7 19.3 %collective-permute-done.22 = bf16[4112,128]{1,0:T(8,128)(2,1)S(1)} collective-permute-done((bf16[4112,128]{1,0:T(8,128)(2,1)}, bf16[4112,128]{1,0:T(8,128)(2,1)S(1)}, u32[]{:S(2)}, u32[]{:S(2)}) %collective-permute-start.22) | collective-permute-done | bytes 1052704 | tf_op jit(solution)/shard_map/ppermute | solution.py:1081
  125.0 7.6 %collective-permute-done.23 = bf16[2048,128]{1,0:T(8,128)(2,1)S(1)} collective-permute-done((bf16[2048,128]{1,0:T(8,128)(2,1)S(1)}, bf16[2048,128]{1,0:T(8,128)(2,1)S(1)}, u32[]{:S(2)}, u32[]{:S(2)}) %collective-permute-start.23) | collective-permute-done | bytes 524320 | tf_op jit(solution)/shard_map/ppermute | solution.py:1081
  136.0 20.4 %collective-permute-done.26 = bf16[4112,128]{1,0:T(8,128)(2,1)S(1)} collective-permute-done((bf16[4112,128]{1,0:T(8,128)(2,1)}, bf16[4112,128]{1,0:T(8,128)(2,1)S(1)}, u32[]{:S(2)}, u32[]{:S(2)}) %collective-permute-start.26) | collective-permute-done | bytes 1052704 | tf_op jit(solution)/shard_map/ppermute | solution.py:1081
  163.3 7.3 %collective-permute-done.28 = bf16[2048,128]{1,0:T(8,128)(2,1)S(1)} collective-permute-done((bf16[2048,128]{1,0:T(8,128)(2,1)S(1)}, bf16[2048,128]{1,0:T(8,128)(2,1)S(1)}, u32[]{:S(2)}, u32[]{:S(2)}) %collective-permute-start.28) | collective-permute-done | bytes 524320 | tf_op jit(solution)/shard_map/ppermute | solution.py:1081
  179.7 14.1 %shard_map.230 = (bf16[3072,384]{1,0:T(8,128)(2,1)}, bf16[2304,384]{1,0:T(8,128)(2,1)}, bf16[768,384]{1,0:T(8,128)(2,1)}, bf16[3072,384]{1,0:T(8,128)(2,1)}, bf1...) custom-call(s32[16]{0:T(128)S(1)} %stack.95.owner, ...), custom_call_target="tpu_custom_call" | custom-call | bytes 33030144 | tf_op jit(solution)/shard_map/pallas_call | solution.py:243
  194.0 6.8 %shard_map.231.refs_0_ = bf16[1024,384]{1,0:T(8,128)(2,1)S(1)} custom-call(s32[1]{0:T(128)} %bitcast.6.half.part, bf16[1024,768]{1,0:T(8,128)(2,1)} %get-tuple-element.164.refs_0_, bf16[1024,768]{1,0:T(8,128)(2,1)} %get-tuple-element.166.refs_1_, bf16[1024,768]{1,0:T(8,128)(2,1)} %get-tuple-element.168.refs_2_, ...), custom_call_target="tpu_custom_call" | custom-call | flops 2415919104 | bytes 9437184 | tf_op jit(solution)/shard_map/pallas_call | solution.py:552
  203.3 4.9 shard_map.232
  208.2 13.2 %shard_map.233 = (bf16[1024,384]{1,0:T(8,128)(2,1)S(1)}, f32[8,1024]{1,0:T(8,128)S(1)}, bf16[1024,768]{1,0:T(8,128)(2,1)S(1)}) custom-call(s32[4]{0:T(128)S(1)} %get-tuple-element.361.low_ref, s32[4]{0:T(128)S(1)} %get-tuple-element.354.high_ref, bf16[1024,384]{1,0:T(8,128)(2,1)S(1)} %get-tuple-element.177.q_ref, ...), custom_call_target="tpu_custom_call" | custom-call | flops 6442450944 | bytes 6291456 | tf_op jit(solution)/shard_map/pallas_call | solution.py:679
  225.9 9.6 %shard_map.234 = (f32[1024,768]{1,0:T(8,128)S(1)}, bf16[1024,768]{1,0:T(8,128)(2,1)}, bf16[1024,1536]{1,0:T(8,128)(2,1)}, bf16[1024,1536]{1,0:T(8,128)(2,1)}, bf16[1024,768]{1,0:T(8,128)(2,1)S(1)}) custom-call(f32[1024,768]{1,0:T(8,128)S(1)} %get-tuple-element.176.base.hid, bf16[1024,768]{1,0:T(8,128)(2,1)S(1)} %get-tuple-element.181.own, ...), custom_call_target="tpu_custom_call" | custom-call | flops 4831838208 | bytes 18874368 | tf_op jit(solution)/shard_map/pallas_call | solution.py:742
  238.9 4.5 shard_map.235
  243.3 13.2 %shard_map.236 = (bf16[1024,384]{1,0:T(8,128)(2,1)S(1)}, f32[8,1024]{1,0:T(8,128)S(1)}, bf16[1024,768]{1,0:T(8,128)(2,1)S(1)}) custom-call(s32[4]{0:T(128)S(1)} %get-tuple-element.361.low_ref, s32[4]{0:T(128)S(1)} %get-tuple-element.354.high_ref, bf16[1024,384]{1,0:T(8,128)(2,1)S(1)} %get-tuple-element.188.q_ref, ...), custom_call_target="tpu_custom_call" | custom-call | flops 6442450944 | bytes 6291456 | tf_op jit(solution)/shard_map/pallas_call | solution.py:679
  260.1 9.5 %shard_map.237 = (f32[1024,768]{1,0:T(8,128)S(1)}, bf16[1024,768]{1,0:T(8,128)(2,1)}, bf16[1024,1536]{1,0:T(8,128)(2,1)}, bf16[1024,1536]{1,0:T(8,128)(2,1)}, bf16[1024,768]{1,0:T(8,128)(2,1)S(1)}) custom-call(f32[1024,768]{1,0:T(8,128)S(1)} %get-tuple-element.187.base.hid, bf16[1024,768]{1,0:T(8,128)(2,1)S(1)} %get-tuple-element.192.own, ...), custom_call_target="tpu_custom_call" | custom-call | flops 4831838208 | bytes 18874368 | tf_op jit(solution)/shard_map/pallas_call | solution.py:742
  271.5 11.3 %shard_map.238 = (bf16[1024,768]{1,0:T(8,128)(2,1)S(1)}, bf16[1024,1536]{1,0:T(8,128)(2,1)S(1)}, bf16[1024,768]{1,0:T(8,128)(2,1)S(1)}, f32[1,768]{1,0:T(1,128)S...) custom-call(bf16[1024,768]{1,0:T(8,128)(2,1)S(1)} %broadcast_select_fusion.refs_0_, ...), custom_call_target="tpu_custom_call" | custom-call | flops 4831838208 | bytes 18874368 | tf_op jit(solution)/shard_map/pallas_call | solution.py:794
  287.9 4.0 convolution_convert_fusion.3.refs_1_
  293.8 20.4 %shard_map.240 = (f32[1024,768]{1,0:T(8,128)S(1)}, bf16[1024,768]{1,0:T(8,128)(2,1)S(1)}, bf16[1024,384]{1,0:T(8,128)(2,1)S(1)}, bf16[1024,384]{1,0:T(8,128)(2,1...) custom-call(s32[4]{0:T(128)S(1)} %get-tuple-element.360.low_ref, s32[4]{0:T(128)S(1)} %get-tuple-element.355.high_ref, ...), custom_call_target="tpu_custom_call" | custom-call | flops 11274289152 | bytes 15728640 | tf_op jit(solution)/shard_map/pallas_call | solution.py:886
  314.2 4.8 collective-permute-done.36.refs_2_
  320.5 5.7 shard_map.242
  329.8 3.5 convolution_convert_fusion.5.refs_2_
  333.3 11.2 %shard_map.243 = (f32[1024,768]{1,0:T(8,128)S(1)}, bf16[1024,768]{1,0:T(8,128)(2,1)S(1)}, bf16[1024,1536]{1,0:T(8,128)(2,1)S(1)}, bf16[1024,768]{1,0:T(8,128)(2,...) custom-call(f32[1024,768]{1,0:T(8,128)S(1)} %get-tuple-element.204.refs_0_, ...), custom_call_target="tpu_custom_call" | custom-call | flops 4831838208 | bytes 18874368 | tf_op jit(solution)/shard_map/pallas_call | solution.py:794
  347.8 6.1 collective-permute-start.39
  353.9 3.9 convolution_convert_fusion.1.refs_1_
  357.8 4.0 convolution_convert_fusion.refs_2_
  368.2 4.2 shard_map.250.refs_1_
  376.4 4.2 shard_map.251.refs_6_
  380.7 20.4 %shard_map.247 = (f32[1024,768]{1,0:T(8,128)S(1)}, bf16[1024,768]{1,0:T(8,128)(2,1)S(1)}, bf16[1024,384]{1,0:T(8,128)(2,1)S(1)}, bf16[1024,384]{1,0:T(8,128)(2,1...) custom-call(s32[4]{0:T(128)S(1)} %get-tuple-element.360.low_ref, s32[4]{0:T(128)S(1)} %get-tuple-element.355.high_ref, ...), custom_call_target="tpu_custom_call" | custom-call | flops 11274289152 | bytes 15728640 | tf_op jit(solution)/shard_map/pallas_call | solution.py:886
  405.3 6.5 %shard_map.253 = (bf16[1024,768]{1,0:T(8,128)(2,1)}, f32[1,768]{1,0:T(1,128)S(1)}, f32[1,768]{1,0:T(1,128)S(1)}, f32[1,384]{1,0:T(1,128)S(1)}, f32[1,384]{1,0:T(1,128)S(1)}) custom-call(bf16[1024,384]{1,0:T(8,128)(2,1)S(1)} %get-tuple-element.230.dq, bf16[1024,384]{1,0:T(8,128)(2,1)S(1)} %get-tuple-element.231.dk, ...), custom_call_target="tpu_custom_call" | custom-call | flops 1811939328 | bytes 7864320 | tf_op jit(solution)/shard_map/pallas_call | solution.py:950
  430.8 6.1 collective-permute-done.46.refs_1_
  449.0 4.2 shard_map.261.refs_1_
  457.8 4.0 shard_map.262.refs_0_
  464.6 11.8 %collective-permute-done.50.refs_3_ = bf16[384,768]{1,0:T(8,128)(2,1)S(1)} collective-permute-done((bf16[384,768]{1,0:T(8,128)(2,1)S(1)}, bf16[384,768]{1,0:T(8,128)(2,1)S(1)}, u32[]{:S(2)}, u32[]{:S(2)}) %collective-permute-start.50) | collective-permute-done | bytes 589856 | tf_op jit(solution)/shard_map/ppermute | solution.py:1081
  483.3 3.6 shard_map.266.refs_1_
  490.9 3.6 shard_map.269.refs_1_
  494.5 5.7 collective-permute-done.53.refs_0_
  515.8 10.2 %shard_map.272.refs_2_ = bf16[3,384,768]{2,1,0:T(8,128)(2,1)S(1)} custom-call(bf16[3072,384]{1,0:T(8,128)(2,1)} %get-tuple-element.283.base, bf16[3,3072,768]{2,1,0:T(8,128)(2,1)} %pinv_ref.9), custom_call_target="tpu_custom_call" | custom-call | flops 5435817984 | bytes 14155776 | tf_op jit(solution)/shard_map/pallas_call | solution.py:470
  539.7 6.4 %collective-permute-done.58.refs_1_ = bf16[4112,128]{1,0:T(8,128)(2,1)S(1)} collective-permute-done((bf16[4112,128]{1,0:T(8,128)(2,1)S(1)}, bf16[4112,128]{1,0:T(8,128)(2,1)S(1)}, u32[]{:S(2)}, u32[]{:S(2)}) %collective-permute-start.58) | collective-permute-done | bytes 1052704 | tf_op jit(solution)/shard_map/ppermute | solution.py:1081
  556.4 3.7 shard_map.279
  564.6 4.6 collective-permute-done.62.refs_2_
  572.2 3.6 shard_map.281
  602.8 3.9 collective-permute-done.68.refs_2_
  626.0 8.7 %shard_map.289 = (f32[32,128,128]{2,1,0:T(8,128)}, f32[32,128,128]{2,1,0:T(8,128)}, f32[32,128,128]{2,1,0:T(8,128)}, f32[32,128,128]{2,1,0:T(8,128)}) custom-call(s32[32]{0:T(128)S(1)} %convert_element_type.148.used, s32[1]{0:T(128)} %bitcast.27.flag.home, bf16[4112,128]{1,0:T(8,128)(2,1)} %shard_map.287.near, ...), custom_call_target="tpu_custom_call" | custom-call | flops 5905580032 | bytes 19922944 | tf_op jit(solution)/shard_map/pallas_call | solution.py:1011
  (502 shorter events, 249.8 us)
Async XLA Ops:
  4.2 26.5 %collective-permute-start.8 = (bf16[4112,128]{1,0:T(8,128)(2,1)}, bf16[4112,128]{1,0:T(8,128)(2,1)}, u32[]{:S(2)}, u32[]{:S(2)}) collective-permute-start(bf16[4112,128]{1,0:T(8,128)(2,1)} %pad_maximum_fusion.2), channel_id=1, source_target_pairs={{0,1},{1,0},{2,3},{3,2},{4,5},{5,4},{6,7},{7,6},{8,9},{9,8},{10,11... | collective-permute-start | bytes 3158024 | tf_op jit(solution)/shard_map/ppermute | solution.py:1081
  7.1 29.1 %collective-permute-start.10 = (bf16[4112,128]{1,0:T(8,128)(2,1)}, bf16[4112,128]{1,0:T(8,128)(2,1)}, u32[]{:S(2)}, u32[]{:S(2)}) collective-permute-start(bf16[4112,128]{1,0:T(8,128)(2,1)} %pad_maximum_fusion.2), channel_id=1, source_target_pairs={{0,4},{1,5},{2,6},{3,7},{4,0},{5,1},{6,2},{7,3},{8,12},{9,13},{10,... | collective-permute-start | bytes 3158024 | tf_op jit(solution)/shard_map/ppermute | solution.py:1081
  8.6 35.8 %collective-permute-start = (bf16[4112,128]{1,0:T(8,128)(2,1)}, bf16[4112,128]{1,0:T(8,128)(2,1)S(1)}, u32[]{:S(2)}, u32[]{:S(2)}) collective-permute-start(bf16[4112,128]{1,0:T(8,128)(2,1)} %pad_maximum_fusion.2), channel_id=1, source_target_pairs={{0,8},{1,9},{2,10},{3,11},{4,12},{5,13},{6,14},{7,15},{8,16},{9,17... | collective-permute-start | bytes 3158024 | tf_op jit(solution)/shard_map/ppermute | solution.py:1081
  11.5 33.0 %collective-permute-start.3 = (s32[1,504]{1,0:T(1,128)S(1)}, s32[1,504]{1,0:T(1,128)S(1)}, u32[]{:S(2)}, u32[]{:S(2)}) collective-permute-start(s32[1,504]{1,0:T(1,128)S(1)} %copy-done.102), channel_id=1, source_target_pairs={{0,1},{1,0},{2,3},{3,2},{4,5},{5,4},{6,7},{7,6},{8,9},{9,8},{10,11... | collective-permute-start | bytes 6056 | tf_op jit(solution)/shard_map/ppermute | solution.py:1081
  12.3 25.0 %collective-permute-start.2 = (bf16[1024,768]{1,0:T(8,128)(2,1)}, bf16[1024,768]{1,0:T(8,128)(2,1)}, u32[]{:S(2)}, u32[]{:S(2)}) collective-permute-start(bf16[1024,768]{1,0:T(8,128)(2,1)} %param.15), channel_id=1, source_target_pairs={{0,2},{3,1},{4,6},{7,5},{8,10},{11,9},{12,14},{15,13},{16,18},{19,... | collective-permute-start | bytes 4718600 | tf_op jit(solution)/shard_map/ppermute | solution.py:1081
  31.8 39.0 %collective-permute-start.12 = (bf16[2064,128]{1,0:T(8,128)(2,1)S(1)}, bf16[2064,128]{1,0:T(8,128)(2,1)S(1)}, u32[]{:S(2)}, u32[]{:S(2)}) collective-permute-start(bf16[2064,128]{1,0:T(8,128)(2,1)S(1)} %slice.149), channel_id=1, source_target_pairs={{0,4},{1,5},{2,6},{3,7},{4,0},{5,1},{6,2},{7,3},{8,12},{9,13},{10,... | collective-permute-start | bytes 1585160 | tf_op jit(solution)/shard_map/ppermute | solution.py:1081
  36.3 136.5 %collective-permute-start.9 = (bf16[4112,128]{1,0:T(8,128)(2,1)S(1)}, bf16[4112,128]{1,0:T(8,128)(2,1)S(1)}, u32[]{:S(2)}, u32[]{:S(2)}) collective-permute-start(bf16[4112,128]{1,0:T(8,128)(2,1)S(1)} %get-tuple-element.342), channel_id=1, source_target_pairs={{0,2},{1,3},{2,0},{3,1},{4,6},{5,7},{6,4},{7,5},{8,10},{9,11},{10,... | collective-permute-start | bytes 3158024 | tf_op jit(solution)/shard_map/ppermute | solution.py:1081
  37.4 29.8 %collective-permute-start.11 = (bf16[2048,128]{1,0:T(8,128)(2,1)S(1)}, bf16[2048,128]{1,0:T(8,128)(2,1)S(1)}, u32[]{:S(2)}, u32[]{:S(2)}) collective-permute-start(bf16[2048,128]{1,0:T(8,128)(2,1)S(1)} %slice.148), channel_id=1, source_target_pairs={{0,1},{1,0},{2,3},{3,2},{4,5},{5,4},{6,7},{7,6},{8,9},{9,8},{10,11... | collective-permute-start | bytes 1572872 | tf_op jit(solution)/shard_map/ppermute | solution.py:1081
  45.4 26.4 %collective-permute-start.16 = (bf16[4112,128]{1,0:T(8,128)(2,1)}, bf16[4112,128]{1,0:T(8,128)(2,1)S(1)}, u32[]{:S(2)}, u32[]{:S(2)}) collective-permute-start(bf16[4112,128]{1,0:T(8,128)(2,1)} %get-tuple-element.165), channel_id=1, source_target_pairs={{0,4},{1,5},{2,6},{3,7},{4,0},{5,1},{6,2},{7,3},{8,12},{9,13},{10,... | collective-permute-start | bytes 3158024 | tf_op jit(solution)/shard_map/ppermute | solution.py:1081
  46.5 27.8 %collective-permute-start.14 = (bf16[4112,128]{1,0:T(8,128)(2,1)}, bf16[4112,128]{1,0:T(8,128)(2,1)S(1)}, u32[]{:S(2)}, u32[]{:S(2)}) collective-permute-start(bf16[4112,128]{1,0:T(8,128)(2,1)} %get-tuple-element.165), channel_id=1, source_target_pairs={{0,1},{1,0},{2,3},{3,2},{4,5},{5,4},{6,7},{7,6},{8,9},{9,8},{10,11... | collective-permute-start | bytes 3158024 | tf_op jit(solution)/shard_map/ppermute | solution.py:1081
  67.2 26.2 %collective-permute-start.5 = (bf16[4112,128]{1,0:T(8,128)(2,1)S(1)}, bf16[4112,128]{1,0:T(8,128)(2,1)S(1)}, u32[]{:S(2)}, u32[]{:S(2)}) collective-permute-start(bf16[4112,128]{1,0:T(8,128)(2,1)S(1)} %copy-done.54), channel_id=1, source_target_pairs={{0,8},{1,9},{2,10},{3,11},{4,12},{5,13},{6,14},{7,15},{8,16},{9,17... | collective-permute-start | bytes 3158024 | tf_op jit(solution)/shard_map/ppermute | solution.py:1081
  71.8 101.9 %collective-permute-start.13 = (bf16[4112,128]{1,0:T(8,128)(2,1)S(1)}, bf16[4112,128]{1,0:T(8,128)(2,1)S(1)}, u32[]{:S(2)}, u32[]{:S(2)}) collective-permute-start(bf16[4112,128]{1,0:T(8,128)(2,1)S(1)} %broadcast_select_fusion.8), channel_id=1, source_target_pairs={{0,2},{1,3},{2,0},{3,1},{4,6},{5,7},{6,4},{7,5},{8,10},{9,11},{10,... | collective-permute-start | bytes 3158024 | tf_op jit(solution)/shard_map/ppermute | solution.py:1081
  71.9 25.1 %collective-permute-start.17 = (bf16[2048,128]{1,0:T(8,128)(2,1)S(1)}, bf16[2048,128]{1,0:T(8,128)(2,1)S(1)}, u32[]{:S(2)}, u32[]{:S(2)}) collective-permute-start(bf16[2048,128]{1,0:T(8,128)(2,1)S(1)} %slice.150), channel_id=1, source_target_pairs={{0,1},{1,0},{2,3},{3,2},{4,5},{5,4},{6,7},{7,6},{8,9},{9,8},{10,11... | collective-permute-start | bytes 1572872 | tf_op jit(solution)/shard_map/ppermute | solution.py:1081
  74.4 23.0 %collective-permute-start.18 = (bf16[2064,128]{1,0:T(8,128)(2,1)S(1)}, bf16[2064,128]{1,0:T(8,128)(2,1)S(1)}, u32[]{:S(2)}, u32[]{:S(2)}) collective-permute-start(bf16[2064,128]{1,0:T(8,128)(2,1)S(1)} %slice.151), channel_id=1, source_target_pairs={{0,4},{1,5},{2,6},{3,7},{4,0},{5,1},{6,2},{7,3},{8,12},{9,13},{10,... | collective-permute-start | bytes 1585160 | tf_op jit(solution)/shard_map/ppermute | solution.py:1081
  94.4 23.6 %collective-permute-start.22 = (bf16[4112,128]{1,0:T(8,128)(2,1)}, bf16[4112,128]{1,0:T(8,128)(2,1)S(1)}, u32[]{:S(2)}, u32[]{:S(2)}) collective-permute-start(bf16[4112,128]{1,0:T(8,128)(2,1)} %get-tuple-element.167), channel_id=1, source_target_pairs={{0,4},{1,5},{2,6},{3,7},{4,0},{5,1},{6,2},{7,3},{8,12},{9,13},{10,... | collective-permute-start | bytes 3158024 | tf_op jit(solution)/shard_map/ppermute | solution.py:1081
  97.1 24.4 %collective-permute-start.20 = (bf16[4112,128]{1,0:T(8,128)(2,1)S(1)}, bf16[4112,128]{1,0:T(8,128)(2,1)S(1)}, u32[]{:S(2)}, u32[]{:S(2)}) collective-permute-start(bf16[4112,128]{1,0:T(8,128)(2,1)S(1)} %copy-done.56), channel_id=1, source_target_pairs={{0,1},{1,0},{2,3},{3,2},{4,5},{5,4},{6,7},{7,6},{8,9},{9,8},{10,11... | collective-permute-start | bytes 3158024 | tf_op jit(solution)/shard_map/ppermute | solution.py:1081
  97.4 26.6 %collective-permute-start.6 = (bf16[4112,128]{1,0:T(8,128)(2,1)S(1)}, bf16[4112,128]{1,0:T(8,128)(2,1)S(1)}, u32[]{:S(2)}, u32[]{:S(2)}) collective-permute-start(bf16[4112,128]{1,0:T(8,128)(2,1)S(1)} %copy-done.56), channel_id=1, source_target_pairs={{0,8},{1,9},{2,10},{3,11},{4,12},{5,13},{6,14},{7,15},{8,16},{9,17... | collective-permute-start | bytes 3158024 | tf_op jit(solution)/shard_map/ppermute | solution.py:1081
  124.0 50.2 %collective-permute-start.15 = (bf16[4112,128]{1,0:T(8,128)(2,1)S(1)}, bf16[4112,128]{1,0:T(8,128)(2,1)S(1)}, u32[]{:S(2)}, u32[]{:S(2)}) collective-permute-start(bf16[4112,128]{1,0:T(8,128)(2,1)S(1)} %broadcast_select_fusion.7), channel_id=1, source_target_pairs={{0,2},{1,3},{2,0},{3,1},{4,6},{5,7},{6,4},{7,5},{8,10},{9,11},{10,... | collective-permute-start | bytes 3158024 | tf_op jit(solution)/shard_map/ppermute | solution.py:1081
  132.6 23.8 %collective-permute-start.26 = (bf16[4112,128]{1,0:T(8,128)(2,1)}, bf16[4112,128]{1,0:T(8,128)(2,1)S(1)}, u32[]{:S(2)}, u32[]{:S(2)}) collective-permute-start(bf16[4112,128]{1,0:T(8,128)(2,1)} %get-tuple-element.169), channel_id=1, source_target_pairs={{0,1},{1,0},{2,3},{3,2},{4,5},{5,4},{6,7},{7,6},{8,9},{9,8},{10,11... | collective-permute-start | bytes 3158024 | tf_op jit(solution)/shard_map/ppermute | solution.py:1081
  134.4 24.3 %collective-permute-start.7 = (bf16[4112,128]{1,0:T(8,128)(2,1)}, bf16[4112,128]{1,0:T(8,128)(2,1)S(1)}, u32[]{:S(2)}, u32[]{:S(2)}) collective-permute-start(bf16[4112,128]{1,0:T(8,128)(2,1)} %get-tuple-element.169), channel_id=1, source_target_pairs={{0,4},{1,5},{2,6},{3,7},{4,0},{5,1},{6,2},{7,3},{8,12},{9,13},{10,... | collective-permute-start | bytes 3158024 | tf_op jit(solution)/shard_map/ppermute | solution.py:1081
  235.6 21.3 %collective-permute-start.4 = (bf16[1024,768]{1,0:T(8,128)(2,1)S(1)}, bf16[1024,768]{1,0:T(8,128)(2,1)S(1)}, u32[]{:S(2)}, u32[]{:S(2)}) collective-permute-start(bf16[1024,768]{1,0:T(8,128)(2,1)S(1)} %copy-done.99), channel_id=1, source_target_pairs={{0,2},{3,1},{4,6},{7,5},{8,10},{11,9},{12,14},{15,13},{16,18},{19,... | collective-permute-start | bytes 4718600 | tf_op jit(solution)/shard_map/ppermute | solution.py:1081
  271.3 20.6 %collective-permute-start.37 = (bf16[1024,768]{1,0:T(8,128)(2,1)S(1)}, bf16[1024,768]{1,0:T(8,128)(2,1)S(1)}, u32[]{:S(2)}, u32[]{:S(2)}) collective-permute-start(bf16[1024,768]{1,0:T(8,128)(2,1)S(1)} %get-tuple-element.211), channel_id=1, source_target_pairs={{0,2},{1,3},{2,0},{3,1},{4,6},{5,7},{6,4},{7,5},{8,10},{9,11},{10,... | collective-permute-start | bytes 4718600 | tf_op jit(solution)/shard_map/ppermute | solution.py:1081
  286.2 32.9 %collective-permute-start.36 = (bf16[1536,768]{1,0:T(8,128)(2,1)S(1)}, bf16[1536,768]{1,0:T(8,128)(2,1)S(1)}, u32[]{:S(2)}, u32[]{:S(2)}) collective-permute-start(bf16[1536,768]{1,0:T(8,128)(2,1)S(1)} %convolution_convert_fusion.2.own), channel_id=1, source_target_pairs={{1,0},{2,3},{5,4},{6,7},{9,8},{10,11},{13,12},{14,15},{17,16},{18,... | collective-permute-start | bytes 7077896 | tf_op jit(solution)/shard_map/ppermute | solution.py:1081
  326.9 35.0 %collective-permute-start.41 = (bf16[768,1536]{1,0:T(8,128)(2,1)S(1)}, bf16[768,1536]{1,0:T(8,128)(2,1)S(1)}, u32[]{:S(2)}, u32[]{:S(2)}) collective-permute-start(bf16[768,1536]{1,0:T(8,128)(2,1)S(1)} %copy-done.50), channel_id=1, source_target_pairs={{1,0},{2,3},{5,4},{6,7},{9,8},{10,11},{13,12},{14,15},{17,16},{18,... | collective-permute-start | bytes 7077896 | tf_op jit(solution)/shard_map/ppermute | solution.py:1081
  347.8 32.9 %collective-permute-start.39 = (bf16[1024,768]{1,0:T(8,128)(2,1)S(1)}, bf16[1024,768]{1,0:T(8,128)(2,1)S(1)}, u32[]{:S(2)}, u32[]{:S(2)}) collective-permute-start(bf16[1024,768]{1,0:T(8,128)(2,1)S(1)} %get-tuple-element.216.own), channel_id=1, source_target_pairs={{0,2},{1,3},{2,0},{3,1},{4,6},{5,7},{6,4},{7,5},{8,10},{9,11},{10,... | collective-permute-start | bytes 4718600 | tf_op jit(solution)/shard_map/ppermute | solution.py:1081
  363.5 38.0 %collective-permute-start.42 = (bf16[1536,768]{1,0:T(8,128)(2,1)}, bf16[1536,768]{1,0:T(8,128)(2,1)S(1)}, u32[]{:S(2)}, u32[]{:S(2)}) collective-permute-start(bf16[1536,768]{1,0:T(8,128)(2,1)} %get-tuple-element.234.own), channel_id=1, source_target_pairs={{1,0},{2,3},{5,4},{6,7},{9,8},{10,11},{13,12},{14,15},{17,16},{18,... | collective-permute-start | bytes 7077896 | tf_op jit(solution)/shard_map/ppermute | solution.py:1081
  367.4 34.1 %collective-permute-start.44 = (bf16[384,1536]{1,0:T(8,128)(2,1)}, bf16[384,1536]{1,0:T(8,128)(2,1)S(1)}, u32[]{:S(2)}, u32[]{:S(2)}) collective-permute-start(bf16[384,1536]{1,0:T(8,128)(2,1)} %shard_map.248), channel_id=1, source_target_pairs={{1,5},{2,6},{5,1},{6,2},{9,13},{10,14},{13,9},{14,10},{17,21},{18,... | collective-permute-start | bytes 3538952 | tf_op jit(solution)/shard_map/ppermute | solution.py:1081
  372.5 29.1 %collective-permute-start.43 = (bf16[384,768]{1,0:T(8,128)(2,1)S(1)}, bf16[384,768]{1,0:T(8,128)(2,1)S(1)}, u32[]{:S(2)}, u32[]{:S(2)}) collective-permute-start(bf16[384,768]{1,0:T(8,128)(2,1)S(1)} %copy-done.73), channel_id=1, source_target_pairs={{1,0},{2,3},{5,4},{6,7},{9,8},{10,11},{13,12},{14,15},{17,16},{18,... | collective-permute-start | bytes 1769480 | tf_op jit(solution)/shard_map/ppermute | solution.py:1081
  416.6 20.3 %collective-permute-start.46 = (bf16[384,1536]{1,0:T(8,128)(2,1)}, bf16[384,1536]{1,0:T(8,128)(2,1)S(1)}, u32[]{:S(2)}, u32[]{:S(2)}) collective-permute-start(bf16[384,1536]{1,0:T(8,128)(2,1)} %shard_map.255), channel_id=1, source_target_pairs={{1,0},{2,3},{5,4},{6,7},{9,8},{10,11},{13,12},{14,15},{17,16},{18,... | collective-permute-start | bytes 3538952 | tf_op jit(solution)/shard_map/ppermute | solution.py:1081
  437.9 39.2 %collective-permute-start.48 = (bf16[1536,384]{1,0:T(8,128)(2,1)}, bf16[1536,384]{1,0:T(8,128)(2,1)S(1)}, u32[]{:S(2)}, u32[]{:S(2)}) collective-permute-start(bf16[1536,384]{1,0:T(8,128)(2,1)} %get-tuple-element.245.own), channel_id=1, source_target_pairs={{1,5},{2,6},{5,1},{6,2},{9,13},{10,14},{13,9},{14,10},{17,21},{18,... | collective-permute-start | bytes 3538952 | tf_op jit(solution)/shard_map/ppermute | solution.py:1081
  438.7 37.6 %collective-permute-start.52 = (bf16[384,1152]{1,0:T(8,128)(2,1)S(1)}, bf16[384,1152]{1,0:T(8,128)(2,1)S(1)}, u32[]{:S(2)}, u32[]{:S(2)}) collective-permute-start(bf16[384,1152]{1,0:T(8,128)(2,1)S(1)} %copy-done.90), channel_id=1, source_target_pairs={{1,0},{2,3},{5,4},{6,7},{9,8},{10,11},{13,12},{14,15},{17,16},{18,... | collective-permute-start | bytes 2654216 | tf_op jit(solution)/shard_map/ppermute | solution.py:1081
  442.7 34.3 %collective-permute-start.49 = (bf16[384,1152]{1,0:T(8,128)(2,1)}, bf16[384,1152]{1,0:T(8,128)(2,1)S(1)}, u32[]{:S(2)}, u32[]{:S(2)}) collective-permute-start(bf16[384,1152]{1,0:T(8,128)(2,1)} %shard_map.258), channel_id=1, source_target_pairs={{1,0},{2,3},{5,4},{6,7},{9,8},{10,11},{13,12},{14,15},{17,16},{18,... | collective-permute-start | bytes 2654216 | tf_op jit(solution)/shard_map/ppermute | solution.py:1081
  444.9 31.5 %collective-permute-start.50 = (bf16[384,768]{1,0:T(8,128)(2,1)S(1)}, bf16[384,768]{1,0:T(8,128)(2,1)S(1)}, u32[]{:S(2)}, u32[]{:S(2)}) collective-permute-start(bf16[384,768]{1,0:T(8,128)(2,1)S(1)} %convolution_convert_fusion.6.own), channel_id=1, source_target_pairs={{1,0},{2,3},{5,4},{6,7},{9,8},{10,11},{13,12},{14,15},{17,16},{18,... | collective-permute-start | bytes 1769480 | tf_op jit(solution)/shard_map/ppermute | solution.py:1081
  454.3 22.7 %collective-permute-start.51 = (bf16[16,16,128]{2,1,0:T(8,128)(2,1)S(1)}, bf16[16,16,128]{2,1,0:T(8,128)(2,1)S(1)}, u32[]{:S(2)}, u32[]{:S(2)}) collective-permute-start(bf16[16,16,128]{2,1,0:T(8,128)(2,1)S(1)} %convert_element_type.138.own), channel_id=1, source_target_pairs={{1,0},{2,3},{5,4},{6,7},{9,8},{10,11},{13,12},{14,15},{17,16},{18,... | collective-permute-start | bytes 196616 | tf_op jit(solution)/shard_map/ppermute | solution.py:1081
  506.8 20.3 %collective-permute-start.55 = (bf16[4112,128]{1,0:T(8,128)(2,1)S(1)}, bf16[4112,128]{1,0:T(8,128)(2,1)S(1)}, u32[]{:S(2)}, u32[]{:S(2)}) collective-permute-start(bf16[4112,128]{1,0:T(8,128)(2,1)S(1)} %get-tuple-element.341), channel_id=1, source_target_pairs={{0,4},{3,7},{4,0},{7,3},{8,12},{11,15},{12,8},{15,11},{16,20},{19,... | collective-permute-start | bytes 3158024 | tf_op jit(solution)/shard_map/ppermute | solution.py:1081
  509.9 42.4 %collective-permute-start.59 = (bf16[4112,128]{1,0:T(8,128)(2,1)S(1)}, bf16[4112,128]{1,0:T(8,128)(2,1)S(1)}, u32[]{:S(2)}, u32[]{:S(2)}) collective-permute-start(bf16[4112,128]{1,0:T(8,128)(2,1)S(1)} %get-tuple-element.339), channel_id=1, source_target_pairs={{0,4},{3,7},{4,0},{7,3},{8,12},{11,15},{12,8},{15,11},{16,20},{19,... | collective-permute-start | bytes 3158024 | tf_op jit(solution)/shard_map/ppermute | solution.py:1081
  512.8 33.4 %collective-permute-start.58 = (bf16[4112,128]{1,0:T(8,128)(2,1)S(1)}, bf16[4112,128]{1,0:T(8,128)(2,1)S(1)}, u32[]{:S(2)}, u32[]{:S(2)}) collective-permute-start(bf16[4112,128]{1,0:T(8,128)(2,1)S(1)} %get-tuple-element.340), channel_id=1, source_target_pairs={{0,4},{3,7},{4,0},{7,3},{8,12},{11,15},{12,8},{15,11},{16,20},{19,... | collective-permute-start | bytes 3158024 | tf_op jit(solution)/shard_map/ppermute | solution.py:1081
  531.5 23.9 %collective-permute-start.60 = (bf16[4112,128]{1,0:T(8,128)(2,1)}, bf16[4112,128]{1,0:T(8,128)(2,1)S(1)}, u32[]{:S(2)}, u32[]{:S(2)}) collective-permute-start(bf16[4112,128]{1,0:T(8,128)(2,1)} %get-tuple-element.288), channel_id=1, source_target_pairs={{0,8},{3,11},{4,12},{7,15},{8,16},{11,19},{12,20},{15,23},{16,24},... | collective-permute-start | bytes 3158024 | tf_op jit(solution)/shard_map/ppermute | solution.py:1081
  536.8 49.9 %collective-permute-start.56 = (bf16[1024,768]{1,0:T(8,128)(2,1)S(1)}, bf16[1024,768]{1,0:T(8,128)(2,1)S(1)}, u32[]{:S(2)}, u32[]{:S(2)}) collective-permute-start(bf16[1024,768]{1,0:T(8,128)(2,1)S(1)} %add_convert_fusion), channel_id=1, source_target_pairs={{0,2},{1,3},{2,0},{3,1},{4,6},{5,7},{6,4},{7,5},{8,10},{9,11},{10,... | collective-permute-start | bytes 4718600 | tf_op jit(solution)/shard_map/ppermute | solution.py:1081
  536.9 25.2 %collective-permute-start.61 = (bf16[4112,128]{1,0:T(8,128)(2,1)S(1)}, bf16[4112,128]{1,0:T(8,128)(2,1)S(1)}, u32[]{:S(2)}, u32[]{:S(2)}) collective-permute-start(bf16[4112,128]{1,0:T(8,128)(2,1)S(1)} %get-tuple-element.338), channel_id=1, source_target_pairs={{0,4},{3,7},{4,0},{7,3},{8,12},{11,15},{12,8},{15,11},{16,20},{19,... | collective-permute-start | bytes 3158024 | tf_op jit(solution)/shard_map/ppermute | solution.py:1081
  552.4 23.4 %collective-permute-start.63 = (bf16[4112,128]{1,0:T(8,128)(2,1)S(1)}, bf16[4112,128]{1,0:T(8,128)(2,1)S(1)}, u32[]{:S(2)}, u32[]{:S(2)}) collective-permute-start(bf16[4112,128]{1,0:T(8,128)(2,1)S(1)} %copy-done.110), channel_id=1, source_target_pairs={{0,4},{3,7},{4,0},{7,3},{8,12},{11,15},{12,8},{15,11},{16,20},{19,... | collective-permute-start | bytes 3158024 | tf_op jit(solution)/shard_map/ppermute | solution.py:1081
  560.1 20.3 %collective-permute-start.64 = (bf16[4112,128]{1,0:T(8,128)(2,1)}, bf16[4112,128]{1,0:T(8,128)(2,1)S(1)}, u32[]{:S(2)}, u32[]{:S(2)}) collective-permute-start(bf16[4112,128]{1,0:T(8,128)(2,1)} %get-tuple-element.296), channel_id=1, source_target_pairs={{0,8},{3,11},{4,12},{7,15},{8,16},{11,19},{12,20},{15,23},{16,24},... | collective-permute-start | bytes 3158024 | tf_op jit(solution)/shard_map/ppermute | solution.py:1081
  562.1 50.3 %collective-permute-start.54 = (bf16[1024,768]{1,0:T(8,128)(2,1)S(1)}, bf16[1024,768]{1,0:T(8,128)(2,1)}, u32[]{:S(2)}, u32[]{:S(2)}) collective-permute-start(bf16[1024,768]{1,0:T(8,128)(2,1)S(1)} %copy-done.49), channel_id=1, source_target_pairs={{0,1},{3,2},{4,5},{7,6},{8,9},{11,10},{12,13},{15,14},{16,17},{19,... | collective-permute-start | bytes 4718600 | tf_op jit(solution)/shard_map/ppermute | solution.py:1081
  569.2 23.4 %collective-permute-start.65 = (bf16[4112,128]{1,0:T(8,128)(2,1)}, bf16[4112,128]{1,0:T(8,128)(2,1)}, u32[]{:S(2)}, u32[]{:S(2)}) collective-permute-start(bf16[4112,128]{1,0:T(8,128)(2,1)} %get-tuple-element.298), channel_id=1, source_target_pairs={{0,4},{3,7},{4,0},{7,3},{8,12},{11,15},{12,8},{15,11},{16,20},{19,... | collective-permute-start | bytes 3158024 | tf_op jit(solution)/shard_map/ppermute | solution.py:1081
  575.8 19.0 %collective-permute-start.66 = (bf16[4112,128]{1,0:T(8,128)(2,1)}, bf16[4112,128]{1,0:T(8,128)(2,1)}, u32[]{:S(2)}, u32[]{:S(2)}) collective-permute-start(bf16[4112,128]{1,0:T(8,128)(2,1)} %get-tuple-element.301), channel_id=1, source_target_pairs={{0,8},{3,11},{4,12},{7,15},{8,16},{11,19},{12,20},{15,23},{16,24},... | collective-permute-start | bytes 3158024 | tf_op jit(solution)/shard_map/ppermute | solution.py:1081
  580.5 20.4 %collective-permute-start.67 = (bf16[4112,128]{1,0:T(8,128)(2,1)}, bf16[4112,128]{1,0:T(8,128)(2,1)}, u32[]{:S(2)}, u32[]{:S(2)}) collective-permute-start(bf16[4112,128]{1,0:T(8,128)(2,1)} %get-tuple-element.303), channel_id=1, source_target_pairs={{0,4},{3,7},{4,0},{7,3},{8,12},{11,15},{12,8},{15,11},{16,20},{19,... | collective-permute-start | bytes 3158024 | tf_op jit(solution)/shard_map/ppermute | solution.py:1081
  592.6 21.7 %collective-permute-start.57 = (bf16[1024,384]{1,0:T(8,128)(2,1)}, bf16[1024,384]{1,0:T(8,128)(2,1)}, u32[]{:S(2)}, u32[]{:S(2)}) collective-permute-start(bf16[1024,384]{1,0:T(8,128)(2,1)} %select_convert_fusion), channel_id=1, source_target_pairs={{0,1},{3,2},{4,5},{7,6},{8,9},{11,10},{12,13},{15,14},{16,17},{19,... | collective-permute-start | bytes 2359304 | tf_op jit(solution)/shard_map/ppermute | solution.py:1081
  594.8 22.3 %collective-permute-start.69 = (bf16[4112,128]{1,0:T(8,128)(2,1)}, bf16[4112,128]{1,0:T(8,128)(2,1)}, u32[]{:S(2)}, u32[]{:S(2)}) collective-permute-start(bf16[4112,128]{1,0:T(8,128)(2,1)} %get-tuple-element.307), channel_id=1, source_target_pairs={{0,4},{3,7},{4,0},{7,3},{8,12},{11,15},{12,8},{15,11},{16,20},{19,... | collective-permute-start | bytes 3158024 | tf_op jit(solution)/shard_map/ppermute | solution.py:1081
  (140 other events, 943.7 us)

commit v13 on v11

--- a/solution.py
+++ b/solution.py
@@ -482,13 +482,13 @@
     )(stay(weights["base", 0]), stay(pinv))
 
 
-def embed_back_kernel(core, base, own, recv, out, bias):
+def embed_back_kernel(core, token, base, own, recv, out, bias):
     low = (base[...] + (own[...].astype(f32) + recv[...].astype(f32))).astype(bf16)
     out[...] = low
     accumulate(bias, jnp.sum(low.astype(f32), axis=0, keepdims=True))
 
 
-def embed_back_call(core, base, own, recv):
+def embed_back_call(core, token, base, own, recv):
     tokens = base.shape[0]
     half = pl.BlockSpec((ROWS, HALF), lambda i, core: (i, core[0]))
     return pl.pallas_call(
@@ -500,12 +500,12 @@
         grid_spec=pltpu.PrefetchScalarGridSpec(
             num_scalar_prefetch=1,
             grid=(tokens // ROWS,),
-            in_specs=[half] * 3,
+            in_specs=[fixed(token.shape)] + [half] * 3,
             out_specs=[rows_spec(HALF), fixed((1, HALF))],
         ),
         compiler_params=params(8),
         cost_estimate=cost(tokens * D, tokens * D * 5),
-    )(core, base, own, recv)
+    )(core, token, base, own, recv)
 
 
 def pack_kernel(vec_per, *refs):
@@ -1165,13 +1165,16 @@
         middle_row = slots_per * BS // 2
         for j in range(4):
             beside_x, beside_y = send(pack, routes.x_all), send(pack, routes.y_all)
+            further = [send(pack, routes.z_all)] if j < 3 else []
+            work = [slot_other] if j == 0 else []
+            beside_x, beside_y, patches, chunk, *more = fence(
+                beside_x, beside_y, patches, expand(j, patches), *further, *work
+            )
+            chunks.append(chunk)
             if j < 3:
-                further = send(pack, routes.z_all)
-            work = [expand(j, patches)] + ([slot_other] if j == 0 else [])
-            beside_x, patches, chunk, *work = fence(beside_x, patches, *work)
-            chunks.append(chunk)
+                further = more.pop(0)
             if j == 0:
-                [slot_other] = work
+                [slot_other] = more
             corner = jnp.concatenate(
                 [send(beside_x[:middle_row], routes.y_all), send(beside_y[middle_row:], routes.x_all)],
                 axis=0,
@@ -1294,10 +1297,10 @@
     other = send(part, routes.core_all)
     gd1 = dot_tn(caches[top][9], grad_low).astype(bf16)
     gu1 = dot_tn(caches[top][8], du).astype(bf16)
-    lse, gd1, gu1, out_low = fence(caches[top][6], gd1, gu1, out_low)
     ad1 = over(gd1)
+    lse, gu1 = fence(caches[top][6], gu1)
     grad, grad_low, dq, dk, dv, dbo = attend_step(top, grad, part, other, lse)
-    vec, dbo, ad1, gu1 = hold(vec, dbo, ad1, gu1)
+    vec, dbo, ad1, gu1, out_low = hold(vec, dbo, ad1, gu1, out_low)
     au1 = over(gu1)
     own, dg1, ds1, dbq, dbv = qkv_back_call(top, dq, dk, dv, caches[top][0], vec, weights)
     recv = send(own, routes.core_all)
@@ -1306,18 +1309,18 @@
     vec_grads[top] = [dg1, ds1, dbq, dbv, dbo, dg2, ds2, db1, db2]
     grad, grad_low, du, part, dg2, ds2, db1, db2 = mlp_step(low, grad, own, recv)
     other = send(part, routes.core_all)
-    db2, au1, go1, gq1 = hold(db2, au1, go1, gq1)
+    db2, go1, gq1 = hold(db2, go1, gq1)
     xq1, ao1 = beside(gq1), over(go1)
     gd0 = dot_tn(caches[low][9], grad_low).astype(bf16)
     gu0 = dot_tn(caches[low][8], du).astype(bf16)
-    lse, gd0, gu0, xq1, ao1 = hold(caches[low][6], gd0, gu0, xq1, ao1)
+    lse, gd0, gu0, xq1, au1 = hold(caches[low][6], gd0, gu0, xq1, au1)
     hq1 = summed(gq1, xq1)
     ad0 = over(gd0)
     xu0 = beside(gu0)
     buffer = place_tiles(("down", top), gd1, ad1, None)
     buffer = place_tiles(("up", top), gu1, au1, buffer)
     grad, grad_low, dq, dk, dv, dbo = attend_step(low, grad, part, other, lse)
-    vec, dbo, ad0, xu0, hq1, buffer = hold(vec, dbo, ad0, xu0, hq1, buffer)
+    vec, dbo, ad0, ao1, xu0, hq1, buffer = hold(vec, dbo, ad0, ao1, xu0, hq1, buffer)
     au0 = over(summed(gu0, xu0))
     aq1 = over(hq1)
     own, dg1, ds1, dbq, dbv = qkv_back_call(low, dq, dk, dv, caches[low][0], vec, weights)
@@ -1325,14 +1328,15 @@
     gq0 = dot_tn(caches[low][1], jnp.concatenate([dq, dk, dv], axis=1)).astype(bf16)
     vec_grads[low] = [dg1, ds1, dbq, dbv, dbo, dg2, ds2, db1, db2]
     xq0 = beside(gq0)
-    grad_emb, grad_emb_bias = embed_back_call(core_flag, grad, own, recv)
+    turn, aq1 = hold(jnp.zeros((8, BS), f32), aq1)
+    grad_emb, grad_emb_bias = embed_back_call(core_flag, turn, grad, own, recv)
     middle = CHUNKS // 2
 
     def base_grad(parts):
         return jnp.concatenate([dot_tn(c, grad_emb).astype(bf16) for c in parts], axis=0)
 
     gbt = base_grad(chunks[middle:])
-    gbt, au0, xq0, aq1 = hold(gbt, au0, xq0, aq1)
+    gbt, au0, xq0 = hold(gbt, au0, xq0)
     xb = send(gbt, routes.x_away) if grid3 else None
     aq0 = over(summed(gq0, xq0))
     gbm = base_grad(chunks[:middle])

time: 667 us -> 635 us (0.952)
  waiting for transfers between devices: 166 us -> 129 us
    ppermute x72, waiting for transfers between devices: 166 us -> 129 us  [send(): return lax.ppermute(value, AXES, route)]
    unnamed x232 -> x254, local copies, waits for them, and re-layouts: 30.1 us -> 29.4 us
  transfers between devices with their start and end apart: 72 -> 72, of which waited for: 27 -> 33; matrix products, arithmetic and copies ran while one was open for 10% -> 10% of each run, Pallas kernels for 31% -> 32%
where the time goes in v13:
time: 635 us; the launch traced here: 625 us
  Pallas kernels  289 us (46%)
  waiting for transfers between devices  129 us (20%)
  starting transfers between devices  100 us (16%)
  local copies, waits for them, and re-layouts  44.3 us (7%)
  matrix products  31.5 us (5%)
  other arithmetic  28.5 us (4%)
    ppermute x72, waiting for transfers between devices, send(): return lax.ppermute(value, AXES, route)  129 us
    ppermute x72, starting transfers between devices, send(): return lax.ppermute(value, AXES, route)  100 us
    pallas_call x2, Pallas kernels, attend_back_call(): pl.pallas_call(attend_back_kernel, out_shape=[shape(D, f32), shape(D, bf1...  46.7 us
    pallas_call x10, Pallas kernels, scatter_matrix(): pl.pallas_call(functools.partial(scatter_kernel, rows_n, cols_n, steps, p...  35.5 us
    pallas_call x2, Pallas kernels, attend_call(): pl.pallas_call(functools.partial(attend_kernel, layer), out_shape=[jax.Sh...  30.5 us
    unnamed x254, local copies, waits for them, and re-layouts  29.4 us
    dot_general x12, matrix products, dot_tn(): lax.dot_general(left, right, (((0,), (0,)), ((), ())), preferred_element_...  28.5 us
    pallas_call x8, Pallas kernels, reduce_call(): pl.pallas_call(functools.partial(reduce_kernel, carried is not None, last...  27.1 us
  transfers between devices with their start and end apart: 72, of which 33 were waited for; matrix products, arithmetic and copies ran while one was open for 10% of the time, Pallas kernels for 32%

profile of v13, /device:TPU:0, one launch (start us, length us, event | category | flops | bytes accessed | tf_op | source)
XLA Modules:
  0.0 625.2 jit_solution(11055284489380654876)
XLA Ops:
  18.9 6.0 shard_map.222.refs_3_
  26.0 6.1 collective-permute-done.5.refs_5_
  43.7 6.2 shard_map.224.refs_3_
  54.7 12.5 %collective-permute-done.12.refs_4_ = bf16[4112,128]{1,0:T(8,128)(2,1)S(1)} collective-permute-done((bf16[4112,128]{1,0:T(8,128)(2,1)}, bf16[4112,128]{1,0:T(8,128)(2,1)S(1)}, u32[]{:S(2)}, u32[]{:S(2)}) %collective-permute-start.12) | collective-permute-done | bytes 1052704 | tf_op jit(solution)/shard_map/ppermute | solution.py:1081
  67.2 5.7 collective-permute-done.11.refs_1_
  80.8 6.0 shard_map.226.refs_3_
  93.6 12.3 %collective-permute-done.19.refs_4_ = bf16[4112,128]{1,0:T(8,128)(2,1)S(1)} collective-permute-done((bf16[4112,128]{1,0:T(8,128)(2,1)S(1)}, bf16[4112,128]{1,0:T(8,128)(2,1)S(1)}, u32[]{:S(2)}, u32[]{:S(2)}) %collective-permute-start.19) | collective-permute-done | bytes 1052704 | tf_op jit(solution)/shard_map/ppermute | solution.py:1081
  105.8 6.1 collective-permute-done.18.refs_1_
  119.8 6.2 shard_map.228.refs_3_
  132.4 16.7 %collective-permute-done.25.refs_1_ = bf16[4112,128]{1,0:T(8,128)(2,1)S(1)} collective-permute-done((bf16[4112,128]{1,0:T(8,128)(2,1)S(1)}, bf16[4112,128]{1,0:T(8,128)(2,1)S(1)}, u32[]{:S(2)}, u32[]{:S(2)}) %collective-permute-start.25) | collective-permute-done | bytes 1052704 | tf_op jit(solution)/shard_map/ppermute | solution.py:1081
  156.9 5.7 collective-permute-done.27
  172.1 14.2 %shard_map.230 = (bf16[3072,384]{1,0:T(8,128)(2,1)}, bf16[2304,384]{1,0:T(8,128)(2,1)}, bf16[768,384]{1,0:T(8,128)(2,1)}, bf16[3072,384]{1,0:T(8,128)(2,1)}, bf1...) custom-call(s32[16]{0:T(128)S(1)} %stack.95.owner, ...), custom_call_target="tpu_custom_call" | custom-call | bytes 33030144 | tf_op jit(solution)/shard_map/pallas_call | solution.py:243
  186.4 6.9 %shard_map.231.refs_0_ = bf16[1024,384]{1,0:T(8,128)(2,1)S(1)} custom-call(s32[1]{0:T(128)} %bitcast.6.half.part, bf16[1024,768]{1,0:T(8,128)(2,1)} %get-tuple-element.175.refs_0_, bf16[1024,768]{1,0:T(8,128)(2,1)} %get-tuple-element.192.refs_1_, bf16[1024,768]{1,0:T(8,128)(2,1)} %get-tuple-element.193.refs_2_, ...), custom_call_target="tpu_custom_call" | custom-call | flops 2415919104 | bytes 9437184 | tf_op jit(solution)/shard_map/pallas_call | solution.py:552
  195.8 4.8 shard_map.232
  200.7 15.2 %shard_map.233 = (bf16[1024,384]{1,0:T(8,128)(2,1)S(1)}, f32[8,1024]{1,0:T(8,128)S(1)}, bf16[1024,768]{1,0:T(8,128)(2,1)S(1)}) custom-call(s32[4]{0:T(128)S(1)} %get-tuple-element.383.low_ref, s32[4]{0:T(128)S(1)} %get-tuple-element.376.high_ref, bf16[1024,384]{1,0:T(8,128)(2,1)S(1)} %get-tuple-element.198.q_ref, ...), custom_call_target="tpu_custom_call" | custom-call | flops 6442450944 | bytes 6291456 | tf_op jit(solution)/shard_map/pallas_call | solution.py:679
  220.3 9.4 %shard_map.234 = (f32[1024,768]{1,0:T(8,128)S(1)}, bf16[1024,768]{1,0:T(8,128)(2,1)}, bf16[1024,1536]{1,0:T(8,128)(2,1)}, bf16[1024,1536]{1,0:T(8,128)(2,1)}, bf16[1024,768]{1,0:T(8,128)(2,1)S(1)}) custom-call(f32[1024,768]{1,0:T(8,128)S(1)} %get-tuple-element.197.base.hid, bf16[1024,768]{1,0:T(8,128)(2,1)S(1)} %get-tuple-element.202.own, ...), custom_call_target="tpu_custom_call" | custom-call | flops 4831838208 | bytes 18874368 | tf_op jit(solution)/shard_map/pallas_call | solution.py:742
  233.1 4.4 shard_map.235
  237.5 15.3 %shard_map.236 = (bf16[1024,384]{1,0:T(8,128)(2,1)S(1)}, f32[8,1024]{1,0:T(8,128)S(1)}, bf16[1024,768]{1,0:T(8,128)(2,1)S(1)}) custom-call(s32[4]{0:T(128)S(1)} %get-tuple-element.383.low_ref, s32[4]{0:T(128)S(1)} %get-tuple-element.376.high_ref, bf16[1024,384]{1,0:T(8,128)(2,1)S(1)} %get-tuple-element.209.q_ref, ...), custom_call_target="tpu_custom_call" | custom-call | flops 6442450944 | bytes 6291456 | tf_op jit(solution)/shard_map/pallas_call | solution.py:679
  256.3 9.4 %shard_map.237 = (f32[1024,768]{1,0:T(8,128)S(1)}, bf16[1024,768]{1,0:T(8,128)(2,1)}, bf16[1024,1536]{1,0:T(8,128)(2,1)}, bf16[1024,1536]{1,0:T(8,128)(2,1)}, bf16[1024,768]{1,0:T(8,128)(2,1)S(1)}) custom-call(f32[1024,768]{1,0:T(8,128)S(1)} %get-tuple-element.208.base.hid, bf16[1024,768]{1,0:T(8,128)(2,1)S(1)} %get-tuple-element.213.own, ...), custom_call_target="tpu_custom_call" | custom-call | flops 4831838208 | bytes 18874368 | tf_op jit(solution)/shard_map/pallas_call | solution.py:742
  267.8 11.3 %shard_map.238 = (bf16[1024,768]{1,0:T(8,128)(2,1)S(1)}, bf16[1024,1536]{1,0:T(8,128)(2,1)S(1)}, bf16[1024,768]{1,0:T(8,128)(2,1)S(1)}, f32[1,768]{1,0:T(1,128)S...) custom-call(bf16[1024,768]{1,0:T(8,128)(2,1)S(1)} %broadcast_select_fusion.refs_0_, ...), custom_call_target="tpu_custom_call" | custom-call | flops 4831838208 | bytes 18874368 | tf_op jit(solution)/shard_map/pallas_call | solution.py:794
  283.8 4.1 convolution_convert_fusion.3.refs_1_
  289.7 23.4 %shard_map.240 = (f32[1024,768]{1,0:T(8,128)S(1)}, bf16[1024,768]{1,0:T(8,128)(2,1)S(1)}, bf16[1024,384]{1,0:T(8,128)(2,1)S(1)}, bf16[1024,384]{1,0:T(8,128)(2,1...) custom-call(s32[4]{0:T(128)S(1)} %get-tuple-element.382.low_ref, s32[4]{0:T(128)S(1)} %get-tuple-element.377.high_ref, ...), custom_call_target="tpu_custom_call" | custom-call | flops 11274289152 | bytes 15728640 | tf_op jit(solution)/shard_map/pallas_call | solution.py:886
  314.6 5.7 shard_map.242
  325.2 3.5 convolution_convert_fusion.5.refs_2_
  328.7 11.1 %shard_map.243 = (f32[1024,768]{1,0:T(8,128)S(1)}, bf16[1024,768]{1,0:T(8,128)(2,1)S(1)}, bf16[1024,1536]{1,0:T(8,128)(2,1)S(1)}, bf16[1024,768]{1,0:T(8,128)(2,...) custom-call(f32[1024,768]{1,0:T(8,128)S(1)} %get-tuple-element.230.refs_0_, ...), custom_call_target="tpu_custom_call" | custom-call | flops 4831838208 | bytes 18874368 | tf_op jit(solution)/shard_map/pallas_call | solution.py:794
  346.2 4.0 convolution_convert_fusion.1.refs_1_
  350.2 4.0 convolution_convert_fusion.refs_2_
  360.6 4.2 shard_map.250.refs_1_
  368.7 4.3 shard_map.251.refs_6_
  373.0 23.3 %shard_map.247 = (f32[1024,768]{1,0:T(8,128)S(1)}, bf16[1024,768]{1,0:T(8,128)(2,1)S(1)}, bf16[1024,384]{1,0:T(8,128)(2,1)S(1)}, bf16[1024,384]{1,0:T(8,128)(2,1...) custom-call(s32[4]{0:T(128)S(1)} %get-tuple-element.382.low_ref, s32[4]{0:T(128)S(1)} %get-tuple-element.377.high_ref, ...), custom_call_target="tpu_custom_call" | custom-call | flops 11274289152 | bytes 15728640 | tf_op jit(solution)/shard_map/pallas_call | solution.py:886
  400.4 6.5 %shard_map.254 = (bf16[1024,768]{1,0:T(8,128)(2,1)}, f32[1,768]{1,0:T(1,128)S(1)}, f32[1,768]{1,0:T(1,128)S(1)}, f32[1,384]{1,0:T(1,128)S(1)}, f32[1,384]{1,0:T(1,128)S(1)}) custom-call(bf16[1024,384]{1,0:T(8,128)(2,1)S(1)} %get-tuple-element.260.dq, bf16[1024,384]{1,0:T(8,128)(2,1)S(1)} %get-tuple-element.261.dk, ...), custom_call_target="tpu_custom_call" | custom-call | flops 1811939328 | bytes 7864320 | tf_op jit(solution)/shard_map/pallas_call | solution.py:950
  415.4 3.5 convolution_convert_fusion.4.own
  431.6 5.4 collective-permute-done.47.refs_1_
  447.9 3.6 shard_map.262.refs_1_
  451.4 4.2 shard_map.263.refs_1_
  460.2 4.0 shard_map.264.refs_0_
  477.5 3.6 shard_map.270.refs_1_
  481.1 9.4 %collective-permute-done.53.refs_0_ = bf16[1536,384]{1,0:T(8,128)(2,1)S(1)} collective-permute-done((bf16[1536,384]{1,0:T(8,128)(2,1)}, bf16[1536,384]{1,0:T(8,128)(2,1)S(1)}, u32[]{:S(2)}, u32[]{:S(2)}) %collective-permute-start.53) | collective-permute-done | bytes 1179680 | tf_op jit(solution)/shard_map/ppermute | solution.py:1081
  505.9 10.2 %shard_map.273.refs_2_ = bf16[3,384,768]{2,1,0:T(8,128)(2,1)S(1)} custom-call(bf16[3072,384]{1,0:T(8,128)(2,1)} %get-tuple-element.305.base, bf16[3,3072,768]{2,1,0:T(8,128)(2,1)} %pinv_ref.9), custom_call_target="tpu_custom_call" | custom-call | flops 5435817984 | bytes 14155776 | tf_op jit(solution)/shard_map/pallas_call | solution.py:470
  518.3 3.4 shard_map.276
  529.9 6.5 %collective-permute-done.58.refs_1_ = bf16[4112,128]{1,0:T(8,128)(2,1)S(1)} collective-permute-done((bf16[4112,128]{1,0:T(8,128)(2,1)S(1)}, bf16[4112,128]{1,0:T(8,128)(2,1)S(1)}, u32[]{:S(2)}, u32[]{:S(2)}) %collective-permute-start.58) | collective-permute-done | bytes 1052704 | tf_op jit(solution)/shard_map/ppermute | solution.py:1081
  537.3 3.3 shard_map.278
  546.4 3.7 shard_map.280
  554.5 4.9 collective-permute-done.62.refs_2_
  562.2 3.6 shard_map.282
  593.0 3.7 collective-permute-done.68.refs_2_
  610.0 3.5 shard_map.288.near
  616.2 8.8 %shard_map.290 = (f32[32,128,128]{2,1,0:T(8,128)}, f32[32,128,128]{2,1,0:T(8,128)}, f32[32,128,128]{2,1,0:T(8,128)}, f32[32,128,128]{2,1,0:T(8,128)}) custom-call(s32[32]{0:T(128)S(1)} %convert_element_type.148.used, s32[1]{0:T(128)} %bitcast.26.flag.home, bf16[4112,128]{1,0:T(8,128)(2,1)} %shard_map.288.near, ...), custom_call_target="tpu_custom_call" | custom-call | flops 5905580032 | bytes 19922944 | tf_op jit(solution)/shard_map/pallas_call | solution.py:1011
  (520 shorter events, 263.0 us)
Async XLA Ops:
  4.2 28.6 %collective-permute-start.4 = (bf16[4112,128]{1,0:T(8,128)(2,1)}, bf16[4112,128]{1,0:T(8,128)(2,1)}, u32[]{:S(2)}, u32[]{:S(2)}) collective-permute-start(bf16[4112,128]{1,0:T(8,128)(2,1)} %pad_maximum_fusion.2), channel_id=1, source_target_pairs={{0,8},{1,9},{2,10},{3,11},{4,12},{5,13},{6,14},{7,15},{8,16},{9,17... | collective-permute-start | bytes 3158024 | tf_op jit(solution)/shard_map/ppermute | solution.py:1081
  7.2 25.6 %collective-permute-start.1 = (bf16[4112,128]{1,0:T(8,128)(2,1)}, bf16[4112,128]{1,0:T(8,128)(2,1)S(1)}, u32[]{:S(2)}, u32[]{:S(2)}) collective-permute-start(bf16[4112,128]{1,0:T(8,128)(2,1)} %pad_maximum_fusion.2), channel_id=1, source_target_pairs={{0,1},{1,0},{2,3},{3,2},{4,5},{5,4},{6,7},{7,6},{8,9},{9,8},{10,11... | collective-permute-start | bytes 3158024 | tf_op jit(solution)/shard_map/ppermute | solution.py:1081
  8.7 24.6 %collective-permute-start = (bf16[4112,128]{1,0:T(8,128)(2,1)}, bf16[4112,128]{1,0:T(8,128)(2,1)S(1)}, u32[]{:S(2)}, u32[]{:S(2)}) collective-permute-start(bf16[4112,128]{1,0:T(8,128)(2,1)} %pad_maximum_fusion.2), channel_id=1, source_target_pairs={{0,4},{1,5},{2,6},{3,7},{4,0},{5,1},{6,2},{7,3},{8,12},{9,13},{10,... | collective-permute-start | bytes 3158024 | tf_op jit(solution)/shard_map/ppermute | solution.py:1081
  14.0 18.2 %collective-permute-start.5 = (s32[1,504]{1,0:T(1,128)S(1)}, s32[1,504]{1,0:T(1,128)S(1)}, u32[]{:S(2)}, u32[]{:S(2)}) collective-permute-start(s32[1,504]{1,0:T(1,128)S(1)} %copy-done.110), channel_id=1, source_target_pairs={{0,1},{1,0},{2,3},{3,2},{4,5},{5,4},{6,7},{7,6},{8,9},{9,8},{10,11... | collective-permute-start | bytes 6056 | tf_op jit(solution)/shard_map/ppermute | solution.py:1081
  41.5 25.6 %collective-permute-start.12 = (bf16[4112,128]{1,0:T(8,128)(2,1)}, bf16[4112,128]{1,0:T(8,128)(2,1)S(1)}, u32[]{:S(2)}, u32[]{:S(2)}) collective-permute-start(bf16[4112,128]{1,0:T(8,128)(2,1)} %get-tuple-element.179), channel_id=1, source_target_pairs={{0,8},{1,9},{2,10},{3,11},{4,12},{5,13},{6,14},{7,15},{8,16},{9,17... | collective-permute-start | bytes 3158024 | tf_op jit(solution)/shard_map/ppermute | solution.py:1081
  42.5 30.3 %collective-permute-start.11 = (bf16[4112,128]{1,0:T(8,128)(2,1)}, bf16[4112,128]{1,0:T(8,128)(2,1)S(1)}, u32[]{:S(2)}, u32[]{:S(2)}) collective-permute-start(bf16[4112,128]{1,0:T(8,128)(2,1)} %get-tuple-element.179), channel_id=1, source_target_pairs={{0,1},{1,0},{2,3},{3,2},{4,5},{5,4},{6,7},{7,6},{8,9},{9,8},{10,11... | collective-permute-start | bytes 3158024 | tf_op jit(solution)/shard_map/ppermute | solution.py:1081
  43.2 30.7 %collective-permute-start.10 = (bf16[4112,128]{1,0:T(8,128)(2,1)}, bf16[4112,128]{1,0:T(8,128)(2,1)S(1)}, u32[]{:S(2)}, u32[]{:S(2)}) collective-permute-start(bf16[4112,128]{1,0:T(8,128)(2,1)} %get-tuple-element.179), channel_id=1, source_target_pairs={{0,4},{1,5},{2,6},{3,7},{4,0},{5,1},{6,2},{7,3},{8,12},{9,13},{10,... | collective-permute-start | bytes 3158024 | tf_op jit(solution)/shard_map/ppermute | solution.py:1081
  52.0 112.9 %collective-permute-start.6 = (bf16[4112,128]{1,0:T(8,128)(2,1)S(1)}, bf16[4112,128]{1,0:T(8,128)(2,1)S(1)}, u32[]{:S(2)}, u32[]{:S(2)}) collective-permute-start(bf16[4112,128]{1,0:T(8,128)(2,1)S(1)} %get-tuple-element.364), channel_id=1, source_target_pairs={{0,2},{1,3},{2,0},{3,1},{4,6},{5,7},{6,4},{7,5},{8,10},{9,11},{10,... | collective-permute-start | bytes 3158024 | tf_op jit(solution)/shard_map/ppermute | solution.py:1081
  54.7 111.7 %collective-permute-start.9 = (bf16[4112,128]{1,0:T(8,128)(2,1)S(1)}, bf16[4112,128]{1,0:T(8,128)(2,1)}, u32[]{:S(2)}, u32[]{:S(2)}) collective-permute-start(bf16[4112,128]{1,0:T(8,128)(2,1)S(1)} %broadcast_select_fusion.8), channel_id=1, source_target_pairs={{0,2},{1,3},{2,0},{3,1},{4,6},{5,7},{6,4},{7,5},{8,10},{9,11},{10,... | collective-permute-start | bytes 3158024 | tf_op jit(solution)/shard_map/ppermute | solution.py:1081
  80.0 25.8 %collective-permute-start.19 = (bf16[4112,128]{1,0:T(8,128)(2,1)S(1)}, bf16[4112,128]{1,0:T(8,128)(2,1)S(1)}, u32[]{:S(2)}, u32[]{:S(2)}) collective-permute-start(bf16[4112,128]{1,0:T(8,128)(2,1)S(1)} %copy-done.68), channel_id=1, source_target_pairs={{0,8},{1,9},{2,10},{3,11},{4,12},{5,13},{6,14},{7,15},{8,16},{9,17... | collective-permute-start | bytes 3158024 | tf_op jit(solution)/shard_map/ppermute | solution.py:1081
  89.3 22.6 %collective-permute-start.18 = (bf16[4112,128]{1,0:T(8,128)(2,1)S(1)}, bf16[4112,128]{1,0:T(8,128)(2,1)S(1)}, u32[]{:S(2)}, u32[]{:S(2)}) collective-permute-start(bf16[4112,128]{1,0:T(8,128)(2,1)S(1)} %copy-done.68), channel_id=1, source_target_pairs={{0,1},{1,0},{2,3},{3,2},{4,5},{5,4},{6,7},{7,6},{8,9},{9,8},{10,11... | collective-permute-start | bytes 3158024 | tf_op jit(solution)/shard_map/ppermute | solution.py:1081
  90.6 22.2 %collective-permute-start.17 = (bf16[4112,128]{1,0:T(8,128)(2,1)S(1)}, bf16[4112,128]{1,0:T(8,128)(2,1)S(1)}, u32[]{:S(2)}, u32[]{:S(2)}) collective-permute-start(bf16[4112,128]{1,0:T(8,128)(2,1)S(1)} %copy-done.68), channel_id=1, source_target_pairs={{0,4},{1,5},{2,6},{3,7},{4,0},{5,1},{6,2},{7,3},{8,12},{9,13},{10,... | collective-permute-start | bytes 3158024 | tf_op jit(solution)/shard_map/ppermute | solution.py:1081
  105.8 60.6 %collective-permute-start.13 = (bf16[4112,128]{1,0:T(8,128)(2,1)S(1)}, bf16[4112,128]{1,0:T(8,128)(2,1)}, u32[]{:S(2)}, u32[]{:S(2)}) collective-permute-start(bf16[4112,128]{1,0:T(8,128)(2,1)S(1)} %broadcast_select_fusion.7), channel_id=1, source_target_pairs={{0,2},{1,3},{2,0},{3,1},{4,6},{5,7},{6,4},{7,5},{8,10},{9,11},{10,... | collective-permute-start | bytes 3158024 | tf_op jit(solution)/shard_map/ppermute | solution.py:1081
  128.3 20.8 %collective-permute-start.25 = (bf16[4112,128]{1,0:T(8,128)(2,1)S(1)}, bf16[4112,128]{1,0:T(8,128)(2,1)S(1)}, u32[]{:S(2)}, u32[]{:S(2)}) collective-permute-start(bf16[4112,128]{1,0:T(8,128)(2,1)S(1)} %copy-done.70), channel_id=1, source_target_pairs={{0,1},{1,0},{2,3},{3,2},{4,5},{5,4},{6,7},{7,6},{8,9},{9,8},{10,11... | collective-permute-start | bytes 3158024 | tf_op jit(solution)/shard_map/ppermute | solution.py:1081
  129.4 20.4 %collective-permute-start.24 = (bf16[4112,128]{1,0:T(8,128)(2,1)S(1)}, bf16[4112,128]{1,0:T(8,128)(2,1)S(1)}, u32[]{:S(2)}, u32[]{:S(2)}) collective-permute-start(bf16[4112,128]{1,0:T(8,128)(2,1)S(1)} %copy-done.70), channel_id=1, source_target_pairs={{0,4},{1,5},{2,6},{3,7},{4,0},{5,1},{6,2},{7,3},{8,12},{9,13},{10,... | collective-permute-start | bytes 3158024 | tf_op jit(solution)/shard_map/ppermute | solution.py:1081
  230.0 23.3 %collective-permute-start.30 = (bf16[1024,768]{1,0:T(8,128)(2,1)S(1)}, bf16[1024,768]{1,0:T(8,128)(2,1)S(1)}, u32[]{:S(2)}, u32[]{:S(2)}) collective-permute-start(bf16[1024,768]{1,0:T(8,128)(2,1)S(1)} %copy-done.107), channel_id=1, source_target_pairs={{0,2},{3,1},{4,6},{7,5},{8,10},{11,9},{12,14},{15,13},{16,18},{19,... | collective-permute-start | bytes 4718600 | tf_op jit(solution)/shard_map/ppermute | solution.py:1081
  267.4 20.5 %collective-permute-start.37 = (bf16[1024,768]{1,0:T(8,128)(2,1)S(1)}, bf16[1024,768]{1,0:T(8,128)(2,1)S(1)}, u32[]{:S(2)}, u32[]{:S(2)}) collective-permute-start(bf16[1024,768]{1,0:T(8,128)(2,1)S(1)} %get-tuple-element.228), channel_id=1, source_target_pairs={{0,2},{1,3},{2,0},{3,1},{4,6},{5,7},{6,4},{7,5},{8,10},{9,11},{10,... | collective-permute-start | bytes 4718600 | tf_op jit(solution)/shard_map/ppermute | solution.py:1081
  282.3 30.8 %collective-permute-start.36 = (bf16[1536,768]{1,0:T(8,128)(2,1)S(1)}, bf16[1536,768]{1,0:T(8,128)(2,1)S(1)}, u32[]{:S(2)}, u32[]{:S(2)}) collective-permute-start(bf16[1536,768]{1,0:T(8,128)(2,1)S(1)} %convolution_convert_fusion.2.own), channel_id=1, source_target_pairs={{1,0},{2,3},{5,4},{6,7},{9,8},{10,11},{13,12},{14,15},{17,16},{18,... | collective-permute-start | bytes 7077896 | tf_op jit(solution)/shard_map/ppermute | solution.py:1081
  322.3 31.9 %collective-permute-start.41 = (bf16[768,1536]{1,0:T(8,128)(2,1)S(1)}, bf16[768,1536]{1,0:T(8,128)(2,1)S(1)}, u32[]{:S(2)}, u32[]{:S(2)}) collective-permute-start(bf16[768,1536]{1,0:T(8,128)(2,1)S(1)} %copy-done.50), channel_id=1, source_target_pairs={{1,0},{2,3},{5,4},{6,7},{9,8},{10,11},{13,12},{14,15},{17,16},{18,... | collective-permute-start | bytes 7077896 | tf_op jit(solution)/shard_map/ppermute | solution.py:1081
  343.1 29.9 %collective-permute-start.39 = (bf16[1024,768]{1,0:T(8,128)(2,1)S(1)}, bf16[1024,768]{1,0:T(8,128)(2,1)S(1)}, u32[]{:S(2)}, u32[]{:S(2)}) collective-permute-start(bf16[1024,768]{1,0:T(8,128)(2,1)S(1)} %get-tuple-element.237.own), channel_id=1, source_target_pairs={{0,2},{1,3},{2,0},{3,1},{4,6},{5,7},{6,4},{7,5},{8,10},{9,11},{10,... | collective-permute-start | bytes 4718600 | tf_op jit(solution)/shard_map/ppermute | solution.py:1081
  355.9 40.5 %collective-permute-start.42 = (bf16[1536,768]{1,0:T(8,128)(2,1)}, bf16[1536,768]{1,0:T(8,128)(2,1)S(1)}, u32[]{:S(2)}, u32[]{:S(2)}) collective-permute-start(bf16[1536,768]{1,0:T(8,128)(2,1)} %get-tuple-element.251.own), channel_id=1, source_target_pairs={{1,0},{2,3},{5,4},{6,7},{9,8},{10,11},{13,12},{14,15},{17,16},{18,... | collective-permute-start | bytes 7077896 | tf_op jit(solution)/shard_map/ppermute | solution.py:1081
  359.8 36.6 %collective-permute-start.44 = (bf16[384,1536]{1,0:T(8,128)(2,1)}, bf16[384,1536]{1,0:T(8,128)(2,1)S(1)}, u32[]{:S(2)}, u32[]{:S(2)}) collective-permute-start(bf16[384,1536]{1,0:T(8,128)(2,1)} %shard_map.248), channel_id=1, source_target_pairs={{1,5},{2,6},{5,1},{6,2},{9,13},{10,14},{13,9},{14,10},{17,21},{18,... | collective-permute-start | bytes 3538952 | tf_op jit(solution)/shard_map/ppermute | solution.py:1081
  364.9 31.5 %collective-permute-start.43 = (bf16[384,768]{1,0:T(8,128)(2,1)S(1)}, bf16[384,768]{1,0:T(8,128)(2,1)S(1)}, u32[]{:S(2)}, u32[]{:S(2)}) collective-permute-start(bf16[384,768]{1,0:T(8,128)(2,1)S(1)} %copy-done.82), channel_id=1, source_target_pairs={{1,0},{2,3},{5,4},{6,7},{9,8},{10,11},{13,12},{14,15},{17,16},{18,... | collective-permute-start | bytes 1769480 | tf_op jit(solution)/shard_map/ppermute | solution.py:1081
  407.0 18.3 %collective-permute-start.46 = (bf16[1024,768]{1,0:T(8,128)(2,1)}, bf16[1024,768]{1,0:T(8,128)(2,1)}, u32[]{:S(2)}, u32[]{:S(2)}) collective-permute-start(bf16[1024,768]{1,0:T(8,128)(2,1)} %get-tuple-element.264.own), channel_id=1, source_target_pairs={{0,2},{1,3},{2,0},{3,1},{4,6},{5,7},{6,4},{7,5},{8,10},{9,11},{10,... | collective-permute-start | bytes 4718600 | tf_op jit(solution)/shard_map/ppermute | solution.py:1081
  409.2 15.1 %collective-permute-start.45 = (bf16[384,1152]{1,0:T(8,128)(2,1)}, bf16[384,1152]{1,0:T(8,128)(2,1)S(1)}, u32[]{:S(2)}, u32[]{:S(2)}) collective-permute-start(bf16[384,1152]{1,0:T(8,128)(2,1)} %get-tuple-element.257), channel_id=1, source_target_pairs={{1,0},{2,3},{5,4},{6,7},{9,8},{10,11},{13,12},{14,15},{17,16},{18,... | collective-permute-start | bytes 2654216 | tf_op jit(solution)/shard_map/ppermute | solution.py:1081
  413.6 23.4 %collective-permute-start.47 = (bf16[384,1536]{1,0:T(8,128)(2,1)}, bf16[384,1536]{1,0:T(8,128)(2,1)S(1)}, u32[]{:S(2)}, u32[]{:S(2)}) collective-permute-start(bf16[384,1536]{1,0:T(8,128)(2,1)} %shard_map.256), channel_id=1, source_target_pairs={{1,0},{2,3},{5,4},{6,7},{9,8},{10,11},{13,12},{14,15},{17,16},{18,... | collective-permute-start | bytes 3538952 | tf_op jit(solution)/shard_map/ppermute | solution.py:1081
  438.0 29.1 %collective-permute-start.49 = (bf16[1536,384]{1,0:T(8,128)(2,1)}, bf16[1536,384]{1,0:T(8,128)(2,1)S(1)}, u32[]{:S(2)}, u32[]{:S(2)}) collective-permute-start(bf16[1536,384]{1,0:T(8,128)(2,1)} %get-tuple-element.268.own), channel_id=1, source_target_pairs={{1,5},{2,6},{5,1},{6,2},{9,13},{10,14},{13,9},{14,10},{17,21},{18,... | collective-permute-start | bytes 3538952 | tf_op jit(solution)/shard_map/ppermute | solution.py:1081
  441.5 25.6 %collective-permute-start.50 = (bf16[384,1152]{1,0:T(8,128)(2,1)}, bf16[384,1152]{1,0:T(8,128)(2,1)S(1)}, u32[]{:S(2)}, u32[]{:S(2)}) collective-permute-start(bf16[384,1152]{1,0:T(8,128)(2,1)} %shard_map.259), channel_id=1, source_target_pairs={{1,0},{2,3},{5,4},{6,7},{9,8},{10,11},{13,12},{14,15},{17,16},{18,... | collective-permute-start | bytes 2654216 | tf_op jit(solution)/shard_map/ppermute | solution.py:1081
  443.7 23.4 %collective-permute-start.51 = (bf16[384,768]{1,0:T(8,128)(2,1)S(1)}, bf16[384,768]{1,0:T(8,128)(2,1)S(1)}, u32[]{:S(2)}, u32[]{:S(2)}) collective-permute-start(bf16[384,768]{1,0:T(8,128)(2,1)S(1)} %convolution_convert_fusion.6.own), channel_id=1, source_target_pairs={{1,0},{2,3},{5,4},{6,7},{9,8},{10,11},{13,12},{14,15},{17,16},{18,... | collective-permute-start | bytes 1769480 | tf_op jit(solution)/shard_map/ppermute | solution.py:1081
  472.1 18.3 %collective-permute-start.53 = (bf16[1536,384]{1,0:T(8,128)(2,1)}, bf16[1536,384]{1,0:T(8,128)(2,1)S(1)}, u32[]{:S(2)}, u32[]{:S(2)}) collective-permute-start(bf16[1536,384]{1,0:T(8,128)(2,1)} %shard_map.267), channel_id=1, source_target_pairs={{1,0},{2,3},{5,4},{6,7},{9,8},{10,11},{13,12},{14,15},{17,16},{18,... | collective-permute-start | bytes 3538952 | tf_op jit(solution)/shard_map/ppermute | solution.py:1081
  497.1 20.2 %collective-permute-start.55 = (bf16[4112,128]{1,0:T(8,128)(2,1)S(1)}, bf16[4112,128]{1,0:T(8,128)(2,1)S(1)}, u32[]{:S(2)}, u32[]{:S(2)}) collective-permute-start(bf16[4112,128]{1,0:T(8,128)(2,1)S(1)} %get-tuple-element.363), channel_id=1, source_target_pairs={{0,4},{3,7},{4,0},{7,3},{8,12},{11,15},{12,8},{15,11},{16,20},{19,... | collective-permute-start | bytes 3158024 | tf_op jit(solution)/shard_map/ppermute | solution.py:1081
  499.9 42.7 %collective-permute-start.59 = (bf16[4112,128]{1,0:T(8,128)(2,1)S(1)}, bf16[4112,128]{1,0:T(8,128)(2,1)S(1)}, u32[]{:S(2)}, u32[]{:S(2)}) collective-permute-start(bf16[4112,128]{1,0:T(8,128)(2,1)S(1)} %get-tuple-element.361), channel_id=1, source_target_pairs={{0,4},{3,7},{4,0},{7,3},{8,12},{11,15},{12,8},{15,11},{16,20},{19,... | collective-permute-start | bytes 3158024 | tf_op jit(solution)/shard_map/ppermute | solution.py:1081
  503.0 33.4 %collective-permute-start.58 = (bf16[4112,128]{1,0:T(8,128)(2,1)S(1)}, bf16[4112,128]{1,0:T(8,128)(2,1)S(1)}, u32[]{:S(2)}, u32[]{:S(2)}) collective-permute-start(bf16[4112,128]{1,0:T(8,128)(2,1)S(1)} %get-tuple-element.362), channel_id=1, source_target_pairs={{0,4},{3,7},{4,0},{7,3},{8,12},{11,15},{12,8},{15,11},{16,20},{19,... | collective-permute-start | bytes 3158024 | tf_op jit(solution)/shard_map/ppermute | solution.py:1081
  521.6 23.7 %collective-permute-start.60 = (bf16[4112,128]{1,0:T(8,128)(2,1)}, bf16[4112,128]{1,0:T(8,128)(2,1)S(1)}, u32[]{:S(2)}, u32[]{:S(2)}) collective-permute-start(bf16[4112,128]{1,0:T(8,128)(2,1)} %get-tuple-element.310), channel_id=1, source_target_pairs={{0,8},{3,11},{4,12},{7,15},{8,16},{11,19},{12,20},{15,23},{16,24},... | collective-permute-start | bytes 3158024 | tf_op jit(solution)/shard_map/ppermute | solution.py:1081
  526.7 50.0 %collective-permute-start.56 = (bf16[1024,768]{1,0:T(8,128)(2,1)S(1)}, bf16[1024,768]{1,0:T(8,128)(2,1)S(1)}, u32[]{:S(2)}, u32[]{:S(2)}) collective-permute-start(bf16[1024,768]{1,0:T(8,128)(2,1)S(1)} %add_convert_fusion), channel_id=1, source_target_pairs={{0,2},{1,3},{2,0},{3,1},{4,6},{5,7},{6,4},{7,5},{8,10},{9,11},{10,... | collective-permute-start | bytes 4718600 | tf_op jit(solution)/shard_map/ppermute | solution.py:1081
  526.8 25.2 %collective-permute-start.61 = (bf16[4112,128]{1,0:T(8,128)(2,1)S(1)}, bf16[4112,128]{1,0:T(8,128)(2,1)S(1)}, u32[]{:S(2)}, u32[]{:S(2)}) collective-permute-start(bf16[4112,128]{1,0:T(8,128)(2,1)S(1)} %get-tuple-element.360), channel_id=1, source_target_pairs={{0,4},{3,7},{4,0},{7,3},{8,12},{11,15},{12,8},{15,11},{16,20},{19,... | collective-permute-start | bytes 3158024 | tf_op jit(solution)/shard_map/ppermute | solution.py:1081
  540.7 18.7 %collective-permute-start.62 = (bf16[4112,128]{1,0:T(8,128)(2,1)}, bf16[4112,128]{1,0:T(8,128)(2,1)S(1)}, u32[]{:S(2)}, u32[]{:S(2)}) collective-permute-start(bf16[4112,128]{1,0:T(8,128)(2,1)} %get-tuple-element.313), channel_id=1, source_target_pairs={{0,8},{3,11},{4,12},{7,15},{8,16},{11,19},{12,20},{15,23},{16,24},... | collective-permute-start | bytes 3158024 | tf_op jit(solution)/shard_map/ppermute | solution.py:1081
  542.6 23.2 %collective-permute-start.63 = (bf16[4112,128]{1,0:T(8,128)(2,1)S(1)}, bf16[4112,128]{1,0:T(8,128)(2,1)S(1)}, u32[]{:S(2)}, u32[]{:S(2)}) collective-permute-start(bf16[4112,128]{1,0:T(8,128)(2,1)S(1)} %copy-done.118), channel_id=1, source_target_pairs={{0,4},{3,7},{4,0},{7,3},{8,12},{11,15},{12,8},{15,11},{16,20},{19,... | collective-permute-start | bytes 3158024 | tf_op jit(solution)/shard_map/ppermute | solution.py:1081
  550.1 20.6 %collective-permute-start.64 = (bf16[4112,128]{1,0:T(8,128)(2,1)}, bf16[4112,128]{1,0:T(8,128)(2,1)S(1)}, u32[]{:S(2)}, u32[]{:S(2)}) collective-permute-start(bf16[4112,128]{1,0:T(8,128)(2,1)} %get-tuple-element.318), channel_id=1, source_target_pairs={{0,8},{3,11},{4,12},{7,15},{8,16},{11,19},{12,20},{15,23},{16,24},... | collective-permute-start | bytes 3158024 | tf_op jit(solution)/shard_map/ppermute | solution.py:1081
  552.0 50.5 %collective-permute-start.54 = (bf16[1024,768]{1,0:T(8,128)(2,1)S(1)}, bf16[1024,768]{1,0:T(8,128)(2,1)}, u32[]{:S(2)}, u32[]{:S(2)}) collective-permute-start(bf16[1024,768]{1,0:T(8,128)(2,1)S(1)} %copy-done.49), channel_id=1, source_target_pairs={{0,1},{3,2},{4,5},{7,6},{8,9},{11,10},{12,13},{15,14},{16,17},{19,... | collective-permute-start | bytes 4718600 | tf_op jit(solution)/shard_map/ppermute | solution.py:1081
  559.4 23.1 %collective-permute-start.65 = (bf16[4112,128]{1,0:T(8,128)(2,1)}, bf16[4112,128]{1,0:T(8,128)(2,1)}, u32[]{:S(2)}, u32[]{:S(2)}) collective-permute-start(bf16[4112,128]{1,0:T(8,128)(2,1)} %get-tuple-element.320), channel_id=1, source_target_pairs={{0,4},{3,7},{4,0},{7,3},{8,12},{11,15},{12,8},{15,11},{16,20},{19,... | collective-permute-start | bytes 3158024 | tf_op jit(solution)/shard_map/ppermute | solution.py:1081
  565.8 18.9 %collective-permute-start.66 = (bf16[4112,128]{1,0:T(8,128)(2,1)}, bf16[4112,128]{1,0:T(8,128)(2,1)}, u32[]{:S(2)}, u32[]{:S(2)}) collective-permute-start(bf16[4112,128]{1,0:T(8,128)(2,1)} %get-tuple-element.323), channel_id=1, source_target_pairs={{0,8},{3,11},{4,12},{7,15},{8,16},{11,19},{12,20},{15,23},{16,24},... | collective-permute-start | bytes 3158024 | tf_op jit(solution)/shard_map/ppermute | solution.py:1081
  570.7 20.4 %collective-permute-start.67 = (bf16[4112,128]{1,0:T(8,128)(2,1)}, bf16[4112,128]{1,0:T(8,128)(2,1)}, u32[]{:S(2)}, u32[]{:S(2)}) collective-permute-start(bf16[4112,128]{1,0:T(8,128)(2,1)} %get-tuple-element.325), channel_id=1, source_target_pairs={{0,4},{3,7},{4,0},{7,3},{8,12},{11,15},{12,8},{15,11},{16,20},{19,... | collective-permute-start | bytes 3158024 | tf_op jit(solution)/shard_map/ppermute | solution.py:1081
  577.8 18.8 %collective-permute-start.68 = (bf16[4112,128]{1,0:T(8,128)(2,1)}, bf16[4112,128]{1,0:T(8,128)(2,1)}, u32[]{:S(2)}, u32[]{:S(2)}) collective-permute-start(bf16[4112,128]{1,0:T(8,128)(2,1)} %shard_map.284), channel_id=1, source_target_pairs={{0,8},{3,11},{4,12},{7,15},{8,16},{11,19},{12,20},{15,23},{16,24},... | collective-permute-start | bytes 3158024 | tf_op jit(solution)/shard_map/ppermute | solution.py:1081
  582.5 21.9 %collective-permute-start.57 = (bf16[1024,384]{1,0:T(8,128)(2,1)}, bf16[1024,384]{1,0:T(8,128)(2,1)}, u32[]{:S(2)}, u32[]{:S(2)}) collective-permute-start(bf16[1024,384]{1,0:T(8,128)(2,1)} %select_convert_fusion), channel_id=1, source_target_pairs={{0,1},{3,2},{4,5},{7,6},{8,9},{11,10},{12,13},{15,14},{16,17},{19,... | collective-permute-start | bytes 2359304 | tf_op jit(solution)/shard_map/ppermute | solution.py:1081
  584.7 22.5 %collective-permute-start.69 = (bf16[4112,128]{1,0:T(8,128)(2,1)}, bf16[4112,128]{1,0:T(8,128)(2,1)}, u32[]{:S(2)}, u32[]{:S(2)}) collective-permute-start(bf16[4112,128]{1,0:T(8,128)(2,1)} %get-tuple-element.329), channel_id=1, source_target_pairs={{0,4},{3,7},{4,0},{7,3},{8,12},{11,15},{12,8},{15,11},{16,20},{19,... | collective-permute-start | bytes 3158024 | tf_op jit(solution)/shard_map/ppermute | solution.py:1081
  591.0 18.8 %collective-permute-start.70 = (bf16[4112,128]{1,0:T(8,128)(2,1)}, bf16[4112,128]{1,0:T(8,128)(2,1)}, u32[]{:S(2)}, u32[]{:S(2)}) collective-permute-start(bf16[4112,128]{1,0:T(8,128)(2,1)} %shard_map.286), channel_id=1, source_target_pairs={{0,8},{3,11},{4,12},{7,15},{8,16},{11,19},{12,20},{15,23},{16,24},... | collective-permute-start | bytes 3158024 | tf_op jit(solution)/shard_map/ppermute | solution.py:1081
  599.9 15.0 %collective-permute-start.71 = (bf16[4112,128]{1,0:T(8,128)(2,1)}, bf16[4112,128]{1,0:T(8,128)(2,1)}, u32[]{:S(2)}, u32[]{:S(2)}) collective-permute-start(bf16[4112,128]{1,0:T(8,128)(2,1)} %shard_map.289), channel_id=1, source_target_pairs={{0,2},{3,1},{4,6},{7,5},{8,10},{11,9},{12,14},{15,13},{16,18},{19,... | collective-permute-start | bytes 3158024 | tf_op jit(solution)/shard_map/ppermute | solution.py:1081
  (148 other events, 910.9 us)

commit v14 on v13

--- a/solution.py
+++ b/solution.py
@@ -1299,36 +1299,36 @@
     gu1 = dot_tn(caches[top][8], du).astype(bf16)
     ad1 = over(gd1)
     lse, gu1 = fence(caches[top][6], gu1)
+    xu1 = beside(gu1)
     grad, grad_low, dq, dk, dv, dbo = attend_step(top, grad, part, other, lse)
-    vec, dbo, ad1, gu1, out_low = hold(vec, dbo, ad1, gu1, out_low)
-    au1 = over(gu1)
+    vec, dbo, ad1, xu1, out_low = hold(vec, dbo, ad1, xu1, out_low)
+    au1 = over(summed(gu1, xu1))
     own, dg1, ds1, dbq, dbv = qkv_back_call(top, dq, dk, dv, caches[top][0], vec, weights)
     recv = send(own, routes.core_all)
     go1 = dot_tn(caches[top][5], grad_low).astype(bf16)
     gq1 = dot_tn(caches[top][1], jnp.concatenate([dq, dk, dv], axis=1)).astype(bf16)
     vec_grads[top] = [dg1, ds1, dbq, dbv, dbo, dg2, ds2, db1, db2]
+    xq1, ao1 = beside(gq1), over(go1)
     grad, grad_low, du, part, dg2, ds2, db1, db2 = mlp_step(low, grad, own, recv)
     other = send(part, routes.core_all)
-    db2, go1, gq1 = hold(db2, go1, gq1)
-    xq1, ao1 = beside(gq1), over(go1)
+    db2, xq1, au1 = hold(db2, xq1, au1)
+    aq1 = over(summed(gq1, xq1))
     gd0 = dot_tn(caches[low][9], grad_low).astype(bf16)
     gu0 = dot_tn(caches[low][8], du).astype(bf16)
-    lse, gd0, gu0, xq1, au1 = hold(caches[low][6], gd0, gu0, xq1, au1)
-    hq1 = summed(gq1, xq1)
+    lse, gd0, gu0, ao1, aq1 = hold(caches[low][6], gd0, gu0, ao1, aq1)
     ad0 = over(gd0)
     xu0 = beside(gu0)
     buffer = place_tiles(("down", top), gd1, ad1, None)
     buffer = place_tiles(("up", top), gu1, au1, buffer)
     grad, grad_low, dq, dk, dv, dbo = attend_step(low, grad, part, other, lse)
-    vec, dbo, ad0, ao1, xu0, hq1, buffer = hold(vec, dbo, ad0, ao1, xu0, hq1, buffer)
+    vec, dbo, ad0, xu0, buffer = hold(vec, dbo, ad0, xu0, buffer)
     au0 = over(summed(gu0, xu0))
-    aq1 = over(hq1)
     own, dg1, ds1, dbq, dbv = qkv_back_call(low, dq, dk, dv, caches[low][0], vec, weights)
     recv = send(own, routes.core_all)
     gq0 = dot_tn(caches[low][1], jnp.concatenate([dq, dk, dv], axis=1)).astype(bf16)
     vec_grads[low] = [dg1, ds1, dbq, dbv, dbo, dg2, ds2, db1, db2]
     xq0 = beside(gq0)
-    turn, aq1 = hold(jnp.zeros((8, BS), f32), aq1)
+    turn = jnp.zeros((8, BS), f32)
     grad_emb, grad_emb_bias = embed_back_call(core_flag, turn, grad, own, recv)
     middle = CHUNKS // 2
 
@@ -1346,10 +1346,10 @@
     buffer = place_tiles(("out", top), go1, ao1, buffer)
     buffer = place_tiles(("qkv", top), gq1, aq1, buffer)
     buffer = place_tiles(("down", low), gd0, ad0, buffer)
+    gbm, xb, aq0, ao0, av, buffer = hold(gbm, xb, aq0, ao0, av, buffer)
+    ab = over(half_sum(half_at * 0, gbm, xb)) if grid3 else None
     buffer = place_tiles(("up", low), gu0, au0, buffer)
     buffer = place_base(1, gbt, None, buffer)
-    gbm, xb, aq0, ao0, av, buffer = hold(gbm, xb, aq0, ao0, av, buffer)
-    ab = over(half_sum(half_at * 0, gbm, xb)) if grid3 else None
     buffer = place_tiles(("out", low), go0, ao0, buffer)
     buffer = scatter_vec(vec_pos, vec_grad, av, buffer)
     buffer = place_tiles(("qkv", low), gq0, aq0, buffer)

time: 635 us -> 637 us (level)
  starting transfers between devices: 100 us -> 120 us
  Pallas kernels: 289 us -> 282 us
  waiting for transfers between devices: 129 us -> 122 us
    ppermute x72 -> x73, starting transfers between devices: 100 us -> 120 us  [send(): return lax.ppermute(value, AXES, route)]
    ppermute x72 -> x73, waiting for transfers between devices: 129 us -> 122 us  [send(): return lax.ppermute(value, AXES, route)]
    pallas_call x4 -> x5, Pallas kernels: 11.2 us -> 14.3 us  [half_sum(): pl.pallas_call(half_sum_kernel, out_shape=pltpu.HBM(block, bf16), grid_sp...]
    unnamed x254 -> x228, local copies, waits for them, and re-layouts: 29.4 us -> 26.9 us
  transfers between devices with their start and end apart: 72 -> 73, of which waited for: 33 -> 34; matrix products, arithmetic and copies ran while one was open for 10% -> 10% of each run, Pallas kernels for 32% -> 32%
where the time goes in v14:
time: 637 us; the launch traced here: 628 us
  Pallas kernels  282 us (44%)
  waiting for transfers between devices  122 us (19%)
  starting transfers between devices  120 us (19%)
  local copies, waits for them, and re-layouts  41.8 us (7%)
  matrix products  30.8 us (5%)
  other arithmetic  28.9 us (5%)
    ppermute x73, waiting for transfers between devices, send(): return lax.ppermute(value, AXES, route)  122 us
    ppermute x73, starting transfers between devices, send(): return lax.ppermute(value, AXES, route)  120 us
    pallas_call x2, Pallas kernels, attend_back_call(): pl.pallas_call(attend_back_kernel, out_shape=[shape(D, f32), shape(D, bf1...  40.9 us
    pallas_call x10, Pallas kernels, scatter_matrix(): pl.pallas_call(functools.partial(scatter_kernel, rows_n, cols_n, steps, p...  35.2 us
    dot_general x12, matrix products, dot_tn(): lax.dot_general(left, right, (((0,), (0,)), ((), ())), preferred_element_...  27.7 us
    pallas_call x8, Pallas kernels, reduce_call(): pl.pallas_call(functools.partial(reduce_kernel, carried is not None, last...  27 us
    unnamed x228, local copies, waits for them, and re-layouts  26.9 us
    pallas_call x2, Pallas kernels, attend_call(): pl.pallas_call(functools.partial(attend_kernel, layer), out_shape=[jax.Sh...  26.5 us
  transfers between devices with their start and end apart: 73, of which 34 were waited for; matrix products, arithmetic and copies ran while one was open for 10% of the time, Pallas kernels for 32%

profile of v14, /device:TPU:0, one launch (start us, length us, event | category | flops | bytes accessed | tf_op | source)
XLA Modules:
  0.0 627.7 jit_solution(7266512324443641053)
XLA Ops:
  18.9 6.0 shard_map.222.refs_3_
  26.1 6.1 collective-permute-done.5.refs_5_
  43.7 6.5 %shard_map.224.refs_3_ = bf16[1024,768]{1,0:T(8,128)(2,1)S(1)} custom-call(s32[4,3]{1,0:T(4,128)S(1)} %convert_element_type.120.present, s32[1]{0:T(128)} %bitcast.6.half.part, bf16[1024,768]{1,0:T(8,128)(2,1)} %get-tuple-element.173.patch_ref.refs_2_, s32[1024,1]{1,0:T(8,128)S(1)} %copy.141.class_ref, bf16[3,3072,768]{2,1,0:T(8,128)(2,1)} %pinv_ref.9), custom_call_target="tpu_custom_call" | custom-call | flops 1811939328 | bytes 6684672 | tf_op jit(solution)/shard_map/pallas_call | solution.py:439
  54.7 12.4 %collective-permute-done.9.refs_4_ = bf16[4112,128]{1,0:T(8,128)(2,1)S(1)} collective-permute-done((bf16[4112,128]{1,0:T(8,128)(2,1)}, bf16[4112,128]{1,0:T(8,128)(2,1)S(1)}, u32[]{:S(2)}, u32[]{:S(2)}) %collective-permute-start.9) | collective-permute-done | bytes 1052704 | tf_op jit(solution)/shard_map/ppermute | solution.py:1081
  67.1 5.7 collective-permute-done.8.refs_1_
  80.8 6.0 shard_map.226.refs_3_
  93.6 12.3 %collective-permute-done.12.refs_4_ = bf16[4112,128]{1,0:T(8,128)(2,1)S(1)} collective-permute-done((bf16[4112,128]{1,0:T(8,128)(2,1)S(1)}, bf16[4112,128]{1,0:T(8,128)(2,1)S(1)}, u32[]{:S(2)}, u32[]{:S(2)}) %collective-permute-start.12) | collective-permute-done | bytes 1052704 | tf_op jit(solution)/shard_map/ppermute | solution.py:1081
  105.8 6.1 collective-permute-done.11.refs_1_
  119.8 6.2 shard_map.228.refs_3_
  132.4 16.6 %collective-permute-done.14.refs_1_ = bf16[4112,128]{1,0:T(8,128)(2,1)S(1)} collective-permute-done((bf16[4112,128]{1,0:T(8,128)(2,1)S(1)}, bf16[4112,128]{1,0:T(8,128)(2,1)S(1)}, u32[]{:S(2)}, u32[]{:S(2)}) %collective-permute-start.14) | collective-permute-done | bytes 1052704 | tf_op jit(solution)/shard_map/ppermute | solution.py:1081
  156.9 5.7 collective-permute-done.28
  172.9 14.2 %shard_map.230 = (bf16[3072,384]{1,0:T(8,128)(2,1)}, bf16[2304,384]{1,0:T(8,128)(2,1)}, bf16[768,384]{1,0:T(8,128)(2,1)}, bf16[3072,384]{1,0:T(8,128)(2,1)}, bf1...) custom-call(s32[16]{0:T(128)S(1)} %stack.95.owner, ...), custom_call_target="tpu_custom_call" | custom-call | bytes 33030144 | tf_op jit(solution)/shard_map/pallas_call | solution.py:243
  187.3 6.8 %shard_map.231.refs_0_ = bf16[1024,384]{1,0:T(8,128)(2,1)S(1)} custom-call(s32[1]{0:T(128)} %bitcast.6.half.part, bf16[1024,768]{1,0:T(8,128)(2,1)} %get-tuple-element.171.refs_0_, bf16[1024,768]{1,0:T(8,128)(2,1)} %get-tuple-element.174.refs_1_, bf16[1024,768]{1,0:T(8,128)(2,1)} %get-tuple-element.177.refs_2_, ...), custom_call_target="tpu_custom_call" | custom-call | flops 2415919104 | bytes 9437184 | tf_op jit(solution)/shard_map/pallas_call | solution.py:552
  196.6 4.8 shard_map.232
  201.5 13.2 %shard_map.233 = (bf16[1024,384]{1,0:T(8,128)(2,1)S(1)}, f32[8,1024]{1,0:T(8,128)S(1)}, bf16[1024,768]{1,0:T(8,128)(2,1)S(1)}) custom-call(s32[4]{0:T(128)S(1)} %get-tuple-element.375.low_ref, s32[4]{0:T(128)S(1)} %get-tuple-element.368.high_ref, bf16[1024,384]{1,0:T(8,128)(2,1)S(1)} %get-tuple-element.194.q_ref, ...), custom_call_target="tpu_custom_call" | custom-call | flops 6442450944 | bytes 6291456 | tf_op jit(solution)/shard_map/pallas_call | solution.py:679
  219.2 9.4 %shard_map.234 = (f32[1024,768]{1,0:T(8,128)S(1)}, bf16[1024,768]{1,0:T(8,128)(2,1)}, bf16[1024,1536]{1,0:T(8,128)(2,1)}, bf16[1024,1536]{1,0:T(8,128)(2,1)}, bf16[1024,768]{1,0:T(8,128)(2,1)S(1)}) custom-call(f32[1024,768]{1,0:T(8,128)S(1)} %get-tuple-element.193.base.hid, bf16[1024,768]{1,0:T(8,128)(2,1)S(1)} %get-tuple-element.198.own, ...), custom_call_target="tpu_custom_call" | custom-call | flops 4831838208 | bytes 18874368 | tf_op jit(solution)/shard_map/pallas_call | solution.py:742
  232.0 4.4 shard_map.235
  236.4 13.2 %shard_map.236 = (bf16[1024,384]{1,0:T(8,128)(2,1)S(1)}, f32[8,1024]{1,0:T(8,128)S(1)}, bf16[1024,768]{1,0:T(8,128)(2,1)S(1)}) custom-call(s32[4]{0:T(128)S(1)} %get-tuple-element.375.low_ref, s32[4]{0:T(128)S(1)} %get-tuple-element.368.high_ref, bf16[1024,384]{1,0:T(8,128)(2,1)S(1)} %get-tuple-element.205.q_ref, ...), custom_call_target="tpu_custom_call" | custom-call | flops 6442450944 | bytes 6291456 | tf_op jit(solution)/shard_map/pallas_call | solution.py:679
  253.2 9.4 %shard_map.237 = (f32[1024,768]{1,0:T(8,128)S(1)}, bf16[1024,768]{1,0:T(8,128)(2,1)}, bf16[1024,1536]{1,0:T(8,128)(2,1)}, bf16[1024,1536]{1,0:T(8,128)(2,1)}, bf16[1024,768]{1,0:T(8,128)(2,1)S(1)}) custom-call(f32[1024,768]{1,0:T(8,128)S(1)} %get-tuple-element.204.base.hid, bf16[1024,768]{1,0:T(8,128)(2,1)S(1)} %get-tuple-element.209.own, ...), custom_call_target="tpu_custom_call" | custom-call | flops 4831838208 | bytes 18874368 | tf_op jit(solution)/shard_map/pallas_call | solution.py:742
  264.6 11.3 %shard_map.238 = (bf16[1024,768]{1,0:T(8,128)(2,1)S(1)}, bf16[1024,1536]{1,0:T(8,128)(2,1)S(1)}, bf16[1024,768]{1,0:T(8,128)(2,1)S(1)}, f32[1,768]{1,0:T(1,128)S...) custom-call(bf16[1024,768]{1,0:T(8,128)(2,1)S(1)} %broadcast_select_fusion.refs_0_, ...), custom_call_target="tpu_custom_call" | custom-call | flops 4831838208 | bytes 18874368 | tf_op jit(solution)/shard_map/pallas_call | solution.py:794
  280.4 4.1 convolution_convert_fusion.3.refs_1_
  289.9 20.4 %shard_map.240 = (f32[1024,768]{1,0:T(8,128)S(1)}, bf16[1024,768]{1,0:T(8,128)(2,1)S(1)}, bf16[1024,384]{1,0:T(8,128)(2,1)S(1)}, bf16[1024,384]{1,0:T(8,128)(2,1...) custom-call(s32[4]{0:T(128)S(1)} %get-tuple-element.374.low_ref, s32[4]{0:T(128)S(1)} %get-tuple-element.369.high_ref, ...), custom_call_target="tpu_custom_call" | custom-call | flops 11274289152 | bytes 15728640 | tf_op jit(solution)/shard_map/pallas_call | solution.py:886
  312.2 5.5 shard_map.243
  317.8 4.1 collective-permute-start.39
  334.8 11.2 %shard_map.244 = (f32[1024,768]{1,0:T(8,128)S(1)}, bf16[1024,768]{1,0:T(8,128)(2,1)S(1)}, bf16[1024,1536]{1,0:T(8,128)(2,1)S(1)}, bf16[1024,768]{1,0:T(8,128)(2,...) custom-call(f32[1024,768]{1,0:T(8,128)S(1)} %get-tuple-element.221.refs_0_, ...), custom_call_target="tpu_custom_call" | custom-call | flops 4831838208 | bytes 18874368 | tf_op jit(solution)/shard_map/pallas_call | solution.py:794
  351.5 3.9 collective-permute-start.40
  355.4 4.0 convolution_convert_fusion.1.refs_1_
  359.4 4.0 convolution_convert_fusion.refs_2_
  363.4 3.9 collective-permute-done.44.refs_4_
  372.9 4.2 shard_map.252.refs_1_
  377.2 4.0 shard_map.253.refs_4_
  381.2 20.4 %shard_map.250 = (f32[1024,768]{1,0:T(8,128)S(1)}, bf16[1024,768]{1,0:T(8,128)(2,1)S(1)}, bf16[1024,384]{1,0:T(8,128)(2,1)S(1)}, bf16[1024,384]{1,0:T(8,128)(2,1...) custom-call(s32[4]{0:T(128)S(1)} %get-tuple-element.374.low_ref, s32[4]{0:T(128)S(1)} %get-tuple-element.369.high_ref, ...), custom_call_target="tpu_custom_call" | custom-call | flops 11274289152 | bytes 15728640 | tf_op jit(solution)/shard_map/pallas_call | solution.py:886
  403.5 5.6 shard_map.255
  425.3 5.4 collective-permute-done.48.refs_1_
  444.9 4.2 shard_map.264.refs_5_
  453.7 9.8 %collective-permute-done.52.refs_3_ = bf16[384,768]{1,0:T(8,128)(2,1)S(1)} collective-permute-done((bf16[384,768]{1,0:T(8,128)(2,1)S(1)}, bf16[384,768]{1,0:T(8,128)(2,1)S(1)}, u32[]{:S(2)}, u32[]{:S(2)}) %collective-permute-start.52) | collective-permute-done | bytes 589856 | tf_op jit(solution)/shard_map/ppermute | solution.py:1081
  470.5 4.0 shard_map.267.refs_0_
  481.4 3.6 shard_map.271.refs_1_
  502.8 10.2 %shard_map.274.refs_2_ = bf16[3,384,768]{2,1,0:T(8,128)(2,1)S(1)} custom-call(bf16[3072,384]{1,0:T(8,128)(2,1)} %get-tuple-element.297.base, bf16[3,3072,768]{2,1,0:T(8,128)(2,1)} %pinv_ref.9), custom_call_target="tpu_custom_call" | custom-call | flops 5435817984 | bytes 14155776 | tf_op jit(solution)/shard_map/pallas_call | solution.py:470
  518.6 10.0 %collective-permute-start.61 = (bf16[4112,128]{1,0:T(8,128)(2,1)}, bf16[4112,128]{1,0:T(8,128)(2,1)S(1)}, u32[]{:S(2)}, u32[]{:S(2)}) collective-permute-start(bf16[4112,128]{1,0:T(8,128)(2,1)} %get-tuple-element.302), channel_id=1, source_target_pairs={{0,8},{3,11},{4,12},{7,15},{8,16},{11,19},{12,20},{15,23},{16,24},... | collective-permute-start | bytes 3158024 | tf_op jit(solution)/shard_map/ppermute | solution.py:1081
  538.0 8.3 %collective-permute-start.63 = (bf16[4112,128]{1,0:T(8,128)(2,1)}, bf16[4112,128]{1,0:T(8,128)(2,1)S(1)}, u32[]{:S(2)}, u32[]{:S(2)}) collective-permute-start(bf16[4112,128]{1,0:T(8,128)(2,1)} %get-tuple-element.305), channel_id=1, source_target_pairs={{0,8},{3,11},{4,12},{7,15},{8,16},{11,19},{12,20},{15,23},{16,24},... | collective-permute-start | bytes 3158024 | tf_op jit(solution)/shard_map/ppermute | solution.py:1081
  546.4 3.9 collective-permute-start.64
  551.3 3.7 shard_map.281
  555.0 3.8 collective-permute-start.65
  563.8 3.6 shard_map.283
  586.6 3.6 collective-permute-start.70
  608.6 3.7 collective-permute-done.71.refs_2_
  618.5 8.7 %shard_map.291 = (f32[32,128,128]{2,1,0:T(8,128)}, f32[32,128,128]{2,1,0:T(8,128)}, f32[32,128,128]{2,1,0:T(8,128)}, f32[32,128,128]{2,1,0:T(8,128)}) custom-call(s32[32]{0:T(128)S(1)} %convert_element_type.148.used, s32[1]{0:T(128)} %bitcast.27.flag.home, bf16[4112,128]{1,0:T(8,128)(2,1)} %shard_map.289.near, ...), custom_call_target="tpu_custom_call" | custom-call | flops 5905580032 | bytes 19922944 | tf_op jit(solution)/shard_map/pallas_call | solution.py:1011
  (496 shorter events, 266.4 us)
Async XLA Ops:
  4.2 28.6 %collective-permute-start.4 = (bf16[4112,128]{1,0:T(8,128)(2,1)}, bf16[4112,128]{1,0:T(8,128)(2,1)}, u32[]{:S(2)}, u32[]{:S(2)}) collective-permute-start(bf16[4112,128]{1,0:T(8,128)(2,1)} %pad_maximum_fusion.2), channel_id=1, source_target_pairs={{0,8},{1,9},{2,10},{3,11},{4,12},{5,13},{6,14},{7,15},{8,16},{9,17... | collective-permute-start | bytes 3158024 | tf_op jit(solution)/shard_map/ppermute | solution.py:1081
  7.2 25.6 %collective-permute-start.1 = (bf16[4112,128]{1,0:T(8,128)(2,1)}, bf16[4112,128]{1,0:T(8,128)(2,1)S(1)}, u32[]{:S(2)}, u32[]{:S(2)}) collective-permute-start(bf16[4112,128]{1,0:T(8,128)(2,1)} %pad_maximum_fusion.2), channel_id=1, source_target_pairs={{0,1},{1,0},{2,3},{3,2},{4,5},{5,4},{6,7},{7,6},{8,9},{9,8},{10,11... | collective-permute-start | bytes 3158024 | tf_op jit(solution)/shard_map/ppermute | solution.py:1081
  8.7 24.6 %collective-permute-start = (bf16[4112,128]{1,0:T(8,128)(2,1)}, bf16[4112,128]{1,0:T(8,128)(2,1)S(1)}, u32[]{:S(2)}, u32[]{:S(2)}) collective-permute-start(bf16[4112,128]{1,0:T(8,128)(2,1)} %pad_maximum_fusion.2), channel_id=1, source_target_pairs={{0,4},{1,5},{2,6},{3,7},{4,0},{5,1},{6,2},{7,3},{8,12},{9,13},{10,... | collective-permute-start | bytes 3158024 | tf_op jit(solution)/shard_map/ppermute | solution.py:1081
  14.0 18.2 %collective-permute-start.5 = (s32[1,504]{1,0:T(1,128)S(1)}, s32[1,504]{1,0:T(1,128)S(1)}, u32[]{:S(2)}, u32[]{:S(2)}) collective-permute-start(s32[1,504]{1,0:T(1,128)S(1)} %copy-done.97), channel_id=1, source_target_pairs={{0,1},{1,0},{2,3},{3,2},{4,5},{5,4},{6,7},{7,6},{8,9},{9,8},{10,11... | collective-permute-start | bytes 6056 | tf_op jit(solution)/shard_map/ppermute | solution.py:1081
  41.5 25.6 %collective-permute-start.9 = (bf16[4112,128]{1,0:T(8,128)(2,1)}, bf16[4112,128]{1,0:T(8,128)(2,1)S(1)}, u32[]{:S(2)}, u32[]{:S(2)}) collective-permute-start(bf16[4112,128]{1,0:T(8,128)(2,1)} %get-tuple-element.172), channel_id=1, source_target_pairs={{0,8},{1,9},{2,10},{3,11},{4,12},{5,13},{6,14},{7,15},{8,16},{9,17... | collective-permute-start | bytes 3158024 | tf_op jit(solution)/shard_map/ppermute | solution.py:1081
  42.4 30.4 %collective-permute-start.8 = (bf16[4112,128]{1,0:T(8,128)(2,1)}, bf16[4112,128]{1,0:T(8,128)(2,1)S(1)}, u32[]{:S(2)}, u32[]{:S(2)}) collective-permute-start(bf16[4112,128]{1,0:T(8,128)(2,1)} %get-tuple-element.172), channel_id=1, source_target_pairs={{0,1},{1,0},{2,3},{3,2},{4,5},{5,4},{6,7},{7,6},{8,9},{9,8},{10,11... | collective-permute-start | bytes 3158024 | tf_op jit(solution)/shard_map/ppermute | solution.py:1081
  43.2 30.7 %collective-permute-start.7 = (bf16[4112,128]{1,0:T(8,128)(2,1)}, bf16[4112,128]{1,0:T(8,128)(2,1)S(1)}, u32[]{:S(2)}, u32[]{:S(2)}) collective-permute-start(bf16[4112,128]{1,0:T(8,128)(2,1)} %get-tuple-element.172), channel_id=1, source_target_pairs={{0,4},{1,5},{2,6},{3,7},{4,0},{5,1},{6,2},{7,3},{8,12},{9,13},{10,... | collective-permute-start | bytes 3158024 | tf_op jit(solution)/shard_map/ppermute | solution.py:1081
  52.0 112.9 %collective-permute-start.15 = (bf16[4112,128]{1,0:T(8,128)(2,1)S(1)}, bf16[4112,128]{1,0:T(8,128)(2,1)S(1)}, u32[]{:S(2)}, u32[]{:S(2)}) collective-permute-start(bf16[4112,128]{1,0:T(8,128)(2,1)S(1)} %get-tuple-element.356), channel_id=1, source_target_pairs={{0,2},{1,3},{2,0},{3,1},{4,6},{5,7},{6,4},{7,5},{8,10},{9,11},{10,... | collective-permute-start | bytes 3158024 | tf_op jit(solution)/shard_map/ppermute | solution.py:1081
  54.7 111.7 %collective-permute-start.18 = (bf16[4112,128]{1,0:T(8,128)(2,1)S(1)}, bf16[4112,128]{1,0:T(8,128)(2,1)}, u32[]{:S(2)}, u32[]{:S(2)}) collective-permute-start(bf16[4112,128]{1,0:T(8,128)(2,1)S(1)} %broadcast_select_fusion.8), channel_id=1, source_target_pairs={{0,2},{1,3},{2,0},{3,1},{4,6},{5,7},{6,4},{7,5},{8,10},{9,11},{10,... | collective-permute-start | bytes 3158024 | tf_op jit(solution)/shard_map/ppermute | solution.py:1081
  80.1 25.8 %collective-permute-start.12 = (bf16[4112,128]{1,0:T(8,128)(2,1)S(1)}, bf16[4112,128]{1,0:T(8,128)(2,1)S(1)}, u32[]{:S(2)}, u32[]{:S(2)}) collective-permute-start(bf16[4112,128]{1,0:T(8,128)(2,1)S(1)} %copy-done.56), channel_id=1, source_target_pairs={{0,8},{1,9},{2,10},{3,11},{4,12},{5,13},{6,14},{7,15},{8,16},{9,17... | collective-permute-start | bytes 3158024 | tf_op jit(solution)/shard_map/ppermute | solution.py:1081
  89.4 22.6 %collective-permute-start.11 = (bf16[4112,128]{1,0:T(8,128)(2,1)S(1)}, bf16[4112,128]{1,0:T(8,128)(2,1)S(1)}, u32[]{:S(2)}, u32[]{:S(2)}) collective-permute-start(bf16[4112,128]{1,0:T(8,128)(2,1)S(1)} %copy-done.56), channel_id=1, source_target_pairs={{0,1},{1,0},{2,3},{3,2},{4,5},{5,4},{6,7},{7,6},{8,9},{9,8},{10,11... | collective-permute-start | bytes 3158024 | tf_op jit(solution)/shard_map/ppermute | solution.py:1081
  90.6 22.2 %collective-permute-start.10 = (bf16[4112,128]{1,0:T(8,128)(2,1)S(1)}, bf16[4112,128]{1,0:T(8,128)(2,1)S(1)}, u32[]{:S(2)}, u32[]{:S(2)}) collective-permute-start(bf16[4112,128]{1,0:T(8,128)(2,1)S(1)} %copy-done.56), channel_id=1, source_target_pairs={{0,4},{1,5},{2,6},{3,7},{4,0},{5,1},{6,2},{7,3},{8,12},{9,13},{10,... | collective-permute-start | bytes 3158024 | tf_op jit(solution)/shard_map/ppermute | solution.py:1081
  105.8 60.6 %collective-permute-start.19 = (bf16[4112,128]{1,0:T(8,128)(2,1)S(1)}, bf16[4112,128]{1,0:T(8,128)(2,1)}, u32[]{:S(2)}, u32[]{:S(2)}) collective-permute-start(bf16[4112,128]{1,0:T(8,128)(2,1)S(1)} %broadcast_select_fusion.7), channel_id=1, source_target_pairs={{0,2},{1,3},{2,0},{3,1},{4,6},{5,7},{6,4},{7,5},{8,10},{9,11},{10,... | collective-permute-start | bytes 3158024 | tf_op jit(solution)/shard_map/ppermute | solution.py:1081
  128.3 20.8 %collective-permute-start.14 = (bf16[4112,128]{1,0:T(8,128)(2,1)S(1)}, bf16[4112,128]{1,0:T(8,128)(2,1)S(1)}, u32[]{:S(2)}, u32[]{:S(2)}) collective-permute-start(bf16[4112,128]{1,0:T(8,128)(2,1)S(1)} %copy-done.58), channel_id=1, source_target_pairs={{0,1},{1,0},{2,3},{3,2},{4,5},{5,4},{6,7},{7,6},{8,9},{9,8},{10,11... | collective-permute-start | bytes 3158024 | tf_op jit(solution)/shard_map/ppermute | solution.py:1081
  129.4 20.4 %collective-permute-start.13 = (bf16[4112,128]{1,0:T(8,128)(2,1)S(1)}, bf16[4112,128]{1,0:T(8,128)(2,1)S(1)}, u32[]{:S(2)}, u32[]{:S(2)}) collective-permute-start(bf16[4112,128]{1,0:T(8,128)(2,1)S(1)} %copy-done.58), channel_id=1, source_target_pairs={{0,4},{1,5},{2,6},{3,7},{4,0},{5,1},{6,2},{7,3},{8,12},{9,13},{10,... | collective-permute-start | bytes 3158024 | tf_op jit(solution)/shard_map/ppermute | solution.py:1081
  228.9 21.3 %collective-permute-start.6 = (bf16[1024,768]{1,0:T(8,128)(2,1)S(1)}, bf16[1024,768]{1,0:T(8,128)(2,1)S(1)}, u32[]{:S(2)}, u32[]{:S(2)}) collective-permute-start(bf16[1024,768]{1,0:T(8,128)(2,1)S(1)} %copy-done.94), channel_id=1, source_target_pairs={{0,2},{3,1},{4,6},{7,5},{8,10},{11,9},{12,14},{15,13},{16,18},{19,... | collective-permute-start | bytes 4718600 | tf_op jit(solution)/shard_map/ppermute | solution.py:1081
  264.2 23.9 %collective-permute-start.38 = (bf16[1024,768]{1,0:T(8,128)(2,1)S(1)}, bf16[1024,768]{1,0:T(8,128)(2,1)S(1)}, u32[]{:S(2)}, u32[]{:S(2)}) collective-permute-start(bf16[1024,768]{1,0:T(8,128)(2,1)S(1)} %get-tuple-element.228), channel_id=1, source_target_pairs={{0,2},{1,3},{2,0},{3,1},{4,6},{5,7},{6,4},{7,5},{8,10},{9,11},{10,... | collective-permute-start | bytes 4718600 | tf_op jit(solution)/shard_map/ppermute | solution.py:1081
  279.1 31.3 %collective-permute-start.36 = (bf16[1536,768]{1,0:T(8,128)(2,1)S(1)}, bf16[1536,768]{1,0:T(8,128)(2,1)S(1)}, u32[]{:S(2)}, u32[]{:S(2)}) collective-permute-start(bf16[1536,768]{1,0:T(8,128)(2,1)S(1)} %convolution_convert_fusion.2.own), channel_id=1, source_target_pairs={{1,0},{2,3},{5,4},{6,7},{9,8},{10,11},{13,12},{14,15},{17,16},{18,... | collective-permute-start | bytes 7077896 | tf_op jit(solution)/shard_map/ppermute | solution.py:1081
  287.0 23.4 %collective-permute-start.37 = (bf16[384,1536]{1,0:T(8,128)(2,1)}, bf16[384,1536]{1,0:T(8,128)(2,1)S(1)}, u32[]{:S(2)}, u32[]{:S(2)}) collective-permute-start(bf16[384,1536]{1,0:T(8,128)(2,1)} %shard_map.241), channel_id=1, source_target_pairs={{1,5},{2,6},{5,1},{6,2},{9,13},{10,14},{13,9},{14,10},{17,21},{18,... | collective-permute-start | bytes 3538952 | tf_op jit(solution)/shard_map/ppermute | solution.py:1081
  317.8 17.0 %collective-permute-start.39 = (bf16[1024,768]{1,0:T(8,128)(2,1)S(1)}, bf16[1024,768]{1,0:T(8,128)(2,1)S(1)}, u32[]{:S(2)}, u32[]{:S(2)}) collective-permute-start(bf16[1024,768]{1,0:T(8,128)(2,1)S(1)} %get-tuple-element.230.refs_1_), channel_id=1, source_target_pairs={{0,2},{1,3},{2,0},{3,1},{4,6},{5,7},{6,4},{7,5},{8,10},{9,11},{10,... | collective-permute-start | bytes 4718600 | tf_op jit(solution)/shard_map/ppermute | solution.py:1081
  324.9 21.1 %collective-permute-start.43 = (bf16[384,1536]{1,0:T(8,128)(2,1)}, bf16[384,1536]{1,0:T(8,128)(2,1)S(1)}, u32[]{:S(2)}, u32[]{:S(2)}) collective-permute-start(bf16[384,1536]{1,0:T(8,128)(2,1)} %shard_map.246), channel_id=1, source_target_pairs={{1,0},{2,3},{5,4},{6,7},{9,8},{10,11},{13,12},{14,15},{17,16},{18,... | collective-permute-start | bytes 3538952 | tf_op jit(solution)/shard_map/ppermute | solution.py:1081
  333.5 29.9 %collective-permute-start.41 = (bf16[384,768]{1,0:T(8,128)(2,1)S(1)}, bf16[384,768]{1,0:T(8,128)(2,1)S(1)}, u32[]{:S(2)}, u32[]{:S(2)}) collective-permute-start(bf16[384,768]{1,0:T(8,128)(2,1)S(1)} %convolution_convert_fusion.11.own), channel_id=1, source_target_pairs={{1,0},{2,3},{5,4},{6,7},{9,8},{10,11},{13,12},{14,15},{17,16},{18,... | collective-permute-start | bytes 1769480 | tf_op jit(solution)/shard_map/ppermute | solution.py:1081
  350.0 17.3 %collective-permute-start.44 = (bf16[384,1152]{1,0:T(8,128)(2,1)}, bf16[384,1152]{1,0:T(8,128)(2,1)S(1)}, u32[]{:S(2)}, u32[]{:S(2)}) collective-permute-start(bf16[384,1152]{1,0:T(8,128)(2,1)} %shard_map.248), channel_id=1, source_target_pairs={{1,0},{2,3},{5,4},{6,7},{9,8},{10,11},{13,12},{14,15},{17,16},{18,... | collective-permute-start | bytes 2654216 | tf_op jit(solution)/shard_map/ppermute | solution.py:1081
  351.5 29.7 %collective-permute-start.40 = (bf16[1024,768]{1,0:T(8,128)(2,1)S(1)}, bf16[1024,768]{1,0:T(8,128)(2,1)S(1)}, u32[]{:S(2)}, u32[]{:S(2)}) collective-permute-start(bf16[1024,768]{1,0:T(8,128)(2,1)S(1)} %get-tuple-element.233.own), channel_id=1, source_target_pairs={{0,2},{1,3},{2,0},{3,1},{4,6},{5,7},{6,4},{7,5},{8,10},{9,11},{10,... | collective-permute-start | bytes 4718600 | tf_op jit(solution)/shard_map/ppermute | solution.py:1081
  368.2 33.5 %collective-permute-start.45 = (bf16[1536,768]{1,0:T(8,128)(2,1)}, bf16[1536,768]{1,0:T(8,128)(2,1)S(1)}, u32[]{:S(2)}, u32[]{:S(2)}) collective-permute-start(bf16[1536,768]{1,0:T(8,128)(2,1)} %get-tuple-element.251.own), channel_id=1, source_target_pairs={{1,0},{2,3},{5,4},{6,7},{9,8},{10,11},{13,12},{14,15},{17,16},{18,... | collective-permute-start | bytes 7077896 | tf_op jit(solution)/shard_map/ppermute | solution.py:1081
  372.1 29.5 %collective-permute-start.46 = (bf16[384,1536]{1,0:T(8,128)(2,1)}, bf16[384,1536]{1,0:T(8,128)(2,1)S(1)}, u32[]{:S(2)}, u32[]{:S(2)}) collective-permute-start(bf16[384,1536]{1,0:T(8,128)(2,1)} %shard_map.251), channel_id=1, source_target_pairs={{1,5},{2,6},{5,1},{6,2},{9,13},{10,14},{13,9},{14,10},{17,21},{18,... | collective-permute-start | bytes 3538952 | tf_op jit(solution)/shard_map/ppermute | solution.py:1081
  412.4 18.3 %collective-permute-start.48 = (bf16[384,1536]{1,0:T(8,128)(2,1)}, bf16[384,1536]{1,0:T(8,128)(2,1)S(1)}, u32[]{:S(2)}, u32[]{:S(2)}) collective-permute-start(bf16[384,1536]{1,0:T(8,128)(2,1)} %shard_map.257), channel_id=1, source_target_pairs={{1,0},{2,3},{5,4},{6,7},{9,8},{10,11},{13,12},{14,15},{17,16},{18,... | collective-permute-start | bytes 3538952 | tf_op jit(solution)/shard_map/ppermute | solution.py:1081
  431.7 32.5 %collective-permute-start.50 = (bf16[1536,384]{1,0:T(8,128)(2,1)}, bf16[1536,384]{1,0:T(8,128)(2,1)S(1)}, u32[]{:S(2)}, u32[]{:S(2)}) collective-permute-start(bf16[1536,384]{1,0:T(8,128)(2,1)} %get-tuple-element.260.own), channel_id=1, source_target_pairs={{1,5},{2,6},{5,1},{6,2},{9,13},{10,14},{13,9},{14,10},{17,21},{18,... | collective-permute-start | bytes 3538952 | tf_op jit(solution)/shard_map/ppermute | solution.py:1081
  435.1 29.1 %collective-permute-start.51 = (bf16[384,1152]{1,0:T(8,128)(2,1)}, bf16[384,1152]{1,0:T(8,128)(2,1)S(1)}, u32[]{:S(2)}, u32[]{:S(2)}) collective-permute-start(bf16[384,1152]{1,0:T(8,128)(2,1)} %shard_map.260), channel_id=1, source_target_pairs={{1,0},{2,3},{5,4},{6,7},{9,8},{10,11},{13,12},{14,15},{17,16},{18,... | collective-permute-start | bytes 2654216 | tf_op jit(solution)/shard_map/ppermute | solution.py:1081
  437.3 26.3 %collective-permute-start.52 = (bf16[384,768]{1,0:T(8,128)(2,1)S(1)}, bf16[384,768]{1,0:T(8,128)(2,1)S(1)}, u32[]{:S(2)}, u32[]{:S(2)}) collective-permute-start(bf16[384,768]{1,0:T(8,128)(2,1)S(1)} %convolution_convert_fusion.6.own), channel_id=1, source_target_pairs={{1,0},{2,3},{5,4},{6,7},{9,8},{10,11},{13,12},{14,15},{17,16},{18,... | collective-permute-start | bytes 1769480 | tf_op jit(solution)/shard_map/ppermute | solution.py:1081
  469.1 18.3 %collective-permute-start.54 = (bf16[1536,384]{1,0:T(8,128)(2,1)}, bf16[1536,384]{1,0:T(8,128)(2,1)S(1)}, u32[]{:S(2)}, u32[]{:S(2)}) collective-permute-start(bf16[1536,384]{1,0:T(8,128)(2,1)} %shard_map.266), channel_id=1, source_target_pairs={{1,0},{2,3},{5,4},{6,7},{9,8},{10,11},{13,12},{14,15},{17,16},{18,... | collective-permute-start | bytes 3538952 | tf_op jit(solution)/shard_map/ppermute | solution.py:1081
  494.0 20.2 %collective-permute-start.56 = (bf16[4112,128]{1,0:T(8,128)(2,1)S(1)}, bf16[4112,128]{1,0:T(8,128)(2,1)S(1)}, u32[]{:S(2)}, u32[]{:S(2)}) collective-permute-start(bf16[4112,128]{1,0:T(8,128)(2,1)S(1)} %get-tuple-element.355), channel_id=1, source_target_pairs={{0,4},{3,7},{4,0},{7,3},{8,12},{11,15},{12,8},{15,11},{16,20},{19,... | collective-permute-start | bytes 3158024 | tf_op jit(solution)/shard_map/ppermute | solution.py:1081
  497.0 49.4 %collective-permute-start.60 = (bf16[4112,128]{1,0:T(8,128)(2,1)S(1)}, bf16[4112,128]{1,0:T(8,128)(2,1)S(1)}, u32[]{:S(2)}, u32[]{:S(2)}) collective-permute-start(bf16[4112,128]{1,0:T(8,128)(2,1)S(1)} %get-tuple-element.353), channel_id=1, source_target_pairs={{0,4},{3,7},{4,0},{7,3},{8,12},{11,15},{12,8},{15,11},{16,20},{19,... | collective-permute-start | bytes 3158024 | tf_op jit(solution)/shard_map/ppermute | solution.py:1081
  499.9 33.8 %collective-permute-start.59 = (bf16[4112,128]{1,0:T(8,128)(2,1)S(1)}, bf16[4112,128]{1,0:T(8,128)(2,1)S(1)}, u32[]{:S(2)}, u32[]{:S(2)}) collective-permute-start(bf16[4112,128]{1,0:T(8,128)(2,1)S(1)} %get-tuple-element.354), channel_id=1, source_target_pairs={{0,4},{3,7},{4,0},{7,3},{8,12},{11,15},{12,8},{15,11},{16,20},{19,... | collective-permute-start | bytes 3158024 | tf_op jit(solution)/shard_map/ppermute | solution.py:1081
  518.6 31.7 %collective-permute-start.61 = (bf16[4112,128]{1,0:T(8,128)(2,1)}, bf16[4112,128]{1,0:T(8,128)(2,1)S(1)}, u32[]{:S(2)}, u32[]{:S(2)}) collective-permute-start(bf16[4112,128]{1,0:T(8,128)(2,1)} %get-tuple-element.302), channel_id=1, source_target_pairs={{0,8},{3,11},{4,12},{7,15},{8,16},{11,19},{12,20},{15,23},{16,24},... | collective-permute-start | bytes 3158024 | tf_op jit(solution)/shard_map/ppermute | solution.py:1081
  531.7 47.2 %collective-permute-start.57 = (bf16[1024,768]{1,0:T(8,128)(2,1)S(1)}, bf16[1024,768]{1,0:T(8,128)(2,1)}, u32[]{:S(2)}, u32[]{:S(2)}) collective-permute-start(bf16[1024,768]{1,0:T(8,128)(2,1)S(1)} %add_convert_fusion), channel_id=1, source_target_pairs={{0,2},{1,3},{2,0},{3,1},{4,6},{5,7},{6,4},{7,5},{8,10},{9,11},{10,... | collective-permute-start | bytes 4718600 | tf_op jit(solution)/shard_map/ppermute | solution.py:1081
  531.8 27.0 %collective-permute-start.62 = (bf16[4112,128]{1,0:T(8,128)(2,1)S(1)}, bf16[4112,128]{1,0:T(8,128)(2,1)S(1)}, u32[]{:S(2)}, u32[]{:S(2)}) collective-permute-start(bf16[4112,128]{1,0:T(8,128)(2,1)S(1)} %get-tuple-element.352), channel_id=1, source_target_pairs={{0,4},{3,7},{4,0},{7,3},{8,12},{11,15},{12,8},{15,11},{16,20},{19,... | collective-permute-start | bytes 3158024 | tf_op jit(solution)/shard_map/ppermute | solution.py:1081
  538.0 23.8 %collective-permute-start.63 = (bf16[4112,128]{1,0:T(8,128)(2,1)}, bf16[4112,128]{1,0:T(8,128)(2,1)S(1)}, u32[]{:S(2)}, u32[]{:S(2)}) collective-permute-start(bf16[4112,128]{1,0:T(8,128)(2,1)} %get-tuple-element.305), channel_id=1, source_target_pairs={{0,8},{3,11},{4,12},{7,15},{8,16},{11,19},{12,20},{15,23},{16,24},... | collective-permute-start | bytes 3158024 | tf_op jit(solution)/shard_map/ppermute | solution.py:1081
  546.4 21.1 %collective-permute-start.64 = (bf16[4112,128]{1,0:T(8,128)(2,1)S(1)}, bf16[4112,128]{1,0:T(8,128)(2,1)S(1)}, u32[]{:S(2)}, u32[]{:S(2)}) collective-permute-start(bf16[4112,128]{1,0:T(8,128)(2,1)S(1)} %copy-done.105), channel_id=1, source_target_pairs={{0,4},{3,7},{4,0},{7,3},{8,12},{11,15},{12,8},{15,11},{16,20},{19,... | collective-permute-start | bytes 3158024 | tf_op jit(solution)/shard_map/ppermute | solution.py:1081
  555.0 18.7 %collective-permute-start.65 = (bf16[4112,128]{1,0:T(8,128)(2,1)}, bf16[4112,128]{1,0:T(8,128)(2,1)S(1)}, u32[]{:S(2)}, u32[]{:S(2)}) collective-permute-start(bf16[4112,128]{1,0:T(8,128)(2,1)} %get-tuple-element.310), channel_id=1, source_target_pairs={{0,8},{3,11},{4,12},{7,15},{8,16},{11,19},{12,20},{15,23},{16,24},... | collective-permute-start | bytes 3158024 | tf_op jit(solution)/shard_map/ppermute | solution.py:1081
  558.8 44.7 %collective-permute-start.55 = (bf16[1024,768]{1,0:T(8,128)(2,1)S(1)}, bf16[1024,768]{1,0:T(8,128)(2,1)}, u32[]{:S(2)}, u32[]{:S(2)}) collective-permute-start(bf16[1024,768]{1,0:T(8,128)(2,1)S(1)} %copy-done.38), channel_id=1, source_target_pairs={{0,1},{3,2},{4,5},{7,6},{8,9},{11,10},{12,13},{15,14},{16,17},{19,... | collective-permute-start | bytes 4718600 | tf_op jit(solution)/shard_map/ppermute | solution.py:1081
  561.9 22.6 %collective-permute-start.66 = (bf16[4112,128]{1,0:T(8,128)(2,1)}, bf16[4112,128]{1,0:T(8,128)(2,1)}, u32[]{:S(2)}, u32[]{:S(2)}) collective-permute-start(bf16[4112,128]{1,0:T(8,128)(2,1)} %get-tuple-element.312), channel_id=1, source_target_pairs={{0,4},{3,7},{4,0},{7,3},{8,12},{11,15},{12,8},{15,11},{16,20},{19,... | collective-permute-start | bytes 3158024 | tf_op jit(solution)/shard_map/ppermute | solution.py:1081
  567.4 19.2 %collective-permute-start.67 = (bf16[4112,128]{1,0:T(8,128)(2,1)}, bf16[4112,128]{1,0:T(8,128)(2,1)}, u32[]{:S(2)}, u32[]{:S(2)}) collective-permute-start(bf16[4112,128]{1,0:T(8,128)(2,1)} %get-tuple-element.315), channel_id=1, source_target_pairs={{0,8},{3,11},{4,12},{7,15},{8,16},{11,19},{12,20},{15,23},{16,24},... | collective-permute-start | bytes 3158024 | tf_op jit(solution)/shard_map/ppermute | solution.py:1081
  573.7 19.7 %collective-permute-start.68 = (bf16[4112,128]{1,0:T(8,128)(2,1)}, bf16[4112,128]{1,0:T(8,128)(2,1)}, u32[]{:S(2)}, u32[]{:S(2)}) collective-permute-start(bf16[4112,128]{1,0:T(8,128)(2,1)} %get-tuple-element.317), channel_id=1, source_target_pairs={{0,4},{3,7},{4,0},{7,3},{8,12},{11,15},{12,8},{15,11},{16,20},{19,... | collective-permute-start | bytes 3158024 | tf_op jit(solution)/shard_map/ppermute | solution.py:1081
  578.9 18.8 %collective-permute-start.69 = (bf16[4112,128]{1,0:T(8,128)(2,1)}, bf16[4112,128]{1,0:T(8,128)(2,1)}, u32[]{:S(2)}, u32[]{:S(2)}) collective-permute-start(bf16[4112,128]{1,0:T(8,128)(2,1)} %shard_map.285), channel_id=1, source_target_pairs={{0,8},{3,11},{4,12},{7,15},{8,16},{11,19},{12,20},{15,23},{16,24},... | collective-permute-start | bytes 3158024 | tf_op jit(solution)/shard_map/ppermute | solution.py:1081
  584.4 20.9 %collective-permute-start.58 = (bf16[1024,384]{1,0:T(8,128)(2,1)}, bf16[1024,384]{1,0:T(8,128)(2,1)}, u32[]{:S(2)}, u32[]{:S(2)}) collective-permute-start(bf16[1024,384]{1,0:T(8,128)(2,1)} %select_convert_fusion), channel_id=1, source_target_pairs={{0,1},{3,2},{4,5},{7,6},{8,9},{11,10},{12,13},{15,14},{16,17},{19,... | collective-permute-start | bytes 2359304 | tf_op jit(solution)/shard_map/ppermute | solution.py:1081
  586.6 21.9 %collective-permute-start.70 = (bf16[4112,128]{1,0:T(8,128)(2,1)}, bf16[4112,128]{1,0:T(8,128)(2,1)}, u32[]{:S(2)}, u32[]{:S(2)}) collective-permute-start(bf16[4112,128]{1,0:T(8,128)(2,1)} %get-tuple-element.321), channel_id=1, source_target_pairs={{0,4},{3,7},{4,0},{7,3},{8,12},{11,15},{12,8},{15,11},{16,20},{19,... | collective-permute-start | bytes 3158024 | tf_op jit(solution)/shard_map/ppermute | solution.py:1081
  593.4 18.8 %collective-permute-start.71 = (bf16[4112,128]{1,0:T(8,128)(2,1)}, bf16[4112,128]{1,0:T(8,128)(2,1)}, u32[]{:S(2)}, u32[]{:S(2)}) collective-permute-start(bf16[4112,128]{1,0:T(8,128)(2,1)} %shard_map.287), channel_id=1, source_target_pairs={{0,8},{3,11},{4,12},{7,15},{8,16},{11,19},{12,20},{15,23},{16,24},... | collective-permute-start | bytes 3158024 | tf_op jit(solution)/shard_map/ppermute | solution.py:1081
  (136 other events, 783.5 us)

commit v15 on v14

--- a/solution.py
+++ b/solution.py
@@ -1036,12 +1036,12 @@
     out[...] = total.astype(bf16)
 
 
-def reduce_call(j, n, buffer, arrived, carried, payload):
-    last = j >= 2
+def reduce_call(j, n, buffer, arrived, carried, payload, x_rel=0):
+    last = j >= 2 or x_rel == 1
     at = lambda j, x_rel: pl.BlockSpec((payload, BS), lambda i: ((j * 2 + x_rel) * 2 + n, 0))
     whole = fixed((payload, BS))
     operands = [stay(buffer), stay(arrived)] + ([] if carried is None else [stay(carried)])
-    specs = [at(j, 0)] + [whole] * (len(operands) - 1)
+    specs = [at(j, x_rel)] + [whole] * (len(operands) - 1)
     if not last:
         operands.append(stay(buffer))
         specs.append(at(j + 2, 1))
@@ -1346,13 +1346,13 @@
     buffer = place_tiles(("out", top), go1, ao1, buffer)
     buffer = place_tiles(("qkv", top), gq1, aq1, buffer)
     buffer = place_tiles(("down", low), gd0, ad0, buffer)
-    gbm, xb, aq0, ao0, av, buffer = hold(gbm, xb, aq0, ao0, av, buffer)
+    gbm, xb, aq0, av, buffer = hold(gbm, xb, aq0, av, buffer)
     ab = over(half_sum(half_at * 0, gbm, xb)) if grid3 else None
     buffer = place_tiles(("up", low), gu0, au0, buffer)
     buffer = place_base(1, gbt, None, buffer)
-    buffer = place_tiles(("out", low), go0, ao0, buffer)
     buffer = scatter_vec(vec_pos, vec_grad, av, buffer)
     buffer = place_tiles(("qkv", low), gq0, aq0, buffer)
+    buffer = place_tiles(("out", low), go0, ao0, buffer)
     base_weight = weights["base", 0]
     ab, buffer, base_weight, out_low = hold(ab, buffer, base_weight, out_low)
     weights["base", 0] = base_weight
@@ -1364,14 +1364,19 @@
         resized = resize_call(weights, pinv)
         carried = {n: None for n in order}
         blocks = buffer.reshape(4, 2, 2, payload, BS)
-        across = {n: send(blocks[0, 1, n], routes.x_home) for n in order}
-        following = {n: blocks[1, 1, n] for n in order}
+        across = {order[1]: send(blocks[0, 1, order[1]], routes.x_home), order[0]: None}
+        following = {order[1]: blocks[1, 1, order[1]], order[0]: blocks[2, 1, order[0]]}
+        far_side = send(blocks[0, 1, order[0]], routes.z_home)
+        carried[order[0]] = send(blocks[0, 0, order[0]], routes.z_home)
         rounded = {}
         for j in range(4):
             for n in order:
                 extra = None
                 if j == 0 and n == order[0]:
-                    extra = resized
+                    token, far_side, resized = hold(token, far_side, resized)
+                    later, unused = reduce_call(1, n, buffer, far_side, None, payload, 1)
+                    across[n] = send(later, routes.x_home)
+                    continue
                 token, across[n], carried[n], extra = hold(token, across[n], carried[n], extra)
                 if extra is not None:
                     resized = extra

time: 637 us -> 637 us (level)
  starting transfers between devices: 120 us -> 106 us
  Pallas kernels: 282 us -> 289 us
    ppermute x73, starting transfers between devices: 120 us -> 106 us  [send(): return lax.ppermute(value, AXES, route)]
    unnamed x228 -> x226, local copies, waits for them, and re-layouts: 26.9 us -> 27.9 us
where the time goes in v15:
time: 637 us; the launch traced here: 626 us
  Pallas kernels  289 us (45%)
  waiting for transfers between devices  125 us (20%)
  starting transfers between devices  106 us (17%)
  local copies, waits for them, and re-layouts  43.2 us (7%)
  matrix products  30.8 us (5%)
  other arithmetic  28.9 us (5%)
    ppermute x73, waiting for transfers between devices, send(): return lax.ppermute(value, AXES, route)  125 us
    ppermute x73, starting transfers between devices, send(): return lax.ppermute(value, AXES, route)  106 us
    pallas_call x2, Pallas kernels, attend_back_call(): pl.pallas_call(attend_back_kernel, out_shape=[shape(D, f32), shape(D, bf1...  45.7 us
    pallas_call x10, Pallas kernels, scatter_matrix(): pl.pallas_call(functools.partial(scatter_kernel, rows_n, cols_n, steps, p...  35.2 us
    pallas_call x2, Pallas kernels, attend_call(): pl.pallas_call(functools.partial(attend_kernel, layer), out_shape=[jax.Sh...  29.7 us
    unnamed x226, local copies, waits for them, and re-layouts  27.9 us
    dot_general x12, matrix products, dot_tn(): lax.dot_general(left, right, (((0,), (0,)), ((), ())), preferred_element_...  27.7 us
    pallas_call x8, Pallas kernels, reduce_call(): pl.pallas_call(functools.partial(reduce_kernel, carried is not None, last...  26.4 us
  transfers between devices with their start and end apart: 73, of which 34 were waited for; matrix products, arithmetic and copies ran while one was open for 10% of the time, Pallas kernels for 32%

profile of v15, /device:TPU:0, one launch (start us, length us, event | category | flops | bytes accessed | tf_op | source)
XLA Modules:
  0.0 626.4 jit_solution(10433248634876954133)
XLA Ops:
  18.9 6.0 shard_map.222.refs_3_
  26.1 6.1 collective-permute-done.5.refs_5_
  43.7 6.5 %shard_map.224.refs_3_ = bf16[1024,768]{1,0:T(8,128)(2,1)S(1)} custom-call(s32[4,3]{1,0:T(4,128)S(1)} %convert_element_type.120.present, s32[1]{0:T(128)} %bitcast.6.half.part, bf16[1024,768]{1,0:T(8,128)(2,1)} %get-tuple-element.170.patch_ref.refs_2_, s32[1024,1]{1,0:T(8,128)S(1)} %copy.140.class_ref, bf16[3,3072,768]{2,1,0:T(8,128)(2,1)} %pinv_ref.9), custom_call_target="tpu_custom_call" | custom-call | flops 1811939328 | bytes 6684672 | tf_op jit(solution)/shard_map/pallas_call | solution.py:439
  54.7 12.4 %collective-permute-done.9.refs_4_ = bf16[4112,128]{1,0:T(8,128)(2,1)S(1)} collective-permute-done((bf16[4112,128]{1,0:T(8,128)(2,1)}, bf16[4112,128]{1,0:T(8,128)(2,1)S(1)}, u32[]{:S(2)}, u32[]{:S(2)}) %collective-permute-start.9) | collective-permute-done | bytes 1052704 | tf_op jit(solution)/shard_map/ppermute | solution.py:1081
  67.1 5.7 collective-permute-done.8.refs_1_
  80.8 6.0 shard_map.226.refs_3_
  93.6 12.3 %collective-permute-done.12.refs_4_ = bf16[4112,128]{1,0:T(8,128)(2,1)S(1)} collective-permute-done((bf16[4112,128]{1,0:T(8,128)(2,1)S(1)}, bf16[4112,128]{1,0:T(8,128)(2,1)S(1)}, u32[]{:S(2)}, u32[]{:S(2)}) %collective-permute-start.12) | collective-permute-done | bytes 1052704 | tf_op jit(solution)/shard_map/ppermute | solution.py:1081
  105.9 6.1 collective-permute-done.11.refs_1_
  119.8 6.2 shard_map.228.refs_3_
  132.4 16.7 %collective-permute-done.14.refs_1_ = bf16[4112,128]{1,0:T(8,128)(2,1)S(1)} collective-permute-done((bf16[4112,128]{1,0:T(8,128)(2,1)S(1)}, bf16[4112,128]{1,0:T(8,128)(2,1)S(1)}, u32[]{:S(2)}, u32[]{:S(2)}) %collective-permute-start.14) | collective-permute-done | bytes 1052704 | tf_op jit(solution)/shard_map/ppermute | solution.py:1081
  157.0 5.7 collective-permute-done.28
  173.0 14.2 %shard_map.230 = (bf16[3072,384]{1,0:T(8,128)(2,1)}, bf16[2304,384]{1,0:T(8,128)(2,1)}, bf16[768,384]{1,0:T(8,128)(2,1)}, bf16[3072,384]{1,0:T(8,128)(2,1)}, bf1...) custom-call(s32[16]{0:T(128)S(1)} %stack.95.owner, ...), custom_call_target="tpu_custom_call" | custom-call | bytes 33030144 | tf_op jit(solution)/shard_map/pallas_call | solution.py:243
  187.3 6.8 %shard_map.231.refs_0_ = bf16[1024,384]{1,0:T(8,128)(2,1)S(1)} custom-call(s32[1]{0:T(128)} %bitcast.6.half.part, bf16[1024,768]{1,0:T(8,128)(2,1)} %get-tuple-element.168.refs_0_, bf16[1024,768]{1,0:T(8,128)(2,1)} %get-tuple-element.171.refs_1_, bf16[1024,768]{1,0:T(8,128)(2,1)} %get-tuple-element.174.refs_2_, ...), custom_call_target="tpu_custom_call" | custom-call | flops 2415919104 | bytes 9437184 | tf_op jit(solution)/shard_map/pallas_call | solution.py:552
  196.7 4.8 shard_map.232
  201.6 14.9 %shard_map.233 = (bf16[1024,384]{1,0:T(8,128)(2,1)S(1)}, f32[8,1024]{1,0:T(8,128)S(1)}, bf16[1024,768]{1,0:T(8,128)(2,1)S(1)}) custom-call(s32[4]{0:T(128)S(1)} %get-tuple-element.370.low_ref, s32[4]{0:T(128)S(1)} %get-tuple-element.363.high_ref, bf16[1024,384]{1,0:T(8,128)(2,1)S(1)} %get-tuple-element.191.q_ref, ...), custom_call_target="tpu_custom_call" | custom-call | flops 6442450944 | bytes 6291456 | tf_op jit(solution)/shard_map/pallas_call | solution.py:679
  220.8 9.4 %shard_map.234 = (f32[1024,768]{1,0:T(8,128)S(1)}, bf16[1024,768]{1,0:T(8,128)(2,1)}, bf16[1024,1536]{1,0:T(8,128)(2,1)}, bf16[1024,1536]{1,0:T(8,128)(2,1)}, bf16[1024,768]{1,0:T(8,128)(2,1)S(1)}) custom-call(f32[1024,768]{1,0:T(8,128)S(1)} %get-tuple-element.190.base.hid, bf16[1024,768]{1,0:T(8,128)(2,1)S(1)} %get-tuple-element.195.own, ...), custom_call_target="tpu_custom_call" | custom-call | flops 4831838208 | bytes 18874368 | tf_op jit(solution)/shard_map/pallas_call | solution.py:742
  233.6 4.4 shard_map.235
  238.1 14.8 %shard_map.236 = (bf16[1024,384]{1,0:T(8,128)(2,1)S(1)}, f32[8,1024]{1,0:T(8,128)S(1)}, bf16[1024,768]{1,0:T(8,128)(2,1)S(1)}) custom-call(s32[4]{0:T(128)S(1)} %get-tuple-element.370.low_ref, s32[4]{0:T(128)S(1)} %get-tuple-element.363.high_ref, bf16[1024,384]{1,0:T(8,128)(2,1)S(1)} %get-tuple-element.202.q_ref, ...), custom_call_target="tpu_custom_call" | custom-call | flops 6442450944 | bytes 6291456 | tf_op jit(solution)/shard_map/pallas_call | solution.py:679
  256.5 9.4 %shard_map.237 = (f32[1024,768]{1,0:T(8,128)S(1)}, bf16[1024,768]{1,0:T(8,128)(2,1)}, bf16[1024,1536]{1,0:T(8,128)(2,1)}, bf16[1024,1536]{1,0:T(8,128)(2,1)}, bf16[1024,768]{1,0:T(8,128)(2,1)S(1)}) custom-call(f32[1024,768]{1,0:T(8,128)S(1)} %get-tuple-element.201.base.hid, bf16[1024,768]{1,0:T(8,128)(2,1)S(1)} %get-tuple-element.206.own, ...), custom_call_target="tpu_custom_call" | custom-call | flops 4831838208 | bytes 18874368 | tf_op jit(solution)/shard_map/pallas_call | solution.py:742
  267.9 11.3 %shard_map.238 = (bf16[1024,768]{1,0:T(8,128)(2,1)S(1)}, bf16[1024,1536]{1,0:T(8,128)(2,1)S(1)}, bf16[1024,768]{1,0:T(8,128)(2,1)S(1)}, f32[1,768]{1,0:T(1,128)S...) custom-call(bf16[1024,768]{1,0:T(8,128)(2,1)S(1)} %broadcast_select_fusion.refs_0_, ...), custom_call_target="tpu_custom_call" | custom-call | flops 4831838208 | bytes 18874368 | tf_op jit(solution)/shard_map/pallas_call | solution.py:794
  283.8 4.0 convolution_convert_fusion.3.refs_1_
  293.2 22.8 %shard_map.240 = (f32[1024,768]{1,0:T(8,128)S(1)}, bf16[1024,768]{1,0:T(8,128)(2,1)S(1)}, bf16[1024,384]{1,0:T(8,128)(2,1)S(1)}, bf16[1024,384]{1,0:T(8,128)(2,1...) custom-call(s32[4]{0:T(128)S(1)} %get-tuple-element.369.low_ref, s32[4]{0:T(128)S(1)} %get-tuple-element.364.high_ref, ...), custom_call_target="tpu_custom_call" | custom-call | flops 11274289152 | bytes 15728640 | tf_op jit(solution)/shard_map/pallas_call | solution.py:886
  317.9 5.5 shard_map.243
  339.4 11.2 %shard_map.244 = (f32[1024,768]{1,0:T(8,128)S(1)}, bf16[1024,768]{1,0:T(8,128)(2,1)S(1)}, bf16[1024,1536]{1,0:T(8,128)(2,1)S(1)}, bf16[1024,768]{1,0:T(8,128)(2,...) custom-call(f32[1024,768]{1,0:T(8,128)S(1)} %get-tuple-element.218.refs_0_, ...), custom_call_target="tpu_custom_call" | custom-call | flops 4831838208 | bytes 18874368 | tf_op jit(solution)/shard_map/pallas_call | solution.py:794
  358.7 4.0 convolution_convert_fusion.1.refs_1_
  362.7 4.1 convolution_convert_fusion.refs_2_
  366.8 4.7 collective-permute-done.44.refs_4_
  377.2 4.3 shard_map.252.refs_1_
  381.4 4.1 shard_map.253.refs_4_
  385.5 22.8 %shard_map.250 = (f32[1024,768]{1,0:T(8,128)S(1)}, bf16[1024,768]{1,0:T(8,128)(2,1)S(1)}, bf16[1024,384]{1,0:T(8,128)(2,1)S(1)}, bf16[1024,384]{1,0:T(8,128)(2,1...) custom-call(s32[4]{0:T(128)S(1)} %get-tuple-element.369.low_ref, s32[4]{0:T(128)S(1)} %get-tuple-element.364.high_ref, ...), custom_call_target="tpu_custom_call" | custom-call | flops 11274289152 | bytes 15728640 | tf_op jit(solution)/shard_map/pallas_call | solution.py:886
  410.2 5.6 shard_map.255
  420.2 3.5 convolution_convert_fusion.4.own
  431.7 5.5 collective-permute-done.48.refs_1_
  445.7 3.5 shard_map.263.refs_1_
  449.2 4.3 shard_map.264.refs_4_
  458.2 6.7 %collective-permute-done.52.refs_3_ = bf16[16,16,128]{2,1,0:T(8,128)(2,1)S(1)} collective-permute-done((bf16[16,16,128]{2,1,0:T(8,128)(2,1)S(1)}, bf16[16,16,128]{2,1,0:T(8,128)(2,1)S(1)}, u32[]{:S(2)}, u32[]{:S(2)}) %collective-permute-start.52) | collective-permute-done | bytes 65568 | tf_op jit(solution)/shard_map/ppermute | solution.py:1081
  473.3 4.0 shard_map.267.refs_0_
  481.4 3.5 shard_map.270.refs_1_
  484.9 9.5 %collective-permute-done.54.refs_0_ = bf16[384,768]{1,0:T(8,128)(2,1)S(1)} collective-permute-done((bf16[384,768]{1,0:T(8,128)(2,1)S(1)}, bf16[384,768]{1,0:T(8,128)(2,1)S(1)}, u32[]{:S(2)}, u32[]{:S(2)}) %collective-permute-start.54) | collective-permute-done | bytes 589856 | tf_op jit(solution)/shard_map/ppermute | solution.py:1081
  509.0 3.7 collective-permute-start.59
  512.7 10.2 %shard_map.274.refs_2_ = bf16[3,384,768]{2,1,0:T(8,128)(2,1)S(1)} custom-call(bf16[3072,384]{1,0:T(8,128)(2,1)} %get-tuple-element.293.base, bf16[3,3072,768]{2,1,0:T(8,128)(2,1)} %pinv_ref.9), custom_call_target="tpu_custom_call" | custom-call | flops 5435817984 | bytes 14155776 | tf_op jit(solution)/shard_map/pallas_call | solution.py:470
  533.5 3.7 collective-permute-start.62
  541.5 3.8 collective-permute-start.63
  545.3 3.9 collective-permute-start.64
  550.2 3.7 shard_map.281
  562.4 3.6 shard_map.283
  567.4 3.8 collective-permute-start.67
  617.2 8.7 %shard_map.291 = (f32[32,128,128]{2,1,0:T(8,128)}, f32[32,128,128]{2,1,0:T(8,128)}, f32[32,128,128]{2,1,0:T(8,128)}, f32[32,128,128]{2,1,0:T(8,128)}) custom-call(s32[32]{0:T(128)S(1)} %convert_element_type.148.used, s32[1]{0:T(128)} %bitcast.27.flag.home, bf16[4112,128]{1,0:T(8,128)(2,1)} %shard_map.289.near, ...), custom_call_target="tpu_custom_call" | custom-call | flops 5905580032 | bytes 19922944 | tf_op jit(solution)/shard_map/pallas_call | solution.py:1011
  (494 shorter events, 265.2 us)
Async XLA Ops:
  4.2 28.6 %collective-permute-start.4 = (bf16[4112,128]{1,0:T(8,128)(2,1)}, bf16[4112,128]{1,0:T(8,128)(2,1)}, u32[]{:S(2)}, u32[]{:S(2)}) collective-permute-start(bf16[4112,128]{1,0:T(8,128)(2,1)} %pad_maximum_fusion.2), channel_id=1, source_target_pairs={{0,8},{1,9},{2,10},{3,11},{4,12},{5,13},{6,14},{7,15},{8,16},{9,17... | collective-permute-start | bytes 3158024 | tf_op jit(solution)/shard_map/ppermute | solution.py:1081
  7.2 25.6 %collective-permute-start.1 = (bf16[4112,128]{1,0:T(8,128)(2,1)}, bf16[4112,128]{1,0:T(8,128)(2,1)S(1)}, u32[]{:S(2)}, u32[]{:S(2)}) collective-permute-start(bf16[4112,128]{1,0:T(8,128)(2,1)} %pad_maximum_fusion.2), channel_id=1, source_target_pairs={{0,1},{1,0},{2,3},{3,2},{4,5},{5,4},{6,7},{7,6},{8,9},{9,8},{10,11... | collective-permute-start | bytes 3158024 | tf_op jit(solution)/shard_map/ppermute | solution.py:1081
  8.7 24.6 %collective-permute-start = (bf16[4112,128]{1,0:T(8,128)(2,1)}, bf16[4112,128]{1,0:T(8,128)(2,1)S(1)}, u32[]{:S(2)}, u32[]{:S(2)}) collective-permute-start(bf16[4112,128]{1,0:T(8,128)(2,1)} %pad_maximum_fusion.2), channel_id=1, source_target_pairs={{0,4},{1,5},{2,6},{3,7},{4,0},{5,1},{6,2},{7,3},{8,12},{9,13},{10,... | collective-permute-start | bytes 3158024 | tf_op jit(solution)/shard_map/ppermute | solution.py:1081
  14.0 18.2 %collective-permute-start.5 = (s32[1,504]{1,0:T(1,128)S(1)}, s32[1,504]{1,0:T(1,128)S(1)}, u32[]{:S(2)}, u32[]{:S(2)}) collective-permute-start(s32[1,504]{1,0:T(1,128)S(1)} %copy-done.97), channel_id=1, source_target_pairs={{0,1},{1,0},{2,3},{3,2},{4,5},{5,4},{6,7},{7,6},{8,9},{9,8},{10,11... | collective-permute-start | bytes 6056 | tf_op jit(solution)/shard_map/ppermute | solution.py:1081
  41.5 25.6 %collective-permute-start.9 = (bf16[4112,128]{1,0:T(8,128)(2,1)}, bf16[4112,128]{1,0:T(8,128)(2,1)S(1)}, u32[]{:S(2)}, u32[]{:S(2)}) collective-permute-start(bf16[4112,128]{1,0:T(8,128)(2,1)} %get-tuple-element.169), channel_id=1, source_target_pairs={{0,8},{1,9},{2,10},{3,11},{4,12},{5,13},{6,14},{7,15},{8,16},{9,17... | collective-permute-start | bytes 3158024 | tf_op jit(solution)/shard_map/ppermute | solution.py:1081
  42.4 30.4 %collective-permute-start.8 = (bf16[4112,128]{1,0:T(8,128)(2,1)}, bf16[4112,128]{1,0:T(8,128)(2,1)S(1)}, u32[]{:S(2)}, u32[]{:S(2)}) collective-permute-start(bf16[4112,128]{1,0:T(8,128)(2,1)} %get-tuple-element.169), channel_id=1, source_target_pairs={{0,1},{1,0},{2,3},{3,2},{4,5},{5,4},{6,7},{7,6},{8,9},{9,8},{10,11... | collective-permute-start | bytes 3158024 | tf_op jit(solution)/shard_map/ppermute | solution.py:1081
  43.2 30.7 %collective-permute-start.7 = (bf16[4112,128]{1,0:T(8,128)(2,1)}, bf16[4112,128]{1,0:T(8,128)(2,1)S(1)}, u32[]{:S(2)}, u32[]{:S(2)}) collective-permute-start(bf16[4112,128]{1,0:T(8,128)(2,1)} %get-tuple-element.169), channel_id=1, source_target_pairs={{0,4},{1,5},{2,6},{3,7},{4,0},{5,1},{6,2},{7,3},{8,12},{9,13},{10,... | collective-permute-start | bytes 3158024 | tf_op jit(solution)/shard_map/ppermute | solution.py:1081
  52.0 113.0 %collective-permute-start.15 = (bf16[4112,128]{1,0:T(8,128)(2,1)S(1)}, bf16[4112,128]{1,0:T(8,128)(2,1)S(1)}, u32[]{:S(2)}, u32[]{:S(2)}) collective-permute-start(bf16[4112,128]{1,0:T(8,128)(2,1)S(1)} %get-tuple-element.351), channel_id=1, source_target_pairs={{0,2},{1,3},{2,0},{3,1},{4,6},{5,7},{6,4},{7,5},{8,10},{9,11},{10,... | collective-permute-start | bytes 3158024 | tf_op jit(solution)/shard_map/ppermute | solution.py:1081
  54.7 111.8 %collective-permute-start.18 = (bf16[4112,128]{1,0:T(8,128)(2,1)S(1)}, bf16[4112,128]{1,0:T(8,128)(2,1)}, u32[]{:S(2)}, u32[]{:S(2)}) collective-permute-start(bf16[4112,128]{1,0:T(8,128)(2,1)S(1)} %broadcast_select_fusion.8), channel_id=1, source_target_pairs={{0,2},{1,3},{2,0},{3,1},{4,6},{5,7},{6,4},{7,5},{8,10},{9,11},{10,... | collective-permute-start | bytes 3158024 | tf_op jit(solution)/shard_map/ppermute | solution.py:1081
  80.1 25.8 %collective-permute-start.12 = (bf16[4112,128]{1,0:T(8,128)(2,1)S(1)}, bf16[4112,128]{1,0:T(8,128)(2,1)S(1)}, u32[]{:S(2)}, u32[]{:S(2)}) collective-permute-start(bf16[4112,128]{1,0:T(8,128)(2,1)S(1)} %copy-done.56), channel_id=1, source_target_pairs={{0,8},{1,9},{2,10},{3,11},{4,12},{5,13},{6,14},{7,15},{8,16},{9,17... | collective-permute-start | bytes 3158024 | tf_op jit(solution)/shard_map/ppermute | solution.py:1081
  89.4 22.6 %collective-permute-start.11 = (bf16[4112,128]{1,0:T(8,128)(2,1)S(1)}, bf16[4112,128]{1,0:T(8,128)(2,1)S(1)}, u32[]{:S(2)}, u32[]{:S(2)}) collective-permute-start(bf16[4112,128]{1,0:T(8,128)(2,1)S(1)} %copy-done.56), channel_id=1, source_target_pairs={{0,1},{1,0},{2,3},{3,2},{4,5},{5,4},{6,7},{7,6},{8,9},{9,8},{10,11... | collective-permute-start | bytes 3158024 | tf_op jit(solution)/shard_map/ppermute | solution.py:1081
  90.6 22.2 %collective-permute-start.10 = (bf16[4112,128]{1,0:T(8,128)(2,1)S(1)}, bf16[4112,128]{1,0:T(8,128)(2,1)S(1)}, u32[]{:S(2)}, u32[]{:S(2)}) collective-permute-start(bf16[4112,128]{1,0:T(8,128)(2,1)S(1)} %copy-done.56), channel_id=1, source_target_pairs={{0,4},{1,5},{2,6},{3,7},{4,0},{5,1},{6,2},{7,3},{8,12},{9,13},{10,... | collective-permute-start | bytes 3158024 | tf_op jit(solution)/shard_map/ppermute | solution.py:1081
  105.8 60.6 %collective-permute-start.19 = (bf16[4112,128]{1,0:T(8,128)(2,1)S(1)}, bf16[4112,128]{1,0:T(8,128)(2,1)}, u32[]{:S(2)}, u32[]{:S(2)}) collective-permute-start(bf16[4112,128]{1,0:T(8,128)(2,1)S(1)} %broadcast_select_fusion.7), channel_id=1, source_target_pairs={{0,2},{1,3},{2,0},{3,1},{4,6},{5,7},{6,4},{7,5},{8,10},{9,11},{10,... | collective-permute-start | bytes 3158024 | tf_op jit(solution)/shard_map/ppermute | solution.py:1081
  128.3 20.8 %collective-permute-start.14 = (bf16[4112,128]{1,0:T(8,128)(2,1)S(1)}, bf16[4112,128]{1,0:T(8,128)(2,1)S(1)}, u32[]{:S(2)}, u32[]{:S(2)}) collective-permute-start(bf16[4112,128]{1,0:T(8,128)(2,1)S(1)} %copy-done.58), channel_id=1, source_target_pairs={{0,1},{1,0},{2,3},{3,2},{4,5},{5,4},{6,7},{7,6},{8,9},{9,8},{10,11... | collective-permute-start | bytes 3158024 | tf_op jit(solution)/shard_map/ppermute | solution.py:1081
  129.4 20.4 %collective-permute-start.13 = (bf16[4112,128]{1,0:T(8,128)(2,1)S(1)}, bf16[4112,128]{1,0:T(8,128)(2,1)S(1)}, u32[]{:S(2)}, u32[]{:S(2)}) collective-permute-start(bf16[4112,128]{1,0:T(8,128)(2,1)S(1)} %copy-done.58), channel_id=1, source_target_pairs={{0,4},{1,5},{2,6},{3,7},{4,0},{5,1},{6,2},{7,3},{8,12},{9,13},{10,... | collective-permute-start | bytes 3158024 | tf_op jit(solution)/shard_map/ppermute | solution.py:1081
  230.6 22.9 %collective-permute-start.6 = (bf16[1024,768]{1,0:T(8,128)(2,1)S(1)}, bf16[1024,768]{1,0:T(8,128)(2,1)S(1)}, u32[]{:S(2)}, u32[]{:S(2)}) collective-permute-start(bf16[1024,768]{1,0:T(8,128)(2,1)S(1)} %copy-done.93), channel_id=1, source_target_pairs={{0,2},{3,1},{4,6},{7,5},{8,10},{11,9},{12,14},{15,13},{16,18},{19,... | collective-permute-start | bytes 4718600 | tf_op jit(solution)/shard_map/ppermute | solution.py:1081
  267.6 23.9 %collective-permute-start.38 = (bf16[1024,768]{1,0:T(8,128)(2,1)S(1)}, bf16[1024,768]{1,0:T(8,128)(2,1)S(1)}, u32[]{:S(2)}, u32[]{:S(2)}) collective-permute-start(bf16[1024,768]{1,0:T(8,128)(2,1)S(1)} %get-tuple-element.225), channel_id=1, source_target_pairs={{0,2},{1,3},{2,0},{3,1},{4,6},{5,7},{6,4},{7,5},{8,10},{9,11},{10,... | collective-permute-start | bytes 4718600 | tf_op jit(solution)/shard_map/ppermute | solution.py:1081
  282.4 33.7 %collective-permute-start.36 = (bf16[1536,768]{1,0:T(8,128)(2,1)S(1)}, bf16[1536,768]{1,0:T(8,128)(2,1)S(1)}, u32[]{:S(2)}, u32[]{:S(2)}) collective-permute-start(bf16[1536,768]{1,0:T(8,128)(2,1)S(1)} %convolution_convert_fusion.2.own), channel_id=1, source_target_pairs={{1,0},{2,3},{5,4},{6,7},{9,8},{10,11},{13,12},{14,15},{17,16},{18,... | collective-permute-start | bytes 7077896 | tf_op jit(solution)/shard_map/ppermute | solution.py:1081
  290.3 25.8 %collective-permute-start.37 = (bf16[384,1536]{1,0:T(8,128)(2,1)}, bf16[384,1536]{1,0:T(8,128)(2,1)S(1)}, u32[]{:S(2)}, u32[]{:S(2)}) collective-permute-start(bf16[384,1536]{1,0:T(8,128)(2,1)} %shard_map.241), channel_id=1, source_target_pairs={{1,5},{2,6},{5,1},{6,2},{9,13},{10,14},{13,9},{14,10},{17,21},{18,... | collective-permute-start | bytes 3538952 | tf_op jit(solution)/shard_map/ppermute | solution.py:1081
  323.5 15.9 %collective-permute-start.39 = (bf16[1024,768]{1,0:T(8,128)(2,1)S(1)}, bf16[1024,768]{1,0:T(8,128)(2,1)S(1)}, u32[]{:S(2)}, u32[]{:S(2)}) collective-permute-start(bf16[1024,768]{1,0:T(8,128)(2,1)S(1)} %get-tuple-element.227.refs_1_), channel_id=1, source_target_pairs={{0,2},{1,3},{2,0},{3,1},{4,6},{5,7},{6,4},{7,5},{8,10},{9,11},{10,... | collective-permute-start | bytes 4718600 | tf_op jit(solution)/shard_map/ppermute | solution.py:1081
  329.5 21.1 %collective-permute-start.43 = (bf16[384,1536]{1,0:T(8,128)(2,1)}, bf16[384,1536]{1,0:T(8,128)(2,1)S(1)}, u32[]{:S(2)}, u32[]{:S(2)}) collective-permute-start(bf16[384,1536]{1,0:T(8,128)(2,1)} %shard_map.246), channel_id=1, source_target_pairs={{1,0},{2,3},{5,4},{6,7},{9,8},{10,11},{13,12},{14,15},{17,16},{18,... | collective-permute-start | bytes 3538952 | tf_op jit(solution)/shard_map/ppermute | solution.py:1081
  338.1 28.7 %collective-permute-start.41 = (bf16[384,768]{1,0:T(8,128)(2,1)S(1)}, bf16[384,768]{1,0:T(8,128)(2,1)S(1)}, u32[]{:S(2)}, u32[]{:S(2)}) collective-permute-start(bf16[384,768]{1,0:T(8,128)(2,1)S(1)} %convolution_convert_fusion.11.own), channel_id=1, source_target_pairs={{1,0},{2,3},{5,4},{6,7},{9,8},{10,11},{13,12},{14,15},{17,16},{18,... | collective-permute-start | bytes 1769480 | tf_op jit(solution)/shard_map/ppermute | solution.py:1081
  354.6 16.9 %collective-permute-start.44 = (bf16[384,1152]{1,0:T(8,128)(2,1)}, bf16[384,1152]{1,0:T(8,128)(2,1)S(1)}, u32[]{:S(2)}, u32[]{:S(2)}) collective-permute-start(bf16[384,1152]{1,0:T(8,128)(2,1)} %shard_map.248), channel_id=1, source_target_pairs={{1,0},{2,3},{5,4},{6,7},{9,8},{10,11},{13,12},{14,15},{17,16},{18,... | collective-permute-start | bytes 2654216 | tf_op jit(solution)/shard_map/ppermute | solution.py:1081
  356.1 29.4 %collective-permute-start.40 = (bf16[1024,768]{1,0:T(8,128)(2,1)S(1)}, bf16[1024,768]{1,0:T(8,128)(2,1)S(1)}, u32[]{:S(2)}, u32[]{:S(2)}) collective-permute-start(bf16[1024,768]{1,0:T(8,128)(2,1)S(1)} %get-tuple-element.230.own), channel_id=1, source_target_pairs={{0,2},{1,3},{2,0},{3,1},{4,6},{5,7},{6,4},{7,5},{8,10},{9,11},{10,... | collective-permute-start | bytes 4718600 | tf_op jit(solution)/shard_map/ppermute | solution.py:1081
  372.5 35.9 %collective-permute-start.45 = (bf16[1536,768]{1,0:T(8,128)(2,1)}, bf16[1536,768]{1,0:T(8,128)(2,1)S(1)}, u32[]{:S(2)}, u32[]{:S(2)}) collective-permute-start(bf16[1536,768]{1,0:T(8,128)(2,1)} %get-tuple-element.248.own), channel_id=1, source_target_pairs={{1,0},{2,3},{5,4},{6,7},{9,8},{10,11},{13,12},{14,15},{17,16},{18,... | collective-permute-start | bytes 7077896 | tf_op jit(solution)/shard_map/ppermute | solution.py:1081
  376.4 32.0 %collective-permute-start.46 = (bf16[384,1536]{1,0:T(8,128)(2,1)}, bf16[384,1536]{1,0:T(8,128)(2,1)S(1)}, u32[]{:S(2)}, u32[]{:S(2)}) collective-permute-start(bf16[384,1536]{1,0:T(8,128)(2,1)} %shard_map.251), channel_id=1, source_target_pairs={{1,5},{2,6},{5,1},{6,2},{9,13},{10,14},{13,9},{14,10},{17,21},{18,... | collective-permute-start | bytes 3538952 | tf_op jit(solution)/shard_map/ppermute | solution.py:1081
  418.9 18.3 %collective-permute-start.48 = (bf16[384,1536]{1,0:T(8,128)(2,1)}, bf16[384,1536]{1,0:T(8,128)(2,1)S(1)}, u32[]{:S(2)}, u32[]{:S(2)}) collective-permute-start(bf16[384,1536]{1,0:T(8,128)(2,1)} %shard_map.257), channel_id=1, source_target_pairs={{1,0},{2,3},{5,4},{6,7},{9,8},{10,11},{13,12},{14,15},{17,16},{18,... | collective-permute-start | bytes 3538952 | tf_op jit(solution)/shard_map/ppermute | solution.py:1081
  438.2 26.7 %collective-permute-start.50 = (bf16[1536,384]{1,0:T(8,128)(2,1)}, bf16[1536,384]{1,0:T(8,128)(2,1)S(1)}, u32[]{:S(2)}, u32[]{:S(2)}) collective-permute-start(bf16[1536,384]{1,0:T(8,128)(2,1)} %get-tuple-element.257.own), channel_id=1, source_target_pairs={{1,5},{2,6},{5,1},{6,2},{9,13},{10,14},{13,9},{14,10},{17,21},{18,... | collective-permute-start | bytes 3538952 | tf_op jit(solution)/shard_map/ppermute | solution.py:1081
  441.6 23.3 %collective-permute-start.51 = (bf16[384,1152]{1,0:T(8,128)(2,1)}, bf16[384,1152]{1,0:T(8,128)(2,1)S(1)}, u32[]{:S(2)}, u32[]{:S(2)}) collective-permute-start(bf16[384,1152]{1,0:T(8,128)(2,1)} %shard_map.260), channel_id=1, source_target_pairs={{1,0},{2,3},{5,4},{6,7},{9,8},{10,11},{13,12},{14,15},{17,16},{18,... | collective-permute-start | bytes 2654216 | tf_op jit(solution)/shard_map/ppermute | solution.py:1081
  469.8 28.3 %collective-permute-start.53 = (bf16[1536,384]{1,0:T(8,128)(2,1)}, bf16[1536,384]{1,0:T(8,128)(2,1)S(1)}, u32[]{:S(2)}, u32[]{:S(2)}) collective-permute-start(bf16[1536,384]{1,0:T(8,128)(2,1)} %shard_map.266), channel_id=1, source_target_pairs={{1,0},{2,3},{5,4},{6,7},{9,8},{10,11},{13,12},{14,15},{17,16},{18,... | collective-permute-start | bytes 3538952 | tf_op jit(solution)/shard_map/ppermute | solution.py:1081
  471.9 22.5 %collective-permute-start.54 = (bf16[384,768]{1,0:T(8,128)(2,1)S(1)}, bf16[384,768]{1,0:T(8,128)(2,1)S(1)}, u32[]{:S(2)}, u32[]{:S(2)}) collective-permute-start(bf16[384,768]{1,0:T(8,128)(2,1)S(1)} %convolution_convert_fusion.6.own), channel_id=1, source_target_pairs={{1,0},{2,3},{5,4},{6,7},{9,8},{10,11},{13,12},{14,15},{17,16},{18,... | collective-permute-start | bytes 1769480 | tf_op jit(solution)/shard_map/ppermute | solution.py:1081
  505.1 19.0 %collective-permute-start.56 = (bf16[4112,128]{1,0:T(8,128)(2,1)S(1)}, bf16[4112,128]{1,0:T(8,128)(2,1)S(1)}, u32[]{:S(2)}, u32[]{:S(2)}) collective-permute-start(bf16[4112,128]{1,0:T(8,128)(2,1)S(1)} %get-tuple-element.350), channel_id=1, source_target_pairs={{0,8},{3,11},{4,12},{7,15},{8,16},{11,19},{12,20},{15,23},{16,24},... | collective-permute-start | bytes 3158024 | tf_op jit(solution)/shard_map/ppermute | solution.py:1081
  507.1 38.2 %collective-permute-start.61 = (bf16[4112,128]{1,0:T(8,128)(2,1)S(1)}, bf16[4112,128]{1,0:T(8,128)(2,1)S(1)}, u32[]{:S(2)}, u32[]{:S(2)}) collective-permute-start(bf16[4112,128]{1,0:T(8,128)(2,1)S(1)} %get-tuple-element.348), channel_id=1, source_target_pairs={{0,8},{3,11},{4,12},{7,15},{8,16},{11,19},{12,20},{15,23},{16,24},... | collective-permute-start | bytes 3158024 | tf_op jit(solution)/shard_map/ppermute | solution.py:1081
  509.0 28.2 %collective-permute-start.59 = (bf16[4112,128]{1,0:T(8,128)(2,1)S(1)}, bf16[4112,128]{1,0:T(8,128)(2,1)S(1)}, u32[]{:S(2)}, u32[]{:S(2)}) collective-permute-start(bf16[4112,128]{1,0:T(8,128)(2,1)S(1)} %get-tuple-element.349), channel_id=1, source_target_pairs={{0,4},{3,7},{4,0},{7,3},{8,12},{11,15},{12,8},{15,11},{16,20},{19,... | collective-permute-start | bytes 3158024 | tf_op jit(solution)/shard_map/ppermute | solution.py:1081
  527.9 21.3 %collective-permute-start.60 = (bf16[4112,128]{1,0:T(8,128)(2,1)}, bf16[4112,128]{1,0:T(8,128)(2,1)S(1)}, u32[]{:S(2)}, u32[]{:S(2)}) collective-permute-start(bf16[4112,128]{1,0:T(8,128)(2,1)} %shard_map.277), channel_id=1, source_target_pairs={{0,4},{3,7},{4,0},{7,3},{8,12},{11,15},{12,8},{15,11},{16,20},{19,... | collective-permute-start | bytes 3158024 | tf_op jit(solution)/shard_map/ppermute | solution.py:1081
  533.5 45.0 %collective-permute-start.57 = (bf16[1024,768]{1,0:T(8,128)(2,1)S(1)}, bf16[1024,768]{1,0:T(8,128)(2,1)}, u32[]{:S(2)}, u32[]{:S(2)}) collective-permute-start(bf16[1024,768]{1,0:T(8,128)(2,1)S(1)} %add_convert_fusion), channel_id=1, source_target_pairs={{0,2},{1,3},{2,0},{3,1},{4,6},{5,7},{6,4},{7,5},{8,10},{9,11},{10,... | collective-permute-start | bytes 4718600 | tf_op jit(solution)/shard_map/ppermute | solution.py:1081
  533.5 23.5 %collective-permute-start.62 = (bf16[4112,128]{1,0:T(8,128)(2,1)S(1)}, bf16[4112,128]{1,0:T(8,128)(2,1)S(1)}, u32[]{:S(2)}, u32[]{:S(2)}) collective-permute-start(bf16[4112,128]{1,0:T(8,128)(2,1)S(1)} %get-tuple-element.347), channel_id=1, source_target_pairs={{0,4},{3,7},{4,0},{7,3},{8,12},{11,15},{12,8},{15,11},{16,20},{19,... | collective-permute-start | bytes 3158024 | tf_op jit(solution)/shard_map/ppermute | solution.py:1081
  541.5 18.7 %collective-permute-start.63 = (bf16[4112,128]{1,0:T(8,128)(2,1)}, bf16[4112,128]{1,0:T(8,128)(2,1)S(1)}, u32[]{:S(2)}, u32[]{:S(2)}) collective-permute-start(bf16[4112,128]{1,0:T(8,128)(2,1)} %get-tuple-element.300), channel_id=1, source_target_pairs={{0,8},{3,11},{4,12},{7,15},{8,16},{11,19},{12,20},{15,23},{16,24},... | collective-permute-start | bytes 3158024 | tf_op jit(solution)/shard_map/ppermute | solution.py:1081
  545.3 22.2 %collective-permute-start.64 = (bf16[4112,128]{1,0:T(8,128)(2,1)S(1)}, bf16[4112,128]{1,0:T(8,128)(2,1)S(1)}, u32[]{:S(2)}, u32[]{:S(2)}) collective-permute-start(bf16[4112,128]{1,0:T(8,128)(2,1)S(1)} %get-tuple-element.346), channel_id=1, source_target_pairs={{0,4},{3,7},{4,0},{7,3},{8,12},{11,15},{12,8},{15,11},{16,20},{19,... | collective-permute-start | bytes 3158024 | tf_op jit(solution)/shard_map/ppermute | solution.py:1081
  553.9 18.7 %collective-permute-start.65 = (bf16[4112,128]{1,0:T(8,128)(2,1)}, bf16[4112,128]{1,0:T(8,128)(2,1)S(1)}, u32[]{:S(2)}, u32[]{:S(2)}) collective-permute-start(bf16[4112,128]{1,0:T(8,128)(2,1)} %get-tuple-element.304), channel_id=1, source_target_pairs={{0,8},{3,11},{4,12},{7,15},{8,16},{11,19},{12,20},{15,23},{16,24},... | collective-permute-start | bytes 3158024 | tf_op jit(solution)/shard_map/ppermute | solution.py:1081
  557.1 46.1 %collective-permute-start.55 = (bf16[1024,768]{1,0:T(8,128)(2,1)S(1)}, bf16[1024,768]{1,0:T(8,128)(2,1)}, u32[]{:S(2)}, u32[]{:S(2)}) collective-permute-start(bf16[1024,768]{1,0:T(8,128)(2,1)S(1)} %copy-done.38), channel_id=1, source_target_pairs={{0,1},{3,2},{4,5},{7,6},{8,9},{11,10},{12,13},{15,14},{16,17},{19,... | collective-permute-start | bytes 4718600 | tf_op jit(solution)/shard_map/ppermute | solution.py:1081
  560.2 24.1 %collective-permute-start.66 = (bf16[4112,128]{1,0:T(8,128)(2,1)}, bf16[4112,128]{1,0:T(8,128)(2,1)}, u32[]{:S(2)}, u32[]{:S(2)}) collective-permute-start(bf16[4112,128]{1,0:T(8,128)(2,1)} %get-tuple-element.306), channel_id=1, source_target_pairs={{0,4},{3,7},{4,0},{7,3},{8,12},{11,15},{12,8},{15,11},{16,20},{19,... | collective-permute-start | bytes 3158024 | tf_op jit(solution)/shard_map/ppermute | solution.py:1081
  567.4 19.1 %collective-permute-start.67 = (bf16[4112,128]{1,0:T(8,128)(2,1)}, bf16[4112,128]{1,0:T(8,128)(2,1)}, u32[]{:S(2)}, u32[]{:S(2)}) collective-permute-start(bf16[4112,128]{1,0:T(8,128)(2,1)} %get-tuple-element.309), channel_id=1, source_target_pairs={{0,8},{3,11},{4,12},{7,15},{8,16},{11,19},{12,20},{15,23},{16,24},... | collective-permute-start | bytes 3158024 | tf_op jit(solution)/shard_map/ppermute | solution.py:1081
  572.6 19.5 %collective-permute-start.68 = (bf16[4112,128]{1,0:T(8,128)(2,1)}, bf16[4112,128]{1,0:T(8,128)(2,1)}, u32[]{:S(2)}, u32[]{:S(2)}) collective-permute-start(bf16[4112,128]{1,0:T(8,128)(2,1)} %get-tuple-element.311), channel_id=1, source_target_pairs={{0,4},{3,7},{4,0},{7,3},{8,12},{11,15},{12,8},{15,11},{16,20},{19,... | collective-permute-start | bytes 3158024 | tf_op jit(solution)/shard_map/ppermute | solution.py:1081
  578.4 19.1 %collective-permute-start.69 = (bf16[4112,128]{1,0:T(8,128)(2,1)}, bf16[4112,128]{1,0:T(8,128)(2,1)}, u32[]{:S(2)}, u32[]{:S(2)}) collective-permute-start(bf16[4112,128]{1,0:T(8,128)(2,1)} %shard_map.285), channel_id=1, source_target_pairs={{0,8},{3,11},{4,12},{7,15},{8,16},{11,19},{12,20},{15,23},{16,24},... | collective-permute-start | bytes 3158024 | tf_op jit(solution)/shard_map/ppermute | solution.py:1081
  584.3 20.8 %collective-permute-start.58 = (bf16[1024,384]{1,0:T(8,128)(2,1)}, bf16[1024,384]{1,0:T(8,128)(2,1)}, u32[]{:S(2)}, u32[]{:S(2)}) collective-permute-start(bf16[1024,384]{1,0:T(8,128)(2,1)} %select_convert_fusion), channel_id=1, source_target_pairs={{0,1},{3,2},{4,5},{7,6},{8,9},{11,10},{12,13},{15,14},{16,17},{19,... | collective-permute-start | bytes 2359304 | tf_op jit(solution)/shard_map/ppermute | solution.py:1081
  586.5 21.9 %collective-permute-start.70 = (bf16[4112,128]{1,0:T(8,128)(2,1)}, bf16[4112,128]{1,0:T(8,128)(2,1)}, u32[]{:S(2)}, u32[]{:S(2)}) collective-permute-start(bf16[4112,128]{1,0:T(8,128)(2,1)} %get-tuple-element.315), channel_id=1, source_target_pairs={{0,4},{3,7},{4,0},{7,3},{8,12},{11,15},{12,8},{15,11},{16,20},{19,... | collective-permute-start | bytes 3158024 | tf_op jit(solution)/shard_map/ppermute | solution.py:1081
  592.1 18.8 %collective-permute-start.71 = (bf16[4112,128]{1,0:T(8,128)(2,1)}, bf16[4112,128]{1,0:T(8,128)(2,1)}, u32[]{:S(2)}, u32[]{:S(2)}) collective-permute-start(bf16[4112,128]{1,0:T(8,128)(2,1)} %shard_map.287), channel_id=1, source_target_pairs={{0,8},{3,11},{4,12},{7,15},{8,16},{11,19},{12,20},{15,23},{16,24},... | collective-permute-start | bytes 3158024 | tf_op jit(solution)/shard_map/ppermute | solution.py:1081
  (135 other events, 778.2 us)

commit v16 on v15

--- a/solution.py
+++ b/solution.py
@@ -24,7 +24,7 @@
 HEADS = HALF // HEAD_DIM
 ROWS = 256
 KEYS = 512
-VEC_ROWS = 16
+VEC_ROWS = 32
 CHUNKS = 4
 
 AXES = ("dp", "tensor")
@@ -1038,8 +1038,12 @@
 
 def reduce_call(j, n, buffer, arrived, carried, payload, x_rel=0):
     last = j >= 2 or x_rel == 1
-    at = lambda j, x_rel: pl.BlockSpec((payload, BS), lambda i: ((j * 2 + x_rel) * 2 + n, 0))
-    whole = fixed((payload, BS))
+    steps = 3
+    rows_n = payload // steps
+    at = lambda j, x_rel: pl.BlockSpec(
+        (rows_n, BS), lambda i: (((j * 2 + x_rel) * 2 + n) * steps + i, 0)
+    )
+    whole = pl.BlockSpec((rows_n, BS), lambda i: (i, 0))
     operands = [stay(buffer), stay(arrived)] + ([] if carried is None else [stay(carried)])
     specs = [at(j, x_rel)] + [whole] * (len(operands) - 1)
     if not last:
@@ -1049,7 +1053,7 @@
     made = pl.pallas_call(
         functools.partial(reduce_kernel, carried is not None, last),
         out_shape=outs,
-        grid=(1,),
+        grid=(steps,),
         in_specs=specs,
         out_specs=[whole] * len(outs),
         compiler_params=params(8),
@@ -1346,7 +1350,7 @@
     buffer = place_tiles(("out", top), go1, ao1, buffer)
     buffer = place_tiles(("qkv", top), gq1, aq1, buffer)
     buffer = place_tiles(("down", low), gd0, ad0, buffer)
-    gbm, xb, aq0, av, buffer = hold(gbm, xb, aq0, av, buffer)
+    gbm, xb, aq0, ao0, av, buffer = hold(gbm, xb, aq0, ao0, av, buffer)
     ab = over(half_sum(half_at * 0, gbm, xb)) if grid3 else None
     buffer = place_tiles(("up", low), gu0, au0, buffer)
     buffer = place_base(1, gbt, None, buffer)

time: 637 us -> 638 us (level)
    unnamed x226 -> x230, local copies, waits for them, and re-layouts: 27.9 us -> 26.9 us
  transfers between devices with their start and end apart: 73 -> 73, of which waited for: 34 -> 36; matrix products, arithmetic and copies ran while one was open for 10% -> 10% of each run, Pallas kernels for 32% -> 33%
where the time goes in v16:
time: 638 us; the launch traced here: 628 us
  Pallas kernels  294 us (46%)
  waiting for transfers between devices  124 us (19%)
  starting transfers between devices  106 us (17%)
  local copies, waits for them, and re-layouts  41.4 us (6%)
  matrix products  30.9 us (5%)
  other arithmetic  28.8 us (5%)
    ppermute x73, waiting for transfers between devices, send(): return lax.ppermute(value, AXES, route)  124 us
    ppermute x73, starting transfers between devices, send(): return lax.ppermute(value, AXES, route)  106 us
    pallas_call x2, Pallas kernels, attend_back_call(): pl.pallas_call(attend_back_kernel, out_shape=[shape(D, f32), shape(D, bf1...  45.7 us
    pallas_call x10, Pallas kernels, scatter_matrix(): pl.pallas_call(functools.partial(scatter_kernel, rows_n, cols_n, steps, p...  35.2 us
    pallas_call x8, Pallas kernels, reduce_call(): pl.pallas_call(functools.partial(reduce_kernel, carried is not None, last...  31.5 us
    pallas_call x2, Pallas kernels, attend_call(): pl.pallas_call(functools.partial(attend_kernel, layer), out_shape=[jax.Sh...  29.7 us
    dot_general x12, matrix products, dot_tn(): lax.dot_general(left, right, (((0,), (0,)), ((), ())), preferred_element_...  27.8 us
    unnamed x230, local copies, waits for them, and re-layouts  26.9 us
  transfers between devices with their start and end apart: 73, of which 36 were waited for; matrix products, arithmetic and copies ran while one was open for 10% of the time, Pallas kernels for 33%

profile of v16, /device:TPU:0, one launch (start us, length us, event | category | flops | bytes accessed | tf_op | source)
XLA Modules:
  0.0 628.4 jit_solution(6000994511172430526)
XLA Ops:
  18.9 6.0 shard_map.222.refs_3_
  26.1 6.2 collective-permute-done.5.refs_5_
  43.8 6.5 %shard_map.224.refs_3_ = bf16[1024,768]{1,0:T(8,128)(2,1)S(1)} custom-call(s32[4,3]{1,0:T(4,128)S(1)} %convert_element_type.120.present, s32[1]{0:T(128)} %bitcast.6.half.part, bf16[1024,768]{1,0:T(8,128)(2,1)} %get-tuple-element.171.patch_ref.refs_2_, s32[1024,1]{1,0:T(8,128)S(1)} %copy.141.class_ref, bf16[3,3072,768]{2,1,0:T(8,128)(2,1)} %pinv_ref.9), custom_call_target="tpu_custom_call" | custom-call | flops 1811939328 | bytes 6684672 | tf_op jit(solution)/shard_map/pallas_call | solution.py:439
  54.9 12.5 %collective-permute-done.9.refs_4_ = bf16[4128,128]{1,0:T(8,128)(2,1)S(1)} collective-permute-done((bf16[4128,128]{1,0:T(8,128)(2,1)}, bf16[4128,128]{1,0:T(8,128)(2,1)S(1)}, u32[]{:S(2)}, u32[]{:S(2)}) %collective-permute-start.9) | collective-permute-done | bytes 1056800 | tf_op jit(solution)/shard_map/ppermute | solution.py:1085
  67.3 5.7 collective-permute-done.8.refs_1_
  81.0 6.0 shard_map.226.refs_3_
  93.7 12.4 %collective-permute-done.12.refs_4_ = bf16[4128,128]{1,0:T(8,128)(2,1)S(1)} collective-permute-done((bf16[4128,128]{1,0:T(8,128)(2,1)S(1)}, bf16[4128,128]{1,0:T(8,128)(2,1)S(1)}, u32[]{:S(2)}, u32[]{:S(2)}) %collective-permute-start.12) | collective-permute-done | bytes 1056800 | tf_op jit(solution)/shard_map/ppermute | solution.py:1085
  106.1 6.1 collective-permute-done.11.refs_1_
  120.1 6.2 shard_map.228.refs_3_
  132.7 16.7 %collective-permute-done.14.refs_1_ = bf16[4128,128]{1,0:T(8,128)(2,1)S(1)} collective-permute-done((bf16[4128,128]{1,0:T(8,128)(2,1)S(1)}, bf16[4128,128]{1,0:T(8,128)(2,1)S(1)}, u32[]{:S(2)}, u32[]{:S(2)}) %collective-permute-start.14) | collective-permute-done | bytes 1056800 | tf_op jit(solution)/shard_map/ppermute | solution.py:1085
  157.3 5.6 collective-permute-done.28
  173.4 14.2 %shard_map.230 = (bf16[3072,384]{1,0:T(8,128)(2,1)}, bf16[2304,384]{1,0:T(8,128)(2,1)}, bf16[768,384]{1,0:T(8,128)(2,1)}, bf16[3072,384]{1,0:T(8,128)(2,1)}, bf1...) custom-call(s32[16]{0:T(128)S(1)} %stack.95.owner, ...), custom_call_target="tpu_custom_call" | custom-call | bytes 33030144 | tf_op jit(solution)/shard_map/pallas_call | solution.py:243
  187.8 6.8 %shard_map.231.refs_0_ = bf16[1024,384]{1,0:T(8,128)(2,1)S(1)} custom-call(s32[1]{0:T(128)} %bitcast.6.half.part, bf16[1024,768]{1,0:T(8,128)(2,1)} %get-tuple-element.169.refs_0_, bf16[1024,768]{1,0:T(8,128)(2,1)} %get-tuple-element.172.refs_1_, bf16[1024,768]{1,0:T(8,128)(2,1)} %get-tuple-element.175.refs_2_, ...), custom_call_target="tpu_custom_call" | custom-call | flops 2415919104 | bytes 9437184 | tf_op jit(solution)/shard_map/pallas_call | solution.py:552
  197.1 4.8 shard_map.232
  202.0 14.9 %shard_map.233 = (bf16[1024,384]{1,0:T(8,128)(2,1)S(1)}, f32[8,1024]{1,0:T(8,128)S(1)}, bf16[1024,768]{1,0:T(8,128)(2,1)S(1)}) custom-call(s32[4]{0:T(128)S(1)} %get-tuple-element.372.low_ref, s32[4]{0:T(128)S(1)} %get-tuple-element.365.high_ref, bf16[1024,384]{1,0:T(8,128)(2,1)S(1)} %get-tuple-element.192.q_ref, ...), custom_call_target="tpu_custom_call" | custom-call | flops 6442450944 | bytes 6291456 | tf_op jit(solution)/shard_map/pallas_call | solution.py:679
  221.3 9.4 %shard_map.234 = (f32[1024,768]{1,0:T(8,128)S(1)}, bf16[1024,768]{1,0:T(8,128)(2,1)}, bf16[1024,1536]{1,0:T(8,128)(2,1)}, bf16[1024,1536]{1,0:T(8,128)(2,1)}, bf16[1024,768]{1,0:T(8,128)(2,1)S(1)}) custom-call(f32[1024,768]{1,0:T(8,128)S(1)} %get-tuple-element.191.base.hid, bf16[1024,768]{1,0:T(8,128)(2,1)S(1)} %get-tuple-element.196.own, ...), custom_call_target="tpu_custom_call" | custom-call | flops 4831838208 | bytes 18874368 | tf_op jit(solution)/shard_map/pallas_call | solution.py:742
  234.0 4.4 shard_map.235
  238.5 14.8 %shard_map.236 = (bf16[1024,384]{1,0:T(8,128)(2,1)S(1)}, f32[8,1024]{1,0:T(8,128)S(1)}, bf16[1024,768]{1,0:T(8,128)(2,1)S(1)}) custom-call(s32[4]{0:T(128)S(1)} %get-tuple-element.372.low_ref, s32[4]{0:T(128)S(1)} %get-tuple-element.365.high_ref, bf16[1024,384]{1,0:T(8,128)(2,1)S(1)} %get-tuple-element.203.q_ref, ...), custom_call_target="tpu_custom_call" | custom-call | flops 6442450944 | bytes 6291456 | tf_op jit(solution)/shard_map/pallas_call | solution.py:679
  256.9 9.4 %shard_map.237 = (f32[1024,768]{1,0:T(8,128)S(1)}, bf16[1024,768]{1,0:T(8,128)(2,1)}, bf16[1024,1536]{1,0:T(8,128)(2,1)}, bf16[1024,1536]{1,0:T(8,128)(2,1)}, bf16[1024,768]{1,0:T(8,128)(2,1)S(1)}) custom-call(f32[1024,768]{1,0:T(8,128)S(1)} %get-tuple-element.202.base.hid, bf16[1024,768]{1,0:T(8,128)(2,1)S(1)} %get-tuple-element.207.own, ...), custom_call_target="tpu_custom_call" | custom-call | flops 4831838208 | bytes 18874368 | tf_op jit(solution)/shard_map/pallas_call | solution.py:742
  268.3 11.3 %shard_map.238 = (bf16[1024,768]{1,0:T(8,128)(2,1)S(1)}, bf16[1024,1536]{1,0:T(8,128)(2,1)S(1)}, bf16[1024,768]{1,0:T(8,128)(2,1)S(1)}, f32[1,768]{1,0:T(1,128)S...) custom-call(bf16[1024,768]{1,0:T(8,128)(2,1)S(1)} %broadcast_select_fusion.refs_0_, ...), custom_call_target="tpu_custom_call" | custom-call | flops 4831838208 | bytes 18874368 | tf_op jit(solution)/shard_map/pallas_call | solution.py:794
  284.1 4.1 convolution_convert_fusion.3.refs_1_
  293.6 22.8 %shard_map.240 = (f32[1024,768]{1,0:T(8,128)S(1)}, bf16[1024,768]{1,0:T(8,128)(2,1)S(1)}, bf16[1024,384]{1,0:T(8,128)(2,1)S(1)}, bf16[1024,384]{1,0:T(8,128)(2,1...) custom-call(s32[4]{0:T(128)S(1)} %get-tuple-element.371.low_ref, s32[4]{0:T(128)S(1)} %get-tuple-element.366.high_ref, ...), custom_call_target="tpu_custom_call" | custom-call | flops 11274289152 | bytes 15728640 | tf_op jit(solution)/shard_map/pallas_call | solution.py:886
  318.3 5.5 shard_map.243
  339.9 11.2 %shard_map.244 = (f32[1024,768]{1,0:T(8,128)S(1)}, bf16[1024,768]{1,0:T(8,128)(2,1)S(1)}, bf16[1024,1536]{1,0:T(8,128)(2,1)S(1)}, bf16[1024,768]{1,0:T(8,128)(2,...) custom-call(f32[1024,768]{1,0:T(8,128)S(1)} %get-tuple-element.219.refs_0_, ...), custom_call_target="tpu_custom_call" | custom-call | flops 4831838208 | bytes 18874368 | tf_op jit(solution)/shard_map/pallas_call | solution.py:794
  356.6 4.6 collective-permute-start.40
  361.2 4.0 convolution_convert_fusion.1.refs_1_
  365.2 4.2 convolution_convert_fusion.refs_2_
  369.3 4.0 collective-permute-done.44.refs_4_
  378.9 4.2 shard_map.252.refs_1_
  383.1 4.1 shard_map.253.refs_4_
  387.3 22.8 %shard_map.250 = (f32[1024,768]{1,0:T(8,128)S(1)}, bf16[1024,768]{1,0:T(8,128)(2,1)S(1)}, bf16[1024,384]{1,0:T(8,128)(2,1)S(1)}, bf16[1024,384]{1,0:T(8,128)(2,1...) custom-call(s32[4]{0:T(128)S(1)} %get-tuple-element.371.low_ref, s32[4]{0:T(128)S(1)} %get-tuple-element.366.high_ref, ...), custom_call_target="tpu_custom_call" | custom-call | flops 11274289152 | bytes 15728640 | tf_op jit(solution)/shard_map/pallas_call | solution.py:886
  411.9 5.6 shard_map.255
  433.8 5.4 collective-permute-done.48.refs_1_
  453.4 4.2 shard_map.264.refs_5_
  462.2 9.1 %collective-permute-done.52.refs_3_ = bf16[384,768]{1,0:T(8,128)(2,1)S(1)} collective-permute-done((bf16[384,768]{1,0:T(8,128)(2,1)S(1)}, bf16[384,768]{1,0:T(8,128)(2,1)S(1)}, u32[]{:S(2)}, u32[]{:S(2)}) %collective-permute-start.52) | collective-permute-done | bytes 589856 | tf_op jit(solution)/shard_map/ppermute | solution.py:1085
  478.9 4.1 shard_map.267.refs_0_
  508.5 3.6 collective-permute-start.59
  512.1 10.2 %shard_map.274.refs_2_ = bf16[3,384,768]{2,1,0:T(8,128)(2,1)S(1)} custom-call(bf16[3072,384]{1,0:T(8,128)(2,1)} %get-tuple-element.295.base, bf16[3,3072,768]{2,1,0:T(8,128)(2,1)} %pinv_ref.9), custom_call_target="tpu_custom_call" | custom-call | flops 5435817984 | bytes 14155776 | tf_op jit(solution)/shard_map/pallas_call | solution.py:470
  533.6 3.6 collective-permute-start.62
  538.3 3.9 shard_map.279
  547.3 4.2 shard_map.281
  551.5 5.1 collective-permute-start.65
  563.1 4.1 shard_map.283
  574.5 3.7 shard_map.285
  589.8 3.7 shard_map.287
  597.8 3.7 shard_map.290
  612.5 4.7 shard_map.289.near
  619.2 8.7 %shard_map.291 = (f32[32,128,128]{2,1,0:T(8,128)}, f32[32,128,128]{2,1,0:T(8,128)}, f32[32,128,128]{2,1,0:T(8,128)}, f32[32,128,128]{2,1,0:T(8,128)}) custom-call(s32[32]{0:T(128)S(1)} %convert_element_type.148.used, s32[1]{0:T(128)} %bitcast.27.flag.home, bf16[4128,128]{1,0:T(8,128)(2,1)} %shard_map.289.near, ...), custom_call_target="tpu_custom_call" | custom-call | flops 5905580032 | bytes 19922944 | tf_op jit(solution)/shard_map/pallas_call | solution.py:1011
  (498 shorter events, 266.5 us)
Async XLA Ops:
  4.2 28.7 %collective-permute-start.4 = (bf16[4128,128]{1,0:T(8,128)(2,1)}, bf16[4128,128]{1,0:T(8,128)(2,1)}, u32[]{:S(2)}, u32[]{:S(2)}) collective-permute-start(bf16[4128,128]{1,0:T(8,128)(2,1)} %pad_maximum_fusion.2), channel_id=1, source_target_pairs={{0,8},{1,9},{2,10},{3,11},{4,12},{5,13},{6,14},{7,15},{8,16},{9,17... | collective-permute-start | bytes 3170312 | tf_op jit(solution)/shard_map/ppermute | solution.py:1085
  7.2 25.7 %collective-permute-start.1 = (bf16[4128,128]{1,0:T(8,128)(2,1)}, bf16[4128,128]{1,0:T(8,128)(2,1)S(1)}, u32[]{:S(2)}, u32[]{:S(2)}) collective-permute-start(bf16[4128,128]{1,0:T(8,128)(2,1)} %pad_maximum_fusion.2), channel_id=1, source_target_pairs={{0,1},{1,0},{2,3},{3,2},{4,5},{5,4},{6,7},{7,6},{8,9},{9,8},{10,11... | collective-permute-start | bytes 3170312 | tf_op jit(solution)/shard_map/ppermute | solution.py:1085
  8.7 24.7 %collective-permute-start = (bf16[4128,128]{1,0:T(8,128)(2,1)}, bf16[4128,128]{1,0:T(8,128)(2,1)S(1)}, u32[]{:S(2)}, u32[]{:S(2)}) collective-permute-start(bf16[4128,128]{1,0:T(8,128)(2,1)} %pad_maximum_fusion.2), channel_id=1, source_target_pairs={{0,4},{1,5},{2,6},{3,7},{4,0},{5,1},{6,2},{7,3},{8,12},{9,13},{10,... | collective-permute-start | bytes 3170312 | tf_op jit(solution)/shard_map/ppermute | solution.py:1085
  14.0 18.3 %collective-permute-start.5 = (s32[1,504]{1,0:T(1,128)S(1)}, s32[1,504]{1,0:T(1,128)S(1)}, u32[]{:S(2)}, u32[]{:S(2)}) collective-permute-start(s32[1,504]{1,0:T(1,128)S(1)} %copy-done.99), channel_id=1, source_target_pairs={{0,1},{1,0},{2,3},{3,2},{4,5},{5,4},{6,7},{7,6},{8,9},{9,8},{10,11... | collective-permute-start | bytes 6056 | tf_op jit(solution)/shard_map/ppermute | solution.py:1085
  41.6 25.7 %collective-permute-start.9 = (bf16[4128,128]{1,0:T(8,128)(2,1)}, bf16[4128,128]{1,0:T(8,128)(2,1)S(1)}, u32[]{:S(2)}, u32[]{:S(2)}) collective-permute-start(bf16[4128,128]{1,0:T(8,128)(2,1)} %get-tuple-element.170), channel_id=1, source_target_pairs={{0,8},{1,9},{2,10},{3,11},{4,12},{5,13},{6,14},{7,15},{8,16},{9,17... | collective-permute-start | bytes 3170312 | tf_op jit(solution)/shard_map/ppermute | solution.py:1085
  42.6 30.4 %collective-permute-start.8 = (bf16[4128,128]{1,0:T(8,128)(2,1)}, bf16[4128,128]{1,0:T(8,128)(2,1)S(1)}, u32[]{:S(2)}, u32[]{:S(2)}) collective-permute-start(bf16[4128,128]{1,0:T(8,128)(2,1)} %get-tuple-element.170), channel_id=1, source_target_pairs={{0,1},{1,0},{2,3},{3,2},{4,5},{5,4},{6,7},{7,6},{8,9},{9,8},{10,11... | collective-permute-start | bytes 3170312 | tf_op jit(solution)/shard_map/ppermute | solution.py:1085
  43.3 30.9 %collective-permute-start.7 = (bf16[4128,128]{1,0:T(8,128)(2,1)}, bf16[4128,128]{1,0:T(8,128)(2,1)S(1)}, u32[]{:S(2)}, u32[]{:S(2)}) collective-permute-start(bf16[4128,128]{1,0:T(8,128)(2,1)} %get-tuple-element.170), channel_id=1, source_target_pairs={{0,4},{1,5},{2,6},{3,7},{4,0},{5,1},{6,2},{7,3},{8,12},{9,13},{10,... | collective-permute-start | bytes 3170312 | tf_op jit(solution)/shard_map/ppermute | solution.py:1085
  52.1 113.3 %collective-permute-start.15 = (bf16[4128,128]{1,0:T(8,128)(2,1)S(1)}, bf16[4128,128]{1,0:T(8,128)(2,1)S(1)}, u32[]{:S(2)}, u32[]{:S(2)}) collective-permute-start(bf16[4128,128]{1,0:T(8,128)(2,1)S(1)} %get-tuple-element.353), channel_id=1, source_target_pairs={{0,2},{1,3},{2,0},{3,1},{4,6},{5,7},{6,4},{7,5},{8,10},{9,11},{10,... | collective-permute-start | bytes 3170312 | tf_op jit(solution)/shard_map/ppermute | solution.py:1085
  54.9 112.0 %collective-permute-start.18 = (bf16[4128,128]{1,0:T(8,128)(2,1)S(1)}, bf16[4128,128]{1,0:T(8,128)(2,1)}, u32[]{:S(2)}, u32[]{:S(2)}) collective-permute-start(bf16[4128,128]{1,0:T(8,128)(2,1)S(1)} %broadcast_select_fusion.8), channel_id=1, source_target_pairs={{0,2},{1,3},{2,0},{3,1},{4,6},{5,7},{6,4},{7,5},{8,10},{9,11},{10,... | collective-permute-start | bytes 3170312 | tf_op jit(solution)/shard_map/ppermute | solution.py:1085
  80.2 25.9 %collective-permute-start.12 = (bf16[4128,128]{1,0:T(8,128)(2,1)S(1)}, bf16[4128,128]{1,0:T(8,128)(2,1)S(1)}, u32[]{:S(2)}, u32[]{:S(2)}) collective-permute-start(bf16[4128,128]{1,0:T(8,128)(2,1)S(1)} %copy-done.58), channel_id=1, source_target_pairs={{0,8},{1,9},{2,10},{3,11},{4,12},{5,13},{6,14},{7,15},{8,16},{9,17... | collective-permute-start | bytes 3170312 | tf_op jit(solution)/shard_map/ppermute | solution.py:1085
  89.6 22.6 %collective-permute-start.11 = (bf16[4128,128]{1,0:T(8,128)(2,1)S(1)}, bf16[4128,128]{1,0:T(8,128)(2,1)S(1)}, u32[]{:S(2)}, u32[]{:S(2)}) collective-permute-start(bf16[4128,128]{1,0:T(8,128)(2,1)S(1)} %copy-done.58), channel_id=1, source_target_pairs={{0,1},{1,0},{2,3},{3,2},{4,5},{5,4},{6,7},{7,6},{8,9},{9,8},{10,11... | collective-permute-start | bytes 3170312 | tf_op jit(solution)/shard_map/ppermute | solution.py:1085
  90.8 22.3 %collective-permute-start.10 = (bf16[4128,128]{1,0:T(8,128)(2,1)S(1)}, bf16[4128,128]{1,0:T(8,128)(2,1)S(1)}, u32[]{:S(2)}, u32[]{:S(2)}) collective-permute-start(bf16[4128,128]{1,0:T(8,128)(2,1)S(1)} %copy-done.58), channel_id=1, source_target_pairs={{0,4},{1,5},{2,6},{3,7},{4,0},{5,1},{6,2},{7,3},{8,12},{9,13},{10,... | collective-permute-start | bytes 3170312 | tf_op jit(solution)/shard_map/ppermute | solution.py:1085
  106.1 60.8 %collective-permute-start.19 = (bf16[4128,128]{1,0:T(8,128)(2,1)S(1)}, bf16[4128,128]{1,0:T(8,128)(2,1)}, u32[]{:S(2)}, u32[]{:S(2)}) collective-permute-start(bf16[4128,128]{1,0:T(8,128)(2,1)S(1)} %broadcast_select_fusion.7), channel_id=1, source_target_pairs={{0,2},{1,3},{2,0},{3,1},{4,6},{5,7},{6,4},{7,5},{8,10},{9,11},{10,... | collective-permute-start | bytes 3170312 | tf_op jit(solution)/shard_map/ppermute | solution.py:1085
  128.6 20.8 %collective-permute-start.14 = (bf16[4128,128]{1,0:T(8,128)(2,1)S(1)}, bf16[4128,128]{1,0:T(8,128)(2,1)S(1)}, u32[]{:S(2)}, u32[]{:S(2)}) collective-permute-start(bf16[4128,128]{1,0:T(8,128)(2,1)S(1)} %copy-done.60), channel_id=1, source_target_pairs={{0,1},{1,0},{2,3},{3,2},{4,5},{5,4},{6,7},{7,6},{8,9},{9,8},{10,11... | collective-permute-start | bytes 3170312 | tf_op jit(solution)/shard_map/ppermute | solution.py:1085
  129.3 20.9 %collective-permute-start.13 = (bf16[4128,128]{1,0:T(8,128)(2,1)S(1)}, bf16[4128,128]{1,0:T(8,128)(2,1)S(1)}, u32[]{:S(2)}, u32[]{:S(2)}) collective-permute-start(bf16[4128,128]{1,0:T(8,128)(2,1)S(1)} %copy-done.60), channel_id=1, source_target_pairs={{0,4},{1,5},{2,6},{3,7},{4,0},{5,1},{6,2},{7,3},{8,12},{9,13},{10,... | collective-permute-start | bytes 3170312 | tf_op jit(solution)/shard_map/ppermute | solution.py:1085
  231.0 22.9 %collective-permute-start.6 = (bf16[1024,768]{1,0:T(8,128)(2,1)S(1)}, bf16[1024,768]{1,0:T(8,128)(2,1)S(1)}, u32[]{:S(2)}, u32[]{:S(2)}) collective-permute-start(bf16[1024,768]{1,0:T(8,128)(2,1)S(1)} %copy-done.96), channel_id=1, source_target_pairs={{0,2},{3,1},{4,6},{7,5},{8,10},{11,9},{12,14},{15,13},{16,18},{19,... | collective-permute-start | bytes 4718600 | tf_op jit(solution)/shard_map/ppermute | solution.py:1085
  267.9 23.9 %collective-permute-start.38 = (bf16[1024,768]{1,0:T(8,128)(2,1)S(1)}, bf16[1024,768]{1,0:T(8,128)(2,1)S(1)}, u32[]{:S(2)}, u32[]{:S(2)}) collective-permute-start(bf16[1024,768]{1,0:T(8,128)(2,1)S(1)} %get-tuple-element.226), channel_id=1, source_target_pairs={{0,2},{1,3},{2,0},{3,1},{4,6},{5,7},{6,4},{7,5},{8,10},{9,11},{10,... | collective-permute-start | bytes 4718600 | tf_op jit(solution)/shard_map/ppermute | solution.py:1085
  282.8 33.7 %collective-permute-start.36 = (bf16[1536,768]{1,0:T(8,128)(2,1)S(1)}, bf16[1536,768]{1,0:T(8,128)(2,1)S(1)}, u32[]{:S(2)}, u32[]{:S(2)}) collective-permute-start(bf16[1536,768]{1,0:T(8,128)(2,1)S(1)} %convolution_convert_fusion.2.own), channel_id=1, source_target_pairs={{1,0},{2,3},{5,4},{6,7},{9,8},{10,11},{13,12},{14,15},{17,16},{18,... | collective-permute-start | bytes 7077896 | tf_op jit(solution)/shard_map/ppermute | solution.py:1085
  290.7 25.8 %collective-permute-start.37 = (bf16[384,1536]{1,0:T(8,128)(2,1)}, bf16[384,1536]{1,0:T(8,128)(2,1)S(1)}, u32[]{:S(2)}, u32[]{:S(2)}) collective-permute-start(bf16[384,1536]{1,0:T(8,128)(2,1)} %shard_map.241), channel_id=1, source_target_pairs={{1,5},{2,6},{5,1},{6,2},{9,13},{10,14},{13,9},{14,10},{17,21},{18,... | collective-permute-start | bytes 3538952 | tf_op jit(solution)/shard_map/ppermute | solution.py:1085
  330.1 21.1 %collective-permute-start.43 = (bf16[384,1536]{1,0:T(8,128)(2,1)}, bf16[384,1536]{1,0:T(8,128)(2,1)S(1)}, u32[]{:S(2)}, u32[]{:S(2)}) collective-permute-start(bf16[384,1536]{1,0:T(8,128)(2,1)} %shard_map.246), channel_id=1, source_target_pairs={{1,0},{2,3},{5,4},{6,7},{9,8},{10,11},{13,12},{14,15},{17,16},{18,... | collective-permute-start | bytes 3538952 | tf_op jit(solution)/shard_map/ppermute | solution.py:1085
  338.6 30.7 %collective-permute-start.41 = (bf16[384,768]{1,0:T(8,128)(2,1)S(1)}, bf16[384,768]{1,0:T(8,128)(2,1)S(1)}, u32[]{:S(2)}, u32[]{:S(2)}) collective-permute-start(bf16[384,768]{1,0:T(8,128)(2,1)S(1)} %convolution_convert_fusion.11.own), channel_id=1, source_target_pairs={{1,0},{2,3},{5,4},{6,7},{9,8},{10,11},{13,12},{14,15},{17,16},{18,... | collective-permute-start | bytes 1769480 | tf_op jit(solution)/shard_map/ppermute | solution.py:1085
  355.2 18.1 %collective-permute-start.44 = (bf16[384,1152]{1,0:T(8,128)(2,1)}, bf16[384,1152]{1,0:T(8,128)(2,1)S(1)}, u32[]{:S(2)}, u32[]{:S(2)}) collective-permute-start(bf16[384,1152]{1,0:T(8,128)(2,1)} %shard_map.248), channel_id=1, source_target_pairs={{1,0},{2,3},{5,4},{6,7},{9,8},{10,11},{13,12},{14,15},{17,16},{18,... | collective-permute-start | bytes 2654216 | tf_op jit(solution)/shard_map/ppermute | solution.py:1085
  356.6 30.6 %collective-permute-start.40 = (bf16[1024,768]{1,0:T(8,128)(2,1)S(1)}, bf16[1024,768]{1,0:T(8,128)(2,1)S(1)}, u32[]{:S(2)}, u32[]{:S(2)}) collective-permute-start(bf16[1024,768]{1,0:T(8,128)(2,1)S(1)} %get-tuple-element.231.own), channel_id=1, source_target_pairs={{0,2},{1,3},{2,0},{3,1},{4,6},{5,7},{6,4},{7,5},{8,10},{9,11},{10,... | collective-permute-start | bytes 4718600 | tf_op jit(solution)/shard_map/ppermute | solution.py:1085
  374.2 35.9 %collective-permute-start.45 = (bf16[1536,768]{1,0:T(8,128)(2,1)}, bf16[1536,768]{1,0:T(8,128)(2,1)S(1)}, u32[]{:S(2)}, u32[]{:S(2)}) collective-permute-start(bf16[1536,768]{1,0:T(8,128)(2,1)} %get-tuple-element.249.own), channel_id=1, source_target_pairs={{1,0},{2,3},{5,4},{6,7},{9,8},{10,11},{13,12},{14,15},{17,16},{18,... | collective-permute-start | bytes 7077896 | tf_op jit(solution)/shard_map/ppermute | solution.py:1085
  378.1 32.0 %collective-permute-start.46 = (bf16[384,1536]{1,0:T(8,128)(2,1)}, bf16[384,1536]{1,0:T(8,128)(2,1)S(1)}, u32[]{:S(2)}, u32[]{:S(2)}) collective-permute-start(bf16[384,1536]{1,0:T(8,128)(2,1)} %shard_map.251), channel_id=1, source_target_pairs={{1,5},{2,6},{5,1},{6,2},{9,13},{10,14},{13,9},{14,10},{17,21},{18,... | collective-permute-start | bytes 3538952 | tf_op jit(solution)/shard_map/ppermute | solution.py:1085
  420.8 18.3 %collective-permute-start.48 = (bf16[384,1536]{1,0:T(8,128)(2,1)}, bf16[384,1536]{1,0:T(8,128)(2,1)S(1)}, u32[]{:S(2)}, u32[]{:S(2)}) collective-permute-start(bf16[384,1536]{1,0:T(8,128)(2,1)} %shard_map.257), channel_id=1, source_target_pairs={{1,0},{2,3},{5,4},{6,7},{9,8},{10,11},{13,12},{14,15},{17,16},{18,... | collective-permute-start | bytes 3538952 | tf_op jit(solution)/shard_map/ppermute | solution.py:1085
  440.2 32.5 %collective-permute-start.50 = (bf16[1536,384]{1,0:T(8,128)(2,1)}, bf16[1536,384]{1,0:T(8,128)(2,1)S(1)}, u32[]{:S(2)}, u32[]{:S(2)}) collective-permute-start(bf16[1536,384]{1,0:T(8,128)(2,1)} %get-tuple-element.258.own), channel_id=1, source_target_pairs={{1,5},{2,6},{5,1},{6,2},{9,13},{10,14},{13,9},{14,10},{17,21},{18,... | collective-permute-start | bytes 3538952 | tf_op jit(solution)/shard_map/ppermute | solution.py:1085
  443.6 29.1 %collective-permute-start.51 = (bf16[384,1152]{1,0:T(8,128)(2,1)}, bf16[384,1152]{1,0:T(8,128)(2,1)S(1)}, u32[]{:S(2)}, u32[]{:S(2)}) collective-permute-start(bf16[384,1152]{1,0:T(8,128)(2,1)} %shard_map.260), channel_id=1, source_target_pairs={{1,0},{2,3},{5,4},{6,7},{9,8},{10,11},{13,12},{14,15},{17,16},{18,... | collective-permute-start | bytes 2654216 | tf_op jit(solution)/shard_map/ppermute | solution.py:1085
  445.7 25.5 %collective-permute-start.52 = (bf16[384,768]{1,0:T(8,128)(2,1)S(1)}, bf16[384,768]{1,0:T(8,128)(2,1)S(1)}, u32[]{:S(2)}, u32[]{:S(2)}) collective-permute-start(bf16[384,768]{1,0:T(8,128)(2,1)S(1)} %convolution_convert_fusion.6.own), channel_id=1, source_target_pairs={{1,0},{2,3},{5,4},{6,7},{9,8},{10,11},{13,12},{14,15},{17,16},{18,... | collective-permute-start | bytes 1769480 | tf_op jit(solution)/shard_map/ppermute | solution.py:1085
  477.6 18.3 %collective-permute-start.54 = (bf16[1536,384]{1,0:T(8,128)(2,1)}, bf16[1536,384]{1,0:T(8,128)(2,1)S(1)}, u32[]{:S(2)}, u32[]{:S(2)}) collective-permute-start(bf16[1536,384]{1,0:T(8,128)(2,1)} %shard_map.266), channel_id=1, source_target_pairs={{1,0},{2,3},{5,4},{6,7},{9,8},{10,11},{13,12},{14,15},{17,16},{18,... | collective-permute-start | bytes 3538952 | tf_op jit(solution)/shard_map/ppermute | solution.py:1085
  502.9 20.6 %collective-permute-start.56 = (bf16[4128,128]{1,0:T(8,128)(2,1)S(1)}, bf16[4128,128]{1,0:T(8,128)(2,1)S(1)}, u32[]{:S(2)}, u32[]{:S(2)}) collective-permute-start(bf16[4128,128]{1,0:T(8,128)(2,1)S(1)} %get-tuple-element.352), channel_id=1, source_target_pairs={{0,8},{3,11},{4,12},{7,15},{8,16},{11,19},{12,20},{15,23},{16,24},... | collective-permute-start | bytes 3170312 | tf_op jit(solution)/shard_map/ppermute | solution.py:1085
  504.9 39.2 %collective-permute-start.61 = (bf16[4128,128]{1,0:T(8,128)(2,1)S(1)}, bf16[4128,128]{1,0:T(8,128)(2,1)S(1)}, u32[]{:S(2)}, u32[]{:S(2)}) collective-permute-start(bf16[4128,128]{1,0:T(8,128)(2,1)S(1)} %get-tuple-element.350), channel_id=1, source_target_pairs={{0,8},{3,11},{4,12},{7,15},{8,16},{11,19},{12,20},{15,23},{16,24},... | collective-permute-start | bytes 3170312 | tf_op jit(solution)/shard_map/ppermute | solution.py:1085
  508.5 28.8 %collective-permute-start.59 = (bf16[4128,128]{1,0:T(8,128)(2,1)S(1)}, bf16[4128,128]{1,0:T(8,128)(2,1)S(1)}, u32[]{:S(2)}, u32[]{:S(2)}) collective-permute-start(bf16[4128,128]{1,0:T(8,128)(2,1)S(1)} %get-tuple-element.351), channel_id=1, source_target_pairs={{0,4},{3,7},{4,0},{7,3},{8,12},{11,15},{12,8},{15,11},{16,20},{19,... | collective-permute-start | bytes 3170312 | tf_op jit(solution)/shard_map/ppermute | solution.py:1085
  528.0 18.3 %collective-permute-start.60 = (bf16[4128,128]{1,0:T(8,128)(2,1)}, bf16[4128,128]{1,0:T(8,128)(2,1)S(1)}, u32[]{:S(2)}, u32[]{:S(2)}) collective-permute-start(bf16[4128,128]{1,0:T(8,128)(2,1)} %shard_map.277), channel_id=1, source_target_pairs={{0,4},{3,7},{4,0},{7,3},{8,12},{11,15},{12,8},{15,11},{16,20},{19,... | collective-permute-start | bytes 3170312 | tf_op jit(solution)/shard_map/ppermute | solution.py:1085
  533.5 44.6 %collective-permute-start.57 = (bf16[1024,768]{1,0:T(8,128)(2,1)S(1)}, bf16[1024,768]{1,0:T(8,128)(2,1)}, u32[]{:S(2)}, u32[]{:S(2)}) collective-permute-start(bf16[1024,768]{1,0:T(8,128)(2,1)S(1)} %add_convert_fusion), channel_id=1, source_target_pairs={{0,2},{1,3},{2,0},{3,1},{4,6},{5,7},{6,4},{7,5},{8,10},{9,11},{10,... | collective-permute-start | bytes 4718600 | tf_op jit(solution)/shard_map/ppermute | solution.py:1085
  533.6 23.0 %collective-permute-start.62 = (bf16[4128,128]{1,0:T(8,128)(2,1)S(1)}, bf16[4128,128]{1,0:T(8,128)(2,1)S(1)}, u32[]{:S(2)}, u32[]{:S(2)}) collective-permute-start(bf16[4128,128]{1,0:T(8,128)(2,1)S(1)} %get-tuple-element.349), channel_id=1, source_target_pairs={{0,4},{3,7},{4,0},{7,3},{8,12},{11,15},{12,8},{15,11},{16,20},{19,... | collective-permute-start | bytes 3170312 | tf_op jit(solution)/shard_map/ppermute | solution.py:1085
  542.1 18.8 %collective-permute-start.63 = (bf16[4128,128]{1,0:T(8,128)(2,1)}, bf16[4128,128]{1,0:T(8,128)(2,1)S(1)}, u32[]{:S(2)}, u32[]{:S(2)}) collective-permute-start(bf16[4128,128]{1,0:T(8,128)(2,1)} %get-tuple-element.302), channel_id=1, source_target_pairs={{0,8},{3,11},{4,12},{7,15},{8,16},{11,19},{12,20},{15,23},{16,24},... | collective-permute-start | bytes 3170312 | tf_op jit(solution)/shard_map/ppermute | solution.py:1085
  544.1 23.5 %collective-permute-start.64 = (bf16[4128,128]{1,0:T(8,128)(2,1)S(1)}, bf16[4128,128]{1,0:T(8,128)(2,1)S(1)}, u32[]{:S(2)}, u32[]{:S(2)}) collective-permute-start(bf16[4128,128]{1,0:T(8,128)(2,1)S(1)} %get-tuple-element.348), channel_id=1, source_target_pairs={{0,4},{3,7},{4,0},{7,3},{8,12},{11,15},{12,8},{15,11},{16,20},{19,... | collective-permute-start | bytes 3170312 | tf_op jit(solution)/shard_map/ppermute | solution.py:1085
  551.5 20.7 %collective-permute-start.65 = (bf16[4128,128]{1,0:T(8,128)(2,1)}, bf16[4128,128]{1,0:T(8,128)(2,1)S(1)}, u32[]{:S(2)}, u32[]{:S(2)}) collective-permute-start(bf16[4128,128]{1,0:T(8,128)(2,1)} %get-tuple-element.306), channel_id=1, source_target_pairs={{0,8},{3,11},{4,12},{7,15},{8,16},{11,19},{12,20},{15,23},{16,24},... | collective-permute-start | bytes 3170312 | tf_op jit(solution)/shard_map/ppermute | solution.py:1085
  556.7 47.3 %collective-permute-start.55 = (bf16[1024,768]{1,0:T(8,128)(2,1)S(1)}, bf16[1024,768]{1,0:T(8,128)(2,1)}, u32[]{:S(2)}, u32[]{:S(2)}) collective-permute-start(bf16[1024,768]{1,0:T(8,128)(2,1)S(1)} %copy-done.40), channel_id=1, source_target_pairs={{0,1},{3,2},{4,5},{7,6},{8,9},{11,10},{12,13},{15,14},{16,17},{19,... | collective-permute-start | bytes 4718600 | tf_op jit(solution)/shard_map/ppermute | solution.py:1085
  560.9 22.8 %collective-permute-start.66 = (bf16[4128,128]{1,0:T(8,128)(2,1)}, bf16[4128,128]{1,0:T(8,128)(2,1)}, u32[]{:S(2)}, u32[]{:S(2)}) collective-permute-start(bf16[4128,128]{1,0:T(8,128)(2,1)} %get-tuple-element.308), channel_id=1, source_target_pairs={{0,4},{3,7},{4,0},{7,3},{8,12},{11,15},{12,8},{15,11},{16,20},{19,... | collective-permute-start | bytes 3170312 | tf_op jit(solution)/shard_map/ppermute | solution.py:1085
  567.6 18.9 %collective-permute-start.67 = (bf16[4128,128]{1,0:T(8,128)(2,1)}, bf16[4128,128]{1,0:T(8,128)(2,1)}, u32[]{:S(2)}, u32[]{:S(2)}) collective-permute-start(bf16[4128,128]{1,0:T(8,128)(2,1)} %get-tuple-element.311), channel_id=1, source_target_pairs={{0,8},{3,11},{4,12},{7,15},{8,16},{11,19},{12,20},{15,23},{16,24},... | collective-permute-start | bytes 3170312 | tf_op jit(solution)/shard_map/ppermute | solution.py:1085
  572.2 21.3 %collective-permute-start.68 = (bf16[4128,128]{1,0:T(8,128)(2,1)}, bf16[4128,128]{1,0:T(8,128)(2,1)}, u32[]{:S(2)}, u32[]{:S(2)}) collective-permute-start(bf16[4128,128]{1,0:T(8,128)(2,1)} %get-tuple-element.313), channel_id=1, source_target_pairs={{0,4},{3,7},{4,0},{7,3},{8,12},{11,15},{12,8},{15,11},{16,20},{19,... | collective-permute-start | bytes 3170312 | tf_op jit(solution)/shard_map/ppermute | solution.py:1085
  578.2 19.6 %collective-permute-start.69 = (bf16[4128,128]{1,0:T(8,128)(2,1)}, bf16[4128,128]{1,0:T(8,128)(2,1)}, u32[]{:S(2)}, u32[]{:S(2)}) collective-permute-start(bf16[4128,128]{1,0:T(8,128)(2,1)} %shard_map.285), channel_id=1, source_target_pairs={{0,8},{3,11},{4,12},{7,15},{8,16},{11,19},{12,20},{15,23},{16,24},... | collective-permute-start | bytes 3170312 | tf_op jit(solution)/shard_map/ppermute | solution.py:1085
  583.7 22.1 %collective-permute-start.58 = (bf16[1024,384]{1,0:T(8,128)(2,1)}, bf16[1024,384]{1,0:T(8,128)(2,1)}, u32[]{:S(2)}, u32[]{:S(2)}) collective-permute-start(bf16[1024,384]{1,0:T(8,128)(2,1)} %select_convert_fusion), channel_id=1, source_target_pairs={{0,1},{3,2},{4,5},{7,6},{8,9},{11,10},{12,13},{15,14},{16,17},{19,... | collective-permute-start | bytes 2359304 | tf_op jit(solution)/shard_map/ppermute | solution.py:1085
  586.5 22.6 %collective-permute-start.70 = (bf16[4128,128]{1,0:T(8,128)(2,1)}, bf16[4128,128]{1,0:T(8,128)(2,1)}, u32[]{:S(2)}, u32[]{:S(2)}) collective-permute-start(bf16[4128,128]{1,0:T(8,128)(2,1)} %get-tuple-element.317), channel_id=1, source_target_pairs={{0,4},{3,7},{4,0},{7,3},{8,12},{11,15},{12,8},{15,11},{16,20},{19,... | collective-permute-start | bytes 3170312 | tf_op jit(solution)/shard_map/ppermute | solution.py:1085
  593.5 18.9 %collective-permute-start.71 = (bf16[4128,128]{1,0:T(8,128)(2,1)}, bf16[4128,128]{1,0:T(8,128)(2,1)}, u32[]{:S(2)}, u32[]{:S(2)}) collective-permute-start(bf16[4128,128]{1,0:T(8,128)(2,1)} %shard_map.287), channel_id=1, source_target_pairs={{0,8},{3,11},{4,12},{7,15},{8,16},{11,19},{12,20},{15,23},{16,24},... | collective-permute-start | bytes 3170312 | tf_op jit(solution)/shard_map/ppermute | solution.py:1085
  601.5 16.3 %collective-permute-start.72 = (bf16[4128,128]{1,0:T(8,128)(2,1)}, bf16[4128,128]{1,0:T(8,128)(2,1)}, u32[]{:S(2)}, u32[]{:S(2)}) collective-permute-start(bf16[4128,128]{1,0:T(8,128)(2,1)} %shard_map.290), channel_id=1, source_target_pairs={{0,2},{3,1},{4,6},{7,5},{8,10},{11,9},{12,14},{15,13},{16,18},{19,... | collective-permute-start | bytes 3170312 | tf_op jit(solution)/shard_map/ppermute | solution.py:1085
  (137 other events, 790.3 us)

commit v17 on v15

--- a/solution.py
+++ b/solution.py
@@ -1023,39 +1023,42 @@
 
 
 def reduce_kernel(carrying, last, *refs):
-    block, arrived, *refs = refs
+    token, block, arrived, *refs = refs
     total = block[...].astype(f32) + arrived[...].astype(f32)
     if carrying:
         carried, *refs = refs
         total = total + carried[...].astype(f32)
     if last:
-        [out] = refs
+        token_out, out = refs
     else:
-        following, out, later = refs
+        following, token_out, out, later = refs
         later[...] = following[...]
     out[...] = total.astype(bf16)
-
-
-def reduce_call(j, n, buffer, arrived, carried, payload, x_rel=0):
+    token_out[...] = token[...]
+
+
+def reduce_call(j, n, token, buffer, arrived, carried, payload, x_rel=0):
     last = j >= 2 or x_rel == 1
     at = lambda j, x_rel: pl.BlockSpec((payload, BS), lambda i: ((j * 2 + x_rel) * 2 + n, 0))
     whole = fixed((payload, BS))
-    operands = [stay(buffer), stay(arrived)] + ([] if carried is None else [stay(carried)])
-    specs = [at(j, x_rel)] + [whole] * (len(operands) - 1)
+    small = fixed(token.shape)
+    operands = [token, stay(buffer), arrived] + ([] if carried is None else [carried])
+    specs = [small, at(j, x_rel)] + [whole] * (len(operands) - 2)
     if not last:
         operands.append(stay(buffer))
         specs.append(at(j + 2, 1))
-    outs = [pltpu.HBM((payload, BS), bf16)] * (1 if last else 2)
+    block = jax.ShapeDtypeStruct((payload, BS), bf16)
+    outs = [jax.ShapeDtypeStruct(token.shape, f32)] + [block] * (1 if last else 2)
     made = pl.pallas_call(
         functools.partial(reduce_kernel, carried is not None, last),
         out_shape=outs,
         grid=(1,),
         in_specs=specs,
-        out_specs=[whole] * len(outs),
-        compiler_params=params(8),
+        out_specs=[small] + [whole] * (len(outs) - 1),
+        compiler_params=params(12),
         cost_estimate=cost(payload * BS * 3, payload * BS * 12),
     )(*operands)
-    return (made[0], None) if last else made
+    return (*made, None) if last else made
 
 
 class Routes:
@@ -1346,7 +1349,7 @@
     buffer = place_tiles(("out", top), go1, ao1, buffer)
     buffer = place_tiles(("qkv", top), gq1, aq1, buffer)
     buffer = place_tiles(("down", low), gd0, ad0, buffer)
-    gbm, xb, aq0, av, buffer = hold(gbm, xb, aq0, av, buffer)
+    gbm, xb, aq0, ao0, av, buffer = hold(gbm, xb, aq0, ao0, av, buffer)
     ab = over(half_sum(half_at * 0, gbm, xb)) if grid3 else None
     buffer = place_tiles(("up", low), gu0, au0, buffer)
     buffer = place_base(1, gbt, None, buffer)
@@ -1369,21 +1372,19 @@
         far_side = send(blocks[0, 1, order[0]], routes.z_home)
         carried[order[0]] = send(blocks[0, 0, order[0]], routes.z_home)
         rounded = {}
+        token, resized = hold(token, resized)
         for j in range(4):
             for n in order:
-                extra = None
                 if j == 0 and n == order[0]:
-                    token, far_side, resized = hold(token, far_side, resized)
-                    later, unused = reduce_call(1, n, buffer, far_side, None, payload, 1)
+                    token, later, unused = reduce_call(1, n, token, buffer, far_side, None, payload, 1)
                     across[n] = send(later, routes.x_home)
                     continue
-                token, across[n], carried[n], extra = hold(token, across[n], carried[n], extra)
-                if extra is not None:
-                    resized = extra
                 arrived = across[n]
                 if j < 3:
                     across[n] = send(following[n], routes.x_home)
-                total, following[n] = reduce_call(j, n, buffer, arrived, carried[n], payload)
+                token, total, following[n] = reduce_call(
+                    j, n, token, buffer, arrived, carried[n], payload
+                )
                 if j < 3:
                     carried[n] = send(total, routes.z_home)
                 else:

time: 637 us -> 638 us (level)
  Pallas kernels: 289 us -> 275 us
  waiting for transfers between devices: 125 us -> 135 us
    ppermute x73, waiting for transfers between devices: 125 us -> 135 us  [send(): return lax.ppermute(value, AXES, route)]
    unnamed x226 -> x222, local copies, waits for them, and re-layouts: 27.9 us -> 26.6 us
  transfers between devices with their start and end apart: 73 -> 73, of which waited for: 34 -> 38; matrix products, arithmetic and copies ran while one was open for 10% -> 11% of each run, Pallas kernels for 32% -> 30%
where the time goes in v17:
time: 638 us; the launch traced here: 627 us
  Pallas kernels  275 us (43%)
  waiting for transfers between devices  135 us (21%)
  starting transfers between devices  111 us (17%)
  local copies, waits for them, and re-layouts  41.5 us (7%)
  matrix products  31.8 us (5%)
  other arithmetic  30.4 us (5%)
    ppermute x73, waiting for transfers between devices, send(): return lax.ppermute(value, AXES, route)  135 us
    ppermute x73, starting transfers between devices, send(): return lax.ppermute(value, AXES, route)  111 us
    pallas_call x2, Pallas kernels, attend_back_call(): pl.pallas_call(attend_back_kernel, out_shape=[shape(D, f32), shape(D, bf1...  40.9 us
    pallas_call x10, Pallas kernels, scatter_matrix(): pl.pallas_call(functools.partial(scatter_kernel, rows_n, cols_n, steps, p...  35.1 us
    dot_general x12, matrix products, dot_tn(): lax.dot_general(left, right, (((0,), (0,)), ((), ())), preferred_element_...  27.7 us
    unnamed x222, local copies, waits for them, and re-layouts  26.6 us
    pallas_call x2, Pallas kernels, attend_call(): pl.pallas_call(functools.partial(attend_kernel, layer), out_shape=[jax.Sh...  26.5 us
    pallas_call x4, Pallas kernels, expand_call(): pl.pallas_call(expand_kernel, out_shape=jax.ShapeDtypeStruct((tokens, siz...  24.7 us
  transfers between devices with their start and end apart: 73, of which 38 were waited for; matrix products, arithmetic and copies ran while one was open for 11% of the time, Pallas kernels for 30%

profile of v17, /device:TPU:0, one launch (start us, length us, event | category | flops | bytes accessed | tf_op | source)
XLA Modules:
  0.0 626.8 jit_solution(18186995765967140890)
XLA Ops:
  18.9 6.0 shard_map.222.refs_3_
  26.1 6.1 collective-permute-done.5.refs_5_
  43.7 6.5 %shard_map.224.refs_3_ = bf16[1024,768]{1,0:T(8,128)(2,1)S(1)} custom-call(s32[4,3]{1,0:T(4,128)S(1)} %convert_element_type.120.present, s32[1]{0:T(128)} %bitcast.6.half.part, bf16[1024,768]{1,0:T(8,128)(2,1)} %get-tuple-element.163.patch_ref.refs_2_, s32[1024,1]{1,0:T(8,128)S(1)} %copy.120.class_ref, bf16[3,3072,768]{2,1,0:T(8,128)(2,1)} %pinv_ref.9), custom_call_target="tpu_custom_call" | custom-call | flops 1811939328 | bytes 6684672 | tf_op jit(solution)/shard_map/pallas_call | solution.py:439
  54.7 12.5 %collective-permute-done.9.refs_4_ = bf16[4112,128]{1,0:T(8,128)(2,1)S(1)} collective-permute-done((bf16[4112,128]{1,0:T(8,128)(2,1)}, bf16[4112,128]{1,0:T(8,128)(2,1)S(1)}, u32[]{:S(2)}, u32[]{:S(2)}) %collective-permute-start.9) | collective-permute-done | bytes 1052704 | tf_op jit(solution)/shard_map/ppermute | solution.py:1084
  67.2 5.7 collective-permute-done.8.refs_1_
  80.8 6.0 shard_map.226.refs_3_
  93.6 12.3 %collective-permute-done.12.refs_4_ = bf16[4112,128]{1,0:T(8,128)(2,1)S(1)} collective-permute-done((bf16[4112,128]{1,0:T(8,128)(2,1)S(1)}, bf16[4112,128]{1,0:T(8,128)(2,1)S(1)}, u32[]{:S(2)}, u32[]{:S(2)}) %collective-permute-start.12) | collective-permute-done | bytes 1052704 | tf_op jit(solution)/shard_map/ppermute | solution.py:1084
  105.9 6.0 collective-permute-done.11.refs_1_
  119.8 6.2 shard_map.228.refs_3_
  132.4 16.7 %collective-permute-done.14.refs_1_ = bf16[4112,128]{1,0:T(8,128)(2,1)S(1)} collective-permute-done((bf16[4112,128]{1,0:T(8,128)(2,1)S(1)}, bf16[4112,128]{1,0:T(8,128)(2,1)S(1)}, u32[]{:S(2)}, u32[]{:S(2)}) %collective-permute-start.14) | collective-permute-done | bytes 1052704 | tf_op jit(solution)/shard_map/ppermute | solution.py:1084
  156.9 5.7 collective-permute-done.28
  172.1 14.2 %shard_map.230 = (bf16[3072,384]{1,0:T(8,128)(2,1)}, bf16[2304,384]{1,0:T(8,128)(2,1)}, bf16[768,384]{1,0:T(8,128)(2,1)}, bf16[3072,384]{1,0:T(8,128)(2,1)}, bf1...) custom-call(s32[16]{0:T(128)S(1)} %stack.95.owner, ...), custom_call_target="tpu_custom_call" | custom-call | bytes 33030144 | tf_op jit(solution)/shard_map/pallas_call | solution.py:243
  186.5 6.8 %shard_map.231.refs_0_ = bf16[1024,384]{1,0:T(8,128)(2,1)S(1)} custom-call(s32[1]{0:T(128)} %bitcast.6.half.part, bf16[1024,768]{1,0:T(8,128)(2,1)} %get-tuple-element.161.refs_0_, bf16[1024,768]{1,0:T(8,128)(2,1)} %get-tuple-element.164.refs_1_, bf16[1024,768]{1,0:T(8,128)(2,1)} %get-tuple-element.167.refs_2_, ...), custom_call_target="tpu_custom_call" | custom-call | flops 2415919104 | bytes 9437184 | tf_op jit(solution)/shard_map/pallas_call | solution.py:552
  195.8 4.8 shard_map.232
  200.7 13.2 %shard_map.233 = (bf16[1024,384]{1,0:T(8,128)(2,1)S(1)}, f32[8,1024]{1,0:T(8,128)S(1)}, bf16[1024,768]{1,0:T(8,128)(2,1)S(1)}) custom-call(s32[4]{0:T(128)S(1)} %get-tuple-element.356.low_ref, s32[4]{0:T(128)S(1)} %get-tuple-element.349.high_ref, bf16[1024,384]{1,0:T(8,128)(2,1)S(1)} %get-tuple-element.184.q_ref, ...), custom_call_target="tpu_custom_call" | custom-call | flops 6442450944 | bytes 6291456 | tf_op jit(solution)/shard_map/pallas_call | solution.py:679
  218.4 9.4 %shard_map.234 = (f32[1024,768]{1,0:T(8,128)S(1)}, bf16[1024,768]{1,0:T(8,128)(2,1)}, bf16[1024,1536]{1,0:T(8,128)(2,1)}, bf16[1024,1536]{1,0:T(8,128)(2,1)}, bf16[1024,768]{1,0:T(8,128)(2,1)S(1)}) custom-call(f32[1024,768]{1,0:T(8,128)S(1)} %get-tuple-element.183.base.hid, bf16[1024,768]{1,0:T(8,128)(2,1)S(1)} %get-tuple-element.188.own, ...), custom_call_target="tpu_custom_call" | custom-call | flops 4831838208 | bytes 18874368 | tf_op jit(solution)/shard_map/pallas_call | solution.py:742
  231.1 4.4 shard_map.235
  235.6 13.2 %shard_map.236 = (bf16[1024,384]{1,0:T(8,128)(2,1)S(1)}, f32[8,1024]{1,0:T(8,128)S(1)}, bf16[1024,768]{1,0:T(8,128)(2,1)S(1)}) custom-call(s32[4]{0:T(128)S(1)} %get-tuple-element.356.low_ref, s32[4]{0:T(128)S(1)} %get-tuple-element.349.high_ref, bf16[1024,384]{1,0:T(8,128)(2,1)S(1)} %get-tuple-element.195.q_ref, ...), custom_call_target="tpu_custom_call" | custom-call | flops 6442450944 | bytes 6291456 | tf_op jit(solution)/shard_map/pallas_call | solution.py:679
  252.4 9.4 %shard_map.237 = (f32[1024,768]{1,0:T(8,128)S(1)}, bf16[1024,768]{1,0:T(8,128)(2,1)}, bf16[1024,1536]{1,0:T(8,128)(2,1)}, bf16[1024,1536]{1,0:T(8,128)(2,1)}, bf16[1024,768]{1,0:T(8,128)(2,1)S(1)}) custom-call(f32[1024,768]{1,0:T(8,128)S(1)} %get-tuple-element.194.base.hid, bf16[1024,768]{1,0:T(8,128)(2,1)S(1)} %get-tuple-element.199.own, ...), custom_call_target="tpu_custom_call" | custom-call | flops 4831838208 | bytes 18874368 | tf_op jit(solution)/shard_map/pallas_call | solution.py:742
  263.7 11.3 %shard_map.238 = (bf16[1024,768]{1,0:T(8,128)(2,1)S(1)}, bf16[1024,1536]{1,0:T(8,128)(2,1)S(1)}, bf16[1024,768]{1,0:T(8,128)(2,1)S(1)}, f32[1,768]{1,0:T(1,128)S...) custom-call(bf16[1024,768]{1,0:T(8,128)(2,1)S(1)} %broadcast_select_fusion.refs_0_, ...), custom_call_target="tpu_custom_call" | custom-call | flops 4831838208 | bytes 18874368 | tf_op jit(solution)/shard_map/pallas_call | solution.py:794
  279.6 4.1 convolution_convert_fusion.3.refs_1_
  289.1 20.4 %shard_map.240 = (f32[1024,768]{1,0:T(8,128)S(1)}, bf16[1024,768]{1,0:T(8,128)(2,1)S(1)}, bf16[1024,384]{1,0:T(8,128)(2,1)S(1)}, bf16[1024,384]{1,0:T(8,128)(2,1...) custom-call(s32[4]{0:T(128)S(1)} %get-tuple-element.355.low_ref, s32[4]{0:T(128)S(1)} %get-tuple-element.350.high_ref, ...), custom_call_target="tpu_custom_call" | custom-call | flops 11274289152 | bytes 15728640 | tf_op jit(solution)/shard_map/pallas_call | solution.py:886
  312.2 5.5 shard_map.243
  317.7 5.7 collective-permute-start.39
  336.4 11.2 %shard_map.244 = (f32[1024,768]{1,0:T(8,128)S(1)}, bf16[1024,768]{1,0:T(8,128)(2,1)S(1)}, bf16[1024,1536]{1,0:T(8,128)(2,1)S(1)}, bf16[1024,768]{1,0:T(8,128)(2,...) custom-call(f32[1024,768]{1,0:T(8,128)S(1)} %get-tuple-element.211.refs_0_, ...), custom_call_target="tpu_custom_call" | custom-call | flops 4831838208 | bytes 18874368 | tf_op jit(solution)/shard_map/pallas_call | solution.py:794
  353.1 3.9 collective-permute-start.40
  357.0 4.0 convolution_convert_fusion.1.refs_1_
  361.0 4.0 convolution_convert_fusion.refs_2_
  365.0 4.8 collective-permute-done.44.refs_4_
  375.4 4.3 shard_map.252.refs_1_
  379.7 4.0 shard_map.253.refs_4_
  383.7 20.4 %shard_map.250 = (f32[1024,768]{1,0:T(8,128)S(1)}, bf16[1024,768]{1,0:T(8,128)(2,1)S(1)}, bf16[1024,384]{1,0:T(8,128)(2,1)S(1)}, bf16[1024,384]{1,0:T(8,128)(2,1...) custom-call(s32[4]{0:T(128)S(1)} %get-tuple-element.355.low_ref, s32[4]{0:T(128)S(1)} %get-tuple-element.350.high_ref, ...), custom_call_target="tpu_custom_call" | custom-call | flops 11274289152 | bytes 15728640 | tf_op jit(solution)/shard_map/pallas_call | solution.py:886
  405.9 5.6 shard_map.255
  427.7 6.5 %collective-permute-done.48.refs_1_ = bf16[384,1536]{1,0:T(8,128)(2,1)S(1)} collective-permute-done((bf16[384,1536]{1,0:T(8,128)(2,1)}, bf16[384,1536]{1,0:T(8,128)(2,1)S(1)}, u32[]{:S(2)}, u32[]{:S(2)}) %collective-permute-start.48) | collective-permute-done | bytes 1179680 | tf_op jit(solution)/shard_map/ppermute | solution.py:1084
  444.9 3.6 shard_map.263.refs_1_
  448.5 4.2 shard_map.264.refs_5_
  457.3 8.8 %collective-permute-done.52.refs_3_ = bf16[384,768]{1,0:T(8,128)(2,1)S(1)} collective-permute-done((bf16[384,768]{1,0:T(8,128)(2,1)S(1)}, bf16[384,768]{1,0:T(8,128)(2,1)S(1)}, u32[]{:S(2)}, u32[]{:S(2)}) %collective-permute-start.52) | collective-permute-done | bytes 589856 | tf_op jit(solution)/shard_map/ppermute | solution.py:1084
  473.0 4.0 shard_map.267.refs_0_
  481.1 3.6 shard_map.270.refs_1_
  496.9 5.3 collective-permute-start.58
  502.3 10.2 %shard_map.273.refs_1_ = bf16[3,384,768]{2,1,0:T(8,128)(2,1)S(1)} custom-call(bf16[3072,384]{1,0:T(8,128)(2,1)} %get-tuple-element.285.base, bf16[3,3072,768]{2,1,0:T(8,128)(2,1)} %pinv_ref.9), custom_call_target="tpu_custom_call" | custom-call | flops 5435817984 | bytes 14155776 | tf_op jit(solution)/shard_map/pallas_call | solution.py:470
  513.7 3.8 collective-permute-start.61
  523.7 3.6 collective-permute-start.60
  536.8 3.8 collective-permute-start.63
  548.4 3.8 collective-permute-start.65
  552.3 4.5 collective-permute-done.62.refs_2_
  568.1 3.8 collective-permute-start.67
  617.7 8.7 %shard_map.284 = (f32[32,128,128]{2,1,0:T(8,128)}, f32[32,128,128]{2,1,0:T(8,128)}, f32[32,128,128]{2,1,0:T(8,128)}, f32[32,128,128]{2,1,0:T(8,128)}) custom-call(s32[32]{0:T(128)S(1)} %convert_element_type.148.used, s32[1]{0:T(128)} %bitcast.27.flag.home, bf16[4112,128]{1,0:T(8,128)(2,1)} %copy-done.24, bf16[4112,128]{1,0:T(8,128)(2,1)} %collective-permute-done.72.far, ...), custom_call_target="tpu_custom_call" | custom-call | flops 5905580032 | bytes 19922944 | tf_op jit(solution)/shard_map/pallas_call | solution.py:1011
  (483 shorter events, 271.1 us)
Async XLA Ops:
  4.2 28.6 %collective-permute-start.4 = (bf16[4112,128]{1,0:T(8,128)(2,1)}, bf16[4112,128]{1,0:T(8,128)(2,1)}, u32[]{:S(2)}, u32[]{:S(2)}) collective-permute-start(bf16[4112,128]{1,0:T(8,128)(2,1)} %pad_maximum_fusion.2), channel_id=1, source_target_pairs={{0,8},{1,9},{2,10},{3,11},{4,12},{5,13},{6,14},{7,15},{8,16},{9,17... | collective-permute-start | bytes 3158024 | tf_op jit(solution)/shard_map/ppermute | solution.py:1084
  7.2 25.6 %collective-permute-start.1 = (bf16[4112,128]{1,0:T(8,128)(2,1)}, bf16[4112,128]{1,0:T(8,128)(2,1)S(1)}, u32[]{:S(2)}, u32[]{:S(2)}) collective-permute-start(bf16[4112,128]{1,0:T(8,128)(2,1)} %pad_maximum_fusion.2), channel_id=1, source_target_pairs={{0,1},{1,0},{2,3},{3,2},{4,5},{5,4},{6,7},{7,6},{8,9},{9,8},{10,11... | collective-permute-start | bytes 3158024 | tf_op jit(solution)/shard_map/ppermute | solution.py:1084
  8.7 24.6 %collective-permute-start = (bf16[4112,128]{1,0:T(8,128)(2,1)}, bf16[4112,128]{1,0:T(8,128)(2,1)S(1)}, u32[]{:S(2)}, u32[]{:S(2)}) collective-permute-start(bf16[4112,128]{1,0:T(8,128)(2,1)} %pad_maximum_fusion.2), channel_id=1, source_target_pairs={{0,4},{1,5},{2,6},{3,7},{4,0},{5,1},{6,2},{7,3},{8,12},{9,13},{10,... | collective-permute-start | bytes 3158024 | tf_op jit(solution)/shard_map/ppermute | solution.py:1084
  14.0 18.2 %collective-permute-start.5 = (s32[1,504]{1,0:T(1,128)S(1)}, s32[1,504]{1,0:T(1,128)S(1)}, u32[]{:S(2)}, u32[]{:S(2)}) collective-permute-start(s32[1,504]{1,0:T(1,128)S(1)} %copy-done.95), channel_id=1, source_target_pairs={{0,1},{1,0},{2,3},{3,2},{4,5},{5,4},{6,7},{7,6},{8,9},{9,8},{10,11... | collective-permute-start | bytes 6056 | tf_op jit(solution)/shard_map/ppermute | solution.py:1084
  41.5 25.6 %collective-permute-start.9 = (bf16[4112,128]{1,0:T(8,128)(2,1)}, bf16[4112,128]{1,0:T(8,128)(2,1)S(1)}, u32[]{:S(2)}, u32[]{:S(2)}) collective-permute-start(bf16[4112,128]{1,0:T(8,128)(2,1)} %get-tuple-element.162), channel_id=1, source_target_pairs={{0,8},{1,9},{2,10},{3,11},{4,12},{5,13},{6,14},{7,15},{8,16},{9,17... | collective-permute-start | bytes 3158024 | tf_op jit(solution)/shard_map/ppermute | solution.py:1084
  42.5 30.3 %collective-permute-start.8 = (bf16[4112,128]{1,0:T(8,128)(2,1)}, bf16[4112,128]{1,0:T(8,128)(2,1)S(1)}, u32[]{:S(2)}, u32[]{:S(2)}) collective-permute-start(bf16[4112,128]{1,0:T(8,128)(2,1)} %get-tuple-element.162), channel_id=1, source_target_pairs={{0,1},{1,0},{2,3},{3,2},{4,5},{5,4},{6,7},{7,6},{8,9},{9,8},{10,11... | collective-permute-start | bytes 3158024 | tf_op jit(solution)/shard_map/ppermute | solution.py:1084
  43.2 30.7 %collective-permute-start.7 = (bf16[4112,128]{1,0:T(8,128)(2,1)}, bf16[4112,128]{1,0:T(8,128)(2,1)S(1)}, u32[]{:S(2)}, u32[]{:S(2)}) collective-permute-start(bf16[4112,128]{1,0:T(8,128)(2,1)} %get-tuple-element.162), channel_id=1, source_target_pairs={{0,4},{1,5},{2,6},{3,7},{4,0},{5,1},{6,2},{7,3},{8,12},{9,13},{10,... | collective-permute-start | bytes 3158024 | tf_op jit(solution)/shard_map/ppermute | solution.py:1084
  52.0 113.0 %collective-permute-start.15 = (bf16[4112,128]{1,0:T(8,128)(2,1)S(1)}, bf16[4112,128]{1,0:T(8,128)(2,1)S(1)}, u32[]{:S(2)}, u32[]{:S(2)}) collective-permute-start(bf16[4112,128]{1,0:T(8,128)(2,1)S(1)} %get-tuple-element.337), channel_id=1, source_target_pairs={{0,2},{1,3},{2,0},{3,1},{4,6},{5,7},{6,4},{7,5},{8,10},{9,11},{10,... | collective-permute-start | bytes 3158024 | tf_op jit(solution)/shard_map/ppermute | solution.py:1084
  54.7 111.8 %collective-permute-start.18 = (bf16[4112,128]{1,0:T(8,128)(2,1)S(1)}, bf16[4112,128]{1,0:T(8,128)(2,1)}, u32[]{:S(2)}, u32[]{:S(2)}) collective-permute-start(bf16[4112,128]{1,0:T(8,128)(2,1)S(1)} %broadcast_select_fusion.8), channel_id=1, source_target_pairs={{0,2},{1,3},{2,0},{3,1},{4,6},{5,7},{6,4},{7,5},{8,10},{9,11},{10,... | collective-permute-start | bytes 3158024 | tf_op jit(solution)/shard_map/ppermute | solution.py:1084
  80.1 25.8 %collective-permute-start.12 = (bf16[4112,128]{1,0:T(8,128)(2,1)S(1)}, bf16[4112,128]{1,0:T(8,128)(2,1)S(1)}, u32[]{:S(2)}, u32[]{:S(2)}) collective-permute-start(bf16[4112,128]{1,0:T(8,128)(2,1)S(1)} %copy-done.60), channel_id=1, source_target_pairs={{0,8},{1,9},{2,10},{3,11},{4,12},{5,13},{6,14},{7,15},{8,16},{9,17... | collective-permute-start | bytes 3158024 | tf_op jit(solution)/shard_map/ppermute | solution.py:1084
  89.4 22.6 %collective-permute-start.11 = (bf16[4112,128]{1,0:T(8,128)(2,1)S(1)}, bf16[4112,128]{1,0:T(8,128)(2,1)S(1)}, u32[]{:S(2)}, u32[]{:S(2)}) collective-permute-start(bf16[4112,128]{1,0:T(8,128)(2,1)S(1)} %copy-done.60), channel_id=1, source_target_pairs={{0,1},{1,0},{2,3},{3,2},{4,5},{5,4},{6,7},{7,6},{8,9},{9,8},{10,11... | collective-permute-start | bytes 3158024 | tf_op jit(solution)/shard_map/ppermute | solution.py:1084
  90.6 22.2 %collective-permute-start.10 = (bf16[4112,128]{1,0:T(8,128)(2,1)S(1)}, bf16[4112,128]{1,0:T(8,128)(2,1)S(1)}, u32[]{:S(2)}, u32[]{:S(2)}) collective-permute-start(bf16[4112,128]{1,0:T(8,128)(2,1)S(1)} %copy-done.60), channel_id=1, source_target_pairs={{0,4},{1,5},{2,6},{3,7},{4,0},{5,1},{6,2},{7,3},{8,12},{9,13},{10,... | collective-permute-start | bytes 3158024 | tf_op jit(solution)/shard_map/ppermute | solution.py:1084
  105.9 60.6 %collective-permute-start.19 = (bf16[4112,128]{1,0:T(8,128)(2,1)S(1)}, bf16[4112,128]{1,0:T(8,128)(2,1)}, u32[]{:S(2)}, u32[]{:S(2)}) collective-permute-start(bf16[4112,128]{1,0:T(8,128)(2,1)S(1)} %broadcast_select_fusion.7), channel_id=1, source_target_pairs={{0,2},{1,3},{2,0},{3,1},{4,6},{5,7},{6,4},{7,5},{8,10},{9,11},{10,... | collective-permute-start | bytes 3158024 | tf_op jit(solution)/shard_map/ppermute | solution.py:1084
  128.3 20.8 %collective-permute-start.14 = (bf16[4112,128]{1,0:T(8,128)(2,1)S(1)}, bf16[4112,128]{1,0:T(8,128)(2,1)S(1)}, u32[]{:S(2)}, u32[]{:S(2)}) collective-permute-start(bf16[4112,128]{1,0:T(8,128)(2,1)S(1)} %copy-done.62), channel_id=1, source_target_pairs={{0,1},{1,0},{2,3},{3,2},{4,5},{5,4},{6,7},{7,6},{8,9},{9,8},{10,11... | collective-permute-start | bytes 3158024 | tf_op jit(solution)/shard_map/ppermute | solution.py:1084
  129.2 20.5 %collective-permute-start.13 = (bf16[4112,128]{1,0:T(8,128)(2,1)S(1)}, bf16[4112,128]{1,0:T(8,128)(2,1)S(1)}, u32[]{:S(2)}, u32[]{:S(2)}) collective-permute-start(bf16[4112,128]{1,0:T(8,128)(2,1)S(1)} %copy-done.62), channel_id=1, source_target_pairs={{0,4},{1,5},{2,6},{3,7},{4,0},{5,1},{6,2},{7,3},{8,12},{9,13},{10,... | collective-permute-start | bytes 3158024 | tf_op jit(solution)/shard_map/ppermute | solution.py:1084
  228.1 21.3 %collective-permute-start.6 = (bf16[1024,768]{1,0:T(8,128)(2,1)S(1)}, bf16[1024,768]{1,0:T(8,128)(2,1)S(1)}, u32[]{:S(2)}, u32[]{:S(2)}) collective-permute-start(bf16[1024,768]{1,0:T(8,128)(2,1)S(1)} %copy-done.92), channel_id=1, source_target_pairs={{0,2},{3,1},{4,6},{7,5},{8,10},{11,9},{12,14},{15,13},{16,18},{19,... | collective-permute-start | bytes 4718600 | tf_op jit(solution)/shard_map/ppermute | solution.py:1084
  263.4 23.9 %collective-permute-start.38 = (bf16[1024,768]{1,0:T(8,128)(2,1)S(1)}, bf16[1024,768]{1,0:T(8,128)(2,1)S(1)}, u32[]{:S(2)}, u32[]{:S(2)}) collective-permute-start(bf16[1024,768]{1,0:T(8,128)(2,1)S(1)} %get-tuple-element.218), channel_id=1, source_target_pairs={{0,2},{1,3},{2,0},{3,1},{4,6},{5,7},{6,4},{7,5},{8,10},{9,11},{10,... | collective-permute-start | bytes 4718600 | tf_op jit(solution)/shard_map/ppermute | solution.py:1084
  278.3 32.5 %collective-permute-start.36 = (bf16[1536,768]{1,0:T(8,128)(2,1)S(1)}, bf16[1536,768]{1,0:T(8,128)(2,1)S(1)}, u32[]{:S(2)}, u32[]{:S(2)}) collective-permute-start(bf16[1536,768]{1,0:T(8,128)(2,1)S(1)} %convolution_convert_fusion.2.own), channel_id=1, source_target_pairs={{1,0},{2,3},{5,4},{6,7},{9,8},{10,11},{13,12},{14,15},{17,16},{18,... | collective-permute-start | bytes 7077896 | tf_op jit(solution)/shard_map/ppermute | solution.py:1084
  286.2 23.4 %collective-permute-start.37 = (bf16[384,1536]{1,0:T(8,128)(2,1)}, bf16[384,1536]{1,0:T(8,128)(2,1)S(1)}, u32[]{:S(2)}, u32[]{:S(2)}) collective-permute-start(bf16[384,1536]{1,0:T(8,128)(2,1)} %shard_map.241), channel_id=1, source_target_pairs={{1,5},{2,6},{5,1},{6,2},{9,13},{10,14},{13,9},{14,10},{17,21},{18,... | collective-permute-start | bytes 3538952 | tf_op jit(solution)/shard_map/ppermute | solution.py:1084
  317.7 18.7 %collective-permute-start.39 = (bf16[1024,768]{1,0:T(8,128)(2,1)S(1)}, bf16[1024,768]{1,0:T(8,128)(2,1)S(1)}, u32[]{:S(2)}, u32[]{:S(2)}) collective-permute-start(bf16[1024,768]{1,0:T(8,128)(2,1)S(1)} %get-tuple-element.220.refs_1_), channel_id=1, source_target_pairs={{0,2},{1,3},{2,0},{3,1},{4,6},{5,7},{6,4},{7,5},{8,10},{9,11},{10,... | collective-permute-start | bytes 4718600 | tf_op jit(solution)/shard_map/ppermute | solution.py:1084
  326.5 21.1 %collective-permute-start.43 = (bf16[384,1536]{1,0:T(8,128)(2,1)}, bf16[384,1536]{1,0:T(8,128)(2,1)S(1)}, u32[]{:S(2)}, u32[]{:S(2)}) collective-permute-start(bf16[384,1536]{1,0:T(8,128)(2,1)} %shard_map.246), channel_id=1, source_target_pairs={{1,0},{2,3},{5,4},{6,7},{9,8},{10,11},{13,12},{14,15},{17,16},{18,... | collective-permute-start | bytes 3538952 | tf_op jit(solution)/shard_map/ppermute | solution.py:1084
  335.1 30.0 %collective-permute-start.41 = (bf16[384,768]{1,0:T(8,128)(2,1)S(1)}, bf16[384,768]{1,0:T(8,128)(2,1)S(1)}, u32[]{:S(2)}, u32[]{:S(2)}) collective-permute-start(bf16[384,768]{1,0:T(8,128)(2,1)S(1)} %convolution_convert_fusion.11.own), channel_id=1, source_target_pairs={{1,0},{2,3},{5,4},{6,7},{9,8},{10,11},{13,12},{14,15},{17,16},{18,... | collective-permute-start | bytes 1769480 | tf_op jit(solution)/shard_map/ppermute | solution.py:1084
  351.6 18.2 %collective-permute-start.44 = (bf16[384,1152]{1,0:T(8,128)(2,1)}, bf16[384,1152]{1,0:T(8,128)(2,1)S(1)}, u32[]{:S(2)}, u32[]{:S(2)}) collective-permute-start(bf16[384,1152]{1,0:T(8,128)(2,1)} %shard_map.248), channel_id=1, source_target_pairs={{1,0},{2,3},{5,4},{6,7},{9,8},{10,11},{13,12},{14,15},{17,16},{18,... | collective-permute-start | bytes 2654216 | tf_op jit(solution)/shard_map/ppermute | solution.py:1084
  353.1 30.6 %collective-permute-start.40 = (bf16[1024,768]{1,0:T(8,128)(2,1)S(1)}, bf16[1024,768]{1,0:T(8,128)(2,1)S(1)}, u32[]{:S(2)}, u32[]{:S(2)}) collective-permute-start(bf16[1024,768]{1,0:T(8,128)(2,1)S(1)} %get-tuple-element.223.own), channel_id=1, source_target_pairs={{0,2},{1,3},{2,0},{3,1},{4,6},{5,7},{6,4},{7,5},{8,10},{9,11},{10,... | collective-permute-start | bytes 4718600 | tf_op jit(solution)/shard_map/ppermute | solution.py:1084
  370.7 33.4 %collective-permute-start.45 = (bf16[1536,768]{1,0:T(8,128)(2,1)}, bf16[1536,768]{1,0:T(8,128)(2,1)S(1)}, u32[]{:S(2)}, u32[]{:S(2)}) collective-permute-start(bf16[1536,768]{1,0:T(8,128)(2,1)} %get-tuple-element.241.own), channel_id=1, source_target_pairs={{1,0},{2,3},{5,4},{6,7},{9,8},{10,11},{13,12},{14,15},{17,16},{18,... | collective-permute-start | bytes 7077896 | tf_op jit(solution)/shard_map/ppermute | solution.py:1084
  374.6 29.5 %collective-permute-start.46 = (bf16[384,1536]{1,0:T(8,128)(2,1)}, bf16[384,1536]{1,0:T(8,128)(2,1)S(1)}, u32[]{:S(2)}, u32[]{:S(2)}) collective-permute-start(bf16[384,1536]{1,0:T(8,128)(2,1)} %shard_map.251), channel_id=1, source_target_pairs={{1,5},{2,6},{5,1},{6,2},{9,13},{10,14},{13,9},{14,10},{17,21},{18,... | collective-permute-start | bytes 3538952 | tf_op jit(solution)/shard_map/ppermute | solution.py:1084
  414.7 19.5 %collective-permute-start.48 = (bf16[384,1536]{1,0:T(8,128)(2,1)}, bf16[384,1536]{1,0:T(8,128)(2,1)S(1)}, u32[]{:S(2)}, u32[]{:S(2)}) collective-permute-start(bf16[384,1536]{1,0:T(8,128)(2,1)} %shard_map.257), channel_id=1, source_target_pairs={{1,0},{2,3},{5,4},{6,7},{9,8},{10,11},{13,12},{14,15},{17,16},{18,... | collective-permute-start | bytes 3538952 | tf_op jit(solution)/shard_map/ppermute | solution.py:1084
  435.2 31.6 %collective-permute-start.50 = (bf16[1536,384]{1,0:T(8,128)(2,1)}, bf16[1536,384]{1,0:T(8,128)(2,1)S(1)}, u32[]{:S(2)}, u32[]{:S(2)}) collective-permute-start(bf16[1536,384]{1,0:T(8,128)(2,1)} %get-tuple-element.250.own), channel_id=1, source_target_pairs={{1,5},{2,6},{5,1},{6,2},{9,13},{10,14},{13,9},{14,10},{17,21},{18,... | collective-permute-start | bytes 3538952 | tf_op jit(solution)/shard_map/ppermute | solution.py:1084
  438.7 28.1 %collective-permute-start.51 = (bf16[384,1152]{1,0:T(8,128)(2,1)}, bf16[384,1152]{1,0:T(8,128)(2,1)S(1)}, u32[]{:S(2)}, u32[]{:S(2)}) collective-permute-start(bf16[384,1152]{1,0:T(8,128)(2,1)} %shard_map.260), channel_id=1, source_target_pairs={{1,0},{2,3},{5,4},{6,7},{9,8},{10,11},{13,12},{14,15},{17,16},{18,... | collective-permute-start | bytes 2654216 | tf_op jit(solution)/shard_map/ppermute | solution.py:1084
  440.8 25.3 %collective-permute-start.52 = (bf16[384,768]{1,0:T(8,128)(2,1)S(1)}, bf16[384,768]{1,0:T(8,128)(2,1)S(1)}, u32[]{:S(2)}, u32[]{:S(2)}) collective-permute-start(bf16[384,768]{1,0:T(8,128)(2,1)S(1)} %convolution_convert_fusion.6.own), channel_id=1, source_target_pairs={{1,0},{2,3},{5,4},{6,7},{9,8},{10,11},{13,12},{14,15},{17,16},{18,... | collective-permute-start | bytes 1769480 | tf_op jit(solution)/shard_map/ppermute | solution.py:1084
  471.6 18.3 %collective-permute-start.54 = (bf16[1536,384]{1,0:T(8,128)(2,1)}, bf16[1536,384]{1,0:T(8,128)(2,1)S(1)}, u32[]{:S(2)}, u32[]{:S(2)}) collective-permute-start(bf16[1536,384]{1,0:T(8,128)(2,1)} %shard_map.266), channel_id=1, source_target_pairs={{1,0},{2,3},{5,4},{6,7},{9,8},{10,11},{13,12},{14,15},{17,16},{18,... | collective-permute-start | bytes 3538952 | tf_op jit(solution)/shard_map/ppermute | solution.py:1084
  496.9 25.2 %collective-permute-start.58 = (bf16[4112,128]{1,0:T(8,128)(2,1)S(1)}, bf16[4112,128]{1,0:T(8,128)(2,1)S(1)}, u32[]{:S(2)}, u32[]{:S(2)}) collective-permute-start(bf16[4112,128]{1,0:T(8,128)(2,1)S(1)} %get-tuple-element.336), channel_id=1, source_target_pairs={{0,8},{3,11},{4,12},{7,15},{8,16},{11,19},{12,20},{15,23},{16,24},... | collective-permute-start | bytes 3158024 | tf_op jit(solution)/shard_map/ppermute | solution.py:1084
  513.7 27.0 %collective-permute-start.61 = (bf16[4112,128]{1,0:T(8,128)(2,1)S(1)}, bf16[4112,128]{1,0:T(8,128)(2,1)S(1)}, u32[]{:S(2)}, u32[]{:S(2)}) collective-permute-start(bf16[4112,128]{1,0:T(8,128)(2,1)S(1)} %get-tuple-element.334), channel_id=1, source_target_pairs={{0,8},{3,11},{4,12},{7,15},{8,16},{11,19},{12,20},{15,23},{16,24},... | collective-permute-start | bytes 3158024 | tf_op jit(solution)/shard_map/ppermute | solution.py:1084
  517.5 16.7 %collective-permute-start.59 = (bf16[4112,128]{1,0:T(8,128)(2,1)S(1)}, bf16[4112,128]{1,0:T(8,128)(2,1)S(1)}, u32[]{:S(2)}, u32[]{:S(2)}) collective-permute-start(bf16[4112,128]{1,0:T(8,128)(2,1)S(1)} %get-tuple-element.335), channel_id=1, source_target_pairs={{0,4},{3,7},{4,0},{7,3},{8,12},{11,15},{12,8},{15,11},{16,20},{19,... | collective-permute-start | bytes 3158024 | tf_op jit(solution)/shard_map/ppermute | solution.py:1084
  523.7 21.8 %collective-permute-start.60 = (bf16[4112,128]{1,0:T(8,128)(2,1)S(1)}, bf16[4112,128]{1,0:T(8,128)(2,1)S(1)}, u32[]{:S(2)}, u32[]{:S(2)}) collective-permute-start(bf16[4112,128]{1,0:T(8,128)(2,1)S(1)} %get-tuple-element.292), channel_id=1, source_target_pairs={{0,4},{3,7},{4,0},{7,3},{8,12},{11,15},{12,8},{15,11},{16,20},{19,... | collective-permute-start | bytes 3158024 | tf_op jit(solution)/shard_map/ppermute | solution.py:1084
  529.5 47.0 %collective-permute-start.56 = (bf16[1024,768]{1,0:T(8,128)(2,1)S(1)}, bf16[1024,768]{1,0:T(8,128)(2,1)S(1)}, u32[]{:S(2)}, u32[]{:S(2)}) collective-permute-start(bf16[1024,768]{1,0:T(8,128)(2,1)S(1)} %add_convert_fusion), channel_id=1, source_target_pairs={{0,2},{1,3},{2,0},{3,1},{4,6},{5,7},{6,4},{7,5},{8,10},{9,11},{10,... | collective-permute-start | bytes 4718600 | tf_op jit(solution)/shard_map/ppermute | solution.py:1084
  529.5 27.3 %collective-permute-start.62 = (bf16[4112,128]{1,0:T(8,128)(2,1)S(1)}, bf16[4112,128]{1,0:T(8,128)(2,1)S(1)}, u32[]{:S(2)}, u32[]{:S(2)}) collective-permute-start(bf16[4112,128]{1,0:T(8,128)(2,1)S(1)} %get-tuple-element.333), channel_id=1, source_target_pairs={{0,4},{3,7},{4,0},{7,3},{8,12},{11,15},{12,8},{15,11},{16,20},{19,... | collective-permute-start | bytes 3158024 | tf_op jit(solution)/shard_map/ppermute | solution.py:1084
  536.8 22.4 %collective-permute-start.63 = (bf16[4112,128]{1,0:T(8,128)(2,1)S(1)}, bf16[4112,128]{1,0:T(8,128)(2,1)S(1)}, u32[]{:S(2)}, u32[]{:S(2)}) collective-permute-start(bf16[4112,128]{1,0:T(8,128)(2,1)S(1)} %get-tuple-element.294), channel_id=1, source_target_pairs={{0,8},{3,11},{4,12},{7,15},{8,16},{11,19},{12,20},{15,23},{16,24},... | collective-permute-start | bytes 3158024 | tf_op jit(solution)/shard_map/ppermute | solution.py:1084
  540.7 27.4 %collective-permute-start.64 = (bf16[4112,128]{1,0:T(8,128)(2,1)S(1)}, bf16[4112,128]{1,0:T(8,128)(2,1)S(1)}, u32[]{:S(2)}, u32[]{:S(2)}) collective-permute-start(bf16[4112,128]{1,0:T(8,128)(2,1)S(1)} %get-tuple-element.332), channel_id=1, source_target_pairs={{0,4},{3,7},{4,0},{7,3},{8,12},{11,15},{12,8},{15,11},{16,20},{19,... | collective-permute-start | bytes 3158024 | tf_op jit(solution)/shard_map/ppermute | solution.py:1084
  548.4 23.5 %collective-permute-start.65 = (bf16[4112,128]{1,0:T(8,128)(2,1)S(1)}, bf16[4112,128]{1,0:T(8,128)(2,1)S(1)}, u32[]{:S(2)}, u32[]{:S(2)}) collective-permute-start(bf16[4112,128]{1,0:T(8,128)(2,1)S(1)} %get-tuple-element.296), channel_id=1, source_target_pairs={{0,8},{3,11},{4,12},{7,15},{8,16},{11,19},{12,20},{15,23},{16,24},... | collective-permute-start | bytes 3158024 | tf_op jit(solution)/shard_map/ppermute | solution.py:1084
  556.8 46.8 %collective-permute-start.55 = (bf16[1024,768]{1,0:T(8,128)(2,1)}, bf16[1024,768]{1,0:T(8,128)(2,1)}, u32[]{:S(2)}, u32[]{:S(2)}) collective-permute-start(bf16[1024,768]{1,0:T(8,128)(2,1)} %get-tuple-element.284), channel_id=1, source_target_pairs={{0,1},{3,2},{4,5},{7,6},{8,9},{11,10},{12,13},{15,14},{16,17},{19,... | collective-permute-start | bytes 4718600 | tf_op jit(solution)/shard_map/ppermute | solution.py:1084
  559.3 23.4 %collective-permute-start.66 = (bf16[4112,128]{1,0:T(8,128)(2,1)}, bf16[4112,128]{1,0:T(8,128)(2,1)S(1)}, u32[]{:S(2)}, u32[]{:S(2)}) collective-permute-start(bf16[4112,128]{1,0:T(8,128)(2,1)} %get-tuple-element.298), channel_id=1, source_target_pairs={{0,4},{3,7},{4,0},{7,3},{8,12},{11,15},{12,8},{15,11},{16,20},{19,... | collective-permute-start | bytes 3158024 | tf_op jit(solution)/shard_map/ppermute | solution.py:1084
  568.1 18.7 %collective-permute-start.67 = (bf16[4112,128]{1,0:T(8,128)(2,1)}, bf16[4112,128]{1,0:T(8,128)(2,1)S(1)}, u32[]{:S(2)}, u32[]{:S(2)}) collective-permute-start(bf16[4112,128]{1,0:T(8,128)(2,1)} %get-tuple-element.299), channel_id=1, source_target_pairs={{0,8},{3,11},{4,12},{7,15},{8,16},{11,19},{12,20},{15,23},{16,24},... | collective-permute-start | bytes 3158024 | tf_op jit(solution)/shard_map/ppermute | solution.py:1084
  571.9 22.2 %collective-permute-start.68 = (bf16[4112,128]{1,0:T(8,128)(2,1)}, bf16[4112,128]{1,0:T(8,128)(2,1)S(1)}, u32[]{:S(2)}, u32[]{:S(2)}) collective-permute-start(bf16[4112,128]{1,0:T(8,128)(2,1)} %get-tuple-element.301), channel_id=1, source_target_pairs={{0,4},{3,7},{4,0},{7,3},{8,12},{11,15},{12,8},{15,11},{16,20},{19,... | collective-permute-start | bytes 3158024 | tf_op jit(solution)/shard_map/ppermute | solution.py:1084
  577.6 20.6 %collective-permute-start.69 = (bf16[4112,128]{1,0:T(8,128)(2,1)}, bf16[4112,128]{1,0:T(8,128)(2,1)}, u32[]{:S(2)}, u32[]{:S(2)}) collective-permute-start(bf16[4112,128]{1,0:T(8,128)(2,1)} %get-tuple-element.302), channel_id=1, source_target_pairs={{0,8},{3,11},{4,12},{7,15},{8,16},{11,19},{12,20},{15,23},{16,24},... | collective-permute-start | bytes 3158024 | tf_op jit(solution)/shard_map/ppermute | solution.py:1084
  582.6 24.4 %collective-permute-start.57 = (bf16[1024,384]{1,0:T(8,128)(2,1)}, bf16[1024,384]{1,0:T(8,128)(2,1)}, u32[]{:S(2)}, u32[]{:S(2)}) collective-permute-start(bf16[1024,384]{1,0:T(8,128)(2,1)} %select_convert_fusion), channel_id=1, source_target_pairs={{0,1},{3,2},{4,5},{7,6},{8,9},{11,10},{12,13},{15,14},{16,17},{19,... | collective-permute-start | bytes 2359304 | tf_op jit(solution)/shard_map/ppermute | solution.py:1084
  587.8 22.1 %collective-permute-start.70 = (bf16[4112,128]{1,0:T(8,128)(2,1)}, bf16[4112,128]{1,0:T(8,128)(2,1)S(1)}, u32[]{:S(2)}, u32[]{:S(2)}) collective-permute-start(bf16[4112,128]{1,0:T(8,128)(2,1)} %get-tuple-element.304), channel_id=1, source_target_pairs={{0,4},{3,7},{4,0},{7,3},{8,12},{11,15},{12,8},{15,11},{16,20},{19,... | collective-permute-start | bytes 3158024 | tf_op jit(solution)/shard_map/ppermute | solution.py:1084
  594.1 18.7 %collective-permute-start.71 = (bf16[4112,128]{1,0:T(8,128)(2,1)}, bf16[4112,128]{1,0:T(8,128)(2,1)S(1)}, u32[]{:S(2)}, u32[]{:S(2)}) collective-permute-start(bf16[4112,128]{1,0:T(8,128)(2,1)} %get-tuple-element.305), channel_id=1, source_target_pairs={{0,8},{3,11},{4,12},{7,15},{8,16},{11,19},{12,20},{15,23},{16,24},... | collective-permute-start | bytes 3158024 | tf_op jit(solution)/shard_map/ppermute | solution.py:1084
  (133 other events, 741.4 us)

commit v18 on v17

--- a/solution.py
+++ b/solution.py
@@ -1372,7 +1372,7 @@
         far_side = send(blocks[0, 1, order[0]], routes.z_home)
         carried[order[0]] = send(blocks[0, 0, order[0]], routes.z_home)
         rounded = {}
-        token, resized = hold(token, resized)
+        token, far_side, across[order[1]], resized = hold(token, far_side, across[order[1]], resized)
         for j in range(4):
             for n in order:
                 if j == 0 and n == order[0]:

time: 638 us -> 637 us (level)
  Pallas kernels: 275 us -> 287 us
  starting transfers between devices: 111 us -> 103 us
  waiting for transfers between devices: 135 us -> 128 us
    ppermute x73, starting transfers between devices: 111 us -> 103 us  [send(): return lax.ppermute(value, AXES, route)]
    ppermute x73, waiting for transfers between devices: 135 us -> 128 us  [send(): return lax.ppermute(value, AXES, route)]
    unnamed x222 -> x230, local copies, waits for them, and re-layouts: 26.6 us -> 29.2 us
  transfers between devices with their start and end apart: 73 -> 73, of which waited for: 38 -> 36; matrix products, arithmetic and copies ran while one was open for 11% -> 10% of each run, Pallas kernels for 30% -> 32%
where the time goes in v18:
time: 637 us; the launch traced here: 626 us
  Pallas kernels  287 us (45%)
  waiting for transfers between devices  128 us (20%)
  starting transfers between devices  103 us (16%)
  local copies, waits for them, and re-layouts  44.1 us (7%)
  matrix products  30.8 us (5%)
  other arithmetic  30.4 us (5%)
    ppermute x73, waiting for transfers between devices, send(): return lax.ppermute(value, AXES, route)  128 us
    ppermute x73, starting transfers between devices, send(): return lax.ppermute(value, AXES, route)  103 us
    pallas_call x2, Pallas kernels, attend_back_call(): pl.pallas_call(attend_back_kernel, out_shape=[shape(D, f32), shape(D, bf1...  46.7 us
    pallas_call x10, Pallas kernels, scatter_matrix(): pl.pallas_call(functools.partial(scatter_kernel, rows_n, cols_n, steps, p...  35.1 us
    pallas_call x2, Pallas kernels, attend_call(): pl.pallas_call(functools.partial(attend_kernel, layer), out_shape=[jax.Sh...  30.5 us
    unnamed x230, local copies, waits for them, and re-layouts  29.2 us
    dot_general x12, matrix products, dot_tn(): lax.dot_general(left, right, (((0,), (0,)), ((), ())), preferred_element_...  27.6 us
    pallas_call x4, Pallas kernels, expand_call(): pl.pallas_call(expand_kernel, out_shape=jax.ShapeDtypeStruct((tokens, siz...  26.7 us
  transfers between devices with their start and end apart: 73, of which 36 were waited for; matrix products, arithmetic and copies ran while one was open for 10% of the time, Pallas kernels for 32%

profile of v18, /device:TPU:0, one launch (start us, length us, event | category | flops | bytes accessed | tf_op | source)
XLA Modules:
  0.0 626.0 jit_solution(14478131761728784952)
XLA Ops:
  18.9 6.5 %shard_map.222.refs_3_ = bf16[1024,768]{1,0:T(8,128)(2,1)S(1)} custom-call(s32[4,3]{1,0:T(4,128)S(1)} %convert_element_type.120.present, s32[1]{0:T(128)} %bitcast.6.half.part, bf16[1024,768]{1,0:T(8,128)(2,1)} %broadcast_select_fusion.1.patch_ref.refs_2_, s32[1024,1]{1,0:T(8,128)S(1)} %copy.122.class_ref, bf16[3,3072,768]{2,1,0:T(8,128)(2,1)} %pinv_ref.9), custom_call_target="tpu_custom_call" | custom-call | flops 1811939328 | bytes 6684672 | tf_op jit(solution)/shard_map/pallas_call | solution.py:439
  26.6 5.6 collective-permute-done.5.refs_5_
  43.7 7.0 %shard_map.224.refs_3_ = bf16[1024,768]{1,0:T(8,128)(2,1)S(1)} custom-call(s32[4,3]{1,0:T(4,128)S(1)} %convert_element_type.120.present, s32[1]{0:T(128)} %bitcast.6.half.part, bf16[1024,768]{1,0:T(8,128)(2,1)} %get-tuple-element.165.patch_ref.refs_2_, s32[1024,1]{1,0:T(8,128)S(1)} %copy.122.class_ref, bf16[3,3072,768]{2,1,0:T(8,128)(2,1)} %pinv_ref.9), custom_call_target="tpu_custom_call" | custom-call | flops 1811939328 | bytes 6684672 | tf_op jit(solution)/shard_map/pallas_call | solution.py:439
  54.7 12.5 %collective-permute-done.9.refs_4_ = bf16[4112,128]{1,0:T(8,128)(2,1)S(1)} collective-permute-done((bf16[4112,128]{1,0:T(8,128)(2,1)}, bf16[4112,128]{1,0:T(8,128)(2,1)S(1)}, u32[]{:S(2)}, u32[]{:S(2)}) %collective-permute-start.9) | collective-permute-done | bytes 1052704 | tf_op jit(solution)/shard_map/ppermute | solution.py:1084
  67.1 5.7 collective-permute-done.8.refs_1_
  80.8 6.5 %shard_map.226.refs_3_ = bf16[1024,768]{1,0:T(8,128)(2,1)S(1)} custom-call(s32[4,3]{1,0:T(4,128)S(1)} %convert_element_type.120.present, s32[1]{0:T(128)} %bitcast.6.half.part, bf16[1024,768]{1,0:T(8,128)(2,1)} %get-tuple-element.168.patch_ref.refs_2_, s32[1024,1]{1,0:T(8,128)S(1)} %copy.122.class_ref, bf16[3,3072,768]{2,1,0:T(8,128)(2,1)} %pinv_ref.9), custom_call_target="tpu_custom_call" | custom-call | flops 1811939328 | bytes 6684672 | tf_op jit(solution)/shard_map/pallas_call | solution.py:439
  93.6 12.3 %collective-permute-done.12.refs_4_ = bf16[4112,128]{1,0:T(8,128)(2,1)S(1)} collective-permute-done((bf16[4112,128]{1,0:T(8,128)(2,1)S(1)}, bf16[4112,128]{1,0:T(8,128)(2,1)S(1)}, u32[]{:S(2)}, u32[]{:S(2)}) %collective-permute-start.12) | collective-permute-done | bytes 1052704 | tf_op jit(solution)/shard_map/ppermute | solution.py:1084
  105.8 6.1 collective-permute-done.11.refs_1_
  119.8 6.7 %shard_map.228.refs_3_ = bf16[1024,768]{1,0:T(8,128)(2,1)S(1)} custom-call(s32[4,3]{1,0:T(4,128)S(1)} %convert_element_type.120.present, s32[1]{0:T(128)} %bitcast.6.half.part, bf16[1024,768]{1,0:T(8,128)(2,1)} %get-tuple-element.171.patch_ref.refs_2_, s32[1024,1]{1,0:T(8,128)S(1)} %copy.122.class_ref, bf16[3,3072,768]{2,1,0:T(8,128)(2,1)} %pinv_ref.9), custom_call_target="tpu_custom_call" | custom-call | flops 1811939328 | bytes 6684672 | tf_op jit(solution)/shard_map/pallas_call | solution.py:439
  132.4 16.7 %collective-permute-done.14.refs_1_ = bf16[4112,128]{1,0:T(8,128)(2,1)S(1)} collective-permute-done((bf16[4112,128]{1,0:T(8,128)(2,1)S(1)}, bf16[4112,128]{1,0:T(8,128)(2,1)S(1)}, u32[]{:S(2)}, u32[]{:S(2)}) %collective-permute-start.14) | collective-permute-done | bytes 1052704 | tf_op jit(solution)/shard_map/ppermute | solution.py:1084
  157.0 5.7 collective-permute-done.28
  172.1 14.2 %shard_map.230 = (bf16[3072,384]{1,0:T(8,128)(2,1)}, bf16[2304,384]{1,0:T(8,128)(2,1)}, bf16[768,384]{1,0:T(8,128)(2,1)}, bf16[3072,384]{1,0:T(8,128)(2,1)}, bf1...) custom-call(s32[16]{0:T(128)S(1)} %stack.95.owner, ...), custom_call_target="tpu_custom_call" | custom-call | bytes 33030144 | tf_op jit(solution)/shard_map/pallas_call | solution.py:243
  186.5 6.9 %shard_map.231.refs_0_ = bf16[1024,384]{1,0:T(8,128)(2,1)S(1)} custom-call(s32[1]{0:T(128)} %bitcast.6.half.part, bf16[1024,768]{1,0:T(8,128)(2,1)} %get-tuple-element.163.refs_0_, bf16[1024,768]{1,0:T(8,128)(2,1)} %get-tuple-element.166.refs_1_, bf16[1024,768]{1,0:T(8,128)(2,1)} %get-tuple-element.169.refs_2_, ...), custom_call_target="tpu_custom_call" | custom-call | flops 2415919104 | bytes 9437184 | tf_op jit(solution)/shard_map/pallas_call | solution.py:552
  195.9 4.8 shard_map.232
  200.8 15.3 %shard_map.233 = (bf16[1024,384]{1,0:T(8,128)(2,1)S(1)}, f32[8,1024]{1,0:T(8,128)S(1)}, bf16[1024,768]{1,0:T(8,128)(2,1)S(1)}) custom-call(s32[4]{0:T(128)S(1)} %get-tuple-element.360.low_ref, s32[4]{0:T(128)S(1)} %get-tuple-element.353.high_ref, bf16[1024,384]{1,0:T(8,128)(2,1)S(1)} %get-tuple-element.186.q_ref, ...), custom_call_target="tpu_custom_call" | custom-call | flops 6442450944 | bytes 6291456 | tf_op jit(solution)/shard_map/pallas_call | solution.py:679
  220.4 9.5 %shard_map.234 = (f32[1024,768]{1,0:T(8,128)S(1)}, bf16[1024,768]{1,0:T(8,128)(2,1)}, bf16[1024,1536]{1,0:T(8,128)(2,1)}, bf16[1024,1536]{1,0:T(8,128)(2,1)}, bf16[1024,768]{1,0:T(8,128)(2,1)S(1)}) custom-call(f32[1024,768]{1,0:T(8,128)S(1)} %get-tuple-element.185.base.hid, bf16[1024,768]{1,0:T(8,128)(2,1)S(1)} %get-tuple-element.190.own, ...), custom_call_target="tpu_custom_call" | custom-call | flops 4831838208 | bytes 18874368 | tf_op jit(solution)/shard_map/pallas_call | solution.py:742
  233.4 4.4 shard_map.235
  237.8 15.3 %shard_map.236 = (bf16[1024,384]{1,0:T(8,128)(2,1)S(1)}, f32[8,1024]{1,0:T(8,128)S(1)}, bf16[1024,768]{1,0:T(8,128)(2,1)S(1)}) custom-call(s32[4]{0:T(128)S(1)} %get-tuple-element.360.low_ref, s32[4]{0:T(128)S(1)} %get-tuple-element.353.high_ref, bf16[1024,384]{1,0:T(8,128)(2,1)S(1)} %get-tuple-element.197.q_ref, ...), custom_call_target="tpu_custom_call" | custom-call | flops 6442450944 | bytes 6291456 | tf_op jit(solution)/shard_map/pallas_call | solution.py:679
  256.6 9.5 %shard_map.237 = (f32[1024,768]{1,0:T(8,128)S(1)}, bf16[1024,768]{1,0:T(8,128)(2,1)}, bf16[1024,1536]{1,0:T(8,128)(2,1)}, bf16[1024,1536]{1,0:T(8,128)(2,1)}, bf16[1024,768]{1,0:T(8,128)(2,1)S(1)}) custom-call(f32[1024,768]{1,0:T(8,128)S(1)} %get-tuple-element.196.base.hid, bf16[1024,768]{1,0:T(8,128)(2,1)S(1)} %get-tuple-element.201.own, ...), custom_call_target="tpu_custom_call" | custom-call | flops 4831838208 | bytes 18874368 | tf_op jit(solution)/shard_map/pallas_call | solution.py:742
  268.2 11.4 %shard_map.238 = (bf16[1024,768]{1,0:T(8,128)(2,1)S(1)}, bf16[1024,1536]{1,0:T(8,128)(2,1)S(1)}, bf16[1024,768]{1,0:T(8,128)(2,1)S(1)}, f32[1,768]{1,0:T(1,128)S...) custom-call(bf16[1024,768]{1,0:T(8,128)(2,1)S(1)} %broadcast_select_fusion.refs_0_, ...), custom_call_target="tpu_custom_call" | custom-call | flops 4831838208 | bytes 18874368 | tf_op jit(solution)/shard_map/pallas_call | solution.py:794
  284.0 4.0 convolution_convert_fusion.3.refs_1_
  293.5 23.4 %shard_map.240 = (f32[1024,768]{1,0:T(8,128)S(1)}, bf16[1024,768]{1,0:T(8,128)(2,1)S(1)}, bf16[1024,384]{1,0:T(8,128)(2,1)S(1)}, bf16[1024,384]{1,0:T(8,128)(2,1...) custom-call(s32[4]{0:T(128)S(1)} %get-tuple-element.359.low_ref, s32[4]{0:T(128)S(1)} %get-tuple-element.354.high_ref, ...), custom_call_target="tpu_custom_call" | custom-call | flops 11274289152 | bytes 15728640 | tf_op jit(solution)/shard_map/pallas_call | solution.py:886
  318.8 5.5 shard_map.243
  331.9 3.5 convolution_convert_fusion.5.own
  340.4 11.2 %shard_map.244 = (f32[1024,768]{1,0:T(8,128)S(1)}, bf16[1024,768]{1,0:T(8,128)(2,1)S(1)}, bf16[1024,1536]{1,0:T(8,128)(2,1)S(1)}, bf16[1024,768]{1,0:T(8,128)(2,...) custom-call(f32[1024,768]{1,0:T(8,128)S(1)} %get-tuple-element.213.refs_0_, ...), custom_call_target="tpu_custom_call" | custom-call | flops 4831838208 | bytes 18874368 | tf_op jit(solution)/shard_map/pallas_call | solution.py:794
  360.3 3.9 convolution_convert_fusion.1.refs_1_
  364.2 4.1 convolution_convert_fusion.refs_2_
  368.3 3.8 collective-permute-done.44.refs_4_
  377.8 4.2 shard_map.252.refs_1_
  382.0 4.1 shard_map.253.refs_4_
  386.1 23.3 %shard_map.250 = (f32[1024,768]{1,0:T(8,128)S(1)}, bf16[1024,768]{1,0:T(8,128)(2,1)S(1)}, bf16[1024,384]{1,0:T(8,128)(2,1)S(1)}, bf16[1024,384]{1,0:T(8,128)(2,1...) custom-call(s32[4]{0:T(128)S(1)} %get-tuple-element.359.low_ref, s32[4]{0:T(128)S(1)} %get-tuple-element.354.high_ref, ...), custom_call_target="tpu_custom_call" | custom-call | flops 11274289152 | bytes 15728640 | tf_op jit(solution)/shard_map/pallas_call | solution.py:886
  411.2 5.5 shard_map.255
  421.6 3.5 convolution_convert_fusion.4.own
  433.3 5.4 collective-permute-done.48.refs_1_
  449.4 3.6 shard_map.263.refs_1_
  453.0 4.3 shard_map.264.refs_5_
  461.8 8.8 %collective-permute-done.52.refs_3_ = bf16[384,768]{1,0:T(8,128)(2,1)S(1)} collective-permute-done((bf16[384,768]{1,0:T(8,128)(2,1)S(1)}, bf16[384,768]{1,0:T(8,128)(2,1)S(1)}, u32[]{:S(2)}, u32[]{:S(2)}) %collective-permute-start.52) | collective-permute-done | bytes 589856 | tf_op jit(solution)/shard_map/ppermute | solution.py:1084
  477.5 4.0 shard_map.267.refs_0_
  485.6 3.5 shard_map.270.refs_1_
  501.5 4.0 collective-permute-start.57
  509.3 10.2 %shard_map.274.refs_3_ = bf16[3,384,768]{2,1,0:T(8,128)(2,1)S(1)} custom-call(bf16[3072,384]{1,0:T(8,128)(2,1)} %get-tuple-element.289.base, bf16[3,3072,768]{2,1,0:T(8,128)(2,1)} %pinv_ref.9), custom_call_target="tpu_custom_call" | custom-call | flops 5435817984 | bytes 14155776 | tf_op jit(solution)/shard_map/pallas_call | solution.py:470
  533.2 3.9 collective-permute-start.62
  539.7 4.0 collective-permute-start.63
  551.1 4.7 collective-permute-done.62.refs_2_
  563.2 3.9 collective-permute-done.64.refs_2_
  567.1 4.0 collective-permute-start.67
  602.6 3.4 select_convert_fusion.1
  616.8 8.8 %shard_map.284 = (f32[32,128,128]{2,1,0:T(8,128)}, f32[32,128,128]{2,1,0:T(8,128)}, f32[32,128,128]{2,1,0:T(8,128)}, f32[32,128,128]{2,1,0:T(8,128)}) custom-call(s32[32]{0:T(128)S(1)} %convert_element_type.148.used, s32[1]{0:T(128)} %bitcast.27.flag.home, bf16[4112,128]{1,0:T(8,128)(2,1)} %copy-done.28, bf16[4112,128]{1,0:T(8,128)(2,1)} %collective-permute-done.72.far, ...), custom_call_target="tpu_custom_call" | custom-call | flops 5905580032 | bytes 19922944 | tf_op jit(solution)/shard_map/pallas_call | solution.py:1011
  (491 shorter events, 264.2 us)
Async XLA Ops:
  4.2 28.6 %collective-permute-start.4 = (bf16[4112,128]{1,0:T(8,128)(2,1)}, bf16[4112,128]{1,0:T(8,128)(2,1)}, u32[]{:S(2)}, u32[]{:S(2)}) collective-permute-start(bf16[4112,128]{1,0:T(8,128)(2,1)} %pad_maximum_fusion.2), channel_id=1, source_target_pairs={{0,8},{1,9},{2,10},{3,11},{4,12},{5,13},{6,14},{7,15},{8,16},{9,17... | collective-permute-start | bytes 3158024 | tf_op jit(solution)/shard_map/ppermute | solution.py:1084
  7.2 25.6 %collective-permute-start.1 = (bf16[4112,128]{1,0:T(8,128)(2,1)}, bf16[4112,128]{1,0:T(8,128)(2,1)S(1)}, u32[]{:S(2)}, u32[]{:S(2)}) collective-permute-start(bf16[4112,128]{1,0:T(8,128)(2,1)} %pad_maximum_fusion.2), channel_id=1, source_target_pairs={{0,1},{1,0},{2,3},{3,2},{4,5},{5,4},{6,7},{7,6},{8,9},{9,8},{10,11... | collective-permute-start | bytes 3158024 | tf_op jit(solution)/shard_map/ppermute | solution.py:1084
  8.7 24.6 %collective-permute-start = (bf16[4112,128]{1,0:T(8,128)(2,1)}, bf16[4112,128]{1,0:T(8,128)(2,1)S(1)}, u32[]{:S(2)}, u32[]{:S(2)}) collective-permute-start(bf16[4112,128]{1,0:T(8,128)(2,1)} %pad_maximum_fusion.2), channel_id=1, source_target_pairs={{0,4},{1,5},{2,6},{3,7},{4,0},{5,1},{6,2},{7,3},{8,12},{9,13},{10,... | collective-permute-start | bytes 3158024 | tf_op jit(solution)/shard_map/ppermute | solution.py:1084
  14.0 18.2 %collective-permute-start.5 = (s32[1,504]{1,0:T(1,128)S(1)}, s32[1,504]{1,0:T(1,128)S(1)}, u32[]{:S(2)}, u32[]{:S(2)}) collective-permute-start(s32[1,504]{1,0:T(1,128)S(1)} %copy-done.99), channel_id=1, source_target_pairs={{0,1},{1,0},{2,3},{3,2},{4,5},{5,4},{6,7},{7,6},{8,9},{9,8},{10,11... | collective-permute-start | bytes 6056 | tf_op jit(solution)/shard_map/ppermute | solution.py:1084
  41.5 25.6 %collective-permute-start.9 = (bf16[4112,128]{1,0:T(8,128)(2,1)}, bf16[4112,128]{1,0:T(8,128)(2,1)S(1)}, u32[]{:S(2)}, u32[]{:S(2)}) collective-permute-start(bf16[4112,128]{1,0:T(8,128)(2,1)} %get-tuple-element.164), channel_id=1, source_target_pairs={{0,8},{1,9},{2,10},{3,11},{4,12},{5,13},{6,14},{7,15},{8,16},{9,17... | collective-permute-start | bytes 3158024 | tf_op jit(solution)/shard_map/ppermute | solution.py:1084
  42.5 30.3 %collective-permute-start.8 = (bf16[4112,128]{1,0:T(8,128)(2,1)}, bf16[4112,128]{1,0:T(8,128)(2,1)S(1)}, u32[]{:S(2)}, u32[]{:S(2)}) collective-permute-start(bf16[4112,128]{1,0:T(8,128)(2,1)} %get-tuple-element.164), channel_id=1, source_target_pairs={{0,1},{1,0},{2,3},{3,2},{4,5},{5,4},{6,7},{7,6},{8,9},{9,8},{10,11... | collective-permute-start | bytes 3158024 | tf_op jit(solution)/shard_map/ppermute | solution.py:1084
  43.2 30.7 %collective-permute-start.7 = (bf16[4112,128]{1,0:T(8,128)(2,1)}, bf16[4112,128]{1,0:T(8,128)(2,1)S(1)}, u32[]{:S(2)}, u32[]{:S(2)}) collective-permute-start(bf16[4112,128]{1,0:T(8,128)(2,1)} %get-tuple-element.164), channel_id=1, source_target_pairs={{0,4},{1,5},{2,6},{3,7},{4,0},{5,1},{6,2},{7,3},{8,12},{9,13},{10,... | collective-permute-start | bytes 3158024 | tf_op jit(solution)/shard_map/ppermute | solution.py:1084
  52.0 113.0 %collective-permute-start.15 = (bf16[4112,128]{1,0:T(8,128)(2,1)S(1)}, bf16[4112,128]{1,0:T(8,128)(2,1)S(1)}, u32[]{:S(2)}, u32[]{:S(2)}) collective-permute-start(bf16[4112,128]{1,0:T(8,128)(2,1)S(1)} %get-tuple-element.341), channel_id=1, source_target_pairs={{0,2},{1,3},{2,0},{3,1},{4,6},{5,7},{6,4},{7,5},{8,10},{9,11},{10,... | collective-permute-start | bytes 3158024 | tf_op jit(solution)/shard_map/ppermute | solution.py:1084
  54.7 111.8 %collective-permute-start.18 = (bf16[4112,128]{1,0:T(8,128)(2,1)S(1)}, bf16[4112,128]{1,0:T(8,128)(2,1)}, u32[]{:S(2)}, u32[]{:S(2)}) collective-permute-start(bf16[4112,128]{1,0:T(8,128)(2,1)S(1)} %broadcast_select_fusion.8), channel_id=1, source_target_pairs={{0,2},{1,3},{2,0},{3,1},{4,6},{5,7},{6,4},{7,5},{8,10},{9,11},{10,... | collective-permute-start | bytes 3158024 | tf_op jit(solution)/shard_map/ppermute | solution.py:1084
  80.1 25.8 %collective-permute-start.12 = (bf16[4112,128]{1,0:T(8,128)(2,1)S(1)}, bf16[4112,128]{1,0:T(8,128)(2,1)S(1)}, u32[]{:S(2)}, u32[]{:S(2)}) collective-permute-start(bf16[4112,128]{1,0:T(8,128)(2,1)S(1)} %copy-done.64), channel_id=1, source_target_pairs={{0,8},{1,9},{2,10},{3,11},{4,12},{5,13},{6,14},{7,15},{8,16},{9,17... | collective-permute-start | bytes 3158024 | tf_op jit(solution)/shard_map/ppermute | solution.py:1084
  89.4 22.6 %collective-permute-start.11 = (bf16[4112,128]{1,0:T(8,128)(2,1)S(1)}, bf16[4112,128]{1,0:T(8,128)(2,1)S(1)}, u32[]{:S(2)}, u32[]{:S(2)}) collective-permute-start(bf16[4112,128]{1,0:T(8,128)(2,1)S(1)} %copy-done.64), channel_id=1, source_target_pairs={{0,1},{1,0},{2,3},{3,2},{4,5},{5,4},{6,7},{7,6},{8,9},{9,8},{10,11... | collective-permute-start | bytes 3158024 | tf_op jit(solution)/shard_map/ppermute | solution.py:1084
  90.6 22.2 %collective-permute-start.10 = (bf16[4112,128]{1,0:T(8,128)(2,1)S(1)}, bf16[4112,128]{1,0:T(8,128)(2,1)S(1)}, u32[]{:S(2)}, u32[]{:S(2)}) collective-permute-start(bf16[4112,128]{1,0:T(8,128)(2,1)S(1)} %copy-done.64), channel_id=1, source_target_pairs={{0,4},{1,5},{2,6},{3,7},{4,0},{5,1},{6,2},{7,3},{8,12},{9,13},{10,... | collective-permute-start | bytes 3158024 | tf_op jit(solution)/shard_map/ppermute | solution.py:1084
  105.8 60.6 %collective-permute-start.19 = (bf16[4112,128]{1,0:T(8,128)(2,1)S(1)}, bf16[4112,128]{1,0:T(8,128)(2,1)}, u32[]{:S(2)}, u32[]{:S(2)}) collective-permute-start(bf16[4112,128]{1,0:T(8,128)(2,1)S(1)} %broadcast_select_fusion.7), channel_id=1, source_target_pairs={{0,2},{1,3},{2,0},{3,1},{4,6},{5,7},{6,4},{7,5},{8,10},{9,11},{10,... | collective-permute-start | bytes 3158024 | tf_op jit(solution)/shard_map/ppermute | solution.py:1084
  128.0 21.1 %collective-permute-start.14 = (bf16[4112,128]{1,0:T(8,128)(2,1)S(1)}, bf16[4112,128]{1,0:T(8,128)(2,1)S(1)}, u32[]{:S(2)}, u32[]{:S(2)}) collective-permute-start(bf16[4112,128]{1,0:T(8,128)(2,1)S(1)} %copy-done.66), channel_id=1, source_target_pairs={{0,1},{1,0},{2,3},{3,2},{4,5},{5,4},{6,7},{7,6},{8,9},{9,8},{10,11... | collective-permute-start | bytes 3158024 | tf_op jit(solution)/shard_map/ppermute | solution.py:1084
  129.4 20.4 %collective-permute-start.13 = (bf16[4112,128]{1,0:T(8,128)(2,1)S(1)}, bf16[4112,128]{1,0:T(8,128)(2,1)S(1)}, u32[]{:S(2)}, u32[]{:S(2)}) collective-permute-start(bf16[4112,128]{1,0:T(8,128)(2,1)S(1)} %copy-done.66), channel_id=1, source_target_pairs={{0,4},{1,5},{2,6},{3,7},{4,0},{5,1},{6,2},{7,3},{8,12},{9,13},{10,... | collective-permute-start | bytes 3158024 | tf_op jit(solution)/shard_map/ppermute | solution.py:1084
  230.3 23.3 %collective-permute-start.6 = (bf16[1024,768]{1,0:T(8,128)(2,1)S(1)}, bf16[1024,768]{1,0:T(8,128)(2,1)S(1)}, u32[]{:S(2)}, u32[]{:S(2)}) collective-permute-start(bf16[1024,768]{1,0:T(8,128)(2,1)S(1)} %copy-done.96), channel_id=1, source_target_pairs={{0,2},{3,1},{4,6},{7,5},{8,10},{11,9},{12,14},{15,13},{16,18},{19,... | collective-permute-start | bytes 4718600 | tf_op jit(solution)/shard_map/ppermute | solution.py:1084
  267.8 23.9 %collective-permute-start.38 = (bf16[1024,768]{1,0:T(8,128)(2,1)S(1)}, bf16[1024,768]{1,0:T(8,128)(2,1)S(1)}, u32[]{:S(2)}, u32[]{:S(2)}) collective-permute-start(bf16[1024,768]{1,0:T(8,128)(2,1)S(1)} %get-tuple-element.220), channel_id=1, source_target_pairs={{0,2},{1,3},{2,0},{3,1},{4,6},{5,7},{6,4},{7,5},{8,10},{9,11},{10,... | collective-permute-start | bytes 4718600 | tf_op jit(solution)/shard_map/ppermute | solution.py:1084
  282.7 34.2 %collective-permute-start.36 = (bf16[1536,768]{1,0:T(8,128)(2,1)S(1)}, bf16[1536,768]{1,0:T(8,128)(2,1)S(1)}, u32[]{:S(2)}, u32[]{:S(2)}) collective-permute-start(bf16[1536,768]{1,0:T(8,128)(2,1)S(1)} %convolution_convert_fusion.2.own), channel_id=1, source_target_pairs={{1,0},{2,3},{5,4},{6,7},{9,8},{10,11},{13,12},{14,15},{17,16},{18,... | collective-permute-start | bytes 7077896 | tf_op jit(solution)/shard_map/ppermute | solution.py:1084
  290.6 26.3 %collective-permute-start.37 = (bf16[384,1536]{1,0:T(8,128)(2,1)}, bf16[384,1536]{1,0:T(8,128)(2,1)S(1)}, u32[]{:S(2)}, u32[]{:S(2)}) collective-permute-start(bf16[384,1536]{1,0:T(8,128)(2,1)} %shard_map.241), channel_id=1, source_target_pairs={{1,5},{2,6},{5,1},{6,2},{9,13},{10,14},{13,9},{14,10},{17,21},{18,... | collective-permute-start | bytes 3538952 | tf_op jit(solution)/shard_map/ppermute | solution.py:1084
  324.3 16.1 %collective-permute-start.39 = (bf16[1024,768]{1,0:T(8,128)(2,1)S(1)}, bf16[1024,768]{1,0:T(8,128)(2,1)S(1)}, u32[]{:S(2)}, u32[]{:S(2)}) collective-permute-start(bf16[1024,768]{1,0:T(8,128)(2,1)S(1)} %get-tuple-element.222.refs_1_), channel_id=1, source_target_pairs={{0,2},{1,3},{2,0},{3,1},{4,6},{5,7},{6,4},{7,5},{8,10},{9,11},{10,... | collective-permute-start | bytes 4718600 | tf_op jit(solution)/shard_map/ppermute | solution.py:1084
  330.6 21.1 %collective-permute-start.43 = (bf16[384,1536]{1,0:T(8,128)(2,1)}, bf16[384,1536]{1,0:T(8,128)(2,1)S(1)}, u32[]{:S(2)}, u32[]{:S(2)}) collective-permute-start(bf16[384,1536]{1,0:T(8,128)(2,1)} %shard_map.246), channel_id=1, source_target_pairs={{1,0},{2,3},{5,4},{6,7},{9,8},{10,11},{13,12},{14,15},{17,16},{18,... | collective-permute-start | bytes 3538952 | tf_op jit(solution)/shard_map/ppermute | solution.py:1084
  339.1 29.2 %collective-permute-start.41 = (bf16[384,768]{1,0:T(8,128)(2,1)S(1)}, bf16[384,768]{1,0:T(8,128)(2,1)S(1)}, u32[]{:S(2)}, u32[]{:S(2)}) collective-permute-start(bf16[384,768]{1,0:T(8,128)(2,1)S(1)} %convolution_convert_fusion.11.own), channel_id=1, source_target_pairs={{1,0},{2,3},{5,4},{6,7},{9,8},{10,11},{13,12},{14,15},{17,16},{18,... | collective-permute-start | bytes 1769480 | tf_op jit(solution)/shard_map/ppermute | solution.py:1084
  355.7 16.4 %collective-permute-start.44 = (bf16[384,1152]{1,0:T(8,128)(2,1)}, bf16[384,1152]{1,0:T(8,128)(2,1)S(1)}, u32[]{:S(2)}, u32[]{:S(2)}) collective-permute-start(bf16[384,1152]{1,0:T(8,128)(2,1)} %shard_map.248), channel_id=1, source_target_pairs={{1,0},{2,3},{5,4},{6,7},{9,8},{10,11},{13,12},{14,15},{17,16},{18,... | collective-permute-start | bytes 2654216 | tf_op jit(solution)/shard_map/ppermute | solution.py:1084
  357.2 28.9 %collective-permute-start.40 = (bf16[1024,768]{1,0:T(8,128)(2,1)S(1)}, bf16[1024,768]{1,0:T(8,128)(2,1)S(1)}, u32[]{:S(2)}, u32[]{:S(2)}) collective-permute-start(bf16[1024,768]{1,0:T(8,128)(2,1)S(1)} %get-tuple-element.225.own), channel_id=1, source_target_pairs={{0,2},{1,3},{2,0},{3,1},{4,6},{5,7},{6,4},{7,5},{8,10},{9,11},{10,... | collective-permute-start | bytes 4718600 | tf_op jit(solution)/shard_map/ppermute | solution.py:1084
  373.1 36.4 %collective-permute-start.45 = (bf16[1536,768]{1,0:T(8,128)(2,1)}, bf16[1536,768]{1,0:T(8,128)(2,1)S(1)}, u32[]{:S(2)}, u32[]{:S(2)}) collective-permute-start(bf16[1536,768]{1,0:T(8,128)(2,1)} %get-tuple-element.243.own), channel_id=1, source_target_pairs={{1,0},{2,3},{5,4},{6,7},{9,8},{10,11},{13,12},{14,15},{17,16},{18,... | collective-permute-start | bytes 7077896 | tf_op jit(solution)/shard_map/ppermute | solution.py:1084
  377.0 32.5 %collective-permute-start.46 = (bf16[384,1536]{1,0:T(8,128)(2,1)}, bf16[384,1536]{1,0:T(8,128)(2,1)S(1)}, u32[]{:S(2)}, u32[]{:S(2)}) collective-permute-start(bf16[384,1536]{1,0:T(8,128)(2,1)} %shard_map.251), channel_id=1, source_target_pairs={{1,5},{2,6},{5,1},{6,2},{9,13},{10,14},{13,9},{14,10},{17,21},{18,... | collective-permute-start | bytes 3538952 | tf_op jit(solution)/shard_map/ppermute | solution.py:1084
  420.3 18.4 %collective-permute-start.48 = (bf16[384,1536]{1,0:T(8,128)(2,1)}, bf16[384,1536]{1,0:T(8,128)(2,1)S(1)}, u32[]{:S(2)}, u32[]{:S(2)}) collective-permute-start(bf16[384,1536]{1,0:T(8,128)(2,1)} %shard_map.257), channel_id=1, source_target_pairs={{1,0},{2,3},{5,4},{6,7},{9,8},{10,11},{13,12},{14,15},{17,16},{18,... | collective-permute-start | bytes 3538952 | tf_op jit(solution)/shard_map/ppermute | solution.py:1084
  439.8 31.5 %collective-permute-start.50 = (bf16[1536,384]{1,0:T(8,128)(2,1)}, bf16[1536,384]{1,0:T(8,128)(2,1)S(1)}, u32[]{:S(2)}, u32[]{:S(2)}) collective-permute-start(bf16[1536,384]{1,0:T(8,128)(2,1)} %get-tuple-element.252.own), channel_id=1, source_target_pairs={{1,5},{2,6},{5,1},{6,2},{9,13},{10,14},{13,9},{14,10},{17,21},{18,... | collective-permute-start | bytes 3538952 | tf_op jit(solution)/shard_map/ppermute | solution.py:1084
  443.2 28.1 %collective-permute-start.51 = (bf16[384,1152]{1,0:T(8,128)(2,1)}, bf16[384,1152]{1,0:T(8,128)(2,1)S(1)}, u32[]{:S(2)}, u32[]{:S(2)}) collective-permute-start(bf16[384,1152]{1,0:T(8,128)(2,1)} %shard_map.260), channel_id=1, source_target_pairs={{1,0},{2,3},{5,4},{6,7},{9,8},{10,11},{13,12},{14,15},{17,16},{18,... | collective-permute-start | bytes 2654216 | tf_op jit(solution)/shard_map/ppermute | solution.py:1084
  445.3 25.3 %collective-permute-start.52 = (bf16[384,768]{1,0:T(8,128)(2,1)S(1)}, bf16[384,768]{1,0:T(8,128)(2,1)S(1)}, u32[]{:S(2)}, u32[]{:S(2)}) collective-permute-start(bf16[384,768]{1,0:T(8,128)(2,1)S(1)} %convolution_convert_fusion.6.own), channel_id=1, source_target_pairs={{1,0},{2,3},{5,4},{6,7},{9,8},{10,11},{13,12},{14,15},{17,16},{18,... | collective-permute-start | bytes 1769480 | tf_op jit(solution)/shard_map/ppermute | solution.py:1084
  476.1 18.3 %collective-permute-start.54 = (bf16[1536,384]{1,0:T(8,128)(2,1)}, bf16[1536,384]{1,0:T(8,128)(2,1)S(1)}, u32[]{:S(2)}, u32[]{:S(2)}) collective-permute-start(bf16[1536,384]{1,0:T(8,128)(2,1)} %shard_map.266), channel_id=1, source_target_pairs={{1,0},{2,3},{5,4},{6,7},{9,8},{10,11},{13,12},{14,15},{17,16},{18,... | collective-permute-start | bytes 3538952 | tf_op jit(solution)/shard_map/ppermute | solution.py:1084
  501.5 19.3 %collective-permute-start.57 = (bf16[4112,128]{1,0:T(8,128)(2,1)S(1)}, bf16[4112,128]{1,0:T(8,128)(2,1)S(1)}, u32[]{:S(2)}, u32[]{:S(2)}) collective-permute-start(bf16[4112,128]{1,0:T(8,128)(2,1)S(1)} %get-tuple-element.339), channel_id=1, source_target_pairs={{0,4},{3,7},{4,0},{7,3},{8,12},{11,15},{12,8},{15,11},{16,20},{19,... | collective-permute-start | bytes 3158024 | tf_op jit(solution)/shard_map/ppermute | solution.py:1084
  505.4 18.5 %collective-permute-start.56 = (bf16[4112,128]{1,0:T(8,128)(2,1)S(1)}, bf16[4112,128]{1,0:T(8,128)(2,1)S(1)}, u32[]{:S(2)}, u32[]{:S(2)}) collective-permute-start(bf16[4112,128]{1,0:T(8,128)(2,1)S(1)} %get-tuple-element.340), channel_id=1, source_target_pairs={{0,8},{3,11},{4,12},{7,15},{8,16},{11,19},{12,20},{15,23},{16,24},... | collective-permute-start | bytes 3158024 | tf_op jit(solution)/shard_map/ppermute | solution.py:1084
  507.4 36.3 %collective-permute-start.61 = (bf16[4112,128]{1,0:T(8,128)(2,1)S(1)}, bf16[4112,128]{1,0:T(8,128)(2,1)S(1)}, u32[]{:S(2)}, u32[]{:S(2)}) collective-permute-start(bf16[4112,128]{1,0:T(8,128)(2,1)S(1)} %get-tuple-element.338), channel_id=1, source_target_pairs={{0,8},{3,11},{4,12},{7,15},{8,16},{11,19},{12,20},{15,23},{16,24},... | collective-permute-start | bytes 3158024 | tf_op jit(solution)/shard_map/ppermute | solution.py:1084
  527.8 17.9 %collective-permute-start.60 = (bf16[4112,128]{1,0:T(8,128)(2,1)S(1)}, bf16[4112,128]{1,0:T(8,128)(2,1)S(1)}, u32[]{:S(2)}, u32[]{:S(2)}) collective-permute-start(bf16[4112,128]{1,0:T(8,128)(2,1)S(1)} %get-tuple-element.296), channel_id=1, source_target_pairs={{0,4},{3,7},{4,0},{7,3},{8,12},{11,15},{12,8},{15,11},{16,20},{19,... | collective-permute-start | bytes 3158024 | tf_op jit(solution)/shard_map/ppermute | solution.py:1084
  533.1 42.4 %collective-permute-start.58 = (bf16[1024,768]{1,0:T(8,128)(2,1)S(1)}, bf16[1024,768]{1,0:T(8,128)(2,1)S(1)}, u32[]{:S(2)}, u32[]{:S(2)}) collective-permute-start(bf16[1024,768]{1,0:T(8,128)(2,1)S(1)} %add_convert_fusion), channel_id=1, source_target_pairs={{0,2},{1,3},{2,0},{3,1},{4,6},{5,7},{6,4},{7,5},{8,10},{9,11},{10,... | collective-permute-start | bytes 4718600 | tf_op jit(solution)/shard_map/ppermute | solution.py:1084
  533.2 22.6 %collective-permute-start.62 = (bf16[4112,128]{1,0:T(8,128)(2,1)S(1)}, bf16[4112,128]{1,0:T(8,128)(2,1)S(1)}, u32[]{:S(2)}, u32[]{:S(2)}) collective-permute-start(bf16[4112,128]{1,0:T(8,128)(2,1)S(1)} %get-tuple-element.337), channel_id=1, source_target_pairs={{0,4},{3,7},{4,0},{7,3},{8,12},{11,15},{12,8},{15,11},{16,20},{19,... | collective-permute-start | bytes 3158024 | tf_op jit(solution)/shard_map/ppermute | solution.py:1084
  539.7 18.5 %collective-permute-start.63 = (bf16[4112,128]{1,0:T(8,128)(2,1)S(1)}, bf16[4112,128]{1,0:T(8,128)(2,1)S(1)}, u32[]{:S(2)}, u32[]{:S(2)}) collective-permute-start(bf16[4112,128]{1,0:T(8,128)(2,1)S(1)} %get-tuple-element.298), channel_id=1, source_target_pairs={{0,8},{3,11},{4,12},{7,15},{8,16},{11,19},{12,20},{15,23},{16,24},... | collective-permute-start | bytes 3158024 | tf_op jit(solution)/shard_map/ppermute | solution.py:1084
  543.7 23.4 %collective-permute-start.64 = (bf16[4112,128]{1,0:T(8,128)(2,1)S(1)}, bf16[4112,128]{1,0:T(8,128)(2,1)S(1)}, u32[]{:S(2)}, u32[]{:S(2)}) collective-permute-start(bf16[4112,128]{1,0:T(8,128)(2,1)S(1)} %get-tuple-element.336), channel_id=1, source_target_pairs={{0,4},{3,7},{4,0},{7,3},{8,12},{11,15},{12,8},{15,11},{16,20},{19,... | collective-permute-start | bytes 3158024 | tf_op jit(solution)/shard_map/ppermute | solution.py:1084
  548.2 22.8 %collective-permute-start.65 = (bf16[4112,128]{1,0:T(8,128)(2,1)S(1)}, bf16[4112,128]{1,0:T(8,128)(2,1)S(1)}, u32[]{:S(2)}, u32[]{:S(2)}) collective-permute-start(bf16[4112,128]{1,0:T(8,128)(2,1)S(1)} %get-tuple-element.300), channel_id=1, source_target_pairs={{0,8},{3,11},{4,12},{7,15},{8,16},{11,19},{12,20},{15,23},{16,24},... | collective-permute-start | bytes 3158024 | tf_op jit(solution)/shard_map/ppermute | solution.py:1084
  555.8 46.8 %collective-permute-start.55 = (bf16[1024,768]{1,0:T(8,128)(2,1)}, bf16[1024,768]{1,0:T(8,128)(2,1)}, u32[]{:S(2)}, u32[]{:S(2)}) collective-permute-start(bf16[1024,768]{1,0:T(8,128)(2,1)} %get-tuple-element.286), channel_id=1, source_target_pairs={{0,1},{3,2},{4,5},{7,6},{8,9},{11,10},{12,13},{15,14},{16,17},{19,... | collective-permute-start | bytes 4718600 | tf_op jit(solution)/shard_map/ppermute | solution.py:1084
  558.3 24.1 %collective-permute-start.66 = (bf16[4112,128]{1,0:T(8,128)(2,1)}, bf16[4112,128]{1,0:T(8,128)(2,1)S(1)}, u32[]{:S(2)}, u32[]{:S(2)}) collective-permute-start(bf16[4112,128]{1,0:T(8,128)(2,1)} %get-tuple-element.302), channel_id=1, source_target_pairs={{0,4},{3,7},{4,0},{7,3},{8,12},{11,15},{12,8},{15,11},{16,20},{19,... | collective-permute-start | bytes 3158024 | tf_op jit(solution)/shard_map/ppermute | solution.py:1084
  567.1 18.7 %collective-permute-start.67 = (bf16[4112,128]{1,0:T(8,128)(2,1)}, bf16[4112,128]{1,0:T(8,128)(2,1)S(1)}, u32[]{:S(2)}, u32[]{:S(2)}) collective-permute-start(bf16[4112,128]{1,0:T(8,128)(2,1)} %get-tuple-element.303), channel_id=1, source_target_pairs={{0,8},{3,11},{4,12},{7,15},{8,16},{11,19},{12,20},{15,23},{16,24},... | collective-permute-start | bytes 3158024 | tf_op jit(solution)/shard_map/ppermute | solution.py:1084
  571.0 22.2 %collective-permute-start.68 = (bf16[4112,128]{1,0:T(8,128)(2,1)}, bf16[4112,128]{1,0:T(8,128)(2,1)S(1)}, u32[]{:S(2)}, u32[]{:S(2)}) collective-permute-start(bf16[4112,128]{1,0:T(8,128)(2,1)} %get-tuple-element.305), channel_id=1, source_target_pairs={{0,4},{3,7},{4,0},{7,3},{8,12},{11,15},{12,8},{15,11},{16,20},{19,... | collective-permute-start | bytes 3158024 | tf_op jit(solution)/shard_map/ppermute | solution.py:1084
  576.7 20.5 %collective-permute-start.69 = (bf16[4112,128]{1,0:T(8,128)(2,1)}, bf16[4112,128]{1,0:T(8,128)(2,1)}, u32[]{:S(2)}, u32[]{:S(2)}) collective-permute-start(bf16[4112,128]{1,0:T(8,128)(2,1)} %get-tuple-element.306), channel_id=1, source_target_pairs={{0,8},{3,11},{4,12},{7,15},{8,16},{11,19},{12,20},{15,23},{16,24},... | collective-permute-start | bytes 3158024 | tf_op jit(solution)/shard_map/ppermute | solution.py:1084
  582.3 23.7 %collective-permute-start.59 = (bf16[1024,384]{1,0:T(8,128)(2,1)}, bf16[1024,384]{1,0:T(8,128)(2,1)}, u32[]{:S(2)}, u32[]{:S(2)}) collective-permute-start(bf16[1024,384]{1,0:T(8,128)(2,1)} %select_convert_fusion), channel_id=1, source_target_pairs={{0,1},{3,2},{4,5},{7,6},{8,9},{11,10},{12,13},{15,14},{16,17},{19,... | collective-permute-start | bytes 2359304 | tf_op jit(solution)/shard_map/ppermute | solution.py:1084
  586.8 22.0 %collective-permute-start.70 = (bf16[4112,128]{1,0:T(8,128)(2,1)}, bf16[4112,128]{1,0:T(8,128)(2,1)S(1)}, u32[]{:S(2)}, u32[]{:S(2)}) collective-permute-start(bf16[4112,128]{1,0:T(8,128)(2,1)} %get-tuple-element.308), channel_id=1, source_target_pairs={{0,4},{3,7},{4,0},{7,3},{8,12},{11,15},{12,8},{15,11},{16,20},{19,... | collective-permute-start | bytes 3158024 | tf_op jit(solution)/shard_map/ppermute | solution.py:1084
  593.2 18.7 %collective-permute-start.71 = (bf16[4112,128]{1,0:T(8,128)(2,1)}, bf16[4112,128]{1,0:T(8,128)(2,1)S(1)}, u32[]{:S(2)}, u32[]{:S(2)}) collective-permute-start(bf16[4112,128]{1,0:T(8,128)(2,1)} %get-tuple-element.309), channel_id=1, source_target_pairs={{0,8},{3,11},{4,12},{7,15},{8,16},{11,19},{12,20},{15,23},{16,24},... | collective-permute-start | bytes 3158024 | tf_op jit(solution)/shard_map/ppermute | solution.py:1084
  (137 other events, 765.2 us)
